TPU v7x, 32 devices: a whole 2x2x4 slice. The times are simulated.
32 devices in a mesh: groups: 2 (over y), tile: 4 (over z), batch: 2 (over x), chan: 2 (over core).
Axes of the slice: x: 2, y: 2, z: 4, core: 2. Of those that a mesh axis runs over, the one named last changes fastest.
Arguments:
- features: bfloat16 [4, 48, 256, 256], P(('groups', 'batch'), 'tile'), parts along dimension 0, may hold values from -6 to 6
- labels: int32 [4, 48, 2304], P(('groups', 'batch'), 'tile'), parts along dimension 0, may hold values from -1 to 11, as said below
- w_shared: bfloat16 [3, 3, 256, 256], P(None, None, None, 'chan'), may hold values from -0.125 to 0.125
- b_shared: float32 [256], P('chan'), may hold values from -3 to 3
- w_cls: bfloat16 [3, 3, 256, 99], P(None, None, 'chan'), may hold values from -0.125 to 0.125
- b_cls: float32 [99], replicated, may hold values from -3 to -1
Outputs:
- grad_shared: float32 [6, 3, 256, 256], P('groups', None, None, 'chan'), parts along dimension 0
- grad_shared_bias: float32 [512], P(('groups', 'chan')), parts along dimension 0
- grad_cls: float32 [6, 3, 256, 99], P('groups', None, 'chan'), parts along dimension 0
- grad_cls_bias: float32 [198], P('groups'), parts along dimension 0
- loss: float32 [2], P('groups'), parts along dimension 0
There are 2 independent parts, one for each index of `groups`. A program takes and returns all parts, laid end to end along the dimension named above; an argument that names none is the same for every part. Nothing has to cross between parts.
Inputs may be any that keep to these rules, and one draw needn't show every extreme that they name: `labels`: each anchor is a background anchor (0), ignored (-1) or names a class of 1 to 11.
All inputs are finite; a program needn't handle non-finite values.
Results may differ from a plain program's by a relative error of at most 0.0027.
Values may be sent and summed in bfloat16 or wider, within the bound.
No kernel may reach another device: no remote copies, remote signals or barrier semaphores. Data moves between devices by JAX's collectives and lax.ppermute only.
A program may use at most 128 MiB of HBM per device.

v0:
```python
import functools

import jax
import jax.numpy as jnp
from jax import lax
from jax.experimental import pallas as pl
from jax.experimental.pallas import tpu as pltpu
from jax.sharding import PartitionSpec as P

ANCH = 9
CLASSES = 11
LOGITS = 99
LANES = 128
CLS_ROWS = 112
BF16 = jnp.bfloat16
F32 = jnp.float32


def shift_cells(field, by):
    cells = field.shape[0]
    rolled = pltpu.roll(field, by % cells, axis=0)
    cell = lax.broadcasted_iota(jnp.int32, field.shape, 0)
    edge = 0 if by > 0 else cells - 1
    return jnp.where(cell == edge, 0.0, rolled)


def dot(left, right, dims=((1,), (0,))):
    return lax.dot_general(left, right, (dims, ((), ())), preferred_element_type=F32)


def head_kernel(
    where_ref, count_ref, f_ref, halo_ref, lab_ref, hlab_ref, w1a_ref, w1b_ref, b1_ref, w2_ref, b2_ref,
    gcls_ref, own_ref, other_ref, small_ref,
    xw_ref, hid_ref, dlog_ref, dt_ref,
):
    half = f_ref.shape[0] // 2
    cols = f_ref.shape[1]
    c = where_ref[0]
    first = where_ref[1]
    total = where_ref[2]
    near = half + 3
    xw_ref[pl.ds(3 - 3 * c, near)] = f_ref[pl.ds((half - 3) * c, near)]
    xw_ref[pl.ds(near * c, 3)] = halo_ref[...]
    w1 = [
        jnp.concatenate(
            [jnp.concatenate([w1a_ref[i, j], w1b_ref[i, j]], axis=1) for j in range(3)], axis=1
        )
        for i in range(3)
    ]
    w1 = jnp.concatenate(w1, axis=0)
    chans = w1.shape[1] // 3
    b1 = b1_ref[...]

    def conv1(h, carry):
        lhs = jnp.concatenate([xw_ref[h], xw_ref[h + 1], xw_ref[h + 2]], axis=1)
        y = dot(lhs, w1)
        pre = shift_cells(y[:, :chans], 1) + y[:, chans : 2 * chans] + shift_cells(y[:, 2 * chans :], -1) + b1
        row = first + h - 2
        inside = jnp.logical_and(row >= 0, row < total)
        hid_ref[h] = jnp.where(inside, jnp.maximum(pre, 0.0), 0.0).astype(BF16)
        return carry

    lax.fori_loop(0, half + 4, conv1, 0)

    lane = lax.broadcasted_iota(jnp.int32, (1, LANES), 1)
    kind = (lane % CLASSES + 1).astype(F32)
    real = lane < LOGITS
    anchor = lax.broadcasted_iota(jnp.int32, (ANCH, LANES), 0)
    column = lax.broadcasted_iota(jnp.int32, (ANCH, LANES), 1)
    spread = jnp.where(jnp.logical_and(column // CLASSES == anchor, column < LOGITS), 1.0, 0.0).astype(BF16)
    w2n = [jnp.concatenate([w2_ref[i, j] for j in range(3)], axis=1) for i in range(3)]
    w2n = jnp.concatenate(w2n, axis=0)
    b2 = b2_ref[...]
    inverse = 1.0 / jnp.full((1, LANES), count_ref[0], F32)

    def focal(l, carry):
        gcb, loss = carry
        lhs = jnp.concatenate([hid_ref[l], hid_ref[l + 1], hid_ref[l + 2]], axis=1)
        y = dot(lhs, w2n)
        z = shift_cells(y[:, :LANES], 1) + y[:, LANES : 2 * LANES] + shift_cells(y[:, 2 * LANES :], -1) + b2
        at_halo = jnp.where(c == 0, l == 0, l == half + 1)
        local = jnp.clip(l - 1 + half * c, 0, 2 * half - 1)
        mine = lab_ref[local]
        lab9 = jnp.where(at_halo, hlab_ref[...], mine)
        lab = dot(lab9, spread)
        hit = lab == kind
        keep = jnp.logical_and(lab >= 0.0, real)
        u = jnp.where(hit, -z, z)
        e = jnp.exp(-jnp.abs(u))
        r = 1.0 / (1.0 + e)
        er = e * r
        up = u >= 0.0
        s = jnp.where(up, r, er)
        comp = jnp.where(up, er, r)
        soft = jnp.maximum(u, 0.0) + jnp.log1p(e)
        ws = jnp.where(keep, jnp.where(hit, 0.25, 0.75), 0.0) * s * s
        slope = ws * (2.0 * comp * soft + s)
        dz = jnp.where(hit, -slope, slope) * inverse
        d16 = dz.astype(BF16)
        dlog_ref[l] = d16
        own = jnp.logical_and(l >= 1, l <= half)
        weight = jnp.where(own, 1.0, 0.0)
        gcb = gcb + weight * jnp.sum(dz, axis=0, keepdims=True)
        loss = loss + weight * jnp.sum(ws * soft, axis=0, keepdims=True)

        @pl.when(own)
        def _():
            turned = jnp.transpose(d16.astype(F32))[:CLS_ROWS]
            cell = lax.broadcasted_iota(jnp.int32, turned.shape, 1)
            left = jnp.where(cell == cols - 1, 0.0, pltpu.roll(turned, cols - 1, axis=1))
            right = jnp.where(cell == 0, 0.0, pltpu.roll(turned, 1, axis=1))
            dt_ref[l - 1] = jnp.concatenate([left, turned, right], axis=0).astype(BF16)

        return gcb, loss

    zero = jnp.zeros((1, LANES), F32)
    gcb, loss = lax.fori_loop(0, half + 2, focal, (zero, zero))

    dt = jnp.concatenate([dt_ref[d] for d in range(half)], axis=1)
    for i in range(3):
        rows = hid_ref[i + 1 : i + 1 + half].reshape(half * cols, chans)
        gcls_ref[i] = dot(dt, rows)

    w2t = [jnp.concatenate([w2_ref[i, j] for i in range(3)], axis=1) for j in range(3)]
    w2t = jnp.concatenate(w2t, axis=0)

    def dpre_row(d, gsb):
        lhs = jnp.concatenate([dlog_ref[d + 2], dlog_ref[d + 1], dlog_ref[d]], axis=1)
        q = dot(lhs, w2t, ((1,), (1,)))
        dhid = shift_cells(q[:, :chans], -1) + q[:, chans : 2 * chans] + shift_cells(q[:, 2 * chans :], 1)
        dpre = jnp.where(hid_ref[d + 2].astype(F32) > 0.0, dhid, 0.0)
        d16 = dpre.astype(BF16)
        own_ref[d] = d16[:, : chans // 2]
        other_ref[d] = d16[:, chans // 2 :]
        return gsb + jnp.sum(dpre, axis=0, keepdims=True)

    gsb = lax.fori_loop(0, half, dpre_row, jnp.zeros((1, chans), F32))
    small_ref[0:1] = gcb
    small_ref[1:2] = jnp.broadcast_to(jnp.sum(loss, axis=1, keepdims=True), (1, LANES)) * inverse
    small_ref[2:3] = jnp.zeros((1, LANES), F32)
    small_ref[3:4] = gsb[:, : chans // 2]
    small_ref[4:5] = gsb[:, chans // 2 :]
    small_ref[5:8] = jnp.zeros((3, LANES), F32)


def shared_kernel(where_ref, f_ref, before_ref, after_ref, own_ref, other_ref, out_ref, x_ref, d_ref):
    rows, cols, chans = f_ref.shape
    half = rows // 2
    c = where_ref[0]
    x_ref[0] = before_ref[...]
    x_ref[1 : rows + 1] = f_ref[...]
    x_ref[rows + 1] = after_ref[...]

    def place(ref, start):
        def body(d, carry):
            mid = ref[d].astype(F32)
            d_ref[start + d] = jnp.concatenate(
                [shift_cells(mid, -1).astype(BF16), ref[d], shift_cells(mid, 1).astype(BF16)], axis=1
            )
            return carry

        lax.fori_loop(0, half, body, 0)

    place(own_ref, half * c)
    place(other_ref, half * (1 - c))
    rhs = d_ref[...].reshape(rows * cols, d_ref.shape[2])
    outs = rhs.shape[1] // 3
    for i in range(3):
        lhs = x_ref[i : i + rows].reshape(rows * cols, chans)
        g = dot(lhs, rhs, ((0,), (0,)))
        for j in range(3):
            out_ref[i, j] = g[:, j * outs : (j + 1) * outs]


def swap(x, axis, bit):
    size = lax.axis_size(axis)
    return lax.ppermute(x, axis, [(i, i ^ bit) for i in range(size)])


def piece(x, index, size):
    return lax.dynamic_slice_in_dim(x, index * size, size, axis=0)


def scatter_sum(x, axis):
    size = lax.axis_size(axis)
    me = lax.axis_index(axis)
    rows = x.shape[0] // size
    total = piece(x, me, rows)
    for bit in range(1, size):
        total = total + swap(piece(x, me ^ bit, rows).astype(BF16), axis, bit).astype(F32)
    return total


def gather(x, axis):
    size = lax.axis_size(axis)
    me = lax.axis_index(axis)
    rows = x.shape[0]
    whole = jnp.zeros((rows * size,) + x.shape[1:], x.dtype)
    whole = lax.dynamic_update_slice_in_dim(whole, x, me * rows, axis=0)
    for bit in range(1, size):
        whole = lax.dynamic_update_slice_in_dim(whole, swap(x, axis, bit), (me ^ bit) * rows, axis=0)
    return whole


def sum_all(x, axis):
    size = lax.axis_size(axis)
    parts = [x] + [swap(x, axis, bit) for bit in range(1, size)]
    while len(parts) > 1:
        parts = [parts[k] + parts[k + 1] for k in range(0, len(parts), 2)]
    return parts[0]


def shards(features, labels, w_shared, b_shared, w_cls, b_cls):
    _, rows, cols, chans = features.shape
    half = rows // 2
    outs = w_shared.shape[3]
    tiles = lax.axis_size("tile")
    c = lax.axis_index("chan")
    t = lax.axis_index("tile")
    f = features[0]

    pairs = []
    for i in range(tiles - 1):
        pairs += [(2 * i + 1, 2 * i + 2), (2 * i + 2, 2 * i + 1)]
    line = ("tile", "chan")
    lab_edge = lax.dynamic_slice_in_dim(labels[0], (rows - 1) * c, 1, axis=0)
    halo = lax.ppermute(lax.dynamic_slice_in_dim(f, (rows - 3) * c, 3, axis=0), line, pairs)
    hlab = lax.ppermute(lab_edge, line, pairs)
    count = jnp.full((8, LANES), jnp.sum((labels > 0).astype(F32)), F32)
    count = sum_all(sum_all(count, "batch"), "tile")[0, :1]
    w1b = swap(w_shared, "chan", 1)
    w2b = swap(w_cls, "chan", 1)
    b1b = swap(b_shared, "chan", 1)

    at_edge = jnp.where(c == 0, t == 0, t == tiles - 1)
    hlab = jnp.where(at_edge, -1, hlab).astype(BF16).reshape(cols, ANCH)
    lab = labels[0].astype(BF16).reshape(rows, cols, ANCH)
    b1 = jnp.concatenate([b_shared, b1b]).reshape(1, 2 * outs)
    w2 = jnp.pad(jnp.concatenate([w_cls, w2b], axis=2), ((0, 0), (0, 0), (0, 0), (0, LANES - LOGITS)))
    b2 = jnp.pad(b_cls, (0, LANES - LOGITS)).reshape(1, LANES)
    where = jnp.stack([c, t * rows + half * c, tiles * rows]).astype(jnp.int32)

    vmem = pl.BlockSpec(memory_space=pltpu.VMEM)
    smem = pl.BlockSpec(memory_space=pltpu.SMEM)
    gcls, own, other, small = pl.pallas_call(
        head_kernel,
        in_specs=[smem, smem] + [vmem] * 9,
        out_specs=[vmem] * 4,
        out_shape=[
            jax.ShapeDtypeStruct((3, 3 * CLS_ROWS, chans), F32),
            jax.ShapeDtypeStruct((half, cols, outs), BF16),
            jax.ShapeDtypeStruct((half, cols, outs), BF16),
            jax.ShapeDtypeStruct((8, LANES), F32),
        ],
        scratch_shapes=[
            pltpu.VMEM((half + 6, cols, chans), BF16),
            pltpu.VMEM((half + 4, cols, chans), BF16),
            pltpu.VMEM((half + 2, cols, LANES), BF16),
            pltpu.VMEM((half, 3 * CLS_ROWS, cols), BF16),
        ],
        compiler_params=pltpu.CompilerParams(vmem_limit_bytes=50 * 1024 * 1024),
        name="head",
    )(where, count, f, halo, lab, hlab, w_shared, w1b, b1, w2, b2)

    theirs = swap(other, "chan", 1)
    near = lax.dynamic_index_in_dim(halo, 2 - 2 * c, axis=0, keepdims=False)
    far = swap(near, "chan", 1)
    before = jnp.where(c == 0, near, far)
    after = jnp.where(c == 0, far, near)
    gsh = pl.pallas_call(
        shared_kernel,
        in_specs=[smem] + [vmem] * 5,
        out_specs=vmem,
        out_shape=jax.ShapeDtypeStruct((3, 3, chans, outs), F32),
        scratch_shapes=[
            pltpu.VMEM((rows + 2, cols, chans), BF16),
            pltpu.VMEM((rows, cols, 3 * outs), BF16),
        ],
        compiler_params=pltpu.CompilerParams(vmem_limit_bytes=50 * 1024 * 1024),
        name="shared",
    )(where, f, before, after, own, theirs)

    gcls = gcls.reshape(9 * CLS_ROWS, chans)
    gcls = gcls[:, :outs] + swap(gcls[:, outs:], "chan", 1)
    gcls = jnp.pad(gcls, ((0, 1024 - 9 * CLS_ROWS), (0, 0)))
    far_small = swap(jnp.concatenate([small[0:3], small[4:5], small[3:4], small[5:8]]), "chan", 1)
    small = small + far_small
    small = sum_all(sum_all(small, "batch"), "tile")

    def reduced(x):
        share = scatter_sum(scatter_sum(x, "batch"), "tile").astype(BF16)
        return gather(gather(share, "tile"), "batch").astype(F32)

    gcls = reduced(gcls)[: 9 * CLS_ROWS].reshape(9, CLS_ROWS, outs)
    grad_cls = jnp.swapaxes(gcls, 1, 2)[:, :, :LOGITS].reshape(3, 3, outs, LOGITS)
    grad_shared = reduced(gsh.reshape(9 * chans, outs)).reshape(3, 3, chans, outs)
    return (
        grad_shared,
        small[3],
        grad_cls,
        small[0, :LOGITS],
        small[1, :1],
    )


def solution(mesh):
    placed = (
        P(("groups", "batch"), "tile", None, None),
        P(("groups", "batch"), "tile", None),
        P(None, None, None, "chan"),
        P("chan"),
        P(None, None, "chan", None),
        P(),
    )
    return jax.shard_map(
        shards,
        mesh=mesh,
        in_specs=placed,
        out_specs=(
            P("groups", None, None, "chan"),
            P(("groups", "chan")),
            P("groups", None, "chan", None),
            P("groups"),
            P("groups"),
        ),
        check_vma=False,
    )
```

profile of v0, /device:TPU:0, one launch (start us, length us, event | category | flops | bytes accessed | tf_op | source)
XLA Modules:
  0.0 109.4 jit_solution(6820924320796957047)
XLA Ops:
  0.6 0.7 dynamic-slice_bitcast_fusion.2
  1.4 0.7 collective-permute-start.6
  2.1 1.7 %fusion.5 = f32[]{:T(128)} fusion(s32[1,12,2304]{2,0,1:T(1,128)} %param.7), kind=kLoop, calls=%fused_computation.20 | loop fusion | flops 82943 | bytes 110596 | tf_op jit(solution)/shard_map/reduce_sum | solution.py:229
  3.8 0.6 broadcast_in_dim.21
  4.4 3.0 %collective-permute-start.2 = (f32[8,128]{1,0:T(8,128)S(1)}, f32[8,128]{1,0:T(8,128)S(1)}, u32[]{:S(2)}, u32[]{:S(2)}) collective-permute-start(f32[8,128]{1,0:T(8,128)S(1)} %broadcast_in_dim.21), channel_id=1, source_target_pairs={{0,2},{2,0},{1,3},{3,1},{4,6},{6,4},{5,7},{7,5},{8,10},{10,8},{9,1... | collective-permute-start | bytes 12296 | tf_op jit(solution)/shard_map/ppermute | solution.py:177
  7.4 2.7 %collective-permute-start.7 = (bf16[3,3,256,128]{3,2,1,0:T(8,128)(2,1)}, bf16[3,3,256,128]{3,2,1,0:T(8,128)(2,1)S(1)}, u32[]{:S(2)}, u32[]{:S(2)}) collective-permute-start(bf16[3,3,256,128]{3,2,1,0:T(8,128)(2,1)} %w1a_ref.1), channel_id=1, source_target_pairs={{0,1},{1,0},{2,3},{3,2},{4,5},{5,4},{6,7},{7,6},{8,9},{9,8},{10,11... | collective-permute-start | bytes 1769480 | tf_op jit(solution)/shard_map/ppermute | solution.py:177
  10.1 1.2 %convert_reduce_fusion = bf16[12,2304]{1,0:T(8,128)(2,1)S(1)} fusion(s32[1,12,2304]{2,0,1:T(1,128)} %param.7), kind=kLoop, calls=%fused_computation.21 | loop fusion | flops 27648 | bytes 165888 | tf_op jit(solution)/shard_map/convert_element_type | solution.py:237
  11.3 0.7 pad_bitcast_fusion.b2_ref
  12.0 1.0 dynamic-slice_bitcast_fusion
  13.0 0.1 pad_add_fusion.where_ref
  13.1 0.2 copy.14
  13.3 1.6 %convert_element_type.77.lab_ref = bf16[12,256,9]{2,1,0:T(8,128)(2,1)S(1)} reshape(bf16[12,2304]{1,0:T(8,128)(2,1)S(1)} %convert_reduce_fusion) | data formatting | bytes 110592 | tf_op jit(solution)/shard_map/convert_element_type | solution.py:237
  15.0 0.7 broadcast_add_fusion
  15.6 1.6 %collective-permute-start.3 = (f32[8,128]{1,0:T(8,128)S(1)}, f32[8,128]{1,0:T(8,128)S(1)}, u32[]{:S(2)}, u32[]{:S(2)}) collective-permute-start(f32[8,128]{1,0:T(8,128)S(1)} %broadcast_add_fusion), channel_id=1, source_target_pairs={{0,4},{4,0},{8,12},{12,8},{1,5},{5,1},{9,13},{13,9},{2,6},{6,2},{1... | collective-permute-start | bytes 12296 | tf_op jit(solution)/shard_map/ppermute | solution.py:177
  17.3 1.7 %collective-permute-start.4 = (f32[8,128]{1,0:T(8,128)S(1)}, f32[8,128]{1,0:T(8,128)S(1)}, u32[]{:S(2)}, u32[]{:S(2)}) collective-permute-start(f32[8,128]{1,0:T(8,128)S(1)} %broadcast_add_fusion), channel_id=1, source_target_pairs={{0,8},{4,12},{8,0},{12,4},{1,9},{5,13},{9,1},{13,5},{2,10},{6,14},... | collective-permute-start | bytes 12296 | tf_op jit(solution)/shard_map/ppermute | solution.py:177
  19.0 1.1 %collective-permute-start.5 = (f32[8,128]{1,0:T(8,128)S(1)}, f32[8,128]{1,0:T(8,128)S(1)}, u32[]{:S(2)}, u32[]{:S(2)}) collective-permute-start(f32[8,128]{1,0:T(8,128)S(1)} %broadcast_add_fusion), channel_id=1, source_target_pairs={{0,12},{4,8},{8,4},{12,0},{1,13},{5,9},{9,5},{13,1},{2,14},{6,10},... | collective-permute-start | bytes 12296 | tf_op jit(solution)/shard_map/ppermute | solution.py:177
  20.1 0.7 collective-permute-start
  20.8 1.0 collective-permute-done.4
  21.8 1.2 %collective-permute-start.9 = (bf16[3,3,128,99]{3,2,1,0:T(8,128)(2,1)S(1)}, bf16[3,3,128,99]{3,2,1,0:T(8,128)(2,1)}, u32[]{:S(2)}, u32[]{:S(2)}) collective-permute-start(bf16[3,3,128,99]{3,2,1,0:T(8,128)(2,1)S(1)} %copy.14), channel_id=1, source_target_pairs={{0,1},{1,0},{2,3},{3,2},{4,5},{5,4},{6,7},{7,6},{8,9},{9,8},{10,11... | collective-permute-start | bytes 684296 | tf_op jit(solution)/shard_map/ppermute | solution.py:177
  23.0 1.4 %collective-permute-done.5 = f32[8,128]{1,0:T(8,128)S(1)} collective-permute-done((f32[8,128]{1,0:T(8,128)S(1)}, f32[8,128]{1,0:T(8,128)S(1)}, u32[]{:S(2)}, u32[]{:S(2)}) %collective-permute-start.5) | collective-permute-done | bytes 4128 | tf_op jit(solution)/shard_map/ppermute | solution.py:177
  24.4 0.7 add_add_fusion.1
  25.0 0.5 slice.38
  25.6 0.2 reshape.46.hlab_ref
  25.8 1.2 %fusion.2.w2_ref = bf16[3,3,256,128]{3,2,1,0:T(8,128)(2,1)S(1)} fusion(bf16[3,3,128,99]{3,2,1,0:T(8,128)(2,1)} %collective-permute-done.9, bf16[3,3,128,99]{3,2,1,0:T(8,128)(2,1)S(1)} %copy.14), kind=kLoop, calls=%fused_computation.3 | loop fusion | flops 2064384 | bytes 1046016 | tf_op jit(solution)/shard_map/concatenate | solution.py:239
  27.0 1.9 %collective-permute-start.1 = (bf16[256,256]{1,0:T(8,128)(2,1)S(1)}, bf16[256,256]{1,0:T(8,128)(2,1)}, u32[]{:S(2)}, u32[]{:S(2)}) collective-permute-start(bf16[256,256]{1,0:T(8,128)(2,1)S(1)} %dynamic-slice_bitcast_fusion.1), channel_id=1, source_target_pairs={{0,1},{1,0},{2,3},{3,2},{4,5},{5,4},{6,7},{7,6},{8,9},{9,8},{10,11... | collective-permute-start | bytes 393224 | tf_op jit(solution)/shard_map/ppermute | solution.py:177
  29.0 16.9 %head.1 = (f32[3,336,256]{2,1,0:T(8,128)}, bf16[6,256,128]{2,1,0:T(8,128)(2,1)S(1)}, bf16[6,256,128]{2,1,0:T(8,128)(2,1)S(1)}, f32[8,128]{1,0:T(8,128)S(1)}) custom-call(s32[3]{0:T(128)S(1)} %pad_add_fusion.where_ref, f32[1]{0:T(128)} %bitcast.5.count_ref, bf16[12,256,256]{2,1,0:T(8,128)(2,1)} %bitcast.29, ...), custom_call_target="tpu_custom_call" | custom-call | tf_op jit(solution)/shard_map/head/pallas_call | solution.py:245
  45.9 0.1 collective-permute-start.19
  46.0 1.1 %collective-permute-done.19 = f32[8,128]{1,0:T(8,128)S(1)} collective-permute-done((f32[8,128]{1,0:T(8,128)S(1)}, f32[8,128]{1,0:T(8,128)S(1)}, u32[]{:S(2)}, u32[]{:S(2)}) %collective-permute-start.19) | collective-permute-done | bytes 4128 | tf_op jit(solution)/shard_map/ppermute | solution.py:177
  47.1 0.5 collective-permute-start.20
  47.6 1.1 slice.51
  48.8 1.9 %collective-permute-done.20 = f32[8,128]{1,0:T(8,128)S(1)} collective-permute-done((f32[8,128]{1,0:T(8,128)S(1)}, f32[8,128]{1,0:T(8,128)S(1)}, u32[]{:S(2)}, u32[]{:S(2)}) %collective-permute-start.20) | collective-permute-done | bytes 4128 | tf_op jit(solution)/shard_map/ppermute | solution.py:177
  50.7 1.3 %collective-permute-start.21 = (f32[8,128]{1,0:T(8,128)S(1)}, f32[8,128]{1,0:T(8,128)S(1)}, u32[]{:S(2)}, u32[]{:S(2)}) collective-permute-start(f32[8,128]{1,0:T(8,128)S(1)} %add.141), channel_id=1, source_target_pairs={{0,4},{4,0},{8,12},{12,8},{1,5},{5,1},{9,13},{13,9},{2,6},{6,2},{1... | collective-permute-start | bytes 12296 | tf_op jit(solution)/shard_map/ppermute | solution.py:177
  52.0 2.5 %collective-permute-start.22 = (f32[8,128]{1,0:T(8,128)S(1)}, f32[8,128]{1,0:T(8,128)S(1)}, u32[]{:S(2)}, u32[]{:S(2)}) collective-permute-start(f32[8,128]{1,0:T(8,128)S(1)} %add.141), channel_id=1, source_target_pairs={{0,8},{4,12},{8,0},{12,4},{1,9},{5,13},{9,1},{13,5},{2,10},{6,14},... | collective-permute-start | bytes 12296 | tf_op jit(solution)/shard_map/ppermute | solution.py:177
  54.5 0.6 collective-permute-start.23
  55.1 0.9 broadcast_select_fusion
  56.1 0.4 collective-permute-done.22
  56.5 3.4 %collective-permute-done.23 = f32[8,128]{1,0:T(8,128)S(1)} collective-permute-done((f32[8,128]{1,0:T(8,128)S(1)}, f32[8,128]{1,0:T(8,128)S(1)}, u32[]{:S(2)}, u32[]{:S(2)}) %collective-permute-start.23) | collective-permute-done | bytes 4128 | tf_op jit(solution)/shard_map/ppermute | solution.py:177
  59.9 0.5 slice_bitcast_fusion
  60.4 3.8 %shared.1 = f32[3,3,256,128]{3,2,1,0:T(8,128)S(1)} custom-call(s32[3]{0:T(128)S(1)} %pad_add_fusion.where_ref, bf16[12,256,256]{2,1,0:T(8,128)(2,1)S(1)} %bitcast.30, bf16[256,256]{1,0:T(8,128)(2,1)S(1)} %get-tuple-element.24.before_ref, bf16[256,256]{1,0:T(8,128)(2,1)S(1)} %get-tuple-element.23.after_ref, ...), custom_call_target="tpu_custom_call" | custom-call | tf_op jit(solution)/shard_map/shared/pallas_call | solution.py:270
  64.4 0.6 collective-permute-start.25
  65.0 1.6 %collective-permute-start.11 = (bf16[1152,128]{1,0:T(8,128)(2,1)S(1)}, bf16[1152,128]{1,0:T(8,128)(2,1)S(1)}, u32[]{:S(2)}, u32[]{:S(2)}) collective-permute-start(bf16[1152,128]{1,0:T(8,128)(2,1)S(1)} %dynamic-slice_convert_fusion), channel_id=1, source_target_pairs={{0,2},{2,0},{1,3},{3,1},{4,6},{6,4},{5,7},{7,5},{8,10},{10,8},{9,1... | collective-permute-start | bytes 884744 | tf_op jit(solution)/shard_map/ppermute | solution.py:177
  66.5 4.0 %collective-permute-done.25 = bf16[512,128]{1,0:T(8,128)(2,1)S(1)} collective-permute-done((bf16[512,128]{1,0:T(8,128)(2,1)S(1)}, bf16[512,128]{1,0:T(8,128)(2,1)S(1)}, u32[]{:S(2)}, u32[]{:S(2)}) %collective-permute-start.25) | collective-permute-done | bytes 131104 | tf_op jit(solution)/shard_map/ppermute | solution.py:177
  70.7 1.4 %collective-permute-start.27 = (bf16[128,128]{1,0:T(8,128)(2,1)S(1)}, bf16[128,128]{1,0:T(8,128)(2,1)S(1)}, u32[]{:S(2)}, u32[]{:S(2)}) collective-permute-start(bf16[128,128]{1,0:T(8,128)(2,1)S(1)} %get-tuple-element.22), channel_id=1, source_target_pairs={{0,8},{4,12},{8,0},{12,4},{1,9},{5,13},{9,1},{13,5},{2,10},{6,14},... | collective-permute-start | bytes 98312 | tf_op jit(solution)/shard_map/ppermute | solution.py:177
  72.1 3.0 %collective-permute-start.28 = (bf16[128,128]{1,0:T(8,128)(2,1)S(1)}, bf16[128,128]{1,0:T(8,128)(2,1)S(1)}, u32[]{:S(2)}, u32[]{:S(2)}) collective-permute-start(bf16[128,128]{1,0:T(8,128)(2,1)S(1)} %get-tuple-element.21), channel_id=1, source_target_pairs={{0,12},{4,8},{8,4},{12,0},{1,13},{5,9},{9,5},{13,1},{2,14},{6,10},... | collective-permute-start | bytes 98312 | tf_op jit(solution)/shard_map/ppermute | solution.py:177
  75.0 0.5 slice_bitcast_fusion.1
  75.5 0.5 slice.49
  76.1 1.8 %collective-permute-done.28 = bf16[128,128]{1,0:T(8,128)(2,1)S(1)} collective-permute-done((bf16[128,128]{1,0:T(8,128)(2,1)S(1)}, bf16[128,128]{1,0:T(8,128)(2,1)S(1)}, u32[]{:S(2)}, u32[]{:S(2)}) %collective-permute-start.28) | collective-permute-done | bytes 32800 | tf_op jit(solution)/shard_map/ppermute | solution.py:177
  78.0 3.5 %collective-permute-start.30 = (bf16[128,128]{1,0:T(8,128)(2,1)S(1)}, bf16[128,128]{1,0:T(8,128)(2,1)S(1)}, u32[]{:S(2)}, u32[]{:S(2)}) collective-permute-start(bf16[128,128]{1,0:T(8,128)(2,1)S(1)} %get-tuple-element.14), channel_id=1, source_target_pairs={{0,8},{4,12},{8,0},{12,4},{1,9},{5,13},{9,1},{13,5},{2,10},{6,14},... | collective-permute-start | bytes 98312 | tf_op jit(solution)/shard_map/ppermute | solution.py:177
  81.5 0.9 collective-permute-start.31
  82.6 3.5 %collective-permute-start.13 = (bf16[288,128]{1,0:T(8,128)(2,1)S(1)}, bf16[288,128]{1,0:T(8,128)(2,1)S(1)}, u32[]{:S(2)}, u32[]{:S(2)}) collective-permute-start(bf16[288,128]{1,0:T(8,128)(2,1)S(1)} %get-tuple-element.19), channel_id=1, source_target_pairs={{0,8},{4,12},{8,0},{12,4},{1,9},{5,13},{9,1},{13,5},{2,10},{6,14},... | collective-permute-start | bytes 221192 | tf_op jit(solution)/shard_map/ppermute | solution.py:177
  86.1 0.9 collective-permute-start.14
  87.0 0.3 collective-permute-done.31
  87.3 0.7 collective-permute-start.32
  88.0 0.7 collective-permute-done.13
  88.7 3.6 %collective-permute-done.14 = bf16[288,128]{1,0:T(8,128)(2,1)S(1)} collective-permute-done((bf16[288,128]{1,0:T(8,128)(2,1)S(1)}, bf16[288,128]{1,0:T(8,128)(2,1)S(1)}, u32[]{:S(2)}, u32[]{:S(2)}) %collective-permute-start.14) | collective-permute-done | bytes 73760 | tf_op jit(solution)/shard_map/ppermute | solution.py:177
  92.5 2.8 %collective-permute-start.16 = (bf16[288,128]{1,0:T(8,128)(2,1)S(1)}, bf16[288,128]{1,0:T(8,128)(2,1)S(1)}, u32[]{:S(2)}, u32[]{:S(2)}) collective-permute-start(bf16[288,128]{1,0:T(8,128)(2,1)S(1)} %get-tuple-element.16), channel_id=1, source_target_pairs={{0,8},{4,12},{8,0},{12,4},{1,9},{5,13},{9,1},{13,5},{2,10},{6,14},... | collective-permute-start | bytes 221192 | tf_op jit(solution)/shard_map/ppermute | solution.py:177
  95.3 1.6 %collective-permute-start.17 = (bf16[288,128]{1,0:T(8,128)(2,1)S(1)}, bf16[288,128]{1,0:T(8,128)(2,1)S(1)}, u32[]{:S(2)}, u32[]{:S(2)}) collective-permute-start(bf16[288,128]{1,0:T(8,128)(2,1)S(1)} %get-tuple-element.16), channel_id=1, source_target_pairs={{0,12},{4,8},{8,4},{12,0},{1,13},{5,9},{9,5},{13,1},{2,14},{6,10},... | collective-permute-start | bytes 221192 | tf_op jit(solution)/shard_map/ppermute | solution.py:177
  96.9 0.9 collective-permute-done.16
  97.8 3.6 %collective-permute-done.17 = bf16[288,128]{1,0:T(8,128)(2,1)S(1)} collective-permute-done((bf16[288,128]{1,0:T(8,128)(2,1)S(1)}, bf16[288,128]{1,0:T(8,128)(2,1)S(1)}, u32[]{:S(2)}, u32[]{:S(2)}) %collective-permute-start.17) | collective-permute-done | bytes 73760 | tf_op jit(solution)/shard_map/ppermute | solution.py:177
  101.5 0.2 collective-permute-start.18
  101.6 0.1 broadcast_in_dim.19
  101.8 0.8 convert.7
  102.7 5.6 %collective-permute-done.18 = bf16[1152,128]{1,0:T(8,128)(2,1)S(1)} collective-permute-done((bf16[1152,128]{1,0:T(8,128)(2,1)S(1)}, bf16[1152,128]{1,0:T(8,128)(2,1)S(1)}, u32[]{:S(2)}, u32[]{:S(2)}) %collective-permute-start.18) | collective-permute-done | bytes 294944 | tf_op jit(solution)/shard_map/ppermute | solution.py:177
  108.3 1.1 %convert.6 = f32[3,3,256,128]{3,2,1,0:T(8,128)} convert(bf16[3,3,256,128]{3,2,1,0:T(8,128)(2,1)S(1)} %bitcast.34) | non-fusion elementwise | flops 294912 | bytes 1769472 | tf_op jit(solution)/shard_map/reshape | solution.py:296
  (69 shorter events, 1.3 us)
Async XLA Ops:
  0.6 12.4 %copy-start.3 = (bf16[3,3,128,99]{2,3,1,0:T(8,128)(2,1)S(1)}, bf16[3,3,128,99]{2,3,1,0:T(8,128)(2,1)}, u32[]{:S(2)}) copy-start(bf16[3,3,128,99]{2,3,1,0:T(8,128)(2,1)} %param.10) | copy-start | bytes 684292
  1.4 24.2 %collective-permute-start.6 = (s32[1,2304]{1,0:T(1,128)S(1)}, s32[1,2304]{1,0:T(1,128)S(1)}, u32[]{:S(2)}, u32[]{:S(2)}) collective-permute-start(s32[1,2304]{1,0:T(1,128)S(1)} %dynamic-slice_bitcast_fusion.2), channel_id=1, source_target_pairs={{1,4},{4,1},{5,8},{8,5},{9,12},{12,9},{3,6},{6,3},{7,10},{10,7},{1... | collective-permute-start | bytes 27656 | tf_op jit(solution)/shard_map/ppermute | solution.py:228
  4.4 10.5 %collective-permute-start.2 = (f32[8,128]{1,0:T(8,128)S(1)}, f32[8,128]{1,0:T(8,128)S(1)}, u32[]{:S(2)}, u32[]{:S(2)}) collective-permute-start(f32[8,128]{1,0:T(8,128)S(1)} %broadcast_in_dim.21), channel_id=1, source_target_pairs={{0,2},{2,0},{1,3},{3,1},{4,6},{6,4},{5,7},{7,5},{8,10},{10,8},{9,1... | collective-permute-start | bytes 12296 | tf_op jit(solution)/shard_map/ppermute | solution.py:177
  7.4 21.5 %collective-permute-start.7 = (bf16[3,3,256,128]{3,2,1,0:T(8,128)(2,1)}, bf16[3,3,256,128]{3,2,1,0:T(8,128)(2,1)S(1)}, u32[]{:S(2)}, u32[]{:S(2)}) collective-permute-start(bf16[3,3,256,128]{3,2,1,0:T(8,128)(2,1)} %w1a_ref.1), channel_id=1, source_target_pairs={{0,1},{1,0},{2,3},{3,2},{4,5},{5,4},{6,7},{7,6},{8,9},{9,8},{10,11... | collective-permute-start | bytes 1769480 | tf_op jit(solution)/shard_map/ppermute | solution.py:177
  10.1 8.9 %collective-permute-start.8 = (f32[128]{0:T(128)}, f32[128]{0:T(128)S(1)}, u32[]{:S(2)}, u32[]{:S(2)}) collective-permute-start(f32[128]{0:T(128)} %param.9), channel_id=1, source_target_pairs={{0,1},{1,0},{2,3},{3,2},{4,5},{5,4},{6,7},{7,6},{8,9},{9,8},{10,11... | collective-permute-start | bytes 1544 | tf_op jit(solution)/shard_map/ppermute | solution.py:177
  10.1 10.0 %copy-start.4 = (f32[128]{0:T(128)S(1)}, f32[128]{0:T(128)}, u32[]{:S(2)}) copy-start(f32[128]{0:T(128)} %param.9) | copy-start | bytes 1540
  13.3 15.7 %copy-start.1 = (bf16[3,3,256,128]{3,2,1,0:T(8,128)(2,1)S(1)}, bf16[3,3,256,128]{3,2,1,0:T(8,128)(2,1)}, u32[]{:S(2)}) copy-start(bf16[3,3,256,128]{3,2,1,0:T(8,128)(2,1)} %w1a_ref.1) | copy-start | bytes 1769476
  15.6 4.5 %collective-permute-start.3 = (f32[8,128]{1,0:T(8,128)S(1)}, f32[8,128]{1,0:T(8,128)S(1)}, u32[]{:S(2)}, u32[]{:S(2)}) collective-permute-start(f32[8,128]{1,0:T(8,128)S(1)} %broadcast_add_fusion), channel_id=1, source_target_pairs={{0,4},{4,0},{8,12},{12,8},{1,5},{5,1},{9,13},{13,9},{2,6},{6,2},{1... | collective-permute-start | bytes 12296 | tf_op jit(solution)/shard_map/ppermute | solution.py:177
  17.3 4.5 %collective-permute-start.4 = (f32[8,128]{1,0:T(8,128)S(1)}, f32[8,128]{1,0:T(8,128)S(1)}, u32[]{:S(2)}, u32[]{:S(2)}) collective-permute-start(f32[8,128]{1,0:T(8,128)S(1)} %broadcast_add_fusion), channel_id=1, source_target_pairs={{0,8},{4,12},{8,0},{12,4},{1,9},{5,13},{9,1},{13,5},{2,10},{6,14},... | collective-permute-start | bytes 12296 | tf_op jit(solution)/shard_map/ppermute | solution.py:177
  19.0 5.4 %collective-permute-start.5 = (f32[8,128]{1,0:T(8,128)S(1)}, f32[8,128]{1,0:T(8,128)S(1)}, u32[]{:S(2)}, u32[]{:S(2)}) collective-permute-start(f32[8,128]{1,0:T(8,128)S(1)} %broadcast_add_fusion), channel_id=1, source_target_pairs={{0,12},{4,8},{8,4},{12,0},{1,13},{5,9},{9,5},{13,1},{2,14},{6,10},... | collective-permute-start | bytes 12296 | tf_op jit(solution)/shard_map/ppermute | solution.py:177
  20.1 6.9 %collective-permute-start = (bf16[3,256,256]{2,1,0:T(8,128)(2,1)S(1)}, bf16[3,256,256]{2,1,0:T(8,128)(2,1)S(1)}, u32[]{:S(2)}, u32[]{:S(2)}) collective-permute-start(bf16[3,256,256]{2,1,0:T(8,128)(2,1)S(1)} %dynamic-slice_bitcast_fusion), channel_id=1, source_target_pairs={{1,4},{4,1},{5,8},{8,5},{9,12},{12,9},{3,6},{6,3},{7,10},{10,7},{1... | collective-permute-start | bytes 1179656 | tf_op jit(solution)/shard_map/ppermute | solution.py:227
  21.8 4.0 %collective-permute-start.9 = (bf16[3,3,128,99]{3,2,1,0:T(8,128)(2,1)S(1)}, bf16[3,3,128,99]{3,2,1,0:T(8,128)(2,1)}, u32[]{:S(2)}, u32[]{:S(2)}) collective-permute-start(bf16[3,3,128,99]{3,2,1,0:T(8,128)(2,1)S(1)} %copy.14), channel_id=1, source_target_pairs={{0,1},{1,0},{2,3},{3,2},{4,5},{5,4},{6,7},{7,6},{8,9},{9,8},{10,11... | collective-permute-start | bytes 684296 | tf_op jit(solution)/shard_map/ppermute | solution.py:177
  27.0 28.0 %collective-permute-start.1 = (bf16[256,256]{1,0:T(8,128)(2,1)S(1)}, bf16[256,256]{1,0:T(8,128)(2,1)}, u32[]{:S(2)}, u32[]{:S(2)}) collective-permute-start(bf16[256,256]{1,0:T(8,128)(2,1)S(1)} %dynamic-slice_bitcast_fusion.1), channel_id=1, source_target_pairs={{0,1},{1,0},{2,3},{3,2},{4,5},{5,4},{6,7},{7,6},{8,9},{9,8},{10,11... | collective-permute-start | bytes 393224 | tf_op jit(solution)/shard_map/ppermute | solution.py:177
  45.8 14.6 %copy-start = (bf16[1,12,256,256]{3,2,1,0:T(8,128)(2,1)S(1)}, bf16[1,12,256,256]{3,2,1,0:T(8,128)(2,1)}, u32[]{:S(2)}) copy-start(bf16[1,12,256,256]{3,2,1,0:T(8,128)(2,1)} %param.6) | copy-start | bytes 4718596
  45.9 1.2 %collective-permute-start.19 = (f32[8,128]{1,0:T(8,128)S(1)}, f32[8,128]{1,0:T(8,128)S(1)}, u32[]{:S(2)}, u32[]{:S(2)}) collective-permute-start(f32[8,128]{1,0:T(8,128)S(1)} %pad_maximum_fusion), channel_id=1, source_target_pairs={{0,1},{1,0},{2,3},{3,2},{4,5},{5,4},{6,7},{7,6},{8,9},{9,8},{10,11... | collective-permute-start | bytes 12296 | tf_op jit(solution)/shard_map/ppermute | solution.py:177
  47.1 3.6 %collective-permute-start.20 = (f32[8,128]{1,0:T(8,128)S(1)}, f32[8,128]{1,0:T(8,128)S(1)}, u32[]{:S(2)}, u32[]{:S(2)}) collective-permute-start(f32[8,128]{1,0:T(8,128)S(1)} %add.140), channel_id=1, source_target_pairs={{0,2},{2,0},{1,3},{3,1},{4,6},{6,4},{5,7},{7,5},{8,10},{10,8},{9,1... | collective-permute-start | bytes 12296 | tf_op jit(solution)/shard_map/ppermute | solution.py:177
  48.7 15.6 %collective-permute-start.24 = (f32[1008,128]{1,0:T(8,128)S(1)}, f32[1008,128]{1,0:T(8,128)S(1)}, u32[]{:S(2)}, u32[]{:S(2)}) collective-permute-start(f32[1008,128]{1,0:T(8,128)S(1)} %slice.51), channel_id=1, source_target_pairs={{0,1},{1,0},{2,3},{3,2},{4,5},{5,4},{6,7},{7,6},{8,9},{9,8},{10,11... | collective-permute-start | bytes 1548296 | tf_op jit(solution)/shard_map/ppermute | solution.py:177
  50.7 5.4 %collective-permute-start.21 = (f32[8,128]{1,0:T(8,128)S(1)}, f32[8,128]{1,0:T(8,128)S(1)}, u32[]{:S(2)}, u32[]{:S(2)}) collective-permute-start(f32[8,128]{1,0:T(8,128)S(1)} %add.141), channel_id=1, source_target_pairs={{0,4},{4,0},{8,12},{12,8},{1,5},{5,1},{9,13},{13,9},{2,6},{6,2},{1... | collective-permute-start | bytes 12296 | tf_op jit(solution)/shard_map/ppermute | solution.py:177
  52.0 4.5 %collective-permute-start.22 = (f32[8,128]{1,0:T(8,128)S(1)}, f32[8,128]{1,0:T(8,128)S(1)}, u32[]{:S(2)}, u32[]{:S(2)}) collective-permute-start(f32[8,128]{1,0:T(8,128)S(1)} %add.141), channel_id=1, source_target_pairs={{0,8},{4,12},{8,0},{12,4},{1,9},{5,13},{9,1},{13,5},{2,10},{6,14},... | collective-permute-start | bytes 12296 | tf_op jit(solution)/shard_map/ppermute | solution.py:177
  54.5 5.4 %collective-permute-start.23 = (f32[8,128]{1,0:T(8,128)S(1)}, f32[8,128]{1,0:T(8,128)S(1)}, u32[]{:S(2)}, u32[]{:S(2)}) collective-permute-start(f32[8,128]{1,0:T(8,128)S(1)} %add.141), channel_id=1, source_target_pairs={{0,12},{4,8},{8,4},{12,0},{1,13},{5,9},{9,5},{13,1},{2,14},{6,10},... | collective-permute-start | bytes 12296 | tf_op jit(solution)/shard_map/ppermute | solution.py:177
  56.0 4.4 %collective-permute-start.10 = (bf16[6,256,128]{2,1,0:T(8,128)(2,1)S(1)}, bf16[6,256,128]{2,1,0:T(8,128)(2,1)S(1)}, u32[]{:S(2)}, u32[]{:S(2)}) collective-permute-start(bf16[6,256,128]{2,1,0:T(8,128)(2,1)S(1)} %get-tuple-element.10), channel_id=1, source_target_pairs={{0,1},{1,0},{2,3},{3,2},{4,5},{5,4},{6,7},{7,6},{8,9},{9,8},{10,11... | collective-permute-start | bytes 1179656 | tf_op jit(solution)/shard_map/ppermute | solution.py:177
  60.4 3.8 %copy-start.2 = (f32[3,336,256]{2,1,0:T(8,128)S(1)}, f32[3,336,256]{2,1,0:T(8,128)}, u32[]{:S(2)}) copy-start(f32[3,336,256]{2,1,0:T(8,128)} %get-tuple-element.12) | copy-start | bytes 3096580
  64.4 6.2 %collective-permute-start.25 = (bf16[512,128]{1,0:T(8,128)(2,1)S(1)}, bf16[512,128]{1,0:T(8,128)(2,1)S(1)}, u32[]{:S(2)}, u32[]{:S(2)}) collective-permute-start(bf16[512,128]{1,0:T(8,128)(2,1)S(1)} %fusion.4), channel_id=1, source_target_pairs={{0,2},{2,0},{1,3},{3,1},{4,6},{6,4},{5,7},{7,5},{8,10},{10,8},{9,1... | collective-permute-start | bytes 393224 | tf_op jit(solution)/shard_map/ppermute | solution.py:177
  65.0 17.4 %collective-permute-start.11 = (bf16[1152,128]{1,0:T(8,128)(2,1)S(1)}, bf16[1152,128]{1,0:T(8,128)(2,1)S(1)}, u32[]{:S(2)}, u32[]{:S(2)}) collective-permute-start(bf16[1152,128]{1,0:T(8,128)(2,1)S(1)} %dynamic-slice_convert_fusion), channel_id=1, source_target_pairs={{0,2},{2,0},{1,3},{3,1},{4,6},{6,4},{5,7},{7,5},{8,10},{10,8},{9,1... | collective-permute-start | bytes 884744 | tf_op jit(solution)/shard_map/ppermute | solution.py:177
  70.6 5.5 %collective-permute-start.26 = (bf16[128,128]{1,0:T(8,128)(2,1)S(1)}, bf16[128,128]{1,0:T(8,128)(2,1)S(1)}, u32[]{:S(2)}, u32[]{:S(2)}) collective-permute-start(bf16[128,128]{1,0:T(8,128)(2,1)S(1)} %get-tuple-element.20), channel_id=1, source_target_pairs={{0,4},{4,0},{8,12},{12,8},{1,5},{5,1},{9,13},{13,9},{2,6},{6,2},{1... | collective-permute-start | bytes 98312 | tf_op jit(solution)/shard_map/ppermute | solution.py:177
  70.7 5.4 %collective-permute-start.27 = (bf16[128,128]{1,0:T(8,128)(2,1)S(1)}, bf16[128,128]{1,0:T(8,128)(2,1)S(1)}, u32[]{:S(2)}, u32[]{:S(2)}) collective-permute-start(bf16[128,128]{1,0:T(8,128)(2,1)S(1)} %get-tuple-element.22), channel_id=1, source_target_pairs={{0,8},{4,12},{8,0},{12,4},{1,9},{5,13},{9,1},{13,5},{2,10},{6,14},... | collective-permute-start | bytes 98312 | tf_op jit(solution)/shard_map/ppermute | solution.py:177
  72.1 5.8 %collective-permute-start.28 = (bf16[128,128]{1,0:T(8,128)(2,1)S(1)}, bf16[128,128]{1,0:T(8,128)(2,1)S(1)}, u32[]{:S(2)}, u32[]{:S(2)}) collective-permute-start(bf16[128,128]{1,0:T(8,128)(2,1)S(1)} %get-tuple-element.21), channel_id=1, source_target_pairs={{0,12},{4,8},{8,4},{12,0},{1,13},{5,9},{9,5},{13,1},{2,14},{6,10},... | collective-permute-start | bytes 98312 | tf_op jit(solution)/shard_map/ppermute | solution.py:177
  78.0 8.1 %collective-permute-start.29 = (bf16[128,128]{1,0:T(8,128)(2,1)S(1)}, bf16[128,128]{1,0:T(8,128)(2,1)S(1)}, u32[]{:S(2)}, u32[]{:S(2)}) collective-permute-start(bf16[128,128]{1,0:T(8,128)(2,1)S(1)} %get-tuple-element.14), channel_id=1, source_target_pairs={{0,4},{4,0},{8,12},{12,8},{1,5},{5,1},{9,13},{13,9},{2,6},{6,2},{1... | collective-permute-start | bytes 98312 | tf_op jit(solution)/shard_map/ppermute | solution.py:177
  78.0 9.0 %collective-permute-start.30 = (bf16[128,128]{1,0:T(8,128)(2,1)S(1)}, bf16[128,128]{1,0:T(8,128)(2,1)S(1)}, u32[]{:S(2)}, u32[]{:S(2)}) collective-permute-start(bf16[128,128]{1,0:T(8,128)(2,1)S(1)} %get-tuple-element.14), channel_id=1, source_target_pairs={{0,8},{4,12},{8,0},{12,4},{1,9},{5,13},{9,1},{13,5},{2,10},{6,14},... | collective-permute-start | bytes 98312 | tf_op jit(solution)/shard_map/ppermute | solution.py:177
  81.5 5.8 %collective-permute-start.31 = (bf16[128,128]{1,0:T(8,128)(2,1)S(1)}, bf16[128,128]{1,0:T(8,128)(2,1)S(1)}, u32[]{:S(2)}, u32[]{:S(2)}) collective-permute-start(bf16[128,128]{1,0:T(8,128)(2,1)S(1)} %get-tuple-element.14), channel_id=1, source_target_pairs={{0,12},{4,8},{8,4},{12,0},{1,13},{5,9},{9,5},{13,1},{2,14},{6,10},... | collective-permute-start | bytes 98312 | tf_op jit(solution)/shard_map/ppermute | solution.py:177
  82.5 5.5 %collective-permute-start.12 = (bf16[288,128]{1,0:T(8,128)(2,1)S(1)}, bf16[288,128]{1,0:T(8,128)(2,1)S(1)}, u32[]{:S(2)}, u32[]{:S(2)}) collective-permute-start(bf16[288,128]{1,0:T(8,128)(2,1)S(1)} %get-tuple-element.17), channel_id=1, source_target_pairs={{0,4},{4,0},{8,12},{12,8},{1,5},{5,1},{9,13},{13,9},{2,6},{6,2},{1... | collective-permute-start | bytes 221192 | tf_op jit(solution)/shard_map/ppermute | solution.py:177
  82.6 6.1 %collective-permute-start.13 = (bf16[288,128]{1,0:T(8,128)(2,1)S(1)}, bf16[288,128]{1,0:T(8,128)(2,1)S(1)}, u32[]{:S(2)}, u32[]{:S(2)}) collective-permute-start(bf16[288,128]{1,0:T(8,128)(2,1)S(1)} %get-tuple-element.19), channel_id=1, source_target_pairs={{0,8},{4,12},{8,0},{12,4},{1,9},{5,13},{9,1},{13,5},{2,10},{6,14},... | collective-permute-start | bytes 221192 | tf_op jit(solution)/shard_map/ppermute | solution.py:177
  86.1 6.2 %collective-permute-start.14 = (bf16[288,128]{1,0:T(8,128)(2,1)S(1)}, bf16[288,128]{1,0:T(8,128)(2,1)S(1)}, u32[]{:S(2)}, u32[]{:S(2)}) collective-permute-start(bf16[288,128]{1,0:T(8,128)(2,1)S(1)} %get-tuple-element.18), channel_id=1, source_target_pairs={{0,12},{4,8},{8,4},{12,0},{1,13},{5,9},{9,5},{13,1},{2,14},{6,10},... | collective-permute-start | bytes 221192 | tf_op jit(solution)/shard_map/ppermute | solution.py:177
  87.3 14.5 %collective-permute-start.32 = (bf16[512,128]{1,0:T(8,128)(2,1)S(1)}, bf16[512,128]{1,0:T(8,128)(2,1)S(1)}, u32[]{:S(2)}, u32[]{:S(2)}) collective-permute-start(bf16[512,128]{1,0:T(8,128)(2,1)S(1)} %constant_dynamic-update-slice_fusion.2), channel_id=1, source_target_pairs={{0,2},{2,0},{1,3},{3,1},{4,6},{6,4},{5,7},{7,5},{8,10},{10,8},{9,1... | collective-permute-start | bytes 393224 | tf_op jit(solution)/shard_map/ppermute | solution.py:177
  92.3 4.6 %collective-permute-start.15 = (bf16[288,128]{1,0:T(8,128)(2,1)S(1)}, bf16[288,128]{1,0:T(8,128)(2,1)S(1)}, u32[]{:S(2)}, u32[]{:S(2)}) collective-permute-start(bf16[288,128]{1,0:T(8,128)(2,1)S(1)} %get-tuple-element.16), channel_id=1, source_target_pairs={{0,4},{4,0},{8,12},{12,8},{1,5},{5,1},{9,13},{13,9},{2,6},{6,2},{1... | collective-permute-start | bytes 221192 | tf_op jit(solution)/shard_map/ppermute | solution.py:177
  92.5 5.3 %collective-permute-start.16 = (bf16[288,128]{1,0:T(8,128)(2,1)S(1)}, bf16[288,128]{1,0:T(8,128)(2,1)S(1)}, u32[]{:S(2)}, u32[]{:S(2)}) collective-permute-start(bf16[288,128]{1,0:T(8,128)(2,1)S(1)} %get-tuple-element.16), channel_id=1, source_target_pairs={{0,8},{4,12},{8,0},{12,4},{1,9},{5,13},{9,1},{13,5},{2,10},{6,14},... | collective-permute-start | bytes 221192 | tf_op jit(solution)/shard_map/ppermute | solution.py:177
  95.3 6.2 %collective-permute-start.17 = (bf16[288,128]{1,0:T(8,128)(2,1)S(1)}, bf16[288,128]{1,0:T(8,128)(2,1)S(1)}, u32[]{:S(2)}, u32[]{:S(2)}) collective-permute-start(bf16[288,128]{1,0:T(8,128)(2,1)S(1)} %get-tuple-element.16), channel_id=1, source_target_pairs={{0,12},{4,8},{8,4},{12,0},{1,13},{5,9},{9,5},{13,1},{2,14},{6,10},... | collective-permute-start | bytes 221192 | tf_op jit(solution)/shard_map/ppermute | solution.py:177
  101.5 6.8 %collective-permute-start.18 = (bf16[1152,128]{1,0:T(8,128)(2,1)S(1)}, bf16[1152,128]{1,0:T(8,128)(2,1)S(1)}, u32[]{:S(2)}, u32[]{:S(2)}) collective-permute-start(bf16[1152,128]{1,0:T(8,128)(2,1)S(1)} %constant_dynamic-update-slice_fusion.8), channel_id=1, source_target_pairs={{0,2},{2,0},{1,3},{3,1},{4,6},{6,4},{5,7},{7,5},{8,10},{10,8},{9,1... | collective-permute-start | bytes 884744 | tf_op jit(solution)/shard_map/ppermute | solution.py:177
where the time goes:
time: 110 us; the launch traced here: 109 us
  starting transfers between devices  40.5 us (37%)
  waiting for transfers between devices  29.7 us (27%)
  Pallas kernels  20.7 us (19%)
  local copies, waits for them, and re-layouts  8.88 us (8%)
  other arithmetic  8.61 us (8%)
    ppermute x31, starting transfers between devices, swap(): return lax.ppermute(x, axis, [(i, i ^ bit) for i in range(size)])  39.2 us
    ppermute x31, waiting for transfers between devices, swap(): return lax.ppermute(x, axis, [(i, i ^ bit) for i in range(size)])  29.7 us
    pallas_call x1, Pallas kernels, shards(): pl.pallas_call(head_kernel, in_specs=[smem, smem] + [vmem] * 9, out_specs...  16.9 us
    pallas_call x1, Pallas kernels, shards(): pl.pallas_call(shared_kernel, in_specs=[smem] + [vmem] * 5, out_specs=vme...  3.81 us
  transfers between devices with their start and end apart: 33, of which 14 were waited for; matrix products, arithmetic and copies ran while one was open for 14% of the time, Pallas kernels for 19%

commit v1 on v0

v1 whole, which is shorter than its diff:
```python
import functools

import jax
import jax.numpy as jnp
from jax import lax
from jax.experimental import pallas as pl
from jax.experimental.pallas import tpu as pltpu
from jax.sharding import PartitionSpec as P

ANCH = 9
CLASSES = 11
LOGITS = 99
LANES = 128
ANCH_ROWS = 16
CLS_ROWS = 112
CLS_TOTAL = 1024
TRIO = 32
BF16 = jnp.bfloat16
F32 = jnp.float32
VMEM = pl.BlockSpec(memory_space=pltpu.VMEM)
SMEM = pl.BlockSpec(memory_space=pltpu.SMEM)


def call(kernel, name, outs, inputs, scratch=()):
    return pl.pallas_call(
        kernel,
        in_specs=[SMEM] + [VMEM] * (len(inputs) - 1),
        out_specs=[VMEM] * len(outs),
        out_shape=[jax.ShapeDtypeStruct(shape, kind) for shape, kind in outs],
        scratch_shapes=[pltpu.VMEM(shape, kind) for shape, kind in scratch],
        compiler_params=pltpu.CompilerParams(vmem_limit_bytes=48 * 1024 * 1024),
        name=name,
    )(*inputs)


def shift_cells(field, by):
    cells = field.shape[0]
    rolled = pltpu.roll(field, by % cells, axis=0)
    cell = lax.broadcasted_iota(jnp.int32, field.shape, 0)
    edge = 0 if by > 0 else cells - 1
    return jnp.where(cell == edge, 0.0, rolled)


def dot(left, right, dims=((1,), (0,))):
    return lax.dot_general(left, right, (dims, ((), ())), preferred_element_type=F32)


def three(x):
    high = x.astype(BF16)
    rest = x - high.astype(F32)
    middle = rest.astype(BF16)
    low = (rest - middle.astype(F32)).astype(BF16)
    return high, middle, low


def put_trio(ref, start, x):
    high, middle, low = three(x)
    ref[start : start + TRIO] = jnp.concatenate([high, middle, low, jnp.zeros_like(low)], axis=0)


def get_trio(ref, start):
    part = ref[start : start + TRIO].astype(F32)
    return part[0:8] + part[8:16] + part[16:24]


def prep_kernel(where_ref, f_ref, lab_ref, w2_ref, b1_ref, msg_ref, labt_ref, pack_ref, count_ref):
    rows, cols, chans = f_ref.shape
    c = where_ref[0]
    for k in range(3):
        msg_ref[cols * k : cols * (k + 1)] = f_ref[(rows - 3) * c + k]
    lab = lab_ref[...]
    count_ref[...] = jnp.full(count_ref.shape, jnp.sum(jnp.where(lab > 0, 1.0, 0.0)), F32)
    size = lab.shape[1]
    place = lax.broadcasted_iota(jnp.int32, (ANCH_ROWS, size), 1) % ANCH
    anchor = lax.broadcasted_iota(jnp.int32, (ANCH_ROWS, size), 0)
    mine = jnp.where(place == anchor, 1.0, 0.0)
    left = jnp.concatenate([mine * lab[r : r + 1].astype(F32) for r in range(rows)], axis=0).astype(BF16)
    offset = lax.broadcasted_iota(jnp.int32, (size, cols), 0) - ANCH * lax.broadcasted_iota(jnp.int32, (size, cols), 1)
    pick = jnp.where(jnp.logical_and(offset >= 0, offset < ANCH), 1.0, 0.0).astype(BF16)
    turned = dot(left, pick).astype(BF16)
    for r in range(rows):
        labt_ref[r] = turned[ANCH_ROWS * r : ANCH_ROWS * (r + 1)]
    msg_ref[3 * cols : 3 * cols + ANCH_ROWS] = jnp.where(
        c == 0, turned[:ANCH_ROWS].astype(F32), turned[ANCH_ROWS * (rows - 1) :].astype(F32)
    ).astype(BF16)
    deep = w2_ref.shape[2]
    for tap in range(9):
        pack_ref[deep * tap : deep * (tap + 1)] = jnp.zeros((deep, LANES), BF16)
        pack_ref[deep * tap : deep * (tap + 1), :LOGITS] = w2_ref[tap // 3, tap % 3]
    bias = jnp.broadcast_to(b1_ref[...], (8, deep))
    put_trio(pack_ref, 9 * deep, bias)


def head_kernel(
    where_ref, f_ref, halo_ref, labt_ref, w1a_ref, w1b_ref, packa_ref, packb_ref, b2_ref, *rest,
):
    *count_refs, hid_ref, dt_ref, own_ref, other_ref, small_ref, xw_ref, dlog_ref = rest

    half = f_ref.shape[0] // 2
    cols = f_ref.shape[1]
    c = where_ref[0]
    first = where_ref[1]
    total = where_ref[2]
    near = half + 3
    xw_ref[pl.ds(3 - 3 * c, near)] = f_ref[pl.ds((half - 3) * c, near)]
    for k in range(3):
        xw_ref[near * c + k] = halo_ref[cols * k : cols * (k + 1)]
    w1 = [
        jnp.concatenate(
            [jnp.concatenate([w1a_ref[i, j], w1b_ref[i, j]], axis=1) for j in range(3)], axis=1
        )
        for i in range(3)
    ]
    w1 = jnp.concatenate(w1, axis=0)
    chans = w1.shape[1] // 3
    deep = chans // 2
    b1 = jnp.concatenate([get_trio(packa_ref, 9 * deep)[:1], get_trio(packb_ref, 9 * deep)[:1]], axis=1)
    counts = [ref[...] for ref in count_refs]
    while len(counts) > 1:
        counts = [counts[k] + counts[k + 1] for k in range(0, len(counts), 2)]

    def conv1(h, carry):
        lhs = jnp.concatenate([xw_ref[h], xw_ref[h + 1], xw_ref[h + 2]], axis=1)
        y = dot(lhs, w1)
        pre = shift_cells(y[:, :chans], 1) + y[:, chans : 2 * chans] + shift_cells(y[:, 2 * chans :], -1) + b1
        row = first + h - 2
        inside = jnp.logical_and(row >= 0, row < total)
        hid_ref[h] = jnp.where(inside, jnp.maximum(pre, 0.0), 0.0).astype(BF16)
        return carry

    lax.fori_loop(0, half + 4, conv1, 0)

    lane = lax.broadcasted_iota(jnp.int32, (1, LANES), 1)
    kind = (lane % CLASSES + 1).astype(F32)
    real = lane < LOGITS
    anchor = lax.broadcasted_iota(jnp.int32, (ANCH_ROWS, LANES), 0)
    column = lax.broadcasted_iota(jnp.int32, (ANCH_ROWS, LANES), 1)
    spread = jnp.where(jnp.logical_and(column // CLASSES == anchor, column < LOGITS), 1.0, 0.0).astype(BF16)


    def tap(ref, i, j):
        return ref[deep * (3 * i + j) : deep * (3 * i + j + 1)]

    w2 = [[jnp.concatenate([tap(packa_ref, i, j), tap(packb_ref, i, j)], axis=0) for j in range(3)] for i in range(3)]
    w2n = [jnp.concatenate(w2[i], axis=1) for i in range(3)]
    w2n = jnp.concatenate(w2n, axis=0)
    b2 = jnp.concatenate([b2_ref[...], jnp.zeros((1, LANES - LOGITS), F32)], axis=1)
    inverse = 1.0 / counts[0][:1]

    def focal(l, carry):
        gcb, loss = carry
        lhs = jnp.concatenate([hid_ref[l], hid_ref[l + 1], hid_ref[l + 2]], axis=1)
        y = dot(lhs, w2n)
        z = shift_cells(y[:, :LANES], 1) + y[:, LANES : 2 * LANES] + shift_cells(y[:, 2 * LANES :], -1) + b2
        at_halo = jnp.where(c == 0, l == 0, l == half + 1)
        local = jnp.clip(l - 1 + half * c, 0, 2 * half - 1)
        mine = labt_ref[local].astype(F32)
        far = halo_ref[3 * cols : 3 * cols + ANCH_ROWS].astype(F32)
        lab = dot(jnp.where(at_halo, far, mine).astype(BF16), spread, ((0,), (0,)))
        row = first + l - 1
        inside = jnp.logical_and(row >= 0, row < total)
        hit = lab == kind
        keep = jnp.logical_and(jnp.logical_and(lab >= 0.0, real), inside)
        u = jnp.where(hit, -z, z)
        e = jnp.exp(-jnp.abs(u))
        r = 1.0 / (1.0 + e)
        er = e * r
        up = u >= 0.0
        s = jnp.where(up, r, er)
        comp = jnp.where(up, er, r)
        soft = jnp.maximum(u, 0.0) + jnp.log1p(e)
        ws = jnp.where(keep, jnp.where(hit, 0.25, 0.75), 0.0) * s * s
        slope = ws * (2.0 * comp * soft + s)
        dz = jnp.where(hit, -slope, slope) * inverse
        d16 = dz.astype(BF16)
        dlog_ref[l] = d16
        own = jnp.logical_and(l >= 1, l <= half)
        weight = jnp.where(own, 1.0, 0.0)
        gcb = gcb + weight * jnp.sum(dz, axis=0, keepdims=True)
        loss = loss + weight * jnp.sum(ws * soft, axis=0, keepdims=True)

        @pl.when(own)
        def _():
            turned = jnp.transpose(d16.astype(F32))[:CLS_ROWS]
            cell = lax.broadcasted_iota(jnp.int32, turned.shape, 1)
            left = jnp.where(cell == cols - 1, 0.0, pltpu.roll(turned, cols - 1, axis=1))
            right = jnp.where(cell == 0, 0.0, pltpu.roll(turned, 1, axis=1))
            dt_ref[l - 1] = jnp.concatenate([left, turned, right], axis=0).astype(BF16)

        return gcb, loss

    zero = jnp.zeros((1, LANES), F32)
    gcb, loss = lax.fori_loop(0, half + 2, focal, (zero, zero))

    w2t = [jnp.concatenate([w2[i][j] for i in range(3)], axis=1) for j in range(3)]
    w2t = jnp.concatenate(w2t, axis=0)

    def dpre_row(d, gsb):
        lhs = jnp.concatenate([dlog_ref[d + 2], dlog_ref[d + 1], dlog_ref[d]], axis=1)
        q = dot(lhs, w2t, ((1,), (1,)))
        dhid = shift_cells(q[:, :chans], -1) + q[:, chans : 2 * chans] + shift_cells(q[:, 2 * chans :], 1)
        dpre = jnp.where(hid_ref[d + 2].astype(F32) > 0.0, dhid, 0.0)
        d16 = dpre.astype(BF16)
        own_ref[d] = d16[:, : chans // 2]
        other_ref[d] = d16[:, chans // 2 :]
        return gsb + jnp.sum(dpre, axis=0, keepdims=True)

    gsb = lax.fori_loop(0, half, dpre_row, jnp.zeros((1, chans), F32))
    small_ref[0:1] = gcb
    small_ref[1:2] = jnp.broadcast_to(jnp.sum(loss, axis=1, keepdims=True), (1, LANES)) * inverse
    small_ref[2:3] = jnp.zeros((1, LANES), F32)
    small_ref[3:4] = gsb[:, : chans // 2]
    small_ref[4:5] = gsb[:, chans // 2 :]
    small_ref[5:8] = jnp.zeros((3, LANES), F32)


def cls_kernel(where_ref, hid_ref, dt_ref, own_ref, other_ref):
    half, _, cols = dt_ref.shape
    chans = hid_ref.shape[2]
    deep = chans // 2
    dt = jnp.concatenate([dt_ref[d] for d in range(half)], axis=1)
    size = 3 * CLS_ROWS
    for i in range(3):
        g = dot(dt, hid_ref[i + 1 : i + 1 + half].reshape(half * cols, chans))
        own_ref[size * i : size * (i + 1)] = g[:, :deep]
        other_ref[size * i : size * (i + 1)] = g[:, deep:]
    blank = jnp.zeros((CLS_TOTAL - 3 * size, deep), F32)
    own_ref[3 * size :] = blank
    other_ref[3 * size :] = blank


def split(total, me, keep_ref, send_refs):
    rows = keep_ref.shape[0]
    keep_ref[...] = total[pl.ds(pl.multiple_of(me * rows, 8), rows)]
    for k, ref in enumerate(send_refs):
        ref[0:rows] = total[pl.ds(pl.multiple_of((me ^ (k + 1)) * rows, 8), rows)].astype(BF16)


def shared_kernel(slot, where_ref, f_ref, halo_ref, far_ref, own_ref, other_ref, small_ref, theirs_ref, *rest):
    keep_ref, sum_ref, *send_refs, x_ref, d_ref, g_ref = rest
    rows, cols, chans = f_ref.shape
    half = rows // 2
    c = where_ref[0]
    near = halo_ref[pl.ds(pl.multiple_of(2 * cols * (1 - c), 16), cols)]
    far = far_ref[pl.ds(pl.multiple_of(2 * cols * c, 16), cols)]
    x_ref[pl.ds((rows + 1) * c, 1)] = near.reshape(1, cols, chans)
    x_ref[pl.ds((rows + 1) * (1 - c), 1)] = far.reshape(1, cols, chans)
    x_ref[1 : rows + 1] = f_ref[...]

    def place(ref, start):
        def body(d, carry):
            mid = ref[d].astype(F32)
            d_ref[start + d] = jnp.concatenate(
                [shift_cells(mid, -1).astype(BF16), ref[d], shift_cells(mid, 1).astype(BF16)], axis=1
            )
            return carry

        lax.fori_loop(0, half, body, 0)

    place(own_ref, half * c)
    place(other_ref, half * (1 - c))
    rhs = d_ref[...].reshape(rows * cols, d_ref.shape[2])
    outs = rhs.shape[1] // 3
    for i in range(3):
        lhs = x_ref[i : i + rows].reshape(rows * cols, chans)
        g = dot(lhs, rhs, ((0,), (0,)))
        for j in range(3):
            start = (3 * i + j) * chans
            g_ref[start : start + chans] = g[:, j * outs : (j + 1) * outs]
    split(g_ref, where_ref[slot], keep_ref, send_refs)
    mine, theirs = small_ref[...], theirs_ref[...]
    sums = jnp.concatenate([mine[0:3] + theirs[0:3], mine[3:4] + theirs[4:5], mine[4:8]], axis=0)
    sum_ref[...] = sums
    for ref in send_refs:
        put_trio(ref, keep_ref.shape[0], sums)


def pair_sum(parts):
    while len(parts) > 1:
        parts = [parts[k] + parts[k + 1] for k in range(0, len(parts), 2)]
    return parts[0]


def step_kernel(slot, n_in, trio, where_ref, *refs):
    base_ref, refs = refs[0], refs[1:]
    if trio:
        small_ref, refs = refs[0], refs[1:]
    in_refs, refs = refs[:n_in], refs[n_in:]
    rows = base_ref.shape[0]
    total = base_ref[...]
    for ref in in_refs:
        total = total + ref[0:rows].astype(F32)
    if trio:
        sums = pair_sum([small_ref[...]] + [get_trio(ref, rows) for ref in in_refs])
    if slot is None:
        refs[0][...] = total.astype(BF16)
        if trio:
            refs[1][...] = sums
        return
    keep_ref, refs = refs[0], refs[1:]
    if trio:
        sum_ref, refs = refs[0], refs[1:]
        sum_ref[...] = sums
    *send_refs, total_ref = refs
    total_ref[...] = total
    split(total_ref, where_ref[slot], keep_ref, send_refs)
    if trio:
        for ref in send_refs:
            put_trio(ref, keep_ref.shape[0], sums)


def step(where, slot, size, base, small, arrived, name):
    trio = TRIO if small is not None else 0
    rows, width = base.shape
    inputs = [where, base] + ([small] if trio else []) + list(arrived)
    smalls = [((8, LANES), F32)] if trio else []
    kernel = functools.partial(step_kernel, slot, len(arrived), trio)
    if slot is None:
        return call(kernel, name, [((rows, width), BF16)] + smalls, inputs)
    share = rows // size
    outs = [((share, width), F32)] + smalls + [((share + trio, width), BF16)] * (size - 1)
    return call(kernel, name, outs, inputs, [((rows, width), F32)])


def join_kernel(slot, where_ref, *refs):
    *in_refs, out_ref = refs
    rows = in_refs[0].shape[0]
    me = where_ref[slot]
    for k, ref in enumerate(in_refs):
        out_ref[pl.ds(pl.multiple_of((me ^ k) * rows, 8), rows)] = ref[...].astype(out_ref.dtype)


def join(where, slot, parts, kind, name):
    rows, width = parts[0].shape
    return call(
        functools.partial(join_kernel, slot), name, [((rows * len(parts), width), kind)], [where] + parts
    )[0]


def join_cls_kernel(slot, where_ref, *refs):
    *in_refs, out_ref, whole_ref = refs
    join_kernel(slot, where_ref, *in_refs, whole_ref)
    for tap in range(9):
        turned = jnp.transpose(whole_ref[CLS_ROWS * tap : CLS_ROWS * tap + LANES])
        out_ref[tap // 3, tap % 3] = turned[:, :LOGITS]


def swap(x, axis, bit=1):
    size = lax.axis_size(axis)
    return lax.ppermute(x, axis, [(i, i ^ bit) for i in range(size)])


def others(x, axis):
    return [swap(x, axis, bit) for bit in range(1, lax.axis_size(axis))]


def exchange(sends, axis):
    return [swap(x, axis, k + 1) for k, x in enumerate(sends)]


def shards(features, labels, w_shared, b_shared, w_cls, b_cls):
    _, rows, cols, chans = features.shape
    half = rows // 2
    outs = w_shared.shape[3]
    tiles = lax.axis_size("tile")
    pages = lax.axis_size("batch")
    c = lax.axis_index("chan")
    t = lax.axis_index("tile")
    f = features[0]
    where = jnp.stack([c, t * rows + half * c, jnp.int32(tiles * rows), t, lax.axis_index("batch")]).astype(jnp.int32)
    TILE, BATCH = 3, 4

    msg, labt, pack, count = call(
        prep_kernel, "prep",
        [
            ((3 * cols + ANCH_ROWS, chans), BF16),
            ((rows, ANCH_ROWS, cols), BF16),
            ((9 * outs + TRIO, LANES), BF16),
            ((8, LANES), F32),
        ],
        [where, f, labels[0], w_cls, b_shared.reshape(1, outs)],
    )
    pairs = []
    for i in range(tiles - 1):
        pairs += [(2 * i + 1, 2 * i + 2), (2 * i + 2, 2 * i + 1)]
    halo = lax.ppermute(msg, ("tile", "chan"), pairs)
    w1b = swap(w_shared, "chan")
    packb = swap(pack, "chan")
    count = pair_sum([count] + others(count, "batch"))
    counts = [count] + others(count, "tile")

    hid, dt, own, other, small = call(
        head_kernel, "head",
        [
            ((half + 4, cols, chans), BF16),
            ((half, 3 * CLS_ROWS, cols), BF16),
            ((half, cols, outs), BF16),
            ((half, cols, outs), BF16),
            ((8, LANES), F32),
        ],
        [where, f, halo, labt, w_shared, w1b, pack, packb, b_cls.reshape(1, LOGITS)] + counts,
        [((half + 6, cols, chans), BF16), ((half + 2, cols, LANES), BF16)],
    )
    theirs = swap(other, "chan")
    far = swap(halo, "chan")
    small_theirs = swap(small, "chan")
    gcls, gcls_other = call(
        cls_kernel, "cls", [((CLS_TOTAL, outs), F32)] * 2, [where, hid, dt]
    )
    gcls_theirs = swap(gcls_other, "chan")

    share = 9 * chans // pages
    keep, small, *sends = call(
        functools.partial(shared_kernel, BATCH), "shared",
        [((share, outs), F32), ((8, LANES), F32)] + [((share + TRIO, outs), BF16)] * (pages - 1),
        [where, f, halo, far, own, theirs, small, small_theirs],
        [((rows + 2, cols, chans), BF16), ((rows, cols, 3 * outs), BF16), ((9 * chans, outs), F32)],
    )
    ckeep, *csends = step(where, TILE, tiles, gcls, None, [gcls_theirs], "cls_tile")

    arrived = exchange(sends, "batch")
    carrived = exchange(csends, "tile")
    keep, small, *sends = step(where, TILE, tiles, keep, small, arrived, "shared_tile")
    ckeep, *csends = step(where, BATCH, pages, ckeep, None, carrived, "cls_batch")
    arrived = exchange(sends, "tile")
    carrived = exchange(csends, "batch")
    done, small = step(where, None, 1, keep, small, arrived, "shared_round")
    (cdone,) = step(where, None, 1, ckeep, None, carrived, "cls_round")
    block = join(where, TILE, [done] + others(done, "tile"), BF16, "shared_join")
    cblock = join(where, BATCH, [cdone] + others(cdone, "batch"), BF16, "cls_join")
    grad_shared = join(where, BATCH, [block] + others(block, "batch"), F32, "shared_out")
    (grad_cls,) = call(
        functools.partial(join_cls_kernel, TILE), "cls_out",
        [((3, 3, outs, LOGITS), F32)],
        [where, cblock] + others(cblock, "tile"),
        [((CLS_TOTAL, outs), F32)],
    )
    return (
        grad_shared.reshape(3, 3, chans, outs),
        small[3],
        grad_cls,
        small[0, :LOGITS],
        small[1, :1],
    )


def solution(mesh):
    placed = (
        P(("groups", "batch"), "tile", None, None),
        P(("groups", "batch"), "tile", None),
        P(None, None, None, "chan"),
        P("chan"),
        P(None, None, "chan", None),
        P(),
    )
    return jax.shard_map(
        shards,
        mesh=mesh,
        in_specs=placed,
        out_specs=(
            P("groups", None, None, "chan"),
            P(("groups", "chan")),
            P("groups", None, "chan", None),
            P("groups"),
            P("groups"),
        ),
        check_vma=False,
    )
```

time: 110 us -> 97.3 us (0.88)
  other arithmetic: 8.61 us -> 0.01 us
  Pallas kernels: 20.7 us -> 27.9 us
  starting transfers between devices: 40.5 us -> 34.1 us
  waiting for transfers between devices: 29.7 us -> 27.3 us
  local copies, waits for them, and re-layouts: 8.88 us -> 6.88 us
    pallas_call x2 -> x13, Pallas kernels: 20.7 us -> 27.9 us  [call(): pl.pallas_call(kernel, in_specs=[SMEM] + [VMEM] * (len(inputs) - 1), out_...]
    ppermute x31 -> x26, starting transfers between devices: 39.2 us -> 33.4 us  [swap(): return lax.ppermute(x, axis, [(i, i ^ bit) for i in range(size)])]
    unnamed x11 -> x13, local copies, waits for them, and re-layouts: 0.25 us -> 5.26 us
    ppermute x31 -> x26, waiting for transfers between devices: 29.7 us -> 27.3 us  [swap(): return lax.ppermute(x, axis, [(i, i ^ bit) for i in range(size)])]
    reshape x2 -> x0, other arithmetic: 1.91 us -> none  [the longest x1 1.11 us: shards(): reduced(gsh.reshape(9 * chans, outs)).reshape(3, 3, chans, outs)]
    dynamic_slice x2 -> x0, local copies, waits for them, and re-layouts: 1.77 us -> none  [the longest x1 1.02 us: shards(): lax.dynamic_slice_in_dim(f, (rows - 3) * c, 3, axis=0)]
    convert_element_type x5 -> x0, local copies, waits for them, and re-layouts: 1.75 us -> none  [the longest x1 1.63 us: shards(): lab = labels[0].astype(BF16).reshape(rows, cols, ANCH)]
    reduce_sum x1 -> x0, other arithmetic: 1.73 us -> none  [shards(): count = jnp.full((8, LANES), jnp.sum((labels > 0).astype(F32)), F32)]
  transfers between devices with their start and end apart: 33 -> 27, of which waited for: 14 -> 12; matrix products, arithmetic and copies ran while one was open for 14% -> 5% of each run, Pallas kernels for 19% -> 27%
where the time goes in v1:
time: 97.3 us; the launch traced here: 97 us
  starting transfers between devices  34.1 us (35%)
  Pallas kernels  27.9 us (29%)
  waiting for transfers between devices  27.3 us (28%)
  local copies, waits for them, and re-layouts  6.88 us (7%)
    ppermute x26, starting transfers between devices, swap(): return lax.ppermute(x, axis, [(i, i ^ bit) for i in range(size)])  33.4 us
    pallas_call x13, Pallas kernels, call(): pl.pallas_call(kernel, in_specs=[SMEM] + [VMEM] * (len(inputs) - 1), out_...  27.9 us
    ppermute x26, waiting for transfers between devices, swap(): return lax.ppermute(x, axis, [(i, i ^ bit) for i in range(size)])  27.3 us
    unnamed x13, local copies, waits for them, and re-layouts  5.26 us
  transfers between devices with their start and end apart: 27, of which 12 were waited for; matrix products, arithmetic and copies ran while one was open for 5% of the time, Pallas kernels for 27%

profile of v1, /device:TPU:0, one launch (start us, length us, event | category | flops | bytes accessed | tf_op | source)
XLA Modules:
  0.0 97.0 jit_solution(957780753704011390)
XLA Ops:
  0.6 0.5 collective-permute-start.2
  1.2 1.2 %copy.11.w2_ref = bf16[3,3,128,99]{3,2,1,0:T(8,128)(2,1)S(1)} copy(bf16[3,3,128,99]{2,3,1,0:T(8,128)(2,1)} %param.10) | data formatting | bytes 456192 | tf_op args[4]
  2.4 0.9 copy.15
  3.3 0.1 stack.19.where_ref
  3.4 1.4 %copy-done = bf16[1,12,256,256]{3,2,1,0:T(8,128)(2,1)S(1)} copy-done((bf16[1,12,256,256]{3,2,1,0:T(8,128)(2,1)S(1)}, bf16[1,12,256,256]{3,2,1,0:T(8,128)(2,1)}, u32[]{:S(2)}) %copy-start) | copy-done | bytes 1572888
  4.8 0.7 copy-done.3
  5.5 1.3 %prep.1 = (bf16[784,256]{1,0:T(8,128)(2,1)S(1)}, bf16[12,16,256]{2,1,0:T(8,128)(2,1)S(1)}, bf16[1184,128]{1,0:T(8,128)(2,1)S(1)}, f32[8,128]{1,0:T(8,128)S(1)}) custom-call(s32[5]{0:T(128)S(1)} %stack.19.where_ref, bf16[12,256,256]{2,1,0:T(8,128)(2,1)S(1)} %bitcast.17, s32[12,2304]{1,0:T(8,128)S(1)} %bitcast.19, bf16[3,3,128,99]{3,2,1,0:T(8,128)(2,1)S(1)} %copy.11.w2_ref, ...), custom_call_target="tpu_custom_call" | custom-call | tf_op jit(solution)/shard_map/prep/pallas_call | solution.py:25
  6.8 0.7 collective-permute-start
  7.5 4.0 %collective-permute-start.3 = (bf16[1184,128]{1,0:T(8,128)(2,1)S(1)}, bf16[1184,128]{1,0:T(8,128)(2,1)S(1)}, u32[]{:S(2)}, u32[]{:S(2)}) collective-permute-start(bf16[1184,128]{1,0:T(8,128)(2,1)S(1)} %get-tuple-element.34.packa_ref), channel_id=1, source_target_pairs={{0,1},{1,0},{2,3},{3,2},{4,5},{5,4},{6,7},{7,6},{8,9},{9,8},{10,11... | collective-permute-start | bytes 909320 | tf_op jit(solution)/shard_map/ppermute | solution.py:350
  11.5 1.5 %collective-permute-start.4 = (f32[8,128]{1,0:T(8,128)S(1)}, f32[8,128]{1,0:T(8,128)S(1)}, u32[]{:S(2)}, u32[]{:S(2)}) collective-permute-start(f32[8,128]{1,0:T(8,128)S(1)} %get-tuple-element.35), channel_id=1, source_target_pairs={{0,2},{2,0},{1,3},{3,1},{4,6},{6,4},{5,7},{7,5},{8,10},{10,8},{9,1... | collective-permute-start | bytes 12296 | tf_op jit(solution)/shard_map/ppermute | solution.py:350
  13.0 2.1 %collective-permute-done.4 = f32[8,128]{1,0:T(8,128)S(1)} collective-permute-done((f32[8,128]{1,0:T(8,128)S(1)}, f32[8,128]{1,0:T(8,128)S(1)}, u32[]{:S(2)}, u32[]{:S(2)}) %collective-permute-start.4) | collective-permute-done | bytes 4128 | tf_op jit(solution)/shard_map/ppermute | solution.py:350
  15.1 1.6 %collective-permute-start.5 = (f32[8,128]{1,0:T(8,128)S(1)}, f32[8,128]{1,0:T(8,128)S(1)}, u32[]{:S(2)}, u32[]{:S(2)}) collective-permute-start(f32[8,128]{1,0:T(8,128)S(1)} %add.7.rest_0_), channel_id=1, source_target_pairs={{0,4},{4,0},{8,12},{12,8},{1,5},{5,1},{9,13},{13,9},{2,6},{6,2},{1... | collective-permute-start | bytes 12296 | tf_op jit(solution)/shard_map/ppermute | solution.py:350
  16.7 0.3 collective-permute-start.1
  17.0 3.1 %collective-permute-start.6 = (f32[8,128]{1,0:T(8,128)S(1)}, f32[8,128]{1,0:T(8,128)S(1)}, u32[]{:S(2)}, u32[]{:S(2)}) collective-permute-start(f32[8,128]{1,0:T(8,128)S(1)} %add.7.rest_0_), channel_id=1, source_target_pairs={{0,8},{4,12},{8,0},{12,4},{1,9},{5,13},{9,1},{13,5},{2,10},{6,14},... | collective-permute-start | bytes 12296 | tf_op jit(solution)/shard_map/ppermute | solution.py:350
  20.1 0.0 collective-permute-done.5.rest_1_
  20.1 1.3 %collective-permute-start.7 = (f32[8,128]{1,0:T(8,128)S(1)}, f32[8,128]{1,0:T(8,128)S(1)}, u32[]{:S(2)}, u32[]{:S(2)}) collective-permute-start(f32[8,128]{1,0:T(8,128)S(1)} %add.7.rest_0_), channel_id=1, source_target_pairs={{0,12},{4,8},{8,4},{12,0},{1,13},{5,9},{9,5},{13,1},{2,14},{6,10},... | collective-permute-start | bytes 12296 | tf_op jit(solution)/shard_map/ppermute | solution.py:350
  21.4 0.3 collective-permute-done.6.rest_2_
  21.7 3.8 %collective-permute-done.7.rest_3_ = f32[8,128]{1,0:T(8,128)S(1)} collective-permute-done((f32[8,128]{1,0:T(8,128)S(1)}, f32[8,128]{1,0:T(8,128)S(1)}, u32[]{:S(2)}, u32[]{:S(2)}) %collective-permute-start.7) | collective-permute-done | bytes 4128 | tf_op jit(solution)/shard_map/ppermute | solution.py:350
  25.5 14.7 %head.1 = (bf16[10,256,256]{2,1,0:T(8,128)(2,1)S(1)}, bf16[6,336,256]{2,1,0:T(8,128)(2,1)S(1)}, bf16[6,256,128]{2,1,0:T(8,128)(2,1)S(1)}, bf16[6,256,128]{2,1,0:T(8,128)(2,1)S(1)}, f32[8,128]{1,0:T(8,128)S(1)}) custom-call(s32[5]{0:T(128)S(1)} %stack.19.where_ref, bf16[12,256,256]{2,1,0:T(8,128)(2,1)} %bitcast.16, ...), custom_call_target="tpu_custom_call" | custom-call | tf_op jit(solution)/shard_map/head/pallas_call | solution.py:25
  40.2 0.0 collective-permute-start.8
  40.3 1.5 %cls.1 = (f32[1024,128]{1,0:T(8,128)S(1)}, f32[1024,128]{1,0:T(8,128)S(1)}) custom-call(s32[5]{0:T(128)S(1)} %stack.19.where_ref, bf16[10,256,256]{2,1,0:T(8,128)(2,1)S(1)} %get-tuple-element.49.hid_ref, bf16[6,336,256]{2,1,0:T(8,128)(2,1)S(1)} %get-tuple-element.50.dt_ref), custom_call_target="tpu_custom_call" | custom-call | tf_op jit(solution)/shard_map/cls/pallas_call | solution.py:25
  41.8 0.6 collective-permute-start.18
  42.3 0.1 collective-permute-start.9
  42.4 1.5 %collective-permute-done.9.theirs_ref = f32[8,128]{1,0:T(8,128)S(1)} collective-permute-done((f32[8,128]{1,0:T(8,128)S(1)}, f32[8,128]{1,0:T(8,128)S(1)}, u32[]{:S(2)}, u32[]{:S(2)}) %collective-permute-start.9) | collective-permute-done | bytes 4128 | tf_op jit(solution)/shard_map/ppermute | solution.py:350
  43.9 3.9 %shared.1 = (f32[1152,128]{1,0:T(8,128)S(1)}, f32[8,128]{1,0:T(8,128)S(1)}, bf16[1184,128]{1,0:T(8,128)(2,1)S(1)}) custom-call(s32[5]{0:T(128)S(1)} %stack.19.where_ref, bf16[12,256,256]{2,1,0:T(8,128)(2,1)S(1)} %bitcast.18, bf16[784,256]{1,0:T(8,128)(2,1)S(1)} %collective-permute-done.halo_ref, bf16[784,256]{1,0:T(8,128)(2,1)S(1)} %collective-permute-done.1.far_ref, ...), custom_call_target="tpu_custom_call" | custom-call | tf_op jit(solution)/shard_map/shared/pallas_call | solution.py:25
  47.8 1.5 %collective-permute-start.10 = (bf16[1184,128]{1,0:T(8,128)(2,1)S(1)}, bf16[1184,128]{1,0:T(8,128)(2,1)S(1)}, u32[]{:S(2)}, u32[]{:S(2)}) collective-permute-start(bf16[1184,128]{1,0:T(8,128)(2,1)S(1)} %get-tuple-element.41), channel_id=1, source_target_pairs={{0,2},{2,0},{1,3},{3,1},{4,6},{6,4},{5,7},{7,5},{8,10},{10,8},{9,1... | collective-permute-start | bytes 909320 | tf_op jit(solution)/shard_map/ppermute | solution.py:350
  49.3 0.6 cls_tile.1
  50.0 0.1 collective-permute-start.19
  50.1 1.9 %collective-permute-start.20 = (bf16[256,128]{1,0:T(8,128)(2,1)S(1)}, bf16[256,128]{1,0:T(8,128)(2,1)S(1)}, u32[]{:S(2)}, u32[]{:S(2)}) collective-permute-start(bf16[256,128]{1,0:T(8,128)(2,1)S(1)} %get-tuple-element.55), channel_id=1, source_target_pairs={{0,8},{4,12},{8,0},{12,4},{1,9},{5,13},{9,1},{13,5},{2,10},{6,14},... | collective-permute-start | bytes 196616 | tf_op jit(solution)/shard_map/ppermute | solution.py:350
  51.9 2.5 %collective-permute-start.21 = (bf16[256,128]{1,0:T(8,128)(2,1)S(1)}, bf16[256,128]{1,0:T(8,128)(2,1)S(1)}, u32[]{:S(2)}, u32[]{:S(2)}) collective-permute-start(bf16[256,128]{1,0:T(8,128)(2,1)S(1)} %get-tuple-element.56), channel_id=1, source_target_pairs={{0,12},{4,8},{8,4},{12,0},{1,13},{5,9},{9,5},{13,1},{2,14},{6,10},... | collective-permute-start | bytes 196616 | tf_op jit(solution)/shard_map/ppermute | solution.py:350
  54.4 0.7 collective-permute-done.19.refs_1_
  55.2 3.4 %collective-permute-done.20.refs_2_ = bf16[256,128]{1,0:T(8,128)(2,1)S(1)} collective-permute-done((bf16[256,128]{1,0:T(8,128)(2,1)S(1)}, bf16[256,128]{1,0:T(8,128)(2,1)S(1)}, u32[]{:S(2)}, u32[]{:S(2)}) %collective-permute-start.20) | collective-permute-done | bytes 65568 | tf_op jit(solution)/shard_map/ppermute | solution.py:350
  58.6 0.0 collective-permute-done.21.refs_3_
  58.6 0.6 cls_batch.1
  59.2 0.6 collective-permute-start.22
  59.8 3.4 %collective-permute-done.22.refs_1_ = bf16[128,128]{1,0:T(8,128)(2,1)S(1)} collective-permute-done((bf16[128,128]{1,0:T(8,128)(2,1)S(1)}, bf16[128,128]{1,0:T(8,128)(2,1)S(1)}, u32[]{:S(2)}, u32[]{:S(2)}) %collective-permute-start.22) | collective-permute-done | bytes 32800 | tf_op jit(solution)/shard_map/ppermute | solution.py:350
  63.2 0.5 cls_round.1.refs_0_
  63.7 0.6 collective-permute-start.23
  64.4 0.6 shared_tile.1
  65.0 1.3 %collective-permute-start.11 = (bf16[320,128]{1,0:T(8,128)(2,1)S(1)}, bf16[320,128]{1,0:T(8,128)(2,1)S(1)}, u32[]{:S(2)}, u32[]{:S(2)}) collective-permute-start(bf16[320,128]{1,0:T(8,128)(2,1)S(1)} %get-tuple-element.44), channel_id=1, source_target_pairs={{0,4},{4,0},{8,12},{12,8},{1,5},{5,1},{9,13},{13,9},{2,6},{6,2},{1... | collective-permute-start | bytes 245768 | tf_op jit(solution)/shard_map/ppermute | solution.py:350
  66.3 1.3 %collective-permute-start.12 = (bf16[320,128]{1,0:T(8,128)(2,1)S(1)}, bf16[320,128]{1,0:T(8,128)(2,1)S(1)}, u32[]{:S(2)}, u32[]{:S(2)}) collective-permute-start(bf16[320,128]{1,0:T(8,128)(2,1)S(1)} %get-tuple-element.45), channel_id=1, source_target_pairs={{0,8},{4,12},{8,0},{12,4},{1,9},{5,13},{9,1},{13,5},{2,10},{6,14},... | collective-permute-start | bytes 245768 | tf_op jit(solution)/shard_map/ppermute | solution.py:350
  67.6 1.8 %collective-permute-start.13 = (bf16[320,128]{1,0:T(8,128)(2,1)S(1)}, bf16[320,128]{1,0:T(8,128)(2,1)S(1)}, u32[]{:S(2)}, u32[]{:S(2)}) collective-permute-start(bf16[320,128]{1,0:T(8,128)(2,1)S(1)} %get-tuple-element.46), channel_id=1, source_target_pairs={{0,12},{4,8},{8,4},{12,0},{1,13},{5,9},{9,5},{13,1},{2,14},{6,10},... | collective-permute-start | bytes 245768 | tf_op jit(solution)/shard_map/ppermute | solution.py:350
  69.5 0.6 cls_join.1.refs_0_
  70.0 0.4 collective-permute-start.24
  70.5 0.9 collective-permute-done.11.refs_2_
  71.4 1.2 %collective-permute-done.12.refs_3_ = bf16[320,128]{1,0:T(8,128)(2,1)S(1)} collective-permute-done((bf16[320,128]{1,0:T(8,128)(2,1)S(1)}, bf16[320,128]{1,0:T(8,128)(2,1)S(1)}, u32[]{:S(2)}, u32[]{:S(2)}) %collective-permute-start.12) | collective-permute-done | bytes 81952 | tf_op jit(solution)/shard_map/ppermute | solution.py:350
  72.6 1.5 %collective-permute-done.13.refs_4_ = bf16[320,128]{1,0:T(8,128)(2,1)S(1)} collective-permute-done((bf16[320,128]{1,0:T(8,128)(2,1)S(1)}, bf16[320,128]{1,0:T(8,128)(2,1)S(1)}, u32[]{:S(2)}, u32[]{:S(2)}) %collective-permute-start.13) | collective-permute-done | bytes 81952 | tf_op jit(solution)/shard_map/ppermute | solution.py:350
  74.0 0.6 shared_round.1
  74.6 0.9 collective-permute-start.14
  75.5 1.5 %collective-permute-start.15 = (bf16[288,128]{1,0:T(8,128)(2,1)S(1)}, bf16[288,128]{1,0:T(8,128)(2,1)S(1)}, u32[]{:S(2)}, u32[]{:S(2)}) collective-permute-start(bf16[288,128]{1,0:T(8,128)(2,1)S(1)} %get-tuple-element.47.refs_0_), channel_id=1, source_target_pairs={{0,8},{4,12},{8,0},{12,4},{1,9},{5,13},{9,1},{13,5},{2,10},{6,14},... | collective-permute-start | bytes 221192 | tf_op jit(solution)/shard_map/ppermute | solution.py:350
  77.1 2.0 %collective-permute-start.16 = (bf16[288,128]{1,0:T(8,128)(2,1)S(1)}, bf16[288,128]{1,0:T(8,128)(2,1)S(1)}, u32[]{:S(2)}, u32[]{:S(2)}) collective-permute-start(bf16[288,128]{1,0:T(8,128)(2,1)S(1)} %get-tuple-element.47.refs_0_), channel_id=1, source_target_pairs={{0,12},{4,8},{8,4},{12,0},{1,13},{5,9},{9,5},{13,1},{2,14},{6,10},... | collective-permute-start | bytes 221192 | tf_op jit(solution)/shard_map/ppermute | solution.py:350
  79.1 0.1 collective-permute-start.25
  79.1 2.2 %collective-permute-start.26 = (bf16[256,128]{1,0:T(8,128)(2,1)S(1)}, bf16[256,128]{1,0:T(8,128)(2,1)S(1)}, u32[]{:S(2)}, u32[]{:S(2)}) collective-permute-start(bf16[256,128]{1,0:T(8,128)(2,1)S(1)} %cls_join.1.refs_0_), channel_id=1, source_target_pairs={{0,12},{4,8},{8,4},{12,0},{1,13},{5,9},{9,5},{13,1},{2,14},{6,10},... | collective-permute-start | bytes 196616 | tf_op jit(solution)/shard_map/ppermute | solution.py:350
  81.4 4.8 %collective-permute-done.25.refs_2_ = bf16[256,128]{1,0:T(8,128)(2,1)S(1)} collective-permute-done((bf16[256,128]{1,0:T(8,128)(2,1)S(1)}, bf16[256,128]{1,0:T(8,128)(2,1)S(1)}, u32[]{:S(2)}, u32[]{:S(2)}) %collective-permute-start.25) | collective-permute-done | bytes 65568 | tf_op jit(solution)/shard_map/ppermute | solution.py:350
  86.2 0.8 cls_out.1
  87.0 1.0 %copy.12 = f32[3,3,128,99]{2,3,1,0:T(8,128)} copy(f32[3,3,128,99]{3,2,1,0:T(8,128)S(1)} %cls_out.1) | data formatting | bytes 912384
  88.0 0.0 collective-permute-done.15.refs_2_
  88.0 0.6 shared_join.1.refs_0_
  88.6 1.6 %collective-permute-start.17 = (bf16[1152,128]{1,0:T(8,128)(2,1)S(1)}, bf16[1152,128]{1,0:T(8,128)(2,1)S(1)}, u32[]{:S(2)}, u32[]{:S(2)}) collective-permute-start(bf16[1152,128]{1,0:T(8,128)(2,1)S(1)} %shared_join.1.refs_0_), channel_id=1, source_target_pairs={{0,2},{2,0},{1,3},{3,1},{4,6},{6,4},{5,7},{7,5},{8,10},{10,8},{9,1... | collective-permute-start | bytes 884744 | tf_op jit(solution)/shard_map/ppermute | solution.py:350
  90.2 0.5 slice_bitcast_fusion
  90.7 0.5 slice.11
  91.2 0.5 slice_bitcast_fusion.1
  91.7 3.7 %collective-permute-done.17.refs_1_ = bf16[1152,128]{1,0:T(8,128)(2,1)S(1)} collective-permute-done((bf16[1152,128]{1,0:T(8,128)(2,1)S(1)}, bf16[1152,128]{1,0:T(8,128)(2,1)S(1)}, u32[]{:S(2)}, u32[]{:S(2)}) %collective-permute-start.17) | collective-permute-done | bytes 294944 | tf_op jit(solution)/shard_map/ppermute | solution.py:350
  95.4 1.6 %shared_out.1 = f32[2304,128]{1,0:T(8,128)} custom-call(s32[5]{0:T(128)S(1)} %stack.19.where_ref, bf16[1152,128]{1,0:T(8,128)(2,1)S(1)} %shared_join.1.refs_0_, bf16[1152,128]{1,0:T(8,128)(2,1)S(1)} %collective-permute-done.17.refs_1_), custom_call_target="tpu_custom_call" | custom-call | tf_op jit(solution)/shard_map/shared_out/pallas_call | solution.py:25
  (21 shorter events, 0.0 us)
Async XLA Ops:
  0.6 24.9 %collective-permute-start.2 = (bf16[3,3,256,128]{3,2,1,0:T(8,128)(2,1)}, bf16[3,3,256,128]{3,2,1,0:T(8,128)(2,1)S(1)}, u32[]{:S(2)}, u32[]{:S(2)}) collective-permute-start(bf16[3,3,256,128]{3,2,1,0:T(8,128)(2,1)} %w1a_ref.1), channel_id=1, source_target_pairs={{0,1},{1,0},{2,3},{3,2},{4,5},{5,4},{6,7},{7,6},{8,9},{9,8},{10,11... | collective-permute-start | bytes 1769480 | tf_op jit(solution)/shard_map/ppermute | solution.py:350
  1.1 24.4 %copy-start.2 = (bf16[3,3,256,128]{3,2,1,0:T(8,128)(2,1)S(1)}, bf16[3,3,256,128]{3,2,1,0:T(8,128)(2,1)}, u32[]{:S(2)}) copy-start(bf16[3,3,256,128]{3,2,1,0:T(8,128)(2,1)} %w1a_ref.1) | copy-start | bytes 1769476
  1.2 24.4 %copy-start.4 = (f32[99]{0:T(128)S(1)}, f32[99]{0:T(128)}, u32[]{:S(2)}) copy-start(f32[99]{0:T(128)} %param.11) | copy-start | bytes 1192
  3.4 1.4 %copy-start = (bf16[1,12,256,256]{3,2,1,0:T(8,128)(2,1)S(1)}, bf16[1,12,256,256]{3,2,1,0:T(8,128)(2,1)}, u32[]{:S(2)}) copy-start(bf16[1,12,256,256]{3,2,1,0:T(8,128)(2,1)} %param.6) | copy-start | bytes 4718596
  4.8 0.7 copy-start.3
  6.8 9.9 %collective-permute-start = (bf16[784,256]{1,0:T(8,128)(2,1)S(1)}, bf16[784,256]{1,0:T(8,128)(2,1)S(1)}, u32[]{:S(2)}, u32[]{:S(2)}) collective-permute-start(bf16[784,256]{1,0:T(8,128)(2,1)S(1)} %get-tuple-element.32), channel_id=1, source_target_pairs={{1,4},{4,1},{5,8},{8,5},{9,12},{12,9},{3,6},{6,3},{7,10},{10,7},{1... | collective-permute-start | bytes 1204232 | tf_op jit(solution)/shard_map/ppermute | solution.py:386
  7.5 18.0 %collective-permute-start.3 = (bf16[1184,128]{1,0:T(8,128)(2,1)S(1)}, bf16[1184,128]{1,0:T(8,128)(2,1)S(1)}, u32[]{:S(2)}, u32[]{:S(2)}) collective-permute-start(bf16[1184,128]{1,0:T(8,128)(2,1)S(1)} %get-tuple-element.34.packa_ref), channel_id=1, source_target_pairs={{0,1},{1,0},{2,3},{3,2},{4,5},{5,4},{6,7},{7,6},{8,9},{9,8},{10,11... | collective-permute-start | bytes 909320 | tf_op jit(solution)/shard_map/ppermute | solution.py:350
  11.5 3.6 %collective-permute-start.4 = (f32[8,128]{1,0:T(8,128)S(1)}, f32[8,128]{1,0:T(8,128)S(1)}, u32[]{:S(2)}, u32[]{:S(2)}) collective-permute-start(f32[8,128]{1,0:T(8,128)S(1)} %get-tuple-element.35), channel_id=1, source_target_pairs={{0,2},{2,0},{1,3},{3,1},{4,6},{6,4},{5,7},{7,5},{8,10},{10,8},{9,1... | collective-permute-start | bytes 12296 | tf_op jit(solution)/shard_map/ppermute | solution.py:350
  15.1 5.0 %collective-permute-start.5 = (f32[8,128]{1,0:T(8,128)S(1)}, f32[8,128]{1,0:T(8,128)S(1)}, u32[]{:S(2)}, u32[]{:S(2)}) collective-permute-start(f32[8,128]{1,0:T(8,128)S(1)} %add.7.rest_0_), channel_id=1, source_target_pairs={{0,4},{4,0},{8,12},{12,8},{1,5},{5,1},{9,13},{13,9},{2,6},{6,2},{1... | collective-permute-start | bytes 12296 | tf_op jit(solution)/shard_map/ppermute | solution.py:350
  16.7 27.2 %collective-permute-start.1 = (bf16[784,256]{1,0:T(8,128)(2,1)S(1)}, bf16[784,256]{1,0:T(8,128)(2,1)S(1)}, u32[]{:S(2)}, u32[]{:S(2)}) collective-permute-start(bf16[784,256]{1,0:T(8,128)(2,1)S(1)} %collective-permute-done.halo_ref), channel_id=1, source_target_pairs={{0,1},{1,0},{2,3},{3,2},{4,5},{5,4},{6,7},{7,6},{8,9},{9,8},{10,11... | collective-permute-start | bytes 1204232 | tf_op jit(solution)/shard_map/ppermute | solution.py:350
  17.0 4.7 %collective-permute-start.6 = (f32[8,128]{1,0:T(8,128)S(1)}, f32[8,128]{1,0:T(8,128)S(1)}, u32[]{:S(2)}, u32[]{:S(2)}) collective-permute-start(f32[8,128]{1,0:T(8,128)S(1)} %add.7.rest_0_), channel_id=1, source_target_pairs={{0,8},{4,12},{8,0},{12,4},{1,9},{5,13},{9,1},{13,5},{2,10},{6,14},... | collective-permute-start | bytes 12296 | tf_op jit(solution)/shard_map/ppermute | solution.py:350
  20.1 5.4 %collective-permute-start.7 = (f32[8,128]{1,0:T(8,128)S(1)}, f32[8,128]{1,0:T(8,128)S(1)}, u32[]{:S(2)}, u32[]{:S(2)}) collective-permute-start(f32[8,128]{1,0:T(8,128)S(1)} %add.7.rest_0_), channel_id=1, source_target_pairs={{0,12},{4,8},{8,4},{12,0},{1,13},{5,9},{9,5},{13,1},{2,14},{6,10},... | collective-permute-start | bytes 12296 | tf_op jit(solution)/shard_map/ppermute | solution.py:350
  40.2 3.7 %copy-start.1 = (bf16[1,12,256,256]{3,2,1,0:T(8,128)(2,1)S(1)}, bf16[1,12,256,256]{3,2,1,0:T(8,128)(2,1)}, u32[]{:S(2)}) copy-start(bf16[1,12,256,256]{3,2,1,0:T(8,128)(2,1)} %param.6) | copy-start | bytes 4718596
  40.2 3.7 %collective-permute-start.8 = (bf16[6,256,128]{2,1,0:T(8,128)(2,1)S(1)}, bf16[6,256,128]{2,1,0:T(8,128)(2,1)S(1)}, u32[]{:S(2)}, u32[]{:S(2)}) collective-permute-start(bf16[6,256,128]{2,1,0:T(8,128)(2,1)S(1)} %get-tuple-element.37), channel_id=1, source_target_pairs={{0,1},{1,0},{2,3},{3,2},{4,5},{5,4},{6,7},{7,6},{8,9},{9,8},{10,11... | collective-permute-start | bytes 1179656 | tf_op jit(solution)/shard_map/ppermute | solution.py:350
  41.8 7.6 %collective-permute-start.18 = (f32[1024,128]{1,0:T(8,128)S(1)}, f32[1024,128]{1,0:T(8,128)S(1)}, u32[]{:S(2)}, u32[]{:S(2)}) collective-permute-start(f32[1024,128]{1,0:T(8,128)S(1)} %get-tuple-element.52), channel_id=1, source_target_pairs={{0,1},{1,0},{2,3},{3,2},{4,5},{5,4},{6,7},{7,6},{8,9},{9,8},{10,11... | collective-permute-start | bytes 1572872 | tf_op jit(solution)/shard_map/ppermute | solution.py:350
  42.3 1.5 %collective-permute-start.9 = (f32[8,128]{1,0:T(8,128)S(1)}, f32[8,128]{1,0:T(8,128)S(1)}, u32[]{:S(2)}, u32[]{:S(2)}) collective-permute-start(f32[8,128]{1,0:T(8,128)S(1)} %get-tuple-element.38.small_ref), channel_id=1, source_target_pairs={{0,1},{1,0},{2,3},{3,2},{4,5},{5,4},{6,7},{7,6},{8,9},{9,8},{10,11... | collective-permute-start | bytes 12296 | tf_op jit(solution)/shard_map/ppermute | solution.py:350
  47.8 16.6 %collective-permute-start.10 = (bf16[1184,128]{1,0:T(8,128)(2,1)S(1)}, bf16[1184,128]{1,0:T(8,128)(2,1)S(1)}, u32[]{:S(2)}, u32[]{:S(2)}) collective-permute-start(bf16[1184,128]{1,0:T(8,128)(2,1)S(1)} %get-tuple-element.41), channel_id=1, source_target_pairs={{0,2},{2,0},{1,3},{3,1},{4,6},{6,4},{5,7},{7,5},{8,10},{10,8},{9,1... | collective-permute-start | bytes 909320 | tf_op jit(solution)/shard_map/ppermute | solution.py:350
  50.0 5.2 %collective-permute-start.19 = (bf16[256,128]{1,0:T(8,128)(2,1)S(1)}, bf16[256,128]{1,0:T(8,128)(2,1)S(1)}, u32[]{:S(2)}, u32[]{:S(2)}) collective-permute-start(bf16[256,128]{1,0:T(8,128)(2,1)S(1)} %get-tuple-element.54), channel_id=1, source_target_pairs={{0,4},{4,0},{8,12},{12,8},{1,5},{5,1},{9,13},{13,9},{2,6},{6,2},{1... | collective-permute-start | bytes 196616 | tf_op jit(solution)/shard_map/ppermute | solution.py:350
  50.1 8.5 %collective-permute-start.20 = (bf16[256,128]{1,0:T(8,128)(2,1)S(1)}, bf16[256,128]{1,0:T(8,128)(2,1)S(1)}, u32[]{:S(2)}, u32[]{:S(2)}) collective-permute-start(bf16[256,128]{1,0:T(8,128)(2,1)S(1)} %get-tuple-element.55), channel_id=1, source_target_pairs={{0,8},{4,12},{8,0},{12,4},{1,9},{5,13},{9,1},{13,5},{2,10},{6,14},... | collective-permute-start | bytes 196616 | tf_op jit(solution)/shard_map/ppermute | solution.py:350
  51.9 6.7 %collective-permute-start.21 = (bf16[256,128]{1,0:T(8,128)(2,1)S(1)}, bf16[256,128]{1,0:T(8,128)(2,1)S(1)}, u32[]{:S(2)}, u32[]{:S(2)}) collective-permute-start(bf16[256,128]{1,0:T(8,128)(2,1)S(1)} %get-tuple-element.56), channel_id=1, source_target_pairs={{0,12},{4,8},{8,4},{12,0},{1,13},{5,9},{9,5},{13,1},{2,14},{6,10},... | collective-permute-start | bytes 196616 | tf_op jit(solution)/shard_map/ppermute | solution.py:350
  59.2 4.0 %collective-permute-start.22 = (bf16[128,128]{1,0:T(8,128)(2,1)S(1)}, bf16[128,128]{1,0:T(8,128)(2,1)S(1)}, u32[]{:S(2)}, u32[]{:S(2)}) collective-permute-start(bf16[128,128]{1,0:T(8,128)(2,1)S(1)} %get-tuple-element.58), channel_id=1, source_target_pairs={{0,2},{2,0},{1,3},{3,1},{4,6},{6,4},{5,7},{7,5},{8,10},{10,8},{9,1... | collective-permute-start | bytes 98312 | tf_op jit(solution)/shard_map/ppermute | solution.py:350
  63.7 5.7 %collective-permute-start.23 = (bf16[128,128]{1,0:T(8,128)(2,1)S(1)}, bf16[128,128]{1,0:T(8,128)(2,1)S(1)}, u32[]{:S(2)}, u32[]{:S(2)}) collective-permute-start(bf16[128,128]{1,0:T(8,128)(2,1)S(1)} %cls_round.1.refs_0_), channel_id=1, source_target_pairs={{0,2},{2,0},{1,3},{3,1},{4,6},{6,4},{5,7},{7,5},{8,10},{10,8},{9,1... | collective-permute-start | bytes 98312 | tf_op jit(solution)/shard_map/ppermute | solution.py:350
  65.0 6.4 %collective-permute-start.11 = (bf16[320,128]{1,0:T(8,128)(2,1)S(1)}, bf16[320,128]{1,0:T(8,128)(2,1)S(1)}, u32[]{:S(2)}, u32[]{:S(2)}) collective-permute-start(bf16[320,128]{1,0:T(8,128)(2,1)S(1)} %get-tuple-element.44), channel_id=1, source_target_pairs={{0,4},{4,0},{8,12},{12,8},{1,5},{5,1},{9,13},{13,9},{2,6},{6,2},{1... | collective-permute-start | bytes 245768 | tf_op jit(solution)/shard_map/ppermute | solution.py:350
  66.3 6.2 %collective-permute-start.12 = (bf16[320,128]{1,0:T(8,128)(2,1)S(1)}, bf16[320,128]{1,0:T(8,128)(2,1)S(1)}, u32[]{:S(2)}, u32[]{:S(2)}) collective-permute-start(bf16[320,128]{1,0:T(8,128)(2,1)S(1)} %get-tuple-element.45), channel_id=1, source_target_pairs={{0,8},{4,12},{8,0},{12,4},{1,9},{5,13},{9,1},{13,5},{2,10},{6,14},... | collective-permute-start | bytes 245768 | tf_op jit(solution)/shard_map/ppermute | solution.py:350
  67.6 6.4 %collective-permute-start.13 = (bf16[320,128]{1,0:T(8,128)(2,1)S(1)}, bf16[320,128]{1,0:T(8,128)(2,1)S(1)}, u32[]{:S(2)}, u32[]{:S(2)}) collective-permute-start(bf16[320,128]{1,0:T(8,128)(2,1)S(1)} %get-tuple-element.46), channel_id=1, source_target_pairs={{0,12},{4,8},{8,4},{12,0},{1,13},{5,9},{9,5},{13,1},{2,14},{6,10},... | collective-permute-start | bytes 245768 | tf_op jit(solution)/shard_map/ppermute | solution.py:350
  70.0 9.1 %collective-permute-start.24 = (bf16[256,128]{1,0:T(8,128)(2,1)S(1)}, bf16[256,128]{1,0:T(8,128)(2,1)S(1)}, u32[]{:S(2)}, u32[]{:S(2)}) collective-permute-start(bf16[256,128]{1,0:T(8,128)(2,1)S(1)} %cls_join.1.refs_0_), channel_id=1, source_target_pairs={{0,4},{4,0},{8,12},{12,8},{1,5},{5,1},{9,13},{13,9},{2,6},{6,2},{1... | collective-permute-start | bytes 196616 | tf_op jit(solution)/shard_map/ppermute | solution.py:350
  74.6 13.4 %collective-permute-start.14 = (bf16[288,128]{1,0:T(8,128)(2,1)S(1)}, bf16[288,128]{1,0:T(8,128)(2,1)S(1)}, u32[]{:S(2)}, u32[]{:S(2)}) collective-permute-start(bf16[288,128]{1,0:T(8,128)(2,1)S(1)} %get-tuple-element.47.refs_0_), channel_id=1, source_target_pairs={{0,4},{4,0},{8,12},{12,8},{1,5},{5,1},{9,13},{13,9},{2,6},{6,2},{1... | collective-permute-start | bytes 221192 | tf_op jit(solution)/shard_map/ppermute | solution.py:350
  75.5 12.5 %collective-permute-start.15 = (bf16[288,128]{1,0:T(8,128)(2,1)S(1)}, bf16[288,128]{1,0:T(8,128)(2,1)S(1)}, u32[]{:S(2)}, u32[]{:S(2)}) collective-permute-start(bf16[288,128]{1,0:T(8,128)(2,1)S(1)} %get-tuple-element.47.refs_0_), channel_id=1, source_target_pairs={{0,8},{4,12},{8,0},{12,4},{1,9},{5,13},{9,1},{13,5},{2,10},{6,14},... | collective-permute-start | bytes 221192 | tf_op jit(solution)/shard_map/ppermute | solution.py:350
  77.1 11.0 %collective-permute-start.16 = (bf16[288,128]{1,0:T(8,128)(2,1)S(1)}, bf16[288,128]{1,0:T(8,128)(2,1)S(1)}, u32[]{:S(2)}, u32[]{:S(2)}) collective-permute-start(bf16[288,128]{1,0:T(8,128)(2,1)S(1)} %get-tuple-element.47.refs_0_), channel_id=1, source_target_pairs={{0,12},{4,8},{8,4},{12,0},{1,13},{5,9},{9,5},{13,1},{2,14},{6,10},... | collective-permute-start | bytes 221192 | tf_op jit(solution)/shard_map/ppermute | solution.py:350
  79.1 7.1 %collective-permute-start.25 = (bf16[256,128]{1,0:T(8,128)(2,1)S(1)}, bf16[256,128]{1,0:T(8,128)(2,1)S(1)}, u32[]{:S(2)}, u32[]{:S(2)}) collective-permute-start(bf16[256,128]{1,0:T(8,128)(2,1)S(1)} %cls_join.1.refs_0_), channel_id=1, source_target_pairs={{0,8},{4,12},{8,0},{12,4},{1,9},{5,13},{9,1},{13,5},{2,10},{6,14},... | collective-permute-start | bytes 196616 | tf_op jit(solution)/shard_map/ppermute | solution.py:350
  79.1 7.1 %collective-permute-start.26 = (bf16[256,128]{1,0:T(8,128)(2,1)S(1)}, bf16[256,128]{1,0:T(8,128)(2,1)S(1)}, u32[]{:S(2)}, u32[]{:S(2)}) collective-permute-start(bf16[256,128]{1,0:T(8,128)(2,1)S(1)} %cls_join.1.refs_0_), channel_id=1, source_target_pairs={{0,12},{4,8},{8,4},{12,0},{1,13},{5,9},{9,5},{13,1},{2,14},{6,10},... | collective-permute-start | bytes 196616 | tf_op jit(solution)/shard_map/ppermute | solution.py:350
  88.6 6.8 %collective-permute-start.17 = (bf16[1152,128]{1,0:T(8,128)(2,1)S(1)}, bf16[1152,128]{1,0:T(8,128)(2,1)S(1)}, u32[]{:S(2)}, u32[]{:S(2)}) collective-permute-start(bf16[1152,128]{1,0:T(8,128)(2,1)S(1)} %shared_join.1.refs_0_), channel_id=1, source_target_pairs={{0,2},{2,0},{1,3},{3,1},{4,6},{6,4},{5,7},{7,5},{8,10},{10,8},{9,1... | collective-permute-start | bytes 884744 | tf_op jit(solution)/shard_map/ppermute | solution.py:350

commit v2 on v1

--- a/solution.py
+++ b/solution.py
@@ -18,13 +18,20 @@
 BF16 = jnp.bfloat16
 F32 = jnp.float32
 VMEM = pl.BlockSpec(memory_space=pltpu.VMEM)
+ANY = pl.BlockSpec(memory_space=pl.ANY)
 SMEM = pl.BlockSpec(memory_space=pltpu.SMEM)
 
 
-def call(kernel, name, outs, inputs, scratch=()):
+def call(kernel, name, outs, inputs, scratch=(), after=()):
+    n = len(inputs)
+    inputs = list(inputs) + list(after)
+
+    def body(*refs):
+        kernel(*refs[:n], *refs[len(inputs) :])
+
     return pl.pallas_call(
-        kernel,
-        in_specs=[SMEM] + [VMEM] * (len(inputs) - 1),
+        body,
+        in_specs=[SMEM] + [VMEM] * (n - 1) + [ANY] * len(after),
         out_specs=[VMEM] * len(outs),
         out_shape=[jax.ShapeDtypeStruct(shape, kind) for shape, kind in outs],
         scratch_shapes=[pltpu.VMEM(shape, kind) for shape, kind in scratch],
@@ -63,18 +70,22 @@
     return part[0:8] + part[8:16] + part[16:24]
 
 
-def prep_kernel(where_ref, f_ref, lab_ref, w2_ref, b1_ref, msg_ref, labt_ref, pack_ref, count_ref):
-    rows, cols, chans = f_ref.shape
+def count_kernel(lab_ref, count_ref):
+    lab = lab_ref[...]
+    count_ref[...] = jnp.full(count_ref.shape, jnp.sum(jnp.where(lab > 0, 1.0, 0.0)), F32)
+
+
+def prep_kernel(where_ref, f_ref, lab_ref, w2_ref, b1_ref, msg_ref, labt_ref, pack_ref):
+    rows = lab_ref.shape[0]
+    cols = f_ref.shape[1]
     c = where_ref[0]
     for k in range(3):
-        msg_ref[cols * k : cols * (k + 1)] = f_ref[(rows - 3) * c + k]
-    lab = lab_ref[...]
-    count_ref[...] = jnp.full(count_ref.shape, jnp.sum(jnp.where(lab > 0, 1.0, 0.0)), F32)
-    size = lab.shape[1]
+        msg_ref[cols * k : cols * (k + 1)] = f_ref[k]
+    size = lab_ref.shape[2]
     place = lax.broadcasted_iota(jnp.int32, (ANCH_ROWS, size), 1) % ANCH
     anchor = lax.broadcasted_iota(jnp.int32, (ANCH_ROWS, size), 0)
     mine = jnp.where(place == anchor, 1.0, 0.0)
-    left = jnp.concatenate([mine * lab[r : r + 1].astype(F32) for r in range(rows)], axis=0).astype(BF16)
+    left = jnp.concatenate([mine * lab_ref[r].astype(F32) for r in range(rows)], axis=0).astype(BF16)
     offset = lax.broadcasted_iota(jnp.int32, (size, cols), 0) - ANCH * lax.broadcasted_iota(jnp.int32, (size, cols), 1)
     pick = jnp.where(jnp.logical_and(offset >= 0, offset < ANCH), 1.0, 0.0).astype(BF16)
     turned = dot(left, pick).astype(BF16)
@@ -83,18 +94,17 @@
     msg_ref[3 * cols : 3 * cols + ANCH_ROWS] = jnp.where(
         c == 0, turned[:ANCH_ROWS].astype(F32), turned[ANCH_ROWS * (rows - 1) :].astype(F32)
     ).astype(BF16)
-    deep = w2_ref.shape[2]
+    deep = w2_ref.shape[3]
     for tap in range(9):
-        pack_ref[deep * tap : deep * (tap + 1)] = jnp.zeros((deep, LANES), BF16)
-        pack_ref[deep * tap : deep * (tap + 1), :LOGITS] = w2_ref[tap // 3, tap % 3]
-    bias = jnp.broadcast_to(b1_ref[...], (8, deep))
-    put_trio(pack_ref, 9 * deep, bias)
+        pack_ref[LANES * tap : LANES * (tap + 1)] = jnp.zeros((LANES, deep), BF16)
+        pack_ref[LANES * tap : LANES * tap + LOGITS] = w2_ref[tap // 3, tap % 3]
+    put_trio(pack_ref, 9 * LANES, jnp.broadcast_to(b1_ref[...], (8, deep)))
 
 
 def head_kernel(
-    where_ref, f_ref, halo_ref, labt_ref, w1a_ref, w1b_ref, packa_ref, packb_ref, b2_ref, *rest,
+    where_ref, f_ref, halo_ref, labt_ref, w1a_ref, w1b_ref, packa_ref, packb_ref, b2_ref,
+    hid_ref, dz_ref, loss_ref, xw_ref,
 ):
-    *count_refs, hid_ref, dt_ref, own_ref, other_ref, small_ref, xw_ref, dlog_ref = rest
 
     half = f_ref.shape[0] // 2
     cols = f_ref.shape[1]
@@ -114,10 +124,7 @@
     w1 = jnp.concatenate(w1, axis=0)
     chans = w1.shape[1] // 3
     deep = chans // 2
-    b1 = jnp.concatenate([get_trio(packa_ref, 9 * deep)[:1], get_trio(packb_ref, 9 * deep)[:1]], axis=1)
-    counts = [ref[...] for ref in count_refs]
-    while len(counts) > 1:
-        counts = [counts[k] + counts[k + 1] for k in range(0, len(counts), 2)]
+    b1 = jnp.concatenate([get_trio(packa_ref, 9 * LANES)[:1], get_trio(packb_ref, 9 * LANES)[:1]], axis=1)
 
     def conv1(h, carry):
         lhs = jnp.concatenate([xw_ref[h], xw_ref[h + 1], xw_ref[h + 2]], axis=1)
@@ -136,21 +143,16 @@
     anchor = lax.broadcasted_iota(jnp.int32, (ANCH_ROWS, LANES), 0)
     column = lax.broadcasted_iota(jnp.int32, (ANCH_ROWS, LANES), 1)
     spread = jnp.where(jnp.logical_and(column // CLASSES == anchor, column < LOGITS), 1.0, 0.0).astype(BF16)
-
-
-    def tap(ref, i, j):
-        return ref[deep * (3 * i + j) : deep * (3 * i + j + 1)]
-
-    w2 = [[jnp.concatenate([tap(packa_ref, i, j), tap(packb_ref, i, j)], axis=0) for j in range(3)] for i in range(3)]
-    w2n = [jnp.concatenate(w2[i], axis=1) for i in range(3)]
-    w2n = jnp.concatenate(w2n, axis=0)
+    w2 = [
+        jnp.concatenate([jnp.concatenate([tap(packa_ref, i, j), tap(packb_ref, i, j)], axis=1) for j in range(3)], axis=0)
+        for i in range(3)
+    ]
+    w2 = jnp.concatenate(w2, axis=1)
     b2 = jnp.concatenate([b2_ref[...], jnp.zeros((1, LANES - LOGITS), F32)], axis=1)
-    inverse = 1.0 / counts[0][:1]
-
-    def focal(l, carry):
-        gcb, loss = carry
+
+    def focal(l, loss):
         lhs = jnp.concatenate([hid_ref[l], hid_ref[l + 1], hid_ref[l + 2]], axis=1)
-        y = dot(lhs, w2n)
+        y = dot(lhs, w2, ((1,), (1,)))
         z = shift_cells(y[:, :LANES], 1) + y[:, LANES : 2 * LANES] + shift_cells(y[:, 2 * LANES :], -1) + b2
         at_halo = jnp.where(c == 0, l == 0, l == half + 1)
         local = jnp.clip(l - 1 + half * c, 0, 2 * half - 1)
@@ -171,33 +173,51 @@
         soft = jnp.maximum(u, 0.0) + jnp.log1p(e)
         ws = jnp.where(keep, jnp.where(hit, 0.25, 0.75), 0.0) * s * s
         slope = ws * (2.0 * comp * soft + s)
-        dz = jnp.where(hit, -slope, slope) * inverse
+        dz_ref[l] = jnp.where(hit, -slope, slope)
+        own = jnp.logical_and(l >= 1, l <= half)
+        return loss + jnp.where(own, 1.0, 0.0) * jnp.sum(ws * soft, axis=0, keepdims=True)
+
+    loss_ref[...] = lax.fori_loop(0, half + 2, focal, jnp.zeros((1, LANES), F32))
+
+
+def tap(ref, i, j):
+    return ref[LANES * (3 * i + j) : LANES * (3 * i + j + 1)]
+
+
+def back_kernel(where_ref, hid_ref, dz_ref, loss_ref, packa_ref, packb_ref, *rest):
+    *count_refs, dt_ref, own_ref, other_ref, small_ref, dlog_ref = rest
+    half, _, cols = dt_ref.shape
+    chans = hid_ref.shape[2]
+    inverse = 1.0 / pair_sum([ref[...] for ref in count_refs])[:1]
+
+    def scaled(l):
+        dz = dz_ref[l] * inverse
         d16 = dz.astype(BF16)
         dlog_ref[l] = d16
-        own = jnp.logical_and(l >= 1, l <= half)
-        weight = jnp.where(own, 1.0, 0.0)
-        gcb = gcb + weight * jnp.sum(dz, axis=0, keepdims=True)
-        loss = loss + weight * jnp.sum(ws * soft, axis=0, keepdims=True)
-
-        @pl.when(own)
-        def _():
-            turned = jnp.transpose(d16.astype(F32))[:CLS_ROWS]
-            cell = lax.broadcasted_iota(jnp.int32, turned.shape, 1)
-            left = jnp.where(cell == cols - 1, 0.0, pltpu.roll(turned, cols - 1, axis=1))
-            right = jnp.where(cell == 0, 0.0, pltpu.roll(turned, 1, axis=1))
-            dt_ref[l - 1] = jnp.concatenate([left, turned, right], axis=0).astype(BF16)
-
-        return gcb, loss
-
-    zero = jnp.zeros((1, LANES), F32)
-    gcb, loss = lax.fori_loop(0, half + 2, focal, (zero, zero))
-
-    w2t = [jnp.concatenate([w2[i][j] for i in range(3)], axis=1) for j in range(3)]
+        return dz, d16
+
+    scaled(0)
+    scaled(half + 1)
+
+    def turn(d, gcb):
+        dz, d16 = scaled(d + 1)
+        turned = jnp.transpose(d16.astype(F32))[:CLS_ROWS]
+        cell = lax.broadcasted_iota(jnp.int32, turned.shape, 1)
+        left = jnp.where(cell == cols - 1, 0.0, pltpu.roll(turned, cols - 1, axis=1))
+        right = jnp.where(cell == 0, 0.0, pltpu.roll(turned, 1, axis=1))
+        dt_ref[d] = jnp.concatenate([left, turned, right], axis=0).astype(BF16)
+        return gcb + jnp.sum(dz, axis=0, keepdims=True)
+
+    gcb = lax.fori_loop(0, half, turn, jnp.zeros((1, LANES), F32))
+    w2t = [
+        jnp.concatenate([x for j in range(3) for x in (tap(packa_ref, i, j), tap(packb_ref, i, j))], axis=1)
+        for i in range(3)
+    ]
     w2t = jnp.concatenate(w2t, axis=0)
 
     def dpre_row(d, gsb):
         lhs = jnp.concatenate([dlog_ref[d + 2], dlog_ref[d + 1], dlog_ref[d]], axis=1)
-        q = dot(lhs, w2t, ((1,), (1,)))
+        q = dot(lhs, w2t)
         dhid = shift_cells(q[:, :chans], -1) + q[:, chans : 2 * chans] + shift_cells(q[:, 2 * chans :], 1)
         dpre = jnp.where(hid_ref[d + 2].astype(F32) > 0.0, dhid, 0.0)
         d16 = dpre.astype(BF16)
@@ -207,7 +227,7 @@
 
     gsb = lax.fori_loop(0, half, dpre_row, jnp.zeros((1, chans), F32))
     small_ref[0:1] = gcb
-    small_ref[1:2] = jnp.broadcast_to(jnp.sum(loss, axis=1, keepdims=True), (1, LANES)) * inverse
+    small_ref[1:2] = jnp.broadcast_to(jnp.sum(loss_ref[...], axis=1, keepdims=True), (1, LANES)) * inverse
     small_ref[2:3] = jnp.zeros((1, LANES), F32)
     small_ref[3:4] = gsb[:, : chans // 2]
     small_ref[4:5] = gsb[:, chans // 2 :]
@@ -309,17 +329,17 @@
             put_trio(ref, keep_ref.shape[0], sums)
 
 
-def step(where, slot, size, base, small, arrived, name):
+def step(where, slot, size, base, small, arrived, name, after=()):
     trio = TRIO if small is not None else 0
     rows, width = base.shape
     inputs = [where, base] + ([small] if trio else []) + list(arrived)
     smalls = [((8, LANES), F32)] if trio else []
     kernel = functools.partial(step_kernel, slot, len(arrived), trio)
     if slot is None:
-        return call(kernel, name, [((rows, width), BF16)] + smalls, inputs)
+        return call(kernel, name, [((rows, width), BF16)] + smalls, inputs, after=after)
     share = rows // size
     outs = [((share, width), F32)] + smalls + [((share + trio, width), BF16)] * (size - 1)
-    return call(kernel, name, outs, inputs, [((rows, width), F32)])
+    return call(kernel, name, outs, inputs, [((rows, width), F32)], after)
 
 
 def join_kernel(slot, where_ref, *refs):
@@ -330,10 +350,10 @@
         out_ref[pl.ds(pl.multiple_of((me ^ k) * rows, 8), rows)] = ref[...].astype(out_ref.dtype)
 
 
-def join(where, slot, parts, kind, name):
+def join(where, slot, parts, kind, name, after=()):
     rows, width = parts[0].shape
     return call(
-        functools.partial(join_kernel, slot), name, [((rows * len(parts), width), kind)], [where] + parts
+        functools.partial(join_kernel, slot), name, [((rows * len(parts), width), kind)], [where] + parts, after=after
     )[0]
 
 
@@ -341,8 +361,7 @@
     *in_refs, out_ref, whole_ref = refs
     join_kernel(slot, where_ref, *in_refs, whole_ref)
     for tap in range(9):
-        turned = jnp.transpose(whole_ref[CLS_ROWS * tap : CLS_ROWS * tap + LANES])
-        out_ref[tap // 3, tap % 3] = turned[:, :LOGITS]
+        out_ref[tap // 3, tap % 3] = whole_ref[CLS_ROWS * tap : CLS_ROWS * tap + LOGITS]
 
 
 def swap(x, axis, bit=1):
@@ -370,16 +389,36 @@
     where = jnp.stack([c, t * rows + half * c, jnp.int32(tiles * rows), t, lax.axis_index("batch")]).astype(jnp.int32)
     TILE, BATCH = 3, 4
 
-    msg, labt, pack, count = call(
-        prep_kernel, "prep",
-        [
-            ((3 * cols + ANCH_ROWS, chans), BF16),
-            ((rows, ANCH_ROWS, cols), BF16),
-            ((9 * outs + TRIO, LANES), BF16),
-            ((8, LANES), F32),
+    lab = labels.reshape(rows, 1, labels.shape[2])
+    count = pl.pallas_call(
+        count_kernel, in_specs=[VMEM], out_specs=VMEM, out_shape=jax.ShapeDtypeStruct((8, LANES), F32), name="count"
+    )(lab)
+    whole = lambda *shape: pl.BlockSpec(shape, lambda g, w: (0,) * len(shape))
+    w2 = jnp.swapaxes(w_cls, 2, 3)
+    msg, labt, pack = pl.pallas_call(
+        prep_kernel,
+        grid_spec=pltpu.PrefetchScalarGridSpec(
+            num_scalar_prefetch=1,
+            grid=(1,),
+            in_specs=[
+                pl.BlockSpec((3, cols, chans), lambda g, w: ((rows // 3 - 1) * w[0], 0, 0)),
+                whole(*lab.shape),
+                whole(*w2.shape),
+                whole(1, outs),
+            ],
+            out_specs=[
+                whole(3 * cols + ANCH_ROWS, chans),
+                whole(rows, ANCH_ROWS, cols),
+                whole(9 * LANES + TRIO, outs),
+            ],
+        ),
+        out_shape=[
+            jax.ShapeDtypeStruct((3 * cols + ANCH_ROWS, chans), BF16),
+            jax.ShapeDtypeStruct((rows, ANCH_ROWS, cols), BF16),
+            jax.ShapeDtypeStruct((9 * LANES + TRIO, outs), BF16),
         ],
-        [where, f, labels[0], w_cls, b_shared.reshape(1, outs)],
-    )
+        name="prep",
+    )(where, f, lab, w2, b_shared.reshape(1, outs))
     pairs = []
     for i in range(tiles - 1):
         pairs += [(2 * i + 1, 2 * i + 2), (2 * i + 2, 2 * i + 1)]
@@ -389,17 +428,22 @@
     count = pair_sum([count] + others(count, "batch"))
     counts = [count] + others(count, "tile")
 
-    hid, dt, own, other, small = call(
+    hid, dz, loss = call(
         head_kernel, "head",
+        [((half + 4, cols, chans), BF16), ((half + 2, cols, LANES), F32), ((1, LANES), F32)],
+        [where, f, halo, labt, w_shared, w1b, pack, packb, b_cls.reshape(1, LOGITS)],
+        [((half + 6, cols, chans), BF16)],
+    )
+    dt, own, other, small = call(
+        back_kernel, "back",
         [
-            ((half + 4, cols, chans), BF16),
             ((half, 3 * CLS_ROWS, cols), BF16),
             ((half, cols, outs), BF16),
             ((half, cols, outs), BF16),
             ((8, LANES), F32),
         ],
-        [where, f, halo, labt, w_shared, w1b, pack, packb, b_cls.reshape(1, LOGITS)] + counts,
-        [((half + 6, cols, chans), BF16), ((half + 2, cols, LANES), BF16)],
+        [where, hid, dz, loss, pack, packb] + counts,
+        [((half + 2, cols, LANES), BF16)],
     )
     theirs = swap(other, "chan")
     far = swap(halo, "chan")
@@ -421,24 +465,24 @@
     arrived = exchange(sends, "batch")
     carrived = exchange(csends, "tile")
     keep, small, *sends = step(where, TILE, tiles, keep, small, arrived, "shared_tile")
-    ckeep, *csends = step(where, BATCH, pages, ckeep, None, carrived, "cls_batch")
+    ckeep, *csends = step(where, BATCH, pages, ckeep, None, carrived, "cls_batch", [small])
     arrived = exchange(sends, "tile")
     carrived = exchange(csends, "batch")
     done, small = step(where, None, 1, keep, small, arrived, "shared_round")
-    (cdone,) = step(where, None, 1, ckeep, None, carrived, "cls_round")
+    (cdone,) = step(where, None, 1, ckeep, None, carrived, "cls_round", [small])
     block = join(where, TILE, [done] + others(done, "tile"), BF16, "shared_join")
-    cblock = join(where, BATCH, [cdone] + others(cdone, "batch"), BF16, "cls_join")
+    cblock = join(where, BATCH, [cdone] + others(cdone, "batch"), BF16, "cls_join", [block])
     grad_shared = join(where, BATCH, [block] + others(block, "batch"), F32, "shared_out")
     (grad_cls,) = call(
         functools.partial(join_cls_kernel, TILE), "cls_out",
-        [((3, 3, outs, LOGITS), F32)],
+        [((3, 3, LOGITS, outs), F32)],
         [where, cblock] + others(cblock, "tile"),
         [((CLS_TOTAL, outs), F32)],
     )
     return (
         grad_shared.reshape(3, 3, chans, outs),
         small[3],
-        grad_cls,
+        jnp.swapaxes(grad_cls, 2, 3),
         small[0, :LOGITS],
         small[1, :1],
     )

time: 97.3 us -> 98.2 us (level)
  waiting for transfers between devices: 27.3 us -> 17.8 us
  starting transfers between devices: 34.1 us -> 41.3 us
  Pallas kernels: 27.9 us -> 33.2 us
  local copies, waits for them, and re-layouts: 6.88 us -> 4.03 us
    ppermute x26, waiting for transfers between devices: 27.3 us -> 17.8 us  [swap(): return lax.ppermute(x, axis, [(i, i ^ bit) for i in range(size)])]
    ppermute x26, starting transfers between devices: 33.4 us -> 40.6 us  [swap(): return lax.ppermute(x, axis, [(i, i ^ bit) for i in range(size)])]
    pallas_call x13 -> x15, Pallas kernels: 27.9 us -> 33.2 us  [the longest x13 27.9 us: call(): pl.pallas_call(body, in_specs=[SMEM] + [VMEM] * (n - 1) + [ANY] * len(aft...]
    unnamed x13 -> x14, local copies, waits for them, and re-layouts: 5.26 us -> 1.87 us
  transfers between devices with their start and end apart: 27 -> 27, of which waited for: 12 -> 6; matrix products, arithmetic and copies ran while one was open for 5% -> 3% of each run, Pallas kernels for 27% -> 32%
where the time goes in v2:
time: 98.2 us; the launch traced here: 97.9 us
  starting transfers between devices  41.3 us (42%)
  Pallas kernels  33.2 us (34%)
  waiting for transfers between devices  17.8 us (18%)
  local copies, waits for them, and re-layouts  4.03 us (4%)
    ppermute x26, starting transfers between devices, swap(): return lax.ppermute(x, axis, [(i, i ^ bit) for i in range(size)])  40.6 us
    pallas_call x13, Pallas kernels, call(): pl.pallas_call(body, in_specs=[SMEM] + [VMEM] * (n - 1) + [ANY] * len(aft...  27.9 us
    ppermute x26, waiting for transfers between devices, swap(): return lax.ppermute(x, axis, [(i, i ^ bit) for i in range(size)])  17.8 us
    pallas_call x1, Pallas kernels, shards(): pl.pallas_call(prep_kernel, grid_spec=pltpu.PrefetchScalarGridSpec(num_sc...  3.5 us
  transfers between devices with their start and end apart: 27, of which 6 were waited for; matrix products, arithmetic and copies ran while one was open for 3% of the time, Pallas kernels for 32%

profile of v2, /device:TPU:0, one launch (start us, length us, event | category | flops | bytes accessed | tf_op | source)
XLA Modules:
  0.0 97.9 jit_solution(1993216303632949165)
XLA Ops:
  0.7 0.5 collective-permute-start.2
  1.2 0.6 stack.19.where_ref.refs_0_
  1.8 3.5 %prep.1 = (bf16[784,256]{1,0:T(8,128)(2,1)}, bf16[12,16,256]{2,1,0:T(8,128)(2,1)}, bf16[1184,128]{1,0:T(8,128)(2,1)}) custom-call(s32[5]{0:T(128)} %stack.19.where_ref.refs_0_, bf16[12,256,256]{2,1,0:T(8,128)(2,1)} %bitcast.16, s32[12,1,2304]{2,1,0:T(1,128)} %bitcast.22, bf16[3,3,99,128]{3,2,1,0:T(8,128)(2,1)} %bitcast.24, f32[1,128]{1,0:T(1,128)} %bitcast.25), custom_call_target="tpu_custom_call" | custom-call | tf_op jit(solution)/shard_map/prep/pallas_call | solution.py:398
  5.3 0.7 collective-permute-start
  6.0 4.0 %collective-permute-start.3 = (bf16[1184,128]{1,0:T(8,128)(2,1)}, bf16[1184,128]{1,0:T(8,128)(2,1)S(1)}, u32[]{:S(2)}, u32[]{:S(2)}) collective-permute-start(bf16[1184,128]{1,0:T(8,128)(2,1)} %get-tuple-element.35.refs_6_.refs_4_), channel_id=1, source_target_pairs={{0,1},{1,0},{2,3},{3,2},{4,5},{5,4},{6,7},{7,6},{8,9},{9,8},{10,11... | collective-permute-start | bytes 909320 | tf_op jit(solution)/shard_map/ppermute | solution.py:369
  10.0 1.8 %count.1 = f32[8,128]{1,0:T(8,128)} custom-call(s32[12,1,2304]{2,1,0:T(1,128)} %bitcast.23), custom_call_target="tpu_custom_call" | custom-call | tf_op jit(solution)/shard_map/count/pallas_call | solution.py:393
  11.8 1.5 %collective-permute-start.4 = (f32[8,128]{1,0:T(8,128)}, f32[8,128]{1,0:T(8,128)S(1)}, u32[]{:S(2)}, u32[]{:S(2)}) collective-permute-start(f32[8,128]{1,0:T(8,128)} %count.1), channel_id=1, source_target_pairs={{0,2},{2,0},{1,3},{3,1},{4,6},{6,4},{5,7},{7,5},{8,10},{10,8},{9,1... | collective-permute-start | bytes 12296 | tf_op jit(solution)/shard_map/ppermute | solution.py:369
  13.3 2.4 %collective-permute-start.1 = (bf16[784,256]{1,0:T(8,128)(2,1)S(1)}, bf16[784,256]{1,0:T(8,128)(2,1)S(1)}, u32[]{:S(2)}, u32[]{:S(2)}) collective-permute-start(bf16[784,256]{1,0:T(8,128)(2,1)S(1)} %collective-permute-done.refs_2_), channel_id=1, source_target_pairs={{0,1},{1,0},{2,3},{3,2},{4,5},{5,4},{6,7},{7,6},{8,9},{9,8},{10,11... | collective-permute-start | bytes 1204232 | tf_op jit(solution)/shard_map/ppermute | solution.py:369
  15.7 0.7 add.7.refs_6_
  16.4 2.0 %collective-permute-start.5 = (f32[8,128]{1,0:T(8,128)S(1)}, f32[8,128]{1,0:T(8,128)S(1)}, u32[]{:S(2)}, u32[]{:S(2)}) collective-permute-start(f32[8,128]{1,0:T(8,128)S(1)} %add.7.refs_6_), channel_id=1, source_target_pairs={{0,4},{4,0},{8,12},{12,8},{1,5},{5,1},{9,13},{13,9},{2,6},{6,2},{1... | collective-permute-start | bytes 12296 | tf_op jit(solution)/shard_map/ppermute | solution.py:369
  18.4 2.1 %collective-permute-start.6 = (f32[8,128]{1,0:T(8,128)S(1)}, f32[8,128]{1,0:T(8,128)S(1)}, u32[]{:S(2)}, u32[]{:S(2)}) collective-permute-start(f32[8,128]{1,0:T(8,128)S(1)} %add.7.refs_6_), channel_id=1, source_target_pairs={{0,8},{4,12},{8,0},{12,4},{1,9},{5,13},{9,1},{13,5},{2,10},{6,14},... | collective-permute-start | bytes 12296 | tf_op jit(solution)/shard_map/ppermute | solution.py:369
  20.5 0.4 collective-permute-start.7
  20.9 0.0 copy-start.1
  21.0 1.0 copy-done.1
  21.9 0.9 copy-done.5
  22.8 11.1 %head.1 = (bf16[10,256,256]{2,1,0:T(8,128)(2,1)S(1)}, f32[8,256,128]{2,1,0:T(8,128)S(1)}, f32[1,128]{1,0:T(1,128)S(1)}) custom-call(s32[5]{0:T(128)S(1)} %copy-done.4, bf16[12,256,256]{2,1,0:T(8,128)(2,1)} %bitcast.17, bf16[784,256]{1,0:T(8,128)(2,1)S(1)} %collective-permute-done.refs_2_, bf16[12,16,256]{2,1,0:T(8,128)(2,1)S(1)} %copy-done.5, ...), custom_call_target="tpu_custom_call" | custom-call | tf_op jit(solution)/shard_map/head/pallas_call | solution.py:32
  33.9 0.0 collective-permute-done.6.refs_8_
  34.0 4.3 %back.1 = (bf16[6,336,256]{2,1,0:T(8,128)(2,1)S(1)}, bf16[6,256,128]{2,1,0:T(8,128)(2,1)S(1)}, bf16[6,256,128]{2,1,0:T(8,128)(2,1)S(1)}, f32[8,128]{1,0:T(8,128)S(1)}) custom-call(s32[5]{0:T(128)S(1)} %copy-done.4, bf16[10,256,256]{2,1,0:T(8,128)(2,1)S(1)} %get-tuple-element.36.refs_1_, f32[8,256,128]{2,1,0:T(8,128)S(1)} %get-tuple-element.37.refs_2_, ...), custom_call_target="tpu_custom_call" | custom-call | tf_op jit(solution)/shard_map/back/pallas_call | solution.py:32
  38.2 0.0 collective-permute-start.8
  38.3 1.5 %cls.1 = (f32[1024,128]{1,0:T(8,128)S(1)}, f32[1024,128]{1,0:T(8,128)S(1)}) custom-call(s32[5]{0:T(128)S(1)} %copy-done.4, bf16[10,256,256]{2,1,0:T(8,128)(2,1)S(1)} %get-tuple-element.36.refs_1_, bf16[6,336,256]{2,1,0:T(8,128)(2,1)S(1)} %get-tuple-element.52.refs_2_), custom_call_target="tpu_custom_call" | custom-call | tf_op jit(solution)/shard_map/cls/pallas_call | solution.py:32
  39.8 0.6 collective-permute-start.18
  40.3 0.1 collective-permute-start.9
  40.4 1.5 %collective-permute-done.9.refs_7_ = f32[8,128]{1,0:T(8,128)S(1)} collective-permute-done((f32[8,128]{1,0:T(8,128)S(1)}, f32[8,128]{1,0:T(8,128)S(1)}, u32[]{:S(2)}, u32[]{:S(2)}) %collective-permute-start.9) | collective-permute-done | bytes 4128 | tf_op jit(solution)/shard_map/ppermute | solution.py:369
  41.9 0.0 collective-permute-done.1.refs_3_
  41.9 0.0 collective-permute-done.8.refs_5_
  41.9 3.9 %shared.1 = (f32[1152,128]{1,0:T(8,128)S(1)}, f32[8,128]{1,0:T(8,128)S(1)}, bf16[1184,128]{1,0:T(8,128)(2,1)S(1)}) custom-call(s32[5]{0:T(128)S(1)} %copy-done.4, bf16[12,256,256]{2,1,0:T(8,128)(2,1)S(1)} %bitcast.18, bf16[784,256]{1,0:T(8,128)(2,1)S(1)} %collective-permute-done.refs_2_, bf16[784,256]{1,0:T(8,128)(2,1)S(1)} %collective-permute-done.1.refs_3_, ...), custom_call_target="tpu_custom_call" | custom-call | tf_op jit(solution)/shard_map/shared/pallas_call | solution.py:32
  45.8 1.9 %collective-permute-start.10 = (bf16[1184,128]{1,0:T(8,128)(2,1)S(1)}, bf16[1184,128]{1,0:T(8,128)(2,1)S(1)}, u32[]{:S(2)}, u32[]{:S(2)}) collective-permute-start(bf16[1184,128]{1,0:T(8,128)(2,1)S(1)} %get-tuple-element.44), channel_id=1, source_target_pairs={{0,2},{2,0},{1,3},{3,1},{4,6},{6,4},{5,7},{7,5},{8,10},{10,8},{9,1... | collective-permute-start | bytes 909320 | tf_op jit(solution)/shard_map/ppermute | solution.py:369
  47.7 7.7 %collective-permute-done.10.refs_3_ = bf16[1184,128]{1,0:T(8,128)(2,1)S(1)} collective-permute-done((bf16[1184,128]{1,0:T(8,128)(2,1)S(1)}, bf16[1184,128]{1,0:T(8,128)(2,1)S(1)}, u32[]{:S(2)}, u32[]{:S(2)}) %collective-permute-start.10) | collective-permute-done | bytes 303136 | tf_op jit(solution)/shard_map/ppermute | solution.py:369
  55.4 0.6 shared_tile.1
  56.0 1.0 %collective-permute-start.11 = (bf16[320,128]{1,0:T(8,128)(2,1)S(1)}, bf16[320,128]{1,0:T(8,128)(2,1)S(1)}, u32[]{:S(2)}, u32[]{:S(2)}) collective-permute-start(bf16[320,128]{1,0:T(8,128)(2,1)S(1)} %get-tuple-element.47), channel_id=1, source_target_pairs={{0,4},{4,0},{8,12},{12,8},{1,5},{5,1},{9,13},{13,9},{2,6},{6,2},{1... | collective-permute-start | bytes 245768 | tf_op jit(solution)/shard_map/ppermute | solution.py:369
  57.0 3.0 %collective-permute-start.12 = (bf16[320,128]{1,0:T(8,128)(2,1)S(1)}, bf16[320,128]{1,0:T(8,128)(2,1)S(1)}, u32[]{:S(2)}, u32[]{:S(2)}) collective-permute-start(bf16[320,128]{1,0:T(8,128)(2,1)S(1)} %get-tuple-element.48), channel_id=1, source_target_pairs={{0,8},{4,12},{8,0},{12,4},{1,9},{5,13},{9,1},{13,5},{2,10},{6,14},... | collective-permute-start | bytes 245768 | tf_op jit(solution)/shard_map/ppermute | solution.py:369
  60.0 0.5 collective-permute-start.13
  60.5 0.6 cls_tile.1
  61.1 0.2 collective-permute-start.19
  61.3 3.8 %collective-permute-start.20 = (bf16[256,128]{1,0:T(8,128)(2,1)S(1)}, bf16[256,128]{1,0:T(8,128)(2,1)S(1)}, u32[]{:S(2)}, u32[]{:S(2)}) collective-permute-start(bf16[256,128]{1,0:T(8,128)(2,1)S(1)} %get-tuple-element.57), channel_id=1, source_target_pairs={{0,8},{4,12},{8,0},{12,4},{1,9},{5,13},{9,1},{13,5},{2,10},{6,14},... | collective-permute-start | bytes 196616 | tf_op jit(solution)/shard_map/ppermute | solution.py:369
  65.1 0.0 collective-permute-done.11.refs_3_
  65.1 0.5 collective-permute-start.21
  65.6 1.5 %collective-permute-done.12.refs_4_ = bf16[320,128]{1,0:T(8,128)(2,1)S(1)} collective-permute-done((bf16[320,128]{1,0:T(8,128)(2,1)S(1)}, bf16[320,128]{1,0:T(8,128)(2,1)S(1)}, u32[]{:S(2)}, u32[]{:S(2)}) %collective-permute-start.12) | collective-permute-done | bytes 81952 | tf_op jit(solution)/shard_map/ppermute | solution.py:369
  67.0 0.6 shared_round.1
  67.6 3.9 %collective-permute-start.14 = (bf16[288,128]{1,0:T(8,128)(2,1)S(1)}, bf16[288,128]{1,0:T(8,128)(2,1)S(1)}, u32[]{:S(2)}, u32[]{:S(2)}) collective-permute-start(bf16[288,128]{1,0:T(8,128)(2,1)S(1)} %get-tuple-element.50.refs_1_), channel_id=1, source_target_pairs={{0,4},{4,0},{8,12},{12,8},{1,5},{5,1},{9,13},{13,9},{2,6},{6,2},{1... | collective-permute-start | bytes 221192 | tf_op jit(solution)/shard_map/ppermute | solution.py:369
  71.5 2.8 %collective-permute-start.15 = (bf16[288,128]{1,0:T(8,128)(2,1)S(1)}, bf16[288,128]{1,0:T(8,128)(2,1)S(1)}, u32[]{:S(2)}, u32[]{:S(2)}) collective-permute-start(bf16[288,128]{1,0:T(8,128)(2,1)S(1)} %get-tuple-element.50.refs_1_), channel_id=1, source_target_pairs={{0,8},{4,12},{8,0},{12,4},{1,9},{5,13},{9,1},{13,5},{2,10},{6,14},... | collective-permute-start | bytes 221192 | tf_op jit(solution)/shard_map/ppermute | solution.py:369
  74.3 0.0 collective-permute-done.19.refs_2_
  74.3 1.4 %collective-permute-start.16 = (bf16[288,128]{1,0:T(8,128)(2,1)S(1)}, bf16[288,128]{1,0:T(8,128)(2,1)S(1)}, u32[]{:S(2)}, u32[]{:S(2)}) collective-permute-start(bf16[288,128]{1,0:T(8,128)(2,1)S(1)} %get-tuple-element.50.refs_1_), channel_id=1, source_target_pairs={{0,12},{4,8},{8,4},{12,0},{1,13},{5,9},{9,5},{13,1},{2,14},{6,10},... | collective-permute-start | bytes 221192 | tf_op jit(solution)/shard_map/ppermute | solution.py:369
  75.7 0.0 collective-permute-done.20.refs_3_
  75.7 0.6 cls_batch.1
  76.3 1.6 %collective-permute-start.22 = (bf16[128,128]{1,0:T(8,128)(2,1)S(1)}, bf16[128,128]{1,0:T(8,128)(2,1)S(1)}, u32[]{:S(2)}, u32[]{:S(2)}) collective-permute-start(bf16[128,128]{1,0:T(8,128)(2,1)S(1)} %get-tuple-element.60), channel_id=1, source_target_pairs={{0,2},{2,0},{1,3},{3,1},{4,6},{6,4},{5,7},{7,5},{8,10},{10,8},{9,1... | collective-permute-start | bytes 98312 | tf_op jit(solution)/shard_map/ppermute | solution.py:369
  77.9 2.8 %collective-permute-done.22.refs_2_ = bf16[128,128]{1,0:T(8,128)(2,1)S(1)} collective-permute-done((bf16[128,128]{1,0:T(8,128)(2,1)S(1)}, bf16[128,128]{1,0:T(8,128)(2,1)S(1)}, u32[]{:S(2)}, u32[]{:S(2)}) %collective-permute-start.22) | collective-permute-done | bytes 32800 | tf_op jit(solution)/shard_map/ppermute | solution.py:369
  80.6 0.5 cls_round.1.refs_1_
  81.2 1.6 %collective-permute-start.23 = (bf16[128,128]{1,0:T(8,128)(2,1)S(1)}, bf16[128,128]{1,0:T(8,128)(2,1)S(1)}, u32[]{:S(2)}, u32[]{:S(2)}) collective-permute-start(bf16[128,128]{1,0:T(8,128)(2,1)S(1)} %cls_round.1.refs_1_), channel_id=1, source_target_pairs={{0,2},{2,0},{1,3},{3,1},{4,6},{6,4},{5,7},{7,5},{8,10},{10,8},{9,1... | collective-permute-start | bytes 98312 | tf_op jit(solution)/shard_map/ppermute | solution.py:369
  82.8 0.0 collective-permute-done.14.refs_2_
  82.8 0.0 collective-permute-done.15.refs_3_
  82.8 0.6 shared_join.1.refs_1_.refs_3_
  83.4 0.5 collective-permute-start.17
  83.9 0.5 slice_bitcast_fusion
  84.4 0.7 collective-permute-done.23.refs_2_
  85.2 0.5 cls_join.1.refs_1_
  85.7 0.3 collective-permute-start.24
  86.0 2.8 %collective-permute-start.25 = (bf16[256,128]{1,0:T(8,128)(2,1)S(1)}, bf16[256,128]{1,0:T(8,128)(2,1)S(1)}, u32[]{:S(2)}, u32[]{:S(2)}) collective-permute-start(bf16[256,128]{1,0:T(8,128)(2,1)S(1)} %cls_join.1.refs_1_), channel_id=1, source_target_pairs={{0,8},{4,12},{8,0},{12,4},{1,9},{5,13},{9,1},{13,5},{2,10},{6,14},... | collective-permute-start | bytes 196616 | tf_op jit(solution)/shard_map/ppermute | solution.py:369
  88.8 1.3 %collective-permute-start.26 = (bf16[256,128]{1,0:T(8,128)(2,1)S(1)}, bf16[256,128]{1,0:T(8,128)(2,1)S(1)}, u32[]{:S(2)}, u32[]{:S(2)}) collective-permute-start(bf16[256,128]{1,0:T(8,128)(2,1)S(1)} %cls_join.1.refs_1_), channel_id=1, source_target_pairs={{0,12},{4,8},{8,4},{12,0},{1,13},{5,9},{9,5},{13,1},{2,14},{6,10},... | collective-permute-start | bytes 196616 | tf_op jit(solution)/shard_map/ppermute | solution.py:369
  90.2 0.5 slice_bitcast_fusion.1
  90.7 0.5 slice.11
  91.2 3.7 %collective-permute-done.26.refs_4_ = bf16[256,128]{1,0:T(8,128)(2,1)S(1)} collective-permute-done((bf16[256,128]{1,0:T(8,128)(2,1)S(1)}, bf16[256,128]{1,0:T(8,128)(2,1)S(1)}, u32[]{:S(2)}, u32[]{:S(2)}) %collective-permute-start.26) | collective-permute-done | bytes 65568 | tf_op jit(solution)/shard_map/ppermute | solution.py:369
  94.9 1.4 %cls_out.1 = f32[3,3,99,128]{3,2,1,0:T(8,128)} custom-call(s32[5]{0:T(128)S(1)} %copy-done.4, bf16[256,128]{1,0:T(8,128)(2,1)S(1)} %cls_join.1.refs_1_, bf16[256,128]{1,0:T(8,128)(2,1)S(1)} %collective-permute-done.24.refs_2_, bf16[256,128]{1,0:T(8,128)(2,1)S(1)} %collective-permute-done.25.refs_3_, bf16[256,128]{1,0:T(8,128)(2,1)S(1)} %collective-permute-done.26.refs_4_), custom_call_target="tpu_custom_call" | custom-call | tf_op jit(solution)/shard_map/cls_out/pallas_call | solution.py:32
  96.3 1.6 %shared_out.1 = f32[2304,128]{1,0:T(8,128)} custom-call(s32[5]{0:T(128)S(1)} %copy-done.4, bf16[1152,128]{1,0:T(8,128)(2,1)S(1)} %shared_join.1.refs_1_.refs_3_, bf16[1152,128]{1,0:T(8,128)(2,1)S(1)} %collective-permute-done.17.refs_2_), custom_call_target="tpu_custom_call" | custom-call | tf_op jit(solution)/shard_map/shared_out/pallas_call | solution.py:32
  (24 shorter events, 0.1 us)
Async XLA Ops:
  0.6 20.3 %copy-start.3 = (bf16[3,3,256,128]{3,2,1,0:T(8,128)(2,1)S(1)}, bf16[3,3,256,128]{3,2,1,0:T(8,128)(2,1)}, u32[]{:S(2)}) copy-start(bf16[3,3,256,128]{3,2,1,0:T(8,128)(2,1)} %refs_4_.1) | copy-start | bytes 1769476
  0.6 20.3 %copy-start.6 = (f32[99]{0:T(128)S(1)}, f32[99]{0:T(128)}, u32[]{:S(2)}) copy-start(f32[99]{0:T(128)} %param.11) | copy-start | bytes 1192
  0.7 20.3 %collective-permute-start.2 = (bf16[3,3,256,128]{3,2,1,0:T(8,128)(2,1)}, bf16[3,3,256,128]{3,2,1,0:T(8,128)(2,1)S(1)}, u32[]{:S(2)}, u32[]{:S(2)}) collective-permute-start(bf16[3,3,256,128]{3,2,1,0:T(8,128)(2,1)} %refs_4_.1), channel_id=1, source_target_pairs={{0,1},{1,0},{2,3},{3,2},{4,5},{5,4},{6,7},{7,6},{8,9},{9,8},{10,11... | collective-permute-start | bytes 1769480 | tf_op jit(solution)/shard_map/ppermute | solution.py:369
  1.8 19.1 %copy-start.4 = (s32[5]{0:T(128)S(1)}, s32[5]{0:T(128)}, u32[]{:S(2)}) copy-start(s32[5]{0:T(128)} %stack.19.where_ref.refs_0_) | copy-start | bytes 64
  5.3 8.0 %collective-permute-start = (bf16[784,256]{1,0:T(8,128)(2,1)}, bf16[784,256]{1,0:T(8,128)(2,1)S(1)}, u32[]{:S(2)}, u32[]{:S(2)}) collective-permute-start(bf16[784,256]{1,0:T(8,128)(2,1)} %get-tuple-element.33), channel_id=1, source_target_pairs={{1,4},{4,1},{5,8},{8,5},{9,12},{12,9},{3,6},{6,3},{7,10},{10,7},{1... | collective-permute-start | bytes 1204232 | tf_op jit(solution)/shard_map/ppermute | solution.py:425
  6.0 14.6 %collective-permute-start.3 = (bf16[1184,128]{1,0:T(8,128)(2,1)}, bf16[1184,128]{1,0:T(8,128)(2,1)S(1)}, u32[]{:S(2)}, u32[]{:S(2)}) collective-permute-start(bf16[1184,128]{1,0:T(8,128)(2,1)} %get-tuple-element.35.refs_6_.refs_4_), channel_id=1, source_target_pairs={{0,1},{1,0},{2,3},{3,2},{4,5},{5,4},{6,7},{7,6},{8,9},{9,8},{10,11... | collective-permute-start | bytes 909320 | tf_op jit(solution)/shard_map/ppermute | solution.py:369
  11.8 3.9 %collective-permute-start.4 = (f32[8,128]{1,0:T(8,128)}, f32[8,128]{1,0:T(8,128)S(1)}, u32[]{:S(2)}, u32[]{:S(2)}) collective-permute-start(f32[8,128]{1,0:T(8,128)} %count.1), channel_id=1, source_target_pairs={{0,2},{2,0},{1,3},{3,1},{4,6},{6,4},{5,7},{7,5},{8,10},{10,8},{9,1... | collective-permute-start | bytes 12296 | tf_op jit(solution)/shard_map/ppermute | solution.py:369
  13.3 28.6 %collective-permute-start.1 = (bf16[784,256]{1,0:T(8,128)(2,1)S(1)}, bf16[784,256]{1,0:T(8,128)(2,1)S(1)}, u32[]{:S(2)}, u32[]{:S(2)}) collective-permute-start(bf16[784,256]{1,0:T(8,128)(2,1)S(1)} %collective-permute-done.refs_2_), channel_id=1, source_target_pairs={{0,1},{1,0},{2,3},{3,2},{4,5},{5,4},{6,7},{7,6},{8,9},{9,8},{10,11... | collective-permute-start | bytes 1204232 | tf_op jit(solution)/shard_map/ppermute | solution.py:369
  16.4 17.5 %collective-permute-start.5 = (f32[8,128]{1,0:T(8,128)S(1)}, f32[8,128]{1,0:T(8,128)S(1)}, u32[]{:S(2)}, u32[]{:S(2)}) collective-permute-start(f32[8,128]{1,0:T(8,128)S(1)} %add.7.refs_6_), channel_id=1, source_target_pairs={{0,4},{4,0},{8,12},{12,8},{1,5},{5,1},{9,13},{13,9},{2,6},{6,2},{1... | collective-permute-start | bytes 12296 | tf_op jit(solution)/shard_map/ppermute | solution.py:369
  18.4 15.5 %collective-permute-start.6 = (f32[8,128]{1,0:T(8,128)S(1)}, f32[8,128]{1,0:T(8,128)S(1)}, u32[]{:S(2)}, u32[]{:S(2)}) collective-permute-start(f32[8,128]{1,0:T(8,128)S(1)} %add.7.refs_6_), channel_id=1, source_target_pairs={{0,8},{4,12},{8,0},{12,4},{1,9},{5,13},{9,1},{13,5},{2,10},{6,14},... | collective-permute-start | bytes 12296 | tf_op jit(solution)/shard_map/ppermute | solution.py:369
  20.5 13.4 %collective-permute-start.7 = (f32[8,128]{1,0:T(8,128)S(1)}, f32[8,128]{1,0:T(8,128)S(1)}, u32[]{:S(2)}, u32[]{:S(2)}) collective-permute-start(f32[8,128]{1,0:T(8,128)S(1)} %add.7.refs_6_), channel_id=1, source_target_pairs={{0,12},{4,8},{8,4},{12,0},{1,13},{5,9},{9,5},{13,1},{2,14},{6,10},... | collective-permute-start | bytes 12296 | tf_op jit(solution)/shard_map/ppermute | solution.py:369
  20.9 1.0 copy-start.1
  21.9 0.9 copy-start.5
  22.8 11.2 %copy-start.2 = (bf16[1184,128]{1,0:T(8,128)(2,1)S(1)}, bf16[1184,128]{1,0:T(8,128)(2,1)}, u32[]{:S(2)}) copy-start(bf16[1184,128]{1,0:T(8,128)(2,1)} %get-tuple-element.35.refs_6_.refs_4_) | copy-start | bytes 909316
  38.2 3.7 %copy-start = (bf16[1,12,256,256]{3,2,1,0:T(8,128)(2,1)S(1)}, bf16[1,12,256,256]{3,2,1,0:T(8,128)(2,1)}, u32[]{:S(2)}) copy-start(bf16[1,12,256,256]{3,2,1,0:T(8,128)(2,1)} %param.6) | copy-start | bytes 4718596
  38.2 3.6 %collective-permute-start.8 = (bf16[6,256,128]{2,1,0:T(8,128)(2,1)S(1)}, bf16[6,256,128]{2,1,0:T(8,128)(2,1)S(1)}, u32[]{:S(2)}, u32[]{:S(2)}) collective-permute-start(bf16[6,256,128]{2,1,0:T(8,128)(2,1)S(1)} %get-tuple-element.40), channel_id=1, source_target_pairs={{0,1},{1,0},{2,3},{3,2},{4,5},{5,4},{6,7},{7,6},{8,9},{9,8},{10,11... | collective-permute-start | bytes 1179656 | tf_op jit(solution)/shard_map/ppermute | solution.py:369
  39.8 20.7 %collective-permute-start.18 = (f32[1024,128]{1,0:T(8,128)S(1)}, f32[1024,128]{1,0:T(8,128)S(1)}, u32[]{:S(2)}, u32[]{:S(2)}) collective-permute-start(f32[1024,128]{1,0:T(8,128)S(1)} %get-tuple-element.54), channel_id=1, source_target_pairs={{0,1},{1,0},{2,3},{3,2},{4,5},{5,4},{6,7},{7,6},{8,9},{9,8},{10,11... | collective-permute-start | bytes 1572872 | tf_op jit(solution)/shard_map/ppermute | solution.py:369
  40.3 1.5 %collective-permute-start.9 = (f32[8,128]{1,0:T(8,128)S(1)}, f32[8,128]{1,0:T(8,128)S(1)}, u32[]{:S(2)}, u32[]{:S(2)}) collective-permute-start(f32[8,128]{1,0:T(8,128)S(1)} %get-tuple-element.41.refs_6_), channel_id=1, source_target_pairs={{0,1},{1,0},{2,3},{3,2},{4,5},{5,4},{6,7},{7,6},{8,9},{9,8},{10,11... | collective-permute-start | bytes 12296 | tf_op jit(solution)/shard_map/ppermute | solution.py:369
  45.8 9.6 %collective-permute-start.10 = (bf16[1184,128]{1,0:T(8,128)(2,1)S(1)}, bf16[1184,128]{1,0:T(8,128)(2,1)S(1)}, u32[]{:S(2)}, u32[]{:S(2)}) collective-permute-start(bf16[1184,128]{1,0:T(8,128)(2,1)S(1)} %get-tuple-element.44), channel_id=1, source_target_pairs={{0,2},{2,0},{1,3},{3,1},{4,6},{6,4},{5,7},{7,5},{8,10},{10,8},{9,1... | collective-permute-start | bytes 909320 | tf_op jit(solution)/shard_map/ppermute | solution.py:369
  56.0 9.1 %collective-permute-start.11 = (bf16[320,128]{1,0:T(8,128)(2,1)S(1)}, bf16[320,128]{1,0:T(8,128)(2,1)S(1)}, u32[]{:S(2)}, u32[]{:S(2)}) collective-permute-start(bf16[320,128]{1,0:T(8,128)(2,1)S(1)} %get-tuple-element.47), channel_id=1, source_target_pairs={{0,4},{4,0},{8,12},{12,8},{1,5},{5,1},{9,13},{13,9},{2,6},{6,2},{1... | collective-permute-start | bytes 245768 | tf_op jit(solution)/shard_map/ppermute | solution.py:369
  57.0 10.0 %collective-permute-start.12 = (bf16[320,128]{1,0:T(8,128)(2,1)S(1)}, bf16[320,128]{1,0:T(8,128)(2,1)S(1)}, u32[]{:S(2)}, u32[]{:S(2)}) collective-permute-start(bf16[320,128]{1,0:T(8,128)(2,1)S(1)} %get-tuple-element.48), channel_id=1, source_target_pairs={{0,8},{4,12},{8,0},{12,4},{1,9},{5,13},{9,1},{13,5},{2,10},{6,14},... | collective-permute-start | bytes 245768 | tf_op jit(solution)/shard_map/ppermute | solution.py:369
  60.0 7.0 %collective-permute-start.13 = (bf16[320,128]{1,0:T(8,128)(2,1)S(1)}, bf16[320,128]{1,0:T(8,128)(2,1)S(1)}, u32[]{:S(2)}, u32[]{:S(2)}) collective-permute-start(bf16[320,128]{1,0:T(8,128)(2,1)S(1)} %get-tuple-element.49), channel_id=1, source_target_pairs={{0,12},{4,8},{8,4},{12,0},{1,13},{5,9},{9,5},{13,1},{2,14},{6,10},... | collective-permute-start | bytes 245768 | tf_op jit(solution)/shard_map/ppermute | solution.py:369
  61.1 13.2 %collective-permute-start.19 = (bf16[256,128]{1,0:T(8,128)(2,1)S(1)}, bf16[256,128]{1,0:T(8,128)(2,1)S(1)}, u32[]{:S(2)}, u32[]{:S(2)}) collective-permute-start(bf16[256,128]{1,0:T(8,128)(2,1)S(1)} %get-tuple-element.56), channel_id=1, source_target_pairs={{0,4},{4,0},{8,12},{12,8},{1,5},{5,1},{9,13},{13,9},{2,6},{6,2},{1... | collective-permute-start | bytes 196616 | tf_op jit(solution)/shard_map/ppermute | solution.py:369
  61.3 14.4 %collective-permute-start.20 = (bf16[256,128]{1,0:T(8,128)(2,1)S(1)}, bf16[256,128]{1,0:T(8,128)(2,1)S(1)}, u32[]{:S(2)}, u32[]{:S(2)}) collective-permute-start(bf16[256,128]{1,0:T(8,128)(2,1)S(1)} %get-tuple-element.57), channel_id=1, source_target_pairs={{0,8},{4,12},{8,0},{12,4},{1,9},{5,13},{9,1},{13,5},{2,10},{6,14},... | collective-permute-start | bytes 196616 | tf_op jit(solution)/shard_map/ppermute | solution.py:369
  65.1 10.6 %collective-permute-start.21 = (bf16[256,128]{1,0:T(8,128)(2,1)S(1)}, bf16[256,128]{1,0:T(8,128)(2,1)S(1)}, u32[]{:S(2)}, u32[]{:S(2)}) collective-permute-start(bf16[256,128]{1,0:T(8,128)(2,1)S(1)} %get-tuple-element.58), channel_id=1, source_target_pairs={{0,12},{4,8},{8,4},{12,0},{1,13},{5,9},{9,5},{13,1},{2,14},{6,10},... | collective-permute-start | bytes 196616 | tf_op jit(solution)/shard_map/ppermute | solution.py:369
  67.6 15.2 %collective-permute-start.14 = (bf16[288,128]{1,0:T(8,128)(2,1)S(1)}, bf16[288,128]{1,0:T(8,128)(2,1)S(1)}, u32[]{:S(2)}, u32[]{:S(2)}) collective-permute-start(bf16[288,128]{1,0:T(8,128)(2,1)S(1)} %get-tuple-element.50.refs_1_), channel_id=1, source_target_pairs={{0,4},{4,0},{8,12},{12,8},{1,5},{5,1},{9,13},{13,9},{2,6},{6,2},{1... | collective-permute-start | bytes 221192 | tf_op jit(solution)/shard_map/ppermute | solution.py:369
  71.5 11.3 %collective-permute-start.15 = (bf16[288,128]{1,0:T(8,128)(2,1)S(1)}, bf16[288,128]{1,0:T(8,128)(2,1)S(1)}, u32[]{:S(2)}, u32[]{:S(2)}) collective-permute-start(bf16[288,128]{1,0:T(8,128)(2,1)S(1)} %get-tuple-element.50.refs_1_), channel_id=1, source_target_pairs={{0,8},{4,12},{8,0},{12,4},{1,9},{5,13},{9,1},{13,5},{2,10},{6,14},... | collective-permute-start | bytes 221192 | tf_op jit(solution)/shard_map/ppermute | solution.py:369
  74.3 8.5 %collective-permute-start.16 = (bf16[288,128]{1,0:T(8,128)(2,1)S(1)}, bf16[288,128]{1,0:T(8,128)(2,1)S(1)}, u32[]{:S(2)}, u32[]{:S(2)}) collective-permute-start(bf16[288,128]{1,0:T(8,128)(2,1)S(1)} %get-tuple-element.50.refs_1_), channel_id=1, source_target_pairs={{0,12},{4,8},{8,4},{12,0},{1,13},{5,9},{9,5},{13,1},{2,14},{6,10},... | collective-permute-start | bytes 221192 | tf_op jit(solution)/shard_map/ppermute | solution.py:369
  76.3 4.3 %collective-permute-start.22 = (bf16[128,128]{1,0:T(8,128)(2,1)S(1)}, bf16[128,128]{1,0:T(8,128)(2,1)S(1)}, u32[]{:S(2)}, u32[]{:S(2)}) collective-permute-start(bf16[128,128]{1,0:T(8,128)(2,1)S(1)} %get-tuple-element.60), channel_id=1, source_target_pairs={{0,2},{2,0},{1,3},{3,1},{4,6},{6,4},{5,7},{7,5},{8,10},{10,8},{9,1... | collective-permute-start | bytes 98312 | tf_op jit(solution)/shard_map/ppermute | solution.py:369
  81.2 4.0 %collective-permute-start.23 = (bf16[128,128]{1,0:T(8,128)(2,1)S(1)}, bf16[128,128]{1,0:T(8,128)(2,1)S(1)}, u32[]{:S(2)}, u32[]{:S(2)}) collective-permute-start(bf16[128,128]{1,0:T(8,128)(2,1)S(1)} %cls_round.1.refs_1_), channel_id=1, source_target_pairs={{0,2},{2,0},{1,3},{3,1},{4,6},{6,4},{5,7},{7,5},{8,10},{10,8},{9,1... | collective-permute-start | bytes 98312 | tf_op jit(solution)/shard_map/ppermute | solution.py:369
  83.4 12.9 %collective-permute-start.17 = (bf16[1152,128]{1,0:T(8,128)(2,1)S(1)}, bf16[1152,128]{1,0:T(8,128)(2,1)S(1)}, u32[]{:S(2)}, u32[]{:S(2)}) collective-permute-start(bf16[1152,128]{1,0:T(8,128)(2,1)S(1)} %shared_join.1.refs_1_.refs_3_), channel_id=1, source_target_pairs={{0,2},{2,0},{1,3},{3,1},{4,6},{6,4},{5,7},{7,5},{8,10},{10,8},{9,1... | collective-permute-start | bytes 884744 | tf_op jit(solution)/shard_map/ppermute | solution.py:369
  85.7 5.5 %collective-permute-start.24 = (bf16[256,128]{1,0:T(8,128)(2,1)S(1)}, bf16[256,128]{1,0:T(8,128)(2,1)S(1)}, u32[]{:S(2)}, u32[]{:S(2)}) collective-permute-start(bf16[256,128]{1,0:T(8,128)(2,1)S(1)} %cls_join.1.refs_1_), channel_id=1, source_target_pairs={{0,4},{4,0},{8,12},{12,8},{1,5},{5,1},{9,13},{13,9},{2,6},{6,2},{1... | collective-permute-start | bytes 196616 | tf_op jit(solution)/shard_map/ppermute | solution.py:369
  86.0 5.2 %collective-permute-start.25 = (bf16[256,128]{1,0:T(8,128)(2,1)S(1)}, bf16[256,128]{1,0:T(8,128)(2,1)S(1)}, u32[]{:S(2)}, u32[]{:S(2)}) collective-permute-start(bf16[256,128]{1,0:T(8,128)(2,1)S(1)} %cls_join.1.refs_1_), channel_id=1, source_target_pairs={{0,8},{4,12},{8,0},{12,4},{1,9},{5,13},{9,1},{13,5},{2,10},{6,14},... | collective-permute-start | bytes 196616 | tf_op jit(solution)/shard_map/ppermute | solution.py:369
  88.8 6.1 %collective-permute-start.26 = (bf16[256,128]{1,0:T(8,128)(2,1)S(1)}, bf16[256,128]{1,0:T(8,128)(2,1)S(1)}, u32[]{:S(2)}, u32[]{:S(2)}) collective-permute-start(bf16[256,128]{1,0:T(8,128)(2,1)S(1)} %cls_join.1.refs_1_), channel_id=1, source_target_pairs={{0,12},{4,8},{8,4},{12,0},{1,13},{5,9},{9,5},{13,1},{2,14},{6,10},... | collective-permute-start | bytes 196616 | tf_op jit(solution)/shard_map/ppermute | solution.py:369

commit v3 on v2

--- a/solution.py
+++ b/solution.py
@@ -14,27 +14,23 @@
 ANCH_ROWS = 16
 CLS_ROWS = 112
 CLS_TOTAL = 1024
+TILE, BATCH = 3, 4
 TRIO = 32
 BF16 = jnp.bfloat16
 F32 = jnp.float32
 VMEM = pl.BlockSpec(memory_space=pltpu.VMEM)
-ANY = pl.BlockSpec(memory_space=pl.ANY)
+HBM = pl.BlockSpec(memory_space=pltpu.HBM)
 SMEM = pl.BlockSpec(memory_space=pltpu.SMEM)
 
 
-def call(kernel, name, outs, inputs, scratch=(), after=()):
-    n = len(inputs)
-    inputs = list(inputs) + list(after)
-
-    def body(*refs):
-        kernel(*refs[:n], *refs[len(inputs) :])
-
+def call(kernel, name, micros, outs, inputs, scratch=(), specs=None):
     return pl.pallas_call(
-        body,
-        in_specs=[SMEM] + [VMEM] * (n - 1) + [ANY] * len(after),
+        kernel,
+        in_specs=specs or [SMEM] + [VMEM] * (len(inputs) - 1),
         out_specs=[VMEM] * len(outs),
         out_shape=[jax.ShapeDtypeStruct(shape, kind) for shape, kind in outs],
-        scratch_shapes=[pltpu.VMEM(shape, kind) for shape, kind in scratch],
+        scratch_shapes=[pltpu.VMEM(*shape) if isinstance(shape, tuple) else shape for shape in scratch],
+        cost_estimate=pl.CostEstimate(flops=int(micros * 1e9), bytes_accessed=int(micros * 1e6), transcendentals=0),
         compiler_params=pltpu.CompilerParams(vmem_limit_bytes=48 * 1024 * 1024),
         name=name,
     )(*inputs)
@@ -70,22 +66,23 @@
     return part[0:8] + part[8:16] + part[16:24]
 
 
-def count_kernel(lab_ref, count_ref):
-    lab = lab_ref[...]
-    count_ref[...] = jnp.full(count_ref.shape, jnp.sum(jnp.where(lab > 0, 1.0, 0.0)), F32)
-
-
-def prep_kernel(where_ref, f_ref, lab_ref, w2_ref, b1_ref, msg_ref, labt_ref, pack_ref):
-    rows = lab_ref.shape[0]
-    cols = f_ref.shape[1]
+def edge_kernel(where_ref, f_ref, lab_ref, msg_ref, labt_ref, count_ref, sem):
+    rows, cols, _ = f_ref.shape
     c = where_ref[0]
-    for k in range(3):
-        msg_ref[cols * k : cols * (k + 1)] = f_ref[k]
+    copies = [
+        pltpu.make_async_copy(f_ref.at[(rows - 3) * c + k], msg_ref.at[pl.ds(cols * k, cols)], sem.at[k])
+        for k in range(3)
+    ]
+    for copy in copies:
+        copy.start()
     size = lab_ref.shape[2]
     place = lax.broadcasted_iota(jnp.int32, (ANCH_ROWS, size), 1) % ANCH
     anchor = lax.broadcasted_iota(jnp.int32, (ANCH_ROWS, size), 0)
-    mine = jnp.where(place == anchor, 1.0, 0.0)
-    left = jnp.concatenate([mine * lab_ref[r].astype(F32) for r in range(rows)], axis=0).astype(BF16)
+    mine = place == anchor
+    labs = [lab_ref[r].astype(F32) for r in range(rows)]
+    named = [jnp.where(lab > 0.0, 1.0, 0.0) for lab in labs]
+    count_ref[...] = jnp.full(count_ref.shape, jnp.sum(sum(named[1:], named[0])), F32)
+    left = jnp.concatenate([jnp.where(mine, lab, 0.0) for lab in labs], axis=0).astype(BF16)
     offset = lax.broadcasted_iota(jnp.int32, (size, cols), 0) - ANCH * lax.broadcasted_iota(jnp.int32, (size, cols), 1)
     pick = jnp.where(jnp.logical_and(offset >= 0, offset < ANCH), 1.0, 0.0).astype(BF16)
     turned = dot(left, pick).astype(BF16)
@@ -94,6 +91,11 @@
     msg_ref[3 * cols : 3 * cols + ANCH_ROWS] = jnp.where(
         c == 0, turned[:ANCH_ROWS].astype(F32), turned[ANCH_ROWS * (rows - 1) :].astype(F32)
     ).astype(BF16)
+    for copy in copies:
+        copy.wait()
+
+
+def pack_kernel(where_ref, w2_ref, b1_ref, pack_ref):
     deep = w2_ref.shape[3]
     for tap in range(9):
         pack_ref[LANES * tap : LANES * (tap + 1)] = jnp.zeros((LANES, deep), BF16)
@@ -256,8 +258,11 @@
         ref[0:rows] = total[pl.ds(pl.multiple_of((me ^ (k + 1)) * rows, 8), rows)].astype(BF16)
 
 
-def shared_kernel(slot, where_ref, f_ref, halo_ref, far_ref, own_ref, other_ref, small_ref, theirs_ref, *rest):
-    keep_ref, sum_ref, *send_refs, x_ref, d_ref, g_ref = rest
+def shared_kernel(
+    n_send, where_ref, f_ref, halo_ref, far_ref, own_ref, other_ref, small_ref, theirs_ref, cls_ref, cls_theirs_ref, *rest
+):
+    keep_ref, sum_ref, *send_refs, x_ref, d_ref, g_ref, cls_total_ref = rest
+    send_refs, cls_keep_ref, cls_send_refs = send_refs[:n_send], send_refs[n_send], send_refs[n_send + 1 :]
     rows, cols, chans = f_ref.shape
     half = rows // 2
     c = where_ref[0]
@@ -287,7 +292,9 @@
         for j in range(3):
             start = (3 * i + j) * chans
             g_ref[start : start + chans] = g[:, j * outs : (j + 1) * outs]
-    split(g_ref, where_ref[slot], keep_ref, send_refs)
+    split(g_ref, where_ref[BATCH], keep_ref, send_refs)
+    cls_total_ref[...] = cls_ref[...] + cls_theirs_ref[...]
+    split(cls_total_ref, where_ref[TILE], cls_keep_ref, cls_send_refs)
     mine, theirs = small_ref[...], theirs_ref[...]
     sums = jnp.concatenate([mine[0:3] + theirs[0:3], mine[3:4] + theirs[4:5], mine[4:8]], axis=0)
     sum_ref[...] = sums
@@ -301,67 +308,60 @@
     return parts[0]
 
 
-def step_kernel(slot, n_in, trio, where_ref, *refs):
-    base_ref, refs = refs[0], refs[1:]
-    if trio:
-        small_ref, refs = refs[0], refs[1:]
+def sum_kernel(n_in, n_cls, n_send, where_ref, base_ref, small_ref, cls_ref, *refs):
     in_refs, refs = refs[:n_in], refs[n_in:]
+    cls_in_refs, refs = refs[:n_cls], refs[n_cls:]
+    keep_ref, sum_ref, *refs, total_ref, cls_total_ref = refs
+    send_refs, cls_keep_ref, cls_send_refs = refs[:n_send], refs[n_send], refs[n_send + 1 :]
     rows = base_ref.shape[0]
     total = base_ref[...]
     for ref in in_refs:
         total = total + ref[0:rows].astype(F32)
-    if trio:
-        sums = pair_sum([small_ref[...]] + [get_trio(ref, rows) for ref in in_refs])
-    if slot is None:
-        refs[0][...] = total.astype(BF16)
-        if trio:
-            refs[1][...] = sums
-        return
-    keep_ref, refs = refs[0], refs[1:]
-    if trio:
-        sum_ref, refs = refs[0], refs[1:]
-        sum_ref[...] = sums
-    *send_refs, total_ref = refs
     total_ref[...] = total
-    split(total_ref, where_ref[slot], keep_ref, send_refs)
-    if trio:
-        for ref in send_refs:
-            put_trio(ref, keep_ref.shape[0], sums)
-
-
-def step(where, slot, size, base, small, arrived, name, after=()):
-    trio = TRIO if small is not None else 0
-    rows, width = base.shape
-    inputs = [where, base] + ([small] if trio else []) + list(arrived)
-    smalls = [((8, LANES), F32)] if trio else []
-    kernel = functools.partial(step_kernel, slot, len(arrived), trio)
-    if slot is None:
-        return call(kernel, name, [((rows, width), BF16)] + smalls, inputs, after=after)
-    share = rows // size
-    outs = [((share, width), F32)] + smalls + [((share + trio, width), BF16)] * (size - 1)
-    return call(kernel, name, outs, inputs, [((rows, width), F32)], after)
-
-
-def join_kernel(slot, where_ref, *refs):
-    *in_refs, out_ref = refs
+    split(total_ref, where_ref[TILE], keep_ref, send_refs)
+    sums = pair_sum([small_ref[...]] + [get_trio(ref, rows) for ref in in_refs])
+    sum_ref[...] = sums
+    for ref in send_refs:
+        put_trio(ref, keep_ref.shape[0], sums)
+    total = cls_ref[...]
+    for ref in cls_in_refs:
+        total = total + ref[...].astype(F32)
+    cls_total_ref[...] = total
+    split(cls_total_ref, where_ref[BATCH], cls_keep_ref, cls_send_refs)
+
+
+def round_kernel(n_in, where_ref, base_ref, small_ref, cls_ref, *refs):
+    in_refs, cls_in_refs = refs[:n_in], refs[n_in:-3]
+    out_ref, sum_ref, cls_out_ref = refs[-3:]
+    rows = base_ref.shape[0]
+    total = base_ref[...]
+    for ref in in_refs:
+        total = total + ref[0:rows].astype(F32)
+    out_ref[...] = total.astype(BF16)
+    sum_ref[...] = pair_sum([small_ref[...]] + [get_trio(ref, rows) for ref in in_refs])
+    total = cls_ref[...]
+    for ref in cls_in_refs:
+        total = total + ref[...].astype(F32)
+    cls_out_ref[...] = total.astype(BF16)
+
+
+def join(me, in_refs, out_ref):
     rows = in_refs[0].shape[0]
-    me = where_ref[slot]
     for k, ref in enumerate(in_refs):
         out_ref[pl.ds(pl.multiple_of((me ^ k) * rows, 8), rows)] = ref[...].astype(out_ref.dtype)
 
 
-def join(where, slot, parts, kind, name, after=()):
-    rows, width = parts[0].shape
-    return call(
-        functools.partial(join_kernel, slot), name, [((rows * len(parts), width), kind)], [where] + parts, after=after
-    )[0]
-
-
-def join_cls_kernel(slot, where_ref, *refs):
-    *in_refs, out_ref, whole_ref = refs
-    join_kernel(slot, where_ref, *in_refs, whole_ref)
+def join_kernel(n_in, where_ref, *refs):
+    join(where_ref[TILE], refs[:n_in], refs[-2])
+    join(where_ref[BATCH], refs[n_in:-2], refs[-1])
+
+
+def out_kernel(n_in, where_ref, *refs):
+    out_ref, cls_out_ref, whole_ref = refs[-3:]
+    join(where_ref[BATCH], refs[:n_in], out_ref)
+    join(where_ref[TILE], refs[n_in:-3], whole_ref)
     for tap in range(9):
-        out_ref[tap // 3, tap % 3] = whole_ref[CLS_ROWS * tap : CLS_ROWS * tap + LOGITS]
+        cls_out_ref[tap // 3, tap % 3] = whole_ref[CLS_ROWS * tap : CLS_ROWS * tap + LOGITS]
 
 
 def swap(x, axis, bit=1):
@@ -387,38 +387,18 @@
     t = lax.axis_index("tile")
     f = features[0]
     where = jnp.stack([c, t * rows + half * c, jnp.int32(tiles * rows), t, lax.axis_index("batch")]).astype(jnp.int32)
-    TILE, BATCH = 3, 4
-
     lab = labels.reshape(rows, 1, labels.shape[2])
-    count = pl.pallas_call(
-        count_kernel, in_specs=[VMEM], out_specs=VMEM, out_shape=jax.ShapeDtypeStruct((8, LANES), F32), name="count"
-    )(lab)
-    whole = lambda *shape: pl.BlockSpec(shape, lambda g, w: (0,) * len(shape))
-    w2 = jnp.swapaxes(w_cls, 2, 3)
-    msg, labt, pack = pl.pallas_call(
-        prep_kernel,
-        grid_spec=pltpu.PrefetchScalarGridSpec(
-            num_scalar_prefetch=1,
-            grid=(1,),
-            in_specs=[
-                pl.BlockSpec((3, cols, chans), lambda g, w: ((rows // 3 - 1) * w[0], 0, 0)),
-                whole(*lab.shape),
-                whole(*w2.shape),
-                whole(1, outs),
-            ],
-            out_specs=[
-                whole(3 * cols + ANCH_ROWS, chans),
-                whole(rows, ANCH_ROWS, cols),
-                whole(9 * LANES + TRIO, outs),
-            ],
-        ),
-        out_shape=[
-            jax.ShapeDtypeStruct((3 * cols + ANCH_ROWS, chans), BF16),
-            jax.ShapeDtypeStruct((rows, ANCH_ROWS, cols), BF16),
-            jax.ShapeDtypeStruct((9 * LANES + TRIO, outs), BF16),
-        ],
-        name="prep",
-    )(where, f, lab, w2, b_shared.reshape(1, outs))
+    msg, labt, count = call(
+        edge_kernel, "edge", 1.5,
+        [((3 * cols + ANCH_ROWS, chans), BF16), ((rows, ANCH_ROWS, cols), BF16), ((8, LANES), F32)],
+        [where, f, lab],
+        [pltpu.SemaphoreType.DMA((3,))],
+        [SMEM, HBM, VMEM],
+    )
+    (pack,) = call(
+        pack_kernel, "pack", 0.8, [((9 * LANES + TRIO, outs), BF16)],
+        [where, jnp.swapaxes(w_cls, 2, 3), b_shared.reshape(1, outs)],
+    )
     pairs = []
     for i in range(tiles - 1):
         pairs += [(2 * i + 1, 2 * i + 2), (2 * i + 2, 2 * i + 1)]
@@ -429,13 +409,13 @@
     counts = [count] + others(count, "tile")
 
     hid, dz, loss = call(
-        head_kernel, "head",
+        head_kernel, "head", 11,
         [((half + 4, cols, chans), BF16), ((half + 2, cols, LANES), F32), ((1, LANES), F32)],
         [where, f, halo, labt, w_shared, w1b, pack, packb, b_cls.reshape(1, LOGITS)],
         [((half + 6, cols, chans), BF16)],
     )
     dt, own, other, small = call(
-        back_kernel, "back",
+        back_kernel, "back", 4,
         [
             ((half, 3 * CLS_ROWS, cols), BF16),
             ((half, cols, outs), BF16),
@@ -449,34 +429,51 @@
     far = swap(halo, "chan")
     small_theirs = swap(small, "chan")
     gcls, gcls_other = call(
-        cls_kernel, "cls", [((CLS_TOTAL, outs), F32)] * 2, [where, hid, dt]
+        cls_kernel, "cls", 1.5, [((CLS_TOTAL, outs), F32)] * 2, [where, hid, dt]
     )
     gcls_theirs = swap(gcls_other, "chan")
 
-    share = 9 * chans // pages
+    total = 9 * chans
+    first, second = total // pages, total // (pages * tiles)
+    cfirst, csecond = CLS_TOTAL // tiles, CLS_TOTAL // (pages * tiles)
     keep, small, *sends = call(
-        functools.partial(shared_kernel, BATCH), "shared",
-        [((share, outs), F32), ((8, LANES), F32)] + [((share + TRIO, outs), BF16)] * (pages - 1),
-        [where, f, halo, far, own, theirs, small, small_theirs],
-        [((rows + 2, cols, chans), BF16), ((rows, cols, 3 * outs), BF16), ((9 * chans, outs), F32)],
-    )
-    ckeep, *csends = step(where, TILE, tiles, gcls, None, [gcls_theirs], "cls_tile")
-
-    arrived = exchange(sends, "batch")
+        functools.partial(shared_kernel, pages - 1), "shared", 4,
+        [((first, outs), F32), ((8, LANES), F32)]
+        + [((first + TRIO, outs), BF16)] * (pages - 1)
+        + [((cfirst, outs), F32)]
+        + [((cfirst, outs), BF16)] * (tiles - 1),
+        [where, f, halo, far, own, theirs, small, small_theirs, gcls, gcls_theirs],
+        [((rows + 2, cols, chans), BF16), ((rows, cols, 3 * outs), BF16), ((total, outs), F32), ((CLS_TOTAL, outs), F32)],
+    )
+    ckeep, csends = sends[pages - 1], sends[pages:]
+    arrived = exchange(sends[: pages - 1], "batch")
     carrived = exchange(csends, "tile")
-    keep, small, *sends = step(where, TILE, tiles, keep, small, arrived, "shared_tile")
-    ckeep, *csends = step(where, BATCH, pages, ckeep, None, carrived, "cls_batch", [small])
-    arrived = exchange(sends, "tile")
+    keep, small, *sends = call(
+        functools.partial(sum_kernel, pages - 1, tiles - 1, tiles - 1), "sum", 0.7,
+        [((second, outs), F32), ((8, LANES), F32)]
+        + [((second + TRIO, outs), BF16)] * (tiles - 1)
+        + [((csecond, outs), F32)]
+        + [((csecond, outs), BF16)] * (pages - 1),
+        [where, keep, small, ckeep] + arrived + carrived,
+        [((first, outs), F32), ((cfirst, outs), F32)],
+    )
+    ckeep, csends = sends[tiles - 1], sends[tiles:]
+    arrived = exchange(sends[: tiles - 1], "tile")
     carrived = exchange(csends, "batch")
-    done, small = step(where, None, 1, keep, small, arrived, "shared_round")
-    (cdone,) = step(where, None, 1, ckeep, None, carrived, "cls_round", [small])
-    block = join(where, TILE, [done] + others(done, "tile"), BF16, "shared_join")
-    cblock = join(where, BATCH, [cdone] + others(cdone, "batch"), BF16, "cls_join", [block])
-    grad_shared = join(where, BATCH, [block] + others(block, "batch"), F32, "shared_out")
-    (grad_cls,) = call(
-        functools.partial(join_cls_kernel, TILE), "cls_out",
-        [((3, 3, LOGITS, outs), F32)],
-        [where, cblock] + others(cblock, "tile"),
+    done, small, cdone = call(
+        functools.partial(round_kernel, tiles - 1), "round", 0.7,
+        [((second, outs), BF16), ((8, LANES), F32), ((csecond, outs), BF16)],
+        [where, keep, small, ckeep] + arrived + carrived,
+    )
+    block, cblock = call(
+        functools.partial(join_kernel, tiles), "join", 0.7,
+        [((first, outs), BF16), ((cfirst, outs), BF16)],
+        [where, done] + others(done, "tile") + [cdone] + others(cdone, "batch"),
+    )
+    grad_shared, grad_cls = call(
+        functools.partial(out_kernel, pages), "out", 1.5,
+        [((total, outs), F32), ((3, 3, LOGITS, outs), F32)],
+        [where, block] + others(block, "batch") + [cblock] + others(cblock, "tile"),
         [((CLS_TOTAL, outs), F32)],
     )
     return (

time: 98.2 us -> 85.5 us (0.87)
  starting transfers between devices: 41.3 us -> 33.7 us
  Pallas kernels: 33.2 us -> 26.9 us
  waiting for transfers between devices: 17.8 us -> 20 us
    ppermute x26, starting transfers between devices: 40.6 us -> 33 us  [swap(): return lax.ppermute(x, axis, [(i, i ^ bit) for i in range(size)])]
    pallas_call x15 -> x10, Pallas kernels: 33.2 us -> 26.9 us  [call(): pl.pallas_call(kernel, in_specs=specs or [SMEM] + [VMEM] * (len(inputs) -...]
    ppermute x26, waiting for transfers between devices: 17.8 us -> 20 us  [swap(): return lax.ppermute(x, axis, [(i, i ^ bit) for i in range(size)])]
  transfers between devices with their start and end apart: 27 -> 27, of which waited for: 6 -> 11; matrix products, arithmetic and copies ran while one was open for 3% -> 2% of each run, Pallas kernels for 32% -> 16%
where the time goes in v3:
time: 85.5 us; the launch traced here: 85.3 us
  starting transfers between devices  33.7 us (39%)
  Pallas kernels  26.9 us (31%)
  waiting for transfers between devices  20 us (23%)
  local copies, waits for them, and re-layouts  3.95 us (5%)
    ppermute x26, starting transfers between devices, swap(): return lax.ppermute(x, axis, [(i, i ^ bit) for i in range(size)])  33 us
    pallas_call x10, Pallas kernels, call(): pl.pallas_call(kernel, in_specs=specs or [SMEM] + [VMEM] * (len(inputs) -...  26.9 us
    ppermute x26, waiting for transfers between devices, swap(): return lax.ppermute(x, axis, [(i, i ^ bit) for i in range(size)])  20 us
    unnamed x14, local copies, waits for them, and re-layouts  2.33 us
  transfers between devices with their start and end apart: 27, of which 11 were waited for; matrix products, arithmetic and copies ran while one was open for 2% of the time, Pallas kernels for 16%

profile of v3, /device:TPU:0, one launch (start us, length us, event | category | flops | bytes accessed | tf_op | source)
XLA Modules:
  0.0 85.3 jit_solution(3941400422987306292)
XLA Ops:
  0.6 0.5 collective-permute-start.2
  1.1 0.1 stack.19.where_ref
  1.2 1.4 %copy-done = bf16[1,12,256,256]{3,2,1,0:T(8,128)(2,1)S(1)} copy-done((bf16[1,12,256,256]{3,2,1,0:T(8,128)(2,1)S(1)}, bf16[1,12,256,256]{3,2,1,0:T(8,128)(2,1)}, u32[]{:S(2)}) %copy-start) | copy-done | bytes 1572888
  2.6 0.9 %copy-done.4 = s32[1,12,2304]{2,0,1:T(1,128)S(1)} copy-done((s32[1,12,2304]{2,0,1:T(1,128)S(1)}, s32[1,12,2304]{2,0,1:T(1,128)}, u32[]{:S(2)}) %copy-start.4) | copy-done | bytes 110616
  3.5 1.7 %edge.1 = (bf16[784,256]{1,0:T(8,128)(2,1)S(1)}, bf16[12,16,256]{2,1,0:T(8,128)(2,1)S(1)}, f32[8,128]{1,0:T(8,128)S(1)}) custom-call(s32[5]{0:T(128)S(1)} %stack.19.where_ref, bf16[12,256,256]{2,1,0:T(8,128)(2,1)S(1)} %bitcast.17, s32[12,1,2304]{2,1,0:T(1,128)S(1)} %bitcast.20), custom_call_target="tpu_custom_call" | custom-call | flops 1500000000 | bytes 1500000 | tf_op jit(solution)/shard_map/edge/pallas_call | solution.py:27
  5.3 0.7 collective-permute-start
  6.0 0.0 copy-start.2
  6.0 0.0 copy-start.6
  6.0 0.6 pack.1.packa_ref
  6.6 4.0 %collective-permute-start.3 = (bf16[1184,128]{1,0:T(8,128)(2,1)S(1)}, bf16[1184,128]{1,0:T(8,128)(2,1)S(1)}, u32[]{:S(2)}, u32[]{:S(2)}) collective-permute-start(bf16[1184,128]{1,0:T(8,128)(2,1)S(1)} %pack.1.packa_ref), channel_id=1, source_target_pairs={{0,1},{1,0},{2,3},{3,2},{4,5},{5,4},{6,7},{7,6},{8,9},{9,8},{10,11... | collective-permute-start | bytes 909320 | tf_op jit(solution)/shard_map/ppermute | solution.py:369
  10.6 1.5 %collective-permute-start.4 = (f32[8,128]{1,0:T(8,128)S(1)}, f32[8,128]{1,0:T(8,128)S(1)}, u32[]{:S(2)}, u32[]{:S(2)}) collective-permute-start(f32[8,128]{1,0:T(8,128)S(1)} %get-tuple-element.43), channel_id=1, source_target_pairs={{0,2},{2,0},{1,3},{3,1},{4,6},{6,4},{5,7},{7,5},{8,10},{10,8},{9,1... | collective-permute-start | bytes 12296 | tf_op jit(solution)/shard_map/ppermute | solution.py:369
  12.1 2.1 %collective-permute-done.4 = f32[8,128]{1,0:T(8,128)S(1)} collective-permute-done((f32[8,128]{1,0:T(8,128)S(1)}, f32[8,128]{1,0:T(8,128)S(1)}, u32[]{:S(2)}, u32[]{:S(2)}) %collective-permute-start.4) | collective-permute-done | bytes 4128 | tf_op jit(solution)/shard_map/ppermute | solution.py:369
  14.3 1.6 %collective-permute-start.5 = (f32[8,128]{1,0:T(8,128)S(1)}, f32[8,128]{1,0:T(8,128)S(1)}, u32[]{:S(2)}, u32[]{:S(2)}) collective-permute-start(f32[8,128]{1,0:T(8,128)S(1)} %add.7.rest_0_), channel_id=1, source_target_pairs={{0,4},{4,0},{8,12},{12,8},{1,5},{5,1},{9,13},{13,9},{2,6},{6,2},{1... | collective-permute-start | bytes 12296 | tf_op jit(solution)/shard_map/ppermute | solution.py:369
  15.8 1.5 %collective-permute-start.6 = (f32[8,128]{1,0:T(8,128)S(1)}, f32[8,128]{1,0:T(8,128)S(1)}, u32[]{:S(2)}, u32[]{:S(2)}) collective-permute-start(f32[8,128]{1,0:T(8,128)S(1)} %add.7.rest_0_), channel_id=1, source_target_pairs={{0,8},{4,12},{8,0},{12,4},{1,9},{5,13},{9,1},{13,5},{2,10},{6,14},... | collective-permute-start | bytes 12296 | tf_op jit(solution)/shard_map/ppermute | solution.py:369
  17.4 0.0 collective-permute-done.3.packb_ref
  17.4 1.3 %collective-permute-start.7 = (f32[8,128]{1,0:T(8,128)S(1)}, f32[8,128]{1,0:T(8,128)S(1)}, u32[]{:S(2)}, u32[]{:S(2)}) collective-permute-start(f32[8,128]{1,0:T(8,128)S(1)} %add.7.rest_0_), channel_id=1, source_target_pairs={{0,12},{4,8},{8,4},{12,0},{1,13},{5,9},{9,5},{13,1},{2,14},{6,10},... | collective-permute-start | bytes 12296 | tf_op jit(solution)/shard_map/ppermute | solution.py:369
  18.7 11.1 %head.1 = (bf16[10,256,256]{2,1,0:T(8,128)(2,1)S(1)}, f32[8,256,128]{2,1,0:T(8,128)S(1)}, f32[1,128]{1,0:T(1,128)S(1)}) custom-call(s32[5]{0:T(128)S(1)} %stack.19.where_ref, bf16[12,256,256]{2,1,0:T(8,128)(2,1)} %bitcast.16, bf16[784,256]{1,0:T(8,128)(2,1)S(1)} %collective-permute-done.halo_ref, bf16[12,16,256]{2,1,0:T(8,128)(2,1)S(1)} %get-tuple-element.39.labt_ref, ...), custom_call_target="tpu_custom_call" | custom-call | flops 11000000512 | bytes 11000000 | tf_op jit(solution)/shard_map/head/pallas_call | solution.py:27
  29.8 0.0 collective-permute-done.5.rest_1_
  29.8 0.0 collective-permute-done.6.rest_2_
  29.8 0.0 collective-permute-done.7.rest_3_
  29.8 4.3 %back.1 = (bf16[6,336,256]{2,1,0:T(8,128)(2,1)S(1)}, bf16[6,256,128]{2,1,0:T(8,128)(2,1)S(1)}, bf16[6,256,128]{2,1,0:T(8,128)(2,1)S(1)}, f32[8,128]{1,0:T(8,128)S(1)}) custom-call(s32[5]{0:T(128)S(1)} %stack.19.where_ref, bf16[10,256,256]{2,1,0:T(8,128)(2,1)S(1)} %get-tuple-element.40.hid_ref, f32[8,256,128]{2,1,0:T(8,128)S(1)} %get-tuple-element.41.dz_ref, ...), custom_call_target="tpu_custom_call" | custom-call | flops 4000000000 | bytes 4000000 | tf_op jit(solution)/shard_map/back/pallas_call | solution.py:27
  34.1 1.5 %cls.1 = (f32[1024,128]{1,0:T(8,128)S(1)}, f32[1024,128]{1,0:T(8,128)S(1)}) custom-call(s32[5]{0:T(128)S(1)} %stack.19.where_ref, bf16[10,256,256]{2,1,0:T(8,128)(2,1)S(1)} %get-tuple-element.40.hid_ref, bf16[6,336,256]{2,1,0:T(8,128)(2,1)S(1)} %get-tuple-element.47.dt_ref), custom_call_target="tpu_custom_call" | custom-call | flops 1500000000 | bytes 1500000 | tf_op jit(solution)/shard_map/cls/pallas_call | solution.py:27
  35.6 0.1 collective-permute-start.10
  35.7 0.5 collective-permute-start.1
  36.2 0.1 collective-permute-start.8
  36.2 0.4 collective-permute-start.9
  36.7 2.0 %collective-permute-done.9.theirs_ref = f32[8,128]{1,0:T(8,128)S(1)} collective-permute-done((f32[8,128]{1,0:T(8,128)S(1)}, f32[8,128]{1,0:T(8,128)S(1)}, u32[]{:S(2)}, u32[]{:S(2)}) %collective-permute-start.9) | collective-permute-done | bytes 4128 | tf_op jit(solution)/shard_map/ppermute | solution.py:369
  38.7 0.0 collective-permute-done.1.far_ref
  38.7 0.0 collective-permute-done.8.other_ref
  38.7 4.0 %shared.1 = (f32[1152,128]{1,0:T(8,128)S(1)}, f32[8,128]{1,0:T(8,128)S(1)}, bf16[1184,128]{1,0:T(8,128)(2,1)S(1)}, f32[256,128]{1,0:T(8,128)S(1)}, bf16[256,128]...) custom-call(s32[5]{0:T(128)S(1)} %stack.19.where_ref, ...), custom_call_target="tpu_custom_call" | custom-call | flops 4000000000 | bytes 4000000 | tf_op jit(solution)/shard_map/shared/pallas_call | solution.py:27
  42.7 1.6 %collective-permute-start.11 = (bf16[1184,128]{1,0:T(8,128)(2,1)S(1)}, bf16[1184,128]{1,0:T(8,128)(2,1)S(1)}, u32[]{:S(2)}, u32[]{:S(2)}) collective-permute-start(bf16[1184,128]{1,0:T(8,128)(2,1)S(1)} %get-tuple-element.53), channel_id=1, source_target_pairs={{0,2},{2,0},{1,3},{3,1},{4,6},{6,4},{5,7},{7,5},{8,10},{10,8},{9,1... | collective-permute-start | bytes 909320 | tf_op jit(solution)/shard_map/ppermute | solution.py:369
  44.3 0.7 collective-permute-start.12
  45.0 2.4 %collective-permute-start.13 = (bf16[256,128]{1,0:T(8,128)(2,1)S(1)}, bf16[256,128]{1,0:T(8,128)(2,1)S(1)}, u32[]{:S(2)}, u32[]{:S(2)}) collective-permute-start(bf16[256,128]{1,0:T(8,128)(2,1)S(1)} %get-tuple-element.55), channel_id=1, source_target_pairs={{0,8},{4,12},{8,0},{12,4},{1,9},{5,13},{9,1},{13,5},{2,10},{6,14},... | collective-permute-start | bytes 196616 | tf_op jit(solution)/shard_map/ppermute | solution.py:369
  47.4 1.3 %collective-permute-start.14 = (bf16[256,128]{1,0:T(8,128)(2,1)S(1)}, bf16[256,128]{1,0:T(8,128)(2,1)S(1)}, u32[]{:S(2)}, u32[]{:S(2)}) collective-permute-start(bf16[256,128]{1,0:T(8,128)(2,1)S(1)} %get-tuple-element.56), channel_id=1, source_target_pairs={{0,12},{4,8},{8,4},{12,0},{1,13},{5,9},{9,5},{13,1},{2,14},{6,10},... | collective-permute-start | bytes 196616 | tf_op jit(solution)/shard_map/ppermute | solution.py:369
  48.7 0.6 collective-permute-done.12.refs_1_
  49.3 3.2 %collective-permute-done.13.refs_2_ = bf16[256,128]{1,0:T(8,128)(2,1)S(1)} collective-permute-done((bf16[256,128]{1,0:T(8,128)(2,1)S(1)}, bf16[256,128]{1,0:T(8,128)(2,1)S(1)}, u32[]{:S(2)}, u32[]{:S(2)}) %collective-permute-start.13) | collective-permute-done | bytes 65568 | tf_op jit(solution)/shard_map/ppermute | solution.py:369
  52.5 1.0 %collective-permute-done.14.refs_3_ = bf16[256,128]{1,0:T(8,128)(2,1)S(1)} collective-permute-done((bf16[256,128]{1,0:T(8,128)(2,1)S(1)}, bf16[256,128]{1,0:T(8,128)(2,1)S(1)}, u32[]{:S(2)}, u32[]{:S(2)}) %collective-permute-start.14) | collective-permute-done | bytes 65568 | tf_op jit(solution)/shard_map/ppermute | solution.py:369
  53.6 0.0 collective-permute-done.11.refs_0_
  53.6 0.7 sum.1
  54.3 1.0 %collective-permute-start.15 = (bf16[320,128]{1,0:T(8,128)(2,1)S(1)}, bf16[320,128]{1,0:T(8,128)(2,1)S(1)}, u32[]{:S(2)}, u32[]{:S(2)}) collective-permute-start(bf16[320,128]{1,0:T(8,128)(2,1)S(1)} %get-tuple-element.60), channel_id=1, source_target_pairs={{0,4},{4,0},{8,12},{12,8},{1,5},{5,1},{9,13},{13,9},{2,6},{6,2},{1... | collective-permute-start | bytes 245768 | tf_op jit(solution)/shard_map/ppermute | solution.py:369
  55.2 1.5 %collective-permute-start.16 = (bf16[320,128]{1,0:T(8,128)(2,1)S(1)}, bf16[320,128]{1,0:T(8,128)(2,1)S(1)}, u32[]{:S(2)}, u32[]{:S(2)}) collective-permute-start(bf16[320,128]{1,0:T(8,128)(2,1)S(1)} %get-tuple-element.61), channel_id=1, source_target_pairs={{0,8},{4,12},{8,0},{12,4},{1,9},{5,13},{9,1},{13,5},{2,10},{6,14},... | collective-permute-start | bytes 245768 | tf_op jit(solution)/shard_map/ppermute | solution.py:369
  56.8 1.9 %collective-permute-start.17 = (bf16[320,128]{1,0:T(8,128)(2,1)S(1)}, bf16[320,128]{1,0:T(8,128)(2,1)S(1)}, u32[]{:S(2)}, u32[]{:S(2)}) collective-permute-start(bf16[320,128]{1,0:T(8,128)(2,1)S(1)} %get-tuple-element.62), channel_id=1, source_target_pairs={{0,12},{4,8},{8,4},{12,0},{1,13},{5,9},{9,5},{13,1},{2,14},{6,10},... | collective-permute-start | bytes 245768 | tf_op jit(solution)/shard_map/ppermute | solution.py:369
  58.7 0.5 collective-permute-start.18
  59.2 3.4 %collective-permute-done.18.refs_3_ = bf16[128,128]{1,0:T(8,128)(2,1)S(1)} collective-permute-done((bf16[128,128]{1,0:T(8,128)(2,1)S(1)}, bf16[128,128]{1,0:T(8,128)(2,1)S(1)}, u32[]{:S(2)}, u32[]{:S(2)}) %collective-permute-start.18) | collective-permute-done | bytes 32800 | tf_op jit(solution)/shard_map/ppermute | solution.py:369
  62.6 0.0 collective-permute-done.15.refs_0_
  62.6 0.5 collective-permute-done.17.refs_2_
  63.1 0.6 round.1
  63.7 1.4 %collective-permute-start.19 = (bf16[288,128]{1,0:T(8,128)(2,1)S(1)}, bf16[288,128]{1,0:T(8,128)(2,1)S(1)}, u32[]{:S(2)}, u32[]{:S(2)}) collective-permute-start(bf16[288,128]{1,0:T(8,128)(2,1)S(1)} %get-tuple-element.64.refs_0_), channel_id=1, source_target_pairs={{0,4},{4,0},{8,12},{12,8},{1,5},{5,1},{9,13},{13,9},{2,6},{6,2},{1... | collective-permute-start | bytes 221192 | tf_op jit(solution)/shard_map/ppermute | solution.py:369
  65.1 1.6 %collective-permute-start.20 = (bf16[288,128]{1,0:T(8,128)(2,1)S(1)}, bf16[288,128]{1,0:T(8,128)(2,1)S(1)}, u32[]{:S(2)}, u32[]{:S(2)}) collective-permute-start(bf16[288,128]{1,0:T(8,128)(2,1)S(1)} %get-tuple-element.64.refs_0_), channel_id=1, source_target_pairs={{0,8},{4,12},{8,0},{12,4},{1,9},{5,13},{9,1},{13,5},{2,10},{6,14},... | collective-permute-start | bytes 221192 | tf_op jit(solution)/shard_map/ppermute | solution.py:369
  66.7 1.4 %collective-permute-start.21 = (bf16[288,128]{1,0:T(8,128)(2,1)S(1)}, bf16[288,128]{1,0:T(8,128)(2,1)S(1)}, u32[]{:S(2)}, u32[]{:S(2)}) collective-permute-start(bf16[288,128]{1,0:T(8,128)(2,1)S(1)} %get-tuple-element.64.refs_0_), channel_id=1, source_target_pairs={{0,12},{4,8},{8,4},{12,0},{1,13},{5,9},{9,5},{13,1},{2,14},{6,10},... | collective-permute-start | bytes 221192 | tf_op jit(solution)/shard_map/ppermute | solution.py:369
  68.1 0.7 collective-permute-start.22
  68.9 3.2 %collective-permute-done.22.refs_5_ = bf16[128,128]{1,0:T(8,128)(2,1)S(1)} collective-permute-done((bf16[128,128]{1,0:T(8,128)(2,1)S(1)}, bf16[128,128]{1,0:T(8,128)(2,1)S(1)}, u32[]{:S(2)}, u32[]{:S(2)}) %collective-permute-start.22) | collective-permute-done | bytes 32800 | tf_op jit(solution)/shard_map/ppermute | solution.py:369
  72.1 0.9 %collective-permute-done.21.refs_3_ = bf16[288,128]{1,0:T(8,128)(2,1)S(1)} collective-permute-done((bf16[288,128]{1,0:T(8,128)(2,1)S(1)}, bf16[288,128]{1,0:T(8,128)(2,1)S(1)}, u32[]{:S(2)}, u32[]{:S(2)}) %collective-permute-start.21) | collective-permute-done | bytes 73760 | tf_op jit(solution)/shard_map/ppermute | solution.py:369
  73.0 0.6 join.1
  73.5 1.1 %collective-permute-start.23 = (bf16[1152,128]{1,0:T(8,128)(2,1)S(1)}, bf16[1152,128]{1,0:T(8,128)(2,1)S(1)}, u32[]{:S(2)}, u32[]{:S(2)}) collective-permute-start(bf16[1152,128]{1,0:T(8,128)(2,1)S(1)} %get-tuple-element.66.refs_0_), channel_id=1, source_target_pairs={{0,2},{2,0},{1,3},{3,1},{4,6},{6,4},{5,7},{7,5},{8,10},{10,8},{9,1... | collective-permute-start | bytes 884744 | tf_op jit(solution)/shard_map/ppermute | solution.py:369
  74.6 0.5 slice_bitcast_fusion
  75.1 0.7 collective-permute-start.24
  75.8 1.7 %collective-permute-start.25 = (bf16[256,128]{1,0:T(8,128)(2,1)S(1)}, bf16[256,128]{1,0:T(8,128)(2,1)S(1)}, u32[]{:S(2)}, u32[]{:S(2)}) collective-permute-start(bf16[256,128]{1,0:T(8,128)(2,1)S(1)} %get-tuple-element.67.refs_2_), channel_id=1, source_target_pairs={{0,8},{4,12},{8,0},{12,4},{1,9},{5,13},{9,1},{13,5},{2,10},{6,14},... | collective-permute-start | bytes 196616 | tf_op jit(solution)/shard_map/ppermute | solution.py:369
  77.5 2.0 %collective-permute-start.26 = (bf16[256,128]{1,0:T(8,128)(2,1)S(1)}, bf16[256,128]{1,0:T(8,128)(2,1)S(1)}, u32[]{:S(2)}, u32[]{:S(2)}) collective-permute-start(bf16[256,128]{1,0:T(8,128)(2,1)S(1)} %get-tuple-element.67.refs_2_), channel_id=1, source_target_pairs={{0,12},{4,8},{8,4},{12,0},{1,13},{5,9},{9,5},{13,1},{2,14},{6,10},... | collective-permute-start | bytes 196616 | tf_op jit(solution)/shard_map/ppermute | solution.py:369
  79.5 0.5 slice_bitcast_fusion.1
  80.0 0.5 slice.11
  80.5 0.6 collective-permute-done.25.refs_4_
  81.1 2.4 %collective-permute-done.26.refs_5_ = bf16[256,128]{1,0:T(8,128)(2,1)S(1)} collective-permute-done((bf16[256,128]{1,0:T(8,128)(2,1)S(1)}, bf16[256,128]{1,0:T(8,128)(2,1)S(1)}, u32[]{:S(2)}, u32[]{:S(2)}) %collective-permute-start.26) | collective-permute-done | bytes 65568 | tf_op jit(solution)/shard_map/ppermute | solution.py:369
  83.5 1.8 %out.1 = (f32[2304,128]{1,0:T(8,128)}, f32[3,3,99,128]{3,2,1,0:T(8,128)}) custom-call(s32[5]{0:T(128)S(1)} %stack.19.where_ref, bf16[1152,128]{1,0:T(8,128)(2,1)S(1)} %get-tuple-element.66.refs_0_, bf16[1152,128]{1,0:T(8,128)(2,1)S(1)} %collective-permute-done.23.refs_1_, bf16[256,128]{1,0:T(8,128)(2,1)S(1)} %get-tuple-element.67.refs_2_, ...), custom_call_target="tpu_custom_call" | custom-call | flops 1500000000 | bytes 1500000 | tf_op jit(solution)/shard_map/out/pallas_call | solution.py:27
  (19 shorter events, 0.0 us)
Async XLA Ops:
  0.6 18.0 %collective-permute-start.2 = (bf16[3,3,256,128]{3,2,1,0:T(8,128)(2,1)}, bf16[3,3,256,128]{3,2,1,0:T(8,128)(2,1)S(1)}, u32[]{:S(2)}, u32[]{:S(2)}) collective-permute-start(bf16[3,3,256,128]{3,2,1,0:T(8,128)(2,1)} %w1a_ref.1), channel_id=1, source_target_pairs={{0,1},{1,0},{2,3},{3,2},{4,5},{5,4},{6,7},{7,6},{8,9},{9,8},{10,11... | collective-permute-start | bytes 1769480 | tf_op jit(solution)/shard_map/ppermute | solution.py:369
  1.2 1.4 %copy-start = (bf16[1,12,256,256]{3,2,1,0:T(8,128)(2,1)S(1)}, bf16[1,12,256,256]{3,2,1,0:T(8,128)(2,1)}, u32[]{:S(2)}) copy-start(bf16[1,12,256,256]{3,2,1,0:T(8,128)(2,1)} %param.6) | copy-start | bytes 4718596
  2.6 0.9 %copy-start.4 = (s32[1,12,2304]{2,0,1:T(1,128)S(1)}, s32[1,12,2304]{2,0,1:T(1,128)}, u32[]{:S(2)}) copy-start(s32[1,12,2304]{2,0,1:T(1,128)} %param.7) | copy-start | bytes 331780
  3.5 2.5 %copy-start.3 = (bf16[3,3,128,99]{2,3,1,0:T(8,128)(2,1)S(1)}, bf16[3,3,128,99]{2,3,1,0:T(8,128)(2,1)}, u32[]{:S(2)}) copy-start(bf16[3,3,128,99]{2,3,1,0:T(8,128)(2,1)} %param.10) | copy-start | bytes 684292
  3.5 2.5 %copy-start.5 = (f32[128]{0:T(128)S(1)}, f32[128]{0:T(128)}, u32[]{:S(2)}) copy-start(f32[128]{0:T(128)} %param.9) | copy-start | bytes 1540
  5.3 13.4 %collective-permute-start = (bf16[784,256]{1,0:T(8,128)(2,1)S(1)}, bf16[784,256]{1,0:T(8,128)(2,1)S(1)}, u32[]{:S(2)}, u32[]{:S(2)}) collective-permute-start(bf16[784,256]{1,0:T(8,128)(2,1)S(1)} %get-tuple-element.38), channel_id=1, source_target_pairs={{1,4},{4,1},{5,8},{8,5},{9,12},{12,9},{3,6},{6,3},{7,10},{10,7},{1... | collective-permute-start | bytes 1204232 | tf_op jit(solution)/shard_map/ppermute | solution.py:405
  6.0 12.6 %copy-start.2 = (bf16[3,3,256,128]{3,2,1,0:T(8,128)(2,1)S(1)}, bf16[3,3,256,128]{3,2,1,0:T(8,128)(2,1)}, u32[]{:S(2)}) copy-start(bf16[3,3,256,128]{3,2,1,0:T(8,128)(2,1)} %w1a_ref.1) | copy-start | bytes 1769476
  6.0 12.6 %copy-start.6 = (f32[99]{0:T(128)S(1)}, f32[99]{0:T(128)}, u32[]{:S(2)}) copy-start(f32[99]{0:T(128)} %param.11) | copy-start | bytes 1192
  6.6 10.7 %collective-permute-start.3 = (bf16[1184,128]{1,0:T(8,128)(2,1)S(1)}, bf16[1184,128]{1,0:T(8,128)(2,1)S(1)}, u32[]{:S(2)}, u32[]{:S(2)}) collective-permute-start(bf16[1184,128]{1,0:T(8,128)(2,1)S(1)} %pack.1.packa_ref), channel_id=1, source_target_pairs={{0,1},{1,0},{2,3},{3,2},{4,5},{5,4},{6,7},{7,6},{8,9},{9,8},{10,11... | collective-permute-start | bytes 909320 | tf_op jit(solution)/shard_map/ppermute | solution.py:369
  10.6 3.6 %collective-permute-start.4 = (f32[8,128]{1,0:T(8,128)S(1)}, f32[8,128]{1,0:T(8,128)S(1)}, u32[]{:S(2)}, u32[]{:S(2)}) collective-permute-start(f32[8,128]{1,0:T(8,128)S(1)} %get-tuple-element.43), channel_id=1, source_target_pairs={{0,2},{2,0},{1,3},{3,1},{4,6},{6,4},{5,7},{7,5},{8,10},{10,8},{9,1... | collective-permute-start | bytes 12296 | tf_op jit(solution)/shard_map/ppermute | solution.py:369
  14.3 15.5 %collective-permute-start.5 = (f32[8,128]{1,0:T(8,128)S(1)}, f32[8,128]{1,0:T(8,128)S(1)}, u32[]{:S(2)}, u32[]{:S(2)}) collective-permute-start(f32[8,128]{1,0:T(8,128)S(1)} %add.7.rest_0_), channel_id=1, source_target_pairs={{0,4},{4,0},{8,12},{12,8},{1,5},{5,1},{9,13},{13,9},{2,6},{6,2},{1... | collective-permute-start | bytes 12296 | tf_op jit(solution)/shard_map/ppermute | solution.py:369
  15.8 14.0 %collective-permute-start.6 = (f32[8,128]{1,0:T(8,128)S(1)}, f32[8,128]{1,0:T(8,128)S(1)}, u32[]{:S(2)}, u32[]{:S(2)}) collective-permute-start(f32[8,128]{1,0:T(8,128)S(1)} %add.7.rest_0_), channel_id=1, source_target_pairs={{0,8},{4,12},{8,0},{12,4},{1,9},{5,13},{9,1},{13,5},{2,10},{6,14},... | collective-permute-start | bytes 12296 | tf_op jit(solution)/shard_map/ppermute | solution.py:369
  17.4 12.4 %collective-permute-start.7 = (f32[8,128]{1,0:T(8,128)S(1)}, f32[8,128]{1,0:T(8,128)S(1)}, u32[]{:S(2)}, u32[]{:S(2)}) collective-permute-start(f32[8,128]{1,0:T(8,128)S(1)} %add.7.rest_0_), channel_id=1, source_target_pairs={{0,12},{4,8},{8,4},{12,0},{1,13},{5,9},{9,5},{13,1},{2,14},{6,10},... | collective-permute-start | bytes 12296 | tf_op jit(solution)/shard_map/ppermute | solution.py:369
  34.1 4.7 %copy-start.1 = (bf16[1,12,256,256]{3,2,1,0:T(8,128)(2,1)S(1)}, bf16[1,12,256,256]{3,2,1,0:T(8,128)(2,1)}, u32[]{:S(2)}) copy-start(bf16[1,12,256,256]{3,2,1,0:T(8,128)(2,1)} %param.6) | copy-start | bytes 4718596
  35.6 3.1 %collective-permute-start.10 = (f32[1024,128]{1,0:T(8,128)S(1)}, f32[1024,128]{1,0:T(8,128)S(1)}, u32[]{:S(2)}, u32[]{:S(2)}) collective-permute-start(f32[1024,128]{1,0:T(8,128)S(1)} %get-tuple-element.49), channel_id=1, source_target_pairs={{0,1},{1,0},{2,3},{3,2},{4,5},{5,4},{6,7},{7,6},{8,9},{9,8},{10,11... | collective-permute-start | bytes 1572872 | tf_op jit(solution)/shard_map/ppermute | solution.py:369
  35.7 3.0 %collective-permute-start.1 = (bf16[784,256]{1,0:T(8,128)(2,1)S(1)}, bf16[784,256]{1,0:T(8,128)(2,1)S(1)}, u32[]{:S(2)}, u32[]{:S(2)}) collective-permute-start(bf16[784,256]{1,0:T(8,128)(2,1)S(1)} %collective-permute-done.halo_ref), channel_id=1, source_target_pairs={{0,1},{1,0},{2,3},{3,2},{4,5},{5,4},{6,7},{7,6},{8,9},{9,8},{10,11... | collective-permute-start | bytes 1204232 | tf_op jit(solution)/shard_map/ppermute | solution.py:369
  36.2 2.5 %collective-permute-start.8 = (bf16[6,256,128]{2,1,0:T(8,128)(2,1)S(1)}, bf16[6,256,128]{2,1,0:T(8,128)(2,1)S(1)}, u32[]{:S(2)}, u32[]{:S(2)}) collective-permute-start(bf16[6,256,128]{2,1,0:T(8,128)(2,1)S(1)} %get-tuple-element.45), channel_id=1, source_target_pairs={{0,1},{1,0},{2,3},{3,2},{4,5},{5,4},{6,7},{7,6},{8,9},{9,8},{10,11... | collective-permute-start | bytes 1179656 | tf_op jit(solution)/shard_map/ppermute | solution.py:369
  36.2 2.5 %collective-permute-start.9 = (f32[8,128]{1,0:T(8,128)S(1)}, f32[8,128]{1,0:T(8,128)S(1)}, u32[]{:S(2)}, u32[]{:S(2)}) collective-permute-start(f32[8,128]{1,0:T(8,128)S(1)} %get-tuple-element.46.small_ref), channel_id=1, source_target_pairs={{0,1},{1,0},{2,3},{3,2},{4,5},{5,4},{6,7},{7,6},{8,9},{9,8},{10,11... | collective-permute-start | bytes 12296 | tf_op jit(solution)/shard_map/ppermute | solution.py:369
  42.7 10.8 %collective-permute-start.11 = (bf16[1184,128]{1,0:T(8,128)(2,1)S(1)}, bf16[1184,128]{1,0:T(8,128)(2,1)S(1)}, u32[]{:S(2)}, u32[]{:S(2)}) collective-permute-start(bf16[1184,128]{1,0:T(8,128)(2,1)S(1)} %get-tuple-element.53), channel_id=1, source_target_pairs={{0,2},{2,0},{1,3},{3,1},{4,6},{6,4},{5,7},{7,5},{8,10},{10,8},{9,1... | collective-permute-start | bytes 909320 | tf_op jit(solution)/shard_map/ppermute | solution.py:369
  44.3 5.0 %collective-permute-start.12 = (bf16[256,128]{1,0:T(8,128)(2,1)S(1)}, bf16[256,128]{1,0:T(8,128)(2,1)S(1)}, u32[]{:S(2)}, u32[]{:S(2)}) collective-permute-start(bf16[256,128]{1,0:T(8,128)(2,1)S(1)} %get-tuple-element.54), channel_id=1, source_target_pairs={{0,4},{4,0},{8,12},{12,8},{1,5},{5,1},{9,13},{13,9},{2,6},{6,2},{1... | collective-permute-start | bytes 196616 | tf_op jit(solution)/shard_map/ppermute | solution.py:369
  45.0 7.5 %collective-permute-start.13 = (bf16[256,128]{1,0:T(8,128)(2,1)S(1)}, bf16[256,128]{1,0:T(8,128)(2,1)S(1)}, u32[]{:S(2)}, u32[]{:S(2)}) collective-permute-start(bf16[256,128]{1,0:T(8,128)(2,1)S(1)} %get-tuple-element.55), channel_id=1, source_target_pairs={{0,8},{4,12},{8,0},{12,4},{1,9},{5,13},{9,1},{13,5},{2,10},{6,14},... | collective-permute-start | bytes 196616 | tf_op jit(solution)/shard_map/ppermute | solution.py:369
  47.4 6.2 %collective-permute-start.14 = (bf16[256,128]{1,0:T(8,128)(2,1)S(1)}, bf16[256,128]{1,0:T(8,128)(2,1)S(1)}, u32[]{:S(2)}, u32[]{:S(2)}) collective-permute-start(bf16[256,128]{1,0:T(8,128)(2,1)S(1)} %get-tuple-element.56), channel_id=1, source_target_pairs={{0,12},{4,8},{8,4},{12,0},{1,13},{5,9},{9,5},{13,1},{2,14},{6,10},... | collective-permute-start | bytes 196616 | tf_op jit(solution)/shard_map/ppermute | solution.py:369
  54.3 8.4 %collective-permute-start.15 = (bf16[320,128]{1,0:T(8,128)(2,1)S(1)}, bf16[320,128]{1,0:T(8,128)(2,1)S(1)}, u32[]{:S(2)}, u32[]{:S(2)}) collective-permute-start(bf16[320,128]{1,0:T(8,128)(2,1)S(1)} %get-tuple-element.60), channel_id=1, source_target_pairs={{0,4},{4,0},{8,12},{12,8},{1,5},{5,1},{9,13},{13,9},{2,6},{6,2},{1... | collective-permute-start | bytes 245768 | tf_op jit(solution)/shard_map/ppermute | solution.py:369
  55.2 7.4 %collective-permute-start.16 = (bf16[320,128]{1,0:T(8,128)(2,1)S(1)}, bf16[320,128]{1,0:T(8,128)(2,1)S(1)}, u32[]{:S(2)}, u32[]{:S(2)}) collective-permute-start(bf16[320,128]{1,0:T(8,128)(2,1)S(1)} %get-tuple-element.61), channel_id=1, source_target_pairs={{0,8},{4,12},{8,0},{12,4},{1,9},{5,13},{9,1},{13,5},{2,10},{6,14},... | collective-permute-start | bytes 245768 | tf_op jit(solution)/shard_map/ppermute | solution.py:369
  56.8 6.3 %collective-permute-start.17 = (bf16[320,128]{1,0:T(8,128)(2,1)S(1)}, bf16[320,128]{1,0:T(8,128)(2,1)S(1)}, u32[]{:S(2)}, u32[]{:S(2)}) collective-permute-start(bf16[320,128]{1,0:T(8,128)(2,1)S(1)} %get-tuple-element.62), channel_id=1, source_target_pairs={{0,12},{4,8},{8,4},{12,0},{1,13},{5,9},{9,5},{13,1},{2,14},{6,10},... | collective-permute-start | bytes 245768 | tf_op jit(solution)/shard_map/ppermute | solution.py:369
  58.7 3.9 %collective-permute-start.18 = (bf16[128,128]{1,0:T(8,128)(2,1)S(1)}, bf16[128,128]{1,0:T(8,128)(2,1)S(1)}, u32[]{:S(2)}, u32[]{:S(2)}) collective-permute-start(bf16[128,128]{1,0:T(8,128)(2,1)S(1)} %get-tuple-element.63), channel_id=1, source_target_pairs={{0,2},{2,0},{1,3},{3,1},{4,6},{6,4},{5,7},{7,5},{8,10},{10,8},{9,1... | collective-permute-start | bytes 98312 | tf_op jit(solution)/shard_map/ppermute | solution.py:369
  63.7 8.4 %collective-permute-start.19 = (bf16[288,128]{1,0:T(8,128)(2,1)S(1)}, bf16[288,128]{1,0:T(8,128)(2,1)S(1)}, u32[]{:S(2)}, u32[]{:S(2)}) collective-permute-start(bf16[288,128]{1,0:T(8,128)(2,1)S(1)} %get-tuple-element.64.refs_0_), channel_id=1, source_target_pairs={{0,4},{4,0},{8,12},{12,8},{1,5},{5,1},{9,13},{13,9},{2,6},{6,2},{1... | collective-permute-start | bytes 221192 | tf_op jit(solution)/shard_map/ppermute | solution.py:369
  65.1 7.0 %collective-permute-start.20 = (bf16[288,128]{1,0:T(8,128)(2,1)S(1)}, bf16[288,128]{1,0:T(8,128)(2,1)S(1)}, u32[]{:S(2)}, u32[]{:S(2)}) collective-permute-start(bf16[288,128]{1,0:T(8,128)(2,1)S(1)} %get-tuple-element.64.refs_0_), channel_id=1, source_target_pairs={{0,8},{4,12},{8,0},{12,4},{1,9},{5,13},{9,1},{13,5},{2,10},{6,14},... | collective-permute-start | bytes 221192 | tf_op jit(solution)/shard_map/ppermute | solution.py:369
  66.7 6.3 %collective-permute-start.21 = (bf16[288,128]{1,0:T(8,128)(2,1)S(1)}, bf16[288,128]{1,0:T(8,128)(2,1)S(1)}, u32[]{:S(2)}, u32[]{:S(2)}) collective-permute-start(bf16[288,128]{1,0:T(8,128)(2,1)S(1)} %get-tuple-element.64.refs_0_), channel_id=1, source_target_pairs={{0,12},{4,8},{8,4},{12,0},{1,13},{5,9},{9,5},{13,1},{2,14},{6,10},... | collective-permute-start | bytes 221192 | tf_op jit(solution)/shard_map/ppermute | solution.py:369
  68.1 3.9 %collective-permute-start.22 = (bf16[128,128]{1,0:T(8,128)(2,1)S(1)}, bf16[128,128]{1,0:T(8,128)(2,1)S(1)}, u32[]{:S(2)}, u32[]{:S(2)}) collective-permute-start(bf16[128,128]{1,0:T(8,128)(2,1)S(1)} %get-tuple-element.65.refs_4_), channel_id=1, source_target_pairs={{0,2},{2,0},{1,3},{3,1},{4,6},{6,4},{5,7},{7,5},{8,10},{10,8},{9,1... | collective-permute-start | bytes 98312 | tf_op jit(solution)/shard_map/ppermute | solution.py:369
  73.5 10.0 %collective-permute-start.23 = (bf16[1152,128]{1,0:T(8,128)(2,1)S(1)}, bf16[1152,128]{1,0:T(8,128)(2,1)S(1)}, u32[]{:S(2)}, u32[]{:S(2)}) collective-permute-start(bf16[1152,128]{1,0:T(8,128)(2,1)S(1)} %get-tuple-element.66.refs_0_), channel_id=1, source_target_pairs={{0,2},{2,0},{1,3},{3,1},{4,6},{6,4},{5,7},{7,5},{8,10},{10,8},{9,1... | collective-permute-start | bytes 884744 | tf_op jit(solution)/shard_map/ppermute | solution.py:369
  75.1 5.4 %collective-permute-start.24 = (bf16[256,128]{1,0:T(8,128)(2,1)S(1)}, bf16[256,128]{1,0:T(8,128)(2,1)S(1)}, u32[]{:S(2)}, u32[]{:S(2)}) collective-permute-start(bf16[256,128]{1,0:T(8,128)(2,1)S(1)} %get-tuple-element.67.refs_2_), channel_id=1, source_target_pairs={{0,4},{4,0},{8,12},{12,8},{1,5},{5,1},{9,13},{13,9},{2,6},{6,2},{1... | collective-permute-start | bytes 196616 | tf_op jit(solution)/shard_map/ppermute | solution.py:369
  75.8 5.3 %collective-permute-start.25 = (bf16[256,128]{1,0:T(8,128)(2,1)S(1)}, bf16[256,128]{1,0:T(8,128)(2,1)S(1)}, u32[]{:S(2)}, u32[]{:S(2)}) collective-permute-start(bf16[256,128]{1,0:T(8,128)(2,1)S(1)} %get-tuple-element.67.refs_2_), channel_id=1, source_target_pairs={{0,8},{4,12},{8,0},{12,4},{1,9},{5,13},{9,1},{13,5},{2,10},{6,14},... | collective-permute-start | bytes 196616 | tf_op jit(solution)/shard_map/ppermute | solution.py:369
  77.5 6.1 %collective-permute-start.26 = (bf16[256,128]{1,0:T(8,128)(2,1)S(1)}, bf16[256,128]{1,0:T(8,128)(2,1)S(1)}, u32[]{:S(2)}, u32[]{:S(2)}) collective-permute-start(bf16[256,128]{1,0:T(8,128)(2,1)S(1)} %get-tuple-element.67.refs_2_), channel_id=1, source_target_pairs={{0,12},{4,8},{8,4},{12,0},{1,13},{5,9},{9,5},{13,1},{2,14},{6,10},... | collective-permute-start | bytes 196616 | tf_op jit(solution)/shard_map/ppermute | solution.py:369

commit v4 on v3

--- a/solution.py
+++ b/solution.py
@@ -23,7 +23,7 @@
 SMEM = pl.BlockSpec(memory_space=pltpu.SMEM)
 
 
-def call(kernel, name, micros, outs, inputs, scratch=(), specs=None):
+def call(kernel, name, micros, outs, inputs, scratch=(), specs=None, mib=48):
     return pl.pallas_call(
         kernel,
         in_specs=specs or [SMEM] + [VMEM] * (len(inputs) - 1),
@@ -31,7 +31,7 @@
         out_shape=[jax.ShapeDtypeStruct(shape, kind) for shape, kind in outs],
         scratch_shapes=[pltpu.VMEM(*shape) if isinstance(shape, tuple) else shape for shape in scratch],
         cost_estimate=pl.CostEstimate(flops=int(micros * 1e9), bytes_accessed=int(micros * 1e6), transcendentals=0),
-        compiler_params=pltpu.CompilerParams(vmem_limit_bytes=48 * 1024 * 1024),
+        compiler_params=pltpu.CompilerParams(vmem_limit_bytes=mib * 1024 * 1024),
         name=name,
     )(*inputs)
 
@@ -66,7 +66,7 @@
     return part[0:8] + part[8:16] + part[16:24]
 
 
-def edge_kernel(where_ref, f_ref, lab_ref, msg_ref, labt_ref, count_ref, sem):
+def edge_kernel(where_ref, f_ref, lab_ref, w2_ref, b1_ref, msg_ref, labt_ref, count_ref, pack_ref, sem):
     rows, cols, _ = f_ref.shape
     c = where_ref[0]
     copies = [
@@ -91,16 +91,13 @@
     msg_ref[3 * cols : 3 * cols + ANCH_ROWS] = jnp.where(
         c == 0, turned[:ANCH_ROWS].astype(F32), turned[ANCH_ROWS * (rows - 1) :].astype(F32)
     ).astype(BF16)
-    for copy in copies:
-        copy.wait()
-
-
-def pack_kernel(where_ref, w2_ref, b1_ref, pack_ref):
     deep = w2_ref.shape[3]
     for tap in range(9):
         pack_ref[LANES * tap : LANES * (tap + 1)] = jnp.zeros((LANES, deep), BF16)
         pack_ref[LANES * tap : LANES * tap + LOGITS] = w2_ref[tap // 3, tap % 3]
     put_trio(pack_ref, 9 * LANES, jnp.broadcast_to(b1_ref[...], (8, deep)))
+    for copy in copies:
+        copy.wait()
 
 
 def head_kernel(
@@ -259,10 +256,9 @@
 
 
 def shared_kernel(
-    n_send, where_ref, f_ref, halo_ref, far_ref, own_ref, other_ref, small_ref, theirs_ref, cls_ref, cls_theirs_ref, *rest
+    where_ref, f_ref, halo_ref, far_ref, own_ref, other_ref, small_ref, keep_ref, *rest
 ):
-    keep_ref, sum_ref, *send_refs, x_ref, d_ref, g_ref, cls_total_ref = rest
-    send_refs, cls_keep_ref, cls_send_refs = send_refs[:n_send], send_refs[n_send], send_refs[n_send + 1 :]
+    *send_refs, x_ref, d_ref, g_ref = rest
     rows, cols, chans = f_ref.shape
     half = rows // 2
     c = where_ref[0]
@@ -293,13 +289,14 @@
             start = (3 * i + j) * chans
             g_ref[start : start + chans] = g[:, j * outs : (j + 1) * outs]
     split(g_ref, where_ref[BATCH], keep_ref, send_refs)
-    cls_total_ref[...] = cls_ref[...] + cls_theirs_ref[...]
-    split(cls_total_ref, where_ref[TILE], cls_keep_ref, cls_send_refs)
-    mine, theirs = small_ref[...], theirs_ref[...]
-    sums = jnp.concatenate([mine[0:3] + theirs[0:3], mine[3:4] + theirs[4:5], mine[4:8]], axis=0)
-    sum_ref[...] = sums
     for ref in send_refs:
-        put_trio(ref, keep_ref.shape[0], sums)
+        put_trio(ref, keep_ref.shape[0], small_ref[...])
+
+
+def cls_split_kernel(where_ref, cls_ref, theirs_ref, keep_ref, *rest):
+    *send_refs, total_ref = rest
+    total_ref[...] = cls_ref[...] + theirs_ref[...]
+    split(total_ref, where_ref[TILE], keep_ref, send_refs)
 
 
 def pair_sum(parts):
@@ -388,16 +385,18 @@
     f = features[0]
     where = jnp.stack([c, t * rows + half * c, jnp.int32(tiles * rows), t, lax.axis_index("batch")]).astype(jnp.int32)
     lab = labels.reshape(rows, 1, labels.shape[2])
-    msg, labt, count = call(
-        edge_kernel, "edge", 1.5,
-        [((3 * cols + ANCH_ROWS, chans), BF16), ((rows, ANCH_ROWS, cols), BF16), ((8, LANES), F32)],
-        [where, f, lab],
+    msg, labt, count, pack = call(
+        edge_kernel, "edge", 2,
+        [
+            ((3 * cols + ANCH_ROWS, chans), BF16),
+            ((rows, ANCH_ROWS, cols), BF16),
+            ((8, LANES), F32),
+            ((9 * LANES + TRIO, outs), BF16),
+        ],
+        [where, f, lab, jnp.swapaxes(w_cls, 2, 3), b_shared.reshape(1, outs)],
         [pltpu.SemaphoreType.DMA((3,))],
-        [SMEM, HBM, VMEM],
-    )
-    (pack,) = call(
-        pack_kernel, "pack", 0.8, [((9 * LANES + TRIO, outs), BF16)],
-        [where, jnp.swapaxes(w_cls, 2, 3), b_shared.reshape(1, outs)],
+        [SMEM, HBM, VMEM, VMEM, VMEM],
+        52,
     )
     pairs = []
     for i in range(tiles - 1):
@@ -427,7 +426,6 @@
     )
     theirs = swap(other, "chan")
     far = swap(halo, "chan")
-    small_theirs = swap(small, "chan")
     gcls, gcls_other = call(
         cls_kernel, "cls", 1.5, [((CLS_TOTAL, outs), F32)] * 2, [where, hid, dt]
     )
@@ -436,17 +434,19 @@
     total = 9 * chans
     first, second = total // pages, total // (pages * tiles)
     cfirst, csecond = CLS_TOTAL // tiles, CLS_TOTAL // (pages * tiles)
-    keep, small, *sends = call(
-        functools.partial(shared_kernel, pages - 1), "shared", 4,
-        [((first, outs), F32), ((8, LANES), F32)]
-        + [((first + TRIO, outs), BF16)] * (pages - 1)
-        + [((cfirst, outs), F32)]
-        + [((cfirst, outs), BF16)] * (tiles - 1),
-        [where, f, halo, far, own, theirs, small, small_theirs, gcls, gcls_theirs],
-        [((rows + 2, cols, chans), BF16), ((rows, cols, 3 * outs), BF16), ((total, outs), F32), ((CLS_TOTAL, outs), F32)],
-    )
-    ckeep, csends = sends[pages - 1], sends[pages:]
-    arrived = exchange(sends[: pages - 1], "batch")
+    keep, *sends = call(
+        shared_kernel, "shared", 4,
+        [((first, outs), F32)] + [((first + TRIO, outs), BF16)] * (pages - 1),
+        [where, f, halo, far, own, theirs, small],
+        [((rows + 2, cols, chans), BF16), ((rows, cols, 3 * outs), BF16), ((total, outs), F32)],
+    )
+    ckeep, *csends = call(
+        cls_split_kernel, "cls_split", 0.6,
+        [((cfirst, outs), F32)] + [((cfirst, outs), BF16)] * (tiles - 1),
+        [where, gcls, gcls_theirs],
+        [((CLS_TOTAL, outs), F32)],
+    )
+    arrived = exchange(sends, "batch")
     carrived = exchange(csends, "tile")
     keep, small, *sends = call(
         functools.partial(sum_kernel, pages - 1, tiles - 1, tiles - 1), "sum", 0.7,
@@ -465,6 +465,7 @@
         [((second, outs), BF16), ((8, LANES), F32), ((csecond, outs), BF16)],
         [where, keep, small, ckeep] + arrived + carrived,
     )
+    small_theirs = swap(small, "chan")
     block, cblock = call(
         functools.partial(join_kernel, tiles), "join", 0.7,
         [((first, outs), BF16), ((cfirst, outs), BF16)],
@@ -478,10 +479,10 @@
     )
     return (
         grad_shared.reshape(3, 3, chans, outs),
-        small[3],
+        small[3] + small_theirs[4],
         jnp.swapaxes(grad_cls, 2, 3),
-        small[0, :LOGITS],
-        small[1, :1],
+        small[0, :LOGITS] + small_theirs[0, :LOGITS],
+        small[1, :1] + small_theirs[1, :1],
     )
 
 

time: 85.5 us -> 85.2 us (level)
  between operations: 0.8 us -> 3.21 us
  waiting for transfers between devices: 20 us -> 17.6 us
  starting transfers between devices: 33.7 us -> 32.4 us
  other arithmetic: 0.01 us -> 1.03 us
    ppermute x26, waiting for transfers between devices: 20 us -> 17.6 us  [swap(): return lax.ppermute(x, axis, [(i, i ^ bit) for i in range(size)])]
    ppermute x26, starting transfers between devices: 33 us -> 31.7 us  [swap(): return lax.ppermute(x, axis, [(i, i ^ bit) for i in range(size)])]
    add x0 -> x2, other arithmetic: none -> 1.03 us  [the longest x1 0.51 us: shards(): small[3] + small_theirs[4]]
    squeeze x2 -> x0, local copies, waits for them, and re-layouts: 1.02 us -> none  [the longest x1 0.51 us: shards(): small[3]]
    unnamed x14 -> x12, local copies, waits for them, and re-layouts: 2.33 us -> 2.5 us
  transfers between devices with their start and end apart: 27 -> 27, of which waited for: 11 -> 10; matrix products, arithmetic and copies ran while one was open for 2% -> 3% of each run, Pallas kernels for 16% -> 28%
where the time goes in v4:
time: 85.2 us; the launch traced here: 84.9 us
  starting transfers between devices  32.4 us (38%)
  Pallas kernels  27.1 us (32%)
  waiting for transfers between devices  17.6 us (21%)
  local copies, waits for them, and re-layouts  3.61 us (4%)
  between operations  3.21 us (4%)
  other arithmetic  1.03 us (1%)
    ppermute x26, starting transfers between devices, swap(): return lax.ppermute(x, axis, [(i, i ^ bit) for i in range(size)])  31.7 us
    pallas_call x10, Pallas kernels, call(): pl.pallas_call(kernel, in_specs=specs or [SMEM] + [VMEM] * (len(inputs) -...  27.1 us
    ppermute x26, waiting for transfers between devices, swap(): return lax.ppermute(x, axis, [(i, i ^ bit) for i in range(size)])  17.6 us
    unnamed x12, local copies, waits for them, and re-layouts  2.5 us
  transfers between devices with their start and end apart: 27, of which 10 were waited for; matrix products, arithmetic and copies ran while one was open for 3% of the time, Pallas kernels for 28%

profile of v4, /device:TPU:0, one launch (start us, length us, event | category | flops | bytes accessed | tf_op | source)
XLA Modules:
  0.0 84.9 jit_solution(7147691775898068941)
XLA Ops:
  0.6 0.5 collective-permute-start.2
  1.1 0.1 stack.19.where_ref
  1.2 0.9 %copy-done.2 = bf16[3,3,128,99]{2,3,1,0:T(8,128)(2,1)S(1)} copy-done((bf16[3,3,128,99]{2,3,1,0:T(8,128)(2,1)S(1)}, bf16[3,3,128,99]{2,3,1,0:T(8,128)(2,1)}, u32[]{:S(2)}) %copy-start.2) | copy-done | bytes 228120
  2.2 0.9 %copy-done.3 = s32[1,12,2304]{2,0,1:T(1,128)S(1)} copy-done((s32[1,12,2304]{2,0,1:T(1,128)S(1)}, s32[1,12,2304]{2,0,1:T(1,128)}, u32[]{:S(2)}) %copy-start.3) | copy-done | bytes 110616
  3.1 0.7 copy-done.4
  3.7 2.1 %edge.1 = (bf16[784,256]{1,0:T(8,128)(2,1)S(1)}, bf16[12,16,256]{2,1,0:T(8,128)(2,1)S(1)}, f32[8,128]{1,0:T(8,128)S(1)}, bf16[1184,128]{1,0:T(8,128)(2,1)S(1)}) custom-call(s32[5]{0:T(128)S(1)} %stack.19.where_ref, bf16[12,256,256]{2,1,0:T(8,128)(2,1)} %bitcast.16, s32[12,1,2304]{2,1,0:T(1,128)S(1)} %bitcast.20, bf16[3,3,99,128]{3,2,1,0:T(8,128)(2,1)S(1)} %bitcast.19, ...), custom_call_target="tpu_custom_call" | custom-call | flops 2000000000 | bytes 2000000 | tf_op jit(solution)/shard_map/edge/pallas_call | solution.py:27
  5.9 0.7 collective-permute-start
  6.6 4.0 %collective-permute-start.3 = (bf16[1184,128]{1,0:T(8,128)(2,1)S(1)}, bf16[1184,128]{1,0:T(8,128)(2,1)S(1)}, u32[]{:S(2)}, u32[]{:S(2)}) collective-permute-start(bf16[1184,128]{1,0:T(8,128)(2,1)S(1)} %get-tuple-element.40.packa_ref), channel_id=1, source_target_pairs={{0,1},{1,0},{2,3},{3,2},{4,5},{5,4},{6,7},{7,6},{8,9},{9,8},{10,11... | collective-permute-start | bytes 909320 | tf_op jit(solution)/shard_map/ppermute | solution.py:366
  10.6 1.5 %collective-permute-start.4 = (f32[8,128]{1,0:T(8,128)S(1)}, f32[8,128]{1,0:T(8,128)S(1)}, u32[]{:S(2)}, u32[]{:S(2)}) collective-permute-start(f32[8,128]{1,0:T(8,128)S(1)} %get-tuple-element.44), channel_id=1, source_target_pairs={{0,2},{2,0},{1,3},{3,1},{4,6},{6,4},{5,7},{7,5},{8,10},{10,8},{9,1... | collective-permute-start | bytes 12296 | tf_op jit(solution)/shard_map/ppermute | solution.py:366
  12.1 2.1 %collective-permute-done.4 = f32[8,128]{1,0:T(8,128)S(1)} collective-permute-done((f32[8,128]{1,0:T(8,128)S(1)}, f32[8,128]{1,0:T(8,128)S(1)}, u32[]{:S(2)}, u32[]{:S(2)}) %collective-permute-start.4) | collective-permute-done | bytes 4128 | tf_op jit(solution)/shard_map/ppermute | solution.py:366
  14.2 1.6 %collective-permute-start.5 = (f32[8,128]{1,0:T(8,128)S(1)}, f32[8,128]{1,0:T(8,128)S(1)}, u32[]{:S(2)}, u32[]{:S(2)}) collective-permute-start(f32[8,128]{1,0:T(8,128)S(1)} %add.25.rest_0_), channel_id=1, source_target_pairs={{0,4},{4,0},{8,12},{12,8},{1,5},{5,1},{9,13},{13,9},{2,6},{6,2},{1... | collective-permute-start | bytes 12296 | tf_op jit(solution)/shard_map/ppermute | solution.py:366
  15.8 1.5 %collective-permute-start.6 = (f32[8,128]{1,0:T(8,128)S(1)}, f32[8,128]{1,0:T(8,128)S(1)}, u32[]{:S(2)}, u32[]{:S(2)}) collective-permute-start(f32[8,128]{1,0:T(8,128)S(1)} %add.25.rest_0_), channel_id=1, source_target_pairs={{0,8},{4,12},{8,0},{12,4},{1,9},{5,13},{9,1},{13,5},{2,10},{6,14},... | collective-permute-start | bytes 12296 | tf_op jit(solution)/shard_map/ppermute | solution.py:366
  17.3 0.0 collective-permute-done.3.packb_ref
  17.3 1.3 %collective-permute-start.7 = (f32[8,128]{1,0:T(8,128)S(1)}, f32[8,128]{1,0:T(8,128)S(1)}, u32[]{:S(2)}, u32[]{:S(2)}) collective-permute-start(f32[8,128]{1,0:T(8,128)S(1)} %add.25.rest_0_), channel_id=1, source_target_pairs={{0,12},{4,8},{8,4},{12,0},{1,13},{5,9},{9,5},{13,1},{2,14},{6,10},... | collective-permute-start | bytes 12296 | tf_op jit(solution)/shard_map/ppermute | solution.py:366
  18.6 0.0 collective-permute-done.halo_ref
  18.6 0.0 collective-permute-start.1
  18.6 0.0 collective-permute-done.2.w1b_ref
  18.6 11.1 %head.1 = (bf16[10,256,256]{2,1,0:T(8,128)(2,1)S(1)}, f32[8,256,128]{2,1,0:T(8,128)S(1)}, f32[1,128]{1,0:T(1,128)S(1)}) custom-call(s32[5]{0:T(128)S(1)} %stack.19.where_ref, bf16[12,256,256]{2,1,0:T(8,128)(2,1)} %bitcast.17, bf16[784,256]{1,0:T(8,128)(2,1)S(1)} %collective-permute-done.halo_ref, bf16[12,16,256]{2,1,0:T(8,128)(2,1)S(1)} %get-tuple-element.39.labt_ref, ...), custom_call_target="tpu_custom_call" | custom-call | flops 11000000512 | bytes 11000000 | tf_op jit(solution)/shard_map/head/pallas_call | solution.py:27
  29.7 4.2 %back.1 = (bf16[6,336,256]{2,1,0:T(8,128)(2,1)S(1)}, bf16[6,256,128]{2,1,0:T(8,128)(2,1)S(1)}, bf16[6,256,128]{2,1,0:T(8,128)(2,1)S(1)}, f32[8,128]{1,0:T(8,128)S(1)}) custom-call(s32[5]{0:T(128)S(1)} %stack.19.where_ref, bf16[10,256,256]{2,1,0:T(8,128)(2,1)S(1)} %get-tuple-element.41.hid_ref, f32[8,256,128]{2,1,0:T(8,128)S(1)} %get-tuple-element.42.dz_ref, ...), custom_call_target="tpu_custom_call" | custom-call | flops 4000000000 | bytes 4000000 | tf_op jit(solution)/shard_map/back/pallas_call | solution.py:27
  33.9 0.5 collective-permute-start.8
  34.5 1.5 %cls.1 = (f32[1024,128]{1,0:T(8,128)S(1)}, f32[1024,128]{1,0:T(8,128)S(1)}) custom-call(s32[5]{0:T(128)S(1)} %stack.19.where_ref, bf16[10,256,256]{2,1,0:T(8,128)(2,1)S(1)} %get-tuple-element.41.hid_ref, bf16[6,336,256]{2,1,0:T(8,128)(2,1)S(1)} %get-tuple-element.49.dt_ref), custom_call_target="tpu_custom_call" | custom-call | flops 1500000000 | bytes 1500000 | tf_op jit(solution)/shard_map/cls/pallas_call | solution.py:27
  36.0 0.1 collective-permute-start.9
  36.1 0.0 collective-permute-done.1.far_ref
  36.1 3.9 %shared.1 = (f32[1152,128]{1,0:T(8,128)S(1)}, bf16[1184,128]{1,0:T(8,128)(2,1)S(1)}) custom-call(s32[5]{0:T(128)S(1)} %stack.19.where_ref, bf16[12,256,256]{2,1,0:T(8,128)(2,1)S(1)} %bitcast.18, bf16[784,256]{1,0:T(8,128)(2,1)S(1)} %collective-permute-done.halo_ref, bf16[784,256]{1,0:T(8,128)(2,1)S(1)} %collective-permute-done.1.far_ref, ...), custom_call_target="tpu_custom_call" | custom-call | flops 4000000000 | bytes 4000000 | tf_op jit(solution)/shard_map/shared/pallas_call | solution.py:27
  40.0 1.6 %collective-permute-start.10 = (bf16[1184,128]{1,0:T(8,128)(2,1)S(1)}, bf16[1184,128]{1,0:T(8,128)(2,1)S(1)}, u32[]{:S(2)}, u32[]{:S(2)}) collective-permute-start(bf16[1184,128]{1,0:T(8,128)(2,1)S(1)} %get-tuple-element.53), channel_id=1, source_target_pairs={{0,2},{2,0},{1,3},{3,1},{4,6},{6,4},{5,7},{7,5},{8,10},{10,8},{9,1... | collective-permute-start | bytes 909320 | tf_op jit(solution)/shard_map/ppermute | solution.py:366
  41.5 0.6 cls_split.1
  42.2 0.7 collective-permute-start.11
  42.9 2.4 %collective-permute-start.12 = (bf16[256,128]{1,0:T(8,128)(2,1)S(1)}, bf16[256,128]{1,0:T(8,128)(2,1)S(1)}, u32[]{:S(2)}, u32[]{:S(2)}) collective-permute-start(bf16[256,128]{1,0:T(8,128)(2,1)S(1)} %get-tuple-element.55), channel_id=1, source_target_pairs={{0,8},{4,12},{8,0},{12,4},{1,9},{5,13},{9,1},{13,5},{2,10},{6,14},... | collective-permute-start | bytes 196616 | tf_op jit(solution)/shard_map/ppermute | solution.py:366
  45.3 1.3 %collective-permute-start.13 = (bf16[256,128]{1,0:T(8,128)(2,1)S(1)}, bf16[256,128]{1,0:T(8,128)(2,1)S(1)}, u32[]{:S(2)}, u32[]{:S(2)}) collective-permute-start(bf16[256,128]{1,0:T(8,128)(2,1)S(1)} %get-tuple-element.56), channel_id=1, source_target_pairs={{0,12},{4,8},{8,4},{12,0},{1,13},{5,9},{9,5},{13,1},{2,14},{6,10},... | collective-permute-start | bytes 196616 | tf_op jit(solution)/shard_map/ppermute | solution.py:366
  46.6 0.6 collective-permute-done.11.refs_1_
  47.2 3.4 %collective-permute-done.12.refs_2_ = bf16[256,128]{1,0:T(8,128)(2,1)S(1)} collective-permute-done((bf16[256,128]{1,0:T(8,128)(2,1)S(1)}, bf16[256,128]{1,0:T(8,128)(2,1)S(1)}, u32[]{:S(2)}, u32[]{:S(2)}) %collective-permute-start.12) | collective-permute-done | bytes 65568 | tf_op jit(solution)/shard_map/ppermute | solution.py:366
  50.6 0.9 %collective-permute-done.13.refs_3_ = bf16[256,128]{1,0:T(8,128)(2,1)S(1)} collective-permute-done((bf16[256,128]{1,0:T(8,128)(2,1)S(1)}, bf16[256,128]{1,0:T(8,128)(2,1)S(1)}, u32[]{:S(2)}, u32[]{:S(2)}) %collective-permute-start.13) | collective-permute-done | bytes 65568 | tf_op jit(solution)/shard_map/ppermute | solution.py:366
  51.5 0.0 collective-permute-done.10.refs_0_
  51.5 0.7 sum.1
  52.2 1.3 %collective-permute-start.14 = (bf16[320,128]{1,0:T(8,128)(2,1)S(1)}, bf16[320,128]{1,0:T(8,128)(2,1)S(1)}, u32[]{:S(2)}, u32[]{:S(2)}) collective-permute-start(bf16[320,128]{1,0:T(8,128)(2,1)S(1)} %get-tuple-element.60), channel_id=1, source_target_pairs={{0,4},{4,0},{8,12},{12,8},{1,5},{5,1},{9,13},{13,9},{2,6},{6,2},{1... | collective-permute-start | bytes 245768 | tf_op jit(solution)/shard_map/ppermute | solution.py:366
  53.5 1.5 %collective-permute-start.15 = (bf16[320,128]{1,0:T(8,128)(2,1)S(1)}, bf16[320,128]{1,0:T(8,128)(2,1)S(1)}, u32[]{:S(2)}, u32[]{:S(2)}) collective-permute-start(bf16[320,128]{1,0:T(8,128)(2,1)S(1)} %get-tuple-element.61), channel_id=1, source_target_pairs={{0,8},{4,12},{8,0},{12,4},{1,9},{5,13},{9,1},{13,5},{2,10},{6,14},... | collective-permute-start | bytes 245768 | tf_op jit(solution)/shard_map/ppermute | solution.py:366
  55.0 1.6 %collective-permute-start.16 = (bf16[320,128]{1,0:T(8,128)(2,1)S(1)}, bf16[320,128]{1,0:T(8,128)(2,1)S(1)}, u32[]{:S(2)}, u32[]{:S(2)}) collective-permute-start(bf16[320,128]{1,0:T(8,128)(2,1)S(1)} %get-tuple-element.62), channel_id=1, source_target_pairs={{0,12},{4,8},{8,4},{12,0},{1,13},{5,9},{9,5},{13,1},{2,14},{6,10},... | collective-permute-start | bytes 245768 | tf_op jit(solution)/shard_map/ppermute | solution.py:366
  56.6 0.5 collective-permute-start.17
  57.1 3.4 %collective-permute-done.17.refs_3_ = bf16[128,128]{1,0:T(8,128)(2,1)S(1)} collective-permute-done((bf16[128,128]{1,0:T(8,128)(2,1)S(1)}, bf16[128,128]{1,0:T(8,128)(2,1)S(1)}, u32[]{:S(2)}, u32[]{:S(2)}) %collective-permute-start.17) | collective-permute-done | bytes 32800 | tf_op jit(solution)/shard_map/ppermute | solution.py:366
  60.6 1.5 %collective-permute-done.15.refs_1_ = bf16[320,128]{1,0:T(8,128)(2,1)S(1)} collective-permute-done((bf16[320,128]{1,0:T(8,128)(2,1)S(1)}, bf16[320,128]{1,0:T(8,128)(2,1)S(1)}, u32[]{:S(2)}, u32[]{:S(2)}) %collective-permute-start.15) | collective-permute-done | bytes 81952 | tf_op jit(solution)/shard_map/ppermute | solution.py:366
  62.1 0.6 round.1
  62.6 1.6 %collective-permute-start.18 = (bf16[288,128]{1,0:T(8,128)(2,1)S(1)}, bf16[288,128]{1,0:T(8,128)(2,1)S(1)}, u32[]{:S(2)}, u32[]{:S(2)}) collective-permute-start(bf16[288,128]{1,0:T(8,128)(2,1)S(1)} %get-tuple-element.64.refs_0_), channel_id=1, source_target_pairs={{0,4},{4,0},{8,12},{12,8},{1,5},{5,1},{9,13},{13,9},{2,6},{6,2},{1... | collective-permute-start | bytes 221192 | tf_op jit(solution)/shard_map/ppermute | solution.py:366
  64.2 0.9 %collective-permute-start.19 = (bf16[288,128]{1,0:T(8,128)(2,1)S(1)}, bf16[288,128]{1,0:T(8,128)(2,1)S(1)}, u32[]{:S(2)}, u32[]{:S(2)}) collective-permute-start(bf16[288,128]{1,0:T(8,128)(2,1)S(1)} %get-tuple-element.64.refs_0_), channel_id=1, source_target_pairs={{0,8},{4,12},{8,0},{12,4},{1,9},{5,13},{9,1},{13,5},{2,10},{6,14},... | collective-permute-start | bytes 221192 | tf_op jit(solution)/shard_map/ppermute | solution.py:366
  65.1 2.0 %collective-permute-start.20 = (bf16[288,128]{1,0:T(8,128)(2,1)S(1)}, bf16[288,128]{1,0:T(8,128)(2,1)S(1)}, u32[]{:S(2)}, u32[]{:S(2)}) collective-permute-start(bf16[288,128]{1,0:T(8,128)(2,1)S(1)} %get-tuple-element.64.refs_0_), channel_id=1, source_target_pairs={{0,12},{4,8},{8,4},{12,0},{1,13},{5,9},{9,5},{13,1},{2,14},{6,10},... | collective-permute-start | bytes 221192 | tf_op jit(solution)/shard_map/ppermute | solution.py:366
  67.1 0.7 collective-permute-start.21
  67.8 0.0 collective-permute-start.26
  67.8 0.5 slice.22
  68.3 2.7 %collective-permute-done.21.refs_5_ = bf16[128,128]{1,0:T(8,128)(2,1)S(1)} collective-permute-done((bf16[128,128]{1,0:T(8,128)(2,1)S(1)}, bf16[128,128]{1,0:T(8,128)(2,1)S(1)}, u32[]{:S(2)}, u32[]{:S(2)}) %collective-permute-start.21) | collective-permute-done | bytes 32800 | tf_op jit(solution)/shard_map/ppermute | solution.py:366
  71.0 0.0 collective-permute-done.18.refs_1_
  71.0 1.1 %collective-permute-done.19.refs_2_ = bf16[288,128]{1,0:T(8,128)(2,1)S(1)} collective-permute-done((bf16[288,128]{1,0:T(8,128)(2,1)S(1)}, bf16[288,128]{1,0:T(8,128)(2,1)S(1)}, u32[]{:S(2)}, u32[]{:S(2)}) %collective-permute-start.19) | collective-permute-done | bytes 73760 | tf_op jit(solution)/shard_map/ppermute | solution.py:366
  72.1 0.0 collective-permute-done.20.refs_3_
  72.1 0.6 join.1
  72.7 0.2 collective-permute-start.22
  72.9 0.0 collective-permute-done.26
  72.9 0.5 add_bitcast_fusion
  73.4 1.3 %collective-permute-start.23 = (bf16[256,128]{1,0:T(8,128)(2,1)S(1)}, bf16[256,128]{1,0:T(8,128)(2,1)S(1)}, u32[]{:S(2)}, u32[]{:S(2)}) collective-permute-start(bf16[256,128]{1,0:T(8,128)(2,1)S(1)} %get-tuple-element.67.refs_2_), channel_id=1, source_target_pairs={{0,4},{4,0},{8,12},{12,8},{1,5},{5,1},{9,13},{13,9},{2,6},{6,2},{1... | collective-permute-start | bytes 196616 | tf_op jit(solution)/shard_map/ppermute | solution.py:366
  74.7 1.1 %collective-permute-start.24 = (bf16[256,128]{1,0:T(8,128)(2,1)S(1)}, bf16[256,128]{1,0:T(8,128)(2,1)S(1)}, u32[]{:S(2)}, u32[]{:S(2)}) collective-permute-start(bf16[256,128]{1,0:T(8,128)(2,1)S(1)} %get-tuple-element.67.refs_2_), channel_id=1, source_target_pairs={{0,8},{4,12},{8,0},{12,4},{1,9},{5,13},{9,1},{13,5},{2,10},{6,14},... | collective-permute-start | bytes 196616 | tf_op jit(solution)/shard_map/ppermute | solution.py:366
  75.8 2.0 %collective-permute-start.25 = (bf16[256,128]{1,0:T(8,128)(2,1)S(1)}, bf16[256,128]{1,0:T(8,128)(2,1)S(1)}, u32[]{:S(2)}, u32[]{:S(2)}) collective-permute-start(bf16[256,128]{1,0:T(8,128)(2,1)S(1)} %get-tuple-element.67.refs_2_), channel_id=1, source_target_pairs={{0,12},{4,8},{8,4},{12,0},{1,13},{5,9},{9,5},{13,1},{2,14},{6,10},... | collective-permute-start | bytes 196616 | tf_op jit(solution)/shard_map/ppermute | solution.py:366
  77.8 0.5 add_bitcast_fusion.1
  78.3 0.5 slice.23
  80.1 0.6 collective-permute-done.24.refs_4_
  80.8 1.2 %collective-permute-done.25.refs_5_ = bf16[256,128]{1,0:T(8,128)(2,1)S(1)} collective-permute-done((bf16[256,128]{1,0:T(8,128)(2,1)S(1)}, bf16[256,128]{1,0:T(8,128)(2,1)S(1)}, u32[]{:S(2)}, u32[]{:S(2)}) %collective-permute-start.25) | collective-permute-done | bytes 65568 | tf_op jit(solution)/shard_map/ppermute | solution.py:366
  82.0 0.0 collective-permute-done.22.refs_1_
  82.0 1.8 %out.1 = (f32[2304,128]{1,0:T(8,128)}, f32[3,3,99,128]{3,2,1,0:T(8,128)}) custom-call(s32[5]{0:T(128)S(1)} %stack.19.where_ref, bf16[1152,128]{1,0:T(8,128)(2,1)S(1)} %get-tuple-element.66.refs_0_, bf16[1152,128]{1,0:T(8,128)(2,1)S(1)} %collective-permute-done.22.refs_1_, bf16[256,128]{1,0:T(8,128)(2,1)S(1)} %get-tuple-element.67.refs_2_, ...), custom_call_target="tpu_custom_call" | custom-call | flops 1500000000 | bytes 1500000 | tf_op jit(solution)/shard_map/out/pallas_call | solution.py:27
  (18 shorter events, 0.0 us)
Async XLA Ops:
  0.6 17.9 %collective-permute-start.2 = (bf16[3,3,256,128]{3,2,1,0:T(8,128)(2,1)}, bf16[3,3,256,128]{3,2,1,0:T(8,128)(2,1)S(1)}, u32[]{:S(2)}, u32[]{:S(2)}) collective-permute-start(bf16[3,3,256,128]{3,2,1,0:T(8,128)(2,1)} %w1a_ref.1), channel_id=1, source_target_pairs={{0,1},{1,0},{2,3},{3,2},{4,5},{5,4},{6,7},{7,6},{8,9},{9,8},{10,11... | collective-permute-start | bytes 1769480 | tf_op jit(solution)/shard_map/ppermute | solution.py:366
  1.2 0.9 %copy-start.2 = (bf16[3,3,128,99]{2,3,1,0:T(8,128)(2,1)S(1)}, bf16[3,3,128,99]{2,3,1,0:T(8,128)(2,1)}, u32[]{:S(2)}) copy-start(bf16[3,3,128,99]{2,3,1,0:T(8,128)(2,1)} %param.10) | copy-start | bytes 684292
  2.2 0.9 %copy-start.3 = (s32[1,12,2304]{2,0,1:T(1,128)S(1)}, s32[1,12,2304]{2,0,1:T(1,128)}, u32[]{:S(2)}) copy-start(s32[1,12,2304]{2,0,1:T(1,128)} %param.7) | copy-start | bytes 331780
  3.1 0.7 copy-start.4
  3.7 14.9 %copy-start.1 = (bf16[3,3,256,128]{3,2,1,0:T(8,128)(2,1)S(1)}, bf16[3,3,256,128]{3,2,1,0:T(8,128)(2,1)}, u32[]{:S(2)}) copy-start(bf16[3,3,256,128]{3,2,1,0:T(8,128)(2,1)} %w1a_ref.1) | copy-start | bytes 1769476
  3.7 14.9 %copy-start.5 = (f32[99]{0:T(128)S(1)}, f32[99]{0:T(128)}, u32[]{:S(2)}) copy-start(f32[99]{0:T(128)} %param.11) | copy-start | bytes 1192
  5.9 12.7 %collective-permute-start = (bf16[784,256]{1,0:T(8,128)(2,1)S(1)}, bf16[784,256]{1,0:T(8,128)(2,1)S(1)}, u32[]{:S(2)}, u32[]{:S(2)}) collective-permute-start(bf16[784,256]{1,0:T(8,128)(2,1)S(1)} %get-tuple-element.38), channel_id=1, source_target_pairs={{1,4},{4,1},{5,8},{8,5},{9,12},{12,9},{3,6},{6,3},{7,10},{10,7},{1... | collective-permute-start | bytes 1204232 | tf_op jit(solution)/shard_map/ppermute | solution.py:404
  6.6 10.7 %collective-permute-start.3 = (bf16[1184,128]{1,0:T(8,128)(2,1)S(1)}, bf16[1184,128]{1,0:T(8,128)(2,1)S(1)}, u32[]{:S(2)}, u32[]{:S(2)}) collective-permute-start(bf16[1184,128]{1,0:T(8,128)(2,1)S(1)} %get-tuple-element.40.packa_ref), channel_id=1, source_target_pairs={{0,1},{1,0},{2,3},{3,2},{4,5},{5,4},{6,7},{7,6},{8,9},{9,8},{10,11... | collective-permute-start | bytes 909320 | tf_op jit(solution)/shard_map/ppermute | solution.py:366
  10.6 3.6 %collective-permute-start.4 = (f32[8,128]{1,0:T(8,128)S(1)}, f32[8,128]{1,0:T(8,128)S(1)}, u32[]{:S(2)}, u32[]{:S(2)}) collective-permute-start(f32[8,128]{1,0:T(8,128)S(1)} %get-tuple-element.44), channel_id=1, source_target_pairs={{0,2},{2,0},{1,3},{3,1},{4,6},{6,4},{5,7},{7,5},{8,10},{10,8},{9,1... | collective-permute-start | bytes 12296 | tf_op jit(solution)/shard_map/ppermute | solution.py:366
  14.2 15.5 %collective-permute-start.5 = (f32[8,128]{1,0:T(8,128)S(1)}, f32[8,128]{1,0:T(8,128)S(1)}, u32[]{:S(2)}, u32[]{:S(2)}) collective-permute-start(f32[8,128]{1,0:T(8,128)S(1)} %add.25.rest_0_), channel_id=1, source_target_pairs={{0,4},{4,0},{8,12},{12,8},{1,5},{5,1},{9,13},{13,9},{2,6},{6,2},{1... | collective-permute-start | bytes 12296 | tf_op jit(solution)/shard_map/ppermute | solution.py:366
  15.8 13.9 %collective-permute-start.6 = (f32[8,128]{1,0:T(8,128)S(1)}, f32[8,128]{1,0:T(8,128)S(1)}, u32[]{:S(2)}, u32[]{:S(2)}) collective-permute-start(f32[8,128]{1,0:T(8,128)S(1)} %add.25.rest_0_), channel_id=1, source_target_pairs={{0,8},{4,12},{8,0},{12,4},{1,9},{5,13},{9,1},{13,5},{2,10},{6,14},... | collective-permute-start | bytes 12296 | tf_op jit(solution)/shard_map/ppermute | solution.py:366
  17.3 12.4 %collective-permute-start.7 = (f32[8,128]{1,0:T(8,128)S(1)}, f32[8,128]{1,0:T(8,128)S(1)}, u32[]{:S(2)}, u32[]{:S(2)}) collective-permute-start(f32[8,128]{1,0:T(8,128)S(1)} %add.25.rest_0_), channel_id=1, source_target_pairs={{0,12},{4,8},{8,4},{12,0},{1,13},{5,9},{9,5},{13,1},{2,14},{6,10},... | collective-permute-start | bytes 12296 | tf_op jit(solution)/shard_map/ppermute | solution.py:366
  18.6 17.5 %collective-permute-start.1 = (bf16[784,256]{1,0:T(8,128)(2,1)S(1)}, bf16[784,256]{1,0:T(8,128)(2,1)S(1)}, u32[]{:S(2)}, u32[]{:S(2)}) collective-permute-start(bf16[784,256]{1,0:T(8,128)(2,1)S(1)} %collective-permute-done.halo_ref), channel_id=1, source_target_pairs={{0,1},{1,0},{2,3},{3,2},{4,5},{5,4},{6,7},{7,6},{8,9},{9,8},{10,11... | collective-permute-start | bytes 1204232 | tf_op jit(solution)/shard_map/ppermute | solution.py:366
  33.9 2.1 %collective-permute-start.8 = (bf16[6,256,128]{2,1,0:T(8,128)(2,1)S(1)}, bf16[6,256,128]{2,1,0:T(8,128)(2,1)S(1)}, u32[]{:S(2)}, u32[]{:S(2)}) collective-permute-start(bf16[6,256,128]{2,1,0:T(8,128)(2,1)S(1)} %get-tuple-element.46), channel_id=1, source_target_pairs={{0,1},{1,0},{2,3},{3,2},{4,5},{5,4},{6,7},{7,6},{8,9},{9,8},{10,11... | collective-permute-start | bytes 1179656 | tf_op jit(solution)/shard_map/ppermute | solution.py:366
  34.4 1.6 %copy-start = (bf16[1,12,256,256]{3,2,1,0:T(8,128)(2,1)S(1)}, bf16[1,12,256,256]{3,2,1,0:T(8,128)(2,1)}, u32[]{:S(2)}) copy-start(bf16[1,12,256,256]{3,2,1,0:T(8,128)(2,1)} %param.6) | copy-start | bytes 4718596
  36.0 5.6 %collective-permute-start.9 = (f32[1024,128]{1,0:T(8,128)S(1)}, f32[1024,128]{1,0:T(8,128)S(1)}, u32[]{:S(2)}, u32[]{:S(2)}) collective-permute-start(f32[1024,128]{1,0:T(8,128)S(1)} %get-tuple-element.51), channel_id=1, source_target_pairs={{0,1},{1,0},{2,3},{3,2},{4,5},{5,4},{6,7},{7,6},{8,9},{9,8},{10,11... | collective-permute-start | bytes 1572872 | tf_op jit(solution)/shard_map/ppermute | solution.py:366
  40.0 11.5 %collective-permute-start.10 = (bf16[1184,128]{1,0:T(8,128)(2,1)S(1)}, bf16[1184,128]{1,0:T(8,128)(2,1)S(1)}, u32[]{:S(2)}, u32[]{:S(2)}) collective-permute-start(bf16[1184,128]{1,0:T(8,128)(2,1)S(1)} %get-tuple-element.53), channel_id=1, source_target_pairs={{0,2},{2,0},{1,3},{3,1},{4,6},{6,4},{5,7},{7,5},{8,10},{10,8},{9,1... | collective-permute-start | bytes 909320 | tf_op jit(solution)/shard_map/ppermute | solution.py:366
  42.2 5.0 %collective-permute-start.11 = (bf16[256,128]{1,0:T(8,128)(2,1)S(1)}, bf16[256,128]{1,0:T(8,128)(2,1)S(1)}, u32[]{:S(2)}, u32[]{:S(2)}) collective-permute-start(bf16[256,128]{1,0:T(8,128)(2,1)S(1)} %get-tuple-element.54), channel_id=1, source_target_pairs={{0,4},{4,0},{8,12},{12,8},{1,5},{5,1},{9,13},{13,9},{2,6},{6,2},{1... | collective-permute-start | bytes 196616 | tf_op jit(solution)/shard_map/ppermute | solution.py:366
  42.9 7.7 %collective-permute-start.12 = (bf16[256,128]{1,0:T(8,128)(2,1)S(1)}, bf16[256,128]{1,0:T(8,128)(2,1)S(1)}, u32[]{:S(2)}, u32[]{:S(2)}) collective-permute-start(bf16[256,128]{1,0:T(8,128)(2,1)S(1)} %get-tuple-element.55), channel_id=1, source_target_pairs={{0,8},{4,12},{8,0},{12,4},{1,9},{5,13},{9,1},{13,5},{2,10},{6,14},... | collective-permute-start | bytes 196616 | tf_op jit(solution)/shard_map/ppermute | solution.py:366
  45.3 6.2 %collective-permute-start.13 = (bf16[256,128]{1,0:T(8,128)(2,1)S(1)}, bf16[256,128]{1,0:T(8,128)(2,1)S(1)}, u32[]{:S(2)}, u32[]{:S(2)}) collective-permute-start(bf16[256,128]{1,0:T(8,128)(2,1)S(1)} %get-tuple-element.56), channel_id=1, source_target_pairs={{0,12},{4,8},{8,4},{12,0},{1,13},{5,9},{9,5},{13,1},{2,14},{6,10},... | collective-permute-start | bytes 196616 | tf_op jit(solution)/shard_map/ppermute | solution.py:366
  52.2 8.4 %collective-permute-start.14 = (bf16[320,128]{1,0:T(8,128)(2,1)S(1)}, bf16[320,128]{1,0:T(8,128)(2,1)S(1)}, u32[]{:S(2)}, u32[]{:S(2)}) collective-permute-start(bf16[320,128]{1,0:T(8,128)(2,1)S(1)} %get-tuple-element.60), channel_id=1, source_target_pairs={{0,4},{4,0},{8,12},{12,8},{1,5},{5,1},{9,13},{13,9},{2,6},{6,2},{1... | collective-permute-start | bytes 245768 | tf_op jit(solution)/shard_map/ppermute | solution.py:366
  53.5 8.6 %collective-permute-start.15 = (bf16[320,128]{1,0:T(8,128)(2,1)S(1)}, bf16[320,128]{1,0:T(8,128)(2,1)S(1)}, u32[]{:S(2)}, u32[]{:S(2)}) collective-permute-start(bf16[320,128]{1,0:T(8,128)(2,1)S(1)} %get-tuple-element.61), channel_id=1, source_target_pairs={{0,8},{4,12},{8,0},{12,4},{1,9},{5,13},{9,1},{13,5},{2,10},{6,14},... | collective-permute-start | bytes 245768 | tf_op jit(solution)/shard_map/ppermute | solution.py:366
  55.0 7.1 %collective-permute-start.16 = (bf16[320,128]{1,0:T(8,128)(2,1)S(1)}, bf16[320,128]{1,0:T(8,128)(2,1)S(1)}, u32[]{:S(2)}, u32[]{:S(2)}) collective-permute-start(bf16[320,128]{1,0:T(8,128)(2,1)S(1)} %get-tuple-element.62), channel_id=1, source_target_pairs={{0,12},{4,8},{8,4},{12,0},{1,13},{5,9},{9,5},{13,1},{2,14},{6,10},... | collective-permute-start | bytes 245768 | tf_op jit(solution)/shard_map/ppermute | solution.py:366
  56.6 3.9 %collective-permute-start.17 = (bf16[128,128]{1,0:T(8,128)(2,1)S(1)}, bf16[128,128]{1,0:T(8,128)(2,1)S(1)}, u32[]{:S(2)}, u32[]{:S(2)}) collective-permute-start(bf16[128,128]{1,0:T(8,128)(2,1)S(1)} %get-tuple-element.63), channel_id=1, source_target_pairs={{0,2},{2,0},{1,3},{3,1},{4,6},{6,4},{5,7},{7,5},{8,10},{10,8},{9,1... | collective-permute-start | bytes 98312 | tf_op jit(solution)/shard_map/ppermute | solution.py:366
  62.6 8.4 %collective-permute-start.18 = (bf16[288,128]{1,0:T(8,128)(2,1)S(1)}, bf16[288,128]{1,0:T(8,128)(2,1)S(1)}, u32[]{:S(2)}, u32[]{:S(2)}) collective-permute-start(bf16[288,128]{1,0:T(8,128)(2,1)S(1)} %get-tuple-element.64.refs_0_), channel_id=1, source_target_pairs={{0,4},{4,0},{8,12},{12,8},{1,5},{5,1},{9,13},{13,9},{2,6},{6,2},{1... | collective-permute-start | bytes 221192 | tf_op jit(solution)/shard_map/ppermute | solution.py:366
  64.2 7.9 %collective-permute-start.19 = (bf16[288,128]{1,0:T(8,128)(2,1)S(1)}, bf16[288,128]{1,0:T(8,128)(2,1)S(1)}, u32[]{:S(2)}, u32[]{:S(2)}) collective-permute-start(bf16[288,128]{1,0:T(8,128)(2,1)S(1)} %get-tuple-element.64.refs_0_), channel_id=1, source_target_pairs={{0,8},{4,12},{8,0},{12,4},{1,9},{5,13},{9,1},{13,5},{2,10},{6,14},... | collective-permute-start | bytes 221192 | tf_op jit(solution)/shard_map/ppermute | solution.py:366
  65.1 7.0 %collective-permute-start.20 = (bf16[288,128]{1,0:T(8,128)(2,1)S(1)}, bf16[288,128]{1,0:T(8,128)(2,1)S(1)}, u32[]{:S(2)}, u32[]{:S(2)}) collective-permute-start(bf16[288,128]{1,0:T(8,128)(2,1)S(1)} %get-tuple-element.64.refs_0_), channel_id=1, source_target_pairs={{0,12},{4,8},{8,4},{12,0},{1,13},{5,9},{9,5},{13,1},{2,14},{6,10},... | collective-permute-start | bytes 221192 | tf_op jit(solution)/shard_map/ppermute | solution.py:366
  67.1 3.9 %collective-permute-start.21 = (bf16[128,128]{1,0:T(8,128)(2,1)S(1)}, bf16[128,128]{1,0:T(8,128)(2,1)S(1)}, u32[]{:S(2)}, u32[]{:S(2)}) collective-permute-start(bf16[128,128]{1,0:T(8,128)(2,1)S(1)} %get-tuple-element.65.refs_4_), channel_id=1, source_target_pairs={{0,2},{2,0},{1,3},{3,1},{4,6},{6,4},{5,7},{7,5},{8,10},{10,8},{9,1... | collective-permute-start | bytes 98312 | tf_op jit(solution)/shard_map/ppermute | solution.py:366
  67.8 5.1 %collective-permute-start.26 = (f32[8,128]{1,0:T(8,128)S(1)}, f32[8,128]{1,0:T(8,128)S(1)}, u32[]{:S(2)}, u32[]{:S(2)}) collective-permute-start(f32[8,128]{1,0:T(8,128)S(1)} %get-tuple-element.69), channel_id=1, source_target_pairs={{0,1},{1,0},{2,3},{3,2},{4,5},{5,4},{6,7},{7,6},{8,9},{9,8},{10,11... | collective-permute-start | bytes 12296 | tf_op jit(solution)/shard_map/ppermute | solution.py:366
  72.7 9.3 %collective-permute-start.22 = (bf16[1152,128]{1,0:T(8,128)(2,1)S(1)}, bf16[1152,128]{1,0:T(8,128)(2,1)S(1)}, u32[]{:S(2)}, u32[]{:S(2)}) collective-permute-start(bf16[1152,128]{1,0:T(8,128)(2,1)S(1)} %get-tuple-element.66.refs_0_), channel_id=1, source_target_pairs={{0,2},{2,0},{1,3},{3,1},{4,6},{6,4},{5,7},{7,5},{8,10},{10,8},{9,1... | collective-permute-start | bytes 884744 | tf_op jit(solution)/shard_map/ppermute | solution.py:366
  73.4 6.7 %collective-permute-start.23 = (bf16[256,128]{1,0:T(8,128)(2,1)S(1)}, bf16[256,128]{1,0:T(8,128)(2,1)S(1)}, u32[]{:S(2)}, u32[]{:S(2)}) collective-permute-start(bf16[256,128]{1,0:T(8,128)(2,1)S(1)} %get-tuple-element.67.refs_2_), channel_id=1, source_target_pairs={{0,4},{4,0},{8,12},{12,8},{1,5},{5,1},{9,13},{13,9},{2,6},{6,2},{1... | collective-permute-start | bytes 196616 | tf_op jit(solution)/shard_map/ppermute | solution.py:366
  74.7 6.0 %collective-permute-start.24 = (bf16[256,128]{1,0:T(8,128)(2,1)S(1)}, bf16[256,128]{1,0:T(8,128)(2,1)S(1)}, u32[]{:S(2)}, u32[]{:S(2)}) collective-permute-start(bf16[256,128]{1,0:T(8,128)(2,1)S(1)} %get-tuple-element.67.refs_2_), channel_id=1, source_target_pairs={{0,8},{4,12},{8,0},{12,4},{1,9},{5,13},{9,1},{13,5},{2,10},{6,14},... | collective-permute-start | bytes 196616 | tf_op jit(solution)/shard_map/ppermute | solution.py:366
  75.8 6.2 %collective-permute-start.25 = (bf16[256,128]{1,0:T(8,128)(2,1)S(1)}, bf16[256,128]{1,0:T(8,128)(2,1)S(1)}, u32[]{:S(2)}, u32[]{:S(2)}) collective-permute-start(bf16[256,128]{1,0:T(8,128)(2,1)S(1)} %get-tuple-element.67.refs_2_), channel_id=1, source_target_pairs={{0,12},{4,8},{8,4},{12,0},{1,13},{5,9},{9,5},{13,1},{2,14},{6,10},... | collective-permute-start | bytes 196616 | tf_op jit(solution)/shard_map/ppermute | solution.py:366

commit v5 on v4

--- a/solution.py
+++ b/solution.py
@@ -15,6 +15,7 @@
 CLS_ROWS = 112
 CLS_TOTAL = 1024
 TILE, BATCH = 3, 4
+BLOCK = 2
 TRIO = 32
 BF16 = jnp.bfloat16
 F32 = jnp.float32
@@ -23,7 +24,7 @@
 SMEM = pl.BlockSpec(memory_space=pltpu.SMEM)
 
 
-def call(kernel, name, micros, outs, inputs, scratch=(), specs=None, mib=48):
+def call(kernel, name, micros, outs, inputs, scratch=(), specs=None, mib=32):
     return pl.pallas_call(
         kernel,
         in_specs=specs or [SMEM] + [VMEM] * (len(inputs) - 1),
@@ -31,7 +32,7 @@
         out_shape=[jax.ShapeDtypeStruct(shape, kind) for shape, kind in outs],
         scratch_shapes=[pltpu.VMEM(*shape) if isinstance(shape, tuple) else shape for shape in scratch],
         cost_estimate=pl.CostEstimate(flops=int(micros * 1e9), bytes_accessed=int(micros * 1e6), transcendentals=0),
-        compiler_params=pltpu.CompilerParams(vmem_limit_bytes=mib * 1024 * 1024),
+        compiler_params=pltpu.CompilerParams(vmem_limit_bytes=int(mib * 1024 * 1024)),
         name=name,
     )(*inputs)
 
@@ -48,6 +49,12 @@
     return lax.dot_general(left, right, (dims, ((), ())), preferred_element_type=F32)
 
 
+def taken(ref, start, rows):
+    cols = ref.shape[1]
+    parts = [ref[pl.ds(start + r, BLOCK)].reshape(BLOCK * cols, ref.shape[2]) for r in rows]
+    return jnp.concatenate(parts, axis=1)
+
+
 def three(x):
     high = x.astype(BF16)
     rest = x - high.astype(F32)
@@ -66,13 +73,15 @@
     return part[0:8] + part[8:16] + part[16:24]
 
 
-def edge_kernel(where_ref, f_ref, lab_ref, w2_ref, b1_ref, msg_ref, labt_ref, count_ref, pack_ref, sem):
+def edge_kernel(where_ref, f_ref, lab_ref, msg_ref, labt_ref, count_ref, near_ref, sem):
     rows, cols, _ = f_ref.shape
     c = where_ref[0]
     copies = [
         pltpu.make_async_copy(f_ref.at[(rows - 3) * c + k], msg_ref.at[pl.ds(cols * k, cols)], sem.at[k])
         for k in range(3)
     ]
+    near = near_ref.shape[0]
+    copies.append(pltpu.make_async_copy(f_ref.at[pl.ds((rows - near) * c, near)], near_ref, sem.at[3]))
     for copy in copies:
         copy.start()
     size = lab_ref.shape[2]
@@ -91,27 +100,22 @@
     msg_ref[3 * cols : 3 * cols + ANCH_ROWS] = jnp.where(
         c == 0, turned[:ANCH_ROWS].astype(F32), turned[ANCH_ROWS * (rows - 1) :].astype(F32)
     ).astype(BF16)
-    deep = w2_ref.shape[3]
-    for tap in range(9):
-        pack_ref[LANES * tap : LANES * (tap + 1)] = jnp.zeros((LANES, deep), BF16)
-        pack_ref[LANES * tap : LANES * tap + LOGITS] = w2_ref[tap // 3, tap % 3]
-    put_trio(pack_ref, 9 * LANES, jnp.broadcast_to(b1_ref[...], (8, deep)))
     for copy in copies:
         copy.wait()
 
 
 def head_kernel(
-    where_ref, f_ref, halo_ref, labt_ref, w1a_ref, w1b_ref, packa_ref, packb_ref, b2_ref,
-    hid_ref, dz_ref, loss_ref, xw_ref,
+    where_ref, near_ref, halo_ref, labt_ref, w1a_ref, w1b_ref, b1a_ref, b1b_ref, w2a_ref, w2b_ref, b2_ref,
+    hid_ref, dz_ref, loss_ref, w2_ref, xw_ref,
 ):
 
-    half = f_ref.shape[0] // 2
-    cols = f_ref.shape[1]
+    near = near_ref.shape[0]
+    half = near - 3
+    cols = near_ref.shape[1]
     c = where_ref[0]
     first = where_ref[1]
     total = where_ref[2]
-    near = half + 3
-    xw_ref[pl.ds(3 - 3 * c, near)] = f_ref[pl.ds((half - 3) * c, near)]
+    xw_ref[pl.ds(3 - 3 * c, near)] = near_ref[...]
     for k in range(3):
         xw_ref[near * c + k] = halo_ref[cols * k : cols * (k + 1)]
     w1 = [
@@ -123,18 +127,25 @@
     w1 = jnp.concatenate(w1, axis=0)
     chans = w1.shape[1] // 3
     deep = chans // 2
-    b1 = jnp.concatenate([get_trio(packa_ref, 9 * LANES)[:1], get_trio(packb_ref, 9 * LANES)[:1]], axis=1)
-
-    def conv1(h, carry):
-        lhs = jnp.concatenate([xw_ref[h], xw_ref[h + 1], xw_ref[h + 2]], axis=1)
-        y = dot(lhs, w1)
-        pre = shift_cells(y[:, :chans], 1) + y[:, chans : 2 * chans] + shift_cells(y[:, 2 * chans :], -1) + b1
-        row = first + h - 2
-        inside = jnp.logical_and(row >= 0, row < total)
-        hid_ref[h] = jnp.where(inside, jnp.maximum(pre, 0.0), 0.0).astype(BF16)
+    b1 = jnp.concatenate([b1a_ref[...], b1b_ref[...]], axis=1)
+    for tap in range(9):
+        end = LANES * tap + LANES
+        w2_ref[end - 32 : end] = jnp.zeros((32, chans), BF16)
+        w2_ref[end - LANES : end - LANES + LOGITS, :deep] = w2a_ref[tap // 3, tap % 3]
+        w2_ref[end - LANES : end - LANES + LOGITS, deep:] = w2b_ref[tap // 3, tap % 3]
+
+    def conv1(g, carry):
+        pair = dot(taken(xw_ref, BLOCK * g, (0, 1, 2)), w1)
+        for k in range(BLOCK):
+            h = BLOCK * g + k
+            y = pair[k * cols : (k + 1) * cols]
+            pre = shift_cells(y[:, :chans], 1) + y[:, chans : 2 * chans] + shift_cells(y[:, 2 * chans :], -1) + b1
+            row = first + h - 2
+            inside = jnp.logical_and(row >= 0, row < total)
+            hid_ref[h] = jnp.where(inside, jnp.maximum(pre, 0.0), 0.0).astype(BF16)
         return carry
 
-    lax.fori_loop(0, half + 4, conv1, 0)
+    lax.fori_loop(0, (half + 4) // BLOCK, conv1, 0, unroll=True)
 
     lane = lax.broadcasted_iota(jnp.int32, (1, LANES), 1)
     kind = (lane % CLASSES + 1).astype(F32)
@@ -142,16 +153,17 @@
     anchor = lax.broadcasted_iota(jnp.int32, (ANCH_ROWS, LANES), 0)
     column = lax.broadcasted_iota(jnp.int32, (ANCH_ROWS, LANES), 1)
     spread = jnp.where(jnp.logical_and(column // CLASSES == anchor, column < LOGITS), 1.0, 0.0).astype(BF16)
-    w2 = [
-        jnp.concatenate([jnp.concatenate([tap(packa_ref, i, j), tap(packb_ref, i, j)], axis=1) for j in range(3)], axis=0)
-        for i in range(3)
-    ]
-    w2 = jnp.concatenate(w2, axis=1)
+    size = 3 * LANES
+    w2 = jnp.concatenate([w2_ref[size * i : size * (i + 1)] for i in range(3)], axis=1)
     b2 = jnp.concatenate([b2_ref[...], jnp.zeros((1, LANES - LOGITS), F32)], axis=1)
 
-    def focal(l, loss):
-        lhs = jnp.concatenate([hid_ref[l], hid_ref[l + 1], hid_ref[l + 2]], axis=1)
-        y = dot(lhs, w2, ((1,), (1,)))
+    def focal(g, loss):
+        pair = dot(taken(hid_ref, BLOCK * g, (0, 1, 2)), w2, ((1,), (1,)))
+        for k in range(BLOCK):
+            loss = loss + focal_row(BLOCK * g + k, pair[k * cols : (k + 1) * cols])
+        return loss
+
+    def focal_row(l, y):
         z = shift_cells(y[:, :LANES], 1) + y[:, LANES : 2 * LANES] + shift_cells(y[:, 2 * LANES :], -1) + b2
         at_halo = jnp.where(c == 0, l == 0, l == half + 1)
         local = jnp.clip(l - 1 + half * c, 0, 2 * half - 1)
@@ -174,16 +186,12 @@
         slope = ws * (2.0 * comp * soft + s)
         dz_ref[l] = jnp.where(hit, -slope, slope)
         own = jnp.logical_and(l >= 1, l <= half)
-        return loss + jnp.where(own, 1.0, 0.0) * jnp.sum(ws * soft, axis=0, keepdims=True)
-
-    loss_ref[...] = lax.fori_loop(0, half + 2, focal, jnp.zeros((1, LANES), F32))
-
-
-def tap(ref, i, j):
-    return ref[LANES * (3 * i + j) : LANES * (3 * i + j + 1)]
-
-
-def back_kernel(where_ref, hid_ref, dz_ref, loss_ref, packa_ref, packb_ref, *rest):
+        return jnp.where(own, 1.0, 0.0) * jnp.sum(ws * soft, axis=0, keepdims=True)
+
+    loss_ref[...] = lax.fori_loop(0, (half + 2) // BLOCK, focal, jnp.zeros((1, LANES), F32), unroll=True)
+
+
+def back_kernel(where_ref, hid_ref, dz_ref, loss_ref, w2_ref, *rest):
     *count_refs, dt_ref, own_ref, other_ref, small_ref, dlog_ref = rest
     half, _, cols = dt_ref.shape
     chans = hid_ref.shape[2]
@@ -207,24 +215,28 @@
         dt_ref[d] = jnp.concatenate([left, turned, right], axis=0).astype(BF16)
         return gcb + jnp.sum(dz, axis=0, keepdims=True)
 
-    gcb = lax.fori_loop(0, half, turn, jnp.zeros((1, LANES), F32))
+    gcb = lax.fori_loop(0, half, turn, jnp.zeros((1, LANES), F32), unroll=True)
     w2t = [
-        jnp.concatenate([x for j in range(3) for x in (tap(packa_ref, i, j), tap(packb_ref, i, j))], axis=1)
+        jnp.concatenate([w2_ref[LANES * (3 * i + j) : LANES * (3 * i + j + 1)] for j in range(3)], axis=1)
         for i in range(3)
     ]
     w2t = jnp.concatenate(w2t, axis=0)
 
-    def dpre_row(d, gsb):
-        lhs = jnp.concatenate([dlog_ref[d + 2], dlog_ref[d + 1], dlog_ref[d]], axis=1)
-        q = dot(lhs, w2t)
+    def dpre(g, gsb):
+        pair = dot(taken(dlog_ref, BLOCK * g, (2, 1, 0)), w2t)
+        for k in range(BLOCK):
+            gsb = gsb + dpre_row(BLOCK * g + k, pair[k * cols : (k + 1) * cols])
+        return gsb
+
+    def dpre_row(d, q):
         dhid = shift_cells(q[:, :chans], -1) + q[:, chans : 2 * chans] + shift_cells(q[:, 2 * chans :], 1)
         dpre = jnp.where(hid_ref[d + 2].astype(F32) > 0.0, dhid, 0.0)
         d16 = dpre.astype(BF16)
         own_ref[d] = d16[:, : chans // 2]
         other_ref[d] = d16[:, chans // 2 :]
-        return gsb + jnp.sum(dpre, axis=0, keepdims=True)
-
-    gsb = lax.fori_loop(0, half, dpre_row, jnp.zeros((1, chans), F32))
+        return jnp.sum(dpre, axis=0, keepdims=True)
+
+    gsb = lax.fori_loop(0, half // BLOCK, dpre, jnp.zeros((1, chans), F32), unroll=True)
     small_ref[0:1] = gcb
     small_ref[1:2] = jnp.broadcast_to(jnp.sum(loss_ref[...], axis=1, keepdims=True), (1, LANES)) * inverse
     small_ref[2:3] = jnp.zeros((1, LANES), F32)
@@ -276,7 +288,7 @@
             )
             return carry
 
-        lax.fori_loop(0, half, body, 0)
+        lax.fori_loop(0, half, body, 0, unroll=True)
 
     place(own_ref, half * c)
     place(other_ref, half * (1 - c))
@@ -385,32 +397,35 @@
     f = features[0]
     where = jnp.stack([c, t * rows + half * c, jnp.int32(tiles * rows), t, lax.axis_index("batch")]).astype(jnp.int32)
     lab = labels.reshape(rows, 1, labels.shape[2])
-    msg, labt, count, pack = call(
+    msg, labt, count, near = call(
         edge_kernel, "edge", 2,
         [
             ((3 * cols + ANCH_ROWS, chans), BF16),
             ((rows, ANCH_ROWS, cols), BF16),
             ((8, LANES), F32),
-            ((9 * LANES + TRIO, outs), BF16),
+            ((half + 3, cols, chans), BF16),
         ],
-        [where, f, lab, jnp.swapaxes(w_cls, 2, 3), b_shared.reshape(1, outs)],
-        [pltpu.SemaphoreType.DMA((3,))],
-        [SMEM, HBM, VMEM, VMEM, VMEM],
-        52,
+        [where, f, lab],
+        [pltpu.SemaphoreType.DMA((4,))],
+        [SMEM, HBM, VMEM],
+        51,
     )
     pairs = []
     for i in range(tiles - 1):
         pairs += [(2 * i + 1, 2 * i + 2), (2 * i + 2, 2 * i + 1)]
     halo = lax.ppermute(msg, ("tile", "chan"), pairs)
     w1b = swap(w_shared, "chan")
-    packb = swap(pack, "chan")
+    w2b = swap(w_cls, "chan")
+    b1b = swap(b_shared, "chan")
     count = pair_sum([count] + others(count, "batch"))
     counts = [count] + others(count, "tile")
 
-    hid, dz, loss = call(
+    hid, dz, loss, w2 = call(
         head_kernel, "head", 11,
-        [((half + 4, cols, chans), BF16), ((half + 2, cols, LANES), F32), ((1, LANES), F32)],
-        [where, f, halo, labt, w_shared, w1b, pack, packb, b_cls.reshape(1, LOGITS)],
+        [((half + 4, cols, chans), BF16), ((half + 2, cols, LANES), F32), ((1, LANES), F32)]
+        + [((9 * LANES, chans), BF16)],
+        [where, near, halo, labt, w_shared, w1b, b_shared.reshape(1, outs), b1b.reshape(1, outs)]
+        + [jnp.swapaxes(w_cls, 2, 3), jnp.swapaxes(w2b, 2, 3), b_cls.reshape(1, LOGITS)],
         [((half + 6, cols, chans), BF16)],
     )
     dt, own, other, small = call(
@@ -421,7 +436,7 @@
             ((half, cols, outs), BF16),
             ((8, LANES), F32),
         ],
-        [where, hid, dz, loss, pack, packb] + counts,
+        [where, hid, dz, loss, w2] + counts,
         [((half + 2, cols, LANES), BF16)],
     )
     theirs = swap(other, "chan")

time: 85.2 us -> 77.2 us (0.906)
  Pallas kernels: 27.1 us -> 20.7 us
  local copies, waits for them, and re-layouts: 3.61 us -> 2.02 us
    pallas_call x10, Pallas kernels: 27.1 us -> 20.7 us  [call(): pl.pallas_call(kernel, in_specs=specs or [SMEM] + [VMEM] * (len(inputs) -...]
    unnamed x12, local copies, waits for them, and re-layouts: 2.5 us -> 0.92 us
    ppermute x26 -> x27, waiting for transfers between devices: 17.6 us -> 17.7 us  [swap(): return lax.ppermute(x, axis, [(i, i ^ bit) for i in range(size)])]
    ppermute x26 -> x27, starting transfers between devices: 31.7 us -> 31.6 us  [swap(): return lax.ppermute(x, axis, [(i, i ^ bit) for i in range(size)])]
  transfers between devices with their start and end apart: 27 -> 28, of which waited for: 10 -> 10; matrix products, arithmetic and copies ran while one was open for 3% -> 3% of each run, Pallas kernels for 28% -> 23%
where the time goes in v5:
time: 77.2 us; the launch traced here: 77 us
  starting transfers between devices  32.3 us (42%)
  Pallas kernels  20.7 us (27%)
  waiting for transfers between devices  17.7 us (23%)
  between operations  3.24 us (4%)
  local copies, waits for them, and re-layouts  2.02 us (3%)
  other arithmetic  1.03 us (1%)
    ppermute x27, starting transfers between devices, swap(): return lax.ppermute(x, axis, [(i, i ^ bit) for i in range(size)])  31.6 us
    pallas_call x10, Pallas kernels, call(): pl.pallas_call(kernel, in_specs=specs or [SMEM] + [VMEM] * (len(inputs) -...  20.7 us
    ppermute x27, waiting for transfers between devices, swap(): return lax.ppermute(x, axis, [(i, i ^ bit) for i in range(size)])  17.7 us
  transfers between devices with their start and end apart: 28, of which 10 were waited for; matrix products, arithmetic and copies ran while one was open for 3% of the time, Pallas kernels for 23%

profile of v5, /device:TPU:0, one launch (start us, length us, event | category | flops | bytes accessed | tf_op | source)
XLA Modules:
  0.0 77.0 jit_solution(6793172392273635272)
XLA Ops:
  0.6 0.5 collective-permute-start.2
  1.1 0.1 stack.19.where_ref
  1.2 0.9 %copy-done.3 = s32[1,12,2304]{2,0,1:T(1,128)S(1)} copy-done((s32[1,12,2304]{2,0,1:T(1,128)S(1)}, s32[1,12,2304]{2,0,1:T(1,128)}, u32[]{:S(2)}) %copy-start.3) | copy-done | bytes 110616
  2.1 2.6 %edge.1 = (bf16[784,256]{1,0:T(8,128)(2,1)S(1)}, bf16[12,16,256]{2,1,0:T(8,128)(2,1)S(1)}, f32[8,128]{1,0:T(8,128)S(1)}, bf16[9,256,256]{2,1,0:T(8,128)(2,1)S(1)}) custom-call(s32[5]{0:T(128)S(1)} %stack.19.where_ref, bf16[12,256,256]{2,1,0:T(8,128)(2,1)} %bitcast.18, s32[12,1,2304]{2,1,0:T(1,128)S(1)} %bitcast.22), custom_call_target="tpu_custom_call" | custom-call | flops 2000000000 | bytes 2000000 | tf_op jit(solution)/shard_map/edge/pallas_call | solution.py:28
  4.7 0.7 collective-permute-start
  5.4 4.0 %collective-permute-start.4 = (bf16[3,3,128,99]{2,3,1,0:T(8,128)(2,1)S(1)}, bf16[3,3,128,99]{2,3,1,0:T(8,128)(2,1)S(1)}, u32[]{:S(2)}, u32[]{:S(2)}) collective-permute-start(bf16[3,3,128,99]{2,3,1,0:T(8,128)(2,1)S(1)} %copy-done.2), channel_id=1, source_target_pairs={{0,1},{1,0},{2,3},{3,2},{4,5},{5,4},{6,7},{7,6},{8,9},{9,8},{10,11... | collective-permute-start | bytes 684296 | tf_op jit(solution)/shard_map/ppermute | solution.py:378
  9.4 1.5 %collective-permute-start.5 = (f32[8,128]{1,0:T(8,128)S(1)}, f32[8,128]{1,0:T(8,128)S(1)}, u32[]{:S(2)}, u32[]{:S(2)}) collective-permute-start(f32[8,128]{1,0:T(8,128)S(1)} %get-tuple-element.46), channel_id=1, source_target_pairs={{0,2},{2,0},{1,3},{3,1},{4,6},{6,4},{5,7},{7,5},{8,10},{10,8},{9,1... | collective-permute-start | bytes 12296 | tf_op jit(solution)/shard_map/ppermute | solution.py:378
  10.9 0.0 collective-permute-start.3
  10.9 2.1 %collective-permute-done.5 = f32[8,128]{1,0:T(8,128)S(1)} collective-permute-done((f32[8,128]{1,0:T(8,128)S(1)}, f32[8,128]{1,0:T(8,128)S(1)}, u32[]{:S(2)}, u32[]{:S(2)}) %collective-permute-start.5) | collective-permute-done | bytes 4128 | tf_op jit(solution)/shard_map/ppermute | solution.py:378
  13.0 1.6 %collective-permute-start.6 = (f32[8,128]{1,0:T(8,128)S(1)}, f32[8,128]{1,0:T(8,128)S(1)}, u32[]{:S(2)}, u32[]{:S(2)}) collective-permute-start(f32[8,128]{1,0:T(8,128)S(1)} %add.25.rest_0_), channel_id=1, source_target_pairs={{0,4},{4,0},{8,12},{12,8},{1,5},{5,1},{9,13},{13,9},{2,6},{6,2},{1... | collective-permute-start | bytes 12296 | tf_op jit(solution)/shard_map/ppermute | solution.py:378
  14.6 0.0 collective-permute-done.3
  14.6 1.5 %collective-permute-start.7 = (f32[8,128]{1,0:T(8,128)S(1)}, f32[8,128]{1,0:T(8,128)S(1)}, u32[]{:S(2)}, u32[]{:S(2)}) collective-permute-start(f32[8,128]{1,0:T(8,128)S(1)} %add.25.rest_0_), channel_id=1, source_target_pairs={{0,8},{4,12},{8,0},{12,4},{1,9},{5,13},{9,1},{13,5},{2,10},{6,14},... | collective-permute-start | bytes 12296 | tf_op jit(solution)/shard_map/ppermute | solution.py:378
  16.1 1.3 %collective-permute-start.8 = (f32[8,128]{1,0:T(8,128)S(1)}, f32[8,128]{1,0:T(8,128)S(1)}, u32[]{:S(2)}, u32[]{:S(2)}) collective-permute-start(f32[8,128]{1,0:T(8,128)S(1)} %add.25.rest_0_), channel_id=1, source_target_pairs={{0,12},{4,8},{8,4},{12,0},{1,13},{5,9},{9,5},{13,1},{2,14},{6,10},... | collective-permute-start | bytes 12296 | tf_op jit(solution)/shard_map/ppermute | solution.py:378
  17.4 0.0 collective-permute-done.halo_ref
  17.4 0.0 collective-permute-start.1
  17.4 0.0 collective-permute-done.2.w1b_ref
  17.5 6.4 %head.1 = (bf16[10,256,256]{2,1,0:T(8,128)(2,1)S(1)}, f32[8,256,128]{2,1,0:T(8,128)S(1)}, f32[1,128]{1,0:T(1,128)S(1)}, bf16[1152,256]{1,0:T(8,128)(2,1)S(1)}) custom-call(s32[5]{0:T(128)S(1)} %stack.19.where_ref, bf16[9,256,256]{2,1,0:T(8,128)(2,1)S(1)} %get-tuple-element.40.near_ref, bf16[784,256]{1,0:T(8,128)(2,1)S(1)} %collective-permute-done.halo_ref, ...), custom_call_target="tpu_custom_call" | custom-call | flops 11000000512 | bytes 11000000 | tf_op jit(solution)/shard_map/head/pallas_call | solution.py:28
  23.9 0.0 collective-permute-done.6.rest_1_
  23.9 0.0 collective-permute-done.7.rest_2_
  23.9 2.2 %back.1 = (bf16[6,336,256]{2,1,0:T(8,128)(2,1)S(1)}, bf16[6,256,128]{2,1,0:T(8,128)(2,1)S(1)}, bf16[6,256,128]{2,1,0:T(8,128)(2,1)S(1)}, f32[8,128]{1,0:T(8,128)S(1)}) custom-call(s32[5]{0:T(128)S(1)} %stack.19.where_ref, bf16[10,256,256]{2,1,0:T(8,128)(2,1)S(1)} %get-tuple-element.42.hid_ref, f32[8,256,128]{2,1,0:T(8,128)S(1)} %get-tuple-element.43.dz_ref, ...), custom_call_target="tpu_custom_call" | custom-call | flops 4000000000 | bytes 4000000 | tf_op jit(solution)/shard_map/back/pallas_call | solution.py:28
  26.1 0.6 collective-permute-start.9
  26.6 1.5 %cls.1 = (f32[1024,128]{1,0:T(8,128)S(1)}, f32[1024,128]{1,0:T(8,128)S(1)}) custom-call(s32[5]{0:T(128)S(1)} %stack.19.where_ref, bf16[10,256,256]{2,1,0:T(8,128)(2,1)S(1)} %get-tuple-element.42.hid_ref, bf16[6,336,256]{2,1,0:T(8,128)(2,1)S(1)} %get-tuple-element.51.dt_ref), custom_call_target="tpu_custom_call" | custom-call | flops 1500000000 | bytes 1500000 | tf_op jit(solution)/shard_map/cls/pallas_call | solution.py:28
  28.1 0.1 collective-permute-start.10
  28.2 0.0 collective-permute-done.1.far_ref
  28.3 3.8 %shared.1 = (f32[1152,128]{1,0:T(8,128)S(1)}, bf16[1184,128]{1,0:T(8,128)(2,1)S(1)}) custom-call(s32[5]{0:T(128)S(1)} %stack.19.where_ref, bf16[12,256,256]{2,1,0:T(8,128)(2,1)S(1)} %bitcast.19, bf16[784,256]{1,0:T(8,128)(2,1)S(1)} %collective-permute-done.halo_ref, bf16[784,256]{1,0:T(8,128)(2,1)S(1)} %collective-permute-done.1.far_ref, ...), custom_call_target="tpu_custom_call" | custom-call | flops 4000000000 | bytes 4000000 | tf_op jit(solution)/shard_map/shared/pallas_call | solution.py:28
  32.1 1.6 %collective-permute-start.11 = (bf16[1184,128]{1,0:T(8,128)(2,1)S(1)}, bf16[1184,128]{1,0:T(8,128)(2,1)S(1)}, u32[]{:S(2)}, u32[]{:S(2)}) collective-permute-start(bf16[1184,128]{1,0:T(8,128)(2,1)S(1)} %get-tuple-element.55), channel_id=1, source_target_pairs={{0,2},{2,0},{1,3},{3,1},{4,6},{6,4},{5,7},{7,5},{8,10},{10,8},{9,1... | collective-permute-start | bytes 909320 | tf_op jit(solution)/shard_map/ppermute | solution.py:378
  33.7 0.0 collective-permute-done.10.theirs_ref
  33.7 0.6 cls_split.1
  34.3 0.7 collective-permute-start.12
  35.1 2.4 %collective-permute-start.13 = (bf16[256,128]{1,0:T(8,128)(2,1)S(1)}, bf16[256,128]{1,0:T(8,128)(2,1)S(1)}, u32[]{:S(2)}, u32[]{:S(2)}) collective-permute-start(bf16[256,128]{1,0:T(8,128)(2,1)S(1)} %get-tuple-element.57), channel_id=1, source_target_pairs={{0,8},{4,12},{8,0},{12,4},{1,9},{5,13},{9,1},{13,5},{2,10},{6,14},... | collective-permute-start | bytes 196616 | tf_op jit(solution)/shard_map/ppermute | solution.py:378
  37.5 1.3 %collective-permute-start.14 = (bf16[256,128]{1,0:T(8,128)(2,1)S(1)}, bf16[256,128]{1,0:T(8,128)(2,1)S(1)}, u32[]{:S(2)}, u32[]{:S(2)}) collective-permute-start(bf16[256,128]{1,0:T(8,128)(2,1)S(1)} %get-tuple-element.58), channel_id=1, source_target_pairs={{0,12},{4,8},{8,4},{12,0},{1,13},{5,9},{9,5},{13,1},{2,14},{6,10},... | collective-permute-start | bytes 196616 | tf_op jit(solution)/shard_map/ppermute | solution.py:378
  38.8 0.6 collective-permute-done.12.refs_1_
  39.3 3.4 %collective-permute-done.13.refs_2_ = bf16[256,128]{1,0:T(8,128)(2,1)S(1)} collective-permute-done((bf16[256,128]{1,0:T(8,128)(2,1)S(1)}, bf16[256,128]{1,0:T(8,128)(2,1)S(1)}, u32[]{:S(2)}, u32[]{:S(2)}) %collective-permute-start.13) | collective-permute-done | bytes 65568 | tf_op jit(solution)/shard_map/ppermute | solution.py:378
  42.8 0.9 %collective-permute-done.14.refs_3_ = bf16[256,128]{1,0:T(8,128)(2,1)S(1)} collective-permute-done((bf16[256,128]{1,0:T(8,128)(2,1)S(1)}, bf16[256,128]{1,0:T(8,128)(2,1)S(1)}, u32[]{:S(2)}, u32[]{:S(2)}) %collective-permute-start.14) | collective-permute-done | bytes 65568 | tf_op jit(solution)/shard_map/ppermute | solution.py:378
  43.6 0.7 sum.1
  44.3 1.3 %collective-permute-start.15 = (bf16[320,128]{1,0:T(8,128)(2,1)S(1)}, bf16[320,128]{1,0:T(8,128)(2,1)S(1)}, u32[]{:S(2)}, u32[]{:S(2)}) collective-permute-start(bf16[320,128]{1,0:T(8,128)(2,1)S(1)} %get-tuple-element.62), channel_id=1, source_target_pairs={{0,4},{4,0},{8,12},{12,8},{1,5},{5,1},{9,13},{13,9},{2,6},{6,2},{1... | collective-permute-start | bytes 245768 | tf_op jit(solution)/shard_map/ppermute | solution.py:378
  45.6 1.6 %collective-permute-start.16 = (bf16[320,128]{1,0:T(8,128)(2,1)S(1)}, bf16[320,128]{1,0:T(8,128)(2,1)S(1)}, u32[]{:S(2)}, u32[]{:S(2)}) collective-permute-start(bf16[320,128]{1,0:T(8,128)(2,1)S(1)} %get-tuple-element.63), channel_id=1, source_target_pairs={{0,8},{4,12},{8,0},{12,4},{1,9},{5,13},{9,1},{13,5},{2,10},{6,14},... | collective-permute-start | bytes 245768 | tf_op jit(solution)/shard_map/ppermute | solution.py:378
  47.2 1.6 %collective-permute-start.17 = (bf16[320,128]{1,0:T(8,128)(2,1)S(1)}, bf16[320,128]{1,0:T(8,128)(2,1)S(1)}, u32[]{:S(2)}, u32[]{:S(2)}) collective-permute-start(bf16[320,128]{1,0:T(8,128)(2,1)S(1)} %get-tuple-element.64), channel_id=1, source_target_pairs={{0,12},{4,8},{8,4},{12,0},{1,13},{5,9},{9,5},{13,1},{2,14},{6,10},... | collective-permute-start | bytes 245768 | tf_op jit(solution)/shard_map/ppermute | solution.py:378
  48.8 0.5 collective-permute-start.18
  49.3 3.4 %collective-permute-done.18.refs_3_ = bf16[128,128]{1,0:T(8,128)(2,1)S(1)} collective-permute-done((bf16[128,128]{1,0:T(8,128)(2,1)S(1)}, bf16[128,128]{1,0:T(8,128)(2,1)S(1)}, u32[]{:S(2)}, u32[]{:S(2)}) %collective-permute-start.18) | collective-permute-done | bytes 32800 | tf_op jit(solution)/shard_map/ppermute | solution.py:378
  52.7 1.5 %collective-permute-done.16.refs_1_ = bf16[320,128]{1,0:T(8,128)(2,1)S(1)} collective-permute-done((bf16[320,128]{1,0:T(8,128)(2,1)S(1)}, bf16[320,128]{1,0:T(8,128)(2,1)S(1)}, u32[]{:S(2)}, u32[]{:S(2)}) %collective-permute-start.16) | collective-permute-done | bytes 81952 | tf_op jit(solution)/shard_map/ppermute | solution.py:378
  54.2 0.0 collective-permute-done.17.refs_2_
  54.2 0.6 round.1
  54.8 1.6 %collective-permute-start.19 = (bf16[288,128]{1,0:T(8,128)(2,1)S(1)}, bf16[288,128]{1,0:T(8,128)(2,1)S(1)}, u32[]{:S(2)}, u32[]{:S(2)}) collective-permute-start(bf16[288,128]{1,0:T(8,128)(2,1)S(1)} %get-tuple-element.66.refs_0_), channel_id=1, source_target_pairs={{0,4},{4,0},{8,12},{12,8},{1,5},{5,1},{9,13},{13,9},{2,6},{6,2},{1... | collective-permute-start | bytes 221192 | tf_op jit(solution)/shard_map/ppermute | solution.py:378
  56.4 0.9 %collective-permute-start.20 = (bf16[288,128]{1,0:T(8,128)(2,1)S(1)}, bf16[288,128]{1,0:T(8,128)(2,1)S(1)}, u32[]{:S(2)}, u32[]{:S(2)}) collective-permute-start(bf16[288,128]{1,0:T(8,128)(2,1)S(1)} %get-tuple-element.66.refs_0_), channel_id=1, source_target_pairs={{0,8},{4,12},{8,0},{12,4},{1,9},{5,13},{9,1},{13,5},{2,10},{6,14},... | collective-permute-start | bytes 221192 | tf_op jit(solution)/shard_map/ppermute | solution.py:378
  57.3 1.9 %collective-permute-start.21 = (bf16[288,128]{1,0:T(8,128)(2,1)S(1)}, bf16[288,128]{1,0:T(8,128)(2,1)S(1)}, u32[]{:S(2)}, u32[]{:S(2)}) collective-permute-start(bf16[288,128]{1,0:T(8,128)(2,1)S(1)} %get-tuple-element.66.refs_0_), channel_id=1, source_target_pairs={{0,12},{4,8},{8,4},{12,0},{1,13},{5,9},{9,5},{13,1},{2,14},{6,10},... | collective-permute-start | bytes 221192 | tf_op jit(solution)/shard_map/ppermute | solution.py:378
  59.3 0.6 collective-permute-start.22
  59.9 0.0 collective-permute-start.27
  59.9 0.5 slice.22
  60.4 2.8 %collective-permute-done.22.refs_5_ = bf16[128,128]{1,0:T(8,128)(2,1)S(1)} collective-permute-done((bf16[128,128]{1,0:T(8,128)(2,1)S(1)}, bf16[128,128]{1,0:T(8,128)(2,1)S(1)}, u32[]{:S(2)}, u32[]{:S(2)}) %collective-permute-start.22) | collective-permute-done | bytes 32800 | tf_op jit(solution)/shard_map/ppermute | solution.py:378
  63.2 1.1 %collective-permute-done.20.refs_2_ = bf16[288,128]{1,0:T(8,128)(2,1)S(1)} collective-permute-done((bf16[288,128]{1,0:T(8,128)(2,1)S(1)}, bf16[288,128]{1,0:T(8,128)(2,1)S(1)}, u32[]{:S(2)}, u32[]{:S(2)}) %collective-permute-start.20) | collective-permute-done | bytes 73760 | tf_op jit(solution)/shard_map/ppermute | solution.py:378
  64.3 0.6 join.1
  64.9 0.1 collective-permute-start.23
  65.0 0.0 collective-permute-done.27
  65.0 0.5 add_bitcast_fusion
  65.5 1.3 %collective-permute-start.24 = (bf16[256,128]{1,0:T(8,128)(2,1)S(1)}, bf16[256,128]{1,0:T(8,128)(2,1)S(1)}, u32[]{:S(2)}, u32[]{:S(2)}) collective-permute-start(bf16[256,128]{1,0:T(8,128)(2,1)S(1)} %get-tuple-element.69.refs_2_), channel_id=1, source_target_pairs={{0,4},{4,0},{8,12},{12,8},{1,5},{5,1},{9,13},{13,9},{2,6},{6,2},{1... | collective-permute-start | bytes 196616 | tf_op jit(solution)/shard_map/ppermute | solution.py:378
  66.9 1.0 %collective-permute-start.25 = (bf16[256,128]{1,0:T(8,128)(2,1)S(1)}, bf16[256,128]{1,0:T(8,128)(2,1)S(1)}, u32[]{:S(2)}, u32[]{:S(2)}) collective-permute-start(bf16[256,128]{1,0:T(8,128)(2,1)S(1)} %get-tuple-element.69.refs_2_), channel_id=1, source_target_pairs={{0,8},{4,12},{8,0},{12,4},{1,9},{5,13},{9,1},{13,5},{2,10},{6,14},... | collective-permute-start | bytes 196616 | tf_op jit(solution)/shard_map/ppermute | solution.py:378
  67.9 2.0 %collective-permute-start.26 = (bf16[256,128]{1,0:T(8,128)(2,1)S(1)}, bf16[256,128]{1,0:T(8,128)(2,1)S(1)}, u32[]{:S(2)}, u32[]{:S(2)}) collective-permute-start(bf16[256,128]{1,0:T(8,128)(2,1)S(1)} %get-tuple-element.69.refs_2_), channel_id=1, source_target_pairs={{0,12},{4,8},{8,4},{12,0},{1,13},{5,9},{9,5},{13,1},{2,14},{6,10},... | collective-permute-start | bytes 196616 | tf_op jit(solution)/shard_map/ppermute | solution.py:378
  69.9 0.5 add_bitcast_fusion.1
  70.4 0.5 slice.23
  72.2 0.0 collective-permute-done.24.refs_3_
  72.2 0.7 collective-permute-done.25.refs_4_
  73.0 1.1 %collective-permute-done.26.refs_5_ = bf16[256,128]{1,0:T(8,128)(2,1)S(1)} collective-permute-done((bf16[256,128]{1,0:T(8,128)(2,1)S(1)}, bf16[256,128]{1,0:T(8,128)(2,1)S(1)}, u32[]{:S(2)}, u32[]{:S(2)}) %collective-permute-start.26) | collective-permute-done | bytes 65568 | tf_op jit(solution)/shard_map/ppermute | solution.py:378
  74.1 1.8 %out.1 = (f32[2304,128]{1,0:T(8,128)}, f32[3,3,99,128]{3,2,1,0:T(8,128)}) custom-call(s32[5]{0:T(128)S(1)} %stack.19.where_ref, bf16[1152,128]{1,0:T(8,128)(2,1)S(1)} %get-tuple-element.68.refs_0_, bf16[1152,128]{1,0:T(8,128)(2,1)S(1)} %collective-permute-done.23.refs_1_, bf16[256,128]{1,0:T(8,128)(2,1)S(1)} %get-tuple-element.69.refs_2_, ...), custom_call_target="tpu_custom_call" | custom-call | flops 1500000000 | bytes 1500000 | tf_op jit(solution)/shard_map/out/pallas_call | solution.py:28
  (20 shorter events, 0.0 us)
Async XLA Ops:
  0.6 16.8 %collective-permute-start.2 = (bf16[3,3,256,128]{3,2,1,0:T(8,128)(2,1)}, bf16[3,3,256,128]{3,2,1,0:T(8,128)(2,1)S(1)}, u32[]{:S(2)}, u32[]{:S(2)}) collective-permute-start(bf16[3,3,256,128]{3,2,1,0:T(8,128)(2,1)} %w1a_ref.1), channel_id=1, source_target_pairs={{0,1},{1,0},{2,3},{3,2},{4,5},{5,4},{6,7},{7,6},{8,9},{9,8},{10,11... | collective-permute-start | bytes 1769480 | tf_op jit(solution)/shard_map/ppermute | solution.py:378
  1.2 0.9 %copy-start.3 = (s32[1,12,2304]{2,0,1:T(1,128)S(1)}, s32[1,12,2304]{2,0,1:T(1,128)}, u32[]{:S(2)}) copy-start(s32[1,12,2304]{2,0,1:T(1,128)} %param.7) | copy-start | bytes 331780
  2.1 3.3 %copy-start.2 = (bf16[3,3,128,99]{2,3,1,0:T(8,128)(2,1)S(1)}, bf16[3,3,128,99]{2,3,1,0:T(8,128)(2,1)}, u32[]{:S(2)}) copy-start(bf16[3,3,128,99]{2,3,1,0:T(8,128)(2,1)} %param.10) | copy-start | bytes 684292
  2.1 8.8 %copy-start.4 = (f32[128]{0:T(128)S(1)}, f32[128]{0:T(128)}, u32[]{:S(2)}) copy-start(f32[128]{0:T(128)} %param.9) | copy-start | bytes 1540
  2.1 15.3 %copy-start.1 = (bf16[3,3,256,128]{3,2,1,0:T(8,128)(2,1)S(1)}, bf16[3,3,256,128]{3,2,1,0:T(8,128)(2,1)}, u32[]{:S(2)}) copy-start(bf16[3,3,256,128]{3,2,1,0:T(8,128)(2,1)} %w1a_ref.1) | copy-start | bytes 1769476
  2.1 15.3 %copy-start.5 = (f32[99]{0:T(128)S(1)}, f32[99]{0:T(128)}, u32[]{:S(2)}) copy-start(f32[99]{0:T(128)} %param.11) | copy-start | bytes 1192
  4.7 12.7 %collective-permute-start = (bf16[784,256]{1,0:T(8,128)(2,1)S(1)}, bf16[784,256]{1,0:T(8,128)(2,1)S(1)}, u32[]{:S(2)}, u32[]{:S(2)}) collective-permute-start(bf16[784,256]{1,0:T(8,128)(2,1)S(1)} %get-tuple-element.39), channel_id=1, source_target_pairs={{1,4},{4,1},{5,8},{8,5},{9,12},{12,9},{3,6},{6,3},{7,10},{10,7},{1... | collective-permute-start | bytes 1204232 | tf_op jit(solution)/shard_map/ppermute | solution.py:416
  5.4 10.7 %collective-permute-start.4 = (bf16[3,3,128,99]{2,3,1,0:T(8,128)(2,1)S(1)}, bf16[3,3,128,99]{2,3,1,0:T(8,128)(2,1)S(1)}, u32[]{:S(2)}, u32[]{:S(2)}) collective-permute-start(bf16[3,3,128,99]{2,3,1,0:T(8,128)(2,1)S(1)} %copy-done.2), channel_id=1, source_target_pairs={{0,1},{1,0},{2,3},{3,2},{4,5},{5,4},{6,7},{7,6},{8,9},{9,8},{10,11... | collective-permute-start | bytes 684296 | tf_op jit(solution)/shard_map/ppermute | solution.py:378
  9.4 3.6 %collective-permute-start.5 = (f32[8,128]{1,0:T(8,128)S(1)}, f32[8,128]{1,0:T(8,128)S(1)}, u32[]{:S(2)}, u32[]{:S(2)}) collective-permute-start(f32[8,128]{1,0:T(8,128)S(1)} %get-tuple-element.46), channel_id=1, source_target_pairs={{0,2},{2,0},{1,3},{3,1},{4,6},{6,4},{5,7},{7,5},{8,10},{10,8},{9,1... | collective-permute-start | bytes 12296 | tf_op jit(solution)/shard_map/ppermute | solution.py:378
  10.9 3.7 %collective-permute-start.3 = (f32[128]{0:T(128)S(1)}, f32[128]{0:T(128)S(1)}, u32[]{:S(2)}, u32[]{:S(2)}) collective-permute-start(f32[128]{0:T(128)S(1)} %copy-done.4), channel_id=1, source_target_pairs={{0,1},{1,0},{2,3},{3,2},{4,5},{5,4},{6,7},{7,6},{8,9},{9,8},{10,11... | collective-permute-start | bytes 1544 | tf_op jit(solution)/shard_map/ppermute | solution.py:378
  13.0 10.8 %collective-permute-start.6 = (f32[8,128]{1,0:T(8,128)S(1)}, f32[8,128]{1,0:T(8,128)S(1)}, u32[]{:S(2)}, u32[]{:S(2)}) collective-permute-start(f32[8,128]{1,0:T(8,128)S(1)} %add.25.rest_0_), channel_id=1, source_target_pairs={{0,4},{4,0},{8,12},{12,8},{1,5},{5,1},{9,13},{13,9},{2,6},{6,2},{1... | collective-permute-start | bytes 12296 | tf_op jit(solution)/shard_map/ppermute | solution.py:378
  14.6 9.3 %collective-permute-start.7 = (f32[8,128]{1,0:T(8,128)S(1)}, f32[8,128]{1,0:T(8,128)S(1)}, u32[]{:S(2)}, u32[]{:S(2)}) collective-permute-start(f32[8,128]{1,0:T(8,128)S(1)} %add.25.rest_0_), channel_id=1, source_target_pairs={{0,8},{4,12},{8,0},{12,4},{1,9},{5,13},{9,1},{13,5},{2,10},{6,14},... | collective-permute-start | bytes 12296 | tf_op jit(solution)/shard_map/ppermute | solution.py:378
  16.1 7.8 %collective-permute-start.8 = (f32[8,128]{1,0:T(8,128)S(1)}, f32[8,128]{1,0:T(8,128)S(1)}, u32[]{:S(2)}, u32[]{:S(2)}) collective-permute-start(f32[8,128]{1,0:T(8,128)S(1)} %add.25.rest_0_), channel_id=1, source_target_pairs={{0,12},{4,8},{8,4},{12,0},{1,13},{5,9},{9,5},{13,1},{2,14},{6,10},... | collective-permute-start | bytes 12296 | tf_op jit(solution)/shard_map/ppermute | solution.py:378
  17.4 10.8 %collective-permute-start.1 = (bf16[784,256]{1,0:T(8,128)(2,1)S(1)}, bf16[784,256]{1,0:T(8,128)(2,1)S(1)}, u32[]{:S(2)}, u32[]{:S(2)}) collective-permute-start(bf16[784,256]{1,0:T(8,128)(2,1)S(1)} %collective-permute-done.halo_ref), channel_id=1, source_target_pairs={{0,1},{1,0},{2,3},{3,2},{4,5},{5,4},{6,7},{7,6},{8,9},{9,8},{10,11... | collective-permute-start | bytes 1204232 | tf_op jit(solution)/shard_map/ppermute | solution.py:378
  26.1 2.2 %collective-permute-start.9 = (bf16[6,256,128]{2,1,0:T(8,128)(2,1)S(1)}, bf16[6,256,128]{2,1,0:T(8,128)(2,1)S(1)}, u32[]{:S(2)}, u32[]{:S(2)}) collective-permute-start(bf16[6,256,128]{2,1,0:T(8,128)(2,1)S(1)} %get-tuple-element.48), channel_id=1, source_target_pairs={{0,1},{1,0},{2,3},{3,2},{4,5},{5,4},{6,7},{7,6},{8,9},{9,8},{10,11... | collective-permute-start | bytes 1179656 | tf_op jit(solution)/shard_map/ppermute | solution.py:378
  26.6 1.6 %copy-start = (bf16[1,12,256,256]{3,2,1,0:T(8,128)(2,1)S(1)}, bf16[1,12,256,256]{3,2,1,0:T(8,128)(2,1)}, u32[]{:S(2)}) copy-start(bf16[1,12,256,256]{3,2,1,0:T(8,128)(2,1)} %param.6) | copy-start | bytes 4718596
  28.1 5.5 %collective-permute-start.10 = (f32[1024,128]{1,0:T(8,128)S(1)}, f32[1024,128]{1,0:T(8,128)S(1)}, u32[]{:S(2)}, u32[]{:S(2)}) collective-permute-start(f32[1024,128]{1,0:T(8,128)S(1)} %get-tuple-element.53), channel_id=1, source_target_pairs={{0,1},{1,0},{2,3},{3,2},{4,5},{5,4},{6,7},{7,6},{8,9},{9,8},{10,11... | collective-permute-start | bytes 1572872 | tf_op jit(solution)/shard_map/ppermute | solution.py:378
  32.1 11.5 %collective-permute-start.11 = (bf16[1184,128]{1,0:T(8,128)(2,1)S(1)}, bf16[1184,128]{1,0:T(8,128)(2,1)S(1)}, u32[]{:S(2)}, u32[]{:S(2)}) collective-permute-start(bf16[1184,128]{1,0:T(8,128)(2,1)S(1)} %get-tuple-element.55), channel_id=1, source_target_pairs={{0,2},{2,0},{1,3},{3,1},{4,6},{6,4},{5,7},{7,5},{8,10},{10,8},{9,1... | collective-permute-start | bytes 909320 | tf_op jit(solution)/shard_map/ppermute | solution.py:378
  34.3 5.0 %collective-permute-start.12 = (bf16[256,128]{1,0:T(8,128)(2,1)S(1)}, bf16[256,128]{1,0:T(8,128)(2,1)S(1)}, u32[]{:S(2)}, u32[]{:S(2)}) collective-permute-start(bf16[256,128]{1,0:T(8,128)(2,1)S(1)} %get-tuple-element.56), channel_id=1, source_target_pairs={{0,4},{4,0},{8,12},{12,8},{1,5},{5,1},{9,13},{13,9},{2,6},{6,2},{1... | collective-permute-start | bytes 196616 | tf_op jit(solution)/shard_map/ppermute | solution.py:378
  35.1 7.7 %collective-permute-start.13 = (bf16[256,128]{1,0:T(8,128)(2,1)S(1)}, bf16[256,128]{1,0:T(8,128)(2,1)S(1)}, u32[]{:S(2)}, u32[]{:S(2)}) collective-permute-start(bf16[256,128]{1,0:T(8,128)(2,1)S(1)} %get-tuple-element.57), channel_id=1, source_target_pairs={{0,8},{4,12},{8,0},{12,4},{1,9},{5,13},{9,1},{13,5},{2,10},{6,14},... | collective-permute-start | bytes 196616 | tf_op jit(solution)/shard_map/ppermute | solution.py:378
  37.5 6.2 %collective-permute-start.14 = (bf16[256,128]{1,0:T(8,128)(2,1)S(1)}, bf16[256,128]{1,0:T(8,128)(2,1)S(1)}, u32[]{:S(2)}, u32[]{:S(2)}) collective-permute-start(bf16[256,128]{1,0:T(8,128)(2,1)S(1)} %get-tuple-element.58), channel_id=1, source_target_pairs={{0,12},{4,8},{8,4},{12,0},{1,13},{5,9},{9,5},{13,1},{2,14},{6,10},... | collective-permute-start | bytes 196616 | tf_op jit(solution)/shard_map/ppermute | solution.py:378
  44.3 8.4 %collective-permute-start.15 = (bf16[320,128]{1,0:T(8,128)(2,1)S(1)}, bf16[320,128]{1,0:T(8,128)(2,1)S(1)}, u32[]{:S(2)}, u32[]{:S(2)}) collective-permute-start(bf16[320,128]{1,0:T(8,128)(2,1)S(1)} %get-tuple-element.62), channel_id=1, source_target_pairs={{0,4},{4,0},{8,12},{12,8},{1,5},{5,1},{9,13},{13,9},{2,6},{6,2},{1... | collective-permute-start | bytes 245768 | tf_op jit(solution)/shard_map/ppermute | solution.py:378
  45.6 8.6 %collective-permute-start.16 = (bf16[320,128]{1,0:T(8,128)(2,1)S(1)}, bf16[320,128]{1,0:T(8,128)(2,1)S(1)}, u32[]{:S(2)}, u32[]{:S(2)}) collective-permute-start(bf16[320,128]{1,0:T(8,128)(2,1)S(1)} %get-tuple-element.63), channel_id=1, source_target_pairs={{0,8},{4,12},{8,0},{12,4},{1,9},{5,13},{9,1},{13,5},{2,10},{6,14},... | collective-permute-start | bytes 245768 | tf_op jit(solution)/shard_map/ppermute | solution.py:378
  47.2 7.1 %collective-permute-start.17 = (bf16[320,128]{1,0:T(8,128)(2,1)S(1)}, bf16[320,128]{1,0:T(8,128)(2,1)S(1)}, u32[]{:S(2)}, u32[]{:S(2)}) collective-permute-start(bf16[320,128]{1,0:T(8,128)(2,1)S(1)} %get-tuple-element.64), channel_id=1, source_target_pairs={{0,12},{4,8},{8,4},{12,0},{1,13},{5,9},{9,5},{13,1},{2,14},{6,10},... | collective-permute-start | bytes 245768 | tf_op jit(solution)/shard_map/ppermute | solution.py:378
  48.8 3.9 %collective-permute-start.18 = (bf16[128,128]{1,0:T(8,128)(2,1)S(1)}, bf16[128,128]{1,0:T(8,128)(2,1)S(1)}, u32[]{:S(2)}, u32[]{:S(2)}) collective-permute-start(bf16[128,128]{1,0:T(8,128)(2,1)S(1)} %get-tuple-element.65), channel_id=1, source_target_pairs={{0,2},{2,0},{1,3},{3,1},{4,6},{6,4},{5,7},{7,5},{8,10},{10,8},{9,1... | collective-permute-start | bytes 98312 | tf_op jit(solution)/shard_map/ppermute | solution.py:378
  54.8 8.4 %collective-permute-start.19 = (bf16[288,128]{1,0:T(8,128)(2,1)S(1)}, bf16[288,128]{1,0:T(8,128)(2,1)S(1)}, u32[]{:S(2)}, u32[]{:S(2)}) collective-permute-start(bf16[288,128]{1,0:T(8,128)(2,1)S(1)} %get-tuple-element.66.refs_0_), channel_id=1, source_target_pairs={{0,4},{4,0},{8,12},{12,8},{1,5},{5,1},{9,13},{13,9},{2,6},{6,2},{1... | collective-permute-start | bytes 221192 | tf_op jit(solution)/shard_map/ppermute | solution.py:378
  56.4 7.9 %collective-permute-start.20 = (bf16[288,128]{1,0:T(8,128)(2,1)S(1)}, bf16[288,128]{1,0:T(8,128)(2,1)S(1)}, u32[]{:S(2)}, u32[]{:S(2)}) collective-permute-start(bf16[288,128]{1,0:T(8,128)(2,1)S(1)} %get-tuple-element.66.refs_0_), channel_id=1, source_target_pairs={{0,8},{4,12},{8,0},{12,4},{1,9},{5,13},{9,1},{13,5},{2,10},{6,14},... | collective-permute-start | bytes 221192 | tf_op jit(solution)/shard_map/ppermute | solution.py:378
  57.3 7.0 %collective-permute-start.21 = (bf16[288,128]{1,0:T(8,128)(2,1)S(1)}, bf16[288,128]{1,0:T(8,128)(2,1)S(1)}, u32[]{:S(2)}, u32[]{:S(2)}) collective-permute-start(bf16[288,128]{1,0:T(8,128)(2,1)S(1)} %get-tuple-element.66.refs_0_), channel_id=1, source_target_pairs={{0,12},{4,8},{8,4},{12,0},{1,13},{5,9},{9,5},{13,1},{2,14},{6,10},... | collective-permute-start | bytes 221192 | tf_op jit(solution)/shard_map/ppermute | solution.py:378
  59.3 3.9 %collective-permute-start.22 = (bf16[128,128]{1,0:T(8,128)(2,1)S(1)}, bf16[128,128]{1,0:T(8,128)(2,1)S(1)}, u32[]{:S(2)}, u32[]{:S(2)}) collective-permute-start(bf16[128,128]{1,0:T(8,128)(2,1)S(1)} %get-tuple-element.67.refs_4_), channel_id=1, source_target_pairs={{0,2},{2,0},{1,3},{3,1},{4,6},{6,4},{5,7},{7,5},{8,10},{10,8},{9,1... | collective-permute-start | bytes 98312 | tf_op jit(solution)/shard_map/ppermute | solution.py:378
  59.9 5.1 %collective-permute-start.27 = (f32[8,128]{1,0:T(8,128)S(1)}, f32[8,128]{1,0:T(8,128)S(1)}, u32[]{:S(2)}, u32[]{:S(2)}) collective-permute-start(f32[8,128]{1,0:T(8,128)S(1)} %get-tuple-element.71), channel_id=1, source_target_pairs={{0,1},{1,0},{2,3},{3,2},{4,5},{5,4},{6,7},{7,6},{8,9},{9,8},{10,11... | collective-permute-start | bytes 12296 | tf_op jit(solution)/shard_map/ppermute | solution.py:378
  64.9 9.2 %collective-permute-start.23 = (bf16[1152,128]{1,0:T(8,128)(2,1)S(1)}, bf16[1152,128]{1,0:T(8,128)(2,1)S(1)}, u32[]{:S(2)}, u32[]{:S(2)}) collective-permute-start(bf16[1152,128]{1,0:T(8,128)(2,1)S(1)} %get-tuple-element.68.refs_0_), channel_id=1, source_target_pairs={{0,2},{2,0},{1,3},{3,1},{4,6},{6,4},{5,7},{7,5},{8,10},{10,8},{9,1... | collective-permute-start | bytes 884744 | tf_op jit(solution)/shard_map/ppermute | solution.py:378
  65.5 6.7 %collective-permute-start.24 = (bf16[256,128]{1,0:T(8,128)(2,1)S(1)}, bf16[256,128]{1,0:T(8,128)(2,1)S(1)}, u32[]{:S(2)}, u32[]{:S(2)}) collective-permute-start(bf16[256,128]{1,0:T(8,128)(2,1)S(1)} %get-tuple-element.69.refs_2_), channel_id=1, source_target_pairs={{0,4},{4,0},{8,12},{12,8},{1,5},{5,1},{9,13},{13,9},{2,6},{6,2},{1... | collective-permute-start | bytes 196616 | tf_op jit(solution)/shard_map/ppermute | solution.py:378
  66.9 6.1 %collective-permute-start.25 = (bf16[256,128]{1,0:T(8,128)(2,1)S(1)}, bf16[256,128]{1,0:T(8,128)(2,1)S(1)}, u32[]{:S(2)}, u32[]{:S(2)}) collective-permute-start(bf16[256,128]{1,0:T(8,128)(2,1)S(1)} %get-tuple-element.69.refs_2_), channel_id=1, source_target_pairs={{0,8},{4,12},{8,0},{12,4},{1,9},{5,13},{9,1},{13,5},{2,10},{6,14},... | collective-permute-start | bytes 196616 | tf_op jit(solution)/shard_map/ppermute | solution.py:378
  67.9 6.2 %collective-permute-start.26 = (bf16[256,128]{1,0:T(8,128)(2,1)S(1)}, bf16[256,128]{1,0:T(8,128)(2,1)S(1)}, u32[]{:S(2)}, u32[]{:S(2)}) collective-permute-start(bf16[256,128]{1,0:T(8,128)(2,1)S(1)} %get-tuple-element.69.refs_2_), channel_id=1, source_target_pairs={{0,12},{4,8},{8,4},{12,0},{1,13},{5,9},{9,5},{13,1},{2,14},{6,10},... | collective-permute-start | bytes 196616 | tf_op jit(solution)/shard_map/ppermute | solution.py:378

commit v6 on v5

--- a/solution.py
+++ b/solution.py
@@ -13,7 +13,6 @@
 LANES = 128
 ANCH_ROWS = 16
 CLS_ROWS = 112
-CLS_TOTAL = 1024
 TILE, BATCH = 3, 4
 BLOCK = 2
 TRIO = 32
@@ -250,35 +249,36 @@
     chans = hid_ref.shape[2]
     deep = chans // 2
     dt = jnp.concatenate([dt_ref[d] for d in range(half)], axis=1)
-    size = 3 * CLS_ROWS
     for i in range(3):
         g = dot(dt, hid_ref[i + 1 : i + 1 + half].reshape(half * cols, chans))
-        own_ref[size * i : size * (i + 1)] = g[:, :deep]
-        other_ref[size * i : size * (i + 1)] = g[:, deep:]
-    blank = jnp.zeros((CLS_TOTAL - 3 * size, deep), F32)
-    own_ref[3 * size :] = blank
-    other_ref[3 * size :] = blank
+        for j in range(3):
+            start = LOGITS * (3 * i + j)
+            own_ref[start : start + LOGITS] = g[CLS_ROWS * j : CLS_ROWS * j + LOGITS, :deep]
+            other_ref[start : start + LOGITS] = g[CLS_ROWS * j : CLS_ROWS * j + LOGITS, deep:]
+    blank = jnp.zeros((own_ref.shape[0] - 9 * LOGITS, deep), F32)
+    own_ref[9 * LOGITS :] = blank
+    other_ref[9 * LOGITS :] = blank
 
 
 def split(total, me, keep_ref, send_refs):
     rows = keep_ref.shape[0]
     keep_ref[...] = total[pl.ds(pl.multiple_of(me * rows, 8), rows)]
+    size = len(send_refs) + 1
     for k, ref in enumerate(send_refs):
-        ref[0:rows] = total[pl.ds(pl.multiple_of((me ^ (k + 1)) * rows, 8), rows)].astype(BF16)
+        ref[0:rows] = total[pl.ds(pl.multiple_of((me ^ (size - 1 - k)) * rows, 8), rows)].astype(BF16)
 
 
 def shared_kernel(
     where_ref, f_ref, halo_ref, far_ref, own_ref, other_ref, small_ref, keep_ref, *rest
 ):
-    *send_refs, x_ref, d_ref, g_ref = rest
+    *send_refs, d_ref, g_ref = rest
     rows, cols, chans = f_ref.shape
     half = rows // 2
     c = where_ref[0]
     near = halo_ref[pl.ds(pl.multiple_of(2 * cols * (1 - c), 16), cols)]
     far = far_ref[pl.ds(pl.multiple_of(2 * cols * c, 16), cols)]
-    x_ref[pl.ds((rows + 1) * c, 1)] = near.reshape(1, cols, chans)
-    x_ref[pl.ds((rows + 1) * (1 - c), 1)] = far.reshape(1, cols, chans)
-    x_ref[1 : rows + 1] = f_ref[...]
+    before = jnp.where(c == 0, near, far)
+    after = jnp.where(c == 0, far, near)
 
     def place(ref, start):
         def body(d, carry):
@@ -292,14 +292,25 @@
 
     place(own_ref, half * c)
     place(other_ref, half * (1 - c))
-    rhs = d_ref[...].reshape(rows * cols, d_ref.shape[2])
-    outs = rhs.shape[1] // 3
+    outs = d_ref.shape[2] // 3
+
+    def part(x, first):
+        n = x.shape[0]
+        rhs = d_ref[first : first + n].reshape(n * cols, 3 * outs)
+        return dot(x.reshape(n * cols, chans), rhs, ((0,), (0,)))
+
     for i in range(3):
-        lhs = x_ref[i : i + rows].reshape(rows * cols, chans)
-        g = dot(lhs, rhs, ((0,), (0,)))
+        if i == 0:
+            g = part(f_ref[0 : rows - 1], 1) + part(before[None], 0)
+        elif i == 1:
+            g = part(f_ref[...], 0)
+        else:
+            g = part(f_ref[1:rows], 0) + part(after[None], rows - 1)
         for j in range(3):
             start = (3 * i + j) * chans
             g_ref[start : start + chans] = g[:, j * outs : (j + 1) * outs]
+    if g_ref.shape[0] > 9 * chans:
+        g_ref[9 * chans :] = jnp.zeros((g_ref.shape[0] - 9 * chans, outs), F32)
     split(g_ref, where_ref[BATCH], keep_ref, send_refs)
     for ref in send_refs:
         put_trio(ref, keep_ref.shape[0], small_ref[...])
@@ -356,8 +367,9 @@
 
 def join(me, in_refs, out_ref):
     rows = in_refs[0].shape[0]
+    size = len(in_refs)
     for k, ref in enumerate(in_refs):
-        out_ref[pl.ds(pl.multiple_of((me ^ k) * rows, 8), rows)] = ref[...].astype(out_ref.dtype)
+        out_ref[pl.ds(pl.multiple_of((me ^ ((size - k) % size)) * rows, 8), rows)] = ref[...].astype(out_ref.dtype)
 
 
 def join_kernel(n_in, where_ref, *refs):
@@ -365,12 +377,21 @@
     join(where_ref[BATCH], refs[n_in:-2], refs[-1])
 
 
-def out_kernel(n_in, where_ref, *refs):
-    out_ref, cls_out_ref, whole_ref = refs[-3:]
-    join(where_ref[BATCH], refs[:n_in], out_ref)
-    join(where_ref[TILE], refs[n_in:-3], whole_ref)
+def out_kernel(n_in, n_cls, where_ref, small_ref, theirs_ref, *refs):
+    in_refs, cls_in_refs, refs = refs[:n_in], refs[n_in : n_in + n_cls], refs[n_in + n_cls :]
+    out_ref, bias_ref, cls_out_ref, cls_bias_ref, loss_ref, cls_whole_ref, *whole_ref = refs
+    if whole_ref:
+        join(where_ref[BATCH], in_refs, whole_ref[0])
+        out_ref[...] = whole_ref[0][: out_ref.shape[0]]
+    else:
+        join(where_ref[BATCH], in_refs, out_ref)
+    join(where_ref[TILE], cls_in_refs, cls_whole_ref)
     for tap in range(9):
-        cls_out_ref[tap // 3, tap % 3] = whole_ref[CLS_ROWS * tap : CLS_ROWS * tap + LOGITS]
+        cls_out_ref[tap // 3, tap % 3] = cls_whole_ref[LOGITS * tap : LOGITS * (tap + 1)]
+    bias_ref[...] = small_ref[3:4] + theirs_ref[4:5]
+    both = small_ref[0:2] + theirs_ref[0:2]
+    cls_bias_ref[...] = both[0:1, :LOGITS]
+    loss_ref[...] = both[1:2, :1]
 
 
 def swap(x, axis, bit=1):
@@ -379,11 +400,16 @@
 
 
 def others(x, axis):
-    return [swap(x, axis, bit) for bit in range(1, lax.axis_size(axis))]
+    return exchange([x] * (lax.axis_size(axis) - 1), axis)
 
 
 def exchange(sends, axis):
-    return [swap(x, axis, k + 1) for k, x in enumerate(sends)]
+    size = len(sends) + 1
+    return [swap(x, axis, size - 1 - k) for k, x in enumerate(sends)]
+
+
+def round_up(n, step):
+    return (n + step - 1) // step * step
 
 
 def shards(features, labels, w_shared, b_shared, w_cls, b_cls):
@@ -410,6 +436,7 @@
         [SMEM, HBM, VMEM],
         51,
     )
+    count = pair_sum([count] + others(count, "batch"))
     pairs = []
     for i in range(tiles - 1):
         pairs += [(2 * i + 1, 2 * i + 2), (2 * i + 2, 2 * i + 1)]
@@ -417,7 +444,6 @@
     w1b = swap(w_shared, "chan")
     w2b = swap(w_cls, "chan")
     b1b = swap(b_shared, "chan")
-    count = pair_sum([count] + others(count, "batch"))
     counts = [count] + others(count, "tile")
 
     hid, dz, loss, w2 = call(
@@ -441,25 +467,26 @@
     )
     theirs = swap(other, "chan")
     far = swap(halo, "chan")
+    cls_total = round_up(9 * LOGITS, 16 * pages * tiles)
     gcls, gcls_other = call(
-        cls_kernel, "cls", 1.5, [((CLS_TOTAL, outs), F32)] * 2, [where, hid, dt]
+        cls_kernel, "cls", 1.5, [((cls_total, outs), F32)] * 2, [where, hid, dt]
     )
     gcls_theirs = swap(gcls_other, "chan")
 
-    total = 9 * chans
+    total = round_up(9 * chans, 16 * pages * tiles)
     first, second = total // pages, total // (pages * tiles)
-    cfirst, csecond = CLS_TOTAL // tiles, CLS_TOTAL // (pages * tiles)
+    cfirst, csecond = cls_total // tiles, cls_total // (pages * tiles)
     keep, *sends = call(
         shared_kernel, "shared", 4,
         [((first, outs), F32)] + [((first + TRIO, outs), BF16)] * (pages - 1),
         [where, f, halo, far, own, theirs, small],
-        [((rows + 2, cols, chans), BF16), ((rows, cols, 3 * outs), BF16), ((total, outs), F32)],
+        [((rows, cols, 3 * outs), BF16), ((total, outs), F32)],
     )
     ckeep, *csends = call(
         cls_split_kernel, "cls_split", 0.6,
         [((cfirst, outs), F32)] + [((cfirst, outs), BF16)] * (tiles - 1),
         [where, gcls, gcls_theirs],
-        [((CLS_TOTAL, outs), F32)],
+        [((cls_total, outs), F32)],
     )
     arrived = exchange(sends, "batch")
     carrived = exchange(csends, "tile")
@@ -486,18 +513,18 @@
         [((first, outs), BF16), ((cfirst, outs), BF16)],
         [where, done] + others(done, "tile") + [cdone] + others(cdone, "batch"),
     )
-    grad_shared, grad_cls = call(
-        functools.partial(out_kernel, pages), "out", 1.5,
-        [((total, outs), F32), ((3, 3, LOGITS, outs), F32)],
-        [where, block] + others(block, "batch") + [cblock] + others(cblock, "tile"),
-        [((CLS_TOTAL, outs), F32)],
+    grad_shared, bias, grad_cls, cls_bias, loss = call(
+        functools.partial(out_kernel, pages, tiles), "out", 1.5,
+        [((9 * chans, outs), F32), ((1, outs), F32), ((3, 3, LOGITS, outs), F32), ((1, LOGITS), F32), ((1, 1), F32)],
+        [where, small, small_theirs, block] + others(block, "batch") + [cblock] + others(cblock, "tile"),
+        [((cls_total, outs), F32)] + ([((total, outs), F32)] if total > 9 * chans else []),
     )
     return (
         grad_shared.reshape(3, 3, chans, outs),
-        small[3] + small_theirs[4],
+        bias.reshape(outs),
         jnp.swapaxes(grad_cls, 2, 3),
-        small[0, :LOGITS] + small_theirs[0, :LOGITS],
-        small[1, :1] + small_theirs[1, :1],
+        cls_bias.reshape(LOGITS),
+        loss.reshape(1),
     )
 
 

time: 77.2 us -> 74.7 us (0.968)
  between operations: 3.24 us -> 0.79 us
  waiting for transfers between devices: 17.7 us -> 19.2 us
  other arithmetic: 1.03 us -> 0.01 us
  local copies, waits for them, and re-layouts: 2.02 us -> 1 us
    ppermute x27, waiting for transfers between devices: 17.7 us -> 19.2 us  [swap(): return lax.ppermute(x, axis, [(i, i ^ bit) for i in range(size)])]
    add x2 -> x0, other arithmetic: 1.03 us -> none  [the longest x1 0.51 us: shards(): small[0, :LOGITS] + small_theirs[0, :LOGITS]]
    slice x2 -> x0, local copies, waits for them, and re-layouts: 1.03 us -> none  [the longest x1 0.51 us: shards(): small[1, :1] + small_theirs[1, :1]]
  transfers between devices with their start and end apart: 28 -> 28, of which waited for: 10 -> 11; matrix products, arithmetic and copies ran while one was open for 3% -> 0% of each run, Pallas kernels for 23% -> 23%
where the time goes in v6:
time: 74.7 us; the launch traced here: 74.5 us
  starting transfers between devices  32.8 us (44%)
  Pallas kernels  20.7 us (28%)
  waiting for transfers between devices  19.2 us (26%)
  local copies, waits for them, and re-layouts  1 us (1%)
  between operations  0.79 us (1%)
    ppermute x27, starting transfers between devices, swap(): return lax.ppermute(x, axis, [(i, i ^ bit) for i in range(size)])  32.1 us
    pallas_call x10, Pallas kernels, call(): pl.pallas_call(kernel, in_specs=specs or [SMEM] + [VMEM] * (len(inputs) -...  20.7 us
    ppermute x27, waiting for transfers between devices, swap(): return lax.ppermute(x, axis, [(i, i ^ bit) for i in range(size)])  19.2 us
  transfers between devices with their start and end apart: 28, of which 11 were waited for; matrix products, arithmetic and copies ran while one was open for 0% of the time, Pallas kernels for 23%

profile of v6, /device:TPU:0, one launch (start us, length us, event | category | flops | bytes accessed | tf_op | source)
XLA Modules:
  0.0 74.5 jit_solution(4310941888872231352)
XLA Ops:
  0.6 0.5 collective-permute-start.2
  1.1 0.1 stack.19.where_ref
  1.2 0.9 %copy-done.3 = s32[1,12,2304]{2,0,1:T(1,128)S(1)} copy-done((s32[1,12,2304]{2,0,1:T(1,128)S(1)}, s32[1,12,2304]{2,0,1:T(1,128)}, u32[]{:S(2)}) %copy-start.3) | copy-done | bytes 110616
  2.1 2.6 %edge.1 = (bf16[784,256]{1,0:T(8,128)(2,1)S(1)}, bf16[12,16,256]{2,1,0:T(8,128)(2,1)S(1)}, f32[8,128]{1,0:T(8,128)S(1)}, bf16[9,256,256]{2,1,0:T(8,128)(2,1)S(1)}) custom-call(s32[5]{0:T(128)S(1)} %stack.19.where_ref, bf16[12,256,256]{2,1,0:T(8,128)(2,1)} %bitcast.16, s32[12,1,2304]{2,1,0:T(1,128)S(1)} %bitcast.20), custom_call_target="tpu_custom_call" | custom-call | flops 2000000000 | bytes 2000000 | tf_op jit(solution)/shard_map/edge/pallas_call | solution.py:27
  4.7 0.7 collective-permute-start
  5.4 4.0 %collective-permute-start.4 = (bf16[3,3,128,99]{2,3,1,0:T(8,128)(2,1)S(1)}, bf16[3,3,128,99]{2,3,1,0:T(8,128)(2,1)S(1)}, u32[]{:S(2)}, u32[]{:S(2)}) collective-permute-start(bf16[3,3,128,99]{2,3,1,0:T(8,128)(2,1)S(1)} %copy-done.2), channel_id=1, source_target_pairs={{0,1},{1,0},{2,3},{3,2},{4,5},{5,4},{6,7},{7,6},{8,9},{9,8},{10,11... | collective-permute-start | bytes 684296 | tf_op jit(solution)/shard_map/ppermute | solution.py:399
  9.4 1.5 %collective-permute-start.5 = (f32[8,128]{1,0:T(8,128)S(1)}, f32[8,128]{1,0:T(8,128)S(1)}, u32[]{:S(2)}, u32[]{:S(2)}) collective-permute-start(f32[8,128]{1,0:T(8,128)S(1)} %get-tuple-element.49), channel_id=1, source_target_pairs={{0,2},{2,0},{1,3},{3,1},{4,6},{6,4},{5,7},{7,5},{8,10},{10,8},{9,1... | collective-permute-start | bytes 12296 | tf_op jit(solution)/shard_map/ppermute | solution.py:399
  10.9 0.0 collective-permute-start.3
  10.9 2.1 %collective-permute-done.5 = f32[8,128]{1,0:T(8,128)S(1)} collective-permute-done((f32[8,128]{1,0:T(8,128)S(1)}, f32[8,128]{1,0:T(8,128)S(1)}, u32[]{:S(2)}, u32[]{:S(2)}) %collective-permute-start.5) | collective-permute-done | bytes 4128 | tf_op jit(solution)/shard_map/ppermute | solution.py:399
  13.0 2.5 %collective-permute-start.6 = (f32[8,128]{1,0:T(8,128)S(1)}, f32[8,128]{1,0:T(8,128)S(1)}, u32[]{:S(2)}, u32[]{:S(2)}) collective-permute-start(f32[8,128]{1,0:T(8,128)S(1)} %add.7.rest_0_), channel_id=1, source_target_pairs={{0,12},{4,8},{8,4},{12,0},{1,13},{5,9},{9,5},{13,1},{2,14},{6,10},... | collective-permute-start | bytes 12296 | tf_op jit(solution)/shard_map/ppermute | solution.py:399
  15.6 0.0 collective-permute-done.3
  15.6 0.5 collective-permute-start.7
  16.1 0.0 collective-permute-done.4
  16.1 1.3 %collective-permute-start.8 = (f32[8,128]{1,0:T(8,128)S(1)}, f32[8,128]{1,0:T(8,128)S(1)}, u32[]{:S(2)}, u32[]{:S(2)}) collective-permute-start(f32[8,128]{1,0:T(8,128)S(1)} %add.7.rest_0_), channel_id=1, source_target_pairs={{0,4},{4,0},{8,12},{12,8},{1,5},{5,1},{9,13},{13,9},{2,6},{6,2},{1... | collective-permute-start | bytes 12296 | tf_op jit(solution)/shard_map/ppermute | solution.py:399
  17.4 0.0 collective-permute-done.halo_ref
  17.4 0.0 collective-permute-start.1
  17.4 0.0 collective-permute-done.2.w1b_ref
  17.5 6.4 %head.1 = (bf16[10,256,256]{2,1,0:T(8,128)(2,1)S(1)}, f32[8,256,128]{2,1,0:T(8,128)S(1)}, f32[1,128]{1,0:T(1,128)S(1)}, bf16[1152,256]{1,0:T(8,128)(2,1)S(1)}) custom-call(s32[5]{0:T(128)S(1)} %stack.19.where_ref, bf16[9,256,256]{2,1,0:T(8,128)(2,1)S(1)} %get-tuple-element.43.near_ref, bf16[784,256]{1,0:T(8,128)(2,1)S(1)} %collective-permute-done.halo_ref, ...), custom_call_target="tpu_custom_call" | custom-call | flops 11000000512 | bytes 11000000 | tf_op jit(solution)/shard_map/head/pallas_call | solution.py:27
  23.9 0.0 collective-permute-done.6.rest_1_
  23.9 0.0 collective-permute-done.8.rest_3_
  23.9 2.2 %back.1 = (bf16[6,336,256]{2,1,0:T(8,128)(2,1)S(1)}, bf16[6,256,128]{2,1,0:T(8,128)(2,1)S(1)}, bf16[6,256,128]{2,1,0:T(8,128)(2,1)S(1)}, f32[8,128]{1,0:T(8,128)S(1)}) custom-call(s32[5]{0:T(128)S(1)} %stack.19.where_ref, bf16[10,256,256]{2,1,0:T(8,128)(2,1)S(1)} %get-tuple-element.45.hid_ref, f32[8,256,128]{2,1,0:T(8,128)S(1)} %get-tuple-element.46.dz_ref, ...), custom_call_target="tpu_custom_call" | custom-call | flops 4000000000 | bytes 4000000 | tf_op jit(solution)/shard_map/back/pallas_call | solution.py:27
  26.1 0.6 collective-permute-start.9
  26.7 1.5 %cls.1 = (f32[896,128]{1,0:T(8,128)S(1)}, f32[896,128]{1,0:T(8,128)S(1)}) custom-call(s32[5]{0:T(128)S(1)} %stack.19.where_ref, bf16[10,256,256]{2,1,0:T(8,128)(2,1)S(1)} %get-tuple-element.45.hid_ref, bf16[6,336,256]{2,1,0:T(8,128)(2,1)S(1)} %get-tuple-element.54.dt_ref), custom_call_target="tpu_custom_call" | custom-call | flops 1500000000 | bytes 1500000 | tf_op jit(solution)/shard_map/cls/pallas_call | solution.py:27
  28.2 0.1 collective-permute-start.10
  28.3 0.0 collective-permute-done.1.far_ref
  28.3 0.0 collective-permute-done.9.other_ref
  28.3 3.9 %shared.1 = (f32[1152,128]{1,0:T(8,128)S(1)}, bf16[1184,128]{1,0:T(8,128)(2,1)S(1)}) custom-call(s32[5]{0:T(128)S(1)} %stack.19.where_ref, bf16[12,256,256]{2,1,0:T(8,128)(2,1)S(1)} %bitcast.17, bf16[784,256]{1,0:T(8,128)(2,1)S(1)} %collective-permute-done.halo_ref, bf16[784,256]{1,0:T(8,128)(2,1)S(1)} %collective-permute-done.1.far_ref, ...), custom_call_target="tpu_custom_call" | custom-call | flops 4000000000 | bytes 4000000 | tf_op jit(solution)/shard_map/shared/pallas_call | solution.py:27
  32.1 1.6 %collective-permute-start.11 = (bf16[1184,128]{1,0:T(8,128)(2,1)S(1)}, bf16[1184,128]{1,0:T(8,128)(2,1)S(1)}, u32[]{:S(2)}, u32[]{:S(2)}) collective-permute-start(bf16[1184,128]{1,0:T(8,128)(2,1)S(1)} %get-tuple-element.58), channel_id=1, source_target_pairs={{0,2},{2,0},{1,3},{3,1},{4,6},{6,4},{5,7},{7,5},{8,10},{10,8},{9,1... | collective-permute-start | bytes 909320 | tf_op jit(solution)/shard_map/ppermute | solution.py:399
  33.7 0.0 collective-permute-done.10.theirs_ref
  33.7 0.6 cls_split.1
  34.3 2.6 %collective-permute-start.12 = (bf16[224,128]{1,0:T(8,128)(2,1)S(1)}, bf16[224,128]{1,0:T(8,128)(2,1)S(1)}, u32[]{:S(2)}, u32[]{:S(2)}) collective-permute-start(bf16[224,128]{1,0:T(8,128)(2,1)S(1)} %get-tuple-element.59), channel_id=1, source_target_pairs={{0,12},{4,8},{8,4},{12,0},{1,13},{5,9},{9,5},{13,1},{2,14},{6,10},... | collective-permute-start | bytes 172040 | tf_op jit(solution)/shard_map/ppermute | solution.py:399
  36.9 0.0 collective-permute-start.13
  36.9 1.9 %collective-permute-start.14 = (bf16[224,128]{1,0:T(8,128)(2,1)S(1)}, bf16[224,128]{1,0:T(8,128)(2,1)S(1)}, u32[]{:S(2)}, u32[]{:S(2)}) collective-permute-start(bf16[224,128]{1,0:T(8,128)(2,1)S(1)} %get-tuple-element.61), channel_id=1, source_target_pairs={{0,4},{4,0},{8,12},{12,8},{1,5},{5,1},{9,13},{13,9},{2,6},{6,2},{1... | collective-permute-start | bytes 172040 | tf_op jit(solution)/shard_map/ppermute | solution.py:399
  38.8 2.1 %collective-permute-done.12.refs_1_ = bf16[224,128]{1,0:T(8,128)(2,1)S(1)} collective-permute-done((bf16[224,128]{1,0:T(8,128)(2,1)S(1)}, bf16[224,128]{1,0:T(8,128)(2,1)S(1)}, u32[]{:S(2)}, u32[]{:S(2)}) %collective-permute-start.12) | collective-permute-done | bytes 57376 | tf_op jit(solution)/shard_map/ppermute | solution.py:399
  40.9 1.8 %collective-permute-done.13.refs_2_ = bf16[224,128]{1,0:T(8,128)(2,1)S(1)} collective-permute-done((bf16[224,128]{1,0:T(8,128)(2,1)S(1)}, bf16[224,128]{1,0:T(8,128)(2,1)S(1)}, u32[]{:S(2)}, u32[]{:S(2)}) %collective-permute-start.13) | collective-permute-done | bytes 57376 | tf_op jit(solution)/shard_map/ppermute | solution.py:399
  42.7 0.0 collective-permute-done.14.refs_3_
  42.7 0.0 collective-permute-done.11.refs_0_
  42.7 0.7 sum.1
  43.3 2.6 %collective-permute-start.15 = (bf16[320,128]{1,0:T(8,128)(2,1)S(1)}, bf16[320,128]{1,0:T(8,128)(2,1)S(1)}, u32[]{:S(2)}, u32[]{:S(2)}) collective-permute-start(bf16[320,128]{1,0:T(8,128)(2,1)S(1)} %get-tuple-element.65), channel_id=1, source_target_pairs={{0,12},{4,8},{8,4},{12,0},{1,13},{5,9},{9,5},{13,1},{2,14},{6,10},... | collective-permute-start | bytes 245768 | tf_op jit(solution)/shard_map/ppermute | solution.py:399
  45.9 1.9 %collective-permute-start.17 = (bf16[320,128]{1,0:T(8,128)(2,1)S(1)}, bf16[320,128]{1,0:T(8,128)(2,1)S(1)}, u32[]{:S(2)}, u32[]{:S(2)}) collective-permute-start(bf16[320,128]{1,0:T(8,128)(2,1)S(1)} %get-tuple-element.67), channel_id=1, source_target_pairs={{0,4},{4,0},{8,12},{12,8},{1,5},{5,1},{9,13},{13,9},{2,6},{6,2},{1... | collective-permute-start | bytes 245768 | tf_op jit(solution)/shard_map/ppermute | solution.py:399
  47.8 0.6 collective-permute-start.18
  48.4 3.3 %collective-permute-done.18.refs_3_ = bf16[112,128]{1,0:T(8,128)(2,1)S(1)} collective-permute-done((bf16[112,128]{1,0:T(8,128)(2,1)S(1)}, bf16[112,128]{1,0:T(8,128)(2,1)S(1)}, u32[]{:S(2)}, u32[]{:S(2)}) %collective-permute-start.18) | collective-permute-done | bytes 28704 | tf_op jit(solution)/shard_map/ppermute | solution.py:399
  51.7 0.0 collective-permute-done.15.refs_0_
  51.7 1.6 %collective-permute-done.16.refs_1_ = bf16[320,128]{1,0:T(8,128)(2,1)S(1)} collective-permute-done((bf16[320,128]{1,0:T(8,128)(2,1)S(1)}, bf16[320,128]{1,0:T(8,128)(2,1)S(1)}, u32[]{:S(2)}, u32[]{:S(2)}) %collective-permute-start.16) | collective-permute-done | bytes 81952 | tf_op jit(solution)/shard_map/ppermute | solution.py:399
  53.3 0.0 collective-permute-done.17.refs_2_
  53.3 0.6 round.1
  53.9 2.4 %collective-permute-start.20 = (bf16[288,128]{1,0:T(8,128)(2,1)S(1)}, bf16[288,128]{1,0:T(8,128)(2,1)S(1)}, u32[]{:S(2)}, u32[]{:S(2)}) collective-permute-start(bf16[288,128]{1,0:T(8,128)(2,1)S(1)} %get-tuple-element.70.refs_0_), channel_id=1, source_target_pairs={{0,12},{4,8},{8,4},{12,0},{1,13},{5,9},{9,5},{13,1},{2,14},{6,10},... | collective-permute-start | bytes 221192 | tf_op jit(solution)/shard_map/ppermute | solution.py:399
  56.3 2.1 %collective-permute-start.22 = (bf16[288,128]{1,0:T(8,128)(2,1)S(1)}, bf16[288,128]{1,0:T(8,128)(2,1)S(1)}, u32[]{:S(2)}, u32[]{:S(2)}) collective-permute-start(bf16[288,128]{1,0:T(8,128)(2,1)S(1)} %get-tuple-element.70.refs_0_), channel_id=1, source_target_pairs={{0,4},{4,0},{8,12},{12,8},{1,5},{5,1},{9,13},{13,9},{2,6},{6,2},{1... | collective-permute-start | bytes 221192 | tf_op jit(solution)/shard_map/ppermute | solution.py:399
  58.3 0.5 collective-permute-start.23
  58.9 3.3 %collective-permute-done.23.refs_5_ = bf16[112,128]{1,0:T(8,128)(2,1)S(1)} collective-permute-done((bf16[112,128]{1,0:T(8,128)(2,1)S(1)}, bf16[112,128]{1,0:T(8,128)(2,1)S(1)}, u32[]{:S(2)}, u32[]{:S(2)}) %collective-permute-start.23) | collective-permute-done | bytes 28704 | tf_op jit(solution)/shard_map/ppermute | solution.py:399
  62.2 0.0 collective-permute-done.20.refs_1_
  62.2 0.9 %collective-permute-done.21.refs_2_ = bf16[288,128]{1,0:T(8,128)(2,1)S(1)} collective-permute-done((bf16[288,128]{1,0:T(8,128)(2,1)S(1)}, bf16[288,128]{1,0:T(8,128)(2,1)S(1)}, u32[]{:S(2)}, u32[]{:S(2)}) %collective-permute-start.21) | collective-permute-done | bytes 73760 | tf_op jit(solution)/shard_map/ppermute | solution.py:399
  63.1 0.6 join.1
  63.7 0.6 collective-permute-start.24
  64.3 2.4 %collective-permute-start.25 = (bf16[224,128]{1,0:T(8,128)(2,1)S(1)}, bf16[224,128]{1,0:T(8,128)(2,1)S(1)}, u32[]{:S(2)}, u32[]{:S(2)}) collective-permute-start(bf16[224,128]{1,0:T(8,128)(2,1)S(1)} %get-tuple-element.73.refs_2_), channel_id=1, source_target_pairs={{0,12},{4,8},{8,4},{12,0},{1,13},{5,9},{9,5},{13,1},{2,14},{6,10},... | collective-permute-start | bytes 172040 | tf_op jit(solution)/shard_map/ppermute | solution.py:399
  66.8 0.0 collective-permute-start.26
  66.8 1.9 %collective-permute-start.27 = (bf16[224,128]{1,0:T(8,128)(2,1)S(1)}, bf16[224,128]{1,0:T(8,128)(2,1)S(1)}, u32[]{:S(2)}, u32[]{:S(2)}) collective-permute-start(bf16[224,128]{1,0:T(8,128)(2,1)S(1)} %get-tuple-element.73.refs_2_), channel_id=1, source_target_pairs={{0,4},{4,0},{8,12},{12,8},{1,5},{5,1},{9,13},{13,9},{2,6},{6,2},{1... | collective-permute-start | bytes 172040 | tf_op jit(solution)/shard_map/ppermute | solution.py:399
  68.7 0.0 collective-permute-start.19
  68.7 1.2 %collective-permute-done.19.theirs_ref = f32[8,128]{1,0:T(8,128)S(1)} collective-permute-done((f32[8,128]{1,0:T(8,128)S(1)}, f32[8,128]{1,0:T(8,128)S(1)}, u32[]{:S(2)}, u32[]{:S(2)}) %collective-permute-start.19) | collective-permute-done | bytes 4128 | tf_op jit(solution)/shard_map/ppermute | solution.py:399
  69.9 0.5 collective-permute-done.25.refs_3_
  70.4 1.9 %collective-permute-done.26.refs_4_ = bf16[224,128]{1,0:T(8,128)(2,1)S(1)} collective-permute-done((bf16[224,128]{1,0:T(8,128)(2,1)S(1)}, bf16[224,128]{1,0:T(8,128)(2,1)S(1)}, u32[]{:S(2)}, u32[]{:S(2)}) %collective-permute-start.26) | collective-permute-done | bytes 57376 | tf_op jit(solution)/shard_map/ppermute | solution.py:399
  72.3 0.0 collective-permute-done.27.refs_5_
  72.3 0.4 collective-permute-done.24.refs_1_
  72.7 1.8 %out.1 = (f32[2304,128]{1,0:T(8,128)}, f32[1,128]{1,0:T(1,128)}, f32[3,3,99,128]{3,2,1,0:T(8,128)}, f32[1,99]{1,0:T(1,128)}, f32[1,1]{1,0:T(1,128)}) custom-call(s32[5]{0:T(128)S(1)} %stack.19.where_ref, f32[8,128]{1,0:T(8,128)S(1)} %get-tuple-element.69.small_ref, f32[8,128]{1,0:T(8,128)S(1)} %collective-permute-done.19.theirs_ref, ...), custom_call_target="tpu_custom_call" | custom-call | flops 1500000000 | bytes 1500000 | tf_op jit(solution)/shard_map/out/pallas_call | solution.py:27
  (16 shorter events, 0.0 us)
Async XLA Ops:
  0.6 16.8 %collective-permute-start.2 = (bf16[3,3,256,128]{3,2,1,0:T(8,128)(2,1)}, bf16[3,3,256,128]{3,2,1,0:T(8,128)(2,1)S(1)}, u32[]{:S(2)}, u32[]{:S(2)}) collective-permute-start(bf16[3,3,256,128]{3,2,1,0:T(8,128)(2,1)} %w1a_ref.1), channel_id=1, source_target_pairs={{0,1},{1,0},{2,3},{3,2},{4,5},{5,4},{6,7},{7,6},{8,9},{9,8},{10,11... | collective-permute-start | bytes 1769480 | tf_op jit(solution)/shard_map/ppermute | solution.py:399
  1.2 0.9 %copy-start.3 = (s32[1,12,2304]{2,0,1:T(1,128)S(1)}, s32[1,12,2304]{2,0,1:T(1,128)}, u32[]{:S(2)}) copy-start(s32[1,12,2304]{2,0,1:T(1,128)} %param.7) | copy-start | bytes 331780
  2.1 3.3 %copy-start.2 = (bf16[3,3,128,99]{2,3,1,0:T(8,128)(2,1)S(1)}, bf16[3,3,128,99]{2,3,1,0:T(8,128)(2,1)}, u32[]{:S(2)}) copy-start(bf16[3,3,128,99]{2,3,1,0:T(8,128)(2,1)} %param.10) | copy-start | bytes 684292
  2.1 8.8 %copy-start.4 = (f32[128]{0:T(128)S(1)}, f32[128]{0:T(128)}, u32[]{:S(2)}) copy-start(f32[128]{0:T(128)} %param.9) | copy-start | bytes 1540
  2.1 15.3 %copy-start.1 = (bf16[3,3,256,128]{3,2,1,0:T(8,128)(2,1)S(1)}, bf16[3,3,256,128]{3,2,1,0:T(8,128)(2,1)}, u32[]{:S(2)}) copy-start(bf16[3,3,256,128]{3,2,1,0:T(8,128)(2,1)} %w1a_ref.1) | copy-start | bytes 1769476
  2.1 15.3 %copy-start.5 = (f32[99]{0:T(128)S(1)}, f32[99]{0:T(128)}, u32[]{:S(2)}) copy-start(f32[99]{0:T(128)} %param.11) | copy-start | bytes 1192
  4.7 12.7 %collective-permute-start = (bf16[784,256]{1,0:T(8,128)(2,1)S(1)}, bf16[784,256]{1,0:T(8,128)(2,1)S(1)}, u32[]{:S(2)}, u32[]{:S(2)}) collective-permute-start(bf16[784,256]{1,0:T(8,128)(2,1)S(1)} %get-tuple-element.42), channel_id=1, source_target_pairs={{1,4},{4,1},{5,8},{8,5},{9,12},{12,9},{3,6},{6,3},{7,10},{10,7},{1... | collective-permute-start | bytes 1204232 | tf_op jit(solution)/shard_map/ppermute | solution.py:443
  5.4 10.7 %collective-permute-start.4 = (bf16[3,3,128,99]{2,3,1,0:T(8,128)(2,1)S(1)}, bf16[3,3,128,99]{2,3,1,0:T(8,128)(2,1)S(1)}, u32[]{:S(2)}, u32[]{:S(2)}) collective-permute-start(bf16[3,3,128,99]{2,3,1,0:T(8,128)(2,1)S(1)} %copy-done.2), channel_id=1, source_target_pairs={{0,1},{1,0},{2,3},{3,2},{4,5},{5,4},{6,7},{7,6},{8,9},{9,8},{10,11... | collective-permute-start | bytes 684296 | tf_op jit(solution)/shard_map/ppermute | solution.py:399
  9.4 3.6 %collective-permute-start.5 = (f32[8,128]{1,0:T(8,128)S(1)}, f32[8,128]{1,0:T(8,128)S(1)}, u32[]{:S(2)}, u32[]{:S(2)}) collective-permute-start(f32[8,128]{1,0:T(8,128)S(1)} %get-tuple-element.49), channel_id=1, source_target_pairs={{0,2},{2,0},{1,3},{3,1},{4,6},{6,4},{5,7},{7,5},{8,10},{10,8},{9,1... | collective-permute-start | bytes 12296 | tf_op jit(solution)/shard_map/ppermute | solution.py:399
  10.9 4.6 %collective-permute-start.3 = (f32[128]{0:T(128)S(1)}, f32[128]{0:T(128)S(1)}, u32[]{:S(2)}, u32[]{:S(2)}) collective-permute-start(f32[128]{0:T(128)S(1)} %copy-done.4), channel_id=1, source_target_pairs={{0,1},{1,0},{2,3},{3,2},{4,5},{5,4},{6,7},{7,6},{8,9},{9,8},{10,11... | collective-permute-start | bytes 1544 | tf_op jit(solution)/shard_map/ppermute | solution.py:399
  13.0 10.9 %collective-permute-start.6 = (f32[8,128]{1,0:T(8,128)S(1)}, f32[8,128]{1,0:T(8,128)S(1)}, u32[]{:S(2)}, u32[]{:S(2)}) collective-permute-start(f32[8,128]{1,0:T(8,128)S(1)} %add.7.rest_0_), channel_id=1, source_target_pairs={{0,12},{4,8},{8,4},{12,0},{1,13},{5,9},{9,5},{13,1},{2,14},{6,10},... | collective-permute-start | bytes 12296 | tf_op jit(solution)/shard_map/ppermute | solution.py:399
  15.6 8.3 %collective-permute-start.7 = (f32[8,128]{1,0:T(8,128)S(1)}, f32[8,128]{1,0:T(8,128)S(1)}, u32[]{:S(2)}, u32[]{:S(2)}) collective-permute-start(f32[8,128]{1,0:T(8,128)S(1)} %add.7.rest_0_), channel_id=1, source_target_pairs={{0,8},{4,12},{8,0},{12,4},{1,9},{5,13},{9,1},{13,5},{2,10},{6,14},... | collective-permute-start | bytes 12296 | tf_op jit(solution)/shard_map/ppermute | solution.py:399
  16.1 7.8 %collective-permute-start.8 = (f32[8,128]{1,0:T(8,128)S(1)}, f32[8,128]{1,0:T(8,128)S(1)}, u32[]{:S(2)}, u32[]{:S(2)}) collective-permute-start(f32[8,128]{1,0:T(8,128)S(1)} %add.7.rest_0_), channel_id=1, source_target_pairs={{0,4},{4,0},{8,12},{12,8},{1,5},{5,1},{9,13},{13,9},{2,6},{6,2},{1... | collective-permute-start | bytes 12296 | tf_op jit(solution)/shard_map/ppermute | solution.py:399
  17.4 10.8 %collective-permute-start.1 = (bf16[784,256]{1,0:T(8,128)(2,1)S(1)}, bf16[784,256]{1,0:T(8,128)(2,1)S(1)}, u32[]{:S(2)}, u32[]{:S(2)}) collective-permute-start(bf16[784,256]{1,0:T(8,128)(2,1)S(1)} %collective-permute-done.halo_ref), channel_id=1, source_target_pairs={{0,1},{1,0},{2,3},{3,2},{4,5},{5,4},{6,7},{7,6},{8,9},{9,8},{10,11... | collective-permute-start | bytes 1204232 | tf_op jit(solution)/shard_map/ppermute | solution.py:399
  26.1 2.2 %collective-permute-start.9 = (bf16[6,256,128]{2,1,0:T(8,128)(2,1)S(1)}, bf16[6,256,128]{2,1,0:T(8,128)(2,1)S(1)}, u32[]{:S(2)}, u32[]{:S(2)}) collective-permute-start(bf16[6,256,128]{2,1,0:T(8,128)(2,1)S(1)} %get-tuple-element.51), channel_id=1, source_target_pairs={{0,1},{1,0},{2,3},{3,2},{4,5},{5,4},{6,7},{7,6},{8,9},{9,8},{10,11... | collective-permute-start | bytes 1179656 | tf_op jit(solution)/shard_map/ppermute | solution.py:399
  26.7 1.6 %copy-start = (bf16[1,12,256,256]{3,2,1,0:T(8,128)(2,1)S(1)}, bf16[1,12,256,256]{3,2,1,0:T(8,128)(2,1)}, u32[]{:S(2)}) copy-start(bf16[1,12,256,256]{3,2,1,0:T(8,128)(2,1)} %param.6) | copy-start | bytes 4718596
  28.2 5.5 %collective-permute-start.10 = (f32[896,128]{1,0:T(8,128)S(1)}, f32[896,128]{1,0:T(8,128)S(1)}, u32[]{:S(2)}, u32[]{:S(2)}) collective-permute-start(f32[896,128]{1,0:T(8,128)S(1)} %get-tuple-element.56), channel_id=1, source_target_pairs={{0,1},{1,0},{2,3},{3,2},{4,5},{5,4},{6,7},{7,6},{8,9},{9,8},{10,11... | collective-permute-start | bytes 1376264 | tf_op jit(solution)/shard_map/ppermute | solution.py:399
  32.1 10.5 %collective-permute-start.11 = (bf16[1184,128]{1,0:T(8,128)(2,1)S(1)}, bf16[1184,128]{1,0:T(8,128)(2,1)S(1)}, u32[]{:S(2)}, u32[]{:S(2)}) collective-permute-start(bf16[1184,128]{1,0:T(8,128)(2,1)S(1)} %get-tuple-element.58), channel_id=1, source_target_pairs={{0,2},{2,0},{1,3},{3,1},{4,6},{6,4},{5,7},{7,5},{8,10},{10,8},{9,1... | collective-permute-start | bytes 909320 | tf_op jit(solution)/shard_map/ppermute | solution.py:399
  34.3 6.6 %collective-permute-start.12 = (bf16[224,128]{1,0:T(8,128)(2,1)S(1)}, bf16[224,128]{1,0:T(8,128)(2,1)S(1)}, u32[]{:S(2)}, u32[]{:S(2)}) collective-permute-start(bf16[224,128]{1,0:T(8,128)(2,1)S(1)} %get-tuple-element.59), channel_id=1, source_target_pairs={{0,12},{4,8},{8,4},{12,0},{1,13},{5,9},{9,5},{13,1},{2,14},{6,10},... | collective-permute-start | bytes 172040 | tf_op jit(solution)/shard_map/ppermute | solution.py:399
  36.9 5.7 %collective-permute-start.13 = (bf16[224,128]{1,0:T(8,128)(2,1)S(1)}, bf16[224,128]{1,0:T(8,128)(2,1)S(1)}, u32[]{:S(2)}, u32[]{:S(2)}) collective-permute-start(bf16[224,128]{1,0:T(8,128)(2,1)S(1)} %get-tuple-element.60), channel_id=1, source_target_pairs={{0,8},{4,12},{8,0},{12,4},{1,9},{5,13},{9,1},{13,5},{2,10},{6,14},... | collective-permute-start | bytes 172040 | tf_op jit(solution)/shard_map/ppermute | solution.py:399
  36.9 5.7 %collective-permute-start.14 = (bf16[224,128]{1,0:T(8,128)(2,1)S(1)}, bf16[224,128]{1,0:T(8,128)(2,1)S(1)}, u32[]{:S(2)}, u32[]{:S(2)}) collective-permute-start(bf16[224,128]{1,0:T(8,128)(2,1)S(1)} %get-tuple-element.61), channel_id=1, source_target_pairs={{0,4},{4,0},{8,12},{12,8},{1,5},{5,1},{9,13},{13,9},{2,6},{6,2},{1... | collective-permute-start | bytes 172040 | tf_op jit(solution)/shard_map/ppermute | solution.py:399
  43.3 8.3 %collective-permute-start.15 = (bf16[320,128]{1,0:T(8,128)(2,1)S(1)}, bf16[320,128]{1,0:T(8,128)(2,1)S(1)}, u32[]{:S(2)}, u32[]{:S(2)}) collective-permute-start(bf16[320,128]{1,0:T(8,128)(2,1)S(1)} %get-tuple-element.65), channel_id=1, source_target_pairs={{0,12},{4,8},{8,4},{12,0},{1,13},{5,9},{9,5},{13,1},{2,14},{6,10},... | collective-permute-start | bytes 245768 | tf_op jit(solution)/shard_map/ppermute | solution.py:399
  45.9 7.4 %collective-permute-start.16 = (bf16[320,128]{1,0:T(8,128)(2,1)S(1)}, bf16[320,128]{1,0:T(8,128)(2,1)S(1)}, u32[]{:S(2)}, u32[]{:S(2)}) collective-permute-start(bf16[320,128]{1,0:T(8,128)(2,1)S(1)} %get-tuple-element.66), channel_id=1, source_target_pairs={{0,8},{4,12},{8,0},{12,4},{1,9},{5,13},{9,1},{13,5},{2,10},{6,14},... | collective-permute-start | bytes 245768 | tf_op jit(solution)/shard_map/ppermute | solution.py:399
  45.9 7.4 %collective-permute-start.17 = (bf16[320,128]{1,0:T(8,128)(2,1)S(1)}, bf16[320,128]{1,0:T(8,128)(2,1)S(1)}, u32[]{:S(2)}, u32[]{:S(2)}) collective-permute-start(bf16[320,128]{1,0:T(8,128)(2,1)S(1)} %get-tuple-element.67), channel_id=1, source_target_pairs={{0,4},{4,0},{8,12},{12,8},{1,5},{5,1},{9,13},{13,9},{2,6},{6,2},{1... | collective-permute-start | bytes 245768 | tf_op jit(solution)/shard_map/ppermute | solution.py:399
  47.8 3.9 %collective-permute-start.18 = (bf16[112,128]{1,0:T(8,128)(2,1)S(1)}, bf16[112,128]{1,0:T(8,128)(2,1)S(1)}, u32[]{:S(2)}, u32[]{:S(2)}) collective-permute-start(bf16[112,128]{1,0:T(8,128)(2,1)S(1)} %get-tuple-element.68), channel_id=1, source_target_pairs={{0,2},{2,0},{1,3},{3,1},{4,6},{6,4},{5,7},{7,5},{8,10},{10,8},{9,1... | collective-permute-start | bytes 86024 | tf_op jit(solution)/shard_map/ppermute | solution.py:399
  53.9 8.3 %collective-permute-start.20 = (bf16[288,128]{1,0:T(8,128)(2,1)S(1)}, bf16[288,128]{1,0:T(8,128)(2,1)S(1)}, u32[]{:S(2)}, u32[]{:S(2)}) collective-permute-start(bf16[288,128]{1,0:T(8,128)(2,1)S(1)} %get-tuple-element.70.refs_0_), channel_id=1, source_target_pairs={{0,12},{4,8},{8,4},{12,0},{1,13},{5,9},{9,5},{13,1},{2,14},{6,10},... | collective-permute-start | bytes 221192 | tf_op jit(solution)/shard_map/ppermute | solution.py:399
  56.3 6.9 %collective-permute-start.21 = (bf16[288,128]{1,0:T(8,128)(2,1)S(1)}, bf16[288,128]{1,0:T(8,128)(2,1)S(1)}, u32[]{:S(2)}, u32[]{:S(2)}) collective-permute-start(bf16[288,128]{1,0:T(8,128)(2,1)S(1)} %get-tuple-element.70.refs_0_), channel_id=1, source_target_pairs={{0,8},{4,12},{8,0},{12,4},{1,9},{5,13},{9,1},{13,5},{2,10},{6,14},... | collective-permute-start | bytes 221192 | tf_op jit(solution)/shard_map/ppermute | solution.py:399
  56.3 6.9 %collective-permute-start.22 = (bf16[288,128]{1,0:T(8,128)(2,1)S(1)}, bf16[288,128]{1,0:T(8,128)(2,1)S(1)}, u32[]{:S(2)}, u32[]{:S(2)}) collective-permute-start(bf16[288,128]{1,0:T(8,128)(2,1)S(1)} %get-tuple-element.70.refs_0_), channel_id=1, source_target_pairs={{0,4},{4,0},{8,12},{12,8},{1,5},{5,1},{9,13},{13,9},{2,6},{6,2},{1... | collective-permute-start | bytes 221192 | tf_op jit(solution)/shard_map/ppermute | solution.py:399
  58.3 3.9 %collective-permute-start.23 = (bf16[112,128]{1,0:T(8,128)(2,1)S(1)}, bf16[112,128]{1,0:T(8,128)(2,1)S(1)}, u32[]{:S(2)}, u32[]{:S(2)}) collective-permute-start(bf16[112,128]{1,0:T(8,128)(2,1)S(1)} %get-tuple-element.71.refs_4_), channel_id=1, source_target_pairs={{0,2},{2,0},{1,3},{3,1},{4,6},{6,4},{5,7},{7,5},{8,10},{10,8},{9,1... | collective-permute-start | bytes 86024 | tf_op jit(solution)/shard_map/ppermute | solution.py:399
  63.7 9.0 %collective-permute-start.24 = (bf16[1152,128]{1,0:T(8,128)(2,1)S(1)}, bf16[1152,128]{1,0:T(8,128)(2,1)S(1)}, u32[]{:S(2)}, u32[]{:S(2)}) collective-permute-start(bf16[1152,128]{1,0:T(8,128)(2,1)S(1)} %get-tuple-element.72.refs_0_), channel_id=1, source_target_pairs={{0,2},{2,0},{1,3},{3,1},{4,6},{6,4},{5,7},{7,5},{8,10},{10,8},{9,1... | collective-permute-start | bytes 884744 | tf_op jit(solution)/shard_map/ppermute | solution.py:399
  64.3 6.1 %collective-permute-start.25 = (bf16[224,128]{1,0:T(8,128)(2,1)S(1)}, bf16[224,128]{1,0:T(8,128)(2,1)S(1)}, u32[]{:S(2)}, u32[]{:S(2)}) collective-permute-start(bf16[224,128]{1,0:T(8,128)(2,1)S(1)} %get-tuple-element.73.refs_2_), channel_id=1, source_target_pairs={{0,12},{4,8},{8,4},{12,0},{1,13},{5,9},{9,5},{13,1},{2,14},{6,10},... | collective-permute-start | bytes 172040 | tf_op jit(solution)/shard_map/ppermute | solution.py:399
  66.8 5.5 %collective-permute-start.26 = (bf16[224,128]{1,0:T(8,128)(2,1)S(1)}, bf16[224,128]{1,0:T(8,128)(2,1)S(1)}, u32[]{:S(2)}, u32[]{:S(2)}) collective-permute-start(bf16[224,128]{1,0:T(8,128)(2,1)S(1)} %get-tuple-element.73.refs_2_), channel_id=1, source_target_pairs={{0,8},{4,12},{8,0},{12,4},{1,9},{5,13},{9,1},{13,5},{2,10},{6,14},... | collective-permute-start | bytes 172040 | tf_op jit(solution)/shard_map/ppermute | solution.py:399
  66.8 5.5 %collective-permute-start.27 = (bf16[224,128]{1,0:T(8,128)(2,1)S(1)}, bf16[224,128]{1,0:T(8,128)(2,1)S(1)}, u32[]{:S(2)}, u32[]{:S(2)}) collective-permute-start(bf16[224,128]{1,0:T(8,128)(2,1)S(1)} %get-tuple-element.73.refs_2_), channel_id=1, source_target_pairs={{0,4},{4,0},{8,12},{12,8},{1,5},{5,1},{9,13},{13,9},{2,6},{6,2},{1... | collective-permute-start | bytes 172040 | tf_op jit(solution)/shard_map/ppermute | solution.py:399
  68.7 1.2 %collective-permute-start.19 = (f32[8,128]{1,0:T(8,128)S(1)}, f32[8,128]{1,0:T(8,128)S(1)}, u32[]{:S(2)}, u32[]{:S(2)}) collective-permute-start(f32[8,128]{1,0:T(8,128)S(1)} %get-tuple-element.69.small_ref), channel_id=1, source_target_pairs={{0,1},{1,0},{2,3},{3,2},{4,5},{5,4},{6,7},{7,6},{8,9},{9,8},{10,11... | collective-permute-start | bytes 12296 | tf_op jit(solution)/shard_map/ppermute | solution.py:399

commit v7 on v6

--- a/solution.py
+++ b/solution.py
@@ -103,48 +103,57 @@
         copy.wait()
 
 
-def head_kernel(
-    where_ref, near_ref, halo_ref, labt_ref, w1a_ref, w1b_ref, b1a_ref, b1b_ref, w2a_ref, w2b_ref, b2_ref,
-    hid_ref, dz_ref, loss_ref, w2_ref, xw_ref,
-):
-
-    near = near_ref.shape[0]
-    half = near - 3
-    cols = near_ref.shape[1]
-    c = where_ref[0]
-    first = where_ref[1]
-    total = where_ref[2]
-    xw_ref[pl.ds(3 - 3 * c, near)] = near_ref[...]
-    for k in range(3):
-        xw_ref[near * c + k] = halo_ref[cols * k : cols * (k + 1)]
+def hidden_rows(x, w1a_ref, w1b_ref, b1a_ref, b1b_ref):
     w1 = [
         jnp.concatenate(
-            [jnp.concatenate([w1a_ref[i, j], w1b_ref[i, j]], axis=1) for j in range(3)], axis=1
+            [part for j in range(3) for part in (w1a_ref[i, j], w1b_ref[i, j])], axis=1
         )
         for i in range(3)
     ]
     w1 = jnp.concatenate(w1, axis=0)
-    chans = w1.shape[1] // 3
+    b1 = jnp.concatenate([b1a_ref[...], b1b_ref[...]], axis=1)
+    n = x.shape[0] - 2
+    cols, chans = x.shape[1:]
+    width = w1.shape[1] // 3
+    for start in range(0, n, 4):
+        count = min(4, n - start)
+        parts = [x[start + r : start + r + count].reshape(count * cols, chans) for r in range(3)]
+        many = dot(jnp.concatenate(parts, axis=1), w1)
+        for k in range(count):
+            y = many[k * cols : (k + 1) * cols]
+            yield shift_cells(y[:, :width], 1) + y[:, width : 2 * width] + shift_cells(y[:, 2 * width :], -1) + b1
+
+
+def inner_kernel(where_ref, near_ref, w1a_ref, w1b_ref, b1a_ref, b1b_ref, out_ref):
+    for k, pre in enumerate(hidden_rows(near_ref, w1a_ref, w1b_ref, b1a_ref, b1b_ref)):
+        out_ref[k] = jnp.maximum(pre, 0.0).astype(BF16)
+
+
+def head_kernel(
+    where_ref, near_ref, inner_ref, halo_ref, labt_ref, w1a_ref, w1b_ref, b1a_ref, b1b_ref, w2a_ref, w2b_ref, b2_ref,
+    hid_ref, dz_ref, loss_ref, w2_ref, xw_ref,
+):
+    near = near_ref.shape[0]
+    half = near - 3
+    cols, chans = near_ref.shape[1:]
+    c = where_ref[0]
+    first = where_ref[1]
+    total = where_ref[2]
+    xw_ref[pl.ds(3 - 3 * c, 2)] = near_ref[pl.ds((near - 2) * c, 2)]
+    for k in range(3):
+        xw_ref[2 * c + k] = halo_ref[cols * k : cols * (k + 1)]
+    hid_ref[pl.ds(3 - 3 * c, near - 2)] = inner_ref[...]
+    for k, pre in enumerate(hidden_rows(xw_ref, w1a_ref, w1b_ref, b1a_ref, b1b_ref)):
+        h = (near - 2) * c + k
+        row = first + h - 2
+        inside = jnp.logical_and(row >= 0, row < total)
+        hid_ref[h] = jnp.where(inside, jnp.maximum(pre, 0.0), 0.0).astype(BF16)
     deep = chans // 2
-    b1 = jnp.concatenate([b1a_ref[...], b1b_ref[...]], axis=1)
     for tap in range(9):
         end = LANES * tap + LANES
         w2_ref[end - 32 : end] = jnp.zeros((32, chans), BF16)
         w2_ref[end - LANES : end - LANES + LOGITS, :deep] = w2a_ref[tap // 3, tap % 3]
         w2_ref[end - LANES : end - LANES + LOGITS, deep:] = w2b_ref[tap // 3, tap % 3]
-
-    def conv1(g, carry):
-        pair = dot(taken(xw_ref, BLOCK * g, (0, 1, 2)), w1)
-        for k in range(BLOCK):
-            h = BLOCK * g + k
-            y = pair[k * cols : (k + 1) * cols]
-            pre = shift_cells(y[:, :chans], 1) + y[:, chans : 2 * chans] + shift_cells(y[:, 2 * chans :], -1) + b1
-            row = first + h - 2
-            inside = jnp.logical_and(row >= 0, row < total)
-            hid_ref[h] = jnp.where(inside, jnp.maximum(pre, 0.0), 0.0).astype(BF16)
-        return carry
-
-    lax.fori_loop(0, (half + 4) // BLOCK, conv1, 0, unroll=True)
 
     lane = lax.broadcasted_iota(jnp.int32, (1, LANES), 1)
     kind = (lane % CLASSES + 1).astype(F32)
@@ -269,7 +278,7 @@
 
 
 def shared_kernel(
-    where_ref, f_ref, halo_ref, far_ref, own_ref, other_ref, small_ref, keep_ref, *rest
+    where_ref, f_ref, halo_ref, far_ref, own_ref, other_ref, keep_ref, *rest
 ):
     *send_refs, d_ref, g_ref = rest
     rows, cols, chans = f_ref.shape
@@ -312,20 +321,32 @@
     if g_ref.shape[0] > 9 * chans:
         g_ref[9 * chans :] = jnp.zeros((g_ref.shape[0] - 9 * chans, outs), F32)
     split(g_ref, where_ref[BATCH], keep_ref, send_refs)
-    for ref in send_refs:
-        put_trio(ref, keep_ref.shape[0], small_ref[...])
-
-
-def cls_split_kernel(where_ref, cls_ref, theirs_ref, keep_ref, *rest):
+
+
+def cls_split_kernel(where_ref, cls_ref, theirs_ref, small_ref, keep_ref, *rest):
     *send_refs, total_ref = rest
     total_ref[...] = cls_ref[...] + theirs_ref[...]
     split(total_ref, where_ref[TILE], keep_ref, send_refs)
+    for ref in send_refs:
+        put_trio(ref, keep_ref.shape[0], small_ref[...])
 
 
 def pair_sum(parts):
     while len(parts) > 1:
         parts = [parts[k] + parts[k + 1] for k in range(0, len(parts), 2)]
     return parts[0]
+
+
+def total_of(base_ref, in_refs):
+    rows = base_ref.shape[0]
+    total = base_ref[...]
+    for ref in in_refs:
+        total = total + ref[0:rows].astype(F32)
+    return total
+
+
+def small_sum(small_ref, in_refs, start):
+    return pair_sum([small_ref[...]] + [get_trio(ref, start) for ref in in_refs])
 
 
 def sum_kernel(n_in, n_cls, n_send, where_ref, base_ref, small_ref, cls_ref, *refs):
@@ -333,36 +354,22 @@
     cls_in_refs, refs = refs[:n_cls], refs[n_cls:]
     keep_ref, sum_ref, *refs, total_ref, cls_total_ref = refs
     send_refs, cls_keep_ref, cls_send_refs = refs[:n_send], refs[n_send], refs[n_send + 1 :]
-    rows = base_ref.shape[0]
-    total = base_ref[...]
-    for ref in in_refs:
-        total = total + ref[0:rows].astype(F32)
-    total_ref[...] = total
+    total_ref[...] = total_of(base_ref, in_refs)
     split(total_ref, where_ref[TILE], keep_ref, send_refs)
-    sums = pair_sum([small_ref[...]] + [get_trio(ref, rows) for ref in in_refs])
+    cls_total_ref[...] = total_of(cls_ref, cls_in_refs)
+    split(cls_total_ref, where_ref[BATCH], cls_keep_ref, cls_send_refs)
+    sums = small_sum(small_ref, cls_in_refs, cls_ref.shape[0])
     sum_ref[...] = sums
-    for ref in send_refs:
-        put_trio(ref, keep_ref.shape[0], sums)
-    total = cls_ref[...]
-    for ref in cls_in_refs:
-        total = total + ref[...].astype(F32)
-    cls_total_ref[...] = total
-    split(cls_total_ref, where_ref[BATCH], cls_keep_ref, cls_send_refs)
+    for ref in cls_send_refs:
+        put_trio(ref, cls_keep_ref.shape[0], sums)
 
 
 def round_kernel(n_in, where_ref, base_ref, small_ref, cls_ref, *refs):
     in_refs, cls_in_refs = refs[:n_in], refs[n_in:-3]
     out_ref, sum_ref, cls_out_ref = refs[-3:]
-    rows = base_ref.shape[0]
-    total = base_ref[...]
-    for ref in in_refs:
-        total = total + ref[0:rows].astype(F32)
-    out_ref[...] = total.astype(BF16)
-    sum_ref[...] = pair_sum([small_ref[...]] + [get_trio(ref, rows) for ref in in_refs])
-    total = cls_ref[...]
-    for ref in cls_in_refs:
-        total = total + ref[...].astype(F32)
-    cls_out_ref[...] = total.astype(BF16)
+    out_ref[...] = total_of(base_ref, in_refs).astype(BF16)
+    cls_out_ref[...] = total_of(cls_ref, cls_in_refs).astype(BF16)
+    sum_ref[...] = small_sum(small_ref, cls_in_refs, cls_ref.shape[0])
 
 
 def join(me, in_refs, out_ref):
@@ -436,7 +443,7 @@
         [SMEM, HBM, VMEM],
         51,
     )
-    count = pair_sum([count] + others(count, "batch"))
+    met = others(count, "batch")
     pairs = []
     for i in range(tiles - 1):
         pairs += [(2 * i + 1, 2 * i + 2), (2 * i + 2, 2 * i + 1)]
@@ -444,15 +451,20 @@
     w1b = swap(w_shared, "chan")
     w2b = swap(w_cls, "chan")
     b1b = swap(b_shared, "chan")
+
+    weights = [w_shared, w1b, b_shared.reshape(1, outs), b1b.reshape(1, outs)]
+    (inner,) = call(inner_kernel, "inner", 3, [((half + 1, cols, chans), BF16)], [where, near] + weights)
+    inner, halo, *met = lax.optimization_barrier((inner, halo, *met))
+    count = pair_sum([count] + met)
     counts = [count] + others(count, "tile")
-
     hid, dz, loss, w2 = call(
-        head_kernel, "head", 11,
+        head_kernel, "head", 5,
         [((half + 4, cols, chans), BF16), ((half + 2, cols, LANES), F32), ((1, LANES), F32)]
         + [((9 * LANES, chans), BF16)],
-        [where, near, halo, labt, w_shared, w1b, b_shared.reshape(1, outs), b1b.reshape(1, outs)]
+        [where, near, inner, halo, labt]
+        + weights
         + [jnp.swapaxes(w_cls, 2, 3), jnp.swapaxes(w2b, 2, 3), b_cls.reshape(1, LOGITS)],
-        [((half + 6, cols, chans), BF16)],
+        [((5, cols, chans), BF16)],
     )
     dt, own, other, small = call(
         back_kernel, "back", 4,
@@ -478,14 +490,14 @@
     cfirst, csecond = cls_total // tiles, cls_total // (pages * tiles)
     keep, *sends = call(
         shared_kernel, "shared", 4,
-        [((first, outs), F32)] + [((first + TRIO, outs), BF16)] * (pages - 1),
-        [where, f, halo, far, own, theirs, small],
+        [((first, outs), F32)] + [((first, outs), BF16)] * (pages - 1),
+        [where, f, halo, far, own, theirs],
         [((rows, cols, 3 * outs), BF16), ((total, outs), F32)],
     )
     ckeep, *csends = call(
         cls_split_kernel, "cls_split", 0.6,
-        [((cfirst, outs), F32)] + [((cfirst, outs), BF16)] * (tiles - 1),
-        [where, gcls, gcls_theirs],
+        [((cfirst, outs), F32)] + [((cfirst + TRIO, outs), BF16)] * (tiles - 1),
+        [where, gcls, gcls_theirs, small],
         [((cls_total, outs), F32)],
     )
     arrived = exchange(sends, "batch")
@@ -493,9 +505,9 @@
     keep, small, *sends = call(
         functools.partial(sum_kernel, pages - 1, tiles - 1, tiles - 1), "sum", 0.7,
         [((second, outs), F32), ((8, LANES), F32)]
-        + [((second + TRIO, outs), BF16)] * (tiles - 1)
+        + [((second, outs), BF16)] * (tiles - 1)
         + [((csecond, outs), F32)]
-        + [((csecond, outs), BF16)] * (pages - 1),
+        + [((csecond + TRIO, outs), BF16)] * (pages - 1),
         [where, keep, small, ckeep] + arrived + carrived,
         [((first, outs), F32), ((cfirst, outs), F32)],
     )

time: 74.7 us -> 75.6 us (1.012)
  waiting for transfers between devices: 19.2 us -> 17.2 us
  starting transfers between devices: 32.8 us -> 34.3 us
  Pallas kernels: 20.7 us -> 22 us
    ppermute x27, waiting for transfers between devices: 19.2 us -> 17.2 us  [swap(): return lax.ppermute(x, axis, [(i, i ^ bit) for i in range(size)])]
    ppermute x27, starting transfers between devices: 32.1 us -> 33.6 us  [swap(): return lax.ppermute(x, axis, [(i, i ^ bit) for i in range(size)])]
    pallas_call x10 -> x11, Pallas kernels: 20.7 us -> 22 us  [call(): pl.pallas_call(kernel, in_specs=specs or [SMEM] + [VMEM] * (len(inputs) -...]
  transfers between devices with their start and end apart: 28 -> 28, of which waited for: 11 -> 11; matrix products, arithmetic and copies ran while one was open for 0% -> 0% of each run, Pallas kernels for 23% -> 24%
where the time goes in v7:
time: 75.6 us; the launch traced here: 75.4 us
  starting transfers between devices  34.3 us (45%)
  Pallas kernels  22 us (29%)
  waiting for transfers between devices  17.2 us (23%)
  local copies, waits for them, and re-layouts  1 us (1%)
  between operations  0.82 us (1%)
    ppermute x27, starting transfers between devices, swap(): return lax.ppermute(x, axis, [(i, i ^ bit) for i in range(size)])  33.6 us
    pallas_call x11, Pallas kernels, call(): pl.pallas_call(kernel, in_specs=specs or [SMEM] + [VMEM] * (len(inputs) -...  22 us
    ppermute x27, waiting for transfers between devices, swap(): return lax.ppermute(x, axis, [(i, i ^ bit) for i in range(size)])  17.2 us
  transfers between devices with their start and end apart: 28, of which 11 were waited for; matrix products, arithmetic and copies ran while one was open for 0% of the time, Pallas kernels for 24%

profile of v7, /device:TPU:0, one launch (start us, length us, event | category | flops | bytes accessed | tf_op | source)
XLA Modules:
  0.0 75.4 jit_solution(16957658263055301738)
XLA Ops:
  0.6 0.5 collective-permute-start
  1.1 0.1 stack.19.where_ref
  1.2 0.9 %copy-done.3 = s32[1,12,2304]{2,0,1:T(1,128)S(1)} copy-done((s32[1,12,2304]{2,0,1:T(1,128)S(1)}, s32[1,12,2304]{2,0,1:T(1,128)}, u32[]{:S(2)}) %copy-start.3) | copy-done | bytes 110616
  2.1 2.6 %edge.1 = (bf16[784,256]{1,0:T(8,128)(2,1)S(1)}, bf16[12,16,256]{2,1,0:T(8,128)(2,1)S(1)}, f32[8,128]{1,0:T(8,128)S(1)}, bf16[9,256,256]{2,1,0:T(8,128)(2,1)S(1)}) custom-call(s32[5]{0:T(128)S(1)} %stack.19.where_ref, bf16[12,256,256]{2,1,0:T(8,128)(2,1)} %bitcast.16, s32[12,1,2304]{2,1,0:T(1,128)S(1)} %bitcast.20), custom_call_target="tpu_custom_call" | custom-call | flops 2000000000 | bytes 2000000 | tf_op jit(solution)/shard_map/edge/pallas_call | solution.py:27
  4.7 0.7 collective-permute-start.2
  5.4 4.0 %collective-permute-start.1 = (f32[128]{0:T(128)S(1)}, f32[128]{0:T(128)S(1)}, u32[]{:S(2)}, u32[]{:S(2)}) collective-permute-start(f32[128]{0:T(128)S(1)} %copy-done.4), channel_id=1, source_target_pairs={{0,1},{1,0},{2,3},{3,2},{4,5},{5,4},{6,7},{7,6},{8,9},{9,8},{10,11... | collective-permute-start | bytes 1544 | tf_op jit(solution)/shard_map/ppermute | solution.py:406
  9.4 0.1 collective-permute-start.5
  9.5 1.5 %collective-permute-start.3 = (f32[8,128]{1,0:T(8,128)S(1)}, f32[8,128]{1,0:T(8,128)S(1)}, u32[]{:S(2)}, u32[]{:S(2)}) collective-permute-start(f32[8,128]{1,0:T(8,128)S(1)} %get-tuple-element.47), channel_id=1, source_target_pairs={{0,2},{2,0},{1,3},{3,1},{4,6},{6,4},{5,7},{7,5},{8,10},{10,8},{9,1... | collective-permute-start | bytes 12296 | tf_op jit(solution)/shard_map/ppermute | solution.py:406
  11.0 0.0 collective-permute-done.1
  11.0 0.0 copy-start.5
  11.0 2.9 %inner.1.inner_ref = bf16[7,256,256]{2,1,0:T(8,128)(2,1)S(1)} custom-call(s32[5]{0:T(128)S(1)} %stack.19.where_ref, bf16[9,256,256]{2,1,0:T(8,128)(2,1)S(1)} %get-tuple-element.45.near_ref, bf16[3,3,256,128]{3,2,1,0:T(8,128)(2,1)S(1)} %copy-done.1, bf16[3,3,256,128]{3,2,1,0:T(8,128)(2,1)S(1)} %collective-permute-done.w1b_ref, f32[1,128]{1,0:T(1,128)S(1)} %bitcast.21, ...), custom_call_target="tpu_custom_call" | custom-call | flops 3000000000 | bytes 3000000 | tf_op jit(solution)/shard_map/inner/pallas_call | solution.py:27
  13.9 0.0 collective-permute-done.3
  14.0 2.5 %collective-permute-start.8 = (f32[8,128]{1,0:T(8,128)S(1)}, f32[8,128]{1,0:T(8,128)S(1)}, u32[]{:S(2)}, u32[]{:S(2)}) collective-permute-start(f32[8,128]{1,0:T(8,128)S(1)} %add.7.rest_0_), channel_id=1, source_target_pairs={{0,4},{4,0},{8,12},{12,8},{1,5},{5,1},{9,13},{13,9},{2,6},{6,2},{1... | collective-permute-start | bytes 12296 | tf_op jit(solution)/shard_map/ppermute | solution.py:406
  16.5 2.6 %collective-permute-start.7 = (f32[8,128]{1,0:T(8,128)S(1)}, f32[8,128]{1,0:T(8,128)S(1)}, u32[]{:S(2)}, u32[]{:S(2)}) collective-permute-start(f32[8,128]{1,0:T(8,128)S(1)} %add.7.rest_0_), channel_id=1, source_target_pairs={{0,8},{4,12},{8,0},{12,4},{1,9},{5,13},{9,1},{13,5},{2,10},{6,14},... | collective-permute-start | bytes 12296 | tf_op jit(solution)/shard_map/ppermute | solution.py:406
  19.1 0.0 collective-permute-start.6
  19.1 0.0 collective-permute-start.4
  19.1 0.0 collective-permute-done.5
  19.1 4.7 %head.1 = (bf16[10,256,256]{2,1,0:T(8,128)(2,1)S(1)}, f32[8,256,128]{2,1,0:T(8,128)S(1)}, f32[1,128]{1,0:T(1,128)S(1)}, bf16[1152,256]{1,0:T(8,128)(2,1)S(1)}) custom-call(s32[5]{0:T(128)S(1)} %stack.19.where_ref, bf16[9,256,256]{2,1,0:T(8,128)(2,1)S(1)} %get-tuple-element.45.near_ref, bf16[7,256,256]{2,1,0:T(8,128)(2,1)S(1)} %inner.1.inner_ref, ...), custom_call_target="tpu_custom_call" | custom-call | flops 5000000000 | bytes 5000000 | tf_op jit(solution)/shard_map/head/pallas_call | solution.py:27
  23.8 0.0 collective-permute-done.8.rest_3_
  23.8 0.0 collective-permute-done.7.rest_2_
  23.8 0.6 collective-permute-done.6.rest_1_
  24.5 2.2 %back.1 = (bf16[6,336,256]{2,1,0:T(8,128)(2,1)S(1)}, bf16[6,256,128]{2,1,0:T(8,128)(2,1)S(1)}, bf16[6,256,128]{2,1,0:T(8,128)(2,1)S(1)}, f32[8,128]{1,0:T(8,128)S(1)}) custom-call(s32[5]{0:T(128)S(1)} %stack.19.where_ref, bf16[10,256,256]{2,1,0:T(8,128)(2,1)S(1)} %get-tuple-element.51.hid_ref, f32[8,256,128]{2,1,0:T(8,128)S(1)} %get-tuple-element.52.dz_ref, ...), custom_call_target="tpu_custom_call" | custom-call | flops 4000000000 | bytes 4000000 | tf_op jit(solution)/shard_map/back/pallas_call | solution.py:27
  26.7 0.1 collective-permute-start.9
  26.7 0.0 copy-start
  26.7 1.5 %cls.1 = (f32[896,128]{1,0:T(8,128)S(1)}, f32[896,128]{1,0:T(8,128)S(1)}) custom-call(s32[5]{0:T(128)S(1)} %stack.19.where_ref, bf16[10,256,256]{2,1,0:T(8,128)(2,1)S(1)} %get-tuple-element.51.hid_ref, bf16[6,336,256]{2,1,0:T(8,128)(2,1)S(1)} %get-tuple-element.60.dt_ref), custom_call_target="tpu_custom_call" | custom-call | flops 1500000000 | bytes 1500000 | tf_op jit(solution)/shard_map/cls/pallas_call | solution.py:27
  28.3 0.5 collective-permute-start.10
  28.8 0.0 collective-permute-done.9.other_ref
  28.8 0.0 collective-permute-done.4.far_ref
  28.8 3.9 %shared.1 = (f32[1152,128]{1,0:T(8,128)S(1)}, bf16[1152,128]{1,0:T(8,128)(2,1)S(1)}) custom-call(s32[5]{0:T(128)S(1)} %stack.19.where_ref, bf16[12,256,256]{2,1,0:T(8,128)(2,1)S(1)} %bitcast.17, bf16[784,256]{1,0:T(8,128)(2,1)S(1)} %collective-permute-done.2.halo_ref, bf16[784,256]{1,0:T(8,128)(2,1)S(1)} %collective-permute-done.4.far_ref, ...), custom_call_target="tpu_custom_call" | custom-call | flops 4000000000 | bytes 4000000 | tf_op jit(solution)/shard_map/shared/pallas_call | solution.py:27
  32.7 1.6 %collective-permute-start.11 = (bf16[1152,128]{1,0:T(8,128)(2,1)S(1)}, bf16[1152,128]{1,0:T(8,128)(2,1)S(1)}, u32[]{:S(2)}, u32[]{:S(2)}) collective-permute-start(bf16[1152,128]{1,0:T(8,128)(2,1)S(1)} %get-tuple-element.64), channel_id=1, source_target_pairs={{0,2},{2,0},{1,3},{3,1},{4,6},{6,4},{5,7},{7,5},{8,10},{10,8},{9,1... | collective-permute-start | bytes 884744 | tf_op jit(solution)/shard_map/ppermute | solution.py:406
  34.3 0.6 cls_split.1
  34.9 3.3 %collective-permute-start.12 = (bf16[256,128]{1,0:T(8,128)(2,1)S(1)}, bf16[256,128]{1,0:T(8,128)(2,1)S(1)}, u32[]{:S(2)}, u32[]{:S(2)}) collective-permute-start(bf16[256,128]{1,0:T(8,128)(2,1)S(1)} %get-tuple-element.65), channel_id=1, source_target_pairs={{0,12},{4,8},{8,4},{12,0},{1,13},{5,9},{9,5},{13,1},{2,14},{6,10},... | collective-permute-start | bytes 196616 | tf_op jit(solution)/shard_map/ppermute | solution.py:406
  38.2 0.0 collective-permute-start.13
  38.2 1.2 %collective-permute-start.14 = (bf16[256,128]{1,0:T(8,128)(2,1)S(1)}, bf16[256,128]{1,0:T(8,128)(2,1)S(1)}, u32[]{:S(2)}, u32[]{:S(2)}) collective-permute-start(bf16[256,128]{1,0:T(8,128)(2,1)S(1)} %get-tuple-element.67), channel_id=1, source_target_pairs={{0,4},{4,0},{8,12},{12,8},{1,5},{5,1},{9,13},{13,9},{2,6},{6,2},{1... | collective-permute-start | bytes 196616 | tf_op jit(solution)/shard_map/ppermute | solution.py:406
  39.4 2.1 %collective-permute-done.12.refs_1_ = bf16[256,128]{1,0:T(8,128)(2,1)S(1)} collective-permute-done((bf16[256,128]{1,0:T(8,128)(2,1)S(1)}, bf16[256,128]{1,0:T(8,128)(2,1)S(1)}, u32[]{:S(2)}, u32[]{:S(2)}) %collective-permute-start.12) | collective-permute-done | bytes 65568 | tf_op jit(solution)/shard_map/ppermute | solution.py:406
  41.5 2.1 %collective-permute-done.13.refs_2_ = bf16[256,128]{1,0:T(8,128)(2,1)S(1)} collective-permute-done((bf16[256,128]{1,0:T(8,128)(2,1)S(1)}, bf16[256,128]{1,0:T(8,128)(2,1)S(1)}, u32[]{:S(2)}, u32[]{:S(2)}) %collective-permute-start.13) | collective-permute-done | bytes 65568 | tf_op jit(solution)/shard_map/ppermute | solution.py:406
  43.5 0.5 collective-permute-done.14.refs_3_
  44.0 0.0 collective-permute-done.11.refs_0_
  44.0 0.7 sum.1
  44.7 2.3 %collective-permute-start.15 = (bf16[288,128]{1,0:T(8,128)(2,1)S(1)}, bf16[288,128]{1,0:T(8,128)(2,1)S(1)}, u32[]{:S(2)}, u32[]{:S(2)}) collective-permute-start(bf16[288,128]{1,0:T(8,128)(2,1)S(1)} %get-tuple-element.71), channel_id=1, source_target_pairs={{0,12},{4,8},{8,4},{12,0},{1,13},{5,9},{9,5},{13,1},{2,14},{6,10},... | collective-permute-start | bytes 221192 | tf_op jit(solution)/shard_map/ppermute | solution.py:406
  47.0 0.4 collective-permute-start.16
  47.4 1.8 %collective-permute-start.17 = (bf16[288,128]{1,0:T(8,128)(2,1)S(1)}, bf16[288,128]{1,0:T(8,128)(2,1)S(1)}, u32[]{:S(2)}, u32[]{:S(2)}) collective-permute-start(bf16[288,128]{1,0:T(8,128)(2,1)S(1)} %get-tuple-element.73), channel_id=1, source_target_pairs={{0,4},{4,0},{8,12},{12,8},{1,5},{5,1},{9,13},{13,9},{2,6},{6,2},{1... | collective-permute-start | bytes 221192 | tf_op jit(solution)/shard_map/ppermute | solution.py:406
  49.2 0.5 collective-permute-start.18
  49.7 3.4 %collective-permute-done.18.refs_3_ = bf16[144,128]{1,0:T(8,128)(2,1)S(1)} collective-permute-done((bf16[144,128]{1,0:T(8,128)(2,1)S(1)}, bf16[144,128]{1,0:T(8,128)(2,1)S(1)}, u32[]{:S(2)}, u32[]{:S(2)}) %collective-permute-start.18) | collective-permute-done | bytes 36896 | tf_op jit(solution)/shard_map/ppermute | solution.py:406
  53.1 0.5 collective-permute-done.16.refs_1_
  53.6 0.6 round.1
  54.2 0.4 collective-permute-start.22
  54.6 2.7 %collective-permute-start.21 = (bf16[288,128]{1,0:T(8,128)(2,1)S(1)}, bf16[288,128]{1,0:T(8,128)(2,1)S(1)}, u32[]{:S(2)}, u32[]{:S(2)}) collective-permute-start(bf16[288,128]{1,0:T(8,128)(2,1)S(1)} %get-tuple-element.76.refs_0_), channel_id=1, source_target_pairs={{0,8},{4,12},{8,0},{12,4},{1,9},{5,13},{9,1},{13,5},{2,10},{6,14},... | collective-permute-start | bytes 221192 | tf_op jit(solution)/shard_map/ppermute | solution.py:406
  57.4 1.3 %collective-permute-start.20 = (bf16[288,128]{1,0:T(8,128)(2,1)S(1)}, bf16[288,128]{1,0:T(8,128)(2,1)S(1)}, u32[]{:S(2)}, u32[]{:S(2)}) collective-permute-start(bf16[288,128]{1,0:T(8,128)(2,1)S(1)} %get-tuple-element.76.refs_0_), channel_id=1, source_target_pairs={{0,12},{4,8},{8,4},{12,0},{1,13},{5,9},{9,5},{13,1},{2,14},{6,10},... | collective-permute-start | bytes 221192 | tf_op jit(solution)/shard_map/ppermute | solution.py:406
  58.7 1.2 %collective-permute-start.23 = (bf16[112,128]{1,0:T(8,128)(2,1)S(1)}, bf16[112,128]{1,0:T(8,128)(2,1)S(1)}, u32[]{:S(2)}, u32[]{:S(2)}) collective-permute-start(bf16[112,128]{1,0:T(8,128)(2,1)S(1)} %get-tuple-element.77.refs_4_), channel_id=1, source_target_pairs={{0,2},{2,0},{1,3},{3,1},{4,6},{6,4},{5,7},{7,5},{8,10},{10,8},{9,1... | collective-permute-start | bytes 86024 | tf_op jit(solution)/shard_map/ppermute | solution.py:406
  59.9 2.7 %collective-permute-done.23.refs_5_ = bf16[112,128]{1,0:T(8,128)(2,1)S(1)} collective-permute-done((bf16[112,128]{1,0:T(8,128)(2,1)S(1)}, bf16[112,128]{1,0:T(8,128)(2,1)S(1)}, u32[]{:S(2)}, u32[]{:S(2)}) %collective-permute-start.23) | collective-permute-done | bytes 28704 | tf_op jit(solution)/shard_map/ppermute | solution.py:406
  62.6 0.0 collective-permute-done.21.refs_2_
  62.6 1.1 %collective-permute-done.20.refs_1_ = bf16[288,128]{1,0:T(8,128)(2,1)S(1)} collective-permute-done((bf16[288,128]{1,0:T(8,128)(2,1)S(1)}, bf16[288,128]{1,0:T(8,128)(2,1)S(1)}, u32[]{:S(2)}, u32[]{:S(2)}) %collective-permute-start.20) | collective-permute-done | bytes 73760 | tf_op jit(solution)/shard_map/ppermute | solution.py:406
  63.6 0.6 join.1
  64.2 0.8 %collective-permute-start.24 = (bf16[1152,128]{1,0:T(8,128)(2,1)S(1)}, bf16[1152,128]{1,0:T(8,128)(2,1)S(1)}, u32[]{:S(2)}, u32[]{:S(2)}) collective-permute-start(bf16[1152,128]{1,0:T(8,128)(2,1)S(1)} %get-tuple-element.78.refs_0_), channel_id=1, source_target_pairs={{0,2},{2,0},{1,3},{3,1},{4,6},{6,4},{5,7},{7,5},{8,10},{10,8},{9,1... | collective-permute-start | bytes 884744 | tf_op jit(solution)/shard_map/ppermute | solution.py:406
  65.0 1.3 %collective-permute-start.27 = (bf16[224,128]{1,0:T(8,128)(2,1)S(1)}, bf16[224,128]{1,0:T(8,128)(2,1)S(1)}, u32[]{:S(2)}, u32[]{:S(2)}) collective-permute-start(bf16[224,128]{1,0:T(8,128)(2,1)S(1)} %get-tuple-element.79.refs_2_), channel_id=1, source_target_pairs={{0,4},{4,0},{8,12},{12,8},{1,5},{5,1},{9,13},{13,9},{2,6},{6,2},{1... | collective-permute-start | bytes 172040 | tf_op jit(solution)/shard_map/ppermute | solution.py:406
  66.3 1.3 %collective-permute-start.26 = (bf16[224,128]{1,0:T(8,128)(2,1)S(1)}, bf16[224,128]{1,0:T(8,128)(2,1)S(1)}, u32[]{:S(2)}, u32[]{:S(2)}) collective-permute-start(bf16[224,128]{1,0:T(8,128)(2,1)S(1)} %get-tuple-element.79.refs_2_), channel_id=1, source_target_pairs={{0,8},{4,12},{8,0},{12,4},{1,9},{5,13},{9,1},{13,5},{2,10},{6,14},... | collective-permute-start | bytes 172040 | tf_op jit(solution)/shard_map/ppermute | solution.py:406
  67.6 1.8 %collective-permute-start.25 = (bf16[224,128]{1,0:T(8,128)(2,1)S(1)}, bf16[224,128]{1,0:T(8,128)(2,1)S(1)}, u32[]{:S(2)}, u32[]{:S(2)}) collective-permute-start(bf16[224,128]{1,0:T(8,128)(2,1)S(1)} %get-tuple-element.79.refs_2_), channel_id=1, source_target_pairs={{0,12},{4,8},{8,4},{12,0},{1,13},{5,9},{9,5},{13,1},{2,14},{6,10},... | collective-permute-start | bytes 172040 | tf_op jit(solution)/shard_map/ppermute | solution.py:406
  69.4 0.0 collective-permute-start.19
  69.4 1.2 %collective-permute-done.19.theirs_ref = f32[8,128]{1,0:T(8,128)S(1)} collective-permute-done((f32[8,128]{1,0:T(8,128)S(1)}, f32[8,128]{1,0:T(8,128)S(1)}, u32[]{:S(2)}, u32[]{:S(2)}) %collective-permute-start.19) | collective-permute-done | bytes 4128 | tf_op jit(solution)/shard_map/ppermute | solution.py:406
  70.6 0.0 collective-permute-done.27.refs_5_
  70.6 1.5 %collective-permute-done.26.refs_4_ = bf16[224,128]{1,0:T(8,128)(2,1)S(1)} collective-permute-done((bf16[224,128]{1,0:T(8,128)(2,1)S(1)}, bf16[224,128]{1,0:T(8,128)(2,1)S(1)}, u32[]{:S(2)}, u32[]{:S(2)}) %collective-permute-start.26) | collective-permute-done | bytes 57376 | tf_op jit(solution)/shard_map/ppermute | solution.py:406
  72.0 1.5 %collective-permute-done.25.refs_3_ = bf16[224,128]{1,0:T(8,128)(2,1)S(1)} collective-permute-done((bf16[224,128]{1,0:T(8,128)(2,1)S(1)}, bf16[224,128]{1,0:T(8,128)(2,1)S(1)}, u32[]{:S(2)}, u32[]{:S(2)}) %collective-permute-start.25) | collective-permute-done | bytes 57376 | tf_op jit(solution)/shard_map/ppermute | solution.py:406
  73.6 1.8 %out.1 = (f32[2304,128]{1,0:T(8,128)}, f32[1,128]{1,0:T(1,128)}, f32[3,3,99,128]{3,2,1,0:T(8,128)}, f32[1,99]{1,0:T(1,128)}, f32[1,1]{1,0:T(1,128)}) custom-call(s32[5]{0:T(128)S(1)} %stack.19.where_ref, f32[8,128]{1,0:T(8,128)S(1)} %get-tuple-element.75.small_ref, f32[8,128]{1,0:T(8,128)S(1)} %collective-permute-done.19.theirs_ref, ...), custom_call_target="tpu_custom_call" | custom-call | flops 1500000000 | bytes 1500000 | tf_op jit(solution)/shard_map/out/pallas_call | solution.py:27
  (17 shorter events, 0.0 us)
Async XLA Ops:
  0.6 10.4 %collective-permute-start = (bf16[3,3,256,128]{3,2,1,0:T(8,128)(2,1)}, bf16[3,3,256,128]{3,2,1,0:T(8,128)(2,1)S(1)}, u32[]{:S(2)}, u32[]{:S(2)}) collective-permute-start(bf16[3,3,256,128]{3,2,1,0:T(8,128)(2,1)} %w1a_ref.3), channel_id=1, source_target_pairs={{0,1},{1,0},{2,3},{3,2},{4,5},{5,4},{6,7},{7,6},{8,9},{9,8},{10,11... | collective-permute-start | bytes 1769480 | tf_op jit(solution)/shard_map/ppermute | solution.py:406
  1.2 0.9 %copy-start.3 = (s32[1,12,2304]{2,0,1:T(1,128)S(1)}, s32[1,12,2304]{2,0,1:T(1,128)}, u32[]{:S(2)}) copy-start(s32[1,12,2304]{2,0,1:T(1,128)} %param.7) | copy-start | bytes 331780
  2.1 3.3 %copy-start.4 = (f32[128]{0:T(128)S(1)}, f32[128]{0:T(128)}, u32[]{:S(2)}) copy-start(f32[128]{0:T(128)} %param.9) | copy-start | bytes 1540
  2.1 7.3 %copy-start.2 = (bf16[3,3,128,99]{2,3,1,0:T(8,128)(2,1)S(1)}, bf16[3,3,128,99]{2,3,1,0:T(8,128)(2,1)}, u32[]{:S(2)}) copy-start(bf16[3,3,128,99]{2,3,1,0:T(8,128)(2,1)} %param.10) | copy-start | bytes 684292
  2.1 8.9 %copy-start.1 = (bf16[3,3,256,128]{3,2,1,0:T(8,128)(2,1)S(1)}, bf16[3,3,256,128]{3,2,1,0:T(8,128)(2,1)}, u32[]{:S(2)}) copy-start(bf16[3,3,256,128]{3,2,1,0:T(8,128)(2,1)} %w1a_ref.3) | copy-start | bytes 1769476
  4.7 9.3 %collective-permute-start.2 = (bf16[784,256]{1,0:T(8,128)(2,1)S(1)}, bf16[784,256]{1,0:T(8,128)(2,1)S(1)}, u32[]{:S(2)}, u32[]{:S(2)}) collective-permute-start(bf16[784,256]{1,0:T(8,128)(2,1)S(1)} %get-tuple-element.46), channel_id=1, source_target_pairs={{1,4},{4,1},{5,8},{8,5},{9,12},{12,9},{3,6},{6,3},{7,10},{10,7},{1... | collective-permute-start | bytes 1204232 | tf_op jit(solution)/shard_map/ppermute | solution.py:450
  5.4 5.6 %collective-permute-start.1 = (f32[128]{0:T(128)S(1)}, f32[128]{0:T(128)S(1)}, u32[]{:S(2)}, u32[]{:S(2)}) collective-permute-start(f32[128]{0:T(128)S(1)} %copy-done.4), channel_id=1, source_target_pairs={{0,1},{1,0},{2,3},{3,2},{4,5},{5,4},{6,7},{7,6},{8,9},{9,8},{10,11... | collective-permute-start | bytes 1544 | tf_op jit(solution)/shard_map/ppermute | solution.py:406
  9.4 9.7 %collective-permute-start.5 = (bf16[3,3,128,99]{2,3,1,0:T(8,128)(2,1)S(1)}, bf16[3,3,128,99]{2,3,1,0:T(8,128)(2,1)S(1)}, u32[]{:S(2)}, u32[]{:S(2)}) collective-permute-start(bf16[3,3,128,99]{2,3,1,0:T(8,128)(2,1)S(1)} %copy-done.2), channel_id=1, source_target_pairs={{0,1},{1,0},{2,3},{3,2},{4,5},{5,4},{6,7},{7,6},{8,9},{9,8},{10,11... | collective-permute-start | bytes 684296 | tf_op jit(solution)/shard_map/ppermute | solution.py:406
  9.5 4.5 %collective-permute-start.3 = (f32[8,128]{1,0:T(8,128)S(1)}, f32[8,128]{1,0:T(8,128)S(1)}, u32[]{:S(2)}, u32[]{:S(2)}) collective-permute-start(f32[8,128]{1,0:T(8,128)S(1)} %get-tuple-element.47), channel_id=1, source_target_pairs={{0,2},{2,0},{1,3},{3,1},{4,6},{6,4},{5,7},{7,5},{8,10},{10,8},{9,1... | collective-permute-start | bytes 12296 | tf_op jit(solution)/shard_map/ppermute | solution.py:406
  11.0 8.1 %copy-start.5 = (f32[99]{0:T(128)S(1)}, f32[99]{0:T(128)}, u32[]{:S(2)}) copy-start(f32[99]{0:T(128)} %param.11) | copy-start | bytes 1192
  14.0 9.8 %collective-permute-start.8 = (f32[8,128]{1,0:T(8,128)S(1)}, f32[8,128]{1,0:T(8,128)S(1)}, u32[]{:S(2)}, u32[]{:S(2)}) collective-permute-start(f32[8,128]{1,0:T(8,128)S(1)} %add.7.rest_0_), channel_id=1, source_target_pairs={{0,4},{4,0},{8,12},{12,8},{1,5},{5,1},{9,13},{13,9},{2,6},{6,2},{1... | collective-permute-start | bytes 12296 | tf_op jit(solution)/shard_map/ppermute | solution.py:406
  16.5 7.4 %collective-permute-start.7 = (f32[8,128]{1,0:T(8,128)S(1)}, f32[8,128]{1,0:T(8,128)S(1)}, u32[]{:S(2)}, u32[]{:S(2)}) collective-permute-start(f32[8,128]{1,0:T(8,128)S(1)} %add.7.rest_0_), channel_id=1, source_target_pairs={{0,8},{4,12},{8,0},{12,4},{1,9},{5,13},{9,1},{13,5},{2,10},{6,14},... | collective-permute-start | bytes 12296 | tf_op jit(solution)/shard_map/ppermute | solution.py:406
  19.1 5.4 %collective-permute-start.6 = (f32[8,128]{1,0:T(8,128)S(1)}, f32[8,128]{1,0:T(8,128)S(1)}, u32[]{:S(2)}, u32[]{:S(2)}) collective-permute-start(f32[8,128]{1,0:T(8,128)S(1)} %add.7.rest_0_), channel_id=1, source_target_pairs={{0,12},{4,8},{8,4},{12,0},{1,13},{5,9},{9,5},{13,1},{2,14},{6,10},... | collective-permute-start | bytes 12296 | tf_op jit(solution)/shard_map/ppermute | solution.py:406
  19.1 9.7 %collective-permute-start.4 = (bf16[784,256]{1,0:T(8,128)(2,1)S(1)}, bf16[784,256]{1,0:T(8,128)(2,1)S(1)}, u32[]{:S(2)}, u32[]{:S(2)}) collective-permute-start(bf16[784,256]{1,0:T(8,128)(2,1)S(1)} %collective-permute-done.2.halo_ref), channel_id=1, source_target_pairs={{0,1},{1,0},{2,3},{3,2},{4,5},{5,4},{6,7},{7,6},{8,9},{9,8},{10,11... | collective-permute-start | bytes 1204232 | tf_op jit(solution)/shard_map/ppermute | solution.py:406
  26.7 2.2 %collective-permute-start.9 = (bf16[6,256,128]{2,1,0:T(8,128)(2,1)S(1)}, bf16[6,256,128]{2,1,0:T(8,128)(2,1)S(1)}, u32[]{:S(2)}, u32[]{:S(2)}) collective-permute-start(bf16[6,256,128]{2,1,0:T(8,128)(2,1)S(1)} %get-tuple-element.57), channel_id=1, source_target_pairs={{0,1},{1,0},{2,3},{3,2},{4,5},{5,4},{6,7},{7,6},{8,9},{9,8},{10,11... | collective-permute-start | bytes 1179656 | tf_op jit(solution)/shard_map/ppermute | solution.py:406
  26.7 2.1 %copy-start = (bf16[1,12,256,256]{3,2,1,0:T(8,128)(2,1)S(1)}, bf16[1,12,256,256]{3,2,1,0:T(8,128)(2,1)}, u32[]{:S(2)}) copy-start(bf16[1,12,256,256]{3,2,1,0:T(8,128)(2,1)} %param.6) | copy-start | bytes 4718596
  28.3 6.0 %collective-permute-start.10 = (f32[896,128]{1,0:T(8,128)S(1)}, f32[896,128]{1,0:T(8,128)S(1)}, u32[]{:S(2)}, u32[]{:S(2)}) collective-permute-start(f32[896,128]{1,0:T(8,128)S(1)} %get-tuple-element.62), channel_id=1, source_target_pairs={{0,1},{1,0},{2,3},{3,2},{4,5},{5,4},{6,7},{7,6},{8,9},{9,8},{10,11... | collective-permute-start | bytes 1376264 | tf_op jit(solution)/shard_map/ppermute | solution.py:406
  32.7 11.3 %collective-permute-start.11 = (bf16[1152,128]{1,0:T(8,128)(2,1)S(1)}, bf16[1152,128]{1,0:T(8,128)(2,1)S(1)}, u32[]{:S(2)}, u32[]{:S(2)}) collective-permute-start(bf16[1152,128]{1,0:T(8,128)(2,1)S(1)} %get-tuple-element.64), channel_id=1, source_target_pairs={{0,2},{2,0},{1,3},{3,1},{4,6},{6,4},{5,7},{7,5},{8,10},{10,8},{9,1... | collective-permute-start | bytes 884744 | tf_op jit(solution)/shard_map/ppermute | solution.py:406
  34.9 6.6 %collective-permute-start.12 = (bf16[256,128]{1,0:T(8,128)(2,1)S(1)}, bf16[256,128]{1,0:T(8,128)(2,1)S(1)}, u32[]{:S(2)}, u32[]{:S(2)}) collective-permute-start(bf16[256,128]{1,0:T(8,128)(2,1)S(1)} %get-tuple-element.65), channel_id=1, source_target_pairs={{0,12},{4,8},{8,4},{12,0},{1,13},{5,9},{9,5},{13,1},{2,14},{6,10},... | collective-permute-start | bytes 196616 | tf_op jit(solution)/shard_map/ppermute | solution.py:406
  38.2 5.3 %collective-permute-start.13 = (bf16[256,128]{1,0:T(8,128)(2,1)S(1)}, bf16[256,128]{1,0:T(8,128)(2,1)S(1)}, u32[]{:S(2)}, u32[]{:S(2)}) collective-permute-start(bf16[256,128]{1,0:T(8,128)(2,1)S(1)} %get-tuple-element.66), channel_id=1, source_target_pairs={{0,8},{4,12},{8,0},{12,4},{1,9},{5,13},{9,1},{13,5},{2,10},{6,14},... | collective-permute-start | bytes 196616 | tf_op jit(solution)/shard_map/ppermute | solution.py:406
  38.2 5.8 %collective-permute-start.14 = (bf16[256,128]{1,0:T(8,128)(2,1)S(1)}, bf16[256,128]{1,0:T(8,128)(2,1)S(1)}, u32[]{:S(2)}, u32[]{:S(2)}) collective-permute-start(bf16[256,128]{1,0:T(8,128)(2,1)S(1)} %get-tuple-element.67), channel_id=1, source_target_pairs={{0,4},{4,0},{8,12},{12,8},{1,5},{5,1},{9,13},{13,9},{2,6},{6,2},{1... | collective-permute-start | bytes 196616 | tf_op jit(solution)/shard_map/ppermute | solution.py:406
  44.7 8.4 %collective-permute-start.15 = (bf16[288,128]{1,0:T(8,128)(2,1)S(1)}, bf16[288,128]{1,0:T(8,128)(2,1)S(1)}, u32[]{:S(2)}, u32[]{:S(2)}) collective-permute-start(bf16[288,128]{1,0:T(8,128)(2,1)S(1)} %get-tuple-element.71), channel_id=1, source_target_pairs={{0,12},{4,8},{8,4},{12,0},{1,13},{5,9},{9,5},{13,1},{2,14},{6,10},... | collective-permute-start | bytes 221192 | tf_op jit(solution)/shard_map/ppermute | solution.py:406
  47.0 6.6 %collective-permute-start.16 = (bf16[288,128]{1,0:T(8,128)(2,1)S(1)}, bf16[288,128]{1,0:T(8,128)(2,1)S(1)}, u32[]{:S(2)}, u32[]{:S(2)}) collective-permute-start(bf16[288,128]{1,0:T(8,128)(2,1)S(1)} %get-tuple-element.72), channel_id=1, source_target_pairs={{0,8},{4,12},{8,0},{12,4},{1,9},{5,13},{9,1},{13,5},{2,10},{6,14},... | collective-permute-start | bytes 221192 | tf_op jit(solution)/shard_map/ppermute | solution.py:406
  47.4 6.2 %collective-permute-start.17 = (bf16[288,128]{1,0:T(8,128)(2,1)S(1)}, bf16[288,128]{1,0:T(8,128)(2,1)S(1)}, u32[]{:S(2)}, u32[]{:S(2)}) collective-permute-start(bf16[288,128]{1,0:T(8,128)(2,1)S(1)} %get-tuple-element.73), channel_id=1, source_target_pairs={{0,4},{4,0},{8,12},{12,8},{1,5},{5,1},{9,13},{13,9},{2,6},{6,2},{1... | collective-permute-start | bytes 221192 | tf_op jit(solution)/shard_map/ppermute | solution.py:406
  49.2 4.0 %collective-permute-start.18 = (bf16[144,128]{1,0:T(8,128)(2,1)S(1)}, bf16[144,128]{1,0:T(8,128)(2,1)S(1)}, u32[]{:S(2)}, u32[]{:S(2)}) collective-permute-start(bf16[144,128]{1,0:T(8,128)(2,1)S(1)} %get-tuple-element.74), channel_id=1, source_target_pairs={{0,2},{2,0},{1,3},{3,1},{4,6},{6,4},{5,7},{7,5},{8,10},{10,8},{9,1... | collective-permute-start | bytes 110600 | tf_op jit(solution)/shard_map/ppermute | solution.py:406
  54.2 8.3 %collective-permute-start.22 = (bf16[288,128]{1,0:T(8,128)(2,1)S(1)}, bf16[288,128]{1,0:T(8,128)(2,1)S(1)}, u32[]{:S(2)}, u32[]{:S(2)}) collective-permute-start(bf16[288,128]{1,0:T(8,128)(2,1)S(1)} %get-tuple-element.76.refs_0_), channel_id=1, source_target_pairs={{0,4},{4,0},{8,12},{12,8},{1,5},{5,1},{9,13},{13,9},{2,6},{6,2},{1... | collective-permute-start | bytes 221192 | tf_op jit(solution)/shard_map/ppermute | solution.py:406
  54.6 7.9 %collective-permute-start.21 = (bf16[288,128]{1,0:T(8,128)(2,1)S(1)}, bf16[288,128]{1,0:T(8,128)(2,1)S(1)}, u32[]{:S(2)}, u32[]{:S(2)}) collective-permute-start(bf16[288,128]{1,0:T(8,128)(2,1)S(1)} %get-tuple-element.76.refs_0_), channel_id=1, source_target_pairs={{0,8},{4,12},{8,0},{12,4},{1,9},{5,13},{9,1},{13,5},{2,10},{6,14},... | collective-permute-start | bytes 221192 | tf_op jit(solution)/shard_map/ppermute | solution.py:406
  57.4 6.3 %collective-permute-start.20 = (bf16[288,128]{1,0:T(8,128)(2,1)S(1)}, bf16[288,128]{1,0:T(8,128)(2,1)S(1)}, u32[]{:S(2)}, u32[]{:S(2)}) collective-permute-start(bf16[288,128]{1,0:T(8,128)(2,1)S(1)} %get-tuple-element.76.refs_0_), channel_id=1, source_target_pairs={{0,12},{4,8},{8,4},{12,0},{1,13},{5,9},{9,5},{13,1},{2,14},{6,10},... | collective-permute-start | bytes 221192 | tf_op jit(solution)/shard_map/ppermute | solution.py:406
  58.7 3.9 %collective-permute-start.23 = (bf16[112,128]{1,0:T(8,128)(2,1)S(1)}, bf16[112,128]{1,0:T(8,128)(2,1)S(1)}, u32[]{:S(2)}, u32[]{:S(2)}) collective-permute-start(bf16[112,128]{1,0:T(8,128)(2,1)S(1)} %get-tuple-element.77.refs_4_), channel_id=1, source_target_pairs={{0,2},{2,0},{1,3},{3,1},{4,6},{6,4},{5,7},{7,5},{8,10},{10,8},{9,1... | collective-permute-start | bytes 86024 | tf_op jit(solution)/shard_map/ppermute | solution.py:406
  64.2 9.4 %collective-permute-start.24 = (bf16[1152,128]{1,0:T(8,128)(2,1)S(1)}, bf16[1152,128]{1,0:T(8,128)(2,1)S(1)}, u32[]{:S(2)}, u32[]{:S(2)}) collective-permute-start(bf16[1152,128]{1,0:T(8,128)(2,1)S(1)} %get-tuple-element.78.refs_0_), channel_id=1, source_target_pairs={{0,2},{2,0},{1,3},{3,1},{4,6},{6,4},{5,7},{7,5},{8,10},{10,8},{9,1... | collective-permute-start | bytes 884744 | tf_op jit(solution)/shard_map/ppermute | solution.py:406
  65.0 5.6 %collective-permute-start.27 = (bf16[224,128]{1,0:T(8,128)(2,1)S(1)}, bf16[224,128]{1,0:T(8,128)(2,1)S(1)}, u32[]{:S(2)}, u32[]{:S(2)}) collective-permute-start(bf16[224,128]{1,0:T(8,128)(2,1)S(1)} %get-tuple-element.79.refs_2_), channel_id=1, source_target_pairs={{0,4},{4,0},{8,12},{12,8},{1,5},{5,1},{9,13},{13,9},{2,6},{6,2},{1... | collective-permute-start | bytes 172040 | tf_op jit(solution)/shard_map/ppermute | solution.py:406
  66.3 5.7 %collective-permute-start.26 = (bf16[224,128]{1,0:T(8,128)(2,1)S(1)}, bf16[224,128]{1,0:T(8,128)(2,1)S(1)}, u32[]{:S(2)}, u32[]{:S(2)}) collective-permute-start(bf16[224,128]{1,0:T(8,128)(2,1)S(1)} %get-tuple-element.79.refs_2_), channel_id=1, source_target_pairs={{0,8},{4,12},{8,0},{12,4},{1,9},{5,13},{9,1},{13,5},{2,10},{6,14},... | collective-permute-start | bytes 172040 | tf_op jit(solution)/shard_map/ppermute | solution.py:406
  67.6 6.0 %collective-permute-start.25 = (bf16[224,128]{1,0:T(8,128)(2,1)S(1)}, bf16[224,128]{1,0:T(8,128)(2,1)S(1)}, u32[]{:S(2)}, u32[]{:S(2)}) collective-permute-start(bf16[224,128]{1,0:T(8,128)(2,1)S(1)} %get-tuple-element.79.refs_2_), channel_id=1, source_target_pairs={{0,12},{4,8},{8,4},{12,0},{1,13},{5,9},{9,5},{13,1},{2,14},{6,10},... | collective-permute-start | bytes 172040 | tf_op jit(solution)/shard_map/ppermute | solution.py:406
  69.4 1.2 %collective-permute-start.19 = (f32[8,128]{1,0:T(8,128)S(1)}, f32[8,128]{1,0:T(8,128)S(1)}, u32[]{:S(2)}, u32[]{:S(2)}) collective-permute-start(f32[8,128]{1,0:T(8,128)S(1)} %get-tuple-element.75.small_ref), channel_id=1, source_target_pairs={{0,1},{1,0},{2,3},{3,2},{4,5},{5,4},{6,7},{7,6},{8,9},{9,8},{10,11... | collective-permute-start | bytes 12296 | tf_op jit(solution)/shard_map/ppermute | solution.py:406

commit v8 on v7

--- a/solution.py
+++ b/solution.py
@@ -15,7 +15,8 @@
 CLS_ROWS = 112
 TILE, BATCH = 3, 4
 BLOCK = 2
-TRIO = 32
+SMALL = 4
+TRIO = 16
 BF16 = jnp.bfloat16
 F32 = jnp.float32
 VMEM = pl.BlockSpec(memory_space=pltpu.VMEM)
@@ -23,17 +24,32 @@
 SMEM = pl.BlockSpec(memory_space=pltpu.SMEM)
 
 
+class Places:
+    def __init__(self, half):
+        self.half = half
+
+    def __getitem__(self, i):
+        c, t = lax.axis_index("chan"), lax.axis_index("tile")
+        if i == 0:
+            return c
+        if i == 1:
+            return (2 * t + c) * self.half
+        if i == 2:
+            return 2 * lax.axis_size("tile") * self.half
+        return t if i == 3 else lax.axis_index("batch")
+
+
 def call(kernel, name, micros, outs, inputs, scratch=(), specs=None, mib=32):
     return pl.pallas_call(
-        kernel,
-        in_specs=specs or [SMEM] + [VMEM] * (len(inputs) - 1),
+        functools.partial(kernel, inputs[0]),
+        in_specs=(specs or [SMEM] + [VMEM] * (len(inputs) - 1))[1:],
         out_specs=[VMEM] * len(outs),
         out_shape=[jax.ShapeDtypeStruct(shape, kind) for shape, kind in outs],
         scratch_shapes=[pltpu.VMEM(*shape) if isinstance(shape, tuple) else shape for shape in scratch],
         cost_estimate=pl.CostEstimate(flops=int(micros * 1e9), bytes_accessed=int(micros * 1e6), transcendentals=0),
         compiler_params=pltpu.CompilerParams(vmem_limit_bytes=int(mib * 1024 * 1024)),
         name=name,
-    )(*inputs)
+    )(*inputs[1:])
 
 
 def shift_cells(field, by):
@@ -63,13 +79,13 @@
 
 
 def put_trio(ref, start, x):
-    high, middle, low = three(x)
-    ref[start : start + TRIO] = jnp.concatenate([high, middle, low, jnp.zeros_like(low)], axis=0)
+    parts = [part.astype(F32) for part in three(x)]
+    ref[start : start + TRIO] = jnp.concatenate(parts + [jnp.zeros_like(x)], axis=0).astype(BF16)
 
 
 def get_trio(ref, start):
     part = ref[start : start + TRIO].astype(F32)
-    return part[0:8] + part[8:16] + part[16:24]
+    return part[0:SMALL] + part[SMALL : 2 * SMALL] + part[2 * SMALL : 3 * SMALL]
 
 
 def edge_kernel(where_ref, f_ref, lab_ref, msg_ref, labt_ref, count_ref, near_ref, sem):
@@ -245,12 +261,11 @@
         return jnp.sum(dpre, axis=0, keepdims=True)
 
     gsb = lax.fori_loop(0, half // BLOCK, dpre, jnp.zeros((1, chans), F32), unroll=True)
-    small_ref[0:1] = gcb
-    small_ref[1:2] = jnp.broadcast_to(jnp.sum(loss_ref[...], axis=1, keepdims=True), (1, LANES)) * inverse
-    small_ref[2:3] = jnp.zeros((1, LANES), F32)
-    small_ref[3:4] = gsb[:, : chans // 2]
-    small_ref[4:5] = gsb[:, chans // 2 :]
-    small_ref[5:8] = jnp.zeros((3, LANES), F32)
+    loss = jnp.sum(loss_ref[...], axis=1, keepdims=True) * inverse[:, :1]
+    small_ref[0:1] = jnp.where(lax.broadcasted_iota(jnp.int32, (1, LANES), 1) < LOGITS, gcb, loss)
+    small_ref[1:2] = jnp.zeros((1, LANES), F32)
+    small_ref[2:3] = gsb[:, : chans // 2]
+    small_ref[3:4] = gsb[:, chans // 2 :]
 
 
 def cls_kernel(where_ref, hid_ref, dt_ref, own_ref, other_ref):
@@ -374,9 +389,8 @@
 
 def join(me, in_refs, out_ref):
     rows = in_refs[0].shape[0]
-    size = len(in_refs)
     for k, ref in enumerate(in_refs):
-        out_ref[pl.ds(pl.multiple_of((me ^ ((size - k) % size)) * rows, 8), rows)] = ref[...].astype(out_ref.dtype)
+        out_ref[pl.ds(pl.multiple_of((me ^ k) * rows, 8), rows)] = ref[...].astype(out_ref.dtype)
 
 
 def join_kernel(n_in, where_ref, *refs):
@@ -395,10 +409,10 @@
     join(where_ref[TILE], cls_in_refs, cls_whole_ref)
     for tap in range(9):
         cls_out_ref[tap // 3, tap % 3] = cls_whole_ref[LOGITS * tap : LOGITS * (tap + 1)]
-    bias_ref[...] = small_ref[3:4] + theirs_ref[4:5]
-    both = small_ref[0:2] + theirs_ref[0:2]
-    cls_bias_ref[...] = both[0:1, :LOGITS]
-    loss_ref[...] = both[1:2, :1]
+    bias_ref[...] = small_ref[2:3] + theirs_ref[3:4]
+    both = small_ref[0:1] + theirs_ref[0:1]
+    cls_bias_ref[...] = both[:, :LOGITS]
+    loss_ref[...] = both[:, LOGITS : LOGITS + 1]
 
 
 def swap(x, axis, bit=1):
@@ -407,7 +421,7 @@
 
 
 def others(x, axis):
-    return exchange([x] * (lax.axis_size(axis) - 1), axis)
+    return [swap(x, axis, bit) for bit in range(1, lax.axis_size(axis))]
 
 
 def exchange(sends, axis):
@@ -428,7 +442,7 @@
     c = lax.axis_index("chan")
     t = lax.axis_index("tile")
     f = features[0]
-    where = jnp.stack([c, t * rows + half * c, jnp.int32(tiles * rows), t, lax.axis_index("batch")]).astype(jnp.int32)
+    where = Places(half)
     lab = labels.reshape(rows, 1, labels.shape[2])
     msg, labt, count, near = call(
         edge_kernel, "edge", 2,
@@ -454,8 +468,9 @@
 
     weights = [w_shared, w1b, b_shared.reshape(1, outs), b1b.reshape(1, outs)]
     (inner,) = call(inner_kernel, "inner", 3, [((half + 1, cols, chans), BF16)], [where, near] + weights)
-    inner, halo, *met = lax.optimization_barrier((inner, halo, *met))
+    inner, *met = lax.optimization_barrier((inner, *met))
     count = pair_sum([count] + met)
+    halo, _ = lax.optimization_barrier((halo, count))
     counts = [count] + others(count, "tile")
     hid, dz, loss, w2 = call(
         head_kernel, "head", 5,
@@ -472,7 +487,7 @@
             ((half, 3 * CLS_ROWS, cols), BF16),
             ((half, cols, outs), BF16),
             ((half, cols, outs), BF16),
-            ((8, LANES), F32),
+            ((SMALL, LANES), F32),
         ],
         [where, hid, dz, loss, w2] + counts,
         [((half + 2, cols, LANES), BF16)],
@@ -504,7 +519,7 @@
     carrived = exchange(csends, "tile")
     keep, small, *sends = call(
         functools.partial(sum_kernel, pages - 1, tiles - 1, tiles - 1), "sum", 0.7,
-        [((second, outs), F32), ((8, LANES), F32)]
+        [((second, outs), F32), ((SMALL, LANES), F32)]
         + [((second, outs), BF16)] * (tiles - 1)
         + [((csecond, outs), F32)]
         + [((csecond + TRIO, outs), BF16)] * (pages - 1),
@@ -516,7 +531,7 @@
     carrived = exchange(csends, "batch")
     done, small, cdone = call(
         functools.partial(round_kernel, tiles - 1), "round", 0.7,
-        [((second, outs), BF16), ((8, LANES), F32), ((csecond, outs), BF16)],
+        [((second, outs), BF16), ((SMALL, LANES), F32), ((csecond, outs), BF16)],
         [where, keep, small, ckeep] + arrived + carrived,
     )
     small_theirs = swap(small, "chan")

time: 75.6 us -> 67.3 us (0.89)
  Pallas kernels: 22 us -> 16 us
  waiting for transfers between devices: 17.2 us -> 15.8 us
  starting transfers between devices: 34.3 us -> 33.5 us
    pallas_call x11, Pallas kernels: 22 us -> 16 us  [call(): pl.pallas_call(functools.partial(kernel, inputs[0]), in_specs=(specs or [...]
    ppermute x27, waiting for transfers between devices: 17.2 us -> 15.8 us  [swap(): return lax.ppermute(x, axis, [(i, i ^ bit) for i in range(size)])]
    ppermute x27, starting transfers between devices: 33.6 us -> 32.8 us  [swap(): return lax.ppermute(x, axis, [(i, i ^ bit) for i in range(size)])]
  transfers between devices with their start and end apart: 28 -> 28, of which waited for: 11 -> 11; matrix products, arithmetic and copies ran while one was open for 0% -> 0% of each run, Pallas kernels for 24% -> 22%
where the time goes in v8:
time: 67.3 us; the launch traced here: 67.1 us
  starting transfers between devices  33.5 us (50%)
  Pallas kernels  16 us (24%)
  waiting for transfers between devices  15.8 us (23%)
  local copies, waits for them, and re-layouts  0.97 us (1%)
  between operations  0.8 us (1%)
    ppermute x27, starting transfers between devices, swap(): return lax.ppermute(x, axis, [(i, i ^ bit) for i in range(size)])  32.8 us
    pallas_call x11, Pallas kernels, call(): pl.pallas_call(functools.partial(kernel, inputs[0]), in_specs=(specs or [...  16 us
    ppermute x27, waiting for transfers between devices, swap(): return lax.ppermute(x, axis, [(i, i ^ bit) for i in range(size)])  15.8 us
  transfers between devices with their start and end apart: 28, of which 11 were waited for; matrix products, arithmetic and copies ran while one was open for 0% of the time, Pallas kernels for 22%

profile of v8, /device:TPU:0, one launch (start us, length us, event | category | flops | bytes accessed | tf_op | source)
XLA Modules:
  0.0 67.1 jit_solution(3880918986417195588)
XLA Ops:
  0.6 0.5 collective-permute-start.1
  1.2 0.9 %copy-done.3 = s32[1,12,2304]{2,0,1:T(1,128)S(1)} copy-done((s32[1,12,2304]{2,0,1:T(1,128)S(1)}, s32[1,12,2304]{2,0,1:T(1,128)}, u32[]{:S(2)}) %copy-start.3) | copy-done | bytes 110616
  2.1 2.0 %edge.1 = (bf16[784,256]{1,0:T(8,128)(2,1)S(1)}, bf16[12,16,256]{2,1,0:T(8,128)(2,1)S(1)}, f32[8,128]{1,0:T(8,128)S(1)}, bf16[9,256,256]{2,1,0:T(8,128)(2,1)S(1)}) custom-call(bf16[12,256,256]{2,1,0:T(8,128)(2,1)} %bitcast.12, s32[12,1,2304]{2,1,0:T(1,128)S(1)} %bitcast.16), custom_call_target="tpu_custom_call" | custom-call | flops 2000000000 | bytes 2000000 | tf_op jit(solution)/shard_map/edge/pallas_call | solution.py:43
  4.1 0.7 %collective-permute-start = (bf16[784,256]{1,0:T(8,128)(2,1)S(1)}, bf16[784,256]{1,0:T(8,128)(2,1)S(1)}, u32[]{:S(2)}, u32[]{:S(2)}) collective-permute-start(bf16[784,256]{1,0:T(8,128)(2,1)S(1)} %get-tuple-element.45), channel_id=1, source_target_pairs={{1,4},{4,1},{5,8},{8,5},{9,12},{12,9},{3,6},{6,3},{7,10},{10,7},{1... | collective-permute-start | bytes 1204232 | tf_op jit(solution)/shard_map/ppermute | solution.py:464
  4.8 4.0 %collective-permute-start.2 = (f32[128]{0:T(128)S(1)}, f32[128]{0:T(128)S(1)}, u32[]{:S(2)}, u32[]{:S(2)}) collective-permute-start(f32[128]{0:T(128)S(1)} %copy-done.4), channel_id=1, source_target_pairs={{0,1},{1,0},{2,3},{3,2},{4,5},{5,4},{6,7},{7,6},{8,9},{9,8},{10,11... | collective-permute-start | bytes 1544 | tf_op jit(solution)/shard_map/ppermute | solution.py:420
  8.8 0.1 collective-permute-start.5
  8.9 1.5 %collective-permute-start.3 = (f32[8,128]{1,0:T(8,128)S(1)}, f32[8,128]{1,0:T(8,128)S(1)}, u32[]{:S(2)}, u32[]{:S(2)}) collective-permute-start(f32[8,128]{1,0:T(8,128)S(1)} %get-tuple-element.46), channel_id=1, source_target_pairs={{0,2},{2,0},{1,3},{3,1},{4,6},{6,4},{5,7},{7,5},{8,10},{10,8},{9,1... | collective-permute-start | bytes 12296 | tf_op jit(solution)/shard_map/ppermute | solution.py:420
  10.4 0.0 collective-permute-done.2
  10.4 0.0 collective-permute-done.1.w1b_ref
  10.4 0.0 copy-start.5
  10.4 2.4 %inner.1.inner_ref = bf16[7,256,256]{2,1,0:T(8,128)(2,1)S(1)} custom-call(bf16[9,256,256]{2,1,0:T(8,128)(2,1)S(1)} %get-tuple-element.47.near_ref, bf16[3,3,256,128]{3,2,1,0:T(8,128)(2,1)S(1)} %copy-done.1, bf16[3,3,256,128]{3,2,1,0:T(8,128)(2,1)S(1)} %collective-permute-done.1.w1b_ref, f32[1,128]{1,0:T(1,128)S(1)} %bitcast.17, f32[1,128]{1,0:T(1,128)S(1)} %bitcast.20), custom_call_target="tpu_custom_call" | custom-call | flops 3000000000 | bytes 3000000 | tf_op jit(solution)/shard_map/inner/pallas_call | solution.py:43
  12.8 0.0 collective-permute-done.3
  12.8 2.9 %collective-permute-start.8 = (f32[8,128]{1,0:T(8,128)S(1)}, f32[8,128]{1,0:T(8,128)S(1)}, u32[]{:S(2)}, u32[]{:S(2)}) collective-permute-start(f32[8,128]{1,0:T(8,128)S(1)} %add.3.rest_0_), channel_id=1, source_target_pairs={{0,12},{4,8},{8,4},{12,0},{1,13},{5,9},{9,5},{13,1},{2,14},{6,10},... | collective-permute-start | bytes 12296 | tf_op jit(solution)/shard_map/ppermute | solution.py:420
  15.7 0.2 collective-permute-start.7
  15.9 1.3 %collective-permute-start.6 = (f32[8,128]{1,0:T(8,128)S(1)}, f32[8,128]{1,0:T(8,128)S(1)}, u32[]{:S(2)}, u32[]{:S(2)}) collective-permute-start(f32[8,128]{1,0:T(8,128)S(1)} %add.3.rest_0_), channel_id=1, source_target_pairs={{0,4},{4,0},{8,12},{12,8},{1,5},{5,1},{9,13},{13,9},{2,6},{6,2},{1... | collective-permute-start | bytes 12296 | tf_op jit(solution)/shard_map/ppermute | solution.py:420
  17.2 0.0 collective-permute-done.halo_ref
  17.2 0.0 collective-permute-start.4
  17.2 0.0 collective-permute-done.5
  17.3 4.0 %head.1 = (bf16[10,256,256]{2,1,0:T(8,128)(2,1)S(1)}, f32[8,256,128]{2,1,0:T(8,128)S(1)}, f32[1,128]{1,0:T(1,128)S(1)}, bf16[1152,256]{1,0:T(8,128)(2,1)S(1)}) custom-call(bf16[9,256,256]{2,1,0:T(8,128)(2,1)S(1)} %get-tuple-element.47.near_ref, bf16[7,256,256]{2,1,0:T(8,128)(2,1)S(1)} %inner.1.inner_ref, bf16[784,256]{1,0:T(8,128)(2,1)S(1)} %collective-permute-done.halo_ref, ...), custom_call_target="tpu_custom_call" | custom-call | flops 5000000000 | bytes 5000000 | tf_op jit(solution)/shard_map/head/pallas_call | solution.py:43
  21.3 0.0 collective-permute-done.8.rest_3_
  21.3 0.0 collective-permute-done.7.rest_2_
  21.3 0.0 collective-permute-done.6.rest_1_
  21.3 1.6 %back.1 = (bf16[6,336,256]{2,1,0:T(8,128)(2,1)S(1)}, bf16[6,256,128]{2,1,0:T(8,128)(2,1)S(1)}, bf16[6,256,128]{2,1,0:T(8,128)(2,1)S(1)}, f32[4,128]{1,0:T(4,128)S(1)}) custom-call(bf16[10,256,256]{2,1,0:T(8,128)(2,1)S(1)} %get-tuple-element.52.hid_ref, f32[8,256,128]{2,1,0:T(8,128)S(1)} %get-tuple-element.53.dz_ref, ...), custom_call_target="tpu_custom_call" | custom-call | flops 4000000000 | bytes 4000000 | tf_op jit(solution)/shard_map/back/pallas_call | solution.py:43
  23.0 0.6 collective-permute-start.9
  23.5 1.0 %cls.1 = (f32[896,128]{1,0:T(8,128)S(1)}, f32[896,128]{1,0:T(8,128)S(1)}) custom-call(bf16[10,256,256]{2,1,0:T(8,128)(2,1)S(1)} %get-tuple-element.52.hid_ref, bf16[6,336,256]{2,1,0:T(8,128)(2,1)S(1)} %get-tuple-element.60.dt_ref), custom_call_target="tpu_custom_call" | custom-call | flops 1500000000 | bytes 1500000 | tf_op jit(solution)/shard_map/cls/pallas_call | solution.py:43
  24.5 0.1 collective-permute-start.10
  24.6 0.3 collective-permute-done.9.other_ref
  24.9 0.0 collective-permute-done.4.far_ref
  24.9 0.1 copy-done
  24.9 3.4 %shared.1 = (f32[1152,128]{1,0:T(8,128)S(1)}, bf16[1152,128]{1,0:T(8,128)(2,1)S(1)}) custom-call(bf16[12,256,256]{2,1,0:T(8,128)(2,1)S(1)} %bitcast.13, bf16[784,256]{1,0:T(8,128)(2,1)S(1)} %collective-permute-done.halo_ref, bf16[784,256]{1,0:T(8,128)(2,1)S(1)} %collective-permute-done.4.far_ref, bf16[6,256,128]{2,1,0:T(8,128)(2,1)S(1)} %get-tuple-element.56.own_ref, ...), custom_call_target="tpu_custom_call" | custom-call | flops 4000000000 | bytes 4000000 | tf_op jit(solution)/shard_map/shared/pallas_call | solution.py:43
  28.4 1.2 %collective-permute-start.11 = (bf16[1152,128]{1,0:T(8,128)(2,1)S(1)}, bf16[1152,128]{1,0:T(8,128)(2,1)S(1)}, u32[]{:S(2)}, u32[]{:S(2)}) collective-permute-start(bf16[1152,128]{1,0:T(8,128)(2,1)S(1)} %get-tuple-element.64), channel_id=1, source_target_pairs={{0,2},{2,0},{1,3},{3,1},{4,6},{6,4},{5,7},{7,5},{8,10},{10,8},{9,1... | collective-permute-start | bytes 884744 | tf_op jit(solution)/shard_map/ppermute | solution.py:420
  29.6 0.1 cls_split.1
  29.7 3.0 %collective-permute-start.12 = (bf16[240,128]{1,0:T(8,128)(2,1)S(1)}, bf16[240,128]{1,0:T(8,128)(2,1)S(1)}, u32[]{:S(2)}, u32[]{:S(2)}) collective-permute-start(bf16[240,128]{1,0:T(8,128)(2,1)S(1)} %get-tuple-element.65), channel_id=1, source_target_pairs={{0,12},{4,8},{8,4},{12,0},{1,13},{5,9},{9,5},{13,1},{2,14},{6,10},... | collective-permute-start | bytes 184328 | tf_op jit(solution)/shard_map/ppermute | solution.py:420
  32.6 0.0 collective-permute-start.13
  32.6 1.5 %collective-permute-start.14 = (bf16[240,128]{1,0:T(8,128)(2,1)S(1)}, bf16[240,128]{1,0:T(8,128)(2,1)S(1)}, u32[]{:S(2)}, u32[]{:S(2)}) collective-permute-start(bf16[240,128]{1,0:T(8,128)(2,1)S(1)} %get-tuple-element.67), channel_id=1, source_target_pairs={{0,4},{4,0},{8,12},{12,8},{1,5},{5,1},{9,13},{13,9},{2,6},{6,2},{1... | collective-permute-start | bytes 184328 | tf_op jit(solution)/shard_map/ppermute | solution.py:420
  34.1 2.1 %collective-permute-done.12.refs_1_ = bf16[240,128]{1,0:T(8,128)(2,1)S(1)} collective-permute-done((bf16[240,128]{1,0:T(8,128)(2,1)S(1)}, bf16[240,128]{1,0:T(8,128)(2,1)S(1)}, u32[]{:S(2)}, u32[]{:S(2)}) %collective-permute-start.12) | collective-permute-done | bytes 61472 | tf_op jit(solution)/shard_map/ppermute | solution.py:420
  36.2 2.0 %collective-permute-done.13.refs_2_ = bf16[240,128]{1,0:T(8,128)(2,1)S(1)} collective-permute-done((bf16[240,128]{1,0:T(8,128)(2,1)S(1)}, bf16[240,128]{1,0:T(8,128)(2,1)S(1)}, u32[]{:S(2)}, u32[]{:S(2)}) %collective-permute-start.13) | collective-permute-done | bytes 61472 | tf_op jit(solution)/shard_map/ppermute | solution.py:420
  38.2 0.1 collective-permute-done.14.refs_3_
  38.3 0.0 collective-permute-done.11.refs_0_
  38.3 0.1 sum.1
  38.4 2.6 %collective-permute-start.15 = (bf16[288,128]{1,0:T(8,128)(2,1)S(1)}, bf16[288,128]{1,0:T(8,128)(2,1)S(1)}, u32[]{:S(2)}, u32[]{:S(2)}) collective-permute-start(bf16[288,128]{1,0:T(8,128)(2,1)S(1)} %get-tuple-element.71), channel_id=1, source_target_pairs={{0,12},{4,8},{8,4},{12,0},{1,13},{5,9},{9,5},{13,1},{2,14},{6,10},... | collective-permute-start | bytes 221192 | tf_op jit(solution)/shard_map/ppermute | solution.py:420
  41.0 0.0 collective-permute-start.16
  41.0 1.9 %collective-permute-start.17 = (bf16[288,128]{1,0:T(8,128)(2,1)S(1)}, bf16[288,128]{1,0:T(8,128)(2,1)S(1)}, u32[]{:S(2)}, u32[]{:S(2)}) collective-permute-start(bf16[288,128]{1,0:T(8,128)(2,1)S(1)} %get-tuple-element.73), channel_id=1, source_target_pairs={{0,4},{4,0},{8,12},{12,8},{1,5},{5,1},{9,13},{13,9},{2,6},{6,2},{1... | collective-permute-start | bytes 221192 | tf_op jit(solution)/shard_map/ppermute | solution.py:420
  42.9 0.9 %collective-permute-start.18 = (bf16[128,128]{1,0:T(8,128)(2,1)S(1)}, bf16[128,128]{1,0:T(8,128)(2,1)S(1)}, u32[]{:S(2)}, u32[]{:S(2)}) collective-permute-start(bf16[128,128]{1,0:T(8,128)(2,1)S(1)} %get-tuple-element.74), channel_id=1, source_target_pairs={{0,2},{2,0},{1,3},{3,1},{4,6},{6,4},{5,7},{7,5},{8,10},{10,8},{9,1... | collective-permute-start | bytes 98312 | tf_op jit(solution)/shard_map/ppermute | solution.py:420
  43.8 3.0 %collective-permute-done.18.refs_3_ = bf16[128,128]{1,0:T(8,128)(2,1)S(1)} collective-permute-done((bf16[128,128]{1,0:T(8,128)(2,1)S(1)}, bf16[128,128]{1,0:T(8,128)(2,1)S(1)}, u32[]{:S(2)}, u32[]{:S(2)}) %collective-permute-start.18) | collective-permute-done | bytes 32800 | tf_op jit(solution)/shard_map/ppermute | solution.py:420
  46.8 1.2 %collective-permute-done.16.refs_1_ = bf16[288,128]{1,0:T(8,128)(2,1)S(1)} collective-permute-done((bf16[288,128]{1,0:T(8,128)(2,1)S(1)}, bf16[288,128]{1,0:T(8,128)(2,1)S(1)}, u32[]{:S(2)}, u32[]{:S(2)}) %collective-permute-start.16) | collective-permute-done | bytes 73760 | tf_op jit(solution)/shard_map/ppermute | solution.py:420
  48.0 0.0 collective-permute-done.17.refs_2_
  48.1 2.0 %collective-permute-start.22 = (bf16[288,128]{1,0:T(8,128)(2,1)S(1)}, bf16[288,128]{1,0:T(8,128)(2,1)S(1)}, u32[]{:S(2)}, u32[]{:S(2)}) collective-permute-start(bf16[288,128]{1,0:T(8,128)(2,1)S(1)} %get-tuple-element.76.refs_0_), channel_id=1, source_target_pairs={{0,12},{4,8},{8,4},{12,0},{1,13},{5,9},{9,5},{13,1},{2,14},{6,10},... | collective-permute-start | bytes 221192 | tf_op jit(solution)/shard_map/ppermute | solution.py:420
  50.1 0.0 collective-permute-start.21
  50.1 2.4 %collective-permute-start.20 = (bf16[288,128]{1,0:T(8,128)(2,1)S(1)}, bf16[288,128]{1,0:T(8,128)(2,1)S(1)}, u32[]{:S(2)}, u32[]{:S(2)}) collective-permute-start(bf16[288,128]{1,0:T(8,128)(2,1)S(1)} %get-tuple-element.76.refs_0_), channel_id=1, source_target_pairs={{0,4},{4,0},{8,12},{12,8},{1,5},{5,1},{9,13},{13,9},{2,6},{6,2},{1... | collective-permute-start | bytes 221192 | tf_op jit(solution)/shard_map/ppermute | solution.py:420
  52.5 0.9 %collective-permute-start.23 = (bf16[112,128]{1,0:T(8,128)(2,1)S(1)}, bf16[112,128]{1,0:T(8,128)(2,1)S(1)}, u32[]{:S(2)}, u32[]{:S(2)}) collective-permute-start(bf16[112,128]{1,0:T(8,128)(2,1)S(1)} %get-tuple-element.77.refs_4_), channel_id=1, source_target_pairs={{0,2},{2,0},{1,3},{3,1},{4,6},{6,4},{5,7},{7,5},{8,10},{10,8},{9,1... | collective-permute-start | bytes 86024 | tf_op jit(solution)/shard_map/ppermute | solution.py:420
  53.4 3.0 %collective-permute-done.23.refs_5_ = bf16[112,128]{1,0:T(8,128)(2,1)S(1)} collective-permute-done((bf16[112,128]{1,0:T(8,128)(2,1)S(1)}, bf16[112,128]{1,0:T(8,128)(2,1)S(1)}, u32[]{:S(2)}, u32[]{:S(2)}) %collective-permute-start.23) | collective-permute-done | bytes 28704 | tf_op jit(solution)/shard_map/ppermute | solution.py:420
  56.4 0.4 collective-permute-done.21.refs_2_
  56.8 0.0 collective-permute-done.20.refs_1_
  56.8 0.9 %collective-permute-start.24 = (bf16[1152,128]{1,0:T(8,128)(2,1)S(1)}, bf16[1152,128]{1,0:T(8,128)(2,1)S(1)}, u32[]{:S(2)}, u32[]{:S(2)}) collective-permute-start(bf16[1152,128]{1,0:T(8,128)(2,1)S(1)} %get-tuple-element.78.refs_0_), channel_id=1, source_target_pairs={{0,2},{2,0},{1,3},{3,1},{4,6},{6,4},{5,7},{7,5},{8,10},{10,8},{9,1... | collective-permute-start | bytes 884744 | tf_op jit(solution)/shard_map/ppermute | solution.py:420
  57.8 2.5 %collective-permute-start.27 = (bf16[224,128]{1,0:T(8,128)(2,1)S(1)}, bf16[224,128]{1,0:T(8,128)(2,1)S(1)}, u32[]{:S(2)}, u32[]{:S(2)}) collective-permute-start(bf16[224,128]{1,0:T(8,128)(2,1)S(1)} %get-tuple-element.79.refs_2_), channel_id=1, source_target_pairs={{0,12},{4,8},{8,4},{12,0},{1,13},{5,9},{9,5},{13,1},{2,14},{6,10},... | collective-permute-start | bytes 172040 | tf_op jit(solution)/shard_map/ppermute | solution.py:420
  60.3 0.0 collective-permute-start.26
  60.3 1.9 %collective-permute-start.25 = (bf16[224,128]{1,0:T(8,128)(2,1)S(1)}, bf16[224,128]{1,0:T(8,128)(2,1)S(1)}, u32[]{:S(2)}, u32[]{:S(2)}) collective-permute-start(bf16[224,128]{1,0:T(8,128)(2,1)S(1)} %get-tuple-element.79.refs_2_), channel_id=1, source_target_pairs={{0,4},{4,0},{8,12},{12,8},{1,5},{5,1},{9,13},{13,9},{2,6},{6,2},{1... | collective-permute-start | bytes 172040 | tf_op jit(solution)/shard_map/ppermute | solution.py:420
  62.1 1.2 %collective-permute-done.19.theirs_ref = f32[4,128]{1,0:T(4,128)S(1)} collective-permute-done((f32[4,128]{1,0:T(4,128)S(1)}, f32[4,128]{1,0:T(4,128)S(1)}, u32[]{:S(2)}, u32[]{:S(2)}) %collective-permute-start.19) | collective-permute-done | bytes 2080 | tf_op jit(solution)/shard_map/ppermute | solution.py:420
  63.3 0.5 collective-permute-done.27.refs_5_
  63.8 2.0 %collective-permute-done.26.refs_4_ = bf16[224,128]{1,0:T(8,128)(2,1)S(1)} collective-permute-done((bf16[224,128]{1,0:T(8,128)(2,1)S(1)}, bf16[224,128]{1,0:T(8,128)(2,1)S(1)}, u32[]{:S(2)}, u32[]{:S(2)}) %collective-permute-start.26) | collective-permute-done | bytes 57376 | tf_op jit(solution)/shard_map/ppermute | solution.py:420
  65.8 0.0 collective-permute-done.25.refs_3_
  65.8 0.0 collective-permute-done.24.refs_1_
  65.8 1.3 %out.1 = (f32[2304,128]{1,0:T(8,128)}, f32[1,128]{1,0:T(1,128)}, f32[3,3,99,128]{3,2,1,0:T(8,128)}, f32[1,99]{1,0:T(1,128)}, f32[1,1]{1,0:T(1,128)}) custom-call(f32[4,128]{1,0:T(4,128)S(1)} %get-tuple-element.75.small_ref, f32[4,128]{1,0:T(4,128)S(1)} %collective-permute-done.19.theirs_ref, bf16[1152,128]{1,0:T(8,128)(2,1)S(1)} %get-tuple-element.78.refs_0_, ...), custom_call_target="tpu_custom_call" | custom-call | flops 1500000000 | bytes 1500000 | tf_op jit(solution)/shard_map/out/pallas_call | solution.py:43
  (16 shorter events, 0.1 us)
Async XLA Ops:
  0.6 9.7 %collective-permute-start.1 = (bf16[3,3,256,128]{3,2,1,0:T(8,128)(2,1)}, bf16[3,3,256,128]{3,2,1,0:T(8,128)(2,1)S(1)}, u32[]{:S(2)}, u32[]{:S(2)}) collective-permute-start(bf16[3,3,256,128]{3,2,1,0:T(8,128)(2,1)} %w1a_ref.3), channel_id=1, source_target_pairs={{0,1},{1,0},{2,3},{3,2},{4,5},{5,4},{6,7},{7,6},{8,9},{9,8},{10,11... | collective-permute-start | bytes 1769480 | tf_op jit(solution)/shard_map/ppermute | solution.py:420
  1.2 0.9 %copy-start.3 = (s32[1,12,2304]{2,0,1:T(1,128)S(1)}, s32[1,12,2304]{2,0,1:T(1,128)}, u32[]{:S(2)}) copy-start(s32[1,12,2304]{2,0,1:T(1,128)} %param.7) | copy-start | bytes 331780
  2.0 2.7 %copy-start.4 = (f32[128]{0:T(128)S(1)}, f32[128]{0:T(128)}, u32[]{:S(2)}) copy-start(f32[128]{0:T(128)} %param.9) | copy-start | bytes 1540
  2.0 6.7 %copy-start.2 = (bf16[3,3,128,99]{2,3,1,0:T(8,128)(2,1)S(1)}, bf16[3,3,128,99]{2,3,1,0:T(8,128)(2,1)}, u32[]{:S(2)}) copy-start(bf16[3,3,128,99]{2,3,1,0:T(8,128)(2,1)} %param.10) | copy-start | bytes 684292
  2.1 8.3 %copy-start.1 = (bf16[3,3,256,128]{3,2,1,0:T(8,128)(2,1)S(1)}, bf16[3,3,256,128]{3,2,1,0:T(8,128)(2,1)}, u32[]{:S(2)}) copy-start(bf16[3,3,256,128]{3,2,1,0:T(8,128)(2,1)} %w1a_ref.3) | copy-start | bytes 1769476
  4.1 13.2 %collective-permute-start = (bf16[784,256]{1,0:T(8,128)(2,1)S(1)}, bf16[784,256]{1,0:T(8,128)(2,1)S(1)}, u32[]{:S(2)}, u32[]{:S(2)}) collective-permute-start(bf16[784,256]{1,0:T(8,128)(2,1)S(1)} %get-tuple-element.45), channel_id=1, source_target_pairs={{1,4},{4,1},{5,8},{8,5},{9,12},{12,9},{3,6},{6,3},{7,10},{10,7},{1... | collective-permute-start | bytes 1204232 | tf_op jit(solution)/shard_map/ppermute | solution.py:464
  4.8 5.6 %collective-permute-start.2 = (f32[128]{0:T(128)S(1)}, f32[128]{0:T(128)S(1)}, u32[]{:S(2)}, u32[]{:S(2)}) collective-permute-start(f32[128]{0:T(128)S(1)} %copy-done.4), channel_id=1, source_target_pairs={{0,1},{1,0},{2,3},{3,2},{4,5},{5,4},{6,7},{7,6},{8,9},{9,8},{10,11... | collective-permute-start | bytes 1544 | tf_op jit(solution)/shard_map/ppermute | solution.py:420
  8.8 8.5 %collective-permute-start.5 = (bf16[3,3,128,99]{2,3,1,0:T(8,128)(2,1)S(1)}, bf16[3,3,128,99]{2,3,1,0:T(8,128)(2,1)S(1)}, u32[]{:S(2)}, u32[]{:S(2)}) collective-permute-start(bf16[3,3,128,99]{2,3,1,0:T(8,128)(2,1)S(1)} %copy-done.2), channel_id=1, source_target_pairs={{0,1},{1,0},{2,3},{3,2},{4,5},{5,4},{6,7},{7,6},{8,9},{9,8},{10,11... | collective-permute-start | bytes 684296 | tf_op jit(solution)/shard_map/ppermute | solution.py:420
  8.9 3.9 %collective-permute-start.3 = (f32[8,128]{1,0:T(8,128)S(1)}, f32[8,128]{1,0:T(8,128)S(1)}, u32[]{:S(2)}, u32[]{:S(2)}) collective-permute-start(f32[8,128]{1,0:T(8,128)S(1)} %get-tuple-element.46), channel_id=1, source_target_pairs={{0,2},{2,0},{1,3},{3,1},{4,6},{6,4},{5,7},{7,5},{8,10},{10,8},{9,1... | collective-permute-start | bytes 12296 | tf_op jit(solution)/shard_map/ppermute | solution.py:420
  10.4 6.9 %copy-start.5 = (f32[99]{0:T(128)S(1)}, f32[99]{0:T(128)}, u32[]{:S(2)}) copy-start(f32[99]{0:T(128)} %param.11) | copy-start | bytes 1192
  12.8 8.5 %collective-permute-start.8 = (f32[8,128]{1,0:T(8,128)S(1)}, f32[8,128]{1,0:T(8,128)S(1)}, u32[]{:S(2)}, u32[]{:S(2)}) collective-permute-start(f32[8,128]{1,0:T(8,128)S(1)} %add.3.rest_0_), channel_id=1, source_target_pairs={{0,12},{4,8},{8,4},{12,0},{1,13},{5,9},{9,5},{13,1},{2,14},{6,10},... | collective-permute-start | bytes 12296 | tf_op jit(solution)/shard_map/ppermute | solution.py:420
  15.7 5.6 %collective-permute-start.7 = (f32[8,128]{1,0:T(8,128)S(1)}, f32[8,128]{1,0:T(8,128)S(1)}, u32[]{:S(2)}, u32[]{:S(2)}) collective-permute-start(f32[8,128]{1,0:T(8,128)S(1)} %add.3.rest_0_), channel_id=1, source_target_pairs={{0,8},{4,12},{8,0},{12,4},{1,9},{5,13},{9,1},{13,5},{2,10},{6,14},... | collective-permute-start | bytes 12296 | tf_op jit(solution)/shard_map/ppermute | solution.py:420
  15.9 5.4 %collective-permute-start.6 = (f32[8,128]{1,0:T(8,128)S(1)}, f32[8,128]{1,0:T(8,128)S(1)}, u32[]{:S(2)}, u32[]{:S(2)}) collective-permute-start(f32[8,128]{1,0:T(8,128)S(1)} %add.3.rest_0_), channel_id=1, source_target_pairs={{0,4},{4,0},{8,12},{12,8},{1,5},{5,1},{9,13},{13,9},{2,6},{6,2},{1... | collective-permute-start | bytes 12296 | tf_op jit(solution)/shard_map/ppermute | solution.py:420
  17.2 7.6 %collective-permute-start.4 = (bf16[784,256]{1,0:T(8,128)(2,1)S(1)}, bf16[784,256]{1,0:T(8,128)(2,1)S(1)}, u32[]{:S(2)}, u32[]{:S(2)}) collective-permute-start(bf16[784,256]{1,0:T(8,128)(2,1)S(1)} %collective-permute-done.halo_ref), channel_id=1, source_target_pairs={{0,1},{1,0},{2,3},{3,2},{4,5},{5,4},{6,7},{7,6},{8,9},{9,8},{10,11... | collective-permute-start | bytes 1204232 | tf_op jit(solution)/shard_map/ppermute | solution.py:420
  23.0 1.9 %collective-permute-start.9 = (bf16[6,256,128]{2,1,0:T(8,128)(2,1)S(1)}, bf16[6,256,128]{2,1,0:T(8,128)(2,1)S(1)}, u32[]{:S(2)}, u32[]{:S(2)}) collective-permute-start(bf16[6,256,128]{2,1,0:T(8,128)(2,1)S(1)} %get-tuple-element.57), channel_id=1, source_target_pairs={{0,1},{1,0},{2,3},{3,2},{4,5},{5,4},{6,7},{7,6},{8,9},{9,8},{10,11... | collective-permute-start | bytes 1179656 | tf_op jit(solution)/shard_map/ppermute | solution.py:420
  23.5 1.4 %copy-start = (bf16[1,12,256,256]{3,2,1,0:T(8,128)(2,1)S(1)}, bf16[1,12,256,256]{3,2,1,0:T(8,128)(2,1)}, u32[]{:S(2)}) copy-start(bf16[1,12,256,256]{3,2,1,0:T(8,128)(2,1)} %param.6) | copy-start | bytes 4718596
  24.5 5.1 %collective-permute-start.10 = (f32[896,128]{1,0:T(8,128)S(1)}, f32[896,128]{1,0:T(8,128)S(1)}, u32[]{:S(2)}, u32[]{:S(2)}) collective-permute-start(f32[896,128]{1,0:T(8,128)S(1)} %get-tuple-element.62), channel_id=1, source_target_pairs={{0,1},{1,0},{2,3},{3,2},{4,5},{5,4},{6,7},{7,6},{8,9},{9,8},{10,11... | collective-permute-start | bytes 1376264 | tf_op jit(solution)/shard_map/ppermute | solution.py:420
  28.4 9.9 %collective-permute-start.11 = (bf16[1152,128]{1,0:T(8,128)(2,1)S(1)}, bf16[1152,128]{1,0:T(8,128)(2,1)S(1)}, u32[]{:S(2)}, u32[]{:S(2)}) collective-permute-start(bf16[1152,128]{1,0:T(8,128)(2,1)S(1)} %get-tuple-element.64), channel_id=1, source_target_pairs={{0,2},{2,0},{1,3},{3,1},{4,6},{6,4},{5,7},{7,5},{8,10},{10,8},{9,1... | collective-permute-start | bytes 884744 | tf_op jit(solution)/shard_map/ppermute | solution.py:420
  29.7 6.5 %collective-permute-start.12 = (bf16[240,128]{1,0:T(8,128)(2,1)S(1)}, bf16[240,128]{1,0:T(8,128)(2,1)S(1)}, u32[]{:S(2)}, u32[]{:S(2)}) collective-permute-start(bf16[240,128]{1,0:T(8,128)(2,1)S(1)} %get-tuple-element.65), channel_id=1, source_target_pairs={{0,12},{4,8},{8,4},{12,0},{1,13},{5,9},{9,5},{13,1},{2,14},{6,10},... | collective-permute-start | bytes 184328 | tf_op jit(solution)/shard_map/ppermute | solution.py:420
  32.6 5.6 %collective-permute-start.13 = (bf16[240,128]{1,0:T(8,128)(2,1)S(1)}, bf16[240,128]{1,0:T(8,128)(2,1)S(1)}, u32[]{:S(2)}, u32[]{:S(2)}) collective-permute-start(bf16[240,128]{1,0:T(8,128)(2,1)S(1)} %get-tuple-element.66), channel_id=1, source_target_pairs={{0,8},{4,12},{8,0},{12,4},{1,9},{5,13},{9,1},{13,5},{2,10},{6,14},... | collective-permute-start | bytes 184328 | tf_op jit(solution)/shard_map/ppermute | solution.py:420
  32.6 5.7 %collective-permute-start.14 = (bf16[240,128]{1,0:T(8,128)(2,1)S(1)}, bf16[240,128]{1,0:T(8,128)(2,1)S(1)}, u32[]{:S(2)}, u32[]{:S(2)}) collective-permute-start(bf16[240,128]{1,0:T(8,128)(2,1)S(1)} %get-tuple-element.67), channel_id=1, source_target_pairs={{0,4},{4,0},{8,12},{12,8},{1,5},{5,1},{9,13},{13,9},{2,6},{6,2},{1... | collective-permute-start | bytes 184328 | tf_op jit(solution)/shard_map/ppermute | solution.py:420
  38.4 8.4 %collective-permute-start.15 = (bf16[288,128]{1,0:T(8,128)(2,1)S(1)}, bf16[288,128]{1,0:T(8,128)(2,1)S(1)}, u32[]{:S(2)}, u32[]{:S(2)}) collective-permute-start(bf16[288,128]{1,0:T(8,128)(2,1)S(1)} %get-tuple-element.71), channel_id=1, source_target_pairs={{0,12},{4,8},{8,4},{12,0},{1,13},{5,9},{9,5},{13,1},{2,14},{6,10},... | collective-permute-start | bytes 221192 | tf_op jit(solution)/shard_map/ppermute | solution.py:420
  41.0 7.0 %collective-permute-start.16 = (bf16[288,128]{1,0:T(8,128)(2,1)S(1)}, bf16[288,128]{1,0:T(8,128)(2,1)S(1)}, u32[]{:S(2)}, u32[]{:S(2)}) collective-permute-start(bf16[288,128]{1,0:T(8,128)(2,1)S(1)} %get-tuple-element.72), channel_id=1, source_target_pairs={{0,8},{4,12},{8,0},{12,4},{1,9},{5,13},{9,1},{13,5},{2,10},{6,14},... | collective-permute-start | bytes 221192 | tf_op jit(solution)/shard_map/ppermute | solution.py:420
  41.0 7.0 %collective-permute-start.17 = (bf16[288,128]{1,0:T(8,128)(2,1)S(1)}, bf16[288,128]{1,0:T(8,128)(2,1)S(1)}, u32[]{:S(2)}, u32[]{:S(2)}) collective-permute-start(bf16[288,128]{1,0:T(8,128)(2,1)S(1)} %get-tuple-element.73), channel_id=1, source_target_pairs={{0,4},{4,0},{8,12},{12,8},{1,5},{5,1},{9,13},{13,9},{2,6},{6,2},{1... | collective-permute-start | bytes 221192 | tf_op jit(solution)/shard_map/ppermute | solution.py:420
  42.9 3.9 %collective-permute-start.18 = (bf16[128,128]{1,0:T(8,128)(2,1)S(1)}, bf16[128,128]{1,0:T(8,128)(2,1)S(1)}, u32[]{:S(2)}, u32[]{:S(2)}) collective-permute-start(bf16[128,128]{1,0:T(8,128)(2,1)S(1)} %get-tuple-element.74), channel_id=1, source_target_pairs={{0,2},{2,0},{1,3},{3,1},{4,6},{6,4},{5,7},{7,5},{8,10},{10,8},{9,1... | collective-permute-start | bytes 98312 | tf_op jit(solution)/shard_map/ppermute | solution.py:420
  48.1 8.3 %collective-permute-start.22 = (bf16[288,128]{1,0:T(8,128)(2,1)S(1)}, bf16[288,128]{1,0:T(8,128)(2,1)S(1)}, u32[]{:S(2)}, u32[]{:S(2)}) collective-permute-start(bf16[288,128]{1,0:T(8,128)(2,1)S(1)} %get-tuple-element.76.refs_0_), channel_id=1, source_target_pairs={{0,12},{4,8},{8,4},{12,0},{1,13},{5,9},{9,5},{13,1},{2,14},{6,10},... | collective-permute-start | bytes 221192 | tf_op jit(solution)/shard_map/ppermute | solution.py:420
  50.1 6.7 %collective-permute-start.21 = (bf16[288,128]{1,0:T(8,128)(2,1)S(1)}, bf16[288,128]{1,0:T(8,128)(2,1)S(1)}, u32[]{:S(2)}, u32[]{:S(2)}) collective-permute-start(bf16[288,128]{1,0:T(8,128)(2,1)S(1)} %get-tuple-element.76.refs_0_), channel_id=1, source_target_pairs={{0,8},{4,12},{8,0},{12,4},{1,9},{5,13},{9,1},{13,5},{2,10},{6,14},... | collective-permute-start | bytes 221192 | tf_op jit(solution)/shard_map/ppermute | solution.py:420
  50.1 6.7 %collective-permute-start.20 = (bf16[288,128]{1,0:T(8,128)(2,1)S(1)}, bf16[288,128]{1,0:T(8,128)(2,1)S(1)}, u32[]{:S(2)}, u32[]{:S(2)}) collective-permute-start(bf16[288,128]{1,0:T(8,128)(2,1)S(1)} %get-tuple-element.76.refs_0_), channel_id=1, source_target_pairs={{0,4},{4,0},{8,12},{12,8},{1,5},{5,1},{9,13},{13,9},{2,6},{6,2},{1... | collective-permute-start | bytes 221192 | tf_op jit(solution)/shard_map/ppermute | solution.py:420
  52.5 3.9 %collective-permute-start.23 = (bf16[112,128]{1,0:T(8,128)(2,1)S(1)}, bf16[112,128]{1,0:T(8,128)(2,1)S(1)}, u32[]{:S(2)}, u32[]{:S(2)}) collective-permute-start(bf16[112,128]{1,0:T(8,128)(2,1)S(1)} %get-tuple-element.77.refs_4_), channel_id=1, source_target_pairs={{0,2},{2,0},{1,3},{3,1},{4,6},{6,4},{5,7},{7,5},{8,10},{10,8},{9,1... | collective-permute-start | bytes 86024 | tf_op jit(solution)/shard_map/ppermute | solution.py:420
  56.8 9.0 %collective-permute-start.24 = (bf16[1152,128]{1,0:T(8,128)(2,1)S(1)}, bf16[1152,128]{1,0:T(8,128)(2,1)S(1)}, u32[]{:S(2)}, u32[]{:S(2)}) collective-permute-start(bf16[1152,128]{1,0:T(8,128)(2,1)S(1)} %get-tuple-element.78.refs_0_), channel_id=1, source_target_pairs={{0,2},{2,0},{1,3},{3,1},{4,6},{6,4},{5,7},{7,5},{8,10},{10,8},{9,1... | collective-permute-start | bytes 884744 | tf_op jit(solution)/shard_map/ppermute | solution.py:420
  57.8 6.1 %collective-permute-start.27 = (bf16[224,128]{1,0:T(8,128)(2,1)S(1)}, bf16[224,128]{1,0:T(8,128)(2,1)S(1)}, u32[]{:S(2)}, u32[]{:S(2)}) collective-permute-start(bf16[224,128]{1,0:T(8,128)(2,1)S(1)} %get-tuple-element.79.refs_2_), channel_id=1, source_target_pairs={{0,12},{4,8},{8,4},{12,0},{1,13},{5,9},{9,5},{13,1},{2,14},{6,10},... | collective-permute-start | bytes 172040 | tf_op jit(solution)/shard_map/ppermute | solution.py:420
  60.3 5.5 %collective-permute-start.26 = (bf16[224,128]{1,0:T(8,128)(2,1)S(1)}, bf16[224,128]{1,0:T(8,128)(2,1)S(1)}, u32[]{:S(2)}, u32[]{:S(2)}) collective-permute-start(bf16[224,128]{1,0:T(8,128)(2,1)S(1)} %get-tuple-element.79.refs_2_), channel_id=1, source_target_pairs={{0,8},{4,12},{8,0},{12,4},{1,9},{5,13},{9,1},{13,5},{2,10},{6,14},... | collective-permute-start | bytes 172040 | tf_op jit(solution)/shard_map/ppermute | solution.py:420
  60.3 5.5 %collective-permute-start.25 = (bf16[224,128]{1,0:T(8,128)(2,1)S(1)}, bf16[224,128]{1,0:T(8,128)(2,1)S(1)}, u32[]{:S(2)}, u32[]{:S(2)}) collective-permute-start(bf16[224,128]{1,0:T(8,128)(2,1)S(1)} %get-tuple-element.79.refs_2_), channel_id=1, source_target_pairs={{0,4},{4,0},{8,12},{12,8},{1,5},{5,1},{9,13},{13,9},{2,6},{6,2},{1... | collective-permute-start | bytes 172040 | tf_op jit(solution)/shard_map/ppermute | solution.py:420
  62.1 1.2 %collective-permute-start.19 = (f32[4,128]{1,0:T(4,128)S(1)}, f32[4,128]{1,0:T(4,128)S(1)}, u32[]{:S(2)}, u32[]{:S(2)}) collective-permute-start(f32[4,128]{1,0:T(4,128)S(1)} %get-tuple-element.75.small_ref), channel_id=1, source_target_pairs={{0,1},{1,0},{2,3},{3,2},{4,5},{5,4},{6,7},{7,6},{8,9},{9,8},{10,11... | collective-permute-start | bytes 6152 | tf_op jit(solution)/shard_map/ppermute | solution.py:420

commit v9 on v8

--- a/solution.py
+++ b/solution.py
@@ -140,13 +140,14 @@
             yield shift_cells(y[:, :width], 1) + y[:, width : 2 * width] + shift_cells(y[:, 2 * width :], -1) + b1
 
 
-def inner_kernel(where_ref, near_ref, w1a_ref, w1b_ref, b1a_ref, b1b_ref, out_ref):
-    for k, pre in enumerate(hidden_rows(near_ref, w1a_ref, w1b_ref, b1a_ref, b1b_ref)):
+def inner_kernel(start, where_ref, near_ref, w1a_ref, w1b_ref, b1a_ref, b1b_ref, out_ref):
+    some = near_ref.at[start : start + out_ref.shape[0] + 2]
+    for k, pre in enumerate(hidden_rows(some, w1a_ref, w1b_ref, b1a_ref, b1b_ref)):
         out_ref[k] = jnp.maximum(pre, 0.0).astype(BF16)
 
 
 def head_kernel(
-    where_ref, near_ref, inner_ref, halo_ref, labt_ref, w1a_ref, w1b_ref, b1a_ref, b1b_ref, w2a_ref, w2b_ref, b2_ref,
+    where_ref, near_ref, inner_ref, later_ref, halo_ref, labt_ref, w1a_ref, w1b_ref, b1a_ref, b1b_ref, w2a_ref, w2b_ref, b2_ref,
     hid_ref, dz_ref, loss_ref, w2_ref, xw_ref,
 ):
     near = near_ref.shape[0]
@@ -158,7 +159,9 @@
     xw_ref[pl.ds(3 - 3 * c, 2)] = near_ref[pl.ds((near - 2) * c, 2)]
     for k in range(3):
         xw_ref[2 * c + k] = halo_ref[cols * k : cols * (k + 1)]
-    hid_ref[pl.ds(3 - 3 * c, near - 2)] = inner_ref[...]
+    early = inner_ref.shape[0]
+    hid_ref[pl.ds(3 - 3 * c, early)] = inner_ref[...]
+    hid_ref[pl.ds(3 - 3 * c + early, later_ref.shape[0])] = later_ref[...]
     for k, pre in enumerate(hidden_rows(xw_ref, w1a_ref, w1b_ref, b1a_ref, b1b_ref)):
         h = (near - 2) * c + k
         row = first + h - 2
@@ -304,18 +307,10 @@
     before = jnp.where(c == 0, near, far)
     after = jnp.where(c == 0, far, near)
 
-    def place(ref, start):
-        def body(d, carry):
-            mid = ref[d].astype(F32)
-            d_ref[start + d] = jnp.concatenate(
-                [shift_cells(mid, -1).astype(BF16), ref[d], shift_cells(mid, 1).astype(BF16)], axis=1
-            )
-            return carry
-
-        lax.fori_loop(0, half, body, 0, unroll=True)
-
-    place(own_ref, half * c)
-    place(other_ref, half * (1 - c))
+    for r in range(rows):
+        mine, theirs = own_ref[r % half].astype(F32), other_ref[r % half].astype(F32)
+        mid = jnp.where(c == (0 if r < half else 1), mine, theirs)
+        d_ref[r] = jnp.concatenate([shift_cells(mid, -1), mid, shift_cells(mid, 1)], axis=1).astype(BF16)
     outs = d_ref.shape[2] // 3
 
     def part(x, first):
@@ -467,16 +462,29 @@
     b1b = swap(b_shared, "chan")
 
     weights = [w_shared, w1b, b_shared.reshape(1, outs), b1b.reshape(1, outs)]
-    (inner,) = call(inner_kernel, "inner", 3, [((half + 1, cols, chans), BF16)], [where, near] + weights)
+    early = (half + 2) // 2
+
+    def rows_of(start, n, name):
+        kernel = functools.partial(inner_kernel, start)
+        return call(kernel, name, 1.3, [((n, cols, chans), BF16)], [where, near] + weights)[0]
+
+    inner = rows_of(0, early, "inner")
     inner, *met = lax.optimization_barrier((inner, *met))
     count = pair_sum([count] + met)
+    later = rows_of(early, half + 1 - early, "later")
+    bit = 1
+    while 2 * bit < tiles:
+        met = swap(count, "tile", bit)
+        later, met = lax.optimization_barrier((later, met))
+        count = count + met
+        bit *= 2
     halo, _ = lax.optimization_barrier((halo, count))
-    counts = [count] + others(count, "tile")
+    counts = [count, swap(count, "tile", bit)]
     hid, dz, loss, w2 = call(
         head_kernel, "head", 5,
         [((half + 4, cols, chans), BF16), ((half + 2, cols, LANES), F32), ((1, LANES), F32)]
         + [((9 * LANES, chans), BF16)],
-        [where, near, inner, halo, labt]
+        [where, near, inner, later, halo, labt]
         + weights
         + [jnp.swapaxes(w_cls, 2, 3), jnp.swapaxes(w2b, 2, 3), b_cls.reshape(1, LOGITS)],
         [((5, cols, chans), BF16)],

time: 67.3 us -> 68.8 us (1.022)
  waiting for transfers between devices: 15.8 us -> 18.2 us
    ppermute x27 -> x26, waiting for transfers between devices: 15.8 us -> 18.2 us  [swap(): return lax.ppermute(x, axis, [(i, i ^ bit) for i in range(size)])]
    ppermute x27 -> x26, starting transfers between devices: 32.8 us -> 32.2 us  [swap(): return lax.ppermute(x, axis, [(i, i ^ bit) for i in range(size)])]
    pallas_call x11 -> x12, Pallas kernels: 16 us -> 15.7 us  [call(): pl.pallas_call(functools.partial(kernel, inputs[0]), in_specs=(specs or [...]
  transfers between devices with their start and end apart: 28 -> 27, of which waited for: 11 -> 13; matrix products, arithmetic and copies ran while one was open for 0% -> 0% of each run, Pallas kernels for 22% -> 21%
where the time goes in v9:
time: 68.8 us; the launch traced here: 68.6 us
  starting transfers between devices  32.9 us (48%)
  waiting for transfers between devices  18.2 us (26%)
  Pallas kernels  15.7 us (23%)
  local copies, waits for them, and re-layouts  0.97 us (1%)
  between operations  0.77 us (1%)
    ppermute x26, starting transfers between devices, swap(): return lax.ppermute(x, axis, [(i, i ^ bit) for i in range(size)])  32.2 us
    ppermute x26, waiting for transfers between devices, swap(): return lax.ppermute(x, axis, [(i, i ^ bit) for i in range(size)])  18.2 us
    pallas_call x12, Pallas kernels, call(): pl.pallas_call(functools.partial(kernel, inputs[0]), in_specs=(specs or [...  15.7 us
  transfers between devices with their start and end apart: 27, of which 13 were waited for; matrix products, arithmetic and copies ran while one was open for 0% of the time, Pallas kernels for 21%

profile of v9, /device:TPU:0, one launch (start us, length us, event | category | flops | bytes accessed | tf_op | source)
XLA Modules:
  0.0 68.6 jit_solution(2229913669392362904)
XLA Ops:
  0.6 0.5 collective-permute-start.1
  1.2 0.9 %copy-done.3 = s32[1,12,2304]{2,0,1:T(1,128)S(1)} copy-done((s32[1,12,2304]{2,0,1:T(1,128)S(1)}, s32[1,12,2304]{2,0,1:T(1,128)}, u32[]{:S(2)}) %copy-start.3) | copy-done | bytes 110616
  2.1 2.0 %edge.1 = (bf16[784,256]{1,0:T(8,128)(2,1)S(1)}, bf16[12,16,256]{2,1,0:T(8,128)(2,1)S(1)}, f32[8,128]{1,0:T(8,128)S(1)}, bf16[9,256,256]{2,1,0:T(8,128)(2,1)S(1)}) custom-call(bf16[12,256,256]{2,1,0:T(8,128)(2,1)} %bitcast.12, s32[12,1,2304]{2,1,0:T(1,128)S(1)} %bitcast.16), custom_call_target="tpu_custom_call" | custom-call | flops 2000000000 | bytes 2000000 | tf_op jit(solution)/shard_map/edge/pallas_call | solution.py:43
  4.1 0.7 %collective-permute-start = (bf16[784,256]{1,0:T(8,128)(2,1)S(1)}, bf16[784,256]{1,0:T(8,128)(2,1)S(1)}, u32[]{:S(2)}, u32[]{:S(2)}) collective-permute-start(bf16[784,256]{1,0:T(8,128)(2,1)S(1)} %get-tuple-element.47), channel_id=1, source_target_pairs={{1,4},{4,1},{5,8},{8,5},{9,12},{12,9},{3,6},{6,3},{7,10},{10,7},{1... | collective-permute-start | bytes 1204232 | tf_op jit(solution)/shard_map/ppermute | solution.py:459
  4.8 4.0 %collective-permute-start.2 = (f32[128]{0:T(128)S(1)}, f32[128]{0:T(128)S(1)}, u32[]{:S(2)}, u32[]{:S(2)}) collective-permute-start(f32[128]{0:T(128)S(1)} %copy-done.4), channel_id=1, source_target_pairs={{0,1},{1,0},{2,3},{3,2},{4,5},{5,4},{6,7},{7,6},{8,9},{9,8},{10,11... | collective-permute-start | bytes 1544 | tf_op jit(solution)/shard_map/ppermute | solution.py:415
  8.8 0.1 collective-permute-start.6
  8.9 1.5 %collective-permute-start.3 = (f32[8,128]{1,0:T(8,128)S(1)}, f32[8,128]{1,0:T(8,128)S(1)}, u32[]{:S(2)}, u32[]{:S(2)}) collective-permute-start(f32[8,128]{1,0:T(8,128)S(1)} %get-tuple-element.48), channel_id=1, source_target_pairs={{0,2},{2,0},{1,3},{3,1},{4,6},{6,4},{5,7},{7,5},{8,10},{10,8},{9,1... | collective-permute-start | bytes 12296 | tf_op jit(solution)/shard_map/ppermute | solution.py:415
  10.4 0.0 collective-permute-done.2
  10.4 0.0 collective-permute-done.1.w1b_ref
  10.4 1.4 %inner.1.inner_ref = bf16[4,256,256]{2,1,0:T(8,128)(2,1)S(1)} custom-call(bf16[9,256,256]{2,1,0:T(8,128)(2,1)S(1)} %get-tuple-element.49.near_ref, bf16[3,3,256,128]{3,2,1,0:T(8,128)(2,1)S(1)} %copy-done.1, bf16[3,3,256,128]{3,2,1,0:T(8,128)(2,1)S(1)} %collective-permute-done.1.w1b_ref, f32[1,128]{1,0:T(1,128)S(1)} %bitcast.17, f32[1,128]{1,0:T(1,128)S(1)} %bitcast.21), custom_call_target="tpu_custom_call" | custom-call | flops 1300000000 | bytes 1300000 | tf_op jit(solution)/shard_map/inner/pallas_call | solution.py:43
  11.8 0.7 %collective-permute-done.3 = f32[8,128]{1,0:T(8,128)S(1)} collective-permute-done((f32[8,128]{1,0:T(8,128)S(1)}, f32[8,128]{1,0:T(8,128)S(1)}, u32[]{:S(2)}, u32[]{:S(2)}) %collective-permute-start.3) | collective-permute-done | bytes 4128 | tf_op jit(solution)/shard_map/ppermute | solution.py:415
  12.5 1.6 %collective-permute-start.4 = (f32[8,128]{1,0:T(8,128)S(1)}, f32[8,128]{1,0:T(8,128)S(1)}, u32[]{:S(2)}, u32[]{:S(2)}) collective-permute-start(f32[8,128]{1,0:T(8,128)S(1)} %add.6), channel_id=1, source_target_pairs={{0,4},{4,0},{8,12},{12,8},{1,5},{5,1},{9,13},{13,9},{2,6},{6,2},{1... | collective-permute-start | bytes 12296 | tf_op jit(solution)/shard_map/ppermute | solution.py:415
  14.1 1.1 %later.1.later_ref = bf16[3,256,256]{2,1,0:T(8,128)(2,1)S(1)} custom-call(bf16[9,256,256]{2,1,0:T(8,128)(2,1)S(1)} %get-tuple-element.49.near_ref, bf16[3,3,256,128]{3,2,1,0:T(8,128)(2,1)S(1)} %copy-done.1, bf16[3,3,256,128]{3,2,1,0:T(8,128)(2,1)S(1)} %collective-permute-done.1.w1b_ref, f32[1,128]{1,0:T(1,128)S(1)} %bitcast.18, f32[1,128]{1,0:T(1,128)S(1)} %bitcast.22), custom_call_target="tpu_custom_call" | custom-call | flops 1300000000 | bytes 1300000 | tf_op jit(solution)/shard_map/later/pallas_call | solution.py:43
  15.2 0.9 %collective-permute-done.4 = f32[8,128]{1,0:T(8,128)S(1)} collective-permute-done((f32[8,128]{1,0:T(8,128)S(1)}, f32[8,128]{1,0:T(8,128)S(1)}, u32[]{:S(2)}, u32[]{:S(2)}) %collective-permute-start.4) | collective-permute-done | bytes 4128 | tf_op jit(solution)/shard_map/ppermute | solution.py:415
  16.1 2.6 %collective-permute-start.7 = (f32[8,128]{1,0:T(8,128)S(1)}, f32[8,128]{1,0:T(8,128)S(1)}, u32[]{:S(2)}, u32[]{:S(2)}) collective-permute-start(f32[8,128]{1,0:T(8,128)S(1)} %add.7.rest_0_), channel_id=1, source_target_pairs={{0,8},{4,12},{8,0},{12,4},{1,9},{5,13},{9,1},{13,5},{2,10},{6,14},... | collective-permute-start | bytes 12296 | tf_op jit(solution)/shard_map/ppermute | solution.py:415
  18.7 0.0 collective-permute-done.halo_ref
  18.7 4.1 %head.1 = (bf16[10,256,256]{2,1,0:T(8,128)(2,1)S(1)}, f32[8,256,128]{2,1,0:T(8,128)S(1)}, f32[1,128]{1,0:T(1,128)S(1)}, bf16[1152,256]{1,0:T(8,128)(2,1)S(1)}) custom-call(bf16[9,256,256]{2,1,0:T(8,128)(2,1)S(1)} %get-tuple-element.49.near_ref, bf16[4,256,256]{2,1,0:T(8,128)(2,1)S(1)} %inner.1.inner_ref, bf16[3,256,256]{2,1,0:T(8,128)(2,1)S(1)} %later.1.later_ref, ...), custom_call_target="tpu_custom_call" | custom-call | flops 5000000000 | bytes 5000000 | tf_op jit(solution)/shard_map/head/pallas_call | solution.py:43
  22.8 0.0 collective-permute-done.7.rest_1_
  22.8 1.6 %back.1 = (bf16[6,336,256]{2,1,0:T(8,128)(2,1)S(1)}, bf16[6,256,128]{2,1,0:T(8,128)(2,1)S(1)}, bf16[6,256,128]{2,1,0:T(8,128)(2,1)S(1)}, f32[4,128]{1,0:T(4,128)S(1)}) custom-call(bf16[10,256,256]{2,1,0:T(8,128)(2,1)S(1)} %get-tuple-element.56.hid_ref, f32[8,256,128]{2,1,0:T(8,128)S(1)} %get-tuple-element.57.dz_ref, ...), custom_call_target="tpu_custom_call" | custom-call | flops 4000000000 | bytes 4000000 | tf_op jit(solution)/shard_map/back/pallas_call | solution.py:43
  24.4 0.6 collective-permute-start.8
  25.0 1.0 %cls.1 = (f32[896,128]{1,0:T(8,128)S(1)}, f32[896,128]{1,0:T(8,128)S(1)}) custom-call(bf16[10,256,256]{2,1,0:T(8,128)(2,1)S(1)} %get-tuple-element.56.hid_ref, bf16[6,336,256]{2,1,0:T(8,128)(2,1)S(1)} %get-tuple-element.64.dt_ref), custom_call_target="tpu_custom_call" | custom-call | flops 1500000000 | bytes 1500000 | tf_op jit(solution)/shard_map/cls/pallas_call | solution.py:43
  26.0 0.1 collective-permute-start.9
  26.1 0.3 collective-permute-done.8.other_ref
  26.3 0.0 collective-permute-done.5.far_ref
  26.3 0.1 copy-done
  26.4 2.9 %shared.1 = (f32[1152,128]{1,0:T(8,128)S(1)}, bf16[1152,128]{1,0:T(8,128)(2,1)S(1)}) custom-call(bf16[12,256,256]{2,1,0:T(8,128)(2,1)S(1)} %bitcast.13, bf16[784,256]{1,0:T(8,128)(2,1)S(1)} %collective-permute-done.halo_ref, bf16[784,256]{1,0:T(8,128)(2,1)S(1)} %collective-permute-done.5.far_ref, bf16[6,256,128]{2,1,0:T(8,128)(2,1)S(1)} %get-tuple-element.60.own_ref, ...), custom_call_target="tpu_custom_call" | custom-call | flops 4000000000 | bytes 4000000 | tf_op jit(solution)/shard_map/shared/pallas_call | solution.py:43
  29.3 1.6 %collective-permute-start.10 = (bf16[1152,128]{1,0:T(8,128)(2,1)S(1)}, bf16[1152,128]{1,0:T(8,128)(2,1)S(1)}, u32[]{:S(2)}, u32[]{:S(2)}) collective-permute-start(bf16[1152,128]{1,0:T(8,128)(2,1)S(1)} %get-tuple-element.68), channel_id=1, source_target_pairs={{0,2},{2,0},{1,3},{3,1},{4,6},{6,4},{5,7},{7,5},{8,10},{10,8},{9,1... | collective-permute-start | bytes 884744 | tf_op jit(solution)/shard_map/ppermute | solution.py:415
  30.9 0.0 collective-permute-done.9.theirs_ref
  30.9 0.1 cls_split.1
  31.0 1.4 %collective-permute-start.11 = (bf16[240,128]{1,0:T(8,128)(2,1)S(1)}, bf16[240,128]{1,0:T(8,128)(2,1)S(1)}, u32[]{:S(2)}, u32[]{:S(2)}) collective-permute-start(bf16[240,128]{1,0:T(8,128)(2,1)S(1)} %get-tuple-element.69), channel_id=1, source_target_pairs={{0,12},{4,8},{8,4},{12,0},{1,13},{5,9},{9,5},{13,1},{2,14},{6,10},... | collective-permute-start | bytes 184328 | tf_op jit(solution)/shard_map/ppermute | solution.py:415
  32.4 1.0 %collective-permute-start.12 = (bf16[240,128]{1,0:T(8,128)(2,1)S(1)}, bf16[240,128]{1,0:T(8,128)(2,1)S(1)}, u32[]{:S(2)}, u32[]{:S(2)}) collective-permute-start(bf16[240,128]{1,0:T(8,128)(2,1)S(1)} %get-tuple-element.70), channel_id=1, source_target_pairs={{0,8},{4,12},{8,0},{12,4},{1,9},{5,13},{9,1},{13,5},{2,10},{6,14},... | collective-permute-start | bytes 184328 | tf_op jit(solution)/shard_map/ppermute | solution.py:415
  33.4 2.1 %collective-permute-start.13 = (bf16[240,128]{1,0:T(8,128)(2,1)S(1)}, bf16[240,128]{1,0:T(8,128)(2,1)S(1)}, u32[]{:S(2)}, u32[]{:S(2)}) collective-permute-start(bf16[240,128]{1,0:T(8,128)(2,1)S(1)} %get-tuple-element.71), channel_id=1, source_target_pairs={{0,4},{4,0},{8,12},{12,8},{1,5},{5,1},{9,13},{13,9},{2,6},{6,2},{1... | collective-permute-start | bytes 184328 | tf_op jit(solution)/shard_map/ppermute | solution.py:415
  35.5 2.4 %collective-permute-done.11.refs_1_ = bf16[240,128]{1,0:T(8,128)(2,1)S(1)} collective-permute-done((bf16[240,128]{1,0:T(8,128)(2,1)S(1)}, bf16[240,128]{1,0:T(8,128)(2,1)S(1)}, u32[]{:S(2)}, u32[]{:S(2)}) %collective-permute-start.11) | collective-permute-done | bytes 61472 | tf_op jit(solution)/shard_map/ppermute | solution.py:415
  37.8 1.7 %collective-permute-done.12.refs_2_ = bf16[240,128]{1,0:T(8,128)(2,1)S(1)} collective-permute-done((bf16[240,128]{1,0:T(8,128)(2,1)S(1)}, bf16[240,128]{1,0:T(8,128)(2,1)S(1)}, u32[]{:S(2)}, u32[]{:S(2)}) %collective-permute-start.12) | collective-permute-done | bytes 61472 | tf_op jit(solution)/shard_map/ppermute | solution.py:415
  39.5 0.0 collective-permute-done.13.refs_3_
  39.6 0.0 collective-permute-done.10.refs_0_
  39.6 0.1 sum.1
  39.7 1.4 %collective-permute-start.14 = (bf16[288,128]{1,0:T(8,128)(2,1)S(1)}, bf16[288,128]{1,0:T(8,128)(2,1)S(1)}, u32[]{:S(2)}, u32[]{:S(2)}) collective-permute-start(bf16[288,128]{1,0:T(8,128)(2,1)S(1)} %get-tuple-element.75), channel_id=1, source_target_pairs={{0,12},{4,8},{8,4},{12,0},{1,13},{5,9},{9,5},{13,1},{2,14},{6,10},... | collective-permute-start | bytes 221192 | tf_op jit(solution)/shard_map/ppermute | solution.py:415
  41.1 0.3 collective-permute-start.15
  41.4 2.8 %collective-permute-start.16 = (bf16[288,128]{1,0:T(8,128)(2,1)S(1)}, bf16[288,128]{1,0:T(8,128)(2,1)S(1)}, u32[]{:S(2)}, u32[]{:S(2)}) collective-permute-start(bf16[288,128]{1,0:T(8,128)(2,1)S(1)} %get-tuple-element.77), channel_id=1, source_target_pairs={{0,4},{4,0},{8,12},{12,8},{1,5},{5,1},{9,13},{13,9},{2,6},{6,2},{1... | collective-permute-start | bytes 221192 | tf_op jit(solution)/shard_map/ppermute | solution.py:415
  44.1 0.6 collective-permute-start.17
  44.7 3.3 %collective-permute-done.17.refs_3_ = bf16[128,128]{1,0:T(8,128)(2,1)S(1)} collective-permute-done((bf16[128,128]{1,0:T(8,128)(2,1)S(1)}, bf16[128,128]{1,0:T(8,128)(2,1)S(1)}, u32[]{:S(2)}, u32[]{:S(2)}) %collective-permute-start.17) | collective-permute-done | bytes 32800 | tf_op jit(solution)/shard_map/ppermute | solution.py:415
  48.1 0.0 collective-permute-done.14.refs_0_
  48.1 0.9 %collective-permute-done.15.refs_1_ = bf16[288,128]{1,0:T(8,128)(2,1)S(1)} collective-permute-done((bf16[288,128]{1,0:T(8,128)(2,1)S(1)}, bf16[288,128]{1,0:T(8,128)(2,1)S(1)}, u32[]{:S(2)}, u32[]{:S(2)}) %collective-permute-start.15) | collective-permute-done | bytes 73760 | tf_op jit(solution)/shard_map/ppermute | solution.py:415
  49.0 0.0 collective-permute-done.16.refs_2_
  49.0 1.3 %collective-permute-start.21 = (bf16[288,128]{1,0:T(8,128)(2,1)S(1)}, bf16[288,128]{1,0:T(8,128)(2,1)S(1)}, u32[]{:S(2)}, u32[]{:S(2)}) collective-permute-start(bf16[288,128]{1,0:T(8,128)(2,1)S(1)} %get-tuple-element.80.refs_0_), channel_id=1, source_target_pairs={{0,12},{4,8},{8,4},{12,0},{1,13},{5,9},{9,5},{13,1},{2,14},{6,10},... | collective-permute-start | bytes 221192 | tf_op jit(solution)/shard_map/ppermute | solution.py:415
  50.4 0.0 collective-permute-start.20
  50.4 3.1 %collective-permute-start.19 = (bf16[288,128]{1,0:T(8,128)(2,1)S(1)}, bf16[288,128]{1,0:T(8,128)(2,1)S(1)}, u32[]{:S(2)}, u32[]{:S(2)}) collective-permute-start(bf16[288,128]{1,0:T(8,128)(2,1)S(1)} %get-tuple-element.80.refs_0_), channel_id=1, source_target_pairs={{0,4},{4,0},{8,12},{12,8},{1,5},{5,1},{9,13},{13,9},{2,6},{6,2},{1... | collective-permute-start | bytes 221192 | tf_op jit(solution)/shard_map/ppermute | solution.py:415
  53.5 0.8 %collective-permute-start.22 = (bf16[112,128]{1,0:T(8,128)(2,1)S(1)}, bf16[112,128]{1,0:T(8,128)(2,1)S(1)}, u32[]{:S(2)}, u32[]{:S(2)}) collective-permute-start(bf16[112,128]{1,0:T(8,128)(2,1)S(1)} %get-tuple-element.81.refs_4_), channel_id=1, source_target_pairs={{0,2},{2,0},{1,3},{3,1},{4,6},{6,4},{5,7},{7,5},{8,10},{10,8},{9,1... | collective-permute-start | bytes 86024 | tf_op jit(solution)/shard_map/ppermute | solution.py:415
  54.3 3.1 %collective-permute-done.22.refs_5_ = bf16[112,128]{1,0:T(8,128)(2,1)S(1)} collective-permute-done((bf16[112,128]{1,0:T(8,128)(2,1)S(1)}, bf16[112,128]{1,0:T(8,128)(2,1)S(1)}, u32[]{:S(2)}, u32[]{:S(2)}) %collective-permute-start.22) | collective-permute-done | bytes 28704 | tf_op jit(solution)/shard_map/ppermute | solution.py:415
  57.4 0.0 collective-permute-done.21.refs_3_
  57.4 0.9 %collective-permute-done.20.refs_2_ = bf16[288,128]{1,0:T(8,128)(2,1)S(1)} collective-permute-done((bf16[288,128]{1,0:T(8,128)(2,1)S(1)}, bf16[288,128]{1,0:T(8,128)(2,1)S(1)}, u32[]{:S(2)}, u32[]{:S(2)}) %collective-permute-start.20) | collective-permute-done | bytes 73760 | tf_op jit(solution)/shard_map/ppermute | solution.py:415
  58.3 0.0 collective-permute-done.19.refs_1_
  58.3 0.6 collective-permute-start.23
  58.9 1.4 %collective-permute-start.26 = (bf16[224,128]{1,0:T(8,128)(2,1)S(1)}, bf16[224,128]{1,0:T(8,128)(2,1)S(1)}, u32[]{:S(2)}, u32[]{:S(2)}) collective-permute-start(bf16[224,128]{1,0:T(8,128)(2,1)S(1)} %get-tuple-element.83.refs_2_), channel_id=1, source_target_pairs={{0,12},{4,8},{8,4},{12,0},{1,13},{5,9},{9,5},{13,1},{2,14},{6,10},... | collective-permute-start | bytes 172040 | tf_op jit(solution)/shard_map/ppermute | solution.py:415
  60.3 0.0 collective-permute-start.25
  60.3 3.0 %collective-permute-start.24 = (bf16[224,128]{1,0:T(8,128)(2,1)S(1)}, bf16[224,128]{1,0:T(8,128)(2,1)S(1)}, u32[]{:S(2)}, u32[]{:S(2)}) collective-permute-start(bf16[224,128]{1,0:T(8,128)(2,1)S(1)} %get-tuple-element.83.refs_2_), channel_id=1, source_target_pairs={{0,4},{4,0},{8,12},{12,8},{1,5},{5,1},{9,13},{13,9},{2,6},{6,2},{1... | collective-permute-start | bytes 172040 | tf_op jit(solution)/shard_map/ppermute | solution.py:415
  63.3 0.0 collective-permute-start.18
  63.3 1.2 %collective-permute-done.18.theirs_ref = f32[4,128]{1,0:T(4,128)S(1)} collective-permute-done((f32[4,128]{1,0:T(4,128)S(1)}, f32[4,128]{1,0:T(4,128)S(1)}, u32[]{:S(2)}, u32[]{:S(2)}) %collective-permute-start.18) | collective-permute-done | bytes 2080 | tf_op jit(solution)/shard_map/ppermute | solution.py:415
  64.5 0.9 %collective-permute-done.26.refs_5_ = bf16[224,128]{1,0:T(8,128)(2,1)S(1)} collective-permute-done((bf16[224,128]{1,0:T(8,128)(2,1)S(1)}, bf16[224,128]{1,0:T(8,128)(2,1)S(1)}, u32[]{:S(2)}, u32[]{:S(2)}) %collective-permute-start.26) | collective-permute-done | bytes 57376 | tf_op jit(solution)/shard_map/ppermute | solution.py:415
  65.3 1.4 %collective-permute-done.25.refs_4_ = bf16[224,128]{1,0:T(8,128)(2,1)S(1)} collective-permute-done((bf16[224,128]{1,0:T(8,128)(2,1)S(1)}, bf16[224,128]{1,0:T(8,128)(2,1)S(1)}, u32[]{:S(2)}, u32[]{:S(2)}) %collective-permute-start.25) | collective-permute-done | bytes 57376 | tf_op jit(solution)/shard_map/ppermute | solution.py:415
  66.8 0.0 collective-permute-done.24.refs_3_
  66.8 0.5 collective-permute-done.23.refs_1_
  67.3 1.3 %out.1 = (f32[2304,128]{1,0:T(8,128)}, f32[1,128]{1,0:T(1,128)}, f32[3,3,99,128]{3,2,1,0:T(8,128)}, f32[1,99]{1,0:T(1,128)}, f32[1,1]{1,0:T(1,128)}) custom-call(f32[4,128]{1,0:T(4,128)S(1)} %get-tuple-element.79.small_ref, f32[4,128]{1,0:T(4,128)S(1)} %collective-permute-done.18.theirs_ref, bf16[1152,128]{1,0:T(8,128)(2,1)S(1)} %get-tuple-element.82.refs_0_, ...), custom_call_target="tpu_custom_call" | custom-call | flops 1500000000 | bytes 1500000 | tf_op jit(solution)/shard_map/out/pallas_call | solution.py:43
  (16 shorter events, 0.1 us)
Async XLA Ops:
  0.6 9.7 %collective-permute-start.1 = (bf16[3,3,256,128]{3,2,1,0:T(8,128)(2,1)}, bf16[3,3,256,128]{3,2,1,0:T(8,128)(2,1)S(1)}, u32[]{:S(2)}, u32[]{:S(2)}) collective-permute-start(bf16[3,3,256,128]{3,2,1,0:T(8,128)(2,1)} %w1a_ref.5), channel_id=1, source_target_pairs={{0,1},{1,0},{2,3},{3,2},{4,5},{5,4},{6,7},{7,6},{8,9},{9,8},{10,11... | collective-permute-start | bytes 1769480 | tf_op jit(solution)/shard_map/ppermute | solution.py:415
  1.2 0.9 %copy-start.3 = (s32[1,12,2304]{2,0,1:T(1,128)S(1)}, s32[1,12,2304]{2,0,1:T(1,128)}, u32[]{:S(2)}) copy-start(s32[1,12,2304]{2,0,1:T(1,128)} %param.7) | copy-start | bytes 331780
  2.0 2.7 %copy-start.4 = (f32[128]{0:T(128)S(1)}, f32[128]{0:T(128)}, u32[]{:S(2)}) copy-start(f32[128]{0:T(128)} %param.9) | copy-start | bytes 1540
  2.0 6.7 %copy-start.2 = (bf16[3,3,128,99]{2,3,1,0:T(8,128)(2,1)S(1)}, bf16[3,3,128,99]{2,3,1,0:T(8,128)(2,1)}, u32[]{:S(2)}) copy-start(bf16[3,3,128,99]{2,3,1,0:T(8,128)(2,1)} %param.10) | copy-start | bytes 684292
  2.1 8.3 %copy-start.1 = (bf16[3,3,256,128]{3,2,1,0:T(8,128)(2,1)S(1)}, bf16[3,3,256,128]{3,2,1,0:T(8,128)(2,1)}, u32[]{:S(2)}) copy-start(bf16[3,3,256,128]{3,2,1,0:T(8,128)(2,1)} %w1a_ref.5) | copy-start | bytes 1769476
  4.1 14.6 %collective-permute-start = (bf16[784,256]{1,0:T(8,128)(2,1)S(1)}, bf16[784,256]{1,0:T(8,128)(2,1)S(1)}, u32[]{:S(2)}, u32[]{:S(2)}) collective-permute-start(bf16[784,256]{1,0:T(8,128)(2,1)S(1)} %get-tuple-element.47), channel_id=1, source_target_pairs={{1,4},{4,1},{5,8},{8,5},{9,12},{12,9},{3,6},{6,3},{7,10},{10,7},{1... | collective-permute-start | bytes 1204232 | tf_op jit(solution)/shard_map/ppermute | solution.py:459
  4.8 5.6 %collective-permute-start.2 = (f32[128]{0:T(128)S(1)}, f32[128]{0:T(128)S(1)}, u32[]{:S(2)}, u32[]{:S(2)}) collective-permute-start(f32[128]{0:T(128)S(1)} %copy-done.4), channel_id=1, source_target_pairs={{0,1},{1,0},{2,3},{3,2},{4,5},{5,4},{6,7},{7,6},{8,9},{9,8},{10,11... | collective-permute-start | bytes 1544 | tf_op jit(solution)/shard_map/ppermute | solution.py:415
  8.8 9.9 %collective-permute-start.6 = (bf16[3,3,128,99]{2,3,1,0:T(8,128)(2,1)S(1)}, bf16[3,3,128,99]{2,3,1,0:T(8,128)(2,1)S(1)}, u32[]{:S(2)}, u32[]{:S(2)}) collective-permute-start(bf16[3,3,128,99]{2,3,1,0:T(8,128)(2,1)S(1)} %copy-done.2), channel_id=1, source_target_pairs={{0,1},{1,0},{2,3},{3,2},{4,5},{5,4},{6,7},{7,6},{8,9},{9,8},{10,11... | collective-permute-start | bytes 684296 | tf_op jit(solution)/shard_map/ppermute | solution.py:415
  8.9 3.6 %collective-permute-start.3 = (f32[8,128]{1,0:T(8,128)S(1)}, f32[8,128]{1,0:T(8,128)S(1)}, u32[]{:S(2)}, u32[]{:S(2)}) collective-permute-start(f32[8,128]{1,0:T(8,128)S(1)} %get-tuple-element.48), channel_id=1, source_target_pairs={{0,2},{2,0},{1,3},{3,1},{4,6},{6,4},{5,7},{7,5},{8,10},{10,8},{9,1... | collective-permute-start | bytes 12296 | tf_op jit(solution)/shard_map/ppermute | solution.py:415
  12.5 6.2 %copy-start.5 = (f32[99]{0:T(128)S(1)}, f32[99]{0:T(128)}, u32[]{:S(2)}) copy-start(f32[99]{0:T(128)} %param.11) | copy-start | bytes 1192
  12.5 3.6 %collective-permute-start.4 = (f32[8,128]{1,0:T(8,128)S(1)}, f32[8,128]{1,0:T(8,128)S(1)}, u32[]{:S(2)}, u32[]{:S(2)}) collective-permute-start(f32[8,128]{1,0:T(8,128)S(1)} %add.6), channel_id=1, source_target_pairs={{0,4},{4,0},{8,12},{12,8},{1,5},{5,1},{9,13},{13,9},{2,6},{6,2},{1... | collective-permute-start | bytes 12296 | tf_op jit(solution)/shard_map/ppermute | solution.py:415
  16.1 6.7 %collective-permute-start.7 = (f32[8,128]{1,0:T(8,128)S(1)}, f32[8,128]{1,0:T(8,128)S(1)}, u32[]{:S(2)}, u32[]{:S(2)}) collective-permute-start(f32[8,128]{1,0:T(8,128)S(1)} %add.7.rest_0_), channel_id=1, source_target_pairs={{0,8},{4,12},{8,0},{12,4},{1,9},{5,13},{9,1},{13,5},{2,10},{6,14},... | collective-permute-start | bytes 12296 | tf_op jit(solution)/shard_map/ppermute | solution.py:415
  18.7 7.7 %collective-permute-start.5 = (bf16[784,256]{1,0:T(8,128)(2,1)S(1)}, bf16[784,256]{1,0:T(8,128)(2,1)S(1)}, u32[]{:S(2)}, u32[]{:S(2)}) collective-permute-start(bf16[784,256]{1,0:T(8,128)(2,1)S(1)} %collective-permute-done.halo_ref), channel_id=1, source_target_pairs={{0,1},{1,0},{2,3},{3,2},{4,5},{5,4},{6,7},{7,6},{8,9},{9,8},{10,11... | collective-permute-start | bytes 1204232 | tf_op jit(solution)/shard_map/ppermute | solution.py:415
  24.4 1.9 %collective-permute-start.8 = (bf16[6,256,128]{2,1,0:T(8,128)(2,1)S(1)}, bf16[6,256,128]{2,1,0:T(8,128)(2,1)S(1)}, u32[]{:S(2)}, u32[]{:S(2)}) collective-permute-start(bf16[6,256,128]{2,1,0:T(8,128)(2,1)S(1)} %get-tuple-element.61), channel_id=1, source_target_pairs={{0,1},{1,0},{2,3},{3,2},{4,5},{5,4},{6,7},{7,6},{8,9},{9,8},{10,11... | collective-permute-start | bytes 1179656 | tf_op jit(solution)/shard_map/ppermute | solution.py:415
  25.0 1.4 %copy-start = (bf16[1,12,256,256]{3,2,1,0:T(8,128)(2,1)S(1)}, bf16[1,12,256,256]{3,2,1,0:T(8,128)(2,1)}, u32[]{:S(2)}) copy-start(bf16[1,12,256,256]{3,2,1,0:T(8,128)(2,1)} %param.6) | copy-start | bytes 4718596
  26.0 5.0 %collective-permute-start.9 = (f32[896,128]{1,0:T(8,128)S(1)}, f32[896,128]{1,0:T(8,128)S(1)}, u32[]{:S(2)}, u32[]{:S(2)}) collective-permute-start(f32[896,128]{1,0:T(8,128)S(1)} %get-tuple-element.66), channel_id=1, source_target_pairs={{0,1},{1,0},{2,3},{3,2},{4,5},{5,4},{6,7},{7,6},{8,9},{9,8},{10,11... | collective-permute-start | bytes 1376264 | tf_op jit(solution)/shard_map/ppermute | solution.py:415
  29.3 10.2 %collective-permute-start.10 = (bf16[1152,128]{1,0:T(8,128)(2,1)S(1)}, bf16[1152,128]{1,0:T(8,128)(2,1)S(1)}, u32[]{:S(2)}, u32[]{:S(2)}) collective-permute-start(bf16[1152,128]{1,0:T(8,128)(2,1)S(1)} %get-tuple-element.68), channel_id=1, source_target_pairs={{0,2},{2,0},{1,3},{3,1},{4,6},{6,4},{5,7},{7,5},{8,10},{10,8},{9,1... | collective-permute-start | bytes 884744 | tf_op jit(solution)/shard_map/ppermute | solution.py:415
  31.0 6.8 %collective-permute-start.11 = (bf16[240,128]{1,0:T(8,128)(2,1)S(1)}, bf16[240,128]{1,0:T(8,128)(2,1)S(1)}, u32[]{:S(2)}, u32[]{:S(2)}) collective-permute-start(bf16[240,128]{1,0:T(8,128)(2,1)S(1)} %get-tuple-element.69), channel_id=1, source_target_pairs={{0,12},{4,8},{8,4},{12,0},{1,13},{5,9},{9,5},{13,1},{2,14},{6,10},... | collective-permute-start | bytes 184328 | tf_op jit(solution)/shard_map/ppermute | solution.py:415
  32.4 7.1 %collective-permute-start.12 = (bf16[240,128]{1,0:T(8,128)(2,1)S(1)}, bf16[240,128]{1,0:T(8,128)(2,1)S(1)}, u32[]{:S(2)}, u32[]{:S(2)}) collective-permute-start(bf16[240,128]{1,0:T(8,128)(2,1)S(1)} %get-tuple-element.70), channel_id=1, source_target_pairs={{0,8},{4,12},{8,0},{12,4},{1,9},{5,13},{9,1},{13,5},{2,10},{6,14},... | collective-permute-start | bytes 184328 | tf_op jit(solution)/shard_map/ppermute | solution.py:415
  33.4 6.1 %collective-permute-start.13 = (bf16[240,128]{1,0:T(8,128)(2,1)S(1)}, bf16[240,128]{1,0:T(8,128)(2,1)S(1)}, u32[]{:S(2)}, u32[]{:S(2)}) collective-permute-start(bf16[240,128]{1,0:T(8,128)(2,1)S(1)} %get-tuple-element.71), channel_id=1, source_target_pairs={{0,4},{4,0},{8,12},{12,8},{1,5},{5,1},{9,13},{13,9},{2,6},{6,2},{1... | collective-permute-start | bytes 184328 | tf_op jit(solution)/shard_map/ppermute | solution.py:415
  39.7 8.4 %collective-permute-start.14 = (bf16[288,128]{1,0:T(8,128)(2,1)S(1)}, bf16[288,128]{1,0:T(8,128)(2,1)S(1)}, u32[]{:S(2)}, u32[]{:S(2)}) collective-permute-start(bf16[288,128]{1,0:T(8,128)(2,1)S(1)} %get-tuple-element.75), channel_id=1, source_target_pairs={{0,12},{4,8},{8,4},{12,0},{1,13},{5,9},{9,5},{13,1},{2,14},{6,10},... | collective-permute-start | bytes 221192 | tf_op jit(solution)/shard_map/ppermute | solution.py:415
  41.1 7.9 %collective-permute-start.15 = (bf16[288,128]{1,0:T(8,128)(2,1)S(1)}, bf16[288,128]{1,0:T(8,128)(2,1)S(1)}, u32[]{:S(2)}, u32[]{:S(2)}) collective-permute-start(bf16[288,128]{1,0:T(8,128)(2,1)S(1)} %get-tuple-element.76), channel_id=1, source_target_pairs={{0,8},{4,12},{8,0},{12,4},{1,9},{5,13},{9,1},{13,5},{2,10},{6,14},... | collective-permute-start | bytes 221192 | tf_op jit(solution)/shard_map/ppermute | solution.py:415
  41.4 7.6 %collective-permute-start.16 = (bf16[288,128]{1,0:T(8,128)(2,1)S(1)}, bf16[288,128]{1,0:T(8,128)(2,1)S(1)}, u32[]{:S(2)}, u32[]{:S(2)}) collective-permute-start(bf16[288,128]{1,0:T(8,128)(2,1)S(1)} %get-tuple-element.77), channel_id=1, source_target_pairs={{0,4},{4,0},{8,12},{12,8},{1,5},{5,1},{9,13},{13,9},{2,6},{6,2},{1... | collective-permute-start | bytes 221192 | tf_op jit(solution)/shard_map/ppermute | solution.py:415
  44.1 3.9 %collective-permute-start.17 = (bf16[128,128]{1,0:T(8,128)(2,1)S(1)}, bf16[128,128]{1,0:T(8,128)(2,1)S(1)}, u32[]{:S(2)}, u32[]{:S(2)}) collective-permute-start(bf16[128,128]{1,0:T(8,128)(2,1)S(1)} %get-tuple-element.78), channel_id=1, source_target_pairs={{0,2},{2,0},{1,3},{3,1},{4,6},{6,4},{5,7},{7,5},{8,10},{10,8},{9,1... | collective-permute-start | bytes 98312 | tf_op jit(solution)/shard_map/ppermute | solution.py:415
  49.0 8.3 %collective-permute-start.21 = (bf16[288,128]{1,0:T(8,128)(2,1)S(1)}, bf16[288,128]{1,0:T(8,128)(2,1)S(1)}, u32[]{:S(2)}, u32[]{:S(2)}) collective-permute-start(bf16[288,128]{1,0:T(8,128)(2,1)S(1)} %get-tuple-element.80.refs_0_), channel_id=1, source_target_pairs={{0,12},{4,8},{8,4},{12,0},{1,13},{5,9},{9,5},{13,1},{2,14},{6,10},... | collective-permute-start | bytes 221192 | tf_op jit(solution)/shard_map/ppermute | solution.py:415
  50.4 7.9 %collective-permute-start.20 = (bf16[288,128]{1,0:T(8,128)(2,1)S(1)}, bf16[288,128]{1,0:T(8,128)(2,1)S(1)}, u32[]{:S(2)}, u32[]{:S(2)}) collective-permute-start(bf16[288,128]{1,0:T(8,128)(2,1)S(1)} %get-tuple-element.80.refs_0_), channel_id=1, source_target_pairs={{0,8},{4,12},{8,0},{12,4},{1,9},{5,13},{9,1},{13,5},{2,10},{6,14},... | collective-permute-start | bytes 221192 | tf_op jit(solution)/shard_map/ppermute | solution.py:415
  50.4 7.9 %collective-permute-start.19 = (bf16[288,128]{1,0:T(8,128)(2,1)S(1)}, bf16[288,128]{1,0:T(8,128)(2,1)S(1)}, u32[]{:S(2)}, u32[]{:S(2)}) collective-permute-start(bf16[288,128]{1,0:T(8,128)(2,1)S(1)} %get-tuple-element.80.refs_0_), channel_id=1, source_target_pairs={{0,4},{4,0},{8,12},{12,8},{1,5},{5,1},{9,13},{13,9},{2,6},{6,2},{1... | collective-permute-start | bytes 221192 | tf_op jit(solution)/shard_map/ppermute | solution.py:415
  53.5 3.9 %collective-permute-start.22 = (bf16[112,128]{1,0:T(8,128)(2,1)S(1)}, bf16[112,128]{1,0:T(8,128)(2,1)S(1)}, u32[]{:S(2)}, u32[]{:S(2)}) collective-permute-start(bf16[112,128]{1,0:T(8,128)(2,1)S(1)} %get-tuple-element.81.refs_4_), channel_id=1, source_target_pairs={{0,2},{2,0},{1,3},{3,1},{4,6},{6,4},{5,7},{7,5},{8,10},{10,8},{9,1... | collective-permute-start | bytes 86024 | tf_op jit(solution)/shard_map/ppermute | solution.py:415
  58.3 9.0 %collective-permute-start.23 = (bf16[1152,128]{1,0:T(8,128)(2,1)S(1)}, bf16[1152,128]{1,0:T(8,128)(2,1)S(1)}, u32[]{:S(2)}, u32[]{:S(2)}) collective-permute-start(bf16[1152,128]{1,0:T(8,128)(2,1)S(1)} %get-tuple-element.82.refs_0_), channel_id=1, source_target_pairs={{0,2},{2,0},{1,3},{3,1},{4,6},{6,4},{5,7},{7,5},{8,10},{10,8},{9,1... | collective-permute-start | bytes 884744 | tf_op jit(solution)/shard_map/ppermute | solution.py:415
  58.9 6.4 %collective-permute-start.26 = (bf16[224,128]{1,0:T(8,128)(2,1)S(1)}, bf16[224,128]{1,0:T(8,128)(2,1)S(1)}, u32[]{:S(2)}, u32[]{:S(2)}) collective-permute-start(bf16[224,128]{1,0:T(8,128)(2,1)S(1)} %get-tuple-element.83.refs_2_), channel_id=1, source_target_pairs={{0,12},{4,8},{8,4},{12,0},{1,13},{5,9},{9,5},{13,1},{2,14},{6,10},... | collective-permute-start | bytes 172040 | tf_op jit(solution)/shard_map/ppermute | solution.py:415
  60.3 6.4 %collective-permute-start.25 = (bf16[224,128]{1,0:T(8,128)(2,1)S(1)}, bf16[224,128]{1,0:T(8,128)(2,1)S(1)}, u32[]{:S(2)}, u32[]{:S(2)}) collective-permute-start(bf16[224,128]{1,0:T(8,128)(2,1)S(1)} %get-tuple-element.83.refs_2_), channel_id=1, source_target_pairs={{0,8},{4,12},{8,0},{12,4},{1,9},{5,13},{9,1},{13,5},{2,10},{6,14},... | collective-permute-start | bytes 172040 | tf_op jit(solution)/shard_map/ppermute | solution.py:415
  60.3 6.4 %collective-permute-start.24 = (bf16[224,128]{1,0:T(8,128)(2,1)S(1)}, bf16[224,128]{1,0:T(8,128)(2,1)S(1)}, u32[]{:S(2)}, u32[]{:S(2)}) collective-permute-start(bf16[224,128]{1,0:T(8,128)(2,1)S(1)} %get-tuple-element.83.refs_2_), channel_id=1, source_target_pairs={{0,4},{4,0},{8,12},{12,8},{1,5},{5,1},{9,13},{13,9},{2,6},{6,2},{1... | collective-permute-start | bytes 172040 | tf_op jit(solution)/shard_map/ppermute | solution.py:415
  63.3 1.2 %collective-permute-start.18 = (f32[4,128]{1,0:T(4,128)S(1)}, f32[4,128]{1,0:T(4,128)S(1)}, u32[]{:S(2)}, u32[]{:S(2)}) collective-permute-start(f32[4,128]{1,0:T(4,128)S(1)} %get-tuple-element.79.small_ref), channel_id=1, source_target_pairs={{0,1},{1,0},{2,3},{3,2},{4,5},{5,4},{6,7},{7,6},{8,9},{9,8},{10,11... | collective-permute-start | bytes 6152 | tf_op jit(solution)/shard_map/ppermute | solution.py:415

commit v10 on v8

--- a/solution.py
+++ b/solution.py
@@ -304,18 +304,10 @@
     before = jnp.where(c == 0, near, far)
     after = jnp.where(c == 0, far, near)
 
-    def place(ref, start):
-        def body(d, carry):
-            mid = ref[d].astype(F32)
-            d_ref[start + d] = jnp.concatenate(
-                [shift_cells(mid, -1).astype(BF16), ref[d], shift_cells(mid, 1).astype(BF16)], axis=1
-            )
-            return carry
-
-        lax.fori_loop(0, half, body, 0, unroll=True)
-
-    place(own_ref, half * c)
-    place(other_ref, half * (1 - c))
+    for r in range(rows):
+        mine, theirs = own_ref[r % half].astype(F32), other_ref[r % half].astype(F32)
+        mid = jnp.where(c == (0 if r < half else 1), mine, theirs)
+        d_ref[r] = jnp.concatenate([shift_cells(mid, -1), mid, shift_cells(mid, 1)], axis=1).astype(BF16)
     outs = d_ref.shape[2] // 3
 
     def part(x, first):

time: 67.3 us -> 66.8 us (level)
  transfers between devices with their start and end apart: 28 -> 28, of which waited for: 11 -> 11; matrix products, arithmetic and copies ran while one was open for 0% -> 0% of each run, Pallas kernels for 22% -> 21%
where the time goes in v10:
time: 66.8 us; the launch traced here: 66.6 us
  starting transfers between devices  33.6 us (50%)
  waiting for transfers between devices  15.7 us (24%)
  Pallas kernels  15.5 us (23%)
  local copies, waits for them, and re-layouts  0.97 us (1%)
  between operations  0.8 us (1%)
    ppermute x27, starting transfers between devices, swap(): return lax.ppermute(x, axis, [(i, i ^ bit) for i in range(size)])  32.9 us
    ppermute x27, waiting for transfers between devices, swap(): return lax.ppermute(x, axis, [(i, i ^ bit) for i in range(size)])  15.7 us
    pallas_call x11, Pallas kernels, call(): pl.pallas_call(functools.partial(kernel, inputs[0]), in_specs=(specs or [...  15.5 us
  transfers between devices with their start and end apart: 28, of which 11 were waited for; matrix products, arithmetic and copies ran while one was open for 0% of the time, Pallas kernels for 21%

profile of v10, /device:TPU:0, one launch (start us, length us, event | category | flops | bytes accessed | tf_op | source)
XLA Modules:
  0.0 66.6 jit_solution(7335642381092685931)
XLA Ops:
  0.6 0.5 collective-permute-start.1
  1.2 0.9 %copy-done.3 = s32[1,12,2304]{2,0,1:T(1,128)S(1)} copy-done((s32[1,12,2304]{2,0,1:T(1,128)S(1)}, s32[1,12,2304]{2,0,1:T(1,128)}, u32[]{:S(2)}) %copy-start.3) | copy-done | bytes 110616
  2.1 2.0 %edge.1 = (bf16[784,256]{1,0:T(8,128)(2,1)S(1)}, bf16[12,16,256]{2,1,0:T(8,128)(2,1)S(1)}, f32[8,128]{1,0:T(8,128)S(1)}, bf16[9,256,256]{2,1,0:T(8,128)(2,1)S(1)}) custom-call(bf16[12,256,256]{2,1,0:T(8,128)(2,1)} %bitcast.12, s32[12,1,2304]{2,1,0:T(1,128)S(1)} %bitcast.16), custom_call_target="tpu_custom_call" | custom-call | flops 2000000000 | bytes 2000000 | tf_op jit(solution)/shard_map/edge/pallas_call | solution.py:43
  4.1 0.7 %collective-permute-start = (bf16[784,256]{1,0:T(8,128)(2,1)S(1)}, bf16[784,256]{1,0:T(8,128)(2,1)S(1)}, u32[]{:S(2)}, u32[]{:S(2)}) collective-permute-start(bf16[784,256]{1,0:T(8,128)(2,1)S(1)} %get-tuple-element.45), channel_id=1, source_target_pairs={{1,4},{4,1},{5,8},{8,5},{9,12},{12,9},{3,6},{6,3},{7,10},{10,7},{1... | collective-permute-start | bytes 1204232 | tf_op jit(solution)/shard_map/ppermute | solution.py:456
  4.8 4.0 %collective-permute-start.2 = (f32[128]{0:T(128)S(1)}, f32[128]{0:T(128)S(1)}, u32[]{:S(2)}, u32[]{:S(2)}) collective-permute-start(f32[128]{0:T(128)S(1)} %copy-done.4), channel_id=1, source_target_pairs={{0,1},{1,0},{2,3},{3,2},{4,5},{5,4},{6,7},{7,6},{8,9},{9,8},{10,11... | collective-permute-start | bytes 1544 | tf_op jit(solution)/shard_map/ppermute | solution.py:412
  8.8 0.1 collective-permute-start.5
  8.9 1.5 %collective-permute-start.3 = (f32[8,128]{1,0:T(8,128)S(1)}, f32[8,128]{1,0:T(8,128)S(1)}, u32[]{:S(2)}, u32[]{:S(2)}) collective-permute-start(f32[8,128]{1,0:T(8,128)S(1)} %get-tuple-element.46), channel_id=1, source_target_pairs={{0,2},{2,0},{1,3},{3,1},{4,6},{6,4},{5,7},{7,5},{8,10},{10,8},{9,1... | collective-permute-start | bytes 12296 | tf_op jit(solution)/shard_map/ppermute | solution.py:412
  10.4 0.0 collective-permute-done.2
  10.4 0.0 collective-permute-done.1.w1b_ref
  10.4 0.0 copy-start.5
  10.4 2.4 %inner.1.inner_ref = bf16[7,256,256]{2,1,0:T(8,128)(2,1)S(1)} custom-call(bf16[9,256,256]{2,1,0:T(8,128)(2,1)S(1)} %get-tuple-element.47.near_ref, bf16[3,3,256,128]{3,2,1,0:T(8,128)(2,1)S(1)} %copy-done.1, bf16[3,3,256,128]{3,2,1,0:T(8,128)(2,1)S(1)} %collective-permute-done.1.w1b_ref, f32[1,128]{1,0:T(1,128)S(1)} %bitcast.17, f32[1,128]{1,0:T(1,128)S(1)} %bitcast.20), custom_call_target="tpu_custom_call" | custom-call | flops 3000000000 | bytes 3000000 | tf_op jit(solution)/shard_map/inner/pallas_call | solution.py:43
  12.8 0.0 collective-permute-done.3
  12.8 2.9 %collective-permute-start.8 = (f32[8,128]{1,0:T(8,128)S(1)}, f32[8,128]{1,0:T(8,128)S(1)}, u32[]{:S(2)}, u32[]{:S(2)}) collective-permute-start(f32[8,128]{1,0:T(8,128)S(1)} %add.3.rest_0_), channel_id=1, source_target_pairs={{0,12},{4,8},{8,4},{12,0},{1,13},{5,9},{9,5},{13,1},{2,14},{6,10},... | collective-permute-start | bytes 12296 | tf_op jit(solution)/shard_map/ppermute | solution.py:412
  15.7 0.2 collective-permute-start.7
  15.9 1.3 %collective-permute-start.6 = (f32[8,128]{1,0:T(8,128)S(1)}, f32[8,128]{1,0:T(8,128)S(1)}, u32[]{:S(2)}, u32[]{:S(2)}) collective-permute-start(f32[8,128]{1,0:T(8,128)S(1)} %add.3.rest_0_), channel_id=1, source_target_pairs={{0,4},{4,0},{8,12},{12,8},{1,5},{5,1},{9,13},{13,9},{2,6},{6,2},{1... | collective-permute-start | bytes 12296 | tf_op jit(solution)/shard_map/ppermute | solution.py:412
  17.2 0.0 collective-permute-done.halo_ref
  17.2 0.0 collective-permute-start.4
  17.2 0.0 collective-permute-done.5
  17.3 4.0 %head.1 = (bf16[10,256,256]{2,1,0:T(8,128)(2,1)S(1)}, f32[8,256,128]{2,1,0:T(8,128)S(1)}, f32[1,128]{1,0:T(1,128)S(1)}, bf16[1152,256]{1,0:T(8,128)(2,1)S(1)}) custom-call(bf16[9,256,256]{2,1,0:T(8,128)(2,1)S(1)} %get-tuple-element.47.near_ref, bf16[7,256,256]{2,1,0:T(8,128)(2,1)S(1)} %inner.1.inner_ref, bf16[784,256]{1,0:T(8,128)(2,1)S(1)} %collective-permute-done.halo_ref, ...), custom_call_target="tpu_custom_call" | custom-call | flops 5000000000 | bytes 5000000 | tf_op jit(solution)/shard_map/head/pallas_call | solution.py:43
  21.3 0.0 collective-permute-done.8.rest_3_
  21.3 0.0 collective-permute-done.7.rest_2_
  21.3 0.0 collective-permute-done.6.rest_1_
  21.3 1.6 %back.1 = (bf16[6,336,256]{2,1,0:T(8,128)(2,1)S(1)}, bf16[6,256,128]{2,1,0:T(8,128)(2,1)S(1)}, bf16[6,256,128]{2,1,0:T(8,128)(2,1)S(1)}, f32[4,128]{1,0:T(4,128)S(1)}) custom-call(bf16[10,256,256]{2,1,0:T(8,128)(2,1)S(1)} %get-tuple-element.52.hid_ref, f32[8,256,128]{2,1,0:T(8,128)S(1)} %get-tuple-element.53.dz_ref, ...), custom_call_target="tpu_custom_call" | custom-call | flops 4000000000 | bytes 4000000 | tf_op jit(solution)/shard_map/back/pallas_call | solution.py:43
  23.0 0.6 collective-permute-start.9
  23.5 1.0 %cls.1 = (f32[896,128]{1,0:T(8,128)S(1)}, f32[896,128]{1,0:T(8,128)S(1)}) custom-call(bf16[10,256,256]{2,1,0:T(8,128)(2,1)S(1)} %get-tuple-element.52.hid_ref, bf16[6,336,256]{2,1,0:T(8,128)(2,1)S(1)} %get-tuple-element.60.dt_ref), custom_call_target="tpu_custom_call" | custom-call | flops 1500000000 | bytes 1500000 | tf_op jit(solution)/shard_map/cls/pallas_call | solution.py:43
  24.5 0.1 collective-permute-start.10
  24.6 0.3 collective-permute-done.9.other_ref
  24.9 0.0 collective-permute-done.4.far_ref
  24.9 0.1 copy-done
  24.9 2.9 %shared.1 = (f32[1152,128]{1,0:T(8,128)S(1)}, bf16[1152,128]{1,0:T(8,128)(2,1)S(1)}) custom-call(bf16[12,256,256]{2,1,0:T(8,128)(2,1)S(1)} %bitcast.13, bf16[784,256]{1,0:T(8,128)(2,1)S(1)} %collective-permute-done.halo_ref, bf16[784,256]{1,0:T(8,128)(2,1)S(1)} %collective-permute-done.4.far_ref, bf16[6,256,128]{2,1,0:T(8,128)(2,1)S(1)} %get-tuple-element.56.own_ref, ...), custom_call_target="tpu_custom_call" | custom-call | flops 4000000000 | bytes 4000000 | tf_op jit(solution)/shard_map/shared/pallas_call | solution.py:43
  27.9 1.2 %collective-permute-start.11 = (bf16[1152,128]{1,0:T(8,128)(2,1)S(1)}, bf16[1152,128]{1,0:T(8,128)(2,1)S(1)}, u32[]{:S(2)}, u32[]{:S(2)}) collective-permute-start(bf16[1152,128]{1,0:T(8,128)(2,1)S(1)} %get-tuple-element.64), channel_id=1, source_target_pairs={{0,2},{2,0},{1,3},{3,1},{4,6},{6,4},{5,7},{7,5},{8,10},{10,8},{9,1... | collective-permute-start | bytes 884744 | tf_op jit(solution)/shard_map/ppermute | solution.py:412
  29.1 0.0 collective-permute-done.10.theirs_ref
  29.1 0.1 cls_split.1
  29.2 3.0 %collective-permute-start.12 = (bf16[240,128]{1,0:T(8,128)(2,1)S(1)}, bf16[240,128]{1,0:T(8,128)(2,1)S(1)}, u32[]{:S(2)}, u32[]{:S(2)}) collective-permute-start(bf16[240,128]{1,0:T(8,128)(2,1)S(1)} %get-tuple-element.65), channel_id=1, source_target_pairs={{0,12},{4,8},{8,4},{12,0},{1,13},{5,9},{9,5},{13,1},{2,14},{6,10},... | collective-permute-start | bytes 184328 | tf_op jit(solution)/shard_map/ppermute | solution.py:412
  32.1 0.0 collective-permute-start.13
  32.1 1.5 %collective-permute-start.14 = (bf16[240,128]{1,0:T(8,128)(2,1)S(1)}, bf16[240,128]{1,0:T(8,128)(2,1)S(1)}, u32[]{:S(2)}, u32[]{:S(2)}) collective-permute-start(bf16[240,128]{1,0:T(8,128)(2,1)S(1)} %get-tuple-element.67), channel_id=1, source_target_pairs={{0,4},{4,0},{8,12},{12,8},{1,5},{5,1},{9,13},{13,9},{2,6},{6,2},{1... | collective-permute-start | bytes 184328 | tf_op jit(solution)/shard_map/ppermute | solution.py:412
  33.6 2.1 %collective-permute-done.12.refs_1_ = bf16[240,128]{1,0:T(8,128)(2,1)S(1)} collective-permute-done((bf16[240,128]{1,0:T(8,128)(2,1)S(1)}, bf16[240,128]{1,0:T(8,128)(2,1)S(1)}, u32[]{:S(2)}, u32[]{:S(2)}) %collective-permute-start.12) | collective-permute-done | bytes 61472 | tf_op jit(solution)/shard_map/ppermute | solution.py:412
  35.7 2.0 %collective-permute-done.13.refs_2_ = bf16[240,128]{1,0:T(8,128)(2,1)S(1)} collective-permute-done((bf16[240,128]{1,0:T(8,128)(2,1)S(1)}, bf16[240,128]{1,0:T(8,128)(2,1)S(1)}, u32[]{:S(2)}, u32[]{:S(2)}) %collective-permute-start.13) | collective-permute-done | bytes 61472 | tf_op jit(solution)/shard_map/ppermute | solution.py:412
  37.7 0.1 collective-permute-done.14.refs_3_
  37.8 0.0 collective-permute-done.11.refs_0_
  37.8 0.1 sum.1
  37.9 2.6 %collective-permute-start.15 = (bf16[288,128]{1,0:T(8,128)(2,1)S(1)}, bf16[288,128]{1,0:T(8,128)(2,1)S(1)}, u32[]{:S(2)}, u32[]{:S(2)}) collective-permute-start(bf16[288,128]{1,0:T(8,128)(2,1)S(1)} %get-tuple-element.71), channel_id=1, source_target_pairs={{0,12},{4,8},{8,4},{12,0},{1,13},{5,9},{9,5},{13,1},{2,14},{6,10},... | collective-permute-start | bytes 221192 | tf_op jit(solution)/shard_map/ppermute | solution.py:412
  40.5 0.0 collective-permute-start.16
  40.5 1.9 %collective-permute-start.17 = (bf16[288,128]{1,0:T(8,128)(2,1)S(1)}, bf16[288,128]{1,0:T(8,128)(2,1)S(1)}, u32[]{:S(2)}, u32[]{:S(2)}) collective-permute-start(bf16[288,128]{1,0:T(8,128)(2,1)S(1)} %get-tuple-element.73), channel_id=1, source_target_pairs={{0,4},{4,0},{8,12},{12,8},{1,5},{5,1},{9,13},{13,9},{2,6},{6,2},{1... | collective-permute-start | bytes 221192 | tf_op jit(solution)/shard_map/ppermute | solution.py:412
  42.4 0.9 %collective-permute-start.18 = (bf16[128,128]{1,0:T(8,128)(2,1)S(1)}, bf16[128,128]{1,0:T(8,128)(2,1)S(1)}, u32[]{:S(2)}, u32[]{:S(2)}) collective-permute-start(bf16[128,128]{1,0:T(8,128)(2,1)S(1)} %get-tuple-element.74), channel_id=1, source_target_pairs={{0,2},{2,0},{1,3},{3,1},{4,6},{6,4},{5,7},{7,5},{8,10},{10,8},{9,1... | collective-permute-start | bytes 98312 | tf_op jit(solution)/shard_map/ppermute | solution.py:412
  43.3 3.0 %collective-permute-done.18.refs_3_ = bf16[128,128]{1,0:T(8,128)(2,1)S(1)} collective-permute-done((bf16[128,128]{1,0:T(8,128)(2,1)S(1)}, bf16[128,128]{1,0:T(8,128)(2,1)S(1)}, u32[]{:S(2)}, u32[]{:S(2)}) %collective-permute-start.18) | collective-permute-done | bytes 32800 | tf_op jit(solution)/shard_map/ppermute | solution.py:412
  46.3 0.0 collective-permute-done.15.refs_0_
  46.3 1.2 %collective-permute-done.16.refs_1_ = bf16[288,128]{1,0:T(8,128)(2,1)S(1)} collective-permute-done((bf16[288,128]{1,0:T(8,128)(2,1)S(1)}, bf16[288,128]{1,0:T(8,128)(2,1)S(1)}, u32[]{:S(2)}, u32[]{:S(2)}) %collective-permute-start.16) | collective-permute-done | bytes 73760 | tf_op jit(solution)/shard_map/ppermute | solution.py:412
  47.5 0.0 collective-permute-done.17.refs_2_
  47.5 2.0 %collective-permute-start.22 = (bf16[288,128]{1,0:T(8,128)(2,1)S(1)}, bf16[288,128]{1,0:T(8,128)(2,1)S(1)}, u32[]{:S(2)}, u32[]{:S(2)}) collective-permute-start(bf16[288,128]{1,0:T(8,128)(2,1)S(1)} %get-tuple-element.76.refs_0_), channel_id=1, source_target_pairs={{0,12},{4,8},{8,4},{12,0},{1,13},{5,9},{9,5},{13,1},{2,14},{6,10},... | collective-permute-start | bytes 221192 | tf_op jit(solution)/shard_map/ppermute | solution.py:412
  49.6 0.0 collective-permute-start.21
  49.6 2.4 %collective-permute-start.20 = (bf16[288,128]{1,0:T(8,128)(2,1)S(1)}, bf16[288,128]{1,0:T(8,128)(2,1)S(1)}, u32[]{:S(2)}, u32[]{:S(2)}) collective-permute-start(bf16[288,128]{1,0:T(8,128)(2,1)S(1)} %get-tuple-element.76.refs_0_), channel_id=1, source_target_pairs={{0,4},{4,0},{8,12},{12,8},{1,5},{5,1},{9,13},{13,9},{2,6},{6,2},{1... | collective-permute-start | bytes 221192 | tf_op jit(solution)/shard_map/ppermute | solution.py:412
  52.0 0.9 %collective-permute-start.23 = (bf16[112,128]{1,0:T(8,128)(2,1)S(1)}, bf16[112,128]{1,0:T(8,128)(2,1)S(1)}, u32[]{:S(2)}, u32[]{:S(2)}) collective-permute-start(bf16[112,128]{1,0:T(8,128)(2,1)S(1)} %get-tuple-element.77.refs_4_), channel_id=1, source_target_pairs={{0,2},{2,0},{1,3},{3,1},{4,6},{6,4},{5,7},{7,5},{8,10},{10,8},{9,1... | collective-permute-start | bytes 86024 | tf_op jit(solution)/shard_map/ppermute | solution.py:412
  52.9 3.0 %collective-permute-done.23.refs_5_ = bf16[112,128]{1,0:T(8,128)(2,1)S(1)} collective-permute-done((bf16[112,128]{1,0:T(8,128)(2,1)S(1)}, bf16[112,128]{1,0:T(8,128)(2,1)S(1)}, u32[]{:S(2)}, u32[]{:S(2)}) %collective-permute-start.23) | collective-permute-done | bytes 28704 | tf_op jit(solution)/shard_map/ppermute | solution.py:412
  55.9 0.0 collective-permute-done.22.refs_3_
  55.9 0.4 collective-permute-done.21.refs_2_
  56.3 1.0 %collective-permute-start.24 = (bf16[1152,128]{1,0:T(8,128)(2,1)S(1)}, bf16[1152,128]{1,0:T(8,128)(2,1)S(1)}, u32[]{:S(2)}, u32[]{:S(2)}) collective-permute-start(bf16[1152,128]{1,0:T(8,128)(2,1)S(1)} %get-tuple-element.78.refs_0_), channel_id=1, source_target_pairs={{0,2},{2,0},{1,3},{3,1},{4,6},{6,4},{5,7},{7,5},{8,10},{10,8},{9,1... | collective-permute-start | bytes 884744 | tf_op jit(solution)/shard_map/ppermute | solution.py:412
  57.3 2.5 %collective-permute-start.27 = (bf16[224,128]{1,0:T(8,128)(2,1)S(1)}, bf16[224,128]{1,0:T(8,128)(2,1)S(1)}, u32[]{:S(2)}, u32[]{:S(2)}) collective-permute-start(bf16[224,128]{1,0:T(8,128)(2,1)S(1)} %get-tuple-element.79.refs_2_), channel_id=1, source_target_pairs={{0,12},{4,8},{8,4},{12,0},{1,13},{5,9},{9,5},{13,1},{2,14},{6,10},... | collective-permute-start | bytes 172040 | tf_op jit(solution)/shard_map/ppermute | solution.py:412
  59.8 1.9 %collective-permute-start.25 = (bf16[224,128]{1,0:T(8,128)(2,1)S(1)}, bf16[224,128]{1,0:T(8,128)(2,1)S(1)}, u32[]{:S(2)}, u32[]{:S(2)}) collective-permute-start(bf16[224,128]{1,0:T(8,128)(2,1)S(1)} %get-tuple-element.79.refs_2_), channel_id=1, source_target_pairs={{0,4},{4,0},{8,12},{12,8},{1,5},{5,1},{9,13},{13,9},{2,6},{6,2},{1... | collective-permute-start | bytes 172040 | tf_op jit(solution)/shard_map/ppermute | solution.py:412
  61.7 1.2 %collective-permute-done.19.theirs_ref = f32[4,128]{1,0:T(4,128)S(1)} collective-permute-done((f32[4,128]{1,0:T(4,128)S(1)}, f32[4,128]{1,0:T(4,128)S(1)}, u32[]{:S(2)}, u32[]{:S(2)}) %collective-permute-start.19) | collective-permute-done | bytes 2080 | tf_op jit(solution)/shard_map/ppermute | solution.py:412
  62.8 0.5 collective-permute-done.27.refs_5_
  63.4 1.9 %collective-permute-done.26.refs_4_ = bf16[224,128]{1,0:T(8,128)(2,1)S(1)} collective-permute-done((bf16[224,128]{1,0:T(8,128)(2,1)S(1)}, bf16[224,128]{1,0:T(8,128)(2,1)S(1)}, u32[]{:S(2)}, u32[]{:S(2)}) %collective-permute-start.26) | collective-permute-done | bytes 57376 | tf_op jit(solution)/shard_map/ppermute | solution.py:412
  65.3 0.0 collective-permute-done.24.refs_1_
  65.3 1.3 %out.1 = (f32[2304,128]{1,0:T(8,128)}, f32[1,128]{1,0:T(1,128)}, f32[3,3,99,128]{3,2,1,0:T(8,128)}, f32[1,99]{1,0:T(1,128)}, f32[1,1]{1,0:T(1,128)}) custom-call(f32[4,128]{1,0:T(4,128)S(1)} %get-tuple-element.75.small_ref, f32[4,128]{1,0:T(4,128)S(1)} %collective-permute-done.19.theirs_ref, bf16[1152,128]{1,0:T(8,128)(2,1)S(1)} %get-tuple-element.78.refs_0_, ...), custom_call_target="tpu_custom_call" | custom-call | flops 1500000000 | bytes 1500000 | tf_op jit(solution)/shard_map/out/pallas_call | solution.py:43
  (16 shorter events, 0.1 us)
Async XLA Ops:
  0.6 9.7 %collective-permute-start.1 = (bf16[3,3,256,128]{3,2,1,0:T(8,128)(2,1)}, bf16[3,3,256,128]{3,2,1,0:T(8,128)(2,1)S(1)}, u32[]{:S(2)}, u32[]{:S(2)}) collective-permute-start(bf16[3,3,256,128]{3,2,1,0:T(8,128)(2,1)} %w1a_ref.3), channel_id=1, source_target_pairs={{0,1},{1,0},{2,3},{3,2},{4,5},{5,4},{6,7},{7,6},{8,9},{9,8},{10,11... | collective-permute-start | bytes 1769480 | tf_op jit(solution)/shard_map/ppermute | solution.py:412
  1.2 0.9 %copy-start.3 = (s32[1,12,2304]{2,0,1:T(1,128)S(1)}, s32[1,12,2304]{2,0,1:T(1,128)}, u32[]{:S(2)}) copy-start(s32[1,12,2304]{2,0,1:T(1,128)} %param.7) | copy-start | bytes 331780
  2.0 2.7 %copy-start.4 = (f32[128]{0:T(128)S(1)}, f32[128]{0:T(128)}, u32[]{:S(2)}) copy-start(f32[128]{0:T(128)} %param.9) | copy-start | bytes 1540
  2.0 6.7 %copy-start.2 = (bf16[3,3,128,99]{2,3,1,0:T(8,128)(2,1)S(1)}, bf16[3,3,128,99]{2,3,1,0:T(8,128)(2,1)}, u32[]{:S(2)}) copy-start(bf16[3,3,128,99]{2,3,1,0:T(8,128)(2,1)} %param.10) | copy-start | bytes 684292
  2.1 8.3 %copy-start.1 = (bf16[3,3,256,128]{3,2,1,0:T(8,128)(2,1)S(1)}, bf16[3,3,256,128]{3,2,1,0:T(8,128)(2,1)}, u32[]{:S(2)}) copy-start(bf16[3,3,256,128]{3,2,1,0:T(8,128)(2,1)} %w1a_ref.3) | copy-start | bytes 1769476
  4.1 13.2 %collective-permute-start = (bf16[784,256]{1,0:T(8,128)(2,1)S(1)}, bf16[784,256]{1,0:T(8,128)(2,1)S(1)}, u32[]{:S(2)}, u32[]{:S(2)}) collective-permute-start(bf16[784,256]{1,0:T(8,128)(2,1)S(1)} %get-tuple-element.45), channel_id=1, source_target_pairs={{1,4},{4,1},{5,8},{8,5},{9,12},{12,9},{3,6},{6,3},{7,10},{10,7},{1... | collective-permute-start | bytes 1204232 | tf_op jit(solution)/shard_map/ppermute | solution.py:456
  4.8 5.6 %collective-permute-start.2 = (f32[128]{0:T(128)S(1)}, f32[128]{0:T(128)S(1)}, u32[]{:S(2)}, u32[]{:S(2)}) collective-permute-start(f32[128]{0:T(128)S(1)} %copy-done.4), channel_id=1, source_target_pairs={{0,1},{1,0},{2,3},{3,2},{4,5},{5,4},{6,7},{7,6},{8,9},{9,8},{10,11... | collective-permute-start | bytes 1544 | tf_op jit(solution)/shard_map/ppermute | solution.py:412
  8.8 8.5 %collective-permute-start.5 = (bf16[3,3,128,99]{2,3,1,0:T(8,128)(2,1)S(1)}, bf16[3,3,128,99]{2,3,1,0:T(8,128)(2,1)S(1)}, u32[]{:S(2)}, u32[]{:S(2)}) collective-permute-start(bf16[3,3,128,99]{2,3,1,0:T(8,128)(2,1)S(1)} %copy-done.2), channel_id=1, source_target_pairs={{0,1},{1,0},{2,3},{3,2},{4,5},{5,4},{6,7},{7,6},{8,9},{9,8},{10,11... | collective-permute-start | bytes 684296 | tf_op jit(solution)/shard_map/ppermute | solution.py:412
  8.9 3.9 %collective-permute-start.3 = (f32[8,128]{1,0:T(8,128)S(1)}, f32[8,128]{1,0:T(8,128)S(1)}, u32[]{:S(2)}, u32[]{:S(2)}) collective-permute-start(f32[8,128]{1,0:T(8,128)S(1)} %get-tuple-element.46), channel_id=1, source_target_pairs={{0,2},{2,0},{1,3},{3,1},{4,6},{6,4},{5,7},{7,5},{8,10},{10,8},{9,1... | collective-permute-start | bytes 12296 | tf_op jit(solution)/shard_map/ppermute | solution.py:412
  10.4 6.9 %copy-start.5 = (f32[99]{0:T(128)S(1)}, f32[99]{0:T(128)}, u32[]{:S(2)}) copy-start(f32[99]{0:T(128)} %param.11) | copy-start | bytes 1192
  12.8 8.5 %collective-permute-start.8 = (f32[8,128]{1,0:T(8,128)S(1)}, f32[8,128]{1,0:T(8,128)S(1)}, u32[]{:S(2)}, u32[]{:S(2)}) collective-permute-start(f32[8,128]{1,0:T(8,128)S(1)} %add.3.rest_0_), channel_id=1, source_target_pairs={{0,12},{4,8},{8,4},{12,0},{1,13},{5,9},{9,5},{13,1},{2,14},{6,10},... | collective-permute-start | bytes 12296 | tf_op jit(solution)/shard_map/ppermute | solution.py:412
  15.7 5.6 %collective-permute-start.7 = (f32[8,128]{1,0:T(8,128)S(1)}, f32[8,128]{1,0:T(8,128)S(1)}, u32[]{:S(2)}, u32[]{:S(2)}) collective-permute-start(f32[8,128]{1,0:T(8,128)S(1)} %add.3.rest_0_), channel_id=1, source_target_pairs={{0,8},{4,12},{8,0},{12,4},{1,9},{5,13},{9,1},{13,5},{2,10},{6,14},... | collective-permute-start | bytes 12296 | tf_op jit(solution)/shard_map/ppermute | solution.py:412
  15.9 5.4 %collective-permute-start.6 = (f32[8,128]{1,0:T(8,128)S(1)}, f32[8,128]{1,0:T(8,128)S(1)}, u32[]{:S(2)}, u32[]{:S(2)}) collective-permute-start(f32[8,128]{1,0:T(8,128)S(1)} %add.3.rest_0_), channel_id=1, source_target_pairs={{0,4},{4,0},{8,12},{12,8},{1,5},{5,1},{9,13},{13,9},{2,6},{6,2},{1... | collective-permute-start | bytes 12296 | tf_op jit(solution)/shard_map/ppermute | solution.py:412
  17.2 7.6 %collective-permute-start.4 = (bf16[784,256]{1,0:T(8,128)(2,1)S(1)}, bf16[784,256]{1,0:T(8,128)(2,1)S(1)}, u32[]{:S(2)}, u32[]{:S(2)}) collective-permute-start(bf16[784,256]{1,0:T(8,128)(2,1)S(1)} %collective-permute-done.halo_ref), channel_id=1, source_target_pairs={{0,1},{1,0},{2,3},{3,2},{4,5},{5,4},{6,7},{7,6},{8,9},{9,8},{10,11... | collective-permute-start | bytes 1204232 | tf_op jit(solution)/shard_map/ppermute | solution.py:412
  23.0 1.9 %collective-permute-start.9 = (bf16[6,256,128]{2,1,0:T(8,128)(2,1)S(1)}, bf16[6,256,128]{2,1,0:T(8,128)(2,1)S(1)}, u32[]{:S(2)}, u32[]{:S(2)}) collective-permute-start(bf16[6,256,128]{2,1,0:T(8,128)(2,1)S(1)} %get-tuple-element.57), channel_id=1, source_target_pairs={{0,1},{1,0},{2,3},{3,2},{4,5},{5,4},{6,7},{7,6},{8,9},{9,8},{10,11... | collective-permute-start | bytes 1179656 | tf_op jit(solution)/shard_map/ppermute | solution.py:412
  23.5 1.4 %copy-start = (bf16[1,12,256,256]{3,2,1,0:T(8,128)(2,1)S(1)}, bf16[1,12,256,256]{3,2,1,0:T(8,128)(2,1)}, u32[]{:S(2)}) copy-start(bf16[1,12,256,256]{3,2,1,0:T(8,128)(2,1)} %param.6) | copy-start | bytes 4718596
  24.5 4.6 %collective-permute-start.10 = (f32[896,128]{1,0:T(8,128)S(1)}, f32[896,128]{1,0:T(8,128)S(1)}, u32[]{:S(2)}, u32[]{:S(2)}) collective-permute-start(f32[896,128]{1,0:T(8,128)S(1)} %get-tuple-element.62), channel_id=1, source_target_pairs={{0,1},{1,0},{2,3},{3,2},{4,5},{5,4},{6,7},{7,6},{8,9},{9,8},{10,11... | collective-permute-start | bytes 1376264 | tf_op jit(solution)/shard_map/ppermute | solution.py:412
  27.9 9.9 %collective-permute-start.11 = (bf16[1152,128]{1,0:T(8,128)(2,1)S(1)}, bf16[1152,128]{1,0:T(8,128)(2,1)S(1)}, u32[]{:S(2)}, u32[]{:S(2)}) collective-permute-start(bf16[1152,128]{1,0:T(8,128)(2,1)S(1)} %get-tuple-element.64), channel_id=1, source_target_pairs={{0,2},{2,0},{1,3},{3,1},{4,6},{6,4},{5,7},{7,5},{8,10},{10,8},{9,1... | collective-permute-start | bytes 884744 | tf_op jit(solution)/shard_map/ppermute | solution.py:412
  29.2 6.5 %collective-permute-start.12 = (bf16[240,128]{1,0:T(8,128)(2,1)S(1)}, bf16[240,128]{1,0:T(8,128)(2,1)S(1)}, u32[]{:S(2)}, u32[]{:S(2)}) collective-permute-start(bf16[240,128]{1,0:T(8,128)(2,1)S(1)} %get-tuple-element.65), channel_id=1, source_target_pairs={{0,12},{4,8},{8,4},{12,0},{1,13},{5,9},{9,5},{13,1},{2,14},{6,10},... | collective-permute-start | bytes 184328 | tf_op jit(solution)/shard_map/ppermute | solution.py:412
  32.1 5.6 %collective-permute-start.13 = (bf16[240,128]{1,0:T(8,128)(2,1)S(1)}, bf16[240,128]{1,0:T(8,128)(2,1)S(1)}, u32[]{:S(2)}, u32[]{:S(2)}) collective-permute-start(bf16[240,128]{1,0:T(8,128)(2,1)S(1)} %get-tuple-element.66), channel_id=1, source_target_pairs={{0,8},{4,12},{8,0},{12,4},{1,9},{5,13},{9,1},{13,5},{2,10},{6,14},... | collective-permute-start | bytes 184328 | tf_op jit(solution)/shard_map/ppermute | solution.py:412
  32.1 5.7 %collective-permute-start.14 = (bf16[240,128]{1,0:T(8,128)(2,1)S(1)}, bf16[240,128]{1,0:T(8,128)(2,1)S(1)}, u32[]{:S(2)}, u32[]{:S(2)}) collective-permute-start(bf16[240,128]{1,0:T(8,128)(2,1)S(1)} %get-tuple-element.67), channel_id=1, source_target_pairs={{0,4},{4,0},{8,12},{12,8},{1,5},{5,1},{9,13},{13,9},{2,6},{6,2},{1... | collective-permute-start | bytes 184328 | tf_op jit(solution)/shard_map/ppermute | solution.py:412
  37.9 8.4 %collective-permute-start.15 = (bf16[288,128]{1,0:T(8,128)(2,1)S(1)}, bf16[288,128]{1,0:T(8,128)(2,1)S(1)}, u32[]{:S(2)}, u32[]{:S(2)}) collective-permute-start(bf16[288,128]{1,0:T(8,128)(2,1)S(1)} %get-tuple-element.71), channel_id=1, source_target_pairs={{0,12},{4,8},{8,4},{12,0},{1,13},{5,9},{9,5},{13,1},{2,14},{6,10},... | collective-permute-start | bytes 221192 | tf_op jit(solution)/shard_map/ppermute | solution.py:412
  40.5 7.0 %collective-permute-start.16 = (bf16[288,128]{1,0:T(8,128)(2,1)S(1)}, bf16[288,128]{1,0:T(8,128)(2,1)S(1)}, u32[]{:S(2)}, u32[]{:S(2)}) collective-permute-start(bf16[288,128]{1,0:T(8,128)(2,1)S(1)} %get-tuple-element.72), channel_id=1, source_target_pairs={{0,8},{4,12},{8,0},{12,4},{1,9},{5,13},{9,1},{13,5},{2,10},{6,14},... | collective-permute-start | bytes 221192 | tf_op jit(solution)/shard_map/ppermute | solution.py:412
  40.5 7.0 %collective-permute-start.17 = (bf16[288,128]{1,0:T(8,128)(2,1)S(1)}, bf16[288,128]{1,0:T(8,128)(2,1)S(1)}, u32[]{:S(2)}, u32[]{:S(2)}) collective-permute-start(bf16[288,128]{1,0:T(8,128)(2,1)S(1)} %get-tuple-element.73), channel_id=1, source_target_pairs={{0,4},{4,0},{8,12},{12,8},{1,5},{5,1},{9,13},{13,9},{2,6},{6,2},{1... | collective-permute-start | bytes 221192 | tf_op jit(solution)/shard_map/ppermute | solution.py:412
  42.4 3.9 %collective-permute-start.18 = (bf16[128,128]{1,0:T(8,128)(2,1)S(1)}, bf16[128,128]{1,0:T(8,128)(2,1)S(1)}, u32[]{:S(2)}, u32[]{:S(2)}) collective-permute-start(bf16[128,128]{1,0:T(8,128)(2,1)S(1)} %get-tuple-element.74), channel_id=1, source_target_pairs={{0,2},{2,0},{1,3},{3,1},{4,6},{6,4},{5,7},{7,5},{8,10},{10,8},{9,1... | collective-permute-start | bytes 98312 | tf_op jit(solution)/shard_map/ppermute | solution.py:412
  47.5 8.3 %collective-permute-start.22 = (bf16[288,128]{1,0:T(8,128)(2,1)S(1)}, bf16[288,128]{1,0:T(8,128)(2,1)S(1)}, u32[]{:S(2)}, u32[]{:S(2)}) collective-permute-start(bf16[288,128]{1,0:T(8,128)(2,1)S(1)} %get-tuple-element.76.refs_0_), channel_id=1, source_target_pairs={{0,12},{4,8},{8,4},{12,0},{1,13},{5,9},{9,5},{13,1},{2,14},{6,10},... | collective-permute-start | bytes 221192 | tf_op jit(solution)/shard_map/ppermute | solution.py:412
  49.6 6.7 %collective-permute-start.21 = (bf16[288,128]{1,0:T(8,128)(2,1)S(1)}, bf16[288,128]{1,0:T(8,128)(2,1)S(1)}, u32[]{:S(2)}, u32[]{:S(2)}) collective-permute-start(bf16[288,128]{1,0:T(8,128)(2,1)S(1)} %get-tuple-element.76.refs_0_), channel_id=1, source_target_pairs={{0,8},{4,12},{8,0},{12,4},{1,9},{5,13},{9,1},{13,5},{2,10},{6,14},... | collective-permute-start | bytes 221192 | tf_op jit(solution)/shard_map/ppermute | solution.py:412
  49.6 6.7 %collective-permute-start.20 = (bf16[288,128]{1,0:T(8,128)(2,1)S(1)}, bf16[288,128]{1,0:T(8,128)(2,1)S(1)}, u32[]{:S(2)}, u32[]{:S(2)}) collective-permute-start(bf16[288,128]{1,0:T(8,128)(2,1)S(1)} %get-tuple-element.76.refs_0_), channel_id=1, source_target_pairs={{0,4},{4,0},{8,12},{12,8},{1,5},{5,1},{9,13},{13,9},{2,6},{6,2},{1... | collective-permute-start | bytes 221192 | tf_op jit(solution)/shard_map/ppermute | solution.py:412
  52.0 3.9 %collective-permute-start.23 = (bf16[112,128]{1,0:T(8,128)(2,1)S(1)}, bf16[112,128]{1,0:T(8,128)(2,1)S(1)}, u32[]{:S(2)}, u32[]{:S(2)}) collective-permute-start(bf16[112,128]{1,0:T(8,128)(2,1)S(1)} %get-tuple-element.77.refs_4_), channel_id=1, source_target_pairs={{0,2},{2,0},{1,3},{3,1},{4,6},{6,4},{5,7},{7,5},{8,10},{10,8},{9,1... | collective-permute-start | bytes 86024 | tf_op jit(solution)/shard_map/ppermute | solution.py:412
  56.3 9.0 %collective-permute-start.24 = (bf16[1152,128]{1,0:T(8,128)(2,1)S(1)}, bf16[1152,128]{1,0:T(8,128)(2,1)S(1)}, u32[]{:S(2)}, u32[]{:S(2)}) collective-permute-start(bf16[1152,128]{1,0:T(8,128)(2,1)S(1)} %get-tuple-element.78.refs_0_), channel_id=1, source_target_pairs={{0,2},{2,0},{1,3},{3,1},{4,6},{6,4},{5,7},{7,5},{8,10},{10,8},{9,1... | collective-permute-start | bytes 884744 | tf_op jit(solution)/shard_map/ppermute | solution.py:412
  57.3 6.1 %collective-permute-start.27 = (bf16[224,128]{1,0:T(8,128)(2,1)S(1)}, bf16[224,128]{1,0:T(8,128)(2,1)S(1)}, u32[]{:S(2)}, u32[]{:S(2)}) collective-permute-start(bf16[224,128]{1,0:T(8,128)(2,1)S(1)} %get-tuple-element.79.refs_2_), channel_id=1, source_target_pairs={{0,12},{4,8},{8,4},{12,0},{1,13},{5,9},{9,5},{13,1},{2,14},{6,10},... | collective-permute-start | bytes 172040 | tf_op jit(solution)/shard_map/ppermute | solution.py:412
  59.8 5.5 %collective-permute-start.26 = (bf16[224,128]{1,0:T(8,128)(2,1)S(1)}, bf16[224,128]{1,0:T(8,128)(2,1)S(1)}, u32[]{:S(2)}, u32[]{:S(2)}) collective-permute-start(bf16[224,128]{1,0:T(8,128)(2,1)S(1)} %get-tuple-element.79.refs_2_), channel_id=1, source_target_pairs={{0,8},{4,12},{8,0},{12,4},{1,9},{5,13},{9,1},{13,5},{2,10},{6,14},... | collective-permute-start | bytes 172040 | tf_op jit(solution)/shard_map/ppermute | solution.py:412
  59.8 5.5 %collective-permute-start.25 = (bf16[224,128]{1,0:T(8,128)(2,1)S(1)}, bf16[224,128]{1,0:T(8,128)(2,1)S(1)}, u32[]{:S(2)}, u32[]{:S(2)}) collective-permute-start(bf16[224,128]{1,0:T(8,128)(2,1)S(1)} %get-tuple-element.79.refs_2_), channel_id=1, source_target_pairs={{0,4},{4,0},{8,12},{12,8},{1,5},{5,1},{9,13},{13,9},{2,6},{6,2},{1... | collective-permute-start | bytes 172040 | tf_op jit(solution)/shard_map/ppermute | solution.py:412
  61.7 1.2 %collective-permute-start.19 = (f32[4,128]{1,0:T(4,128)S(1)}, f32[4,128]{1,0:T(4,128)S(1)}, u32[]{:S(2)}, u32[]{:S(2)}) collective-permute-start(f32[4,128]{1,0:T(4,128)S(1)} %get-tuple-element.75.small_ref), channel_id=1, source_target_pairs={{0,1},{1,0},{2,3},{3,2},{4,5},{5,4},{6,7},{7,6},{8,9},{9,8},{10,11... | collective-permute-start | bytes 6152 | tf_op jit(solution)/shard_map/ppermute | solution.py:412

commit v11 on v10

--- a/solution.py
+++ b/solution.py
@@ -330,6 +330,67 @@
     split(g_ref, where_ref[BATCH], keep_ref, send_refs)
 
 
+def lane_half(shape):
+    return lax.broadcasted_iota(jnp.int32, shape, len(shape) - 1) < LANES // 2
+
+
+def low_pair(a, b):
+    return jnp.where(lane_half(a.shape), a, pltpu.roll(b, LANES // 2, axis=1))
+
+
+def high_pair(a, b):
+    return jnp.where(lane_half(a.shape), pltpu.roll(a, LANES // 2, axis=1), b)
+
+
+def half_kernel(flip, where_ref, f_ref, halo_ref, far_ref, own_ref, other_ref, out_ref, d_ref):
+    rows, cols, chans = f_ref.shape
+    half = rows // 2
+    c = where_ref[0]
+    upper = (where_ref[BATCH] ^ flip) == 1
+    near = halo_ref[pl.ds(pl.multiple_of(2 * cols * (1 - c), 16), cols)]
+    far = far_ref[pl.ds(pl.multiple_of(2 * cols * c, 16), cols)]
+    before = jnp.where(c == 0, near, far)
+    after = jnp.where(c == 0, far, near)
+    for r in range(rows):
+        mine, theirs = own_ref[r % half].astype(F32), other_ref[r % half].astype(F32)
+        mid = jnp.where(c == (0 if r < half else 1), mine, theirs)
+        mid = jnp.where(upper, pltpu.roll(mid, LANES // 2, axis=1), mid)
+        pair = low_pair(shift_cells(mid, -1), mid)
+        d_ref[r] = jnp.concatenate([pair, shift_cells(mid, 1)], axis=1).astype(BF16)
+
+    def part(x, first):
+        n = x.shape[0]
+        rhs = d_ref[first : first + n].reshape(n * cols, 2 * LANES)
+        return dot(x.reshape(n * cols, chans), rhs, ((0,), (0,)))
+
+    taps = [
+        part(f_ref[0 : rows - 1], 1) + part(before[None], 0),
+        part(f_ref[...], 0),
+        part(f_ref[1:rows], 0) + part(after[None], rows - 1),
+    ]
+    last = [g[:, LANES:] for g in taps]
+    for i in range(3):
+        out_ref[chans * i : chans * (i + 1)] = taps[i][:, :LANES].astype(out_ref.dtype)
+    out_ref[3 * chans : 4 * chans] = low_pair(last[0], last[1]).astype(out_ref.dtype)
+    out_ref[4 * chans :] = low_pair(last[2][: chans // 2], last[2][chans // 2 :]).astype(out_ref.dtype)
+
+
+def unpack(place, own_ref, other_ref, out_ref):
+    rows = own_ref.shape[0]
+    chans = out_ref.shape[0] // 9
+    own, other = own_ref[...].astype(F32), other_ref[...].astype(F32)
+    low = jnp.where(place == 0, own, other)
+    high = jnp.where(place == 0, other, own)
+    first, second = low_pair(low, high), high_pair(low, high)
+    for i in range(3):
+        out_ref[chans * 3 * i : chans * (3 * i + 1)] = first[chans * i : chans * (i + 1)]
+        out_ref[chans * (3 * i + 1) : chans * (3 * i + 2)] = second[chans * i : chans * (i + 1)]
+    out_ref[chans * 2 : chans * 3] = first[3 * chans : 4 * chans]
+    out_ref[chans * 5 : chans * 6] = second[3 * chans : 4 * chans]
+    out_ref[chans * 8 : chans * 8 + chans // 2] = first[4 * chans : rows]
+    out_ref[chans * 8 + chans // 2 : chans * 9] = second[4 * chans : rows]
+
+
 def cls_split_kernel(where_ref, cls_ref, theirs_ref, small_ref, keep_ref, *rest):
     *send_refs, total_ref = rest
     total_ref[...] = cls_ref[...] + theirs_ref[...]
@@ -390,10 +451,12 @@
     join(where_ref[BATCH], refs[n_in:-2], refs[-1])
 
 
-def out_kernel(n_in, n_cls, where_ref, small_ref, theirs_ref, *refs):
+def out_kernel(n_in, n_cls, halves, where_ref, small_ref, theirs_ref, *refs):
     in_refs, cls_in_refs, refs = refs[:n_in], refs[n_in : n_in + n_cls], refs[n_in + n_cls :]
     out_ref, bias_ref, cls_out_ref, cls_bias_ref, loss_ref, cls_whole_ref, *whole_ref = refs
-    if whole_ref:
+    if halves:
+        unpack(where_ref[BATCH], in_refs[0], in_refs[1], out_ref)
+    elif whole_ref:
         join(where_ref[BATCH], in_refs, whole_ref[0])
         out_ref[...] = whole_ref[0][: out_ref.shape[0]]
     else:
@@ -485,7 +548,8 @@
         [((half + 2, cols, LANES), BF16)],
     )
     theirs = swap(other, "chan")
-    far = swap(halo, "chan")
+    later, _ = lax.optimization_barrier((halo, loss))
+    far = swap(later, "chan")
     cls_total = round_up(9 * LOGITS, 16 * pages * tiles)
     gcls, gcls_other = call(
         cls_kernel, "cls", 1.5, [((cls_total, outs), F32)] * 2, [where, hid, dt]
@@ -495,12 +559,23 @@
     total = round_up(9 * chans, 16 * pages * tiles)
     first, second = total // pages, total // (pages * tiles)
     cfirst, csecond = cls_total // tiles, cls_total // (pages * tiles)
-    keep, *sends = call(
-        shared_kernel, "shared", 4,
-        [((first, outs), F32)] + [((first, outs), BF16)] * (pages - 1),
-        [where, f, halo, far, own, theirs],
-        [((rows, cols, 3 * outs), BF16), ((total, outs), F32)],
-    )
+    halves = pages == 2 and outs == LANES and first % (16 * tiles) == 0 and total == 9 * chans
+    shared_inputs = [where, f, halo, far, own, theirs]
+    if halves:
+        scratch = [((rows, cols, 2 * LANES), BF16)]
+        sends = call(
+            functools.partial(half_kernel, 1), "shared_sent", 2, [((first, outs), BF16)], shared_inputs, scratch
+        )
+        (keep,) = call(
+            functools.partial(half_kernel, 0), "shared_kept", 2, [((first, outs), F32)], shared_inputs, scratch
+        )
+    else:
+        keep, *sends = call(
+            shared_kernel, "shared", 4,
+            [((first, outs), F32)] + [((first, outs), BF16)] * (pages - 1),
+            shared_inputs,
+            [((rows, cols, 3 * outs), BF16), ((total, outs), F32)],
+        )
     ckeep, *csends = call(
         cls_split_kernel, "cls_split", 0.6,
         [((cfirst, outs), F32)] + [((cfirst + TRIO, outs), BF16)] * (tiles - 1),
@@ -533,7 +608,7 @@
         [where, done] + others(done, "tile") + [cdone] + others(cdone, "batch"),
     )
     grad_shared, bias, grad_cls, cls_bias, loss = call(
-        functools.partial(out_kernel, pages, tiles), "out", 1.5,
+        functools.partial(out_kernel, pages, tiles, halves), "out", 1.5,
         [((9 * chans, outs), F32), ((1, outs), F32), ((3, 3, LOGITS, outs), F32), ((1, LOGITS), F32), ((1, 1), F32)],
         [where, small, small_theirs, block] + others(block, "batch") + [cblock] + others(cblock, "tile"),
         [((cls_total, outs), F32)] + ([((total, outs), F32)] if total > 9 * chans else []),

time: 66.8 us -> 66.8 us (level)
  waiting for transfers between devices: 15.7 us -> 12.8 us
  Pallas kernels: 15.5 us -> 18.3 us
    ppermute x27, waiting for transfers between devices: 15.7 us -> 12.8 us  [swap(): return lax.ppermute(x, axis, [(i, i ^ bit) for i in range(size)])]
    pallas_call x11 -> x12, Pallas kernels: 15.5 us -> 18.3 us  [call(): pl.pallas_call(functools.partial(kernel, inputs[0]), in_specs=(specs or [...]
  transfers between devices with their start and end apart: 28 -> 28, of which waited for: 11 -> 10; matrix products, arithmetic and copies ran while one was open for 0% -> 0% of each run, Pallas kernels for 21% -> 25%
where the time goes in v11:
time: 66.8 us; the launch traced here: 66.6 us
  starting transfers between devices  33.7 us (50%)
  Pallas kernels  18.3 us (27%)
  waiting for transfers between devices  12.8 us (19%)
  local copies, waits for them, and re-layouts  0.97 us (1%)
  between operations  0.81 us (1%)
    ppermute x27, starting transfers between devices, swap(): return lax.ppermute(x, axis, [(i, i ^ bit) for i in range(size)])  33 us
    pallas_call x12, Pallas kernels, call(): pl.pallas_call(functools.partial(kernel, inputs[0]), in_specs=(specs or [...  18.3 us
    ppermute x27, waiting for transfers between devices, swap(): return lax.ppermute(x, axis, [(i, i ^ bit) for i in range(size)])  12.8 us
  transfers between devices with their start and end apart: 28, of which 10 were waited for; matrix products, arithmetic and copies ran while one was open for 0% of the time, Pallas kernels for 25%

profile of v11, /device:TPU:0, one launch (start us, length us, event | category | flops | bytes accessed | tf_op | source)
XLA Modules:
  0.0 66.6 jit_solution(2992603824228977389)
XLA Ops:
  0.6 0.5 collective-permute-start.1
  1.2 0.9 %copy-done.3 = s32[1,12,2304]{2,0,1:T(1,128)S(1)} copy-done((s32[1,12,2304]{2,0,1:T(1,128)S(1)}, s32[1,12,2304]{2,0,1:T(1,128)}, u32[]{:S(2)}) %copy-start.3) | copy-done | bytes 110616
  2.1 2.0 %edge.1 = (bf16[784,256]{1,0:T(8,128)(2,1)S(1)}, bf16[12,16,256]{2,1,0:T(8,128)(2,1)S(1)}, f32[8,128]{1,0:T(8,128)S(1)}, bf16[9,256,256]{2,1,0:T(8,128)(2,1)S(1)}) custom-call(bf16[12,256,256]{2,1,0:T(8,128)(2,1)} %bitcast.12, s32[12,1,2304]{2,1,0:T(1,128)S(1)} %bitcast.17), custom_call_target="tpu_custom_call" | custom-call | flops 2000000000 | bytes 2000000 | tf_op jit(solution)/shard_map/edge/pallas_call | solution.py:43
  4.1 0.7 %collective-permute-start = (bf16[784,256]{1,0:T(8,128)(2,1)S(1)}, bf16[784,256]{1,0:T(8,128)(2,1)S(1)}, u32[]{:S(2)}, u32[]{:S(2)}) collective-permute-start(bf16[784,256]{1,0:T(8,128)(2,1)S(1)} %get-tuple-element.44), channel_id=1, source_target_pairs={{1,4},{4,1},{5,8},{8,5},{9,12},{12,9},{3,6},{6,3},{7,10},{10,7},{1... | collective-permute-start | bytes 1204232 | tf_op jit(solution)/shard_map/ppermute | solution.py:519
  4.8 4.0 %collective-permute-start.2 = (f32[128]{0:T(128)S(1)}, f32[128]{0:T(128)S(1)}, u32[]{:S(2)}, u32[]{:S(2)}) collective-permute-start(f32[128]{0:T(128)S(1)} %copy-done.4), channel_id=1, source_target_pairs={{0,1},{1,0},{2,3},{3,2},{4,5},{5,4},{6,7},{7,6},{8,9},{9,8},{10,11... | collective-permute-start | bytes 1544 | tf_op jit(solution)/shard_map/ppermute | solution.py:475
  8.8 0.1 collective-permute-start.4
  8.9 1.5 %collective-permute-start.3 = (f32[8,128]{1,0:T(8,128)S(1)}, f32[8,128]{1,0:T(8,128)S(1)}, u32[]{:S(2)}, u32[]{:S(2)}) collective-permute-start(f32[8,128]{1,0:T(8,128)S(1)} %get-tuple-element.45), channel_id=1, source_target_pairs={{0,2},{2,0},{1,3},{3,1},{4,6},{6,4},{5,7},{7,5},{8,10},{10,8},{9,1... | collective-permute-start | bytes 12296 | tf_op jit(solution)/shard_map/ppermute | solution.py:475
  10.4 0.0 collective-permute-done.2
  10.4 0.0 collective-permute-done.1.w1b_ref
  10.4 0.0 copy-start.5
  10.4 2.4 %inner.1.inner_ref = bf16[7,256,256]{2,1,0:T(8,128)(2,1)S(1)} custom-call(bf16[9,256,256]{2,1,0:T(8,128)(2,1)S(1)} %get-tuple-element.46.near_ref, bf16[3,3,256,128]{3,2,1,0:T(8,128)(2,1)S(1)} %copy-done.1, bf16[3,3,256,128]{3,2,1,0:T(8,128)(2,1)S(1)} %collective-permute-done.1.w1b_ref, f32[1,128]{1,0:T(1,128)S(1)} %bitcast.18, f32[1,128]{1,0:T(1,128)S(1)} %bitcast.21), custom_call_target="tpu_custom_call" | custom-call | flops 3000000000 | bytes 3000000 | tf_op jit(solution)/shard_map/inner/pallas_call | solution.py:43
  12.8 0.0 collective-permute-done.3
  12.8 2.9 %collective-permute-start.8 = (f32[8,128]{1,0:T(8,128)S(1)}, f32[8,128]{1,0:T(8,128)S(1)}, u32[]{:S(2)}, u32[]{:S(2)}) collective-permute-start(f32[8,128]{1,0:T(8,128)S(1)} %add.3.rest_0_), channel_id=1, source_target_pairs={{0,12},{4,8},{8,4},{12,0},{1,13},{5,9},{9,5},{13,1},{2,14},{6,10},... | collective-permute-start | bytes 12296 | tf_op jit(solution)/shard_map/ppermute | solution.py:475
  15.7 0.2 collective-permute-start.7
  15.9 1.3 %collective-permute-start.6 = (f32[8,128]{1,0:T(8,128)S(1)}, f32[8,128]{1,0:T(8,128)S(1)}, u32[]{:S(2)}, u32[]{:S(2)}) collective-permute-start(f32[8,128]{1,0:T(8,128)S(1)} %add.3.rest_0_), channel_id=1, source_target_pairs={{0,4},{4,0},{8,12},{12,8},{1,5},{5,1},{9,13},{13,9},{2,6},{6,2},{1... | collective-permute-start | bytes 12296 | tf_op jit(solution)/shard_map/ppermute | solution.py:475
  17.2 0.0 collective-permute-done.halo_ref
  17.2 0.0 collective-permute-done.4
  17.2 4.1 %head.1 = (bf16[10,256,256]{2,1,0:T(8,128)(2,1)S(1)}, f32[8,256,128]{2,1,0:T(8,128)S(1)}, f32[1,128]{1,0:T(1,128)S(1)}, bf16[1152,256]{1,0:T(8,128)(2,1)S(1)}) custom-call(bf16[9,256,256]{2,1,0:T(8,128)(2,1)S(1)} %get-tuple-element.46.near_ref, bf16[7,256,256]{2,1,0:T(8,128)(2,1)S(1)} %inner.1.inner_ref, bf16[784,256]{1,0:T(8,128)(2,1)S(1)} %collective-permute-done.halo_ref, ...), custom_call_target="tpu_custom_call" | custom-call | flops 5000000000 | bytes 5000000 | tf_op jit(solution)/shard_map/head/pallas_call | solution.py:43
  21.3 0.1 collective-permute-start.5
  21.4 0.0 collective-permute-done.7.rest_2_
  21.4 0.0 collective-permute-done.6.rest_1_
  21.4 1.6 %back.1 = (bf16[6,336,256]{2,1,0:T(8,128)(2,1)S(1)}, bf16[6,256,128]{2,1,0:T(8,128)(2,1)S(1)}, bf16[6,256,128]{2,1,0:T(8,128)(2,1)S(1)}, f32[4,128]{1,0:T(4,128)S(1)}) custom-call(bf16[10,256,256]{2,1,0:T(8,128)(2,1)S(1)} %get-tuple-element.53.hid_ref, f32[8,256,128]{2,1,0:T(8,128)S(1)} %get-tuple-element.54.dz_ref, ...), custom_call_target="tpu_custom_call" | custom-call | flops 4000000000 | bytes 4000000 | tf_op jit(solution)/shard_map/back/pallas_call | solution.py:43
  23.1 0.5 collective-permute-start.9
  23.6 1.0 %cls.1 = (f32[896,128]{1,0:T(8,128)S(1)}, f32[896,128]{1,0:T(8,128)S(1)}) custom-call(bf16[10,256,256]{2,1,0:T(8,128)(2,1)S(1)} %get-tuple-element.53.hid_ref, bf16[6,336,256]{2,1,0:T(8,128)(2,1)S(1)} %get-tuple-element.59.dt_ref), custom_call_target="tpu_custom_call" | custom-call | flops 1500000000 | bytes 1500000 | tf_op jit(solution)/shard_map/cls/pallas_call | solution.py:43
  24.6 0.1 collective-permute-start.10
  24.7 0.3 collective-permute-done.9.other_ref
  25.0 0.1 copy-done
  25.0 2.6 %shared_sent.1 = bf16[1152,128]{1,0:T(8,128)(2,1)S(1)} custom-call(bf16[12,256,256]{2,1,0:T(8,128)(2,1)S(1)} %bitcast.13, bf16[784,256]{1,0:T(8,128)(2,1)S(1)} %collective-permute-done.halo_ref, bf16[784,256]{1,0:T(8,128)(2,1)S(1)} %collective-permute-done.5.far_ref, bf16[6,256,128]{2,1,0:T(8,128)(2,1)S(1)} %get-tuple-element.56.own_ref, ...), custom_call_target="tpu_custom_call" | custom-call | flops 2000000000 | bytes 2000000 | tf_op jit(solution)/shard_map/shared_sent/pallas_call | solution.py:43
  27.7 1.2 %collective-permute-start.11 = (bf16[1152,128]{1,0:T(8,128)(2,1)S(1)}, bf16[1152,128]{1,0:T(8,128)(2,1)S(1)}, u32[]{:S(2)}, u32[]{:S(2)}) collective-permute-start(bf16[1152,128]{1,0:T(8,128)(2,1)S(1)} %shared_sent.1), channel_id=1, source_target_pairs={{0,2},{2,0},{1,3},{3,1},{4,6},{6,4},{5,7},{7,5},{8,10},{10,8},{9,1... | collective-permute-start | bytes 884744 | tf_op jit(solution)/shard_map/ppermute | solution.py:475
  28.9 0.1 cls_split.1
  28.9 2.9 %collective-permute-start.12 = (bf16[240,128]{1,0:T(8,128)(2,1)S(1)}, bf16[240,128]{1,0:T(8,128)(2,1)S(1)}, u32[]{:S(2)}, u32[]{:S(2)}) collective-permute-start(bf16[240,128]{1,0:T(8,128)(2,1)S(1)} %get-tuple-element.63), channel_id=1, source_target_pairs={{0,12},{4,8},{8,4},{12,0},{1,13},{5,9},{9,5},{13,1},{2,14},{6,10},... | collective-permute-start | bytes 184328 | tf_op jit(solution)/shard_map/ppermute | solution.py:475
  31.9 1.5 %collective-permute-start.14 = (bf16[240,128]{1,0:T(8,128)(2,1)S(1)}, bf16[240,128]{1,0:T(8,128)(2,1)S(1)}, u32[]{:S(2)}, u32[]{:S(2)}) collective-permute-start(bf16[240,128]{1,0:T(8,128)(2,1)S(1)} %get-tuple-element.65), channel_id=1, source_target_pairs={{0,4},{4,0},{8,12},{12,8},{1,5},{5,1},{9,13},{13,9},{2,6},{6,2},{1... | collective-permute-start | bytes 184328 | tf_op jit(solution)/shard_map/ppermute | solution.py:475
  33.4 2.8 %shared_kept.1.base_ref = f32[1152,128]{1,0:T(8,128)S(1)} custom-call(bf16[12,256,256]{2,1,0:T(8,128)(2,1)S(1)} %bitcast.14, bf16[784,256]{1,0:T(8,128)(2,1)S(1)} %collective-permute-done.halo_ref, bf16[784,256]{1,0:T(8,128)(2,1)S(1)} %collective-permute-done.5.far_ref, bf16[6,256,128]{2,1,0:T(8,128)(2,1)S(1)} %get-tuple-element.56.own_ref, ...), custom_call_target="tpu_custom_call" | custom-call | flops 2000000000 | bytes 2000000 | tf_op jit(solution)/shard_map/shared_kept/pallas_call | solution.py:43
  36.2 0.0 collective-permute-done.12.refs_1_
  36.3 1.2 %collective-permute-done.13.refs_2_ = bf16[240,128]{1,0:T(8,128)(2,1)S(1)} collective-permute-done((bf16[240,128]{1,0:T(8,128)(2,1)S(1)}, bf16[240,128]{1,0:T(8,128)(2,1)S(1)}, u32[]{:S(2)}, u32[]{:S(2)}) %collective-permute-start.13) | collective-permute-done | bytes 61472 | tf_op jit(solution)/shard_map/ppermute | solution.py:475
  37.5 0.1 collective-permute-done.14.refs_3_
  37.5 0.0 collective-permute-done.11.refs_0_
  37.6 0.1 sum.1
  37.7 2.6 %collective-permute-start.15 = (bf16[288,128]{1,0:T(8,128)(2,1)S(1)}, bf16[288,128]{1,0:T(8,128)(2,1)S(1)}, u32[]{:S(2)}, u32[]{:S(2)}) collective-permute-start(bf16[288,128]{1,0:T(8,128)(2,1)S(1)} %get-tuple-element.69), channel_id=1, source_target_pairs={{0,12},{4,8},{8,4},{12,0},{1,13},{5,9},{9,5},{13,1},{2,14},{6,10},... | collective-permute-start | bytes 221192 | tf_op jit(solution)/shard_map/ppermute | solution.py:475
  40.3 0.0 collective-permute-start.16
  40.3 1.9 %collective-permute-start.17 = (bf16[288,128]{1,0:T(8,128)(2,1)S(1)}, bf16[288,128]{1,0:T(8,128)(2,1)S(1)}, u32[]{:S(2)}, u32[]{:S(2)}) collective-permute-start(bf16[288,128]{1,0:T(8,128)(2,1)S(1)} %get-tuple-element.71), channel_id=1, source_target_pairs={{0,4},{4,0},{8,12},{12,8},{1,5},{5,1},{9,13},{13,9},{2,6},{6,2},{1... | collective-permute-start | bytes 221192 | tf_op jit(solution)/shard_map/ppermute | solution.py:475
  42.1 0.9 %collective-permute-start.18 = (bf16[128,128]{1,0:T(8,128)(2,1)S(1)}, bf16[128,128]{1,0:T(8,128)(2,1)S(1)}, u32[]{:S(2)}, u32[]{:S(2)}) collective-permute-start(bf16[128,128]{1,0:T(8,128)(2,1)S(1)} %get-tuple-element.72), channel_id=1, source_target_pairs={{0,2},{2,0},{1,3},{3,1},{4,6},{6,4},{5,7},{7,5},{8,10},{10,8},{9,1... | collective-permute-start | bytes 98312 | tf_op jit(solution)/shard_map/ppermute | solution.py:475
  43.1 3.0 %collective-permute-done.18.refs_3_ = bf16[128,128]{1,0:T(8,128)(2,1)S(1)} collective-permute-done((bf16[128,128]{1,0:T(8,128)(2,1)S(1)}, bf16[128,128]{1,0:T(8,128)(2,1)S(1)}, u32[]{:S(2)}, u32[]{:S(2)}) %collective-permute-start.18) | collective-permute-done | bytes 32800 | tf_op jit(solution)/shard_map/ppermute | solution.py:475
  46.1 0.0 collective-permute-done.15.refs_0_
  46.1 1.2 %collective-permute-done.16.refs_1_ = bf16[288,128]{1,0:T(8,128)(2,1)S(1)} collective-permute-done((bf16[288,128]{1,0:T(8,128)(2,1)S(1)}, bf16[288,128]{1,0:T(8,128)(2,1)S(1)}, u32[]{:S(2)}, u32[]{:S(2)}) %collective-permute-start.16) | collective-permute-done | bytes 73760 | tf_op jit(solution)/shard_map/ppermute | solution.py:475
  47.3 0.0 collective-permute-done.17.refs_2_
  47.3 2.0 %collective-permute-start.22 = (bf16[288,128]{1,0:T(8,128)(2,1)S(1)}, bf16[288,128]{1,0:T(8,128)(2,1)S(1)}, u32[]{:S(2)}, u32[]{:S(2)}) collective-permute-start(bf16[288,128]{1,0:T(8,128)(2,1)S(1)} %get-tuple-element.74.refs_0_), channel_id=1, source_target_pairs={{0,12},{4,8},{8,4},{12,0},{1,13},{5,9},{9,5},{13,1},{2,14},{6,10},... | collective-permute-start | bytes 221192 | tf_op jit(solution)/shard_map/ppermute | solution.py:475
  49.4 0.0 collective-permute-start.21
  49.4 2.4 %collective-permute-start.20 = (bf16[288,128]{1,0:T(8,128)(2,1)S(1)}, bf16[288,128]{1,0:T(8,128)(2,1)S(1)}, u32[]{:S(2)}, u32[]{:S(2)}) collective-permute-start(bf16[288,128]{1,0:T(8,128)(2,1)S(1)} %get-tuple-element.74.refs_0_), channel_id=1, source_target_pairs={{0,4},{4,0},{8,12},{12,8},{1,5},{5,1},{9,13},{13,9},{2,6},{6,2},{1... | collective-permute-start | bytes 221192 | tf_op jit(solution)/shard_map/ppermute | solution.py:475
  51.8 0.9 %collective-permute-start.23 = (bf16[112,128]{1,0:T(8,128)(2,1)S(1)}, bf16[112,128]{1,0:T(8,128)(2,1)S(1)}, u32[]{:S(2)}, u32[]{:S(2)}) collective-permute-start(bf16[112,128]{1,0:T(8,128)(2,1)S(1)} %get-tuple-element.75.refs_4_), channel_id=1, source_target_pairs={{0,2},{2,0},{1,3},{3,1},{4,6},{6,4},{5,7},{7,5},{8,10},{10,8},{9,1... | collective-permute-start | bytes 86024 | tf_op jit(solution)/shard_map/ppermute | solution.py:475
  52.7 3.0 %collective-permute-done.23.refs_5_ = bf16[112,128]{1,0:T(8,128)(2,1)S(1)} collective-permute-done((bf16[112,128]{1,0:T(8,128)(2,1)S(1)}, bf16[112,128]{1,0:T(8,128)(2,1)S(1)}, u32[]{:S(2)}, u32[]{:S(2)}) %collective-permute-start.23) | collective-permute-done | bytes 28704 | tf_op jit(solution)/shard_map/ppermute | solution.py:475
  55.6 0.4 collective-permute-done.21.refs_2_
  56.1 0.0 collective-permute-done.20.refs_1_
  56.1 1.0 %collective-permute-start.24 = (bf16[1152,128]{1,0:T(8,128)(2,1)S(1)}, bf16[1152,128]{1,0:T(8,128)(2,1)S(1)}, u32[]{:S(2)}, u32[]{:S(2)}) collective-permute-start(bf16[1152,128]{1,0:T(8,128)(2,1)S(1)} %get-tuple-element.76.refs_0_), channel_id=1, source_target_pairs={{0,2},{2,0},{1,3},{3,1},{4,6},{6,4},{5,7},{7,5},{8,10},{10,8},{9,1... | collective-permute-start | bytes 884744 | tf_op jit(solution)/shard_map/ppermute | solution.py:475
  57.1 2.5 %collective-permute-start.27 = (bf16[224,128]{1,0:T(8,128)(2,1)S(1)}, bf16[224,128]{1,0:T(8,128)(2,1)S(1)}, u32[]{:S(2)}, u32[]{:S(2)}) collective-permute-start(bf16[224,128]{1,0:T(8,128)(2,1)S(1)} %get-tuple-element.77.refs_2_), channel_id=1, source_target_pairs={{0,12},{4,8},{8,4},{12,0},{1,13},{5,9},{9,5},{13,1},{2,14},{6,10},... | collective-permute-start | bytes 172040 | tf_op jit(solution)/shard_map/ppermute | solution.py:475
  59.6 0.0 collective-permute-start.26
  59.6 1.9 %collective-permute-start.25 = (bf16[224,128]{1,0:T(8,128)(2,1)S(1)}, bf16[224,128]{1,0:T(8,128)(2,1)S(1)}, u32[]{:S(2)}, u32[]{:S(2)}) collective-permute-start(bf16[224,128]{1,0:T(8,128)(2,1)S(1)} %get-tuple-element.77.refs_2_), channel_id=1, source_target_pairs={{0,4},{4,0},{8,12},{12,8},{1,5},{5,1},{9,13},{13,9},{2,6},{6,2},{1... | collective-permute-start | bytes 172040 | tf_op jit(solution)/shard_map/ppermute | solution.py:475
  61.5 0.0 collective-permute-start.19
  61.5 1.2 %collective-permute-done.19.theirs_ref = f32[4,128]{1,0:T(4,128)S(1)} collective-permute-done((f32[4,128]{1,0:T(4,128)S(1)}, f32[4,128]{1,0:T(4,128)S(1)}, u32[]{:S(2)}, u32[]{:S(2)}) %collective-permute-start.19) | collective-permute-done | bytes 2080 | tf_op jit(solution)/shard_map/ppermute | solution.py:475
  62.6 0.5 collective-permute-done.27.refs_5_
  63.2 1.9 %collective-permute-done.26.refs_4_ = bf16[224,128]{1,0:T(8,128)(2,1)S(1)} collective-permute-done((bf16[224,128]{1,0:T(8,128)(2,1)S(1)}, bf16[224,128]{1,0:T(8,128)(2,1)S(1)}, u32[]{:S(2)}, u32[]{:S(2)}) %collective-permute-start.26) | collective-permute-done | bytes 57376 | tf_op jit(solution)/shard_map/ppermute | solution.py:475
  65.1 0.0 collective-permute-done.25.refs_3_
  65.1 0.0 collective-permute-done.24.refs_1_
  65.1 1.5 %out.1 = (f32[2304,128]{1,0:T(8,128)}, f32[1,128]{1,0:T(1,128)}, f32[3,3,99,128]{3,2,1,0:T(8,128)}, f32[1,99]{1,0:T(1,128)}, f32[1,1]{1,0:T(1,128)}) custom-call(f32[4,128]{1,0:T(4,128)S(1)} %get-tuple-element.73.small_ref, f32[4,128]{1,0:T(4,128)S(1)} %collective-permute-done.19.theirs_ref, bf16[1152,128]{1,0:T(8,128)(2,1)S(1)} %get-tuple-element.76.refs_0_, ...), custom_call_target="tpu_custom_call" | custom-call | flops 1500000000 | bytes 1500000 | tf_op jit(solution)/shard_map/out/pallas_call | solution.py:43
  (17 shorter events, 0.1 us)
Async XLA Ops:
  0.6 9.7 %collective-permute-start.1 = (bf16[3,3,256,128]{3,2,1,0:T(8,128)(2,1)}, bf16[3,3,256,128]{3,2,1,0:T(8,128)(2,1)S(1)}, u32[]{:S(2)}, u32[]{:S(2)}) collective-permute-start(bf16[3,3,256,128]{3,2,1,0:T(8,128)(2,1)} %w1a_ref.3), channel_id=1, source_target_pairs={{0,1},{1,0},{2,3},{3,2},{4,5},{5,4},{6,7},{7,6},{8,9},{9,8},{10,11... | collective-permute-start | bytes 1769480 | tf_op jit(solution)/shard_map/ppermute | solution.py:475
  1.2 0.9 %copy-start.3 = (s32[1,12,2304]{2,0,1:T(1,128)S(1)}, s32[1,12,2304]{2,0,1:T(1,128)}, u32[]{:S(2)}) copy-start(s32[1,12,2304]{2,0,1:T(1,128)} %param.7) | copy-start | bytes 331780
  2.0 2.7 %copy-start.4 = (f32[128]{0:T(128)S(1)}, f32[128]{0:T(128)}, u32[]{:S(2)}) copy-start(f32[128]{0:T(128)} %param.9) | copy-start | bytes 1540
  2.0 6.7 %copy-start.2 = (bf16[3,3,128,99]{2,3,1,0:T(8,128)(2,1)S(1)}, bf16[3,3,128,99]{2,3,1,0:T(8,128)(2,1)}, u32[]{:S(2)}) copy-start(bf16[3,3,128,99]{2,3,1,0:T(8,128)(2,1)} %param.10) | copy-start | bytes 684292
  2.1 8.3 %copy-start.1 = (bf16[3,3,256,128]{3,2,1,0:T(8,128)(2,1)S(1)}, bf16[3,3,256,128]{3,2,1,0:T(8,128)(2,1)}, u32[]{:S(2)}) copy-start(bf16[3,3,256,128]{3,2,1,0:T(8,128)(2,1)} %w1a_ref.3) | copy-start | bytes 1769476
  4.1 13.2 %collective-permute-start = (bf16[784,256]{1,0:T(8,128)(2,1)S(1)}, bf16[784,256]{1,0:T(8,128)(2,1)S(1)}, u32[]{:S(2)}, u32[]{:S(2)}) collective-permute-start(bf16[784,256]{1,0:T(8,128)(2,1)S(1)} %get-tuple-element.44), channel_id=1, source_target_pairs={{1,4},{4,1},{5,8},{8,5},{9,12},{12,9},{3,6},{6,3},{7,10},{10,7},{1... | collective-permute-start | bytes 1204232 | tf_op jit(solution)/shard_map/ppermute | solution.py:519
  4.8 5.6 %collective-permute-start.2 = (f32[128]{0:T(128)S(1)}, f32[128]{0:T(128)S(1)}, u32[]{:S(2)}, u32[]{:S(2)}) collective-permute-start(f32[128]{0:T(128)S(1)} %copy-done.4), channel_id=1, source_target_pairs={{0,1},{1,0},{2,3},{3,2},{4,5},{5,4},{6,7},{7,6},{8,9},{9,8},{10,11... | collective-permute-start | bytes 1544 | tf_op jit(solution)/shard_map/ppermute | solution.py:475
  8.8 8.5 %collective-permute-start.4 = (bf16[3,3,128,99]{2,3,1,0:T(8,128)(2,1)S(1)}, bf16[3,3,128,99]{2,3,1,0:T(8,128)(2,1)S(1)}, u32[]{:S(2)}, u32[]{:S(2)}) collective-permute-start(bf16[3,3,128,99]{2,3,1,0:T(8,128)(2,1)S(1)} %copy-done.2), channel_id=1, source_target_pairs={{0,1},{1,0},{2,3},{3,2},{4,5},{5,4},{6,7},{7,6},{8,9},{9,8},{10,11... | collective-permute-start | bytes 684296 | tf_op jit(solution)/shard_map/ppermute | solution.py:475
  8.9 3.9 %collective-permute-start.3 = (f32[8,128]{1,0:T(8,128)S(1)}, f32[8,128]{1,0:T(8,128)S(1)}, u32[]{:S(2)}, u32[]{:S(2)}) collective-permute-start(f32[8,128]{1,0:T(8,128)S(1)} %get-tuple-element.45), channel_id=1, source_target_pairs={{0,2},{2,0},{1,3},{3,1},{4,6},{6,4},{5,7},{7,5},{8,10},{10,8},{9,1... | collective-permute-start | bytes 12296 | tf_op jit(solution)/shard_map/ppermute | solution.py:475
  10.4 6.9 %copy-start.5 = (f32[99]{0:T(128)S(1)}, f32[99]{0:T(128)}, u32[]{:S(2)}) copy-start(f32[99]{0:T(128)} %param.11) | copy-start | bytes 1192
  12.8 8.6 %collective-permute-start.8 = (f32[8,128]{1,0:T(8,128)S(1)}, f32[8,128]{1,0:T(8,128)S(1)}, u32[]{:S(2)}, u32[]{:S(2)}) collective-permute-start(f32[8,128]{1,0:T(8,128)S(1)} %add.3.rest_0_), channel_id=1, source_target_pairs={{0,12},{4,8},{8,4},{12,0},{1,13},{5,9},{9,5},{13,1},{2,14},{6,10},... | collective-permute-start | bytes 12296 | tf_op jit(solution)/shard_map/ppermute | solution.py:475
  15.7 5.7 %collective-permute-start.7 = (f32[8,128]{1,0:T(8,128)S(1)}, f32[8,128]{1,0:T(8,128)S(1)}, u32[]{:S(2)}, u32[]{:S(2)}) collective-permute-start(f32[8,128]{1,0:T(8,128)S(1)} %add.3.rest_0_), channel_id=1, source_target_pairs={{0,8},{4,12},{8,0},{12,4},{1,9},{5,13},{9,1},{13,5},{2,10},{6,14},... | collective-permute-start | bytes 12296 | tf_op jit(solution)/shard_map/ppermute | solution.py:475
  15.9 5.5 %collective-permute-start.6 = (f32[8,128]{1,0:T(8,128)S(1)}, f32[8,128]{1,0:T(8,128)S(1)}, u32[]{:S(2)}, u32[]{:S(2)}) collective-permute-start(f32[8,128]{1,0:T(8,128)S(1)} %add.3.rest_0_), channel_id=1, source_target_pairs={{0,4},{4,0},{8,12},{12,8},{1,5},{5,1},{9,13},{13,9},{2,6},{6,2},{1... | collective-permute-start | bytes 12296 | tf_op jit(solution)/shard_map/ppermute | solution.py:475
  21.3 3.7 %collective-permute-start.5 = (bf16[784,256]{1,0:T(8,128)(2,1)S(1)}, bf16[784,256]{1,0:T(8,128)(2,1)S(1)}, u32[]{:S(2)}, u32[]{:S(2)}) collective-permute-start(bf16[784,256]{1,0:T(8,128)(2,1)S(1)} %collective-permute-done.halo_ref), channel_id=1, source_target_pairs={{0,1},{1,0},{2,3},{3,2},{4,5},{5,4},{6,7},{7,6},{8,9},{9,8},{10,11... | collective-permute-start | bytes 1204232 | tf_op jit(solution)/shard_map/ppermute | solution.py:475
  23.1 1.9 %collective-permute-start.9 = (bf16[6,256,128]{2,1,0:T(8,128)(2,1)S(1)}, bf16[6,256,128]{2,1,0:T(8,128)(2,1)S(1)}, u32[]{:S(2)}, u32[]{:S(2)}) collective-permute-start(bf16[6,256,128]{2,1,0:T(8,128)(2,1)S(1)} %get-tuple-element.57), channel_id=1, source_target_pairs={{0,1},{1,0},{2,3},{3,2},{4,5},{5,4},{6,7},{7,6},{8,9},{9,8},{10,11... | collective-permute-start | bytes 1179656 | tf_op jit(solution)/shard_map/ppermute | solution.py:475
  23.6 1.4 %copy-start = (bf16[1,12,256,256]{3,2,1,0:T(8,128)(2,1)S(1)}, bf16[1,12,256,256]{3,2,1,0:T(8,128)(2,1)}, u32[]{:S(2)}) copy-start(bf16[1,12,256,256]{3,2,1,0:T(8,128)(2,1)} %param.6) | copy-start | bytes 4718596
  24.6 4.3 %collective-permute-start.10 = (f32[896,128]{1,0:T(8,128)S(1)}, f32[896,128]{1,0:T(8,128)S(1)}, u32[]{:S(2)}, u32[]{:S(2)}) collective-permute-start(f32[896,128]{1,0:T(8,128)S(1)} %get-tuple-element.61), channel_id=1, source_target_pairs={{0,1},{1,0},{2,3},{3,2},{4,5},{5,4},{6,7},{7,6},{8,9},{9,8},{10,11... | collective-permute-start | bytes 1376264 | tf_op jit(solution)/shard_map/ppermute | solution.py:475
  27.7 9.9 %collective-permute-start.11 = (bf16[1152,128]{1,0:T(8,128)(2,1)S(1)}, bf16[1152,128]{1,0:T(8,128)(2,1)S(1)}, u32[]{:S(2)}, u32[]{:S(2)}) collective-permute-start(bf16[1152,128]{1,0:T(8,128)(2,1)S(1)} %shared_sent.1), channel_id=1, source_target_pairs={{0,2},{2,0},{1,3},{3,1},{4,6},{6,4},{5,7},{7,5},{8,10},{10,8},{9,1... | collective-permute-start | bytes 884744 | tf_op jit(solution)/shard_map/ppermute | solution.py:475
  28.9 7.3 %collective-permute-start.12 = (bf16[240,128]{1,0:T(8,128)(2,1)S(1)}, bf16[240,128]{1,0:T(8,128)(2,1)S(1)}, u32[]{:S(2)}, u32[]{:S(2)}) collective-permute-start(bf16[240,128]{1,0:T(8,128)(2,1)S(1)} %get-tuple-element.63), channel_id=1, source_target_pairs={{0,12},{4,8},{8,4},{12,0},{1,13},{5,9},{9,5},{13,1},{2,14},{6,10},... | collective-permute-start | bytes 184328 | tf_op jit(solution)/shard_map/ppermute | solution.py:475
  31.9 5.6 %collective-permute-start.13 = (bf16[240,128]{1,0:T(8,128)(2,1)S(1)}, bf16[240,128]{1,0:T(8,128)(2,1)S(1)}, u32[]{:S(2)}, u32[]{:S(2)}) collective-permute-start(bf16[240,128]{1,0:T(8,128)(2,1)S(1)} %get-tuple-element.64), channel_id=1, source_target_pairs={{0,8},{4,12},{8,0},{12,4},{1,9},{5,13},{9,1},{13,5},{2,10},{6,14},... | collective-permute-start | bytes 184328 | tf_op jit(solution)/shard_map/ppermute | solution.py:475
  31.9 5.7 %collective-permute-start.14 = (bf16[240,128]{1,0:T(8,128)(2,1)S(1)}, bf16[240,128]{1,0:T(8,128)(2,1)S(1)}, u32[]{:S(2)}, u32[]{:S(2)}) collective-permute-start(bf16[240,128]{1,0:T(8,128)(2,1)S(1)} %get-tuple-element.65), channel_id=1, source_target_pairs={{0,4},{4,0},{8,12},{12,8},{1,5},{5,1},{9,13},{13,9},{2,6},{6,2},{1... | collective-permute-start | bytes 184328 | tf_op jit(solution)/shard_map/ppermute | solution.py:475
  37.7 8.4 %collective-permute-start.15 = (bf16[288,128]{1,0:T(8,128)(2,1)S(1)}, bf16[288,128]{1,0:T(8,128)(2,1)S(1)}, u32[]{:S(2)}, u32[]{:S(2)}) collective-permute-start(bf16[288,128]{1,0:T(8,128)(2,1)S(1)} %get-tuple-element.69), channel_id=1, source_target_pairs={{0,12},{4,8},{8,4},{12,0},{1,13},{5,9},{9,5},{13,1},{2,14},{6,10},... | collective-permute-start | bytes 221192 | tf_op jit(solution)/shard_map/ppermute | solution.py:475
  40.3 7.0 %collective-permute-start.16 = (bf16[288,128]{1,0:T(8,128)(2,1)S(1)}, bf16[288,128]{1,0:T(8,128)(2,1)S(1)}, u32[]{:S(2)}, u32[]{:S(2)}) collective-permute-start(bf16[288,128]{1,0:T(8,128)(2,1)S(1)} %get-tuple-element.70), channel_id=1, source_target_pairs={{0,8},{4,12},{8,0},{12,4},{1,9},{5,13},{9,1},{13,5},{2,10},{6,14},... | collective-permute-start | bytes 221192 | tf_op jit(solution)/shard_map/ppermute | solution.py:475
  40.3 7.0 %collective-permute-start.17 = (bf16[288,128]{1,0:T(8,128)(2,1)S(1)}, bf16[288,128]{1,0:T(8,128)(2,1)S(1)}, u32[]{:S(2)}, u32[]{:S(2)}) collective-permute-start(bf16[288,128]{1,0:T(8,128)(2,1)S(1)} %get-tuple-element.71), channel_id=1, source_target_pairs={{0,4},{4,0},{8,12},{12,8},{1,5},{5,1},{9,13},{13,9},{2,6},{6,2},{1... | collective-permute-start | bytes 221192 | tf_op jit(solution)/shard_map/ppermute | solution.py:475
  42.1 3.9 %collective-permute-start.18 = (bf16[128,128]{1,0:T(8,128)(2,1)S(1)}, bf16[128,128]{1,0:T(8,128)(2,1)S(1)}, u32[]{:S(2)}, u32[]{:S(2)}) collective-permute-start(bf16[128,128]{1,0:T(8,128)(2,1)S(1)} %get-tuple-element.72), channel_id=1, source_target_pairs={{0,2},{2,0},{1,3},{3,1},{4,6},{6,4},{5,7},{7,5},{8,10},{10,8},{9,1... | collective-permute-start | bytes 98312 | tf_op jit(solution)/shard_map/ppermute | solution.py:475
  47.3 8.3 %collective-permute-start.22 = (bf16[288,128]{1,0:T(8,128)(2,1)S(1)}, bf16[288,128]{1,0:T(8,128)(2,1)S(1)}, u32[]{:S(2)}, u32[]{:S(2)}) collective-permute-start(bf16[288,128]{1,0:T(8,128)(2,1)S(1)} %get-tuple-element.74.refs_0_), channel_id=1, source_target_pairs={{0,12},{4,8},{8,4},{12,0},{1,13},{5,9},{9,5},{13,1},{2,14},{6,10},... | collective-permute-start | bytes 221192 | tf_op jit(solution)/shard_map/ppermute | solution.py:475
  49.4 6.7 %collective-permute-start.21 = (bf16[288,128]{1,0:T(8,128)(2,1)S(1)}, bf16[288,128]{1,0:T(8,128)(2,1)S(1)}, u32[]{:S(2)}, u32[]{:S(2)}) collective-permute-start(bf16[288,128]{1,0:T(8,128)(2,1)S(1)} %get-tuple-element.74.refs_0_), channel_id=1, source_target_pairs={{0,8},{4,12},{8,0},{12,4},{1,9},{5,13},{9,1},{13,5},{2,10},{6,14},... | collective-permute-start | bytes 221192 | tf_op jit(solution)/shard_map/ppermute | solution.py:475
  49.4 6.7 %collective-permute-start.20 = (bf16[288,128]{1,0:T(8,128)(2,1)S(1)}, bf16[288,128]{1,0:T(8,128)(2,1)S(1)}, u32[]{:S(2)}, u32[]{:S(2)}) collective-permute-start(bf16[288,128]{1,0:T(8,128)(2,1)S(1)} %get-tuple-element.74.refs_0_), channel_id=1, source_target_pairs={{0,4},{4,0},{8,12},{12,8},{1,5},{5,1},{9,13},{13,9},{2,6},{6,2},{1... | collective-permute-start | bytes 221192 | tf_op jit(solution)/shard_map/ppermute | solution.py:475
  51.8 3.9 %collective-permute-start.23 = (bf16[112,128]{1,0:T(8,128)(2,1)S(1)}, bf16[112,128]{1,0:T(8,128)(2,1)S(1)}, u32[]{:S(2)}, u32[]{:S(2)}) collective-permute-start(bf16[112,128]{1,0:T(8,128)(2,1)S(1)} %get-tuple-element.75.refs_4_), channel_id=1, source_target_pairs={{0,2},{2,0},{1,3},{3,1},{4,6},{6,4},{5,7},{7,5},{8,10},{10,8},{9,1... | collective-permute-start | bytes 86024 | tf_op jit(solution)/shard_map/ppermute | solution.py:475
  56.1 9.0 %collective-permute-start.24 = (bf16[1152,128]{1,0:T(8,128)(2,1)S(1)}, bf16[1152,128]{1,0:T(8,128)(2,1)S(1)}, u32[]{:S(2)}, u32[]{:S(2)}) collective-permute-start(bf16[1152,128]{1,0:T(8,128)(2,1)S(1)} %get-tuple-element.76.refs_0_), channel_id=1, source_target_pairs={{0,2},{2,0},{1,3},{3,1},{4,6},{6,4},{5,7},{7,5},{8,10},{10,8},{9,1... | collective-permute-start | bytes 884744 | tf_op jit(solution)/shard_map/ppermute | solution.py:475
  57.1 6.1 %collective-permute-start.27 = (bf16[224,128]{1,0:T(8,128)(2,1)S(1)}, bf16[224,128]{1,0:T(8,128)(2,1)S(1)}, u32[]{:S(2)}, u32[]{:S(2)}) collective-permute-start(bf16[224,128]{1,0:T(8,128)(2,1)S(1)} %get-tuple-element.77.refs_2_), channel_id=1, source_target_pairs={{0,12},{4,8},{8,4},{12,0},{1,13},{5,9},{9,5},{13,1},{2,14},{6,10},... | collective-permute-start | bytes 172040 | tf_op jit(solution)/shard_map/ppermute | solution.py:475
  59.6 5.5 %collective-permute-start.26 = (bf16[224,128]{1,0:T(8,128)(2,1)S(1)}, bf16[224,128]{1,0:T(8,128)(2,1)S(1)}, u32[]{:S(2)}, u32[]{:S(2)}) collective-permute-start(bf16[224,128]{1,0:T(8,128)(2,1)S(1)} %get-tuple-element.77.refs_2_), channel_id=1, source_target_pairs={{0,8},{4,12},{8,0},{12,4},{1,9},{5,13},{9,1},{13,5},{2,10},{6,14},... | collective-permute-start | bytes 172040 | tf_op jit(solution)/shard_map/ppermute | solution.py:475
  59.6 5.5 %collective-permute-start.25 = (bf16[224,128]{1,0:T(8,128)(2,1)S(1)}, bf16[224,128]{1,0:T(8,128)(2,1)S(1)}, u32[]{:S(2)}, u32[]{:S(2)}) collective-permute-start(bf16[224,128]{1,0:T(8,128)(2,1)S(1)} %get-tuple-element.77.refs_2_), channel_id=1, source_target_pairs={{0,4},{4,0},{8,12},{12,8},{1,5},{5,1},{9,13},{13,9},{2,6},{6,2},{1... | collective-permute-start | bytes 172040 | tf_op jit(solution)/shard_map/ppermute | solution.py:475
  61.5 1.2 %collective-permute-start.19 = (f32[4,128]{1,0:T(4,128)S(1)}, f32[4,128]{1,0:T(4,128)S(1)}, u32[]{:S(2)}, u32[]{:S(2)}) collective-permute-start(f32[4,128]{1,0:T(4,128)S(1)} %get-tuple-element.73.small_ref), channel_id=1, source_target_pairs={{0,1},{1,0},{2,3},{3,2},{4,5},{5,4},{6,7},{7,6},{8,9},{9,8},{10,11... | collective-permute-start | bytes 6152 | tf_op jit(solution)/shard_map/ppermute | solution.py:475

commit v12 on v10

--- a/solution.py
+++ b/solution.py
@@ -58,6 +58,10 @@
     cell = lax.broadcasted_iota(jnp.int32, field.shape, 0)
     edge = 0 if by > 0 else cells - 1
     return jnp.where(cell == edge, 0.0, rolled)
+
+
+def beside(row):
+    return jnp.concatenate([shift_cells(row, -1), row, shift_cells(row, 1)], axis=1).astype(BF16)
 
 
 def dot(left, right, dims=((1,), (0,))):
@@ -256,7 +260,7 @@
         dhid = shift_cells(q[:, :chans], -1) + q[:, chans : 2 * chans] + shift_cells(q[:, 2 * chans :], 1)
         dpre = jnp.where(hid_ref[d + 2].astype(F32) > 0.0, dhid, 0.0)
         d16 = dpre.astype(BF16)
-        own_ref[d] = d16[:, : chans // 2]
+        own_ref[d] = beside(d16[:, : chans // 2].astype(F32))
         other_ref[d] = d16[:, chans // 2 :]
         return jnp.sum(dpre, axis=0, keepdims=True)
 
@@ -304,10 +308,9 @@
     before = jnp.where(c == 0, near, far)
     after = jnp.where(c == 0, far, near)
 
-    for r in range(rows):
-        mine, theirs = own_ref[r % half].astype(F32), other_ref[r % half].astype(F32)
-        mid = jnp.where(c == (0 if r < half else 1), mine, theirs)
-        d_ref[r] = jnp.concatenate([shift_cells(mid, -1), mid, shift_cells(mid, 1)], axis=1).astype(BF16)
+    d_ref[pl.ds(half * c, half)] = own_ref[...]
+    for r in range(half):
+        d_ref[half * (1 - c) + r] = beside(other_ref[r].astype(F32))
     outs = d_ref.shape[2] // 3
 
     def part(x, first):
@@ -454,7 +457,8 @@
     for i in range(tiles - 1):
         pairs += [(2 * i + 1, 2 * i + 2), (2 * i + 2, 2 * i + 1)]
     halo = lax.ppermute(msg, ("tile", "chan"), pairs)
-    w1b = swap(w_shared, "chan")
+    later, _ = lax.optimization_barrier((w_shared, msg))
+    w1b = swap(later, "chan")
     w2b = swap(w_cls, "chan")
     b1b = swap(b_shared, "chan")
 
@@ -477,7 +481,7 @@
         back_kernel, "back", 4,
         [
             ((half, 3 * CLS_ROWS, cols), BF16),
-            ((half, cols, outs), BF16),
+            ((half, cols, 3 * outs), BF16),
             ((half, cols, outs), BF16),
             ((SMALL, LANES), F32),
         ],
@@ -485,7 +489,8 @@
         [((half + 2, cols, LANES), BF16)],
     )
     theirs = swap(other, "chan")
-    far = swap(halo, "chan")
+    later, _ = lax.optimization_barrier((halo, loss))
+    far = swap(later, "chan")
     cls_total = round_up(9 * LOGITS, 16 * pages * tiles)
     gcls, gcls_other = call(
         cls_kernel, "cls", 1.5, [((cls_total, outs), F32)] * 2, [where, hid, dt]

time: 66.8 us -> 67.5 us (1.010)
  transfers between devices with their start and end apart: 28 -> 28, of which waited for: 11 -> 11; matrix products, arithmetic and copies ran while one was open for 0% -> 0% of each run, Pallas kernels for 21% -> 19%
where the time goes in v12:
time: 67.5 us; the launch traced here: 67.2 us
  starting transfers between devices  33.6 us (50%)
  Pallas kernels  16.1 us (24%)
  waiting for transfers between devices  15.8 us (23%)
  local copies, waits for them, and re-layouts  0.96 us (1%)
  between operations  0.8 us (1%)
    ppermute x27, starting transfers between devices, swap(): return lax.ppermute(x, axis, [(i, i ^ bit) for i in range(size)])  32.9 us
    pallas_call x11, Pallas kernels, call(): pl.pallas_call(functools.partial(kernel, inputs[0]), in_specs=(specs or [...  16.1 us
    ppermute x27, waiting for transfers between devices, swap(): return lax.ppermute(x, axis, [(i, i ^ bit) for i in range(size)])  15.8 us
  transfers between devices with their start and end apart: 28, of which 11 were waited for; matrix products, arithmetic and copies ran while one was open for 0% of the time, Pallas kernels for 19%

profile of v12, /device:TPU:0, one launch (start us, length us, event | category | flops | bytes accessed | tf_op | source)
XLA Modules:
  0.0 67.2 jit_solution(9976764141948316819)
XLA Ops:
  0.6 0.9 %copy-done.3 = s32[1,12,2304]{2,0,1:T(1,128)S(1)} copy-done((s32[1,12,2304]{2,0,1:T(1,128)S(1)}, s32[1,12,2304]{2,0,1:T(1,128)}, u32[]{:S(2)}) %copy-start.3) | copy-done | bytes 110616
  1.5 2.0 %edge.1 = (bf16[784,256]{1,0:T(8,128)(2,1)S(1)}, bf16[12,16,256]{2,1,0:T(8,128)(2,1)S(1)}, f32[8,128]{1,0:T(8,128)S(1)}, bf16[9,256,256]{2,1,0:T(8,128)(2,1)S(1)}) custom-call(bf16[12,256,256]{2,1,0:T(8,128)(2,1)} %bitcast.12, s32[12,1,2304]{2,1,0:T(1,128)S(1)} %bitcast.16), custom_call_target="tpu_custom_call" | custom-call | flops 2000000000 | bytes 2000000 | tf_op jit(solution)/shard_map/edge/pallas_call | solution.py:43
  3.6 0.5 collective-permute-start.1
  4.1 0.7 %collective-permute-start = (bf16[784,256]{1,0:T(8,128)(2,1)S(1)}, bf16[784,256]{1,0:T(8,128)(2,1)S(1)}, u32[]{:S(2)}, u32[]{:S(2)}) collective-permute-start(bf16[784,256]{1,0:T(8,128)(2,1)S(1)} %get-tuple-element.47), channel_id=1, source_target_pairs={{1,4},{4,1},{5,8},{8,5},{9,12},{12,9},{3,6},{6,3},{7,10},{10,7},{1... | collective-permute-start | bytes 1204232 | tf_op jit(solution)/shard_map/ppermute | solution.py:459
  4.8 4.0 %collective-permute-start.2 = (f32[128]{0:T(128)S(1)}, f32[128]{0:T(128)S(1)}, u32[]{:S(2)}, u32[]{:S(2)}) collective-permute-start(f32[128]{0:T(128)S(1)} %copy-done.4), channel_id=1, source_target_pairs={{0,1},{1,0},{2,3},{3,2},{4,5},{5,4},{6,7},{7,6},{8,9},{9,8},{10,11... | collective-permute-start | bytes 1544 | tf_op jit(solution)/shard_map/ppermute | solution.py:415
  8.8 0.1 collective-permute-start.4
  8.9 1.5 %collective-permute-start.3 = (f32[8,128]{1,0:T(8,128)S(1)}, f32[8,128]{1,0:T(8,128)S(1)}, u32[]{:S(2)}, u32[]{:S(2)}) collective-permute-start(f32[8,128]{1,0:T(8,128)S(1)} %get-tuple-element.48), channel_id=1, source_target_pairs={{0,2},{2,0},{1,3},{3,1},{4,6},{6,4},{5,7},{7,5},{8,10},{10,8},{9,1... | collective-permute-start | bytes 12296 | tf_op jit(solution)/shard_map/ppermute | solution.py:415
  10.4 0.0 collective-permute-done.2
  10.4 0.0 collective-permute-done.1.w1b_ref
  10.4 2.4 %inner.1.inner_ref = bf16[7,256,256]{2,1,0:T(8,128)(2,1)S(1)} custom-call(bf16[9,256,256]{2,1,0:T(8,128)(2,1)S(1)} %get-tuple-element.49.near_ref, bf16[3,3,256,128]{3,2,1,0:T(8,128)(2,1)S(1)} %copy-done.1, bf16[3,3,256,128]{3,2,1,0:T(8,128)(2,1)S(1)} %collective-permute-done.1.w1b_ref, f32[1,128]{1,0:T(1,128)S(1)} %bitcast.17, f32[1,128]{1,0:T(1,128)S(1)} %bitcast.20), custom_call_target="tpu_custom_call" | custom-call | flops 3000000000 | bytes 3000000 | tf_op jit(solution)/shard_map/inner/pallas_call | solution.py:43
  12.8 0.0 collective-permute-done.3
  12.8 2.9 %collective-permute-start.8 = (f32[8,128]{1,0:T(8,128)S(1)}, f32[8,128]{1,0:T(8,128)S(1)}, u32[]{:S(2)}, u32[]{:S(2)}) collective-permute-start(f32[8,128]{1,0:T(8,128)S(1)} %add.3.rest_0_), channel_id=1, source_target_pairs={{0,12},{4,8},{8,4},{12,0},{1,13},{5,9},{9,5},{13,1},{2,14},{6,10},... | collective-permute-start | bytes 12296 | tf_op jit(solution)/shard_map/ppermute | solution.py:415
  15.7 0.2 collective-permute-start.7
  15.9 1.4 %collective-permute-start.6 = (f32[8,128]{1,0:T(8,128)S(1)}, f32[8,128]{1,0:T(8,128)S(1)}, u32[]{:S(2)}, u32[]{:S(2)}) collective-permute-start(f32[8,128]{1,0:T(8,128)S(1)} %add.3.rest_0_), channel_id=1, source_target_pairs={{0,4},{4,0},{8,12},{12,8},{1,5},{5,1},{9,13},{13,9},{2,6},{6,2},{1... | collective-permute-start | bytes 12296 | tf_op jit(solution)/shard_map/ppermute | solution.py:415
  17.2 0.0 collective-permute-done.halo_ref
  17.2 0.0 collective-permute-done.4
  17.2 4.1 %head.1 = (bf16[10,256,256]{2,1,0:T(8,128)(2,1)S(1)}, f32[8,256,128]{2,1,0:T(8,128)S(1)}, f32[1,128]{1,0:T(1,128)S(1)}, bf16[1152,256]{1,0:T(8,128)(2,1)S(1)}) custom-call(bf16[9,256,256]{2,1,0:T(8,128)(2,1)S(1)} %get-tuple-element.49.near_ref, bf16[7,256,256]{2,1,0:T(8,128)(2,1)S(1)} %inner.1.inner_ref, bf16[784,256]{1,0:T(8,128)(2,1)S(1)} %collective-permute-done.halo_ref, ...), custom_call_target="tpu_custom_call" | custom-call | flops 5000000000 | bytes 5000000 | tf_op jit(solution)/shard_map/head/pallas_call | solution.py:43
  21.3 0.1 collective-permute-start.5
  21.4 0.0 collective-permute-done.8.rest_3_
  21.4 0.0 collective-permute-done.7.rest_2_
  21.4 0.0 collective-permute-done.6.rest_1_
  21.4 1.9 %back.1 = (bf16[6,336,256]{2,1,0:T(8,128)(2,1)S(1)}, bf16[6,256,384]{2,1,0:T(8,128)(2,1)S(1)}, bf16[6,256,128]{2,1,0:T(8,128)(2,1)S(1)}, f32[4,128]{1,0:T(4,128)S(1)}) custom-call(bf16[10,256,256]{2,1,0:T(8,128)(2,1)S(1)} %get-tuple-element.57.hid_ref, f32[8,256,128]{2,1,0:T(8,128)S(1)} %get-tuple-element.58.dz_ref, ...), custom_call_target="tpu_custom_call" | custom-call | flops 4000000000 | bytes 4000000 | tf_op jit(solution)/shard_map/back/pallas_call | solution.py:43
  23.3 0.5 collective-permute-start.9
  23.8 1.0 %cls.1 = (f32[896,128]{1,0:T(8,128)S(1)}, f32[896,128]{1,0:T(8,128)S(1)}) custom-call(bf16[10,256,256]{2,1,0:T(8,128)(2,1)S(1)} %get-tuple-element.57.hid_ref, bf16[6,336,256]{2,1,0:T(8,128)(2,1)S(1)} %get-tuple-element.64.dt_ref), custom_call_target="tpu_custom_call" | custom-call | flops 1500000000 | bytes 1500000 | tf_op jit(solution)/shard_map/cls/pallas_call | solution.py:43
  24.8 0.1 collective-permute-start.10
  24.9 0.3 collective-permute-done.9.other_ref
  25.2 0.0 collective-permute-done.5.far_ref
  25.2 0.1 copy-done
  25.3 3.2 %shared.1 = (f32[1152,128]{1,0:T(8,128)S(1)}, bf16[1152,128]{1,0:T(8,128)(2,1)S(1)}) custom-call(bf16[12,256,256]{2,1,0:T(8,128)(2,1)S(1)} %bitcast.13, bf16[784,256]{1,0:T(8,128)(2,1)S(1)} %collective-permute-done.halo_ref, bf16[784,256]{1,0:T(8,128)(2,1)S(1)} %collective-permute-done.5.far_ref, bf16[6,256,384]{2,1,0:T(8,128)(2,1)S(1)} %get-tuple-element.60.own_ref, ...), custom_call_target="tpu_custom_call" | custom-call | flops 4000000000 | bytes 4000000 | tf_op jit(solution)/shard_map/shared/pallas_call | solution.py:43
  28.5 1.2 %collective-permute-start.11 = (bf16[1152,128]{1,0:T(8,128)(2,1)S(1)}, bf16[1152,128]{1,0:T(8,128)(2,1)S(1)}, u32[]{:S(2)}, u32[]{:S(2)}) collective-permute-start(bf16[1152,128]{1,0:T(8,128)(2,1)S(1)} %get-tuple-element.68), channel_id=1, source_target_pairs={{0,2},{2,0},{1,3},{3,1},{4,6},{6,4},{5,7},{7,5},{8,10},{10,8},{9,1... | collective-permute-start | bytes 884744 | tf_op jit(solution)/shard_map/ppermute | solution.py:415
  29.7 0.0 collective-permute-done.10.theirs_ref
  29.7 0.1 cls_split.1
  29.8 2.9 %collective-permute-start.12 = (bf16[240,128]{1,0:T(8,128)(2,1)S(1)}, bf16[240,128]{1,0:T(8,128)(2,1)S(1)}, u32[]{:S(2)}, u32[]{:S(2)}) collective-permute-start(bf16[240,128]{1,0:T(8,128)(2,1)S(1)} %get-tuple-element.69), channel_id=1, source_target_pairs={{0,12},{4,8},{8,4},{12,0},{1,13},{5,9},{9,5},{13,1},{2,14},{6,10},... | collective-permute-start | bytes 184328 | tf_op jit(solution)/shard_map/ppermute | solution.py:415
  32.7 0.0 collective-permute-start.13
  32.7 1.5 %collective-permute-start.14 = (bf16[240,128]{1,0:T(8,128)(2,1)S(1)}, bf16[240,128]{1,0:T(8,128)(2,1)S(1)}, u32[]{:S(2)}, u32[]{:S(2)}) collective-permute-start(bf16[240,128]{1,0:T(8,128)(2,1)S(1)} %get-tuple-element.71), channel_id=1, source_target_pairs={{0,4},{4,0},{8,12},{12,8},{1,5},{5,1},{9,13},{13,9},{2,6},{6,2},{1... | collective-permute-start | bytes 184328 | tf_op jit(solution)/shard_map/ppermute | solution.py:415
  34.2 2.1 %collective-permute-done.12.refs_1_ = bf16[240,128]{1,0:T(8,128)(2,1)S(1)} collective-permute-done((bf16[240,128]{1,0:T(8,128)(2,1)S(1)}, bf16[240,128]{1,0:T(8,128)(2,1)S(1)}, u32[]{:S(2)}, u32[]{:S(2)}) %collective-permute-start.12) | collective-permute-done | bytes 61472 | tf_op jit(solution)/shard_map/ppermute | solution.py:415
  36.3 2.0 %collective-permute-done.13.refs_2_ = bf16[240,128]{1,0:T(8,128)(2,1)S(1)} collective-permute-done((bf16[240,128]{1,0:T(8,128)(2,1)S(1)}, bf16[240,128]{1,0:T(8,128)(2,1)S(1)}, u32[]{:S(2)}, u32[]{:S(2)}) %collective-permute-start.13) | collective-permute-done | bytes 61472 | tf_op jit(solution)/shard_map/ppermute | solution.py:415
  38.3 0.1 collective-permute-done.14.refs_3_
  38.4 0.0 collective-permute-done.11.refs_0_
  38.4 0.1 sum.1
  38.5 2.6 %collective-permute-start.15 = (bf16[288,128]{1,0:T(8,128)(2,1)S(1)}, bf16[288,128]{1,0:T(8,128)(2,1)S(1)}, u32[]{:S(2)}, u32[]{:S(2)}) collective-permute-start(bf16[288,128]{1,0:T(8,128)(2,1)S(1)} %get-tuple-element.75), channel_id=1, source_target_pairs={{0,12},{4,8},{8,4},{12,0},{1,13},{5,9},{9,5},{13,1},{2,14},{6,10},... | collective-permute-start | bytes 221192 | tf_op jit(solution)/shard_map/ppermute | solution.py:415
  41.1 0.0 collective-permute-start.16
  41.1 1.9 %collective-permute-start.17 = (bf16[288,128]{1,0:T(8,128)(2,1)S(1)}, bf16[288,128]{1,0:T(8,128)(2,1)S(1)}, u32[]{:S(2)}, u32[]{:S(2)}) collective-permute-start(bf16[288,128]{1,0:T(8,128)(2,1)S(1)} %get-tuple-element.77), channel_id=1, source_target_pairs={{0,4},{4,0},{8,12},{12,8},{1,5},{5,1},{9,13},{13,9},{2,6},{6,2},{1... | collective-permute-start | bytes 221192 | tf_op jit(solution)/shard_map/ppermute | solution.py:415
  43.0 0.9 %collective-permute-start.18 = (bf16[128,128]{1,0:T(8,128)(2,1)S(1)}, bf16[128,128]{1,0:T(8,128)(2,1)S(1)}, u32[]{:S(2)}, u32[]{:S(2)}) collective-permute-start(bf16[128,128]{1,0:T(8,128)(2,1)S(1)} %get-tuple-element.78), channel_id=1, source_target_pairs={{0,2},{2,0},{1,3},{3,1},{4,6},{6,4},{5,7},{7,5},{8,10},{10,8},{9,1... | collective-permute-start | bytes 98312 | tf_op jit(solution)/shard_map/ppermute | solution.py:415
  43.8 3.0 %collective-permute-done.18.refs_3_ = bf16[128,128]{1,0:T(8,128)(2,1)S(1)} collective-permute-done((bf16[128,128]{1,0:T(8,128)(2,1)S(1)}, bf16[128,128]{1,0:T(8,128)(2,1)S(1)}, u32[]{:S(2)}, u32[]{:S(2)}) %collective-permute-start.18) | collective-permute-done | bytes 32800 | tf_op jit(solution)/shard_map/ppermute | solution.py:415
  46.9 0.0 collective-permute-done.15.refs_0_
  46.9 1.2 %collective-permute-done.16.refs_1_ = bf16[288,128]{1,0:T(8,128)(2,1)S(1)} collective-permute-done((bf16[288,128]{1,0:T(8,128)(2,1)S(1)}, bf16[288,128]{1,0:T(8,128)(2,1)S(1)}, u32[]{:S(2)}, u32[]{:S(2)}) %collective-permute-start.16) | collective-permute-done | bytes 73760 | tf_op jit(solution)/shard_map/ppermute | solution.py:415
  48.1 0.0 collective-permute-done.17.refs_2_
  48.2 2.0 %collective-permute-start.22 = (bf16[288,128]{1,0:T(8,128)(2,1)S(1)}, bf16[288,128]{1,0:T(8,128)(2,1)S(1)}, u32[]{:S(2)}, u32[]{:S(2)}) collective-permute-start(bf16[288,128]{1,0:T(8,128)(2,1)S(1)} %get-tuple-element.80.refs_0_), channel_id=1, source_target_pairs={{0,12},{4,8},{8,4},{12,0},{1,13},{5,9},{9,5},{13,1},{2,14},{6,10},... | collective-permute-start | bytes 221192 | tf_op jit(solution)/shard_map/ppermute | solution.py:415
  50.2 0.0 collective-permute-start.21
  50.2 2.4 %collective-permute-start.20 = (bf16[288,128]{1,0:T(8,128)(2,1)S(1)}, bf16[288,128]{1,0:T(8,128)(2,1)S(1)}, u32[]{:S(2)}, u32[]{:S(2)}) collective-permute-start(bf16[288,128]{1,0:T(8,128)(2,1)S(1)} %get-tuple-element.80.refs_0_), channel_id=1, source_target_pairs={{0,4},{4,0},{8,12},{12,8},{1,5},{5,1},{9,13},{13,9},{2,6},{6,2},{1... | collective-permute-start | bytes 221192 | tf_op jit(solution)/shard_map/ppermute | solution.py:415
  52.6 0.9 %collective-permute-start.23 = (bf16[112,128]{1,0:T(8,128)(2,1)S(1)}, bf16[112,128]{1,0:T(8,128)(2,1)S(1)}, u32[]{:S(2)}, u32[]{:S(2)}) collective-permute-start(bf16[112,128]{1,0:T(8,128)(2,1)S(1)} %get-tuple-element.81.refs_4_), channel_id=1, source_target_pairs={{0,2},{2,0},{1,3},{3,1},{4,6},{6,4},{5,7},{7,5},{8,10},{10,8},{9,1... | collective-permute-start | bytes 86024 | tf_op jit(solution)/shard_map/ppermute | solution.py:415
  53.5 3.0 %collective-permute-done.23.refs_5_ = bf16[112,128]{1,0:T(8,128)(2,1)S(1)} collective-permute-done((bf16[112,128]{1,0:T(8,128)(2,1)S(1)}, bf16[112,128]{1,0:T(8,128)(2,1)S(1)}, u32[]{:S(2)}, u32[]{:S(2)}) %collective-permute-start.23) | collective-permute-done | bytes 28704 | tf_op jit(solution)/shard_map/ppermute | solution.py:415
  56.5 0.0 collective-permute-done.22.refs_3_
  56.5 0.4 collective-permute-done.21.refs_2_
  56.9 0.0 collective-permute-done.20.refs_1_
  57.0 1.0 %collective-permute-start.24 = (bf16[1152,128]{1,0:T(8,128)(2,1)S(1)}, bf16[1152,128]{1,0:T(8,128)(2,1)S(1)}, u32[]{:S(2)}, u32[]{:S(2)}) collective-permute-start(bf16[1152,128]{1,0:T(8,128)(2,1)S(1)} %get-tuple-element.82.refs_0_), channel_id=1, source_target_pairs={{0,2},{2,0},{1,3},{3,1},{4,6},{6,4},{5,7},{7,5},{8,10},{10,8},{9,1... | collective-permute-start | bytes 884744 | tf_op jit(solution)/shard_map/ppermute | solution.py:415
  57.9 2.5 %collective-permute-start.27 = (bf16[224,128]{1,0:T(8,128)(2,1)S(1)}, bf16[224,128]{1,0:T(8,128)(2,1)S(1)}, u32[]{:S(2)}, u32[]{:S(2)}) collective-permute-start(bf16[224,128]{1,0:T(8,128)(2,1)S(1)} %get-tuple-element.83.refs_2_), channel_id=1, source_target_pairs={{0,12},{4,8},{8,4},{12,0},{1,13},{5,9},{9,5},{13,1},{2,14},{6,10},... | collective-permute-start | bytes 172040 | tf_op jit(solution)/shard_map/ppermute | solution.py:415
  60.4 1.9 %collective-permute-start.25 = (bf16[224,128]{1,0:T(8,128)(2,1)S(1)}, bf16[224,128]{1,0:T(8,128)(2,1)S(1)}, u32[]{:S(2)}, u32[]{:S(2)}) collective-permute-start(bf16[224,128]{1,0:T(8,128)(2,1)S(1)} %get-tuple-element.83.refs_2_), channel_id=1, source_target_pairs={{0,4},{4,0},{8,12},{12,8},{1,5},{5,1},{9,13},{13,9},{2,6},{6,2},{1... | collective-permute-start | bytes 172040 | tf_op jit(solution)/shard_map/ppermute | solution.py:415
  62.3 1.2 %collective-permute-done.19.theirs_ref = f32[4,128]{1,0:T(4,128)S(1)} collective-permute-done((f32[4,128]{1,0:T(4,128)S(1)}, f32[4,128]{1,0:T(4,128)S(1)}, u32[]{:S(2)}, u32[]{:S(2)}) %collective-permute-start.19) | collective-permute-done | bytes 2080 | tf_op jit(solution)/shard_map/ppermute | solution.py:415
  63.5 0.5 collective-permute-done.27.refs_5_
  64.0 1.9 %collective-permute-done.26.refs_4_ = bf16[224,128]{1,0:T(8,128)(2,1)S(1)} collective-permute-done((bf16[224,128]{1,0:T(8,128)(2,1)S(1)}, bf16[224,128]{1,0:T(8,128)(2,1)S(1)}, u32[]{:S(2)}, u32[]{:S(2)}) %collective-permute-start.26) | collective-permute-done | bytes 57376 | tf_op jit(solution)/shard_map/ppermute | solution.py:415
  65.9 0.0 collective-permute-done.24.refs_1_
  66.0 1.3 %out.1 = (f32[2304,128]{1,0:T(8,128)}, f32[1,128]{1,0:T(1,128)}, f32[3,3,99,128]{3,2,1,0:T(8,128)}, f32[1,99]{1,0:T(1,128)}, f32[1,1]{1,0:T(1,128)}) custom-call(f32[4,128]{1,0:T(4,128)S(1)} %get-tuple-element.79.small_ref, f32[4,128]{1,0:T(4,128)S(1)} %collective-permute-done.19.theirs_ref, bf16[1152,128]{1,0:T(8,128)(2,1)S(1)} %get-tuple-element.82.refs_0_, ...), custom_call_target="tpu_custom_call" | custom-call | flops 1500000000 | bytes 1500000 | tf_op jit(solution)/shard_map/out/pallas_call | solution.py:43
  (16 shorter events, 0.1 us)
Async XLA Ops:
  0.6 0.9 %copy-start.3 = (s32[1,12,2304]{2,0,1:T(1,128)S(1)}, s32[1,12,2304]{2,0,1:T(1,128)}, u32[]{:S(2)}) copy-start(s32[1,12,2304]{2,0,1:T(1,128)} %param.7) | copy-start | bytes 331780
  1.5 2.0 %copy-start.1 = (bf16[3,3,256,128]{3,2,1,0:T(8,128)(2,1)S(1)}, bf16[3,3,256,128]{3,2,1,0:T(8,128)(2,1)}, u32[]{:S(2)}) copy-start(bf16[3,3,256,128]{3,2,1,0:T(8,128)(2,1)} %w1a_ref.3) | copy-start | bytes 1769476
  1.5 3.2 %copy-start.4 = (f32[128]{0:T(128)S(1)}, f32[128]{0:T(128)}, u32[]{:S(2)}) copy-start(f32[128]{0:T(128)} %param.9) | copy-start | bytes 1540
  1.5 7.3 %copy-start.2 = (bf16[3,3,128,99]{2,3,1,0:T(8,128)(2,1)S(1)}, bf16[3,3,128,99]{2,3,1,0:T(8,128)(2,1)}, u32[]{:S(2)}) copy-start(bf16[3,3,128,99]{2,3,1,0:T(8,128)(2,1)} %param.10) | copy-start | bytes 684292
  3.6 6.8 %collective-permute-start.1 = (bf16[3,3,256,128]{3,2,1,0:T(8,128)(2,1)S(1)}, bf16[3,3,256,128]{3,2,1,0:T(8,128)(2,1)S(1)}, u32[]{:S(2)}, u32[]{:S(2)}) collective-permute-start(bf16[3,3,256,128]{3,2,1,0:T(8,128)(2,1)S(1)} %copy-done.1), channel_id=1, source_target_pairs={{0,1},{1,0},{2,3},{3,2},{4,5},{5,4},{6,7},{7,6},{8,9},{9,8},{10,11... | collective-permute-start | bytes 1769480 | tf_op jit(solution)/shard_map/ppermute | solution.py:415
  4.1 13.1 %collective-permute-start = (bf16[784,256]{1,0:T(8,128)(2,1)S(1)}, bf16[784,256]{1,0:T(8,128)(2,1)S(1)}, u32[]{:S(2)}, u32[]{:S(2)}) collective-permute-start(bf16[784,256]{1,0:T(8,128)(2,1)S(1)} %get-tuple-element.47), channel_id=1, source_target_pairs={{1,4},{4,1},{5,8},{8,5},{9,12},{12,9},{3,6},{6,3},{7,10},{10,7},{1... | collective-permute-start | bytes 1204232 | tf_op jit(solution)/shard_map/ppermute | solution.py:459
  4.8 5.6 %collective-permute-start.2 = (f32[128]{0:T(128)S(1)}, f32[128]{0:T(128)S(1)}, u32[]{:S(2)}, u32[]{:S(2)}) collective-permute-start(f32[128]{0:T(128)S(1)} %copy-done.4), channel_id=1, source_target_pairs={{0,1},{1,0},{2,3},{3,2},{4,5},{5,4},{6,7},{7,6},{8,9},{9,8},{10,11... | collective-permute-start | bytes 1544 | tf_op jit(solution)/shard_map/ppermute | solution.py:415
  8.8 8.5 %collective-permute-start.4 = (bf16[3,3,128,99]{2,3,1,0:T(8,128)(2,1)S(1)}, bf16[3,3,128,99]{2,3,1,0:T(8,128)(2,1)S(1)}, u32[]{:S(2)}, u32[]{:S(2)}) collective-permute-start(bf16[3,3,128,99]{2,3,1,0:T(8,128)(2,1)S(1)} %copy-done.2), channel_id=1, source_target_pairs={{0,1},{1,0},{2,3},{3,2},{4,5},{5,4},{6,7},{7,6},{8,9},{9,8},{10,11... | collective-permute-start | bytes 684296 | tf_op jit(solution)/shard_map/ppermute | solution.py:415
  8.9 3.9 %collective-permute-start.3 = (f32[8,128]{1,0:T(8,128)S(1)}, f32[8,128]{1,0:T(8,128)S(1)}, u32[]{:S(2)}, u32[]{:S(2)}) collective-permute-start(f32[8,128]{1,0:T(8,128)S(1)} %get-tuple-element.48), channel_id=1, source_target_pairs={{0,2},{2,0},{1,3},{3,1},{4,6},{6,4},{5,7},{7,5},{8,10},{10,8},{9,1... | collective-permute-start | bytes 12296 | tf_op jit(solution)/shard_map/ppermute | solution.py:415
  10.4 6.9 %copy-start.5 = (f32[99]{0:T(128)S(1)}, f32[99]{0:T(128)}, u32[]{:S(2)}) copy-start(f32[99]{0:T(128)} %param.11) | copy-start | bytes 1192
  12.8 8.6 %collective-permute-start.8 = (f32[8,128]{1,0:T(8,128)S(1)}, f32[8,128]{1,0:T(8,128)S(1)}, u32[]{:S(2)}, u32[]{:S(2)}) collective-permute-start(f32[8,128]{1,0:T(8,128)S(1)} %add.3.rest_0_), channel_id=1, source_target_pairs={{0,12},{4,8},{8,4},{12,0},{1,13},{5,9},{9,5},{13,1},{2,14},{6,10},... | collective-permute-start | bytes 12296 | tf_op jit(solution)/shard_map/ppermute | solution.py:415
  15.7 5.7 %collective-permute-start.7 = (f32[8,128]{1,0:T(8,128)S(1)}, f32[8,128]{1,0:T(8,128)S(1)}, u32[]{:S(2)}, u32[]{:S(2)}) collective-permute-start(f32[8,128]{1,0:T(8,128)S(1)} %add.3.rest_0_), channel_id=1, source_target_pairs={{0,8},{4,12},{8,0},{12,4},{1,9},{5,13},{9,1},{13,5},{2,10},{6,14},... | collective-permute-start | bytes 12296 | tf_op jit(solution)/shard_map/ppermute | solution.py:415
  15.9 5.6 %collective-permute-start.6 = (f32[8,128]{1,0:T(8,128)S(1)}, f32[8,128]{1,0:T(8,128)S(1)}, u32[]{:S(2)}, u32[]{:S(2)}) collective-permute-start(f32[8,128]{1,0:T(8,128)S(1)} %add.3.rest_0_), channel_id=1, source_target_pairs={{0,4},{4,0},{8,12},{12,8},{1,5},{5,1},{9,13},{13,9},{2,6},{6,2},{1... | collective-permute-start | bytes 12296 | tf_op jit(solution)/shard_map/ppermute | solution.py:415
  21.3 3.9 %collective-permute-start.5 = (bf16[784,256]{1,0:T(8,128)(2,1)S(1)}, bf16[784,256]{1,0:T(8,128)(2,1)S(1)}, u32[]{:S(2)}, u32[]{:S(2)}) collective-permute-start(bf16[784,256]{1,0:T(8,128)(2,1)S(1)} %collective-permute-done.halo_ref), channel_id=1, source_target_pairs={{0,1},{1,0},{2,3},{3,2},{4,5},{5,4},{6,7},{7,6},{8,9},{9,8},{10,11... | collective-permute-start | bytes 1204232 | tf_op jit(solution)/shard_map/ppermute | solution.py:415
  23.3 1.9 %collective-permute-start.9 = (bf16[6,256,128]{2,1,0:T(8,128)(2,1)S(1)}, bf16[6,256,128]{2,1,0:T(8,128)(2,1)S(1)}, u32[]{:S(2)}, u32[]{:S(2)}) collective-permute-start(bf16[6,256,128]{2,1,0:T(8,128)(2,1)S(1)} %get-tuple-element.61), channel_id=1, source_target_pairs={{0,1},{1,0},{2,3},{3,2},{4,5},{5,4},{6,7},{7,6},{8,9},{9,8},{10,11... | collective-permute-start | bytes 1179656 | tf_op jit(solution)/shard_map/ppermute | solution.py:415
  23.8 1.4 %copy-start = (bf16[1,12,256,256]{3,2,1,0:T(8,128)(2,1)S(1)}, bf16[1,12,256,256]{3,2,1,0:T(8,128)(2,1)}, u32[]{:S(2)}) copy-start(bf16[1,12,256,256]{3,2,1,0:T(8,128)(2,1)} %param.6) | copy-start | bytes 4718596
  24.8 4.9 %collective-permute-start.10 = (f32[896,128]{1,0:T(8,128)S(1)}, f32[896,128]{1,0:T(8,128)S(1)}, u32[]{:S(2)}, u32[]{:S(2)}) collective-permute-start(f32[896,128]{1,0:T(8,128)S(1)} %get-tuple-element.66), channel_id=1, source_target_pairs={{0,1},{1,0},{2,3},{3,2},{4,5},{5,4},{6,7},{7,6},{8,9},{9,8},{10,11... | collective-permute-start | bytes 1376264 | tf_op jit(solution)/shard_map/ppermute | solution.py:415
  28.5 9.9 %collective-permute-start.11 = (bf16[1152,128]{1,0:T(8,128)(2,1)S(1)}, bf16[1152,128]{1,0:T(8,128)(2,1)S(1)}, u32[]{:S(2)}, u32[]{:S(2)}) collective-permute-start(bf16[1152,128]{1,0:T(8,128)(2,1)S(1)} %get-tuple-element.68), channel_id=1, source_target_pairs={{0,2},{2,0},{1,3},{3,1},{4,6},{6,4},{5,7},{7,5},{8,10},{10,8},{9,1... | collective-permute-start | bytes 884744 | tf_op jit(solution)/shard_map/ppermute | solution.py:415
  29.8 6.5 %collective-permute-start.12 = (bf16[240,128]{1,0:T(8,128)(2,1)S(1)}, bf16[240,128]{1,0:T(8,128)(2,1)S(1)}, u32[]{:S(2)}, u32[]{:S(2)}) collective-permute-start(bf16[240,128]{1,0:T(8,128)(2,1)S(1)} %get-tuple-element.69), channel_id=1, source_target_pairs={{0,12},{4,8},{8,4},{12,0},{1,13},{5,9},{9,5},{13,1},{2,14},{6,10},... | collective-permute-start | bytes 184328 | tf_op jit(solution)/shard_map/ppermute | solution.py:415
  32.7 5.6 %collective-permute-start.13 = (bf16[240,128]{1,0:T(8,128)(2,1)S(1)}, bf16[240,128]{1,0:T(8,128)(2,1)S(1)}, u32[]{:S(2)}, u32[]{:S(2)}) collective-permute-start(bf16[240,128]{1,0:T(8,128)(2,1)S(1)} %get-tuple-element.70), channel_id=1, source_target_pairs={{0,8},{4,12},{8,0},{12,4},{1,9},{5,13},{9,1},{13,5},{2,10},{6,14},... | collective-permute-start | bytes 184328 | tf_op jit(solution)/shard_map/ppermute | solution.py:415
  32.7 5.6 %collective-permute-start.14 = (bf16[240,128]{1,0:T(8,128)(2,1)S(1)}, bf16[240,128]{1,0:T(8,128)(2,1)S(1)}, u32[]{:S(2)}, u32[]{:S(2)}) collective-permute-start(bf16[240,128]{1,0:T(8,128)(2,1)S(1)} %get-tuple-element.71), channel_id=1, source_target_pairs={{0,4},{4,0},{8,12},{12,8},{1,5},{5,1},{9,13},{13,9},{2,6},{6,2},{1... | collective-permute-start | bytes 184328 | tf_op jit(solution)/shard_map/ppermute | solution.py:415
  38.5 8.4 %collective-permute-start.15 = (bf16[288,128]{1,0:T(8,128)(2,1)S(1)}, bf16[288,128]{1,0:T(8,128)(2,1)S(1)}, u32[]{:S(2)}, u32[]{:S(2)}) collective-permute-start(bf16[288,128]{1,0:T(8,128)(2,1)S(1)} %get-tuple-element.75), channel_id=1, source_target_pairs={{0,12},{4,8},{8,4},{12,0},{1,13},{5,9},{9,5},{13,1},{2,14},{6,10},... | collective-permute-start | bytes 221192 | tf_op jit(solution)/shard_map/ppermute | solution.py:415
  41.1 7.0 %collective-permute-start.16 = (bf16[288,128]{1,0:T(8,128)(2,1)S(1)}, bf16[288,128]{1,0:T(8,128)(2,1)S(1)}, u32[]{:S(2)}, u32[]{:S(2)}) collective-permute-start(bf16[288,128]{1,0:T(8,128)(2,1)S(1)} %get-tuple-element.76), channel_id=1, source_target_pairs={{0,8},{4,12},{8,0},{12,4},{1,9},{5,13},{9,1},{13,5},{2,10},{6,14},... | collective-permute-start | bytes 221192 | tf_op jit(solution)/shard_map/ppermute | solution.py:415
  41.1 7.0 %collective-permute-start.17 = (bf16[288,128]{1,0:T(8,128)(2,1)S(1)}, bf16[288,128]{1,0:T(8,128)(2,1)S(1)}, u32[]{:S(2)}, u32[]{:S(2)}) collective-permute-start(bf16[288,128]{1,0:T(8,128)(2,1)S(1)} %get-tuple-element.77), channel_id=1, source_target_pairs={{0,4},{4,0},{8,12},{12,8},{1,5},{5,1},{9,13},{13,9},{2,6},{6,2},{1... | collective-permute-start | bytes 221192 | tf_op jit(solution)/shard_map/ppermute | solution.py:415
  43.0 3.9 %collective-permute-start.18 = (bf16[128,128]{1,0:T(8,128)(2,1)S(1)}, bf16[128,128]{1,0:T(8,128)(2,1)S(1)}, u32[]{:S(2)}, u32[]{:S(2)}) collective-permute-start(bf16[128,128]{1,0:T(8,128)(2,1)S(1)} %get-tuple-element.78), channel_id=1, source_target_pairs={{0,2},{2,0},{1,3},{3,1},{4,6},{6,4},{5,7},{7,5},{8,10},{10,8},{9,1... | collective-permute-start | bytes 98312 | tf_op jit(solution)/shard_map/ppermute | solution.py:415
  48.2 8.3 %collective-permute-start.22 = (bf16[288,128]{1,0:T(8,128)(2,1)S(1)}, bf16[288,128]{1,0:T(8,128)(2,1)S(1)}, u32[]{:S(2)}, u32[]{:S(2)}) collective-permute-start(bf16[288,128]{1,0:T(8,128)(2,1)S(1)} %get-tuple-element.80.refs_0_), channel_id=1, source_target_pairs={{0,12},{4,8},{8,4},{12,0},{1,13},{5,9},{9,5},{13,1},{2,14},{6,10},... | collective-permute-start | bytes 221192 | tf_op jit(solution)/shard_map/ppermute | solution.py:415
  50.2 6.7 %collective-permute-start.21 = (bf16[288,128]{1,0:T(8,128)(2,1)S(1)}, bf16[288,128]{1,0:T(8,128)(2,1)S(1)}, u32[]{:S(2)}, u32[]{:S(2)}) collective-permute-start(bf16[288,128]{1,0:T(8,128)(2,1)S(1)} %get-tuple-element.80.refs_0_), channel_id=1, source_target_pairs={{0,8},{4,12},{8,0},{12,4},{1,9},{5,13},{9,1},{13,5},{2,10},{6,14},... | collective-permute-start | bytes 221192 | tf_op jit(solution)/shard_map/ppermute | solution.py:415
  50.2 6.7 %collective-permute-start.20 = (bf16[288,128]{1,0:T(8,128)(2,1)S(1)}, bf16[288,128]{1,0:T(8,128)(2,1)S(1)}, u32[]{:S(2)}, u32[]{:S(2)}) collective-permute-start(bf16[288,128]{1,0:T(8,128)(2,1)S(1)} %get-tuple-element.80.refs_0_), channel_id=1, source_target_pairs={{0,4},{4,0},{8,12},{12,8},{1,5},{5,1},{9,13},{13,9},{2,6},{6,2},{1... | collective-permute-start | bytes 221192 | tf_op jit(solution)/shard_map/ppermute | solution.py:415
  52.6 3.9 %collective-permute-start.23 = (bf16[112,128]{1,0:T(8,128)(2,1)S(1)}, bf16[112,128]{1,0:T(8,128)(2,1)S(1)}, u32[]{:S(2)}, u32[]{:S(2)}) collective-permute-start(bf16[112,128]{1,0:T(8,128)(2,1)S(1)} %get-tuple-element.81.refs_4_), channel_id=1, source_target_pairs={{0,2},{2,0},{1,3},{3,1},{4,6},{6,4},{5,7},{7,5},{8,10},{10,8},{9,1... | collective-permute-start | bytes 86024 | tf_op jit(solution)/shard_map/ppermute | solution.py:415
  57.0 9.0 %collective-permute-start.24 = (bf16[1152,128]{1,0:T(8,128)(2,1)S(1)}, bf16[1152,128]{1,0:T(8,128)(2,1)S(1)}, u32[]{:S(2)}, u32[]{:S(2)}) collective-permute-start(bf16[1152,128]{1,0:T(8,128)(2,1)S(1)} %get-tuple-element.82.refs_0_), channel_id=1, source_target_pairs={{0,2},{2,0},{1,3},{3,1},{4,6},{6,4},{5,7},{7,5},{8,10},{10,8},{9,1... | collective-permute-start | bytes 884744 | tf_op jit(solution)/shard_map/ppermute | solution.py:415
  57.9 6.1 %collective-permute-start.27 = (bf16[224,128]{1,0:T(8,128)(2,1)S(1)}, bf16[224,128]{1,0:T(8,128)(2,1)S(1)}, u32[]{:S(2)}, u32[]{:S(2)}) collective-permute-start(bf16[224,128]{1,0:T(8,128)(2,1)S(1)} %get-tuple-element.83.refs_2_), channel_id=1, source_target_pairs={{0,12},{4,8},{8,4},{12,0},{1,13},{5,9},{9,5},{13,1},{2,14},{6,10},... | collective-permute-start | bytes 172040 | tf_op jit(solution)/shard_map/ppermute | solution.py:415
  60.4 5.5 %collective-permute-start.26 = (bf16[224,128]{1,0:T(8,128)(2,1)S(1)}, bf16[224,128]{1,0:T(8,128)(2,1)S(1)}, u32[]{:S(2)}, u32[]{:S(2)}) collective-permute-start(bf16[224,128]{1,0:T(8,128)(2,1)S(1)} %get-tuple-element.83.refs_2_), channel_id=1, source_target_pairs={{0,8},{4,12},{8,0},{12,4},{1,9},{5,13},{9,1},{13,5},{2,10},{6,14},... | collective-permute-start | bytes 172040 | tf_op jit(solution)/shard_map/ppermute | solution.py:415
  60.4 5.5 %collective-permute-start.25 = (bf16[224,128]{1,0:T(8,128)(2,1)S(1)}, bf16[224,128]{1,0:T(8,128)(2,1)S(1)}, u32[]{:S(2)}, u32[]{:S(2)}) collective-permute-start(bf16[224,128]{1,0:T(8,128)(2,1)S(1)} %get-tuple-element.83.refs_2_), channel_id=1, source_target_pairs={{0,4},{4,0},{8,12},{12,8},{1,5},{5,1},{9,13},{13,9},{2,6},{6,2},{1... | collective-permute-start | bytes 172040 | tf_op jit(solution)/shard_map/ppermute | solution.py:415
  62.3 1.2 %collective-permute-start.19 = (f32[4,128]{1,0:T(4,128)S(1)}, f32[4,128]{1,0:T(4,128)S(1)}, u32[]{:S(2)}, u32[]{:S(2)}) collective-permute-start(f32[4,128]{1,0:T(4,128)S(1)} %get-tuple-element.79.small_ref), channel_id=1, source_target_pairs={{0,1},{1,0},{2,3},{3,2},{4,5},{5,4},{6,7},{7,6},{8,9},{9,8},{10,11... | collective-permute-start | bytes 6152 | tf_op jit(solution)/shard_map/ppermute | solution.py:415

commit v13 on v10

--- a/solution.py
+++ b/solution.py
@@ -215,7 +215,7 @@
     loss_ref[...] = lax.fori_loop(0, (half + 2) // BLOCK, focal, jnp.zeros((1, LANES), F32), unroll=True)
 
 
-def back_kernel(where_ref, hid_ref, dz_ref, loss_ref, w2_ref, *rest):
+def back_kernel(where_ref, hid_ref, dz_ref, loss_ref, w2_ref, halo_ref, *rest):
     *count_refs, dt_ref, own_ref, other_ref, small_ref, dlog_ref = rest
     half, _, cols = dt_ref.shape
     chans = hid_ref.shape[2]
@@ -261,6 +261,9 @@
         return jnp.sum(dpre, axis=0, keepdims=True)
 
     gsb = lax.fori_loop(0, half // BLOCK, dpre, jnp.zeros((1, chans), F32), unroll=True)
+    near = halo_ref[pl.ds(pl.multiple_of(2 * cols * (1 - where_ref[0]), 16), cols)]
+    other_ref[half] = near[:, : chans // 2]
+    other_ref[half + 1] = near[:, chans // 2 :]
     loss = jnp.sum(loss_ref[...], axis=1, keepdims=True) * inverse[:, :1]
     small_ref[0:1] = jnp.where(lax.broadcasted_iota(jnp.int32, (1, LANES), 1) < LOGITS, gcb, loss)
     small_ref[1:2] = jnp.zeros((1, LANES), F32)
@@ -293,14 +296,14 @@
 
 
 def shared_kernel(
-    where_ref, f_ref, halo_ref, far_ref, own_ref, other_ref, keep_ref, *rest
+    where_ref, f_ref, halo_ref, own_ref, other_ref, keep_ref, *rest
 ):
     *send_refs, d_ref, g_ref = rest
     rows, cols, chans = f_ref.shape
     half = rows // 2
     c = where_ref[0]
     near = halo_ref[pl.ds(pl.multiple_of(2 * cols * (1 - c), 16), cols)]
-    far = far_ref[pl.ds(pl.multiple_of(2 * cols * c, 16), cols)]
+    far = jnp.concatenate([other_ref[half], other_ref[half + 1]], axis=1)
     before = jnp.where(c == 0, near, far)
     after = jnp.where(c == 0, far, near)
 
@@ -478,14 +481,13 @@
         [
             ((half, 3 * CLS_ROWS, cols), BF16),
             ((half, cols, outs), BF16),
-            ((half, cols, outs), BF16),
+            ((half + 2, cols, outs), BF16),
             ((SMALL, LANES), F32),
         ],
-        [where, hid, dz, loss, w2] + counts,
+        [where, hid, dz, loss, w2, halo] + counts,
         [((half + 2, cols, LANES), BF16)],
     )
     theirs = swap(other, "chan")
-    far = swap(halo, "chan")
     cls_total = round_up(9 * LOGITS, 16 * pages * tiles)
     gcls, gcls_other = call(
         cls_kernel, "cls", 1.5, [((cls_total, outs), F32)] * 2, [where, hid, dt]
@@ -498,7 +500,7 @@
     keep, *sends = call(
         shared_kernel, "shared", 4,
         [((first, outs), F32)] + [((first, outs), BF16)] * (pages - 1),
-        [where, f, halo, far, own, theirs],
+        [where, f, halo, own, theirs],
         [((rows, cols, 3 * outs), BF16), ((total, outs), F32)],
     )
     ckeep, *csends = call(

time: 66.8 us -> 66.7 us (level)
    ppermute x27 -> x26, waiting for transfers between devices: 15.7 us -> 15.6 us  [swap(): return lax.ppermute(x, axis, [(i, i ^ bit) for i in range(size)])]
    ppermute x27 -> x26, starting transfers between devices: 32.9 us -> 32.8 us  [swap(): return lax.ppermute(x, axis, [(i, i ^ bit) for i in range(size)])]
  transfers between devices with their start and end apart: 28 -> 27, of which waited for: 11 -> 11; matrix products, arithmetic and copies ran while one was open for 0% -> 0% of each run, Pallas kernels for 21% -> 19%
where the time goes in v13:
time: 66.7 us; the launch traced here: 66.5 us
  starting transfers between devices  33.5 us (50%)
  Pallas kernels  15.7 us (24%)
  waiting for transfers between devices  15.6 us (23%)
  local copies, waits for them, and re-layouts  0.92 us (1%)
  between operations  0.8 us (1%)
    ppermute x26, starting transfers between devices, swap(): return lax.ppermute(x, axis, [(i, i ^ bit) for i in range(size)])  32.8 us
    pallas_call x11, Pallas kernels, call(): pl.pallas_call(functools.partial(kernel, inputs[0]), in_specs=(specs or [...  15.7 us
    ppermute x26, waiting for transfers between devices, swap(): return lax.ppermute(x, axis, [(i, i ^ bit) for i in range(size)])  15.6 us
  transfers between devices with their start and end apart: 27, of which 11 were waited for; matrix products, arithmetic and copies ran while one was open for 0% of the time, Pallas kernels for 19%

profile of v13, /device:TPU:0, one launch (start us, length us, event | category | flops | bytes accessed | tf_op | source)
XLA Modules:
  0.0 66.5 jit_solution(16381891167066558685)
XLA Ops:
  0.6 0.5 collective-permute-start.1
  1.2 0.9 %copy-done.3 = s32[1,12,2304]{2,0,1:T(1,128)S(1)} copy-done((s32[1,12,2304]{2,0,1:T(1,128)S(1)}, s32[1,12,2304]{2,0,1:T(1,128)}, u32[]{:S(2)}) %copy-start.3) | copy-done | bytes 110616
  2.1 2.0 %edge.1 = (bf16[784,256]{1,0:T(8,128)(2,1)S(1)}, bf16[12,16,256]{2,1,0:T(8,128)(2,1)S(1)}, f32[8,128]{1,0:T(8,128)S(1)}, bf16[9,256,256]{2,1,0:T(8,128)(2,1)S(1)}) custom-call(bf16[12,256,256]{2,1,0:T(8,128)(2,1)} %bitcast.12, s32[12,1,2304]{2,1,0:T(1,128)S(1)} %bitcast.16), custom_call_target="tpu_custom_call" | custom-call | flops 2000000000 | bytes 2000000 | tf_op jit(solution)/shard_map/edge/pallas_call | solution.py:43
  4.1 0.7 %collective-permute-start = (bf16[784,256]{1,0:T(8,128)(2,1)S(1)}, bf16[784,256]{1,0:T(8,128)(2,1)S(1)}, u32[]{:S(2)}, u32[]{:S(2)}) collective-permute-start(bf16[784,256]{1,0:T(8,128)(2,1)S(1)} %get-tuple-element.45), channel_id=1, source_target_pairs={{1,4},{4,1},{5,8},{8,5},{9,12},{12,9},{3,6},{6,3},{7,10},{10,7},{1... | collective-permute-start | bytes 1204232 | tf_op jit(solution)/shard_map/ppermute | solution.py:459
  4.8 4.0 %collective-permute-start.2 = (f32[128]{0:T(128)S(1)}, f32[128]{0:T(128)S(1)}, u32[]{:S(2)}, u32[]{:S(2)}) collective-permute-start(f32[128]{0:T(128)S(1)} %copy-done.4), channel_id=1, source_target_pairs={{0,1},{1,0},{2,3},{3,2},{4,5},{5,4},{6,7},{7,6},{8,9},{9,8},{10,11... | collective-permute-start | bytes 1544 | tf_op jit(solution)/shard_map/ppermute | solution.py:415
  8.8 0.1 collective-permute-start.4
  8.9 1.5 %collective-permute-start.3 = (f32[8,128]{1,0:T(8,128)S(1)}, f32[8,128]{1,0:T(8,128)S(1)}, u32[]{:S(2)}, u32[]{:S(2)}) collective-permute-start(f32[8,128]{1,0:T(8,128)S(1)} %get-tuple-element.46), channel_id=1, source_target_pairs={{0,2},{2,0},{1,3},{3,1},{4,6},{6,4},{5,7},{7,5},{8,10},{10,8},{9,1... | collective-permute-start | bytes 12296 | tf_op jit(solution)/shard_map/ppermute | solution.py:415
  10.4 0.0 collective-permute-done.2
  10.4 0.0 collective-permute-done.1.w1b_ref
  10.4 0.0 copy-start.5
  10.4 2.4 %inner.1.inner_ref = bf16[7,256,256]{2,1,0:T(8,128)(2,1)S(1)} custom-call(bf16[9,256,256]{2,1,0:T(8,128)(2,1)S(1)} %get-tuple-element.47.near_ref, bf16[3,3,256,128]{3,2,1,0:T(8,128)(2,1)S(1)} %copy-done.1, bf16[3,3,256,128]{3,2,1,0:T(8,128)(2,1)S(1)} %collective-permute-done.1.w1b_ref, f32[1,128]{1,0:T(1,128)S(1)} %bitcast.17, f32[1,128]{1,0:T(1,128)S(1)} %bitcast.20), custom_call_target="tpu_custom_call" | custom-call | flops 3000000000 | bytes 3000000 | tf_op jit(solution)/shard_map/inner/pallas_call | solution.py:43
  12.8 0.0 collective-permute-done.3
  12.8 2.9 %collective-permute-start.7 = (f32[8,128]{1,0:T(8,128)S(1)}, f32[8,128]{1,0:T(8,128)S(1)}, u32[]{:S(2)}, u32[]{:S(2)}) collective-permute-start(f32[8,128]{1,0:T(8,128)S(1)} %add.3.rest_0_), channel_id=1, source_target_pairs={{0,12},{4,8},{8,4},{12,0},{1,13},{5,9},{9,5},{13,1},{2,14},{6,10},... | collective-permute-start | bytes 12296 | tf_op jit(solution)/shard_map/ppermute | solution.py:415
  15.7 0.2 collective-permute-start.6
  15.9 1.3 %collective-permute-start.5 = (f32[8,128]{1,0:T(8,128)S(1)}, f32[8,128]{1,0:T(8,128)S(1)}, u32[]{:S(2)}, u32[]{:S(2)}) collective-permute-start(f32[8,128]{1,0:T(8,128)S(1)} %add.3.rest_0_), channel_id=1, source_target_pairs={{0,4},{4,0},{8,12},{12,8},{1,5},{5,1},{9,13},{13,9},{2,6},{6,2},{1... | collective-permute-start | bytes 12296 | tf_op jit(solution)/shard_map/ppermute | solution.py:415
  17.2 0.0 collective-permute-done.halo_ref
  17.2 0.0 collective-permute-done.4
  17.2 4.1 %head.1 = (bf16[10,256,256]{2,1,0:T(8,128)(2,1)S(1)}, f32[8,256,128]{2,1,0:T(8,128)S(1)}, f32[1,128]{1,0:T(1,128)S(1)}, bf16[1152,256]{1,0:T(8,128)(2,1)S(1)}) custom-call(bf16[9,256,256]{2,1,0:T(8,128)(2,1)S(1)} %get-tuple-element.47.near_ref, bf16[7,256,256]{2,1,0:T(8,128)(2,1)S(1)} %inner.1.inner_ref, bf16[784,256]{1,0:T(8,128)(2,1)S(1)} %collective-permute-done.halo_ref, ...), custom_call_target="tpu_custom_call" | custom-call | flops 5000000000 | bytes 5000000 | tf_op jit(solution)/shard_map/head/pallas_call | solution.py:43
  21.3 0.0 collective-permute-done.7.rest_3_
  21.4 0.0 collective-permute-done.6.rest_2_
  21.4 0.0 collective-permute-done.5.rest_1_
  21.4 1.6 %back.1 = (bf16[6,336,256]{2,1,0:T(8,128)(2,1)S(1)}, bf16[6,256,128]{2,1,0:T(8,128)(2,1)S(1)}, bf16[8,256,128]{2,1,0:T(8,128)(2,1)S(1)}, f32[4,128]{1,0:T(4,128)S(1)}) custom-call(bf16[10,256,256]{2,1,0:T(8,128)(2,1)S(1)} %get-tuple-element.52.hid_ref, f32[8,256,128]{2,1,0:T(8,128)S(1)} %get-tuple-element.53.dz_ref, ...), custom_call_target="tpu_custom_call" | custom-call | flops 4000000000 | bytes 4000000 | tf_op jit(solution)/shard_map/back/pallas_call | solution.py:43
  23.0 0.1 collective-permute-start.8
  23.1 0.0 copy-start
  23.1 1.0 %cls.1 = (f32[896,128]{1,0:T(8,128)S(1)}, f32[896,128]{1,0:T(8,128)S(1)}) custom-call(bf16[10,256,256]{2,1,0:T(8,128)(2,1)S(1)} %get-tuple-element.52.hid_ref, bf16[6,336,256]{2,1,0:T(8,128)(2,1)S(1)} %get-tuple-element.60.dt_ref), custom_call_target="tpu_custom_call" | custom-call | flops 1500000000 | bytes 1500000 | tf_op jit(solution)/shard_map/cls/pallas_call | solution.py:43
  24.1 0.6 collective-permute-start.9
  24.7 0.4 collective-permute-done.8.other_ref
  25.0 3.0 %shared.1 = (f32[1152,128]{1,0:T(8,128)S(1)}, bf16[1152,128]{1,0:T(8,128)(2,1)S(1)}) custom-call(bf16[12,256,256]{2,1,0:T(8,128)(2,1)S(1)} %bitcast.13, bf16[784,256]{1,0:T(8,128)(2,1)S(1)} %collective-permute-done.halo_ref, bf16[6,256,128]{2,1,0:T(8,128)(2,1)S(1)} %get-tuple-element.56.own_ref, bf16[8,256,128]{2,1,0:T(8,128)(2,1)S(1)} %collective-permute-done.8.other_ref), custom_call_target="tpu_custom_call" | custom-call | flops 4000000000 | bytes 4000000 | tf_op jit(solution)/shard_map/shared/pallas_call | solution.py:43
  28.0 1.2 %collective-permute-start.10 = (bf16[1152,128]{1,0:T(8,128)(2,1)S(1)}, bf16[1152,128]{1,0:T(8,128)(2,1)S(1)}, u32[]{:S(2)}, u32[]{:S(2)}) collective-permute-start(bf16[1152,128]{1,0:T(8,128)(2,1)S(1)} %get-tuple-element.64), channel_id=1, source_target_pairs={{0,2},{2,0},{1,3},{3,1},{4,6},{6,4},{5,7},{7,5},{8,10},{10,8},{9,1... | collective-permute-start | bytes 884744 | tf_op jit(solution)/shard_map/ppermute | solution.py:415
  29.2 0.0 collective-permute-done.9.theirs_ref
  29.2 0.1 cls_split.1
  29.3 3.0 %collective-permute-start.11 = (bf16[240,128]{1,0:T(8,128)(2,1)S(1)}, bf16[240,128]{1,0:T(8,128)(2,1)S(1)}, u32[]{:S(2)}, u32[]{:S(2)}) collective-permute-start(bf16[240,128]{1,0:T(8,128)(2,1)S(1)} %get-tuple-element.65), channel_id=1, source_target_pairs={{0,12},{4,8},{8,4},{12,0},{1,13},{5,9},{9,5},{13,1},{2,14},{6,10},... | collective-permute-start | bytes 184328 | tf_op jit(solution)/shard_map/ppermute | solution.py:415
  32.3 0.0 collective-permute-start.12
  32.3 1.5 %collective-permute-start.13 = (bf16[240,128]{1,0:T(8,128)(2,1)S(1)}, bf16[240,128]{1,0:T(8,128)(2,1)S(1)}, u32[]{:S(2)}, u32[]{:S(2)}) collective-permute-start(bf16[240,128]{1,0:T(8,128)(2,1)S(1)} %get-tuple-element.67), channel_id=1, source_target_pairs={{0,4},{4,0},{8,12},{12,8},{1,5},{5,1},{9,13},{13,9},{2,6},{6,2},{1... | collective-permute-start | bytes 184328 | tf_op jit(solution)/shard_map/ppermute | solution.py:415
  33.8 2.0 %collective-permute-done.11.refs_1_ = bf16[240,128]{1,0:T(8,128)(2,1)S(1)} collective-permute-done((bf16[240,128]{1,0:T(8,128)(2,1)S(1)}, bf16[240,128]{1,0:T(8,128)(2,1)S(1)}, u32[]{:S(2)}, u32[]{:S(2)}) %collective-permute-start.11) | collective-permute-done | bytes 61472 | tf_op jit(solution)/shard_map/ppermute | solution.py:415
  35.8 2.0 %collective-permute-done.12.refs_2_ = bf16[240,128]{1,0:T(8,128)(2,1)S(1)} collective-permute-done((bf16[240,128]{1,0:T(8,128)(2,1)S(1)}, bf16[240,128]{1,0:T(8,128)(2,1)S(1)}, u32[]{:S(2)}, u32[]{:S(2)}) %collective-permute-start.12) | collective-permute-done | bytes 61472 | tf_op jit(solution)/shard_map/ppermute | solution.py:415
  37.8 0.0 collective-permute-done.13.refs_3_
  37.8 0.0 collective-permute-done.10.refs_0_
  37.8 0.1 sum.1
  37.9 2.5 %collective-permute-start.14 = (bf16[288,128]{1,0:T(8,128)(2,1)S(1)}, bf16[288,128]{1,0:T(8,128)(2,1)S(1)}, u32[]{:S(2)}, u32[]{:S(2)}) collective-permute-start(bf16[288,128]{1,0:T(8,128)(2,1)S(1)} %get-tuple-element.71), channel_id=1, source_target_pairs={{0,12},{4,8},{8,4},{12,0},{1,13},{5,9},{9,5},{13,1},{2,14},{6,10},... | collective-permute-start | bytes 221192 | tf_op jit(solution)/shard_map/ppermute | solution.py:415
  40.4 0.0 collective-permute-start.15
  40.4 1.9 %collective-permute-start.16 = (bf16[288,128]{1,0:T(8,128)(2,1)S(1)}, bf16[288,128]{1,0:T(8,128)(2,1)S(1)}, u32[]{:S(2)}, u32[]{:S(2)}) collective-permute-start(bf16[288,128]{1,0:T(8,128)(2,1)S(1)} %get-tuple-element.73), channel_id=1, source_target_pairs={{0,4},{4,0},{8,12},{12,8},{1,5},{5,1},{9,13},{13,9},{2,6},{6,2},{1... | collective-permute-start | bytes 221192 | tf_op jit(solution)/shard_map/ppermute | solution.py:415
  42.4 0.9 %collective-permute-start.17 = (bf16[128,128]{1,0:T(8,128)(2,1)S(1)}, bf16[128,128]{1,0:T(8,128)(2,1)S(1)}, u32[]{:S(2)}, u32[]{:S(2)}) collective-permute-start(bf16[128,128]{1,0:T(8,128)(2,1)S(1)} %get-tuple-element.74), channel_id=1, source_target_pairs={{0,2},{2,0},{1,3},{3,1},{4,6},{6,4},{5,7},{7,5},{8,10},{10,8},{9,1... | collective-permute-start | bytes 98312 | tf_op jit(solution)/shard_map/ppermute | solution.py:415
  43.3 3.0 %collective-permute-done.17.refs_3_ = bf16[128,128]{1,0:T(8,128)(2,1)S(1)} collective-permute-done((bf16[128,128]{1,0:T(8,128)(2,1)S(1)}, bf16[128,128]{1,0:T(8,128)(2,1)S(1)}, u32[]{:S(2)}, u32[]{:S(2)}) %collective-permute-start.17) | collective-permute-done | bytes 32800 | tf_op jit(solution)/shard_map/ppermute | solution.py:415
  46.3 0.0 collective-permute-done.14.refs_0_
  46.3 1.1 %collective-permute-done.15.refs_1_ = bf16[288,128]{1,0:T(8,128)(2,1)S(1)} collective-permute-done((bf16[288,128]{1,0:T(8,128)(2,1)S(1)}, bf16[288,128]{1,0:T(8,128)(2,1)S(1)}, u32[]{:S(2)}, u32[]{:S(2)}) %collective-permute-start.15) | collective-permute-done | bytes 73760 | tf_op jit(solution)/shard_map/ppermute | solution.py:415
  47.5 2.2 %collective-permute-start.21 = (bf16[288,128]{1,0:T(8,128)(2,1)S(1)}, bf16[288,128]{1,0:T(8,128)(2,1)S(1)}, u32[]{:S(2)}, u32[]{:S(2)}) collective-permute-start(bf16[288,128]{1,0:T(8,128)(2,1)S(1)} %get-tuple-element.76.refs_0_), channel_id=1, source_target_pairs={{0,12},{4,8},{8,4},{12,0},{1,13},{5,9},{9,5},{13,1},{2,14},{6,10},... | collective-permute-start | bytes 221192 | tf_op jit(solution)/shard_map/ppermute | solution.py:415
  49.7 2.2 %collective-permute-start.19 = (bf16[288,128]{1,0:T(8,128)(2,1)S(1)}, bf16[288,128]{1,0:T(8,128)(2,1)S(1)}, u32[]{:S(2)}, u32[]{:S(2)}) collective-permute-start(bf16[288,128]{1,0:T(8,128)(2,1)S(1)} %get-tuple-element.76.refs_0_), channel_id=1, source_target_pairs={{0,4},{4,0},{8,12},{12,8},{1,5},{5,1},{9,13},{13,9},{2,6},{6,2},{1... | collective-permute-start | bytes 221192 | tf_op jit(solution)/shard_map/ppermute | solution.py:415
  51.9 0.9 %collective-permute-start.22 = (bf16[112,128]{1,0:T(8,128)(2,1)S(1)}, bf16[112,128]{1,0:T(8,128)(2,1)S(1)}, u32[]{:S(2)}, u32[]{:S(2)}) collective-permute-start(bf16[112,128]{1,0:T(8,128)(2,1)S(1)} %get-tuple-element.77.refs_4_), channel_id=1, source_target_pairs={{0,2},{2,0},{1,3},{3,1},{4,6},{6,4},{5,7},{7,5},{8,10},{10,8},{9,1... | collective-permute-start | bytes 86024 | tf_op jit(solution)/shard_map/ppermute | solution.py:415
  52.8 3.0 %collective-permute-done.22.refs_5_ = bf16[112,128]{1,0:T(8,128)(2,1)S(1)} collective-permute-done((bf16[112,128]{1,0:T(8,128)(2,1)S(1)}, bf16[112,128]{1,0:T(8,128)(2,1)S(1)}, u32[]{:S(2)}, u32[]{:S(2)}) %collective-permute-start.22) | collective-permute-done | bytes 28704 | tf_op jit(solution)/shard_map/ppermute | solution.py:415
  55.8 0.0 collective-permute-done.21.refs_3_
  55.8 0.4 collective-permute-done.20.refs_2_
  56.2 0.0 collective-permute-done.19.refs_1_
  56.3 1.0 %collective-permute-start.23 = (bf16[1152,128]{1,0:T(8,128)(2,1)S(1)}, bf16[1152,128]{1,0:T(8,128)(2,1)S(1)}, u32[]{:S(2)}, u32[]{:S(2)}) collective-permute-start(bf16[1152,128]{1,0:T(8,128)(2,1)S(1)} %get-tuple-element.78.refs_0_), channel_id=1, source_target_pairs={{0,2},{2,0},{1,3},{3,1},{4,6},{6,4},{5,7},{7,5},{8,10},{10,8},{9,1... | collective-permute-start | bytes 884744 | tf_op jit(solution)/shard_map/ppermute | solution.py:415
  57.2 2.4 %collective-permute-start.26 = (bf16[224,128]{1,0:T(8,128)(2,1)S(1)}, bf16[224,128]{1,0:T(8,128)(2,1)S(1)}, u32[]{:S(2)}, u32[]{:S(2)}) collective-permute-start(bf16[224,128]{1,0:T(8,128)(2,1)S(1)} %get-tuple-element.79.refs_2_), channel_id=1, source_target_pairs={{0,12},{4,8},{8,4},{12,0},{1,13},{5,9},{9,5},{13,1},{2,14},{6,10},... | collective-permute-start | bytes 172040 | tf_op jit(solution)/shard_map/ppermute | solution.py:415
  59.6 0.0 collective-permute-start.25
  59.6 2.0 %collective-permute-start.24 = (bf16[224,128]{1,0:T(8,128)(2,1)S(1)}, bf16[224,128]{1,0:T(8,128)(2,1)S(1)}, u32[]{:S(2)}, u32[]{:S(2)}) collective-permute-start(bf16[224,128]{1,0:T(8,128)(2,1)S(1)} %get-tuple-element.79.refs_2_), channel_id=1, source_target_pairs={{0,4},{4,0},{8,12},{12,8},{1,5},{5,1},{9,13},{13,9},{2,6},{6,2},{1... | collective-permute-start | bytes 172040 | tf_op jit(solution)/shard_map/ppermute | solution.py:415
  61.6 0.0 collective-permute-start.18
  61.6 1.2 %collective-permute-done.18.theirs_ref = f32[4,128]{1,0:T(4,128)S(1)} collective-permute-done((f32[4,128]{1,0:T(4,128)S(1)}, f32[4,128]{1,0:T(4,128)S(1)}, u32[]{:S(2)}, u32[]{:S(2)}) %collective-permute-start.18) | collective-permute-done | bytes 2080 | tf_op jit(solution)/shard_map/ppermute | solution.py:415
  62.8 0.5 collective-permute-done.26.refs_5_
  63.3 1.9 %collective-permute-done.25.refs_4_ = bf16[224,128]{1,0:T(8,128)(2,1)S(1)} collective-permute-done((bf16[224,128]{1,0:T(8,128)(2,1)S(1)}, bf16[224,128]{1,0:T(8,128)(2,1)S(1)}, u32[]{:S(2)}, u32[]{:S(2)}) %collective-permute-start.25) | collective-permute-done | bytes 57376 | tf_op jit(solution)/shard_map/ppermute | solution.py:415
  65.1 0.0 collective-permute-done.24.refs_3_
  65.1 0.1 collective-permute-done.23.refs_1_
  65.2 1.3 %out.1 = (f32[2304,128]{1,0:T(8,128)}, f32[1,128]{1,0:T(1,128)}, f32[3,3,99,128]{3,2,1,0:T(8,128)}, f32[1,99]{1,0:T(1,128)}, f32[1,1]{1,0:T(1,128)}) custom-call(f32[4,128]{1,0:T(4,128)S(1)} %get-tuple-element.75.small_ref, f32[4,128]{1,0:T(4,128)S(1)} %collective-permute-done.18.theirs_ref, bf16[1152,128]{1,0:T(8,128)(2,1)S(1)} %get-tuple-element.78.refs_0_, ...), custom_call_target="tpu_custom_call" | custom-call | flops 1500000000 | bytes 1500000 | tf_op jit(solution)/shard_map/out/pallas_call | solution.py:43
  (14 shorter events, 0.1 us)
Async XLA Ops:
  0.6 9.7 %collective-permute-start.1 = (bf16[3,3,256,128]{3,2,1,0:T(8,128)(2,1)}, bf16[3,3,256,128]{3,2,1,0:T(8,128)(2,1)S(1)}, u32[]{:S(2)}, u32[]{:S(2)}) collective-permute-start(bf16[3,3,256,128]{3,2,1,0:T(8,128)(2,1)} %w1a_ref.3), channel_id=1, source_target_pairs={{0,1},{1,0},{2,3},{3,2},{4,5},{5,4},{6,7},{7,6},{8,9},{9,8},{10,11... | collective-permute-start | bytes 1769480 | tf_op jit(solution)/shard_map/ppermute | solution.py:415
  1.2 0.9 %copy-start.3 = (s32[1,12,2304]{2,0,1:T(1,128)S(1)}, s32[1,12,2304]{2,0,1:T(1,128)}, u32[]{:S(2)}) copy-start(s32[1,12,2304]{2,0,1:T(1,128)} %param.7) | copy-start | bytes 331780
  2.0 2.7 %copy-start.4 = (f32[128]{0:T(128)S(1)}, f32[128]{0:T(128)}, u32[]{:S(2)}) copy-start(f32[128]{0:T(128)} %param.9) | copy-start | bytes 1540
  2.0 6.7 %copy-start.2 = (bf16[3,3,128,99]{2,3,1,0:T(8,128)(2,1)S(1)}, bf16[3,3,128,99]{2,3,1,0:T(8,128)(2,1)}, u32[]{:S(2)}) copy-start(bf16[3,3,128,99]{2,3,1,0:T(8,128)(2,1)} %param.10) | copy-start | bytes 684292
  2.1 8.3 %copy-start.1 = (bf16[3,3,256,128]{3,2,1,0:T(8,128)(2,1)S(1)}, bf16[3,3,256,128]{3,2,1,0:T(8,128)(2,1)}, u32[]{:S(2)}) copy-start(bf16[3,3,256,128]{3,2,1,0:T(8,128)(2,1)} %w1a_ref.3) | copy-start | bytes 1769476
  4.1 13.2 %collective-permute-start = (bf16[784,256]{1,0:T(8,128)(2,1)S(1)}, bf16[784,256]{1,0:T(8,128)(2,1)S(1)}, u32[]{:S(2)}, u32[]{:S(2)}) collective-permute-start(bf16[784,256]{1,0:T(8,128)(2,1)S(1)} %get-tuple-element.45), channel_id=1, source_target_pairs={{1,4},{4,1},{5,8},{8,5},{9,12},{12,9},{3,6},{6,3},{7,10},{10,7},{1... | collective-permute-start | bytes 1204232 | tf_op jit(solution)/shard_map/ppermute | solution.py:459
  4.8 5.6 %collective-permute-start.2 = (f32[128]{0:T(128)S(1)}, f32[128]{0:T(128)S(1)}, u32[]{:S(2)}, u32[]{:S(2)}) collective-permute-start(f32[128]{0:T(128)S(1)} %copy-done.4), channel_id=1, source_target_pairs={{0,1},{1,0},{2,3},{3,2},{4,5},{5,4},{6,7},{7,6},{8,9},{9,8},{10,11... | collective-permute-start | bytes 1544 | tf_op jit(solution)/shard_map/ppermute | solution.py:415
  8.8 8.5 %collective-permute-start.4 = (bf16[3,3,128,99]{2,3,1,0:T(8,128)(2,1)S(1)}, bf16[3,3,128,99]{2,3,1,0:T(8,128)(2,1)S(1)}, u32[]{:S(2)}, u32[]{:S(2)}) collective-permute-start(bf16[3,3,128,99]{2,3,1,0:T(8,128)(2,1)S(1)} %copy-done.2), channel_id=1, source_target_pairs={{0,1},{1,0},{2,3},{3,2},{4,5},{5,4},{6,7},{7,6},{8,9},{9,8},{10,11... | collective-permute-start | bytes 684296 | tf_op jit(solution)/shard_map/ppermute | solution.py:415
  8.9 3.9 %collective-permute-start.3 = (f32[8,128]{1,0:T(8,128)S(1)}, f32[8,128]{1,0:T(8,128)S(1)}, u32[]{:S(2)}, u32[]{:S(2)}) collective-permute-start(f32[8,128]{1,0:T(8,128)S(1)} %get-tuple-element.46), channel_id=1, source_target_pairs={{0,2},{2,0},{1,3},{3,1},{4,6},{6,4},{5,7},{7,5},{8,10},{10,8},{9,1... | collective-permute-start | bytes 12296 | tf_op jit(solution)/shard_map/ppermute | solution.py:415
  10.4 6.9 %copy-start.5 = (f32[99]{0:T(128)S(1)}, f32[99]{0:T(128)}, u32[]{:S(2)}) copy-start(f32[99]{0:T(128)} %param.11) | copy-start | bytes 1192
  12.8 8.6 %collective-permute-start.7 = (f32[8,128]{1,0:T(8,128)S(1)}, f32[8,128]{1,0:T(8,128)S(1)}, u32[]{:S(2)}, u32[]{:S(2)}) collective-permute-start(f32[8,128]{1,0:T(8,128)S(1)} %add.3.rest_0_), channel_id=1, source_target_pairs={{0,12},{4,8},{8,4},{12,0},{1,13},{5,9},{9,5},{13,1},{2,14},{6,10},... | collective-permute-start | bytes 12296 | tf_op jit(solution)/shard_map/ppermute | solution.py:415
  15.7 5.6 %collective-permute-start.6 = (f32[8,128]{1,0:T(8,128)S(1)}, f32[8,128]{1,0:T(8,128)S(1)}, u32[]{:S(2)}, u32[]{:S(2)}) collective-permute-start(f32[8,128]{1,0:T(8,128)S(1)} %add.3.rest_0_), channel_id=1, source_target_pairs={{0,8},{4,12},{8,0},{12,4},{1,9},{5,13},{9,1},{13,5},{2,10},{6,14},... | collective-permute-start | bytes 12296 | tf_op jit(solution)/shard_map/ppermute | solution.py:415
  15.9 5.5 %collective-permute-start.5 = (f32[8,128]{1,0:T(8,128)S(1)}, f32[8,128]{1,0:T(8,128)S(1)}, u32[]{:S(2)}, u32[]{:S(2)}) collective-permute-start(f32[8,128]{1,0:T(8,128)S(1)} %add.3.rest_0_), channel_id=1, source_target_pairs={{0,4},{4,0},{8,12},{12,8},{1,5},{5,1},{9,13},{13,9},{2,6},{6,2},{1... | collective-permute-start | bytes 12296 | tf_op jit(solution)/shard_map/ppermute | solution.py:415
  23.0 2.0 %collective-permute-start.8 = (bf16[8,256,128]{2,1,0:T(8,128)(2,1)S(1)}, bf16[8,256,128]{2,1,0:T(8,128)(2,1)S(1)}, u32[]{:S(2)}, u32[]{:S(2)}) collective-permute-start(bf16[8,256,128]{2,1,0:T(8,128)(2,1)S(1)} %get-tuple-element.57), channel_id=1, source_target_pairs={{0,1},{1,0},{2,3},{3,2},{4,5},{5,4},{6,7},{7,6},{8,9},{9,8},{10,11... | collective-permute-start | bytes 1572872 | tf_op jit(solution)/shard_map/ppermute | solution.py:415
  23.1 1.9 %copy-start = (bf16[1,12,256,256]{3,2,1,0:T(8,128)(2,1)S(1)}, bf16[1,12,256,256]{3,2,1,0:T(8,128)(2,1)}, u32[]{:S(2)}) copy-start(bf16[1,12,256,256]{3,2,1,0:T(8,128)(2,1)} %param.6) | copy-start | bytes 4718596
  24.1 5.1 %collective-permute-start.9 = (f32[896,128]{1,0:T(8,128)S(1)}, f32[896,128]{1,0:T(8,128)S(1)}, u32[]{:S(2)}, u32[]{:S(2)}) collective-permute-start(f32[896,128]{1,0:T(8,128)S(1)} %get-tuple-element.62), channel_id=1, source_target_pairs={{0,1},{1,0},{2,3},{3,2},{4,5},{5,4},{6,7},{7,6},{8,9},{9,8},{10,11... | collective-permute-start | bytes 1376264 | tf_op jit(solution)/shard_map/ppermute | solution.py:415
  28.0 9.8 %collective-permute-start.10 = (bf16[1152,128]{1,0:T(8,128)(2,1)S(1)}, bf16[1152,128]{1,0:T(8,128)(2,1)S(1)}, u32[]{:S(2)}, u32[]{:S(2)}) collective-permute-start(bf16[1152,128]{1,0:T(8,128)(2,1)S(1)} %get-tuple-element.64), channel_id=1, source_target_pairs={{0,2},{2,0},{1,3},{3,1},{4,6},{6,4},{5,7},{7,5},{8,10},{10,8},{9,1... | collective-permute-start | bytes 884744 | tf_op jit(solution)/shard_map/ppermute | solution.py:415
  29.3 6.5 %collective-permute-start.11 = (bf16[240,128]{1,0:T(8,128)(2,1)S(1)}, bf16[240,128]{1,0:T(8,128)(2,1)S(1)}, u32[]{:S(2)}, u32[]{:S(2)}) collective-permute-start(bf16[240,128]{1,0:T(8,128)(2,1)S(1)} %get-tuple-element.65), channel_id=1, source_target_pairs={{0,12},{4,8},{8,4},{12,0},{1,13},{5,9},{9,5},{13,1},{2,14},{6,10},... | collective-permute-start | bytes 184328 | tf_op jit(solution)/shard_map/ppermute | solution.py:415
  32.3 5.5 %collective-permute-start.12 = (bf16[240,128]{1,0:T(8,128)(2,1)S(1)}, bf16[240,128]{1,0:T(8,128)(2,1)S(1)}, u32[]{:S(2)}, u32[]{:S(2)}) collective-permute-start(bf16[240,128]{1,0:T(8,128)(2,1)S(1)} %get-tuple-element.66), channel_id=1, source_target_pairs={{0,8},{4,12},{8,0},{12,4},{1,9},{5,13},{9,1},{13,5},{2,10},{6,14},... | collective-permute-start | bytes 184328 | tf_op jit(solution)/shard_map/ppermute | solution.py:415
  32.3 5.5 %collective-permute-start.13 = (bf16[240,128]{1,0:T(8,128)(2,1)S(1)}, bf16[240,128]{1,0:T(8,128)(2,1)S(1)}, u32[]{:S(2)}, u32[]{:S(2)}) collective-permute-start(bf16[240,128]{1,0:T(8,128)(2,1)S(1)} %get-tuple-element.67), channel_id=1, source_target_pairs={{0,4},{4,0},{8,12},{12,8},{1,5},{5,1},{9,13},{13,9},{2,6},{6,2},{1... | collective-permute-start | bytes 184328 | tf_op jit(solution)/shard_map/ppermute | solution.py:415
  37.9 8.4 %collective-permute-start.14 = (bf16[288,128]{1,0:T(8,128)(2,1)S(1)}, bf16[288,128]{1,0:T(8,128)(2,1)S(1)}, u32[]{:S(2)}, u32[]{:S(2)}) collective-permute-start(bf16[288,128]{1,0:T(8,128)(2,1)S(1)} %get-tuple-element.71), channel_id=1, source_target_pairs={{0,12},{4,8},{8,4},{12,0},{1,13},{5,9},{9,5},{13,1},{2,14},{6,10},... | collective-permute-start | bytes 221192 | tf_op jit(solution)/shard_map/ppermute | solution.py:415
  40.4 7.0 %collective-permute-start.15 = (bf16[288,128]{1,0:T(8,128)(2,1)S(1)}, bf16[288,128]{1,0:T(8,128)(2,1)S(1)}, u32[]{:S(2)}, u32[]{:S(2)}) collective-permute-start(bf16[288,128]{1,0:T(8,128)(2,1)S(1)} %get-tuple-element.72), channel_id=1, source_target_pairs={{0,8},{4,12},{8,0},{12,4},{1,9},{5,13},{9,1},{13,5},{2,10},{6,14},... | collective-permute-start | bytes 221192 | tf_op jit(solution)/shard_map/ppermute | solution.py:415
  40.4 7.0 %collective-permute-start.16 = (bf16[288,128]{1,0:T(8,128)(2,1)S(1)}, bf16[288,128]{1,0:T(8,128)(2,1)S(1)}, u32[]{:S(2)}, u32[]{:S(2)}) collective-permute-start(bf16[288,128]{1,0:T(8,128)(2,1)S(1)} %get-tuple-element.73), channel_id=1, source_target_pairs={{0,4},{4,0},{8,12},{12,8},{1,5},{5,1},{9,13},{13,9},{2,6},{6,2},{1... | collective-permute-start | bytes 221192 | tf_op jit(solution)/shard_map/ppermute | solution.py:415
  42.4 3.9 %collective-permute-start.17 = (bf16[128,128]{1,0:T(8,128)(2,1)S(1)}, bf16[128,128]{1,0:T(8,128)(2,1)S(1)}, u32[]{:S(2)}, u32[]{:S(2)}) collective-permute-start(bf16[128,128]{1,0:T(8,128)(2,1)S(1)} %get-tuple-element.74), channel_id=1, source_target_pairs={{0,2},{2,0},{1,3},{3,1},{4,6},{6,4},{5,7},{7,5},{8,10},{10,8},{9,1... | collective-permute-start | bytes 98312 | tf_op jit(solution)/shard_map/ppermute | solution.py:415
  47.5 8.3 %collective-permute-start.21 = (bf16[288,128]{1,0:T(8,128)(2,1)S(1)}, bf16[288,128]{1,0:T(8,128)(2,1)S(1)}, u32[]{:S(2)}, u32[]{:S(2)}) collective-permute-start(bf16[288,128]{1,0:T(8,128)(2,1)S(1)} %get-tuple-element.76.refs_0_), channel_id=1, source_target_pairs={{0,12},{4,8},{8,4},{12,0},{1,13},{5,9},{9,5},{13,1},{2,14},{6,10},... | collective-permute-start | bytes 221192 | tf_op jit(solution)/shard_map/ppermute | solution.py:415
  49.7 6.5 %collective-permute-start.20 = (bf16[288,128]{1,0:T(8,128)(2,1)S(1)}, bf16[288,128]{1,0:T(8,128)(2,1)S(1)}, u32[]{:S(2)}, u32[]{:S(2)}) collective-permute-start(bf16[288,128]{1,0:T(8,128)(2,1)S(1)} %get-tuple-element.76.refs_0_), channel_id=1, source_target_pairs={{0,8},{4,12},{8,0},{12,4},{1,9},{5,13},{9,1},{13,5},{2,10},{6,14},... | collective-permute-start | bytes 221192 | tf_op jit(solution)/shard_map/ppermute | solution.py:415
  49.7 6.5 %collective-permute-start.19 = (bf16[288,128]{1,0:T(8,128)(2,1)S(1)}, bf16[288,128]{1,0:T(8,128)(2,1)S(1)}, u32[]{:S(2)}, u32[]{:S(2)}) collective-permute-start(bf16[288,128]{1,0:T(8,128)(2,1)S(1)} %get-tuple-element.76.refs_0_), channel_id=1, source_target_pairs={{0,4},{4,0},{8,12},{12,8},{1,5},{5,1},{9,13},{13,9},{2,6},{6,2},{1... | collective-permute-start | bytes 221192 | tf_op jit(solution)/shard_map/ppermute | solution.py:415
  51.9 3.9 %collective-permute-start.22 = (bf16[112,128]{1,0:T(8,128)(2,1)S(1)}, bf16[112,128]{1,0:T(8,128)(2,1)S(1)}, u32[]{:S(2)}, u32[]{:S(2)}) collective-permute-start(bf16[112,128]{1,0:T(8,128)(2,1)S(1)} %get-tuple-element.77.refs_4_), channel_id=1, source_target_pairs={{0,2},{2,0},{1,3},{3,1},{4,6},{6,4},{5,7},{7,5},{8,10},{10,8},{9,1... | collective-permute-start | bytes 86024 | tf_op jit(solution)/shard_map/ppermute | solution.py:415
  56.3 9.0 %collective-permute-start.23 = (bf16[1152,128]{1,0:T(8,128)(2,1)S(1)}, bf16[1152,128]{1,0:T(8,128)(2,1)S(1)}, u32[]{:S(2)}, u32[]{:S(2)}) collective-permute-start(bf16[1152,128]{1,0:T(8,128)(2,1)S(1)} %get-tuple-element.78.refs_0_), channel_id=1, source_target_pairs={{0,2},{2,0},{1,3},{3,1},{4,6},{6,4},{5,7},{7,5},{8,10},{10,8},{9,1... | collective-permute-start | bytes 884744 | tf_op jit(solution)/shard_map/ppermute | solution.py:415
  57.2 6.1 %collective-permute-start.26 = (bf16[224,128]{1,0:T(8,128)(2,1)S(1)}, bf16[224,128]{1,0:T(8,128)(2,1)S(1)}, u32[]{:S(2)}, u32[]{:S(2)}) collective-permute-start(bf16[224,128]{1,0:T(8,128)(2,1)S(1)} %get-tuple-element.79.refs_2_), channel_id=1, source_target_pairs={{0,12},{4,8},{8,4},{12,0},{1,13},{5,9},{9,5},{13,1},{2,14},{6,10},... | collective-permute-start | bytes 172040 | tf_op jit(solution)/shard_map/ppermute | solution.py:415
  59.6 5.5 %collective-permute-start.25 = (bf16[224,128]{1,0:T(8,128)(2,1)S(1)}, bf16[224,128]{1,0:T(8,128)(2,1)S(1)}, u32[]{:S(2)}, u32[]{:S(2)}) collective-permute-start(bf16[224,128]{1,0:T(8,128)(2,1)S(1)} %get-tuple-element.79.refs_2_), channel_id=1, source_target_pairs={{0,8},{4,12},{8,0},{12,4},{1,9},{5,13},{9,1},{13,5},{2,10},{6,14},... | collective-permute-start | bytes 172040 | tf_op jit(solution)/shard_map/ppermute | solution.py:415
  59.6 5.5 %collective-permute-start.24 = (bf16[224,128]{1,0:T(8,128)(2,1)S(1)}, bf16[224,128]{1,0:T(8,128)(2,1)S(1)}, u32[]{:S(2)}, u32[]{:S(2)}) collective-permute-start(bf16[224,128]{1,0:T(8,128)(2,1)S(1)} %get-tuple-element.79.refs_2_), channel_id=1, source_target_pairs={{0,4},{4,0},{8,12},{12,8},{1,5},{5,1},{9,13},{13,9},{2,6},{6,2},{1... | collective-permute-start | bytes 172040 | tf_op jit(solution)/shard_map/ppermute | solution.py:415
  61.6 1.2 %collective-permute-start.18 = (f32[4,128]{1,0:T(4,128)S(1)}, f32[4,128]{1,0:T(4,128)S(1)}, u32[]{:S(2)}, u32[]{:S(2)}) collective-permute-start(f32[4,128]{1,0:T(4,128)S(1)} %get-tuple-element.75.small_ref), channel_id=1, source_target_pairs={{0,1},{1,0},{2,3},{3,2},{4,5},{5,4},{6,7},{7,6},{8,9},{9,8},{10,11... | collective-permute-start | bytes 6152 | tf_op jit(solution)/shard_map/ppermute | solution.py:415

commit v14 on v13

--- a/solution.py
+++ b/solution.py
@@ -287,12 +287,15 @@
     other_ref[9 * LOGITS :] = blank
 
 
+def partners(size):
+    return [2, 3, 1] if size == 4 else list(range(size - 1, 0, -1))
+
+
 def split(total, me, keep_ref, send_refs):
     rows = keep_ref.shape[0]
     keep_ref[...] = total[pl.ds(pl.multiple_of(me * rows, 8), rows)]
-    size = len(send_refs) + 1
-    for k, ref in enumerate(send_refs):
-        ref[0:rows] = total[pl.ds(pl.multiple_of((me ^ (size - 1 - k)) * rows, 8), rows)].astype(BF16)
+    for bit, ref in zip(partners(len(send_refs) + 1), send_refs):
+        ref[0:rows] = total[pl.ds(pl.multiple_of((me ^ bit) * rows, 8), rows)].astype(BF16)
 
 
 def shared_kernel(
@@ -384,8 +387,8 @@
 
 def join(me, in_refs, out_ref):
     rows = in_refs[0].shape[0]
-    for k, ref in enumerate(in_refs):
-        out_ref[pl.ds(pl.multiple_of((me ^ k) * rows, 8), rows)] = ref[...].astype(out_ref.dtype)
+    for bit, ref in zip([0] + partners(len(in_refs))[::-1], in_refs):
+        out_ref[pl.ds(pl.multiple_of((me ^ bit) * rows, 8), rows)] = ref[...].astype(out_ref.dtype)
 
 
 def join_kernel(n_in, where_ref, *refs):
@@ -416,12 +419,11 @@
 
 
 def others(x, axis):
-    return [swap(x, axis, bit) for bit in range(1, lax.axis_size(axis))]
+    return [swap(x, axis, bit) for bit in partners(lax.axis_size(axis))[::-1]]
 
 
 def exchange(sends, axis):
-    size = len(sends) + 1
-    return [swap(x, axis, size - 1 - k) for k, x in enumerate(sends)]
+    return [swap(x, axis, bit) for bit, x in zip(partners(len(sends) + 1), sends)]
 
 
 def round_up(n, step):

time: 66.7 us -> 65.8 us (0.987)
  starting transfers between devices: 33.5 us -> 30.5 us
  waiting for transfers between devices: 15.6 us -> 17.7 us
    ppermute x26, starting transfers between devices: 32.8 us -> 29.8 us  [swap(): return lax.ppermute(x, axis, [(i, i ^ bit) for i in range(size)])]
    ppermute x26, waiting for transfers between devices: 15.6 us -> 17.7 us  [swap(): return lax.ppermute(x, axis, [(i, i ^ bit) for i in range(size)])]
  transfers between devices with their start and end apart: 27 -> 27, of which waited for: 11 -> 13; matrix products, arithmetic and copies ran while one was open for 0% -> 0% of each run, Pallas kernels for 19% -> 19%
where the time goes in v14:
time: 65.8 us; the launch traced here: 65.6 us
  starting transfers between devices  30.5 us (46%)
  waiting for transfers between devices  17.7 us (27%)
  Pallas kernels  15.7 us (24%)
  local copies, waits for them, and re-layouts  0.92 us (1%)
  between operations  0.81 us (1%)
    ppermute x26, starting transfers between devices, swap(): return lax.ppermute(x, axis, [(i, i ^ bit) for i in range(size)])  29.8 us
    ppermute x26, waiting for transfers between devices, swap(): return lax.ppermute(x, axis, [(i, i ^ bit) for i in range(size)])  17.7 us
    pallas_call x11, Pallas kernels, call(): pl.pallas_call(functools.partial(kernel, inputs[0]), in_specs=(specs or [...  15.7 us
  transfers between devices with their start and end apart: 27, of which 13 were waited for; matrix products, arithmetic and copies ran while one was open for 0% of the time, Pallas kernels for 19%

profile of v14, /device:TPU:0, one launch (start us, length us, event | category | flops | bytes accessed | tf_op | source)
XLA Modules:
  0.0 65.6 jit_solution(3657037882732460515)
XLA Ops:
  0.6 0.5 collective-permute-start.1
  1.2 0.9 %copy-done.3 = s32[1,12,2304]{2,0,1:T(1,128)S(1)} copy-done((s32[1,12,2304]{2,0,1:T(1,128)S(1)}, s32[1,12,2304]{2,0,1:T(1,128)}, u32[]{:S(2)}) %copy-start.3) | copy-done | bytes 110616
  2.1 2.0 %edge.1 = (bf16[784,256]{1,0:T(8,128)(2,1)S(1)}, bf16[12,16,256]{2,1,0:T(8,128)(2,1)S(1)}, f32[8,128]{1,0:T(8,128)S(1)}, bf16[9,256,256]{2,1,0:T(8,128)(2,1)S(1)}) custom-call(bf16[12,256,256]{2,1,0:T(8,128)(2,1)} %bitcast.12, s32[12,1,2304]{2,1,0:T(1,128)S(1)} %bitcast.16), custom_call_target="tpu_custom_call" | custom-call | flops 2000000000 | bytes 2000000 | tf_op jit(solution)/shard_map/edge/pallas_call | solution.py:43
  4.1 0.7 %collective-permute-start = (bf16[784,256]{1,0:T(8,128)(2,1)S(1)}, bf16[784,256]{1,0:T(8,128)(2,1)S(1)}, u32[]{:S(2)}, u32[]{:S(2)}) collective-permute-start(bf16[784,256]{1,0:T(8,128)(2,1)S(1)} %get-tuple-element.45), channel_id=1, source_target_pairs={{1,4},{4,1},{5,8},{8,5},{9,12},{12,9},{3,6},{6,3},{7,10},{10,7},{1... | collective-permute-start | bytes 1204232 | tf_op jit(solution)/shard_map/ppermute | solution.py:461
  4.8 4.0 %collective-permute-start.2 = (f32[128]{0:T(128)S(1)}, f32[128]{0:T(128)S(1)}, u32[]{:S(2)}, u32[]{:S(2)}) collective-permute-start(f32[128]{0:T(128)S(1)} %copy-done.4), channel_id=1, source_target_pairs={{0,1},{1,0},{2,3},{3,2},{4,5},{5,4},{6,7},{7,6},{8,9},{9,8},{10,11... | collective-permute-start | bytes 1544 | tf_op jit(solution)/shard_map/ppermute | solution.py:418
  8.8 0.1 collective-permute-start.4
  8.9 1.5 %collective-permute-start.3 = (f32[8,128]{1,0:T(8,128)S(1)}, f32[8,128]{1,0:T(8,128)S(1)}, u32[]{:S(2)}, u32[]{:S(2)}) collective-permute-start(f32[8,128]{1,0:T(8,128)S(1)} %get-tuple-element.46), channel_id=1, source_target_pairs={{0,2},{2,0},{1,3},{3,1},{4,6},{6,4},{5,7},{7,5},{8,10},{10,8},{9,1... | collective-permute-start | bytes 12296 | tf_op jit(solution)/shard_map/ppermute | solution.py:418
  10.4 0.0 collective-permute-done.2
  10.4 0.0 collective-permute-done.1.w1b_ref
  10.4 0.0 copy-start.5
  10.4 2.4 %inner.1.inner_ref = bf16[7,256,256]{2,1,0:T(8,128)(2,1)S(1)} custom-call(bf16[9,256,256]{2,1,0:T(8,128)(2,1)S(1)} %get-tuple-element.47.near_ref, bf16[3,3,256,128]{3,2,1,0:T(8,128)(2,1)S(1)} %copy-done.1, bf16[3,3,256,128]{3,2,1,0:T(8,128)(2,1)S(1)} %collective-permute-done.1.w1b_ref, f32[1,128]{1,0:T(1,128)S(1)} %bitcast.17, f32[1,128]{1,0:T(1,128)S(1)} %bitcast.20), custom_call_target="tpu_custom_call" | custom-call | flops 3000000000 | bytes 3000000 | tf_op jit(solution)/shard_map/inner/pallas_call | solution.py:43
  12.8 0.0 collective-permute-done.3
  12.8 2.7 %collective-permute-start.7 = (f32[8,128]{1,0:T(8,128)S(1)}, f32[8,128]{1,0:T(8,128)S(1)}, u32[]{:S(2)}, u32[]{:S(2)}) collective-permute-start(f32[8,128]{1,0:T(8,128)S(1)} %add.3.rest_0_), channel_id=1, source_target_pairs={{0,8},{4,12},{8,0},{12,4},{1,9},{5,13},{9,1},{13,5},{2,10},{6,14},... | collective-permute-start | bytes 12296 | tf_op jit(solution)/shard_map/ppermute | solution.py:418
  15.4 1.3 %collective-permute-start.6 = (f32[8,128]{1,0:T(8,128)S(1)}, f32[8,128]{1,0:T(8,128)S(1)}, u32[]{:S(2)}, u32[]{:S(2)}) collective-permute-start(f32[8,128]{1,0:T(8,128)S(1)} %add.3.rest_0_), channel_id=1, source_target_pairs={{0,12},{4,8},{8,4},{12,0},{1,13},{5,9},{9,5},{13,1},{2,14},{6,10},... | collective-permute-start | bytes 12296 | tf_op jit(solution)/shard_map/ppermute | solution.py:418
  16.8 0.0 collective-permute-start.5
  16.8 0.0 collective-permute-done.halo_ref
  16.8 0.0 collective-permute-done.4
  16.8 4.1 %head.1 = (bf16[10,256,256]{2,1,0:T(8,128)(2,1)S(1)}, f32[8,256,128]{2,1,0:T(8,128)S(1)}, f32[1,128]{1,0:T(1,128)S(1)}, bf16[1152,256]{1,0:T(8,128)(2,1)S(1)}) custom-call(bf16[9,256,256]{2,1,0:T(8,128)(2,1)S(1)} %get-tuple-element.47.near_ref, bf16[7,256,256]{2,1,0:T(8,128)(2,1)S(1)} %inner.1.inner_ref, bf16[784,256]{1,0:T(8,128)(2,1)S(1)} %collective-permute-done.halo_ref, ...), custom_call_target="tpu_custom_call" | custom-call | flops 5000000000 | bytes 5000000 | tf_op jit(solution)/shard_map/head/pallas_call | solution.py:43
  20.9 0.0 collective-permute-done.7.rest_3_
  20.9 0.0 collective-permute-done.6.rest_2_
  20.9 0.0 collective-permute-done.5.rest_1_
  20.9 1.6 %back.1 = (bf16[6,336,256]{2,1,0:T(8,128)(2,1)S(1)}, bf16[6,256,128]{2,1,0:T(8,128)(2,1)S(1)}, bf16[8,256,128]{2,1,0:T(8,128)(2,1)S(1)}, f32[4,128]{1,0:T(4,128)S(1)}) custom-call(bf16[10,256,256]{2,1,0:T(8,128)(2,1)S(1)} %get-tuple-element.52.hid_ref, f32[8,256,128]{2,1,0:T(8,128)S(1)} %get-tuple-element.53.dz_ref, ...), custom_call_target="tpu_custom_call" | custom-call | flops 4000000000 | bytes 4000000 | tf_op jit(solution)/shard_map/back/pallas_call | solution.py:43
  22.6 0.1 collective-permute-start.8
  22.7 0.0 copy-start
  22.7 1.0 %cls.1 = (f32[896,128]{1,0:T(8,128)S(1)}, f32[896,128]{1,0:T(8,128)S(1)}) custom-call(bf16[10,256,256]{2,1,0:T(8,128)(2,1)S(1)} %get-tuple-element.52.hid_ref, bf16[6,336,256]{2,1,0:T(8,128)(2,1)S(1)} %get-tuple-element.60.dt_ref), custom_call_target="tpu_custom_call" | custom-call | flops 1500000000 | bytes 1500000 | tf_op jit(solution)/shard_map/cls/pallas_call | solution.py:43
  23.7 0.6 collective-permute-start.9
  24.2 0.4 collective-permute-done.8.other_ref
  24.6 3.0 %shared.1 = (f32[1152,128]{1,0:T(8,128)S(1)}, bf16[1152,128]{1,0:T(8,128)(2,1)S(1)}) custom-call(bf16[12,256,256]{2,1,0:T(8,128)(2,1)S(1)} %bitcast.13, bf16[784,256]{1,0:T(8,128)(2,1)S(1)} %collective-permute-done.halo_ref, bf16[6,256,128]{2,1,0:T(8,128)(2,1)S(1)} %get-tuple-element.56.own_ref, bf16[8,256,128]{2,1,0:T(8,128)(2,1)S(1)} %collective-permute-done.8.other_ref), custom_call_target="tpu_custom_call" | custom-call | flops 4000000000 | bytes 4000000 | tf_op jit(solution)/shard_map/shared/pallas_call | solution.py:43
  27.6 1.2 %collective-permute-start.10 = (bf16[1152,128]{1,0:T(8,128)(2,1)S(1)}, bf16[1152,128]{1,0:T(8,128)(2,1)S(1)}, u32[]{:S(2)}, u32[]{:S(2)}) collective-permute-start(bf16[1152,128]{1,0:T(8,128)(2,1)S(1)} %get-tuple-element.64), channel_id=1, source_target_pairs={{0,2},{2,0},{1,3},{3,1},{4,6},{6,4},{5,7},{7,5},{8,10},{10,8},{9,1... | collective-permute-start | bytes 884744 | tf_op jit(solution)/shard_map/ppermute | solution.py:418
  28.8 0.0 collective-permute-done.9.theirs_ref
  28.8 0.1 cls_split.1
  28.9 3.1 %collective-permute-start.11 = (bf16[240,128]{1,0:T(8,128)(2,1)S(1)}, bf16[240,128]{1,0:T(8,128)(2,1)S(1)}, u32[]{:S(2)}, u32[]{:S(2)}) collective-permute-start(bf16[240,128]{1,0:T(8,128)(2,1)S(1)} %get-tuple-element.65), channel_id=1, source_target_pairs={{0,8},{4,12},{8,0},{12,4},{1,9},{5,13},{9,1},{13,5},{2,10},{6,14},... | collective-permute-start | bytes 184328 | tf_op jit(solution)/shard_map/ppermute | solution.py:418
  32.0 1.3 %collective-permute-start.12 = (bf16[240,128]{1,0:T(8,128)(2,1)S(1)}, bf16[240,128]{1,0:T(8,128)(2,1)S(1)}, u32[]{:S(2)}, u32[]{:S(2)}) collective-permute-start(bf16[240,128]{1,0:T(8,128)(2,1)S(1)} %get-tuple-element.66), channel_id=1, source_target_pairs={{0,12},{4,8},{8,4},{12,0},{1,13},{5,9},{9,5},{13,1},{2,14},{6,10},... | collective-permute-start | bytes 184328 | tf_op jit(solution)/shard_map/ppermute | solution.py:418
  33.3 0.0 collective-permute-start.13
  33.3 3.5 %collective-permute-done.11.refs_1_ = bf16[240,128]{1,0:T(8,128)(2,1)S(1)} collective-permute-done((bf16[240,128]{1,0:T(8,128)(2,1)S(1)}, bf16[240,128]{1,0:T(8,128)(2,1)S(1)}, u32[]{:S(2)}, u32[]{:S(2)}) %collective-permute-start.11) | collective-permute-done | bytes 61472 | tf_op jit(solution)/shard_map/ppermute | solution.py:418
  36.8 1.4 %collective-permute-done.12.refs_2_ = bf16[240,128]{1,0:T(8,128)(2,1)S(1)} collective-permute-done((bf16[240,128]{1,0:T(8,128)(2,1)S(1)}, bf16[240,128]{1,0:T(8,128)(2,1)S(1)}, u32[]{:S(2)}, u32[]{:S(2)}) %collective-permute-start.12) | collective-permute-done | bytes 61472 | tf_op jit(solution)/shard_map/ppermute | solution.py:418
  38.1 0.0 collective-permute-done.13.refs_3_
  38.2 0.0 collective-permute-done.10.refs_0_
  38.2 0.1 sum.1
  38.3 1.6 %collective-permute-start.14 = (bf16[288,128]{1,0:T(8,128)(2,1)S(1)}, bf16[288,128]{1,0:T(8,128)(2,1)S(1)}, u32[]{:S(2)}, u32[]{:S(2)}) collective-permute-start(bf16[288,128]{1,0:T(8,128)(2,1)S(1)} %get-tuple-element.71), channel_id=1, source_target_pairs={{0,8},{4,12},{8,0},{12,4},{1,9},{5,13},{9,1},{13,5},{2,10},{6,14},... | collective-permute-start | bytes 221192 | tf_op jit(solution)/shard_map/ppermute | solution.py:418
  39.9 1.4 %collective-permute-start.15 = (bf16[288,128]{1,0:T(8,128)(2,1)S(1)}, bf16[288,128]{1,0:T(8,128)(2,1)S(1)}, u32[]{:S(2)}, u32[]{:S(2)}) collective-permute-start(bf16[288,128]{1,0:T(8,128)(2,1)S(1)} %get-tuple-element.72), channel_id=1, source_target_pairs={{0,12},{4,8},{8,4},{12,0},{1,13},{5,9},{9,5},{13,1},{2,14},{6,10},... | collective-permute-start | bytes 221192 | tf_op jit(solution)/shard_map/ppermute | solution.py:418
  41.3 0.5 collective-permute-start.16
  41.9 0.9 %collective-permute-start.17 = (bf16[128,128]{1,0:T(8,128)(2,1)S(1)}, bf16[128,128]{1,0:T(8,128)(2,1)S(1)}, u32[]{:S(2)}, u32[]{:S(2)}) collective-permute-start(bf16[128,128]{1,0:T(8,128)(2,1)S(1)} %get-tuple-element.74), channel_id=1, source_target_pairs={{0,2},{2,0},{1,3},{3,1},{4,6},{6,4},{5,7},{7,5},{8,10},{10,8},{9,1... | collective-permute-start | bytes 98312 | tf_op jit(solution)/shard_map/ppermute | solution.py:418
  42.8 3.0 %collective-permute-done.17.refs_3_ = bf16[128,128]{1,0:T(8,128)(2,1)S(1)} collective-permute-done((bf16[128,128]{1,0:T(8,128)(2,1)S(1)}, bf16[128,128]{1,0:T(8,128)(2,1)S(1)}, u32[]{:S(2)}, u32[]{:S(2)}) %collective-permute-start.17) | collective-permute-done | bytes 32800 | tf_op jit(solution)/shard_map/ppermute | solution.py:418
  45.8 0.0 collective-permute-done.14.refs_0_
  45.8 0.4 collective-permute-done.15.refs_1_
  46.2 0.6 collective-permute-done.16.refs_2_
  46.9 1.5 %collective-permute-start.21 = (bf16[288,128]{1,0:T(8,128)(2,1)S(1)}, bf16[288,128]{1,0:T(8,128)(2,1)S(1)}, u32[]{:S(2)}, u32[]{:S(2)}) collective-permute-start(bf16[288,128]{1,0:T(8,128)(2,1)S(1)} %get-tuple-element.76.refs_0_), channel_id=1, source_target_pairs={{0,8},{4,12},{8,0},{12,4},{1,9},{5,13},{9,1},{13,5},{2,10},{6,14},... | collective-permute-start | bytes 221192 | tf_op jit(solution)/shard_map/ppermute | solution.py:418
  48.4 1.5 %collective-permute-start.20 = (bf16[288,128]{1,0:T(8,128)(2,1)S(1)}, bf16[288,128]{1,0:T(8,128)(2,1)S(1)}, u32[]{:S(2)}, u32[]{:S(2)}) collective-permute-start(bf16[288,128]{1,0:T(8,128)(2,1)S(1)} %get-tuple-element.76.refs_0_), channel_id=1, source_target_pairs={{0,12},{4,8},{8,4},{12,0},{1,13},{5,9},{9,5},{13,1},{2,14},{6,10},... | collective-permute-start | bytes 221192 | tf_op jit(solution)/shard_map/ppermute | solution.py:418
  49.9 0.6 collective-permute-start.19
  50.5 0.9 %collective-permute-start.22 = (bf16[112,128]{1,0:T(8,128)(2,1)S(1)}, bf16[112,128]{1,0:T(8,128)(2,1)S(1)}, u32[]{:S(2)}, u32[]{:S(2)}) collective-permute-start(bf16[112,128]{1,0:T(8,128)(2,1)S(1)} %get-tuple-element.77.refs_4_), channel_id=1, source_target_pairs={{0,2},{2,0},{1,3},{3,1},{4,6},{6,4},{5,7},{7,5},{8,10},{10,8},{9,1... | collective-permute-start | bytes 86024 | tf_op jit(solution)/shard_map/ppermute | solution.py:418
  51.4 2.9 %collective-permute-done.22.refs_5_ = bf16[112,128]{1,0:T(8,128)(2,1)S(1)} collective-permute-done((bf16[112,128]{1,0:T(8,128)(2,1)S(1)}, bf16[112,128]{1,0:T(8,128)(2,1)S(1)}, u32[]{:S(2)}, u32[]{:S(2)}) %collective-permute-start.22) | collective-permute-done | bytes 28704 | tf_op jit(solution)/shard_map/ppermute | solution.py:418
  54.3 0.3 collective-permute-done.20.refs_2_
  54.7 0.4 collective-permute-done.19.refs_1_
  55.1 1.0 %collective-permute-start.23 = (bf16[1152,128]{1,0:T(8,128)(2,1)S(1)}, bf16[1152,128]{1,0:T(8,128)(2,1)S(1)}, u32[]{:S(2)}, u32[]{:S(2)}) collective-permute-start(bf16[1152,128]{1,0:T(8,128)(2,1)S(1)} %get-tuple-element.78.refs_0_), channel_id=1, source_target_pairs={{0,2},{2,0},{1,3},{3,1},{4,6},{6,4},{5,7},{7,5},{8,10},{10,8},{9,1... | collective-permute-start | bytes 884744 | tf_op jit(solution)/shard_map/ppermute | solution.py:418
  56.1 2.0 %collective-permute-start.26 = (bf16[224,128]{1,0:T(8,128)(2,1)S(1)}, bf16[224,128]{1,0:T(8,128)(2,1)S(1)}, u32[]{:S(2)}, u32[]{:S(2)}) collective-permute-start(bf16[224,128]{1,0:T(8,128)(2,1)S(1)} %get-tuple-element.79.refs_2_), channel_id=1, source_target_pairs={{0,8},{4,12},{8,0},{12,4},{1,9},{5,13},{9,1},{13,5},{2,10},{6,14},... | collective-permute-start | bytes 172040 | tf_op jit(solution)/shard_map/ppermute | solution.py:418
  58.1 1.4 %collective-permute-start.25 = (bf16[224,128]{1,0:T(8,128)(2,1)S(1)}, bf16[224,128]{1,0:T(8,128)(2,1)S(1)}, u32[]{:S(2)}, u32[]{:S(2)}) collective-permute-start(bf16[224,128]{1,0:T(8,128)(2,1)S(1)} %get-tuple-element.79.refs_2_), channel_id=1, source_target_pairs={{0,12},{4,8},{8,4},{12,0},{1,13},{5,9},{9,5},{13,1},{2,14},{6,10},... | collective-permute-start | bytes 172040 | tf_op jit(solution)/shard_map/ppermute | solution.py:418
  59.5 0.1 collective-permute-start.24
  59.6 0.0 collective-permute-start.18
  59.6 1.2 %collective-permute-done.18.theirs_ref = f32[4,128]{1,0:T(4,128)S(1)} collective-permute-done((f32[4,128]{1,0:T(4,128)S(1)}, f32[4,128]{1,0:T(4,128)S(1)}, u32[]{:S(2)}, u32[]{:S(2)}) %collective-permute-start.18) | collective-permute-done | bytes 2080 | tf_op jit(solution)/shard_map/ppermute | solution.py:418
  60.8 1.0 %collective-permute-done.26.refs_5_ = bf16[224,128]{1,0:T(8,128)(2,1)S(1)} collective-permute-done((bf16[224,128]{1,0:T(8,128)(2,1)S(1)}, bf16[224,128]{1,0:T(8,128)(2,1)S(1)}, u32[]{:S(2)}, u32[]{:S(2)}) %collective-permute-start.26) | collective-permute-done | bytes 57376 | tf_op jit(solution)/shard_map/ppermute | solution.py:418
  61.8 2.4 %collective-permute-done.25.refs_4_ = bf16[224,128]{1,0:T(8,128)(2,1)S(1)} collective-permute-done((bf16[224,128]{1,0:T(8,128)(2,1)S(1)}, bf16[224,128]{1,0:T(8,128)(2,1)S(1)}, u32[]{:S(2)}, u32[]{:S(2)}) %collective-permute-start.25) | collective-permute-done | bytes 57376 | tf_op jit(solution)/shard_map/ppermute | solution.py:418
  64.2 0.1 collective-permute-done.24.refs_3_
  64.3 1.3 %out.1 = (f32[2304,128]{1,0:T(8,128)}, f32[1,128]{1,0:T(1,128)}, f32[3,3,99,128]{3,2,1,0:T(8,128)}, f32[1,99]{1,0:T(1,128)}, f32[1,1]{1,0:T(1,128)}) custom-call(f32[4,128]{1,0:T(4,128)S(1)} %get-tuple-element.75.small_ref, f32[4,128]{1,0:T(4,128)S(1)} %collective-permute-done.18.theirs_ref, bf16[1152,128]{1,0:T(8,128)(2,1)S(1)} %get-tuple-element.78.refs_0_, ...), custom_call_target="tpu_custom_call" | custom-call | flops 1500000000 | bytes 1500000 | tf_op jit(solution)/shard_map/out/pallas_call | solution.py:43
  (14 shorter events, 0.1 us)
Async XLA Ops:
  0.6 9.7 %collective-permute-start.1 = (bf16[3,3,256,128]{3,2,1,0:T(8,128)(2,1)}, bf16[3,3,256,128]{3,2,1,0:T(8,128)(2,1)S(1)}, u32[]{:S(2)}, u32[]{:S(2)}) collective-permute-start(bf16[3,3,256,128]{3,2,1,0:T(8,128)(2,1)} %w1a_ref.3), channel_id=1, source_target_pairs={{0,1},{1,0},{2,3},{3,2},{4,5},{5,4},{6,7},{7,6},{8,9},{9,8},{10,11... | collective-permute-start | bytes 1769480 | tf_op jit(solution)/shard_map/ppermute | solution.py:418
  1.2 0.9 %copy-start.3 = (s32[1,12,2304]{2,0,1:T(1,128)S(1)}, s32[1,12,2304]{2,0,1:T(1,128)}, u32[]{:S(2)}) copy-start(s32[1,12,2304]{2,0,1:T(1,128)} %param.7) | copy-start | bytes 331780
  2.0 2.7 %copy-start.4 = (f32[128]{0:T(128)S(1)}, f32[128]{0:T(128)}, u32[]{:S(2)}) copy-start(f32[128]{0:T(128)} %param.9) | copy-start | bytes 1540
  2.0 6.7 %copy-start.2 = (bf16[3,3,128,99]{2,3,1,0:T(8,128)(2,1)S(1)}, bf16[3,3,128,99]{2,3,1,0:T(8,128)(2,1)}, u32[]{:S(2)}) copy-start(bf16[3,3,128,99]{2,3,1,0:T(8,128)(2,1)} %param.10) | copy-start | bytes 684292
  2.1 8.3 %copy-start.1 = (bf16[3,3,256,128]{3,2,1,0:T(8,128)(2,1)S(1)}, bf16[3,3,256,128]{3,2,1,0:T(8,128)(2,1)}, u32[]{:S(2)}) copy-start(bf16[3,3,256,128]{3,2,1,0:T(8,128)(2,1)} %w1a_ref.3) | copy-start | bytes 1769476
  4.1 12.7 %collective-permute-start = (bf16[784,256]{1,0:T(8,128)(2,1)S(1)}, bf16[784,256]{1,0:T(8,128)(2,1)S(1)}, u32[]{:S(2)}, u32[]{:S(2)}) collective-permute-start(bf16[784,256]{1,0:T(8,128)(2,1)S(1)} %get-tuple-element.45), channel_id=1, source_target_pairs={{1,4},{4,1},{5,8},{8,5},{9,12},{12,9},{3,6},{6,3},{7,10},{10,7},{1... | collective-permute-start | bytes 1204232 | tf_op jit(solution)/shard_map/ppermute | solution.py:461
  4.8 5.6 %collective-permute-start.2 = (f32[128]{0:T(128)S(1)}, f32[128]{0:T(128)S(1)}, u32[]{:S(2)}, u32[]{:S(2)}) collective-permute-start(f32[128]{0:T(128)S(1)} %copy-done.4), channel_id=1, source_target_pairs={{0,1},{1,0},{2,3},{3,2},{4,5},{5,4},{6,7},{7,6},{8,9},{9,8},{10,11... | collective-permute-start | bytes 1544 | tf_op jit(solution)/shard_map/ppermute | solution.py:418
  8.8 8.0 %collective-permute-start.4 = (bf16[3,3,128,99]{2,3,1,0:T(8,128)(2,1)S(1)}, bf16[3,3,128,99]{2,3,1,0:T(8,128)(2,1)S(1)}, u32[]{:S(2)}, u32[]{:S(2)}) collective-permute-start(bf16[3,3,128,99]{2,3,1,0:T(8,128)(2,1)S(1)} %copy-done.2), channel_id=1, source_target_pairs={{0,1},{1,0},{2,3},{3,2},{4,5},{5,4},{6,7},{7,6},{8,9},{9,8},{10,11... | collective-permute-start | bytes 684296 | tf_op jit(solution)/shard_map/ppermute | solution.py:418
  8.9 3.9 %collective-permute-start.3 = (f32[8,128]{1,0:T(8,128)S(1)}, f32[8,128]{1,0:T(8,128)S(1)}, u32[]{:S(2)}, u32[]{:S(2)}) collective-permute-start(f32[8,128]{1,0:T(8,128)S(1)} %get-tuple-element.46), channel_id=1, source_target_pairs={{0,2},{2,0},{1,3},{3,1},{4,6},{6,4},{5,7},{7,5},{8,10},{10,8},{9,1... | collective-permute-start | bytes 12296 | tf_op jit(solution)/shard_map/ppermute | solution.py:418
  10.4 6.4 %copy-start.5 = (f32[99]{0:T(128)S(1)}, f32[99]{0:T(128)}, u32[]{:S(2)}) copy-start(f32[99]{0:T(128)} %param.11) | copy-start | bytes 1192
  12.8 8.1 %collective-permute-start.7 = (f32[8,128]{1,0:T(8,128)S(1)}, f32[8,128]{1,0:T(8,128)S(1)}, u32[]{:S(2)}, u32[]{:S(2)}) collective-permute-start(f32[8,128]{1,0:T(8,128)S(1)} %add.3.rest_0_), channel_id=1, source_target_pairs={{0,8},{4,12},{8,0},{12,4},{1,9},{5,13},{9,1},{13,5},{2,10},{6,14},... | collective-permute-start | bytes 12296 | tf_op jit(solution)/shard_map/ppermute | solution.py:418
  15.4 5.5 %collective-permute-start.6 = (f32[8,128]{1,0:T(8,128)S(1)}, f32[8,128]{1,0:T(8,128)S(1)}, u32[]{:S(2)}, u32[]{:S(2)}) collective-permute-start(f32[8,128]{1,0:T(8,128)S(1)} %add.3.rest_0_), channel_id=1, source_target_pairs={{0,12},{4,8},{8,4},{12,0},{1,13},{5,9},{9,5},{13,1},{2,14},{6,10},... | collective-permute-start | bytes 12296 | tf_op jit(solution)/shard_map/ppermute | solution.py:418
  16.8 4.1 %collective-permute-start.5 = (f32[8,128]{1,0:T(8,128)S(1)}, f32[8,128]{1,0:T(8,128)S(1)}, u32[]{:S(2)}, u32[]{:S(2)}) collective-permute-start(f32[8,128]{1,0:T(8,128)S(1)} %add.3.rest_0_), channel_id=1, source_target_pairs={{0,4},{4,0},{8,12},{12,8},{1,5},{5,1},{9,13},{13,9},{2,6},{6,2},{1... | collective-permute-start | bytes 12296 | tf_op jit(solution)/shard_map/ppermute | solution.py:418
  22.6 2.0 %collective-permute-start.8 = (bf16[8,256,128]{2,1,0:T(8,128)(2,1)S(1)}, bf16[8,256,128]{2,1,0:T(8,128)(2,1)S(1)}, u32[]{:S(2)}, u32[]{:S(2)}) collective-permute-start(bf16[8,256,128]{2,1,0:T(8,128)(2,1)S(1)} %get-tuple-element.57), channel_id=1, source_target_pairs={{0,1},{1,0},{2,3},{3,2},{4,5},{5,4},{6,7},{7,6},{8,9},{9,8},{10,11... | collective-permute-start | bytes 1572872 | tf_op jit(solution)/shard_map/ppermute | solution.py:418
  22.7 1.9 %copy-start = (bf16[1,12,256,256]{3,2,1,0:T(8,128)(2,1)S(1)}, bf16[1,12,256,256]{3,2,1,0:T(8,128)(2,1)}, u32[]{:S(2)}) copy-start(bf16[1,12,256,256]{3,2,1,0:T(8,128)(2,1)} %param.6) | copy-start | bytes 4718596
  23.7 5.1 %collective-permute-start.9 = (f32[896,128]{1,0:T(8,128)S(1)}, f32[896,128]{1,0:T(8,128)S(1)}, u32[]{:S(2)}, u32[]{:S(2)}) collective-permute-start(f32[896,128]{1,0:T(8,128)S(1)} %get-tuple-element.62), channel_id=1, source_target_pairs={{0,1},{1,0},{2,3},{3,2},{4,5},{5,4},{6,7},{7,6},{8,9},{9,8},{10,11... | collective-permute-start | bytes 1376264 | tf_op jit(solution)/shard_map/ppermute | solution.py:418
  27.6 10.6 %collective-permute-start.10 = (bf16[1152,128]{1,0:T(8,128)(2,1)S(1)}, bf16[1152,128]{1,0:T(8,128)(2,1)S(1)}, u32[]{:S(2)}, u32[]{:S(2)}) collective-permute-start(bf16[1152,128]{1,0:T(8,128)(2,1)S(1)} %get-tuple-element.64), channel_id=1, source_target_pairs={{0,2},{2,0},{1,3},{3,1},{4,6},{6,4},{5,7},{7,5},{8,10},{10,8},{9,1... | collective-permute-start | bytes 884744 | tf_op jit(solution)/shard_map/ppermute | solution.py:418
  28.9 7.9 %collective-permute-start.11 = (bf16[240,128]{1,0:T(8,128)(2,1)S(1)}, bf16[240,128]{1,0:T(8,128)(2,1)S(1)}, u32[]{:S(2)}, u32[]{:S(2)}) collective-permute-start(bf16[240,128]{1,0:T(8,128)(2,1)S(1)} %get-tuple-element.65), channel_id=1, source_target_pairs={{0,8},{4,12},{8,0},{12,4},{1,9},{5,13},{9,1},{13,5},{2,10},{6,14},... | collective-permute-start | bytes 184328 | tf_op jit(solution)/shard_map/ppermute | solution.py:418
  32.0 6.2 %collective-permute-start.12 = (bf16[240,128]{1,0:T(8,128)(2,1)S(1)}, bf16[240,128]{1,0:T(8,128)(2,1)S(1)}, u32[]{:S(2)}, u32[]{:S(2)}) collective-permute-start(bf16[240,128]{1,0:T(8,128)(2,1)S(1)} %get-tuple-element.66), channel_id=1, source_target_pairs={{0,12},{4,8},{8,4},{12,0},{1,13},{5,9},{9,5},{13,1},{2,14},{6,10},... | collective-permute-start | bytes 184328 | tf_op jit(solution)/shard_map/ppermute | solution.py:418
  33.3 4.9 %collective-permute-start.13 = (bf16[240,128]{1,0:T(8,128)(2,1)S(1)}, bf16[240,128]{1,0:T(8,128)(2,1)S(1)}, u32[]{:S(2)}, u32[]{:S(2)}) collective-permute-start(bf16[240,128]{1,0:T(8,128)(2,1)S(1)} %get-tuple-element.67), channel_id=1, source_target_pairs={{0,4},{4,0},{8,12},{12,8},{1,5},{5,1},{9,13},{13,9},{2,6},{6,2},{1... | collective-permute-start | bytes 184328 | tf_op jit(solution)/shard_map/ppermute | solution.py:418
  38.3 7.5 %collective-permute-start.14 = (bf16[288,128]{1,0:T(8,128)(2,1)S(1)}, bf16[288,128]{1,0:T(8,128)(2,1)S(1)}, u32[]{:S(2)}, u32[]{:S(2)}) collective-permute-start(bf16[288,128]{1,0:T(8,128)(2,1)S(1)} %get-tuple-element.71), channel_id=1, source_target_pairs={{0,8},{4,12},{8,0},{12,4},{1,9},{5,13},{9,1},{13,5},{2,10},{6,14},... | collective-permute-start | bytes 221192 | tf_op jit(solution)/shard_map/ppermute | solution.py:418
  39.9 6.3 %collective-permute-start.15 = (bf16[288,128]{1,0:T(8,128)(2,1)S(1)}, bf16[288,128]{1,0:T(8,128)(2,1)S(1)}, u32[]{:S(2)}, u32[]{:S(2)}) collective-permute-start(bf16[288,128]{1,0:T(8,128)(2,1)S(1)} %get-tuple-element.72), channel_id=1, source_target_pairs={{0,12},{4,8},{8,4},{12,0},{1,13},{5,9},{9,5},{13,1},{2,14},{6,10},... | collective-permute-start | bytes 221192 | tf_op jit(solution)/shard_map/ppermute | solution.py:418
  41.3 5.5 %collective-permute-start.16 = (bf16[288,128]{1,0:T(8,128)(2,1)S(1)}, bf16[288,128]{1,0:T(8,128)(2,1)S(1)}, u32[]{:S(2)}, u32[]{:S(2)}) collective-permute-start(bf16[288,128]{1,0:T(8,128)(2,1)S(1)} %get-tuple-element.73), channel_id=1, source_target_pairs={{0,4},{4,0},{8,12},{12,8},{1,5},{5,1},{9,13},{13,9},{2,6},{6,2},{1... | collective-permute-start | bytes 221192 | tf_op jit(solution)/shard_map/ppermute | solution.py:418
  41.9 3.9 %collective-permute-start.17 = (bf16[128,128]{1,0:T(8,128)(2,1)S(1)}, bf16[128,128]{1,0:T(8,128)(2,1)S(1)}, u32[]{:S(2)}, u32[]{:S(2)}) collective-permute-start(bf16[128,128]{1,0:T(8,128)(2,1)S(1)} %get-tuple-element.74), channel_id=1, source_target_pairs={{0,2},{2,0},{1,3},{3,1},{4,6},{6,4},{5,7},{7,5},{8,10},{10,8},{9,1... | collective-permute-start | bytes 98312 | tf_op jit(solution)/shard_map/ppermute | solution.py:418
  46.9 7.4 %collective-permute-start.21 = (bf16[288,128]{1,0:T(8,128)(2,1)S(1)}, bf16[288,128]{1,0:T(8,128)(2,1)S(1)}, u32[]{:S(2)}, u32[]{:S(2)}) collective-permute-start(bf16[288,128]{1,0:T(8,128)(2,1)S(1)} %get-tuple-element.76.refs_0_), channel_id=1, source_target_pairs={{0,8},{4,12},{8,0},{12,4},{1,9},{5,13},{9,1},{13,5},{2,10},{6,14},... | collective-permute-start | bytes 221192 | tf_op jit(solution)/shard_map/ppermute | solution.py:418
  48.4 6.3 %collective-permute-start.20 = (bf16[288,128]{1,0:T(8,128)(2,1)S(1)}, bf16[288,128]{1,0:T(8,128)(2,1)S(1)}, u32[]{:S(2)}, u32[]{:S(2)}) collective-permute-start(bf16[288,128]{1,0:T(8,128)(2,1)S(1)} %get-tuple-element.76.refs_0_), channel_id=1, source_target_pairs={{0,12},{4,8},{8,4},{12,0},{1,13},{5,9},{9,5},{13,1},{2,14},{6,10},... | collective-permute-start | bytes 221192 | tf_op jit(solution)/shard_map/ppermute | solution.py:418
  49.9 5.1 %collective-permute-start.19 = (bf16[288,128]{1,0:T(8,128)(2,1)S(1)}, bf16[288,128]{1,0:T(8,128)(2,1)S(1)}, u32[]{:S(2)}, u32[]{:S(2)}) collective-permute-start(bf16[288,128]{1,0:T(8,128)(2,1)S(1)} %get-tuple-element.76.refs_0_), channel_id=1, source_target_pairs={{0,4},{4,0},{8,12},{12,8},{1,5},{5,1},{9,13},{13,9},{2,6},{6,2},{1... | collective-permute-start | bytes 221192 | tf_op jit(solution)/shard_map/ppermute | solution.py:418
  50.5 3.9 %collective-permute-start.22 = (bf16[112,128]{1,0:T(8,128)(2,1)S(1)}, bf16[112,128]{1,0:T(8,128)(2,1)S(1)}, u32[]{:S(2)}, u32[]{:S(2)}) collective-permute-start(bf16[112,128]{1,0:T(8,128)(2,1)S(1)} %get-tuple-element.77.refs_4_), channel_id=1, source_target_pairs={{0,2},{2,0},{1,3},{3,1},{4,6},{6,4},{5,7},{7,5},{8,10},{10,8},{9,1... | collective-permute-start | bytes 86024 | tf_op jit(solution)/shard_map/ppermute | solution.py:418
  55.1 9.2 %collective-permute-start.23 = (bf16[1152,128]{1,0:T(8,128)(2,1)S(1)}, bf16[1152,128]{1,0:T(8,128)(2,1)S(1)}, u32[]{:S(2)}, u32[]{:S(2)}) collective-permute-start(bf16[1152,128]{1,0:T(8,128)(2,1)S(1)} %get-tuple-element.78.refs_0_), channel_id=1, source_target_pairs={{0,2},{2,0},{1,3},{3,1},{4,6},{6,4},{5,7},{7,5},{8,10},{10,8},{9,1... | collective-permute-start | bytes 884744 | tf_op jit(solution)/shard_map/ppermute | solution.py:418
  56.1 5.7 %collective-permute-start.26 = (bf16[224,128]{1,0:T(8,128)(2,1)S(1)}, bf16[224,128]{1,0:T(8,128)(2,1)S(1)}, u32[]{:S(2)}, u32[]{:S(2)}) collective-permute-start(bf16[224,128]{1,0:T(8,128)(2,1)S(1)} %get-tuple-element.79.refs_2_), channel_id=1, source_target_pairs={{0,8},{4,12},{8,0},{12,4},{1,9},{5,13},{9,1},{13,5},{2,10},{6,14},... | collective-permute-start | bytes 172040 | tf_op jit(solution)/shard_map/ppermute | solution.py:418
  58.1 6.1 %collective-permute-start.25 = (bf16[224,128]{1,0:T(8,128)(2,1)S(1)}, bf16[224,128]{1,0:T(8,128)(2,1)S(1)}, u32[]{:S(2)}, u32[]{:S(2)}) collective-permute-start(bf16[224,128]{1,0:T(8,128)(2,1)S(1)} %get-tuple-element.79.refs_2_), channel_id=1, source_target_pairs={{0,12},{4,8},{8,4},{12,0},{1,13},{5,9},{9,5},{13,1},{2,14},{6,10},... | collective-permute-start | bytes 172040 | tf_op jit(solution)/shard_map/ppermute | solution.py:418
  59.5 4.8 %collective-permute-start.24 = (bf16[224,128]{1,0:T(8,128)(2,1)S(1)}, bf16[224,128]{1,0:T(8,128)(2,1)S(1)}, u32[]{:S(2)}, u32[]{:S(2)}) collective-permute-start(bf16[224,128]{1,0:T(8,128)(2,1)S(1)} %get-tuple-element.79.refs_2_), channel_id=1, source_target_pairs={{0,4},{4,0},{8,12},{12,8},{1,5},{5,1},{9,13},{13,9},{2,6},{6,2},{1... | collective-permute-start | bytes 172040 | tf_op jit(solution)/shard_map/ppermute | solution.py:418
  59.6 1.2 %collective-permute-start.18 = (f32[4,128]{1,0:T(4,128)S(1)}, f32[4,128]{1,0:T(4,128)S(1)}, u32[]{:S(2)}, u32[]{:S(2)}) collective-permute-start(f32[4,128]{1,0:T(4,128)S(1)} %get-tuple-element.75.small_ref), channel_id=1, source_target_pairs={{0,1},{1,0},{2,3},{3,2},{4,5},{5,4},{6,7},{7,6},{8,9},{9,8},{10,11... | collective-permute-start | bytes 6152 | tf_op jit(solution)/shard_map/ppermute | solution.py:418

commit v15 on v14

--- a/solution.py
+++ b/solution.py
@@ -287,14 +287,23 @@
     other_ref[9 * LOGITS :] = blank
 
 
-def partners(size):
-    return [2, 3, 1] if size == 4 else list(range(size - 1, 0, -1))
-
-
-def split(total, me, keep_ref, send_refs):
+def partners(size, core=0):
+    if size == 4:
+        return [3, 2, 1] if core else [2, 3, 1]
+    return list(range(size - 1, 0, -1))
+
+
+def partner_of(size, k, where_ref):
+    even, odd = partners(size)[k], partners(size, 1)[k]
+    return even if even == odd else jnp.where(where_ref[0] == 0, even, odd)
+
+
+def split(total, where_ref, slot, keep_ref, send_refs):
     rows = keep_ref.shape[0]
+    me = where_ref[slot]
     keep_ref[...] = total[pl.ds(pl.multiple_of(me * rows, 8), rows)]
-    for bit, ref in zip(partners(len(send_refs) + 1), send_refs):
+    for k, ref in enumerate(send_refs):
+        bit = partner_of(len(send_refs) + 1, k, where_ref)
         ref[0:rows] = total[pl.ds(pl.multiple_of((me ^ bit) * rows, 8), rows)].astype(BF16)
 
 
@@ -333,13 +342,13 @@
             g_ref[start : start + chans] = g[:, j * outs : (j + 1) * outs]
     if g_ref.shape[0] > 9 * chans:
         g_ref[9 * chans :] = jnp.zeros((g_ref.shape[0] - 9 * chans, outs), F32)
-    split(g_ref, where_ref[BATCH], keep_ref, send_refs)
+    split(g_ref, where_ref, BATCH, keep_ref, send_refs)
 
 
 def cls_split_kernel(where_ref, cls_ref, theirs_ref, small_ref, keep_ref, *rest):
     *send_refs, total_ref = rest
     total_ref[...] = cls_ref[...] + theirs_ref[...]
-    split(total_ref, where_ref[TILE], keep_ref, send_refs)
+    split(total_ref, where_ref, TILE, keep_ref, send_refs)
     for ref in send_refs:
         put_trio(ref, keep_ref.shape[0], small_ref[...])
 
@@ -368,9 +377,9 @@
     keep_ref, sum_ref, *refs, total_ref, cls_total_ref = refs
     send_refs, cls_keep_ref, cls_send_refs = refs[:n_send], refs[n_send], refs[n_send + 1 :]
     total_ref[...] = total_of(base_ref, in_refs)
-    split(total_ref, where_ref[TILE], keep_ref, send_refs)
+    split(total_ref, where_ref, TILE, keep_ref, send_refs)
     cls_total_ref[...] = total_of(cls_ref, cls_in_refs)
-    split(cls_total_ref, where_ref[BATCH], cls_keep_ref, cls_send_refs)
+    split(cls_total_ref, where_ref, BATCH, cls_keep_ref, cls_send_refs)
     sums = small_sum(small_ref, cls_in_refs, cls_ref.shape[0])
     sum_ref[...] = sums
     for ref in cls_send_refs:
@@ -385,26 +394,29 @@
     sum_ref[...] = small_sum(small_ref, cls_in_refs, cls_ref.shape[0])
 
 
-def join(me, in_refs, out_ref):
+def join(where_ref, slot, in_refs, out_ref):
     rows = in_refs[0].shape[0]
-    for bit, ref in zip([0] + partners(len(in_refs))[::-1], in_refs):
+    me = where_ref[slot]
+    size = len(in_refs)
+    for k, ref in enumerate(in_refs):
+        bit = partner_of(size, size - 1 - k, where_ref) if k else 0
         out_ref[pl.ds(pl.multiple_of((me ^ bit) * rows, 8), rows)] = ref[...].astype(out_ref.dtype)
 
 
 def join_kernel(n_in, where_ref, *refs):
-    join(where_ref[TILE], refs[:n_in], refs[-2])
-    join(where_ref[BATCH], refs[n_in:-2], refs[-1])
+    join(where_ref, TILE, refs[:n_in], refs[-2])
+    join(where_ref, BATCH, refs[n_in:-2], refs[-1])
 
 
 def out_kernel(n_in, n_cls, where_ref, small_ref, theirs_ref, *refs):
     in_refs, cls_in_refs, refs = refs[:n_in], refs[n_in : n_in + n_cls], refs[n_in + n_cls :]
     out_ref, bias_ref, cls_out_ref, cls_bias_ref, loss_ref, cls_whole_ref, *whole_ref = refs
     if whole_ref:
-        join(where_ref[BATCH], in_refs, whole_ref[0])
+        join(where_ref, BATCH, in_refs, whole_ref[0])
         out_ref[...] = whole_ref[0][: out_ref.shape[0]]
     else:
-        join(where_ref[BATCH], in_refs, out_ref)
-    join(where_ref[TILE], cls_in_refs, cls_whole_ref)
+        join(where_ref, BATCH, in_refs, out_ref)
+    join(where_ref, TILE, cls_in_refs, cls_whole_ref)
     for tap in range(9):
         cls_out_ref[tap // 3, tap % 3] = cls_whole_ref[LOGITS * tap : LOGITS * (tap + 1)]
     bias_ref[...] = small_ref[2:3] + theirs_ref[3:4]
@@ -418,12 +430,20 @@
     return lax.ppermute(x, axis, [(i, i ^ bit) for i in range(size)])
 
 
+def send(x, axis, k):
+    size, cores = lax.axis_size(axis), lax.axis_size("chan")
+    pairs = [
+        (i * cores + core, (i ^ partners(size, core % 2)[k]) * cores + core) for i in range(size) for core in range(cores)
+    ]
+    return lax.ppermute(x, (axis, "chan"), pairs)
+
+
 def others(x, axis):
-    return [swap(x, axis, bit) for bit in partners(lax.axis_size(axis))[::-1]]
+    return [send(x, axis, k) for k in reversed(range(lax.axis_size(axis) - 1))]
 
 
 def exchange(sends, axis):
-    return [swap(x, axis, bit) for bit, x in zip(partners(len(sends) + 1), sends)]
+    return [send(x, axis, k) for k, x in enumerate(sends)]
 
 
 def round_up(n, step):

time: 65.8 us -> 67 us (1.018)
  waiting for transfers between devices: 17.7 us -> 18.4 us
    ppermute x0 -> x20, starting transfers between devices: none -> 25 us  [send(): return lax.ppermute(x, (axis, 'chan'), pairs)]
    ppermute x26 -> x6, starting transfers between devices: 29.8 us -> 5.21 us  [swap(): return lax.ppermute(x, axis, [(i, i ^ bit) for i in range(size)])]
    ppermute x0 -> x20, waiting for transfers between devices: none -> 16.9 us  [send(): return lax.ppermute(x, (axis, 'chan'), pairs)]
    ppermute x26 -> x6, waiting for transfers between devices: 17.7 us -> 1.52 us  [swap(): return lax.ppermute(x, axis, [(i, i ^ bit) for i in range(size)])]
where the time goes in v15:
time: 67 us; the launch traced here: 66.8 us
  starting transfers between devices  30.9 us (46%)
  waiting for transfers between devices  18.4 us (27%)
  Pallas kernels  15.7 us (23%)
  local copies, waits for them, and re-layouts  0.92 us (1%)
  between operations  0.81 us (1%)
    ppermute x20, starting transfers between devices, send(): return lax.ppermute(x, (axis, 'chan'), pairs)  25 us
    ppermute x20, waiting for transfers between devices, send(): return lax.ppermute(x, (axis, 'chan'), pairs)  16.9 us
    pallas_call x11, Pallas kernels, call(): pl.pallas_call(functools.partial(kernel, inputs[0]), in_specs=(specs or [...  15.7 us
    ppermute x6, starting transfers between devices, swap(): return lax.ppermute(x, axis, [(i, i ^ bit) for i in range(size)])  5.21 us
    ppermute x6, waiting for transfers between devices, swap(): return lax.ppermute(x, axis, [(i, i ^ bit) for i in range(size)])  1.52 us
  transfers between devices with their start and end apart: 27, of which 13 were waited for; matrix products, arithmetic and copies ran while one was open for 0% of the time, Pallas kernels for 19%

profile of v15, /device:TPU:0, one launch (start us, length us, event | category | flops | bytes accessed | tf_op | source)
XLA Modules:
  0.0 66.8 jit_solution(1538035207884681582)
XLA Ops:
  0.6 0.5 collective-permute-start.1
  1.2 0.9 %copy-done.3 = s32[1,12,2304]{2,0,1:T(1,128)S(1)} copy-done((s32[1,12,2304]{2,0,1:T(1,128)S(1)}, s32[1,12,2304]{2,0,1:T(1,128)}, u32[]{:S(2)}) %copy-start.3) | copy-done | bytes 110616
  2.1 2.0 %edge.1 = (bf16[784,256]{1,0:T(8,128)(2,1)S(1)}, bf16[12,16,256]{2,1,0:T(8,128)(2,1)S(1)}, f32[8,128]{1,0:T(8,128)S(1)}, bf16[9,256,256]{2,1,0:T(8,128)(2,1)S(1)}) custom-call(bf16[12,256,256]{2,1,0:T(8,128)(2,1)} %bitcast.12, s32[12,1,2304]{2,1,0:T(1,128)S(1)} %bitcast.16), custom_call_target="tpu_custom_call" | custom-call | flops 2000000000 | bytes 2000000 | tf_op jit(solution)/shard_map/edge/pallas_call | solution.py:43
  4.1 0.7 %collective-permute-start = (bf16[784,256]{1,0:T(8,128)(2,1)S(1)}, bf16[784,256]{1,0:T(8,128)(2,1)S(1)}, u32[]{:S(2)}, u32[]{:S(2)}) collective-permute-start(bf16[784,256]{1,0:T(8,128)(2,1)S(1)} %get-tuple-element.45), channel_id=1, source_target_pairs={{1,4},{4,1},{5,8},{8,5},{9,12},{12,9},{3,6},{6,3},{7,10},{10,7},{1... | collective-permute-start | bytes 1204232 | tf_op jit(solution)/shard_map/ppermute | solution.py:481
  4.8 4.0 %collective-permute-start.2 = (f32[128]{0:T(128)S(1)}, f32[128]{0:T(128)S(1)}, u32[]{:S(2)}, u32[]{:S(2)}) collective-permute-start(f32[128]{0:T(128)S(1)} %copy-done.4), channel_id=1, source_target_pairs={{0,1},{1,0},{2,3},{3,2},{4,5},{5,4},{6,7},{7,6},{8,9},{9,8},{10,11... | collective-permute-start | bytes 1544 | tf_op jit(solution)/shard_map/ppermute | solution.py:430
  8.8 0.1 collective-permute-start.4
  8.9 1.5 %collective-permute-start.3 = (f32[8,128]{1,0:T(8,128)S(1)}, f32[8,128]{1,0:T(8,128)S(1)}, u32[]{:S(2)}, u32[]{:S(2)}) collective-permute-start(f32[8,128]{1,0:T(8,128)S(1)} %get-tuple-element.46), channel_id=1, source_target_pairs={{0,2},{1,3},{2,0},{3,1},{4,6},{5,7},{6,4},{7,5},{8,10},{9,11},{10,... | collective-permute-start | bytes 12296 | tf_op jit(solution)/shard_map/ppermute | solution.py:438
  10.4 0.0 collective-permute-done.2
  10.4 0.0 collective-permute-done.1.w1b_ref
  10.4 0.0 copy-start.5
  10.4 2.4 %inner.1.inner_ref = bf16[7,256,256]{2,1,0:T(8,128)(2,1)S(1)} custom-call(bf16[9,256,256]{2,1,0:T(8,128)(2,1)S(1)} %get-tuple-element.47.near_ref, bf16[3,3,256,128]{3,2,1,0:T(8,128)(2,1)S(1)} %copy-done.1, bf16[3,3,256,128]{3,2,1,0:T(8,128)(2,1)S(1)} %collective-permute-done.1.w1b_ref, f32[1,128]{1,0:T(1,128)S(1)} %bitcast.17, f32[1,128]{1,0:T(1,128)S(1)} %bitcast.20), custom_call_target="tpu_custom_call" | custom-call | flops 3000000000 | bytes 3000000 | tf_op jit(solution)/shard_map/inner/pallas_call | solution.py:43
  12.8 0.0 collective-permute-done.3
  12.8 2.7 %collective-permute-start.7 = (f32[8,128]{1,0:T(8,128)S(1)}, f32[8,128]{1,0:T(8,128)S(1)}, u32[]{:S(2)}, u32[]{:S(2)}) collective-permute-start(f32[8,128]{1,0:T(8,128)S(1)} %add.3.rest_0_), channel_id=1, source_target_pairs={{0,8},{1,13},{4,12},{5,9},{8,0},{9,5},{12,4},{13,1},{2,10},{3,15},... | collective-permute-start | bytes 12296 | tf_op jit(solution)/shard_map/ppermute | solution.py:438
  15.4 1.3 %collective-permute-start.6 = (f32[8,128]{1,0:T(8,128)S(1)}, f32[8,128]{1,0:T(8,128)S(1)}, u32[]{:S(2)}, u32[]{:S(2)}) collective-permute-start(f32[8,128]{1,0:T(8,128)S(1)} %add.3.rest_0_), channel_id=1, source_target_pairs={{0,12},{1,9},{4,8},{5,13},{8,4},{9,1},{12,0},{13,5},{2,14},{3,11},... | collective-permute-start | bytes 12296 | tf_op jit(solution)/shard_map/ppermute | solution.py:438
  16.8 0.0 collective-permute-start.5
  16.8 0.0 collective-permute-done.halo_ref
  16.8 0.0 collective-permute-done.4
  16.8 4.1 %head.1 = (bf16[10,256,256]{2,1,0:T(8,128)(2,1)S(1)}, f32[8,256,128]{2,1,0:T(8,128)S(1)}, f32[1,128]{1,0:T(1,128)S(1)}, bf16[1152,256]{1,0:T(8,128)(2,1)S(1)}) custom-call(bf16[9,256,256]{2,1,0:T(8,128)(2,1)S(1)} %get-tuple-element.47.near_ref, bf16[7,256,256]{2,1,0:T(8,128)(2,1)S(1)} %inner.1.inner_ref, bf16[784,256]{1,0:T(8,128)(2,1)S(1)} %collective-permute-done.halo_ref, ...), custom_call_target="tpu_custom_call" | custom-call | flops 5000000000 | bytes 5000000 | tf_op jit(solution)/shard_map/head/pallas_call | solution.py:43
  20.9 0.0 collective-permute-done.7.rest_3_
  20.9 0.0 collective-permute-done.6.rest_2_
  20.9 0.0 collective-permute-done.5.rest_1_
  20.9 1.6 %back.1 = (bf16[6,336,256]{2,1,0:T(8,128)(2,1)S(1)}, bf16[6,256,128]{2,1,0:T(8,128)(2,1)S(1)}, bf16[8,256,128]{2,1,0:T(8,128)(2,1)S(1)}, f32[4,128]{1,0:T(4,128)S(1)}) custom-call(bf16[10,256,256]{2,1,0:T(8,128)(2,1)S(1)} %get-tuple-element.52.hid_ref, f32[8,256,128]{2,1,0:T(8,128)S(1)} %get-tuple-element.53.dz_ref, ...), custom_call_target="tpu_custom_call" | custom-call | flops 4000000000 | bytes 4000000 | tf_op jit(solution)/shard_map/back/pallas_call | solution.py:43
  22.6 0.1 collective-permute-start.8
  22.7 0.0 copy-start
  22.7 1.0 %cls.1 = (f32[896,128]{1,0:T(8,128)S(1)}, f32[896,128]{1,0:T(8,128)S(1)}) custom-call(bf16[10,256,256]{2,1,0:T(8,128)(2,1)S(1)} %get-tuple-element.52.hid_ref, bf16[6,336,256]{2,1,0:T(8,128)(2,1)S(1)} %get-tuple-element.60.dt_ref), custom_call_target="tpu_custom_call" | custom-call | flops 1500000000 | bytes 1500000 | tf_op jit(solution)/shard_map/cls/pallas_call | solution.py:43
  23.7 0.6 collective-permute-start.9
  24.2 0.4 collective-permute-done.8.other_ref
  24.6 3.0 %shared.1 = (f32[1152,128]{1,0:T(8,128)S(1)}, bf16[1152,128]{1,0:T(8,128)(2,1)S(1)}) custom-call(bf16[12,256,256]{2,1,0:T(8,128)(2,1)S(1)} %bitcast.13, bf16[784,256]{1,0:T(8,128)(2,1)S(1)} %collective-permute-done.halo_ref, bf16[6,256,128]{2,1,0:T(8,128)(2,1)S(1)} %get-tuple-element.56.own_ref, bf16[8,256,128]{2,1,0:T(8,128)(2,1)S(1)} %collective-permute-done.8.other_ref), custom_call_target="tpu_custom_call" | custom-call | flops 4000000000 | bytes 4000000 | tf_op jit(solution)/shard_map/shared/pallas_call | solution.py:43
  27.6 1.2 %collective-permute-start.10 = (bf16[1152,128]{1,0:T(8,128)(2,1)S(1)}, bf16[1152,128]{1,0:T(8,128)(2,1)S(1)}, u32[]{:S(2)}, u32[]{:S(2)}) collective-permute-start(bf16[1152,128]{1,0:T(8,128)(2,1)S(1)} %get-tuple-element.64), channel_id=1, source_target_pairs={{0,2},{1,3},{2,0},{3,1},{4,6},{5,7},{6,4},{7,5},{8,10},{9,11},{10,... | collective-permute-start | bytes 884744 | tf_op jit(solution)/shard_map/ppermute | solution.py:438
  28.8 0.0 collective-permute-done.9.theirs_ref
  28.8 0.1 cls_split.1
  28.9 3.1 %collective-permute-start.11 = (bf16[240,128]{1,0:T(8,128)(2,1)S(1)}, bf16[240,128]{1,0:T(8,128)(2,1)S(1)}, u32[]{:S(2)}, u32[]{:S(2)}) collective-permute-start(bf16[240,128]{1,0:T(8,128)(2,1)S(1)} %get-tuple-element.65), channel_id=1, source_target_pairs={{0,8},{1,13},{4,12},{5,9},{8,0},{9,5},{12,4},{13,1},{2,10},{3,15},... | collective-permute-start | bytes 184328 | tf_op jit(solution)/shard_map/ppermute | solution.py:438
  32.0 1.3 %collective-permute-start.12 = (bf16[240,128]{1,0:T(8,128)(2,1)S(1)}, bf16[240,128]{1,0:T(8,128)(2,1)S(1)}, u32[]{:S(2)}, u32[]{:S(2)}) collective-permute-start(bf16[240,128]{1,0:T(8,128)(2,1)S(1)} %get-tuple-element.66), channel_id=1, source_target_pairs={{0,12},{1,9},{4,8},{5,13},{8,4},{9,1},{12,0},{13,5},{2,14},{3,11},... | collective-permute-start | bytes 184328 | tf_op jit(solution)/shard_map/ppermute | solution.py:438
  33.3 0.0 collective-permute-start.13
  33.3 3.1 %collective-permute-done.11.refs_1_ = bf16[240,128]{1,0:T(8,128)(2,1)S(1)} collective-permute-done((bf16[240,128]{1,0:T(8,128)(2,1)S(1)}, bf16[240,128]{1,0:T(8,128)(2,1)S(1)}, u32[]{:S(2)}, u32[]{:S(2)}) %collective-permute-start.11) | collective-permute-done | bytes 61472 | tf_op jit(solution)/shard_map/ppermute | solution.py:438
  36.5 1.7 %collective-permute-done.12.refs_2_ = bf16[240,128]{1,0:T(8,128)(2,1)S(1)} collective-permute-done((bf16[240,128]{1,0:T(8,128)(2,1)S(1)}, bf16[240,128]{1,0:T(8,128)(2,1)S(1)}, u32[]{:S(2)}, u32[]{:S(2)}) %collective-permute-start.12) | collective-permute-done | bytes 61472 | tf_op jit(solution)/shard_map/ppermute | solution.py:438
  38.1 0.2 collective-permute-done.13.refs_3_
  38.3 0.0 collective-permute-done.10.refs_0_
  38.3 0.1 sum.1
  38.5 1.5 %collective-permute-start.14 = (bf16[288,128]{1,0:T(8,128)(2,1)S(1)}, bf16[288,128]{1,0:T(8,128)(2,1)S(1)}, u32[]{:S(2)}, u32[]{:S(2)}) collective-permute-start(bf16[288,128]{1,0:T(8,128)(2,1)S(1)} %get-tuple-element.71), channel_id=1, source_target_pairs={{0,8},{1,13},{4,12},{5,9},{8,0},{9,5},{12,4},{13,1},{2,10},{3,15},... | collective-permute-start | bytes 221192 | tf_op jit(solution)/shard_map/ppermute | solution.py:438
  39.9 1.3 %collective-permute-start.15 = (bf16[288,128]{1,0:T(8,128)(2,1)S(1)}, bf16[288,128]{1,0:T(8,128)(2,1)S(1)}, u32[]{:S(2)}, u32[]{:S(2)}) collective-permute-start(bf16[288,128]{1,0:T(8,128)(2,1)S(1)} %get-tuple-element.72), channel_id=1, source_target_pairs={{0,12},{1,9},{4,8},{5,13},{8,4},{9,1},{12,0},{13,5},{2,14},{3,11},... | collective-permute-start | bytes 221192 | tf_op jit(solution)/shard_map/ppermute | solution.py:438
  41.3 0.7 %collective-permute-start.16 = (bf16[288,128]{1,0:T(8,128)(2,1)S(1)}, bf16[288,128]{1,0:T(8,128)(2,1)S(1)}, u32[]{:S(2)}, u32[]{:S(2)}) collective-permute-start(bf16[288,128]{1,0:T(8,128)(2,1)S(1)} %get-tuple-element.73), channel_id=1, source_target_pairs={{0,4},{1,5},{4,0},{5,1},{8,12},{9,13},{12,8},{13,9},{2,6},{3,7},{6... | collective-permute-start | bytes 221192 | tf_op jit(solution)/shard_map/ppermute | solution.py:438
  42.0 0.9 %collective-permute-start.17 = (bf16[128,128]{1,0:T(8,128)(2,1)S(1)}, bf16[128,128]{1,0:T(8,128)(2,1)S(1)}, u32[]{:S(2)}, u32[]{:S(2)}) collective-permute-start(bf16[128,128]{1,0:T(8,128)(2,1)S(1)} %get-tuple-element.74), channel_id=1, source_target_pairs={{0,2},{1,3},{2,0},{3,1},{4,6},{5,7},{6,4},{7,5},{8,10},{9,11},{10,... | collective-permute-start | bytes 98312 | tf_op jit(solution)/shard_map/ppermute | solution.py:438
  42.9 3.0 %collective-permute-done.17.refs_3_ = bf16[128,128]{1,0:T(8,128)(2,1)S(1)} collective-permute-done((bf16[128,128]{1,0:T(8,128)(2,1)S(1)}, bf16[128,128]{1,0:T(8,128)(2,1)S(1)}, u32[]{:S(2)}, u32[]{:S(2)}) %collective-permute-start.17) | collective-permute-done | bytes 32800 | tf_op jit(solution)/shard_map/ppermute | solution.py:438
  45.9 0.5 collective-permute-done.14.refs_0_
  46.4 0.0 collective-permute-done.15.refs_1_
  46.4 0.7 %collective-permute-done.16.refs_2_ = bf16[288,128]{1,0:T(8,128)(2,1)S(1)} collective-permute-done((bf16[288,128]{1,0:T(8,128)(2,1)S(1)}, bf16[288,128]{1,0:T(8,128)(2,1)S(1)}, u32[]{:S(2)}, u32[]{:S(2)}) %collective-permute-start.16) | collective-permute-done | bytes 73760 | tf_op jit(solution)/shard_map/ppermute | solution.py:438
  47.2 1.7 %collective-permute-start.21 = (bf16[288,128]{1,0:T(8,128)(2,1)S(1)}, bf16[288,128]{1,0:T(8,128)(2,1)S(1)}, u32[]{:S(2)}, u32[]{:S(2)}) collective-permute-start(bf16[288,128]{1,0:T(8,128)(2,1)S(1)} %get-tuple-element.76.refs_0_), channel_id=1, source_target_pairs={{0,8},{1,13},{4,12},{5,9},{8,0},{9,5},{12,4},{13,1},{2,10},{3,15},... | collective-permute-start | bytes 221192 | tf_op jit(solution)/shard_map/ppermute | solution.py:438
  48.9 1.3 %collective-permute-start.20 = (bf16[288,128]{1,0:T(8,128)(2,1)S(1)}, bf16[288,128]{1,0:T(8,128)(2,1)S(1)}, u32[]{:S(2)}, u32[]{:S(2)}) collective-permute-start(bf16[288,128]{1,0:T(8,128)(2,1)S(1)} %get-tuple-element.76.refs_0_), channel_id=1, source_target_pairs={{0,12},{1,9},{4,8},{5,13},{8,4},{9,1},{12,0},{13,5},{2,14},{3,11},... | collective-permute-start | bytes 221192 | tf_op jit(solution)/shard_map/ppermute | solution.py:438
  50.2 0.6 collective-permute-start.19
  50.8 1.2 %collective-permute-start.22 = (bf16[112,128]{1,0:T(8,128)(2,1)S(1)}, bf16[112,128]{1,0:T(8,128)(2,1)S(1)}, u32[]{:S(2)}, u32[]{:S(2)}) collective-permute-start(bf16[112,128]{1,0:T(8,128)(2,1)S(1)} %get-tuple-element.77.refs_4_), channel_id=1, source_target_pairs={{0,2},{1,3},{2,0},{3,1},{4,6},{5,7},{6,4},{7,5},{8,10},{9,11},{10,... | collective-permute-start | bytes 86024 | tf_op jit(solution)/shard_map/ppermute | solution.py:438
  51.9 2.7 %collective-permute-done.22.refs_5_ = bf16[112,128]{1,0:T(8,128)(2,1)S(1)} collective-permute-done((bf16[112,128]{1,0:T(8,128)(2,1)S(1)}, bf16[112,128]{1,0:T(8,128)(2,1)S(1)}, u32[]{:S(2)}, u32[]{:S(2)}) %collective-permute-start.22) | collective-permute-done | bytes 28704 | tf_op jit(solution)/shard_map/ppermute | solution.py:438
  54.6 1.2 %collective-permute-done.21.refs_3_ = bf16[288,128]{1,0:T(8,128)(2,1)S(1)} collective-permute-done((bf16[288,128]{1,0:T(8,128)(2,1)S(1)}, bf16[288,128]{1,0:T(8,128)(2,1)S(1)}, u32[]{:S(2)}, u32[]{:S(2)}) %collective-permute-start.21) | collective-permute-done | bytes 73760 | tf_op jit(solution)/shard_map/ppermute | solution.py:438
  55.8 0.0 collective-permute-done.20.refs_2_
  55.8 0.7 %collective-permute-done.19.refs_1_ = bf16[288,128]{1,0:T(8,128)(2,1)S(1)} collective-permute-done((bf16[288,128]{1,0:T(8,128)(2,1)S(1)}, bf16[288,128]{1,0:T(8,128)(2,1)S(1)}, u32[]{:S(2)}, u32[]{:S(2)}) %collective-permute-start.19) | collective-permute-done | bytes 73760 | tf_op jit(solution)/shard_map/ppermute | solution.py:438
  56.5 1.2 %collective-permute-start.23 = (bf16[1152,128]{1,0:T(8,128)(2,1)S(1)}, bf16[1152,128]{1,0:T(8,128)(2,1)S(1)}, u32[]{:S(2)}, u32[]{:S(2)}) collective-permute-start(bf16[1152,128]{1,0:T(8,128)(2,1)S(1)} %get-tuple-element.78.refs_0_), channel_id=1, source_target_pairs={{0,2},{1,3},{2,0},{3,1},{4,6},{5,7},{6,4},{7,5},{8,10},{9,11},{10,... | collective-permute-start | bytes 884744 | tf_op jit(solution)/shard_map/ppermute | solution.py:438
  57.8 0.5 collective-permute-start.26
  58.2 2.5 %collective-permute-start.25 = (bf16[224,128]{1,0:T(8,128)(2,1)S(1)}, bf16[224,128]{1,0:T(8,128)(2,1)S(1)}, u32[]{:S(2)}, u32[]{:S(2)}) collective-permute-start(bf16[224,128]{1,0:T(8,128)(2,1)S(1)} %get-tuple-element.79.refs_2_), channel_id=1, source_target_pairs={{0,12},{1,9},{4,8},{5,13},{8,4},{9,1},{12,0},{13,5},{2,14},{3,11},... | collective-permute-start | bytes 172040 | tf_op jit(solution)/shard_map/ppermute | solution.py:438
  60.7 0.5 collective-permute-start.24
  61.2 1.2 %collective-permute-done.18.theirs_ref = f32[4,128]{1,0:T(4,128)S(1)} collective-permute-done((f32[4,128]{1,0:T(4,128)S(1)}, f32[4,128]{1,0:T(4,128)S(1)}, u32[]{:S(2)}, u32[]{:S(2)}) %collective-permute-start.18) | collective-permute-done | bytes 2080 | tf_op jit(solution)/shard_map/ppermute | solution.py:430
  62.4 2.5 %collective-permute-done.26.refs_5_ = bf16[224,128]{1,0:T(8,128)(2,1)S(1)} collective-permute-done((bf16[224,128]{1,0:T(8,128)(2,1)S(1)}, bf16[224,128]{1,0:T(8,128)(2,1)S(1)}, u32[]{:S(2)}, u32[]{:S(2)}) %collective-permute-start.26) | collective-permute-done | bytes 57376 | tf_op jit(solution)/shard_map/ppermute | solution.py:438
  64.9 0.6 collective-permute-done.24.refs_3_
  65.5 0.0 collective-permute-done.23.refs_1_
  65.5 1.3 %out.1 = (f32[2304,128]{1,0:T(8,128)}, f32[1,128]{1,0:T(1,128)}, f32[3,3,99,128]{3,2,1,0:T(8,128)}, f32[1,99]{1,0:T(1,128)}, f32[1,1]{1,0:T(1,128)}) custom-call(f32[4,128]{1,0:T(4,128)S(1)} %get-tuple-element.75.small_ref, f32[4,128]{1,0:T(4,128)S(1)} %collective-permute-done.18.theirs_ref, bf16[1152,128]{1,0:T(8,128)(2,1)S(1)} %get-tuple-element.78.refs_0_, ...), custom_call_target="tpu_custom_call" | custom-call | flops 1500000000 | bytes 1500000 | tf_op jit(solution)/shard_map/out/pallas_call | solution.py:43
  (14 shorter events, 0.1 us)
Async XLA Ops:
  0.6 9.7 %collective-permute-start.1 = (bf16[3,3,256,128]{3,2,1,0:T(8,128)(2,1)}, bf16[3,3,256,128]{3,2,1,0:T(8,128)(2,1)S(1)}, u32[]{:S(2)}, u32[]{:S(2)}) collective-permute-start(bf16[3,3,256,128]{3,2,1,0:T(8,128)(2,1)} %w1a_ref.3), channel_id=1, source_target_pairs={{0,1},{1,0},{2,3},{3,2},{4,5},{5,4},{6,7},{7,6},{8,9},{9,8},{10,11... | collective-permute-start | bytes 1769480 | tf_op jit(solution)/shard_map/ppermute | solution.py:430
  1.2 0.9 %copy-start.3 = (s32[1,12,2304]{2,0,1:T(1,128)S(1)}, s32[1,12,2304]{2,0,1:T(1,128)}, u32[]{:S(2)}) copy-start(s32[1,12,2304]{2,0,1:T(1,128)} %param.7) | copy-start | bytes 331780
  2.0 2.7 %copy-start.4 = (f32[128]{0:T(128)S(1)}, f32[128]{0:T(128)}, u32[]{:S(2)}) copy-start(f32[128]{0:T(128)} %param.9) | copy-start | bytes 1540
  2.0 6.7 %copy-start.2 = (bf16[3,3,128,99]{2,3,1,0:T(8,128)(2,1)S(1)}, bf16[3,3,128,99]{2,3,1,0:T(8,128)(2,1)}, u32[]{:S(2)}) copy-start(bf16[3,3,128,99]{2,3,1,0:T(8,128)(2,1)} %param.10) | copy-start | bytes 684292
  2.1 8.3 %copy-start.1 = (bf16[3,3,256,128]{3,2,1,0:T(8,128)(2,1)S(1)}, bf16[3,3,256,128]{3,2,1,0:T(8,128)(2,1)}, u32[]{:S(2)}) copy-start(bf16[3,3,256,128]{3,2,1,0:T(8,128)(2,1)} %w1a_ref.3) | copy-start | bytes 1769476
  4.1 12.7 %collective-permute-start = (bf16[784,256]{1,0:T(8,128)(2,1)S(1)}, bf16[784,256]{1,0:T(8,128)(2,1)S(1)}, u32[]{:S(2)}, u32[]{:S(2)}) collective-permute-start(bf16[784,256]{1,0:T(8,128)(2,1)S(1)} %get-tuple-element.45), channel_id=1, source_target_pairs={{1,4},{4,1},{5,8},{8,5},{9,12},{12,9},{3,6},{6,3},{7,10},{10,7},{1... | collective-permute-start | bytes 1204232 | tf_op jit(solution)/shard_map/ppermute | solution.py:481
  4.8 5.6 %collective-permute-start.2 = (f32[128]{0:T(128)S(1)}, f32[128]{0:T(128)S(1)}, u32[]{:S(2)}, u32[]{:S(2)}) collective-permute-start(f32[128]{0:T(128)S(1)} %copy-done.4), channel_id=1, source_target_pairs={{0,1},{1,0},{2,3},{3,2},{4,5},{5,4},{6,7},{7,6},{8,9},{9,8},{10,11... | collective-permute-start | bytes 1544 | tf_op jit(solution)/shard_map/ppermute | solution.py:430
  8.8 8.0 %collective-permute-start.4 = (bf16[3,3,128,99]{2,3,1,0:T(8,128)(2,1)S(1)}, bf16[3,3,128,99]{2,3,1,0:T(8,128)(2,1)S(1)}, u32[]{:S(2)}, u32[]{:S(2)}) collective-permute-start(bf16[3,3,128,99]{2,3,1,0:T(8,128)(2,1)S(1)} %copy-done.2), channel_id=1, source_target_pairs={{0,1},{1,0},{2,3},{3,2},{4,5},{5,4},{6,7},{7,6},{8,9},{9,8},{10,11... | collective-permute-start | bytes 684296 | tf_op jit(solution)/shard_map/ppermute | solution.py:430
  8.9 3.9 %collective-permute-start.3 = (f32[8,128]{1,0:T(8,128)S(1)}, f32[8,128]{1,0:T(8,128)S(1)}, u32[]{:S(2)}, u32[]{:S(2)}) collective-permute-start(f32[8,128]{1,0:T(8,128)S(1)} %get-tuple-element.46), channel_id=1, source_target_pairs={{0,2},{1,3},{2,0},{3,1},{4,6},{5,7},{6,4},{7,5},{8,10},{9,11},{10,... | collective-permute-start | bytes 12296 | tf_op jit(solution)/shard_map/ppermute | solution.py:438
  10.4 6.4 %copy-start.5 = (f32[99]{0:T(128)S(1)}, f32[99]{0:T(128)}, u32[]{:S(2)}) copy-start(f32[99]{0:T(128)} %param.11) | copy-start | bytes 1192
  12.8 8.1 %collective-permute-start.7 = (f32[8,128]{1,0:T(8,128)S(1)}, f32[8,128]{1,0:T(8,128)S(1)}, u32[]{:S(2)}, u32[]{:S(2)}) collective-permute-start(f32[8,128]{1,0:T(8,128)S(1)} %add.3.rest_0_), channel_id=1, source_target_pairs={{0,8},{1,13},{4,12},{5,9},{8,0},{9,5},{12,4},{13,1},{2,10},{3,15},... | collective-permute-start | bytes 12296 | tf_op jit(solution)/shard_map/ppermute | solution.py:438
  15.4 5.5 %collective-permute-start.6 = (f32[8,128]{1,0:T(8,128)S(1)}, f32[8,128]{1,0:T(8,128)S(1)}, u32[]{:S(2)}, u32[]{:S(2)}) collective-permute-start(f32[8,128]{1,0:T(8,128)S(1)} %add.3.rest_0_), channel_id=1, source_target_pairs={{0,12},{1,9},{4,8},{5,13},{8,4},{9,1},{12,0},{13,5},{2,14},{3,11},... | collective-permute-start | bytes 12296 | tf_op jit(solution)/shard_map/ppermute | solution.py:438
  16.8 4.1 %collective-permute-start.5 = (f32[8,128]{1,0:T(8,128)S(1)}, f32[8,128]{1,0:T(8,128)S(1)}, u32[]{:S(2)}, u32[]{:S(2)}) collective-permute-start(f32[8,128]{1,0:T(8,128)S(1)} %add.3.rest_0_), channel_id=1, source_target_pairs={{0,4},{1,5},{4,0},{5,1},{8,12},{9,13},{12,8},{13,9},{2,6},{3,7},{6... | collective-permute-start | bytes 12296 | tf_op jit(solution)/shard_map/ppermute | solution.py:438
  22.6 2.0 %collective-permute-start.8 = (bf16[8,256,128]{2,1,0:T(8,128)(2,1)S(1)}, bf16[8,256,128]{2,1,0:T(8,128)(2,1)S(1)}, u32[]{:S(2)}, u32[]{:S(2)}) collective-permute-start(bf16[8,256,128]{2,1,0:T(8,128)(2,1)S(1)} %get-tuple-element.57), channel_id=1, source_target_pairs={{0,1},{1,0},{2,3},{3,2},{4,5},{5,4},{6,7},{7,6},{8,9},{9,8},{10,11... | collective-permute-start | bytes 1572872 | tf_op jit(solution)/shard_map/ppermute | solution.py:430
  22.7 1.9 %copy-start = (bf16[1,12,256,256]{3,2,1,0:T(8,128)(2,1)S(1)}, bf16[1,12,256,256]{3,2,1,0:T(8,128)(2,1)}, u32[]{:S(2)}) copy-start(bf16[1,12,256,256]{3,2,1,0:T(8,128)(2,1)} %param.6) | copy-start | bytes 4718596
  23.7 5.1 %collective-permute-start.9 = (f32[896,128]{1,0:T(8,128)S(1)}, f32[896,128]{1,0:T(8,128)S(1)}, u32[]{:S(2)}, u32[]{:S(2)}) collective-permute-start(f32[896,128]{1,0:T(8,128)S(1)} %get-tuple-element.62), channel_id=1, source_target_pairs={{0,1},{1,0},{2,3},{3,2},{4,5},{5,4},{6,7},{7,6},{8,9},{9,8},{10,11... | collective-permute-start | bytes 1376264 | tf_op jit(solution)/shard_map/ppermute | solution.py:430
  27.6 10.8 %collective-permute-start.10 = (bf16[1152,128]{1,0:T(8,128)(2,1)S(1)}, bf16[1152,128]{1,0:T(8,128)(2,1)S(1)}, u32[]{:S(2)}, u32[]{:S(2)}) collective-permute-start(bf16[1152,128]{1,0:T(8,128)(2,1)S(1)} %get-tuple-element.64), channel_id=1, source_target_pairs={{0,2},{1,3},{2,0},{3,1},{4,6},{5,7},{6,4},{7,5},{8,10},{9,11},{10,... | collective-permute-start | bytes 884744 | tf_op jit(solution)/shard_map/ppermute | solution.py:438
  28.9 7.6 %collective-permute-start.11 = (bf16[240,128]{1,0:T(8,128)(2,1)S(1)}, bf16[240,128]{1,0:T(8,128)(2,1)S(1)}, u32[]{:S(2)}, u32[]{:S(2)}) collective-permute-start(bf16[240,128]{1,0:T(8,128)(2,1)S(1)} %get-tuple-element.65), channel_id=1, source_target_pairs={{0,8},{1,13},{4,12},{5,9},{8,0},{9,5},{12,4},{13,1},{2,10},{3,15},... | collective-permute-start | bytes 184328 | tf_op jit(solution)/shard_map/ppermute | solution.py:438
  32.0 6.2 %collective-permute-start.12 = (bf16[240,128]{1,0:T(8,128)(2,1)S(1)}, bf16[240,128]{1,0:T(8,128)(2,1)S(1)}, u32[]{:S(2)}, u32[]{:S(2)}) collective-permute-start(bf16[240,128]{1,0:T(8,128)(2,1)S(1)} %get-tuple-element.66), channel_id=1, source_target_pairs={{0,12},{1,9},{4,8},{5,13},{8,4},{9,1},{12,0},{13,5},{2,14},{3,11},... | collective-permute-start | bytes 184328 | tf_op jit(solution)/shard_map/ppermute | solution.py:438
  33.3 5.0 %collective-permute-start.13 = (bf16[240,128]{1,0:T(8,128)(2,1)S(1)}, bf16[240,128]{1,0:T(8,128)(2,1)S(1)}, u32[]{:S(2)}, u32[]{:S(2)}) collective-permute-start(bf16[240,128]{1,0:T(8,128)(2,1)S(1)} %get-tuple-element.67), channel_id=1, source_target_pairs={{0,4},{1,5},{4,0},{5,1},{8,12},{9,13},{12,8},{13,9},{2,6},{3,7},{6... | collective-permute-start | bytes 184328 | tf_op jit(solution)/shard_map/ppermute | solution.py:438
  38.5 8.0 %collective-permute-start.14 = (bf16[288,128]{1,0:T(8,128)(2,1)S(1)}, bf16[288,128]{1,0:T(8,128)(2,1)S(1)}, u32[]{:S(2)}, u32[]{:S(2)}) collective-permute-start(bf16[288,128]{1,0:T(8,128)(2,1)S(1)} %get-tuple-element.71), channel_id=1, source_target_pairs={{0,8},{1,13},{4,12},{5,9},{8,0},{9,5},{12,4},{13,1},{2,10},{3,15},... | collective-permute-start | bytes 221192 | tf_op jit(solution)/shard_map/ppermute | solution.py:438
  39.9 6.5 %collective-permute-start.15 = (bf16[288,128]{1,0:T(8,128)(2,1)S(1)}, bf16[288,128]{1,0:T(8,128)(2,1)S(1)}, u32[]{:S(2)}, u32[]{:S(2)}) collective-permute-start(bf16[288,128]{1,0:T(8,128)(2,1)S(1)} %get-tuple-element.72), channel_id=1, source_target_pairs={{0,12},{1,9},{4,8},{5,13},{8,4},{9,1},{12,0},{13,5},{2,14},{3,11},... | collective-permute-start | bytes 221192 | tf_op jit(solution)/shard_map/ppermute | solution.py:438
  41.3 5.9 %collective-permute-start.16 = (bf16[288,128]{1,0:T(8,128)(2,1)S(1)}, bf16[288,128]{1,0:T(8,128)(2,1)S(1)}, u32[]{:S(2)}, u32[]{:S(2)}) collective-permute-start(bf16[288,128]{1,0:T(8,128)(2,1)S(1)} %get-tuple-element.73), channel_id=1, source_target_pairs={{0,4},{1,5},{4,0},{5,1},{8,12},{9,13},{12,8},{13,9},{2,6},{3,7},{6... | collective-permute-start | bytes 221192 | tf_op jit(solution)/shard_map/ppermute | solution.py:438
  42.0 3.9 %collective-permute-start.17 = (bf16[128,128]{1,0:T(8,128)(2,1)S(1)}, bf16[128,128]{1,0:T(8,128)(2,1)S(1)}, u32[]{:S(2)}, u32[]{:S(2)}) collective-permute-start(bf16[128,128]{1,0:T(8,128)(2,1)S(1)} %get-tuple-element.74), channel_id=1, source_target_pairs={{0,2},{1,3},{2,0},{3,1},{4,6},{5,7},{6,4},{7,5},{8,10},{9,11},{10,... | collective-permute-start | bytes 98312 | tf_op jit(solution)/shard_map/ppermute | solution.py:438
  47.2 8.6 %collective-permute-start.21 = (bf16[288,128]{1,0:T(8,128)(2,1)S(1)}, bf16[288,128]{1,0:T(8,128)(2,1)S(1)}, u32[]{:S(2)}, u32[]{:S(2)}) collective-permute-start(bf16[288,128]{1,0:T(8,128)(2,1)S(1)} %get-tuple-element.76.refs_0_), channel_id=1, source_target_pairs={{0,8},{1,13},{4,12},{5,9},{8,0},{9,5},{12,4},{13,1},{2,10},{3,15},... | collective-permute-start | bytes 221192 | tf_op jit(solution)/shard_map/ppermute | solution.py:438
  48.9 6.9 %collective-permute-start.20 = (bf16[288,128]{1,0:T(8,128)(2,1)S(1)}, bf16[288,128]{1,0:T(8,128)(2,1)S(1)}, u32[]{:S(2)}, u32[]{:S(2)}) collective-permute-start(bf16[288,128]{1,0:T(8,128)(2,1)S(1)} %get-tuple-element.76.refs_0_), channel_id=1, source_target_pairs={{0,12},{1,9},{4,8},{5,13},{8,4},{9,1},{12,0},{13,5},{2,14},{3,11},... | collective-permute-start | bytes 221192 | tf_op jit(solution)/shard_map/ppermute | solution.py:438
  50.2 6.3 %collective-permute-start.19 = (bf16[288,128]{1,0:T(8,128)(2,1)S(1)}, bf16[288,128]{1,0:T(8,128)(2,1)S(1)}, u32[]{:S(2)}, u32[]{:S(2)}) collective-permute-start(bf16[288,128]{1,0:T(8,128)(2,1)S(1)} %get-tuple-element.76.refs_0_), channel_id=1, source_target_pairs={{0,4},{1,5},{4,0},{5,1},{8,12},{9,13},{12,8},{13,9},{2,6},{3,7},{6... | collective-permute-start | bytes 221192 | tf_op jit(solution)/shard_map/ppermute | solution.py:438
  50.8 3.9 %collective-permute-start.22 = (bf16[112,128]{1,0:T(8,128)(2,1)S(1)}, bf16[112,128]{1,0:T(8,128)(2,1)S(1)}, u32[]{:S(2)}, u32[]{:S(2)}) collective-permute-start(bf16[112,128]{1,0:T(8,128)(2,1)S(1)} %get-tuple-element.77.refs_4_), channel_id=1, source_target_pairs={{0,2},{1,3},{2,0},{3,1},{4,6},{5,7},{6,4},{7,5},{8,10},{9,11},{10,... | collective-permute-start | bytes 86024 | tf_op jit(solution)/shard_map/ppermute | solution.py:438
  56.5 8.9 %collective-permute-start.23 = (bf16[1152,128]{1,0:T(8,128)(2,1)S(1)}, bf16[1152,128]{1,0:T(8,128)(2,1)S(1)}, u32[]{:S(2)}, u32[]{:S(2)}) collective-permute-start(bf16[1152,128]{1,0:T(8,128)(2,1)S(1)} %get-tuple-element.78.refs_0_), channel_id=1, source_target_pairs={{0,2},{1,3},{2,0},{3,1},{4,6},{5,7},{6,4},{7,5},{8,10},{9,11},{10,... | collective-permute-start | bytes 884744 | tf_op jit(solution)/shard_map/ppermute | solution.py:438
  57.8 7.2 %collective-permute-start.26 = (bf16[224,128]{1,0:T(8,128)(2,1)S(1)}, bf16[224,128]{1,0:T(8,128)(2,1)S(1)}, u32[]{:S(2)}, u32[]{:S(2)}) collective-permute-start(bf16[224,128]{1,0:T(8,128)(2,1)S(1)} %get-tuple-element.79.refs_2_), channel_id=1, source_target_pairs={{0,8},{1,13},{4,12},{5,9},{8,0},{9,5},{12,4},{13,1},{2,10},{3,15},... | collective-permute-start | bytes 172040 | tf_op jit(solution)/shard_map/ppermute | solution.py:438
  58.2 6.7 %collective-permute-start.25 = (bf16[224,128]{1,0:T(8,128)(2,1)S(1)}, bf16[224,128]{1,0:T(8,128)(2,1)S(1)}, u32[]{:S(2)}, u32[]{:S(2)}) collective-permute-start(bf16[224,128]{1,0:T(8,128)(2,1)S(1)} %get-tuple-element.79.refs_2_), channel_id=1, source_target_pairs={{0,12},{1,9},{4,8},{5,13},{8,4},{9,1},{12,0},{13,5},{2,14},{3,11},... | collective-permute-start | bytes 172040 | tf_op jit(solution)/shard_map/ppermute | solution.py:438
  60.7 4.8 %collective-permute-start.24 = (bf16[224,128]{1,0:T(8,128)(2,1)S(1)}, bf16[224,128]{1,0:T(8,128)(2,1)S(1)}, u32[]{:S(2)}, u32[]{:S(2)}) collective-permute-start(bf16[224,128]{1,0:T(8,128)(2,1)S(1)} %get-tuple-element.79.refs_2_), channel_id=1, source_target_pairs={{0,4},{1,5},{4,0},{5,1},{8,12},{9,13},{12,8},{13,9},{2,6},{3,7},{6... | collective-permute-start | bytes 172040 | tf_op jit(solution)/shard_map/ppermute | solution.py:438
  61.2 1.2 %collective-permute-start.18 = (f32[4,128]{1,0:T(4,128)S(1)}, f32[4,128]{1,0:T(4,128)S(1)}, u32[]{:S(2)}, u32[]{:S(2)}) collective-permute-start(f32[4,128]{1,0:T(4,128)S(1)} %get-tuple-element.75.small_ref), channel_id=1, source_target_pairs={{0,1},{1,0},{2,3},{3,2},{4,5},{5,4},{6,7},{7,6},{8,9},{9,8},{10,11... | collective-permute-start | bytes 6152 | tf_op jit(solution)/shard_map/ppermute | solution.py:430
